TPU v7x, 128 devices: a whole 4x4x4 slice. The times are simulated.
128 devices in a mesh: fsdp: 16 (over z_hi, y, core), ctx: 8 (over z_lo, x).
Axes of the slice: x: 4, y: 4, z: 4 (z_hi: 2, z_lo: 2; z = z_hi * 2 + z_lo), core: 2. Of those that a mesh axis runs over, the one named last changes fastest.
Arguments:
- tokens: bfloat16 [16, 2048, 1024], P('fsdp', 'ctx'), may hold values from -6 to 6
- first_value: bfloat16 [16, 2048, 1024], P('fsdp', 'ctx'), may hold values from -6 to 6
- query_weight: bfloat16 [1024, 1024], P('fsdp'), may hold values from -0.1875 to 0.1875
- key_weight: bfloat16 [1024, 1024], P('fsdp'), may hold values from -0.1875 to 0.1875
- value_weight: bfloat16 [1024, 1024], P('fsdp'), may hold values from -0.1875 to 0.1875
- out_weight: bfloat16 [1024, 1024], P('fsdp'), may hold values from -1.5 to 1.5
- gate_weight: bfloat16 [1024, 2816], P('fsdp'), may hold values from -0.1875 to 0.1875
- up_weight: bfloat16 [1024, 2816], P('fsdp'), may hold values from -0.1875 to 0.1875
- down_weight: bfloat16 [2816, 1024], P('fsdp'), may hold values from -0.109375 to 0.109375
- prenorm_gain: bfloat16 [1024], P('fsdp'), may hold values from 0.5 to 1.5
- midnorm_gain: bfloat16 [1024], P('fsdp'), may hold values from 0.5 to 1.5
- cotangent: bfloat16 [16, 2048, 1024], P('fsdp', 'ctx'), may hold values from -6 to 6
- lengths: int32 [16], replicated, may hold values from 1 to 2048, 22528 in all
- assignment: int32 [16], replicated, may hold values from 0 to 15, each once
Outputs:
- layer_out: bfloat16 [16, 2048, 1024], P('fsdp', 'ctx')
- tokens_grad: float32 [16, 2048, 1024], P('fsdp', 'ctx')
- first_grad: float32 [16, 2048, 1024], P('fsdp', 'ctx')
- query_grad: float32 [1024, 1024], P('fsdp')
- key_grad: float32 [1024, 1024], P('fsdp')
- value_grad: float32 [1024, 1024], P('fsdp')
- out_grad: float32 [1024, 1024], P('fsdp')
- gate_grad: float32 [1024, 2816], P('fsdp')
- up_grad: float32 [1024, 2816], P('fsdp')
- down_grad: float32 [2816, 1024], P('fsdp')
- prenorm_grad: float32 [1024], P('fsdp')
- midnorm_grad: float32 [1024], P('fsdp')
Inputs may be any that keep to these rules, and one draw needn't show every extreme that they name: lengths of the sequences sum to 22528; the longest is exactly 2048. `assignment`: each sequence stands in exactly one slot.
All inputs are finite; a program needn't handle non-finite values.
Results may differ from a plain program's by a relative error of at most 0.025.
Values may be sent and summed in bfloat16 or wider, within the bound.
No kernel may reach another device: no remote copies, remote signals or barrier semaphores. Data moves between devices by JAX's collectives and lax.ppermute only.
A program may use at most 256 MiB of HBM per device.

v0:
```python
import math

import jax
import jax.numpy as jnp
from jax import lax
from jax.sharding import PartitionSpec as P

H = 16


EPS = 1e-06
MASKED = -1e30


def rope_tables(positions, half):
    freq = jnp.exp(
        jnp.arange(half, dtype=jnp.int32).astype(jnp.float32) * (-math.log(10000.0) / half)
    )
    angle = positions.astype(jnp.float32)[:, None] * freq[None, :]
    return (jnp.cos(angle), jnp.sin(angle))


def rotate(value_rows, cosine, sine):
    half = value_rows.shape[-1] // 2
    first = value_rows[..., :half]
    second = value_rows[..., half:]
    return jnp.concatenate(
        [first * cosine - second * sine, second * cosine + first * sine], axis=-1
    )


def norm_apply(value_rows, gain):
    inverse = lax.rsqrt(jnp.mean(value_rows * value_rows, axis=-1, keepdims=True) + EPS)
    return (value_rows * inverse * gain, inverse)


def norm_back(value_rows, inverse, gain, upstream):
    scaled = upstream * gain
    gain_part = jnp.sum(upstream * value_rows * inverse, axis=(0, 1))
    inner = jnp.mean(scaled * value_rows, axis=-1, keepdims=True)
    return (inverse * scaled - value_rows * inverse * inverse * inverse * inner, gain_part)


def attn_inputs(attn_full, tokens_wide, first_wide, cos_rows, sin_rows, head_count):
    query_mat, key_mat, value_mat, out_mat, gain_mat = attn_full
    normed, inverse = norm_apply(tokens_wide, gain_mat.astype(jnp.float32))
    normed_low = normed.astype(jnp.bfloat16)
    query = jnp.dot(normed_low, query_mat, preferred_element_type=jnp.float32)
    keyed = jnp.dot(normed_low, key_mat, preferred_element_type=jnp.float32)
    own_value = jnp.dot(normed_low, value_mat, preferred_element_type=jnp.float32)
    heads_shape = query.shape[:2] + (head_count, query.shape[2] // head_count)
    query_rotated_rows = rotate(query.reshape(heads_shape), cos_rows, sin_rows).astype(jnp.bfloat16)
    key_rot = (
        rotate(keyed.reshape(heads_shape), cos_rows, sin_rows)
        .astype(jnp.bfloat16)
        .reshape(query.shape)
    )
    value_mix = (0.5 * own_value + 0.5 * first_wide).astype(jnp.bfloat16)
    return (normed_low, inverse, query_rotated_rows, key_rot, value_mix)


def attention(query_rotated_rows, keys_all, values_all, allowed, head_count, score_scale):
    slots, span, width = keys_all.shape
    rows = query_rotated_rows.shape[1]
    key_rows_per_head = keys_all.reshape(slots, span, head_count, width // head_count)
    value_rows_per_head = values_all.reshape(slots, span, head_count, width // head_count)
    scores = (
        jnp.einsum(
            "biuv,bfuv->buif",
            query_rotated_rows,
            key_rows_per_head,
            preferred_element_type=jnp.float32,
        )
        * score_scale
    )
    scores = jnp.where(allowed[:, None], scores, MASKED)
    peak = jnp.max(scores, axis=-1, keepdims=True)
    raised = jnp.exp(scores - peak)
    denominator = jnp.sum(raised, axis=-1, keepdims=True)
    shares = raised / denominator
    attention_share_narrow = shares.astype(jnp.bfloat16)
    mixed = jnp.einsum(
        "ytjo,yotv->yjtv",
        attention_share_narrow,
        value_rows_per_head,
        preferred_element_type=jnp.float32,
    )
    return (
        shares,
        attention_share_narrow,
        mixed.astype(jnp.bfloat16).reshape(slots, rows, width),
        key_rows_per_head,
        value_rows_per_head,
        peak,
        denominator,
    )


def mlp_inputs(mlp_full, middle):
    gate_mat, upper_mat, down_mat, gain_mat = mlp_full
    normed, inverse = norm_apply(middle, gain_mat.astype(jnp.float32))
    normed_low = normed.astype(jnp.bfloat16)
    gate = jnp.dot(normed_low, gate_mat, preferred_element_type=jnp.float32)
    upper = jnp.dot(normed_low, upper_mat, preferred_element_type=jnp.float32)
    hidden = (jax.nn.silu(gate) * upper).astype(jnp.bfloat16)
    branch = jnp.dot(hidden, down_mat, preferred_element_type=jnp.float32)
    return (normed_low, inverse, gate, upper, hidden, branch)


def body(
    tokens,
    first_value,
    query_weight,
    key_weight,
    value_weight,
    out_weight,
    gate_weight,
    up_weight,
    down_weight,
    prenorm_gain,
    midnorm_gain,
    cotangent,
    lengths,
    assignment,
):
    slots, rows, width = tokens.shape
    head_count = H
    head_dim = width // head_count
    score_scale = head_dim ** (-0.5)
    total_len = rows * lax.axis_size("ctx")
    slot_count = assignment.shape[0]
    chosen = assignment[:, None] == jnp.arange(slot_count, dtype=jnp.int32)[None, :]
    lengths_all = jnp.sum(jnp.where(chosen, lengths[None, :], 0), axis=1)
    slot_lengths = lax.dynamic_slice_in_dim(lengths_all, lax.axis_index("fsdp") * slots, slots)
    query_places = lax.axis_index("ctx") * rows + jnp.arange(rows, dtype=jnp.int32)
    key_places = jnp.arange(total_len, dtype=jnp.int32)
    valid = query_places[None, :] < slot_lengths[:, None]
    allowed = (key_places[None, None, :] <= query_places[None, :, None]) & (
        key_places[None, None, :] < slot_lengths[:, None, None]
    )
    cosine, sine = rope_tables(query_places, head_dim // 2)
    cos_rows = cosine[None, :, None, :]
    sin_rows = sine[None, :, None, :]
    valid_wide = valid[:, :, None]
    tokens_wide = tokens.astype(jnp.float32)
    first_wide = first_value.astype(jnp.float32)
    attn_full = (
        lax.all_gather(query_weight, "fsdp", axis=0, tiled=True),
        lax.all_gather(key_weight, "fsdp", axis=0, tiled=True),
        lax.all_gather(value_weight, "fsdp", axis=0, tiled=True),
        lax.all_gather(out_weight, "fsdp", axis=0, tiled=True),
        lax.all_gather(prenorm_gain, "fsdp", axis=0, tiled=True),
    )
    normed_low, inverse, query_rotated_rows, key_rot, value_mix = attn_inputs(
        attn_full, tokens_wide, first_wide, cos_rows, sin_rows, head_count
    )
    keys_all, values_all = (
        lax.all_gather(key_rot, "ctx", axis=1, tiled=True),
        lax.all_gather(value_mix, "ctx", axis=1, tiled=True),
    )
    (
        shares,
        attention_share_narrow,
        mixed_low,
        key_rows_per_head,
        value_rows_per_head,
        peak,
        denominator,
    ) = attention(query_rotated_rows, keys_all, values_all, allowed, head_count, score_scale)
    middle = tokens_wide + jnp.dot(mixed_low, attn_full[3], preferred_element_type=jnp.float32)
    mlp_full = (
        lax.all_gather(gate_weight, "fsdp", axis=0, tiled=True),
        lax.all_gather(up_weight, "fsdp", axis=0, tiled=True),
        lax.all_gather(down_weight, "fsdp", axis=0, tiled=True),
        lax.all_gather(midnorm_gain, "fsdp", axis=0, tiled=True),
    )
    normed_two, inverse_two, gate, upper, hidden, branch = mlp_inputs(mlp_full, middle)
    layer_out = jnp.where(valid_wide, middle + branch, 0.0).astype(jnp.bfloat16)
    held = lax.optimization_barrier(
        (
            layer_out,
            query_weight,
            key_weight,
            value_weight,
            out_weight,
            prenorm_gain,
            gate_weight,
            up_weight,
            down_weight,
            midnorm_gain,
            tokens,
            first_value,
        )
    )
    (
        layer_hold,
        query_again,
        key_again,
        value_again,
        out_again,
        prenorm_again,
        gate_again,
        upper_again,
        down_again,
        midnorm_again,
        tokens_again,
        first_again,
    ) = held
    attn_full = (
        lax.all_gather(query_again, "fsdp", axis=0, tiled=True),
        lax.all_gather(key_again, "fsdp", axis=0, tiled=True),
        lax.all_gather(value_again, "fsdp", axis=0, tiled=True),
        lax.all_gather(out_again, "fsdp", axis=0, tiled=True),
        lax.all_gather(prenorm_again, "fsdp", axis=0, tiled=True),
    )
    tokens_wide = tokens_again.astype(jnp.float32)
    normed_low, inverse, query_rotated_rows, key_rot, value_mix = attn_inputs(
        attn_full, tokens_wide, first_again.astype(jnp.float32), cos_rows, sin_rows, head_count
    )
    keys_all, values_all = (
        lax.all_gather(key_rot, "ctx", axis=1, tiled=True),
        lax.all_gather(value_mix, "ctx", axis=1, tiled=True),
    )
    mlp_full = (
        lax.all_gather(gate_again, "fsdp", axis=0, tiled=True),
        lax.all_gather(upper_again, "fsdp", axis=0, tiled=True),
        lax.all_gather(down_again, "fsdp", axis=0, tiled=True),
        lax.all_gather(midnorm_again, "fsdp", axis=0, tiled=True),
    )
    (
        shares,
        attention_share_narrow,
        mixed_low,
        key_rows_per_head,
        value_rows_per_head,
        peak,
        denominator,
    ) = attention(query_rotated_rows, keys_all, values_all, allowed, head_count, score_scale)
    middle = tokens_wide + jnp.dot(mixed_low, attn_full[3], preferred_element_type=jnp.float32)
    normed_two, inverse_two, gate, upper, hidden, branch = mlp_inputs(mlp_full, middle)
    query_mat, key_mat, value_mat, out_mat, prenorm_full = attn_full
    gate_mat, upper_mat, down_mat, middle_norm_complete = mlp_full
    cot_wide = jnp.where(valid_wide, cotangent.astype(jnp.float32), 0.0)
    cot_low = cot_wide.astype(jnp.bfloat16)
    down_total = jnp.einsum("srf,sre->fe", hidden, cot_low, preferred_element_type=jnp.float32)
    hidden_back = jnp.einsum("sre,fe->srf", cot_low, down_mat, preferred_element_type=jnp.float32)
    sigma = jax.nn.sigmoid(gate)
    gate_back = (hidden_back * upper * sigma * (1.0 + gate * (1.0 - sigma))).astype(jnp.bfloat16)
    upper_back = (hidden_back * gate * sigma).astype(jnp.bfloat16)
    gate_total = jnp.einsum(
        "srd,srf->df", normed_two, gate_back, preferred_element_type=jnp.float32
    )
    upper_total = jnp.einsum(
        "srd,srf->df", normed_two, upper_back, preferred_element_type=jnp.float32
    )
    normed_two_back = jnp.einsum(
        "srf,df->srd", gate_back, gate_mat, preferred_element_type=jnp.float32
    )
    normed_two_back = normed_two_back + jnp.einsum(
        "srf,df->srd", upper_back, upper_mat, preferred_element_type=jnp.float32
    )
    middle_norm_back, midnorm_total = norm_back(
        middle, inverse_two, middle_norm_complete.astype(jnp.float32), normed_two_back
    )
    middle_back = cot_wide + middle_norm_back
    middle_low = middle_back.astype(jnp.bfloat16)
    out_total = jnp.einsum("srd,sre->de", mixed_low, middle_low, preferred_element_type=jnp.float32)
    blended_value_gradient = jnp.einsum(
        "sre,de->srd", middle_low, out_mat, preferred_element_type=jnp.float32
    ).astype(jnp.bfloat16)
    blended_value_gradient = blended_value_gradient.reshape(slots, rows, head_count, head_dim)
    prob_back = jnp.einsum(
        "biuv,bfuv->buif",
        blended_value_gradient,
        value_rows_per_head,
        preferred_element_type=jnp.float32,
    )
    inner = jnp.sum(shares * prob_back, axis=-1, keepdims=True)
    score_gradient = (shares * (prob_back - inner)).astype(jnp.bfloat16)
    query_rot_back = (
        jnp.einsum(
            "ytjo,yotv->yjtv", score_gradient, key_rows_per_head, preferred_element_type=jnp.float32
        )
        * score_scale
    )
    count = rows * lax.axis_size("ctx")
    key_part = (
        jnp.einsum(
            "xtfk,xfty->kxty",
            score_gradient,
            query_rotated_rows,
            preferred_element_type=jnp.float32,
        )
        * score_scale
    )
    value_part = jnp.einsum(
        "xtfk,xfty->kxty",
        attention_share_narrow,
        blended_value_gradient,
        preferred_element_type=jnp.float32,
    )
    key_value = lax.psum_scatter(
        jnp.concatenate(
            [key_part.reshape(count, slots, width), value_part.reshape(count, slots, width)],
            axis=-1,
        ).astype(jnp.bfloat16),
        "ctx",
        scatter_dimension=0,
        tiled=True,
    ).astype(jnp.float32)
    key_value = jnp.swapaxes(key_value, 0, 1)
    key_rot_back = key_value[..., :width].reshape(slots, rows, head_count, head_dim)
    value_mix_back = key_value[..., width:]
    first_grad = 0.5 * value_mix_back
    query_back = (
        rotate(query_rot_back, cos_rows, -sin_rows).reshape(slots, rows, width).astype(jnp.bfloat16)
    )
    key_back = (
        rotate(key_rot_back, cos_rows, -sin_rows).reshape(slots, rows, width).astype(jnp.bfloat16)
    )
    value_back = (0.5 * value_mix_back).astype(jnp.bfloat16)
    query_total = jnp.einsum(
        "srd,sre->de", normed_low, query_back, preferred_element_type=jnp.float32
    )
    key_total = jnp.einsum("srd,sre->de", normed_low, key_back, preferred_element_type=jnp.float32)
    value_total = jnp.einsum(
        "srd,sre->de", normed_low, value_back, preferred_element_type=jnp.float32
    )
    normed_back = jnp.einsum(
        "sre,de->srd", query_back, query_mat, preferred_element_type=jnp.float32
    )
    normed_back = normed_back + jnp.einsum(
        "sre,de->srd", key_back, key_mat, preferred_element_type=jnp.float32
    )
    normed_back = normed_back + jnp.einsum(
        "sre,de->srd", value_back, value_mat, preferred_element_type=jnp.float32
    )
    tokens_norm_back, prenorm_total = norm_back(
        tokens_wide, inverse, prenorm_full.astype(jnp.float32), normed_back
    )
    tokens_grad = middle_back + tokens_norm_back
    shards = (
        lax.psum_scatter(
            query_total.astype(jnp.bfloat16), "fsdp", scatter_dimension=0, tiled=True
        ).astype(jnp.float32),
        lax.psum_scatter(
            key_total.astype(jnp.bfloat16), "fsdp", scatter_dimension=0, tiled=True
        ).astype(jnp.float32),
        lax.psum_scatter(
            value_total.astype(jnp.bfloat16), "fsdp", scatter_dimension=0, tiled=True
        ).astype(jnp.float32),
        lax.psum_scatter(
            out_total.astype(jnp.bfloat16), "fsdp", scatter_dimension=0, tiled=True
        ).astype(jnp.float32),
        lax.psum_scatter(
            gate_total.astype(jnp.bfloat16), "fsdp", scatter_dimension=0, tiled=True
        ).astype(jnp.float32),
        lax.psum_scatter(
            upper_total.astype(jnp.bfloat16), "fsdp", scatter_dimension=0, tiled=True
        ).astype(jnp.float32),
        lax.psum_scatter(
            down_total.astype(jnp.bfloat16), "fsdp", scatter_dimension=0, tiled=True
        ).astype(jnp.float32),
        lax.psum_scatter(
            prenorm_total.astype(jnp.bfloat16), "fsdp", scatter_dimension=0, tiled=True
        ).astype(jnp.float32),
        lax.psum_scatter(
            midnorm_total.astype(jnp.bfloat16), "fsdp", scatter_dimension=0, tiled=True
        ).astype(jnp.float32),
    )
    shards = (
        lax.psum(shards[0].astype(jnp.bfloat16), "ctx").astype(jnp.float32),
        lax.psum(shards[1].astype(jnp.bfloat16), "ctx").astype(jnp.float32),
        lax.psum(shards[2].astype(jnp.bfloat16), "ctx").astype(jnp.float32),
        lax.psum(shards[3].astype(jnp.bfloat16), "ctx").astype(jnp.float32),
        lax.psum(shards[4].astype(jnp.bfloat16), "ctx").astype(jnp.float32),
        lax.psum(shards[5].astype(jnp.bfloat16), "ctx").astype(jnp.float32),
        lax.psum(shards[6].astype(jnp.bfloat16), "ctx").astype(jnp.float32),
        lax.psum(shards[7].astype(jnp.bfloat16), "ctx").astype(jnp.float32),
        lax.psum(shards[8].astype(jnp.bfloat16), "ctx").astype(jnp.float32),
    )
    return (layer_out, tokens_grad, first_grad) + tuple(shards)


def solution(mesh):
    placed = (
        P("fsdp", "ctx", None),
        P("fsdp", "ctx", None),
        P("fsdp", None),
        P("fsdp", None),
        P("fsdp", None),
        P("fsdp", None),
        P("fsdp", None),
        P("fsdp", None),
        P("fsdp", None),
        P("fsdp"),
        P("fsdp"),
        P("fsdp", "ctx", None),
        P(),
        P(),
    )
    return jax.shard_map(
        body,
        mesh=mesh,
        in_specs=placed,
        out_specs=(
            P("fsdp", "ctx", None),
            P("fsdp", "ctx", None),
            P("fsdp", "ctx", None),
            P("fsdp", None),
            P("fsdp", None),
            P("fsdp", None),
            P("fsdp", None),
            P("fsdp", None),
            P("fsdp", None),
            P("fsdp", None),
            P("fsdp"),
            P("fsdp"),
        ),
        check_vma=False,
    )
```

profile of v0, /device:TPU:0, one launch (start us, length us, event | category | flops | bytes accessed | tf_op | source)
XLA Modules:
  0.0 1898.2 jit_solution(7592437245151458701)
XLA Ops:
  13.1 39.3 %all-reduce.8 = (bf16[1024]{0:T(1024)(128)(2,1)S(1)}, bf16[1024]{0:T(1024)(128)(2,1)S(1)}) all-reduce(bf16[1024]{0:T(1024)(128)(2,1)S(1)} %dynamic-update-slice, bf16[1024]{0:T(1024)(128)(2,1)S(1)} %dynamic-update-slice.1), channel_id=1, replica_groups=mesh['fsdp'=16,'ctx'=8] {'fsdp'}, use_global_device_ids=true, to_apply=%add | all-reduce | flops 2048 | bytes 8192
  53.6 7.8 all-gather.19.cloned.1.call-done
  61.4 3.4 fusion.29
  65.7 45.3 %all-gather.23.cloned.1.call-done = bf16[1024,1024]{1,0:T(8,128)(2,1)} async-done(((bf16[64,1024]{1,0:T(8,128)(2,1)}), bf16[1024,1024]{1,0:T(8,128)(2,1)}) %all-gather.23.cloned.1.call-update) | async-done | bytes 2097168 | tf_op jit(solution)/shard_map/all_gather | solution.py:148
  111.0 2.9 copy.60
  113.9 46.7 %all-gather.25.cloned.1.call-done = bf16[1024,1024]{1,0:T(8,128)(2,1)} async-done(((bf16[64,1024]{1,0:T(8,128)(2,1)}), bf16[1024,1024]{1,0:T(8,128)(2,1)}) %all-gather.25.cloned.1.call-update) | async-done | bytes 2097168 | tf_op jit(solution)/shard_map/all_gather | solution.py:149
  160.6 4.0 copy.61
  174.7 39.3 %all-gather.21.cloned.1.call-done = bf16[1,2048,1024]{2,1,0:T(8,128)(2,1)} async-done(((bf16[1,256,1024]{2,1,0:T(8,128)(2,1)}), bf16[1,2048,1024]{2,1,0:T(8,128)(2,1)}) %all-gather.21.cloned.1.call-update) | async-done | bytes 4194320 | tf_op jit(solution)/shard_map/all_gather | solution.py:159
  214.0 6.5 copy.59
  220.4 54.0 %all-gather.27.cloned.1.call-done = bf16[1,2048,1024]{1,2,0:T(8,128)(2,1)} async-done(((bf16[1,256,1024]{1,2,0:T(8,128)(2,1)}), bf16[1,2048,1024]{1,2,0:T(8,128)(2,1)}) %all-gather.27.cloned.1.call-update) | async-done | bytes 4194320 | tf_op jit(solution)/shard_map/all_gather | solution.py:158
  274.5 15.5 fusion.61
  290.0 38.4 %fusion.120 = (f32[16,256]{1,0:T(8,128)S(1)}, f32[16,256,2048]{2,1,0:T(8,128)}) fusion(f32[16,256,2048]{2,1,0:T(8,128)} %fusion.61, pred[256,2048]{1,0:T(8,128)(4,1)S(1)} %fusion.19), kind=kOutput, calls=%fused_computation.185 | output fusion | flops 50333696 | bytes 67649536 | tf_op jit(solution)/shard_map/sub | solution.py:78
  328.4 15.6 fusion.34
  346.4 43.4 %all-gather.31.cloned.1.call-done = bf16[1024,2816]{1,0:T(8,128)(2,1)} async-done(((bf16[64,2816]{1,0:T(8,128)(2,1)}), bf16[1024,2816]{1,0:T(8,128)(2,1)}) %all-gather.31.cloned.1.call-update) | async-done | bytes 5767184 | tf_op jit(solution)/shard_map/all_gather | solution.py:172
  389.8 5.9 fusion.57
  395.7 57.1 %all-gather.33.cloned.1.call-done = bf16[1024,2816]{1,0:T(8,128)(2,1)} async-done(((bf16[64,2816]{1,0:T(8,128)(2,1)}), bf16[1024,2816]{1,0:T(8,128)(2,1)}) %all-gather.33.cloned.1.call-update) | async-done | bytes 5767184 | tf_op jit(solution)/shard_map/all_gather | solution.py:173
  452.8 63.1 %all-gather.35.cloned.1.call-done = bf16[2816,1024]{1,0:T(8,128)(2,1)} async-done(((bf16[176,1024]{1,0:T(8,128)(2,1)}), bf16[2816,1024]{1,0:T(8,128)(2,1)}) %all-gather.35.cloned.1.call-update) | async-done | bytes 5767184 | tf_op jit(solution)/shard_map/all_gather | solution.py:174
  515.9 9.3 fusion.30
  527.0 35.5 %all-reduce.7 = (bf16[1024]{0:T(1024)(128)(2,1)S(1)}, bf16[1024]{0:T(1024)(128)(2,1)S(1)}) all-reduce(bf16[1024]{0:T(1024)(128)(2,1)S(1)} %dynamic-update-slice.2, bf16[1024]{0:T(1024)(128)(2,1)S(1)} %dynamic-update-slice.3), channel_id=1, replica_groups=mesh['fsdp'=16,'ctx'=8] {'fsdp'}, use_global_device_ids=true, to_apply=%add.2 | all-reduce | flops 2048 | bytes 8192
  562.7 9.7 all-gather.37.cloned.1.call-done
  572.4 3.1 fusion.28
  575.6 46.4 %all-gather.43.cloned.1.call-done = bf16[1024,1024]{1,0:T(8,128)(2,1)} async-done(((bf16[64,1024]{1,0:T(8,128)(2,1)}), bf16[1024,1024]{1,0:T(8,128)(2,1)}) %all-gather.43.cloned.1.call-update) | async-done | bytes 2097168 | tf_op jit(solution)/shard_map/all_gather | solution.py:211
  621.9 2.9 copy.64
  624.8 46.6 %all-gather.41.cloned.1.call-done = bf16[1024,1024]{1,0:T(8,128)(2,1)} async-done(((bf16[64,1024]{1,0:T(8,128)(2,1)}), bf16[1024,1024]{1,0:T(8,128)(2,1)}) %all-gather.41.cloned.1.call-update) | async-done | bytes 2097168 | tf_op jit(solution)/shard_map/all_gather | solution.py:210
  671.4 3.9 copy.63
  682.3 42.6 %all-gather.39.cloned.1.call-done = bf16[1,2048,1024]{2,1,0:T(8,128)(2,1)} async-done(((bf16[1,256,1024]{2,1,0:T(8,128)(2,1)}), bf16[1,2048,1024]{2,1,0:T(8,128)(2,1)}) %all-gather.39.cloned.1.call-update) | async-done | bytes 4194320 | tf_op jit(solution)/shard_map/all_gather | solution.py:222
  724.9 7.0 copy.62
  731.9 53.5 %all-gather.45.cloned.1.call-done = bf16[1,2048,1024]{1,2,0:T(8,128)(2,1)} async-done(((bf16[1,256,1024]{1,2,0:T(8,128)(2,1)}), bf16[1,2048,1024]{1,2,0:T(8,128)(2,1)}) %all-gather.45.cloned.1.call-update) | async-done | bytes 4194320 | tf_op jit(solution)/shard_map/all_gather | solution.py:221
  785.4 15.5 fusion.84
  800.9 38.4 %fusion.121 = (f32[16,256]{1,0:T(8,128)S(1)}, f32[16,256,2048]{2,1,0:T(8,128)}) fusion(f32[16,256,2048]{2,1,0:T(8,128)} %fusion.84, pred[256,2048]{1,0:T(8,128)(4,1)S(1)} %fusion.19), kind=kOutput, calls=%fused_computation.186 | output fusion | flops 50333696 | bytes 67649536 | tf_op jit(solution)/shard_map/sub | solution.py:78
  839.2 15.5 fusion.31
  857.4 43.2 %all-gather.53.cloned.1.call-done = bf16[1024,2816]{1,0:T(8,128)(2,1)} async-done(((bf16[64,2816]{1,0:T(8,128)(2,1)}), bf16[1024,2816]{1,0:T(8,128)(2,1)}) %all-gather.53.cloned.1.call-update) | async-done | bytes 5767184 | tf_op jit(solution)/shard_map/all_gather | solution.py:225
  900.6 5.9 fusion.123
  906.4 57.0 %all-gather.51.cloned.1.call-done = bf16[1024,2816]{1,0:T(8,128)(2,1)} async-done(((bf16[64,2816]{1,0:T(8,128)(2,1)}), bf16[1024,2816]{1,0:T(8,128)(2,1)}) %all-gather.51.cloned.1.call-update) | async-done | bytes 5767184 | tf_op jit(solution)/shard_map/all_gather | solution.py:226
  963.5 5.9 fusion.122
  969.4 57.0 %all-gather.49.cloned.1.call-done = bf16[2816,1024]{1,0:T(8,128)(2,1)} async-done(((bf16[176,1024]{1,0:T(8,128)(2,1)}), bf16[2816,1024]{1,0:T(8,128)(2,1)}) %all-gather.49.cloned.1.call-update) | async-done | bytes 5767184 | tf_op jit(solution)/shard_map/all_gather | solution.py:227
  1026.4 8.1 multiply_convert_fusion.3
  1034.5 5.4 fusion.124
  1043.8 14.3 fusion.16
  1058.1 22.7 %multiply_reduce_fusion = (f32[16,256]{1,0:T(8,128)S(1)}, f32[16,256,2048]{2,1,0:T(8,128)}) fusion(f32[16,256,2048]{2,1,0:T(8,128)} %get-tuple-element.85, f32[16,256]{1,0:T(8,128)S(1)} %get-tuple-element.84, bf16[256,16,64]{0,2,1:T(8,128)(2,1)S(1)} %bitcast.235, bf16[2048,16,64]{0,2,1:T(8,128)(2,1)} %bitcast.220), kind=kOutput, calls=%fused_computation.3 | convolution fusion | flops 1098903552 | bytes 71860224 | tf_op jit(solution)/shard_map/biuv,bfuv->buif/dot_general | solution.py:272
  1080.9 6.6 copy.67
  1087.5 27.6 %multiply_convert_fusion = bf16[16,256,2048]{2,1,0:T(8,128)(2,1)} fusion(f32[16,256,2048]{2,1,0:T(8,128)} %get-tuple-element.90, f32[16,256]{1,0:T(8,128)S(1)} %get-tuple-element.89, f32[16,256,2048]{2,1,0:T(8,128)} %get-tuple-element.85, f32[16,256]{1,0:T(8,128)S(1)} %get-tuple-element.84), kind=kLoop, calls=%fused_computation.2 | loop fusion | flops 33554432 | bytes 83918848 | tf_op jit(solution)/shard_map/convert_element_type | solution.py:279
  1115.1 10.8 multiply_convert_fusion.1
  1125.8 6.4 copy.66
  1132.3 8.2 pad_maximum_fusion
  1142.7 7.1 convolution_convert_fusion
  1151.3 4.1 convolution_convert_fusion.1
  1156.9 4.2 convolution_convert_fusion.2
  1161.4 13.5 fusion.21
  1174.9 57.0 %reduce-scatter.9.cloned.1.call-done = bf16[256,1,2048]{2,0,1:T(8,128)(2,1)} async-done(((bf16[2048,1,2048]{2,0,1:T(8,128)(2,1)}), bf16[256,1,2048]{2,0,1:T(8,128)(2,1)}) %reduce-scatter.9.cloned.1.call-update) | async-done | bytes 1048592 | tf_op jit(solution)/shard_map/reduce_scatter | solution.py:302
  1234.6 3.0 copy.68
  1242.6 3.2 convolution_convert_fusion.6
  1248.3 57.1 %reduce-scatter.17.cloned.1.call-done = bf16[64,1024]{1,0:T(8,128)(2,1)} async-done(((bf16[1024,1024]{1,0:T(8,128)(2,1)}), bf16[64,1024]{1,0:T(8,128)(2,1)}) %reduce-scatter.17.cloned.1.call-update) | async-done | bytes 131088 | tf_op jit(solution)/shard_map/reduce_scatter | solution.py:352
  1305.4 90.3 %reduce-scatter.23.cloned.1.call-done = bf16[176,1024]{1,0:T(8,128)(2,1)} async-done(((bf16[2816,1024]{1,0:T(8,128)(2,1)}), bf16[176,1024]{1,0:T(8,128)(2,1)}) %reduce-scatter.23.cloned.1.call-update) | async-done | bytes 360464 | tf_op jit(solution)/shard_map/reduce_scatter | solution.py:361
  1395.7 89.9 %reduce-scatter.21.cloned.1.call-done = bf16[64,2816]{1,0:T(8,128)(2,1)} async-done(((bf16[1024,2816]{1,0:T(8,128)(2,1)}), bf16[64,2816]{1,0:T(8,128)(2,1)}) %reduce-scatter.21.cloned.1.call-update) | async-done | bytes 360464 | tf_op jit(solution)/shard_map/reduce_scatter | solution.py:358
  1485.5 89.9 %reduce-scatter.19.cloned.1.call-done = bf16[64,2816]{1,0:T(8,128)(2,1)} async-done(((bf16[1024,2816]{1,0:T(8,128)(2,1)}), bf16[64,2816]{1,0:T(8,128)(2,1)}) %reduce-scatter.19.cloned.1.call-update) | async-done | bytes 360464 | tf_op jit(solution)/shard_map/reduce_scatter | solution.py:355
  1575.4 73.2 %reduce-scatter.13.cloned.1.call-done = bf16[64,1024]{1,0:T(8,128)(2,1)} async-done(((bf16[1024,1024]{1,0:T(8,128)(2,1)}), bf16[64,1024]{1,0:T(8,128)(2,1)}) %reduce-scatter.13.cloned.1.call-update) | async-done | bytes 131088 | tf_op jit(solution)/shard_map/reduce_scatter | solution.py:346
  1648.6 73.8 %reduce-scatter.11.cloned.1.call-done = bf16[64,1024]{1,0:T(8,128)(2,1)} async-done(((bf16[1024,1024]{1,0:T(8,128)(2,1)}), bf16[64,1024]{1,0:T(8,128)(2,1)}) %reduce-scatter.11.cloned.1.call-update) | async-done | bytes 131088 | tf_op jit(solution)/shard_map/reduce_scatter | solution.py:343
  1722.5 73.7 %reduce-scatter.15.cloned.1.call-done = bf16[64,1024]{1,0:T(8,128)(2,1)} async-done(((bf16[1024,1024]{1,0:T(8,128)(2,1)}), bf16[64,1024]{1,0:T(8,128)(2,1)}) %reduce-scatter.15.cloned.1.call-update) | async-done | bytes 131088 | tf_op jit(solution)/shard_map/reduce_scatter | solution.py:349
  1796.9 2.7 fusion.125
  1802.3 33.4 %all-reduce.6 = (bf16[1024]{0:T(1024)(128)(2,1)S(1)}, bf16[1024]{0:T(1024)(128)(2,1)S(1)}) all-reduce(bf16[1024]{0:T(1024)(128)(2,1)S(1)} %get-tuple-element.36, bf16[1024]{0:T(1024)(128)(2,1)S(1)} %copy-done.26), channel_id=10, replica_groups=mesh['fsdp'=16,'ctx'=8] {'fsdp'}, use_global_device_ids=true, to_apply=%region_28.29.clone | all-reduce | flops 2048 | bytes 8192
  1835.9 19.4 %all-reduce.9 = (bf16[64]{0:T(256)(128)(2,1)S(1)}, bf16[64]{0:T(256)(128)(2,1)S(1)}) all-reduce(bf16[64]{0:T(256)(128)(2,1)S(1)} %dynamic-slice.5, bf16[64]{0:T(256)(128)(2,1)S(1)} %dynamic-slice.7), channel_id=1, replica_groups=mesh['fsdp'=16,'ctx'=8] {'ctx'}, use_global_device_ids=true, to_apply=%region_29.30 | all-reduce | flops 128 | bytes 512 | tf_op jit(solution)/shard_map/psum | solution.py:379
  1856.3 2.6 fusion.41
  1858.9 19.9 %all-reduce.13.cloned.1.call-done = (bf16[64,1024]{1,0:T(8,128)(2,1)}, bf16[64,1024]{1,0:T(8,128)(2,1)}, bf16[64,1024]{1,0:T(8,128)(2,1)}, bf16[64,1024]{1,0:T(8...) async-done(((bf16[64,1024]{1,0:T(8,128)(2,1)}, bf16[64,1024]{1,0:T(8,128)(2,1)}, bf16[64,1024]{1,0:T(8,128)(2,1)}, ...) | async-done | bytes 1605648 | tf_op jit(solution)/shard_map/psum | solution.py:372
  (187 shorter events, 66.8 us)
Async XLA Ops:
  7.2 54.3 %all-gather.19.cloned.1.call-start = ((), (), s32[]{:S(2)}) async-start(), calls=%async_computation.8 | async-start | bytes 2228224 | tf_op jit(solution)/shard_map/all_gather | solution.py:150
  7.9 103.1 %all-gather.23.cloned.1.call-start = ((), (), s32[]{:S(2)}) async-start(), calls=%async_computation.10 | async-start | bytes 2228224 | tf_op jit(solution)/shard_map/all_gather | solution.py:148
  8.7 151.9 %all-gather.25.cloned.1.call-start = ((), (), s32[]{:S(2)}) async-start(), calls=%async_computation.11 | async-start | bytes 2228224 | tf_op jit(solution)/shard_map/all_gather | solution.py:149
  9.4 204.6 %all-gather.21.cloned.1.call-start = ((), (), s32[]{:S(2)}) async-start(), calls=%async_computation.9 | async-start | bytes 4718592 | tf_op jit(solution)/shard_map/all_gather | solution.py:159
  64.8 209.6 %all-gather.27.cloned.1.call-start = ((), (), s32[]{:S(2)}) async-start(), calls=%async_computation.12 | async-start | bytes 4718592 | tf_op jit(solution)/shard_map/all_gather | solution.py:158
  65.7 612.9 %copy-start.16 = (f32[256,32]{0,1:T(8,128)}, f32[256,32]{0,1:T(8,128)S(1)}, u32[]{:S(2)}) copy-start(f32[256,32]{0,1:T(8,128)S(1)} %get-tuple-element.77) | copy-start | bytes 98308
  111.0 53.6 %copy-start = (bf16[1,256,1024]{2,1,0:T(8,128)(2,1)S(1)}, bf16[1,256,1024]{2,1,0:T(8,128)(2,1)}, u32[]{:S(2)}) copy-start(bf16[1,256,1024]{2,1,0:T(8,128)(2,1)} %param.14) | copy-start | bytes 1572868
  165.4 6.8 copy-start.29
  165.4 6.8 copy-start.30
  169.1 174.9 %all-gather.29.cloned.1.call-start = ((), (), s32[]{:S(2)}) async-start(), calls=%async_computation.13 | async-start | bytes 2228224 | tf_op jit(solution)/shard_map/all_gather | solution.py:151
  169.7 220.1 %all-gather.31.cloned.1.call-start = ((), (), s32[]{:S(2)}) async-start(), calls=%async_computation.14 | async-start | bytes 6127616 | tf_op jit(solution)/shard_map/all_gather | solution.py:172
  170.4 282.4 %all-gather.33.cloned.1.call-start = ((), (), s32[]{:S(2)}) async-start(), calls=%async_computation.15 | async-start | bytes 6127616 | tf_op jit(solution)/shard_map/all_gather | solution.py:173
  171.2 344.7 %all-gather.35.cloned.1.call-start = ((), (), s32[]{:S(2)}) async-start(), calls=%async_computation.16 | async-start | bytes 6127616 | tf_op jit(solution)/shard_map/all_gather | solution.py:174
  171.9 400.4 %all-gather.37.cloned.1.call-start = ((), (), s32[]{:S(2)}) async-start(), calls=%async_computation.17 | async-start | bytes 2228224 | tf_op jit(solution)/shard_map/all_gather | solution.py:212
  395.7 130.9 %copy-start.31 = (bf16[64]{0:T(256)(128)(2,1)S(1)}, bf16[64]{0:T(256)(128)(2,1)}, u32[]{:S(2)}) copy-start(bf16[64]{0:T(256)(128)(2,1)} %param.24) | copy-start | bytes 388
  395.7 131.1 %copy-start.32 = (bf16[64]{0:T(256)(128)(2,1)S(1)}, bf16[64]{0:T(256)(128)(2,1)}, u32[]{:S(2)}) copy-start(bf16[64]{0:T(256)(128)(2,1)} %param.23) | copy-start | bytes 388
  395.7 176.7 %copy-start.28 = (bf16[1,256,1024]{2,1,0:T(8,128)(2,1)S(1)}, bf16[1,256,1024]{2,1,0:T(8,128)(2,1)}, u32[]{:S(2)}) copy-start(bf16[1,256,1024]{2,1,0:T(8,128)(2,1)} %param.15) | copy-start | bytes 1572868
  525.2 96.8 %all-gather.43.cloned.1.call-start = ((), (), s32[]{:S(2)}) async-start(), calls=%async_computation.20 | async-start | bytes 2228224 | tf_op jit(solution)/shard_map/all_gather | solution.py:211
  525.9 145.5 %all-gather.41.cloned.1.call-start = ((), (), s32[]{:S(2)}) async-start(), calls=%async_computation.19 | async-start | bytes 2228224 | tf_op jit(solution)/shard_map/all_gather | solution.py:210
  526.5 198.4 %all-gather.39.cloned.1.call-start = ((), (), s32[]{:S(2)}) async-start(), calls=%async_computation.18 | async-start | bytes 4718592 | tf_op jit(solution)/shard_map/all_gather | solution.py:222
  562.5 113.7 %copy-start.21 = (f32[1024]{0:T(1024)}, f32[1024]{0:T(1024)S(1)}, u32[]{:S(2)}) copy-start(f32[1024]{0:T(1024)S(1)} %convert_element_type.304) | copy-start | bytes 12292
  562.7 113.5 %copy-start.24 = (f32[256]{0:T(256)}, f32[256]{0:T(256)S(1)}, u32[]{:S(2)}) copy-start(f32[256]{0:T(256)S(1)} %add_rsqrt_fusion.1) | copy-start | bytes 3076
  575.5 209.9 %all-gather.45.cloned.1.call-start = ((), (), s32[]{:S(2)}) async-start(), calls=%async_computation.21 | async-start | bytes 4718592 | tf_op jit(solution)/shard_map/all_gather | solution.py:221
  679.0 106.5 %copy-start.7 = (bf16[256,16,32]{0,2,1:T(8,128)(2,1)}, bf16[256,16,32]{0,2,1:T(8,128)(2,1)S(1)}, u32[]{:S(2)}) copy-start(bf16[256,16,32]{0,2,1:T(8,128)(2,1)S(1)} %get-tuple-element.61) | copy-start | bytes 786436
  679.0 106.4 %copy-start.9 = (bf16[256,16,32]{0,2,1:T(8,128)(2,1)}, bf16[256,16,32]{0,2,1:T(8,128)(2,1)S(1)}, u32[]{:S(2)}) copy-start(bf16[256,16,32]{0,2,1:T(8,128)(2,1)S(1)} %get-tuple-element.62) | copy-start | bytes 786436
  679.9 174.9 %all-gather.47.cloned.1.call-start = ((), (), s32[]{:S(2)}) async-start(), calls=%async_computation.22 | async-start | bytes 2228224 | tf_op jit(solution)/shard_map/all_gather | solution.py:213
  680.5 220.1 %all-gather.53.cloned.1.call-start = ((), (), s32[]{:S(2)}) async-start(), calls=%async_computation.25 | async-start | bytes 6127616 | tf_op jit(solution)/shard_map/all_gather | solution.py:225
  681.1 282.4 %all-gather.51.cloned.1.call-start = ((), (), s32[]{:S(2)}) async-start(), calls=%async_computation.24 | async-start | bytes 6127616 | tf_op jit(solution)/shard_map/all_gather | solution.py:226
  681.7 344.7 %all-gather.49.cloned.1.call-start = ((), (), s32[]{:S(2)}) async-start(), calls=%async_computation.23 | async-start | bytes 6127616 | tf_op jit(solution)/shard_map/all_gather | solution.py:227
  682.2 549.7 %reduce-scatter.9.cloned.1.call-start = ((), (), s32[]{:S(2)}) async-start(), calls=%async_computation.26 | async-start | bytes 9437184 | tf_op jit(solution)/shard_map/reduce_scatter | solution.py:302
  857.4 106.1 %copy-start.5 = (bf16[256,1024]{1,0:T(8,128)(2,1)}, bf16[256,1024]{1,0:T(8,128)(2,1)S(1)}, u32[]{:S(2)}) copy-start(bf16[256,1024]{1,0:T(8,128)(2,1)S(1)} %fusion.60) | copy-start | bytes 1572868
  906.4 119.9 %copy-start.18 = (bf16[1,256,1024]{2,1,0:T(8,128)(2,1)S(1)}, bf16[1,256,1024]{2,1,0:T(8,128)(2,1)}, u32[]{:S(2)}) copy-start(bf16[1,256,1024]{2,1,0:T(8,128)(2,1)} %param.25) | copy-start | bytes 1572868
  1034.4 5.4 copy-start.12
  1034.5 5.4 copy-start.14
  1034.5 5.4 copy-start.27
  1039.9 2.4 copy-start.19
  1039.9 2.9 copy-start.3
  1087.5 27.6 %copy-start.8 = (bf16[256,16,32]{0,2,1:T(8,128)(2,1)S(1)}, bf16[256,16,32]{0,2,1:T(8,128)(2,1)}, u32[]{:S(2)}) copy-start(bf16[256,16,32]{0,2,1:T(8,128)(2,1)} %copy-done.7) | copy-start | bytes 786436
  1087.5 27.6 %copy-start.10 = (bf16[256,16,32]{0,2,1:T(8,128)(2,1)S(1)}, bf16[256,16,32]{0,2,1:T(8,128)(2,1)}, u32[]{:S(2)}) copy-start(bf16[256,16,32]{0,2,1:T(8,128)(2,1)} %copy-done.9) | copy-start | bytes 786436
  1140.6 2.2 copy-start.20
  1140.6 164.8 %reduce-scatter.17.cloned.1.call-start = ((), (), s32[]{:S(2)}) async-start(), calls=%async_computation.30 | async-start | bytes 2228224 | tf_op jit(solution)/shard_map/reduce_scatter | solution.py:352
  1142.7 253.0 %reduce-scatter.23.cloned.1.call-start = ((), (), s32[]{:S(2)}) async-start(), calls=%async_computation.33 | async-start | bytes 6127616 | tf_op jit(solution)/shard_map/reduce_scatter | solution.py:361
  1149.8 1.0 copy-start.6
  1149.8 1.5 copy-start.15
  1149.8 335.7 %reduce-scatter.21.cloned.1.call-start = ((), (), s32[]{:S(2)}) async-start(), calls=%async_computation.32 | async-start | bytes 6127616 | tf_op jit(solution)/shard_map/reduce_scatter | solution.py:358
  1155.5 1.4 copy-start.13
  1155.5 419.9 %reduce-scatter.19.cloned.1.call-start = ((), (), s32[]{:S(2)}) async-start(), calls=%async_computation.31 | async-start | bytes 6127616 | tf_op jit(solution)/shard_map/reduce_scatter | solution.py:355
  1161.1 487.5 %reduce-scatter.13.cloned.1.call-start = ((), (), s32[]{:S(2)}) async-start(), calls=%async_computation.28 | async-start | bytes 2228224 | tf_op jit(solution)/shard_map/reduce_scatter | solution.py:346
  1174.9 62.6 %copy-start.17 = (f32[256,32]{0,1:T(8,128)S(1)}, f32[256,32]{0,1:T(8,128)}, u32[]{:S(2)}) copy-start(f32[256,32]{0,1:T(8,128)} %copy-done.16) | copy-start | bytes 98308
  1174.9 62.6 %copy-start.23 = (f32[256,32]{0,1:T(8,128)S(1)}, f32[256,32]{0,1:T(8,128)}, u32[]{:S(2)}) copy-start(f32[256,32]{0,1:T(8,128)} %get-tuple-element.75) | copy-start | bytes 98308
  1234.6 565.8 %copy-start.2 = (f32[1,256,1024]{2,1,0:T(8,128)}, f32[1,256,1024]{2,1,0:T(8,128)S(1)}, u32[]{:S(2)}) copy-start(f32[1,256,1024]{2,1,0:T(8,128)S(1)} %get-tuple-element.55) | copy-start | bytes 3145732
  1234.6 5.7 copy-start.1
  1234.6 5.7 copy-start.22
  1234.6 5.7 copy-start.25
  1242.6 479.9 %reduce-scatter.11.cloned.1.call-start = ((), (), s32[]{:S(2)}) async-start(), calls=%async_computation.27 | async-start | bytes 2228224 | tf_op jit(solution)/shard_map/reduce_scatter | solution.py:343
  1245.8 550.3 %reduce-scatter.15.cloned.1.call-start = ((), (), s32[]{:S(2)}) async-start(), calls=%async_computation.29 | async-start | bytes 2228224 | tf_op jit(solution)/shard_map/reduce_scatter | solution.py:349
  1248.2 630.5 %all-reduce.13.cloned.1.call-start = ((), (), s32[]{:S(2)}) async-start(), calls=%async_computation.34 | async-start | bytes 3211264 | tf_op jit(solution)/shard_map/psum | solution.py:372
  1796.8 2.7 copy-start.4
  1796.9 3.5 copy-start.11
  1799.5 2.8 copy-start.26
Sparse Core Ops, SparseCore 0:
  10.5 50.9 all-gather.18
  63.9 47.0 all-gather.22
  113.5 47.0 all-gather.24
  162.7 51.2 all-gather.20
  216.0 58.4 all-gather.26
  276.8 49.7 all-gather.28
  329.0 60.7 all-gather.30
  392.2 60.5 all-gather.32
  455.3 60.5 all-gather.34
  525.3 46.9 all-gather.36
  574.8 47.0 all-gather.42
  624.2 47.0 all-gather.40
  673.6 51.2 all-gather.38
  726.9 58.4 all-gather.44
  787.7 49.7 all-gather.46
  839.8 60.7 all-gather.52
  902.8 60.5 all-gather.50
  965.7 60.5 all-gather.48
  1140.7 91.1 reduce-scatter.8
  1235.7 69.6 reduce-scatter.16
  1309.5 86.1 reduce-scatter.22
  1399.8 85.7 reduce-scatter.20
  1489.6 85.7 reduce-scatter.18
  1579.2 69.3 reduce-scatter.12
  1652.6 69.8 reduce-scatter.10
  1726.3 69.8 reduce-scatter.14
  1799.1 79.5 all-reduce.12
where the time goes:
time: 1900 us
  waiting for transfers between devices  1350 us (71%)
  matrix products  216 us (11%)
  other arithmetic  141 us (7%)
  blocking collectives  127 us (7%)
  local copies, waits for them, and re-layouts  50.6 us (3%)
    unnamed x3, blocking collectives  108 us
    all_gather x2, waiting for transfers between devices, body(): lax.all_gather(key_rot, 'ctx', axis=1, tiled=True)  108 us
    reduce_scatter x1, waiting for transfers between devices, body(): lax.psum_scatter(down_total.astype(jnp.bfloat16), 'fsdp', scatter_dimensi...  90.3 us
    reduce_scatter x1, waiting for transfers between devices, body(): lax.psum_scatter(gate_total.astype(jnp.bfloat16), 'fsdp', scatter_dimensi...  89.9 us
    reduce_scatter x1, waiting for transfers between devices, body(): lax.psum_scatter(upper_total.astype(jnp.bfloat16), 'fsdp', scatter_dimens...  89.9 us
    all_gather x2, waiting for transfers between devices, body(): lax.all_gather(value_mix, 'ctx', axis=1, tiled=True)  81.8 us
    sub x2, other arithmetic, attention(): raised = jnp.exp(scores - peak)  76.7 us
    reduce_scatter x1, waiting for transfers between devices, body(): lax.psum_scatter(query_total.astype(jnp.bfloat16), 'fsdp', scatter_dimens...  73.8 us
  transfers between devices with their start and end apart: 27, of which 25 were waited for; matrix products, arithmetic and copies ran while one was open for 14% of the time, Pallas kernels for 0%

commit v1 on v0

v1 whole, which is shorter than its diff:
```python
import math

import jax
import jax.numpy as jnp
from jax import lax
from jax.sharding import PartitionSpec as P

H = 16


EPS = 1e-06
MASKED = -1e30
GAIN_ROWS = 16


def rope_tables(positions, half):
    freq = jnp.exp(
        jnp.arange(half, dtype=jnp.int32).astype(jnp.float32) * (-math.log(10000.0) / half)
    )
    angle = positions.astype(jnp.float32)[:, None] * freq[None, :]
    return (jnp.cos(angle), jnp.sin(angle))


def rotate(value_rows, cosine, sine):
    half = value_rows.shape[-1] // 2
    first = value_rows[..., :half]
    second = value_rows[..., half:]
    return jnp.concatenate(
        [first * cosine - second * sine, second * cosine + first * sine], axis=-1
    )


def norm_apply(value_rows, gain):
    inverse = lax.rsqrt(jnp.mean(value_rows * value_rows, axis=-1, keepdims=True) + EPS)
    return (value_rows * inverse * gain, inverse)


def norm_back(value_rows, inverse, gain, upstream):
    scaled = upstream * gain
    gain_part = jnp.sum(upstream * value_rows * inverse, axis=(0, 1))
    inner = jnp.mean(scaled * value_rows, axis=-1, keepdims=True)
    return (inverse * scaled - value_rows * inverse * inverse * inverse * inner, gain_part)


def gain_block(first, second, width, leading=()):
    pad_cols = width - first.shape[-1] - second.shape[-1]
    row = jnp.concatenate(
        [first, second, jnp.zeros(leading + (pad_cols,), first.dtype)], axis=-1
    )
    row = row[..., None, :]
    pads = [(0, 0)] * len(leading) + [(0, GAIN_ROWS - 1), (0, 0)]
    return jnp.pad(row, pads)


def body(
    tokens,
    first_value,
    query_weight,
    key_weight,
    value_weight,
    out_weight,
    gate_weight,
    up_weight,
    down_weight,
    prenorm_gain,
    midnorm_gain,
    cotangent,
    lengths,
    assignment,
):
    slots, rows, width = tokens.shape
    head_count = H
    head_dim = width // head_count
    score_scale = head_dim ** (-0.5)
    n_fsdp = lax.axis_size("fsdp")
    n_ctx = lax.axis_size("ctx")
    total_len = rows * n_ctx
    w_rows = query_weight.shape[0]
    g_len = prenorm_gain.shape[0]
    ff = gate_weight.shape[1]
    d_rows = down_weight.shape[0]

    slot_count = assignment.shape[0]
    chosen = assignment[:, None] == jnp.arange(slot_count, dtype=jnp.int32)[None, :]
    lengths_all = jnp.sum(jnp.where(chosen, lengths[None, :], 0), axis=1)
    slot_lengths = lax.dynamic_slice_in_dim(lengths_all, lax.axis_index("fsdp") * slots, slots)
    query_places = lax.axis_index("ctx") * rows + jnp.arange(rows, dtype=jnp.int32)
    key_places = jnp.arange(total_len, dtype=jnp.int32)
    valid = query_places[None, :] < slot_lengths[:, None]
    allowed = (key_places[None, None, :] <= query_places[None, :, None]) & (
        key_places[None, None, :] < slot_lengths[:, None, None]
    )
    cosine, sine = rope_tables(query_places, head_dim // 2)
    cos_rows = cosine[None, :, None, :]
    sin_rows = sine[None, :, None, :]
    valid_wide = valid[:, :, None]

    attn_pack = jnp.concatenate(
        [query_weight, key_weight, value_weight, out_weight,
         gain_block(prenorm_gain, midnorm_gain, width)],
        axis=0,
    )
    attn_all = lax.all_gather(attn_pack, "fsdp", axis=0, tiled=False)

    def attn_part(i):
        return attn_all[:, i * w_rows:(i + 1) * w_rows, :].reshape(n_fsdp * w_rows, width)

    query_mat, key_mat, value_mat, out_mat = (attn_part(i) for i in range(4))
    prenorm_full = attn_all[:, 4 * w_rows, 0:g_len].reshape(n_fsdp * g_len)
    midnorm_full = attn_all[:, 4 * w_rows, g_len:2 * g_len].reshape(n_fsdp * g_len)

    mlp_pack = jnp.concatenate(
        [gate_weight, up_weight, down_weight.reshape(w_rows, ff)], axis=1
    )
    mlp_all = lax.all_gather(mlp_pack, "fsdp", axis=0, tiled=False)
    gate_mat = mlp_all[:, :, 0:ff].reshape(n_fsdp * w_rows, ff)
    upper_mat = mlp_all[:, :, ff:2 * ff].reshape(n_fsdp * w_rows, ff)
    down_mat = mlp_all[:, :, 2 * ff:].reshape(n_fsdp, d_rows, width).reshape(n_fsdp * d_rows, width)

    tokens_wide = tokens.astype(jnp.float32)
    first_wide = first_value.astype(jnp.float32)
    normed, inverse = norm_apply(tokens_wide, prenorm_full.astype(jnp.float32))
    normed_low = normed.astype(jnp.bfloat16)
    query = jnp.dot(normed_low, query_mat, preferred_element_type=jnp.float32)
    keyed = jnp.dot(normed_low, key_mat, preferred_element_type=jnp.float32)
    own_value = jnp.dot(normed_low, value_mat, preferred_element_type=jnp.float32)
    heads_shape = query.shape[:2] + (head_count, head_dim)
    query_rotated_rows = rotate(query.reshape(heads_shape), cos_rows, sin_rows).astype(jnp.bfloat16)
    key_rot = (
        rotate(keyed.reshape(heads_shape), cos_rows, sin_rows)
        .astype(jnp.bfloat16)
        .reshape(query.shape)
    )
    value_mix = (0.5 * own_value + 0.5 * first_wide).astype(jnp.bfloat16)

    kv_all = lax.all_gather(
        jnp.concatenate([key_rot, value_mix], axis=-1), "ctx", axis=1, tiled=True
    )
    key_rows_per_head = kv_all[..., :width].reshape(slots, total_len, head_count, head_dim)
    value_rows_per_head = kv_all[..., width:].reshape(slots, total_len, head_count, head_dim)

    scores = (
        jnp.einsum(
            "biuv,bfuv->buif",
            query_rotated_rows,
            key_rows_per_head,
            preferred_element_type=jnp.float32,
        )
        * score_scale
    )
    scores = jnp.where(allowed[:, None], scores, MASKED)
    peak = jnp.max(scores, axis=-1, keepdims=True)
    raised = jnp.exp(scores - peak)
    denominator = jnp.sum(raised, axis=-1, keepdims=True)
    shares = raised / denominator
    attention_share_narrow = shares.astype(jnp.bfloat16)
    mixed = jnp.einsum(
        "ytjo,yotv->yjtv",
        attention_share_narrow,
        value_rows_per_head,
        preferred_element_type=jnp.float32,
    )
    mixed_low = mixed.astype(jnp.bfloat16).reshape(slots, rows, width)

    middle = tokens_wide + jnp.dot(mixed_low, out_mat, preferred_element_type=jnp.float32)
    normed_two, inverse_two = norm_apply(middle, midnorm_full.astype(jnp.float32))
    normed_two = normed_two.astype(jnp.bfloat16)
    gate = jnp.dot(normed_two, gate_mat, preferred_element_type=jnp.float32)
    upper = jnp.dot(normed_two, upper_mat, preferred_element_type=jnp.float32)
    hidden = (jax.nn.silu(gate) * upper).astype(jnp.bfloat16)
    branch = jnp.dot(hidden, down_mat, preferred_element_type=jnp.float32)
    layer_out = jnp.where(valid_wide, middle + branch, 0.0).astype(jnp.bfloat16)

    cot_wide = jnp.where(valid_wide, cotangent.astype(jnp.float32), 0.0)
    cot_low = cot_wide.astype(jnp.bfloat16)
    down_total = jnp.einsum("srf,sre->fe", hidden, cot_low, preferred_element_type=jnp.float32)
    hidden_back = jnp.einsum("sre,fe->srf", cot_low, down_mat, preferred_element_type=jnp.float32)
    sigma = jax.nn.sigmoid(gate)
    gate_back = (hidden_back * upper * sigma * (1.0 + gate * (1.0 - sigma))).astype(jnp.bfloat16)
    upper_back = (hidden_back * gate * sigma).astype(jnp.bfloat16)
    gate_total = jnp.einsum(
        "srd,srf->df", normed_two, gate_back, preferred_element_type=jnp.float32
    )
    upper_total = jnp.einsum(
        "srd,srf->df", normed_two, upper_back, preferred_element_type=jnp.float32
    )
    normed_two_back = jnp.einsum(
        "srf,df->srd", gate_back, gate_mat, preferred_element_type=jnp.float32
    )
    normed_two_back = normed_two_back + jnp.einsum(
        "srf,df->srd", upper_back, upper_mat, preferred_element_type=jnp.float32
    )
    middle_norm_back, midnorm_total = norm_back(
        middle, inverse_two, midnorm_full.astype(jnp.float32), normed_two_back
    )
    middle_back = cot_wide + middle_norm_back
    middle_low = middle_back.astype(jnp.bfloat16)
    out_total = jnp.einsum("srd,sre->de", mixed_low, middle_low, preferred_element_type=jnp.float32)

    mlp_grads = jnp.concatenate(
        [
            gate_total.reshape(n_fsdp, w_rows, ff),
            upper_total.reshape(n_fsdp, w_rows, ff),
            down_total.reshape(n_fsdp, d_rows, width).reshape(n_fsdp, w_rows, ff),
            out_total.reshape(n_fsdp, w_rows, width),
        ],
        axis=2,
    ).astype(jnp.bfloat16)
    mlp_share = lax.psum_scatter(mlp_grads, "fsdp", scatter_dimension=0, tiled=False)

    blended_value_gradient = jnp.einsum(
        "sre,de->srd", middle_low, out_mat, preferred_element_type=jnp.float32
    ).astype(jnp.bfloat16)
    blended_value_gradient = blended_value_gradient.reshape(slots, rows, head_count, head_dim)
    prob_back = jnp.einsum(
        "biuv,bfuv->buif",
        blended_value_gradient,
        value_rows_per_head,
        preferred_element_type=jnp.float32,
    )
    inner = jnp.sum(shares * prob_back, axis=-1, keepdims=True)
    score_gradient = (shares * (prob_back - inner)).astype(jnp.bfloat16)
    query_rot_back = (
        jnp.einsum(
            "ytjo,yotv->yjtv", score_gradient, key_rows_per_head, preferred_element_type=jnp.float32
        )
        * score_scale
    )
    key_part = (
        jnp.einsum(
            "xtfk,xfty->kxty",
            score_gradient,
            query_rotated_rows,
            preferred_element_type=jnp.float32,
        )
        * score_scale
    )
    value_part = jnp.einsum(
        "xtfk,xfty->kxty",
        attention_share_narrow,
        blended_value_gradient,
        preferred_element_type=jnp.float32,
    )
    key_value = lax.psum_scatter(
        jnp.concatenate(
            [key_part.reshape(total_len, slots, width), value_part.reshape(total_len, slots, width)],
            axis=-1,
        ).astype(jnp.bfloat16),
        "ctx",
        scatter_dimension=0,
        tiled=True,
    ).astype(jnp.float32)
    key_value = jnp.swapaxes(key_value, 0, 1)
    key_rot_back = key_value[..., :width].reshape(slots, rows, head_count, head_dim)
    value_mix_back = key_value[..., width:]
    first_grad = 0.5 * value_mix_back
    query_back = (
        rotate(query_rot_back, cos_rows, -sin_rows).reshape(slots, rows, width).astype(jnp.bfloat16)
    )
    key_back = (
        rotate(key_rot_back, cos_rows, -sin_rows).reshape(slots, rows, width).astype(jnp.bfloat16)
    )
    value_back = (0.5 * value_mix_back).astype(jnp.bfloat16)
    query_total = jnp.einsum(
        "srd,sre->de", normed_low, query_back, preferred_element_type=jnp.float32
    )
    key_total = jnp.einsum("srd,sre->de", normed_low, key_back, preferred_element_type=jnp.float32)
    value_total = jnp.einsum(
        "srd,sre->de", normed_low, value_back, preferred_element_type=jnp.float32
    )
    normed_back = jnp.einsum(
        "sre,de->srd", query_back, query_mat, preferred_element_type=jnp.float32
    )
    normed_back = normed_back + jnp.einsum(
        "sre,de->srd", key_back, key_mat, preferred_element_type=jnp.float32
    )
    normed_back = normed_back + jnp.einsum(
        "sre,de->srd", value_back, value_mat, preferred_element_type=jnp.float32
    )
    tokens_norm_back, prenorm_total = norm_back(
        tokens_wide, inverse, prenorm_full.astype(jnp.float32), normed_back
    )
    tokens_grad = middle_back + tokens_norm_back

    attn_grads = jnp.concatenate(
        [
            query_total.reshape(n_fsdp, w_rows, width),
            key_total.reshape(n_fsdp, w_rows, width),
            value_total.reshape(n_fsdp, w_rows, width),
            gain_block(
                prenorm_total.reshape(n_fsdp, g_len),
                midnorm_total.reshape(n_fsdp, g_len),
                width,
                leading=(n_fsdp,),
            ),
        ],
        axis=1,
    ).astype(jnp.bfloat16)
    attn_share = lax.psum_scatter(attn_grads, "fsdp", scatter_dimension=0, tiled=False)

    attn_share, mlp_share = lax.psum((attn_share, mlp_share), "ctx")
    attn_share = attn_share.astype(jnp.float32)
    mlp_share = mlp_share.astype(jnp.float32)

    def attn_grad(i):
        return attn_share[i * w_rows:(i + 1) * w_rows]

    query_grad, key_grad, value_grad = (attn_grad(i) for i in range(3))
    prenorm_grad = attn_share[3 * w_rows, 0:g_len]
    midnorm_grad = attn_share[3 * w_rows, g_len:2 * g_len]
    gate_grad = mlp_share[:, 0:ff]
    up_grad = mlp_share[:, ff:2 * ff]
    down_grad = mlp_share[:, 2 * ff:3 * ff].reshape(d_rows, width)
    out_grad = mlp_share[:, 3 * ff:]
    return (
        layer_out,
        tokens_grad,
        first_grad,
        query_grad,
        key_grad,
        value_grad,
        out_grad,
        gate_grad,
        up_grad,
        down_grad,
        prenorm_grad,
        midnorm_grad,
    )


def solution(mesh):
    placed = (
        P("fsdp", "ctx", None),
        P("fsdp", "ctx", None),
        P("fsdp", None),
        P("fsdp", None),
        P("fsdp", None),
        P("fsdp", None),
        P("fsdp", None),
        P("fsdp", None),
        P("fsdp", None),
        P("fsdp"),
        P("fsdp"),
        P("fsdp", "ctx", None),
        P(),
        P(),
    )
    return jax.shard_map(
        body,
        mesh=mesh,
        in_specs=placed,
        out_specs=(
            P("fsdp", "ctx", None),
            P("fsdp", "ctx", None),
            P("fsdp", "ctx", None),
            P("fsdp", None),
            P("fsdp", None),
            P("fsdp", None),
            P("fsdp", None),
            P("fsdp", None),
            P("fsdp", None),
            P("fsdp", None),
            P("fsdp"),
            P("fsdp"),
        ),
        check_vma=False,
    )
```

time: 1900 us -> 930 us (0.49)
  waiting for transfers between devices: 1350 us -> 541 us
  blocking collectives: 127 us -> 0 us
  matrix products: 216 us -> 152 us
  local copies, waits for them, and re-layouts: 50.6 us -> 104 us
  other arithmetic: 141 us -> 111 us
    all_gather x18 -> x3, waiting for transfers between devices: 713 us -> 182 us  [the longest x1 84.4 us: body(): lax.all_gather(jnp.concatenate([key_rot, value_mix], axis=-1), 'ctx', axi...]
    reduce_scatter x8 -> x3, waiting for transfers between devices: 605 us -> 285 us  [the longest x1 165 us: body(): lax.psum_scatter(mlp_grads, 'fsdp', scatter_dimension=0, tiled=False)]
    unnamed x3 -> x0, blocking collectives: 108 us -> none
    psum x1, waiting for transfers between devices: 19.9 us -> 73.4 us  [body(): attn_share, mlp_share = lax.psum((attn_share, mlp_share), 'ctx')]
    dot_general x16 -> x9, matrix products: 107 us -> 55.9 us  [the longest x1 15.9 us: body(): jnp.einsum('ytjo,yotv->yjtv', attention_share_narrow, value_rows_per_head...]
    slice x0 -> x8, local copies, waits for them, and re-layouts: none -> 41.6 us  [the longest x2 13 us: body(): kv_all[..., :width].reshape(slots, total_len, head_count, head_dim)]
    sub x3 -> x1, other arithmetic: 78.6 us -> 38.3 us  [body(): raised = jnp.exp(scores - peak)]
    another operation x0 -> x2, local copies, waits for them, and re-layouts: none -> 24.2 us  [the longest x1 12.1 us: body(): down_total.reshape(n_fsdp, d_rows, width).reshape(n_fsdp, w_rows, ff)]
  transfers between devices with their start and end apart: 27 -> 7, of which waited for: 25 -> 7; matrix products, arithmetic and copies ran while one was open for 14% -> 18% of each run, Pallas kernels for 0% -> 0%
where the time goes in v1:
time: 930 us; the launch traced here: 924 us
  waiting for transfers between devices  541 us (58%)
  matrix products  152 us (16%)
  other arithmetic  111 us (12%)
  local copies, waits for them, and re-layouts  104 us (11%)
  between operations  15.1 us (2%)
    reduce_scatter x1, waiting for transfers between devices, body(): lax.psum_scatter(mlp_grads, 'fsdp', scatter_dimension=0, tiled=False)  165 us
    all_gather x1, waiting for transfers between devices, body(): lax.all_gather(jnp.concatenate([key_rot, value_mix], axis=-1), 'ctx', axi...  84.4 us
    reduce_scatter x1, waiting for transfers between devices, body(): lax.psum_scatter(jnp.concatenate([key_part.reshape(total_len, slots, widt...  76.3 us
    all_gather x1, waiting for transfers between devices, body(): attn_all = lax.all_gather(attn_pack, 'fsdp', axis=0, tiled=False)  75.5 us
    psum x1, waiting for transfers between devices, body(): attn_share, mlp_share = lax.psum((attn_share, mlp_share), 'ctx')  73.4 us
    reduce_scatter x1, waiting for transfers between devices, body(): lax.psum_scatter(attn_grads, 'fsdp', scatter_dimension=0, tiled=False)  43.7 us
    sub x1, other arithmetic, body(): raised = jnp.exp(scores - peak)  38.3 us
    convert_element_type x1, other arithmetic, body(): score_gradient = (shares * (prob_back - inner)).astype(jnp.bfloat16)  27.7 us
  transfers between devices with their start and end apart: 7, of which 7 were waited for; matrix products, arithmetic and copies ran while one was open for 18% of the time, Pallas kernels for 0%

profile of v1, /device:TPU:0, one launch (start us, length us, event | category | flops | bytes accessed | tf_op | source)
XLA Modules:
  0.0 923.7 jit_solution(8580043544185926141)
XLA Ops:
  7.2 1.2 fusion.85
  9.4 0.9 constant_dynamic-update-slice_fusion.2
  13.1 1.2 fusion.34
  15.1 75.5 %all-gather.8.cloned.1.call-done = bf16[4352,1024]{1,0:T(8,128)(2,1)} async-done(((bf16[272,1024]{1,0:T(8,128)(2,1)}), bf16[4352,1024]{1,0:T(8,128)(2,1)}) %all-gather.8.cloned.1.call-update) | async-done | bytes 8912912 | tf_op jit(solution)/shard_map/all_gather | solution.py:103
  90.6 1.0 fusion.66
  91.6 5.8 fusion.81
  97.5 4.0 copy.59
  101.5 3.9 copy.62
  105.4 2.4 convolution_bitcast_fusion.3
  107.9 2.4 convolution_bitcast_fusion.1
  111.5 2.1 copy.60
  113.6 2.5 fusion.22
  116.2 1.1 pad_maximum_fusion.3
  117.8 2.2 pad_maximum_fusion.2
  122.6 84.4 %all-gather.6.cloned.1.call-done = bf16[1,2048,2048]{2,1,0:T(8,128)(2,1)} async-done(((bf16[1,256,2048]{2,1,0:T(8,128)(2,1)}), bf16[1,2048,2048]{2,1,0:T(8,128)(2,1)}) %all-gather.6.cloned.1.call-update) | async-done | bytes 8388624 | tf_op jit(solution)/shard_map/all_gather | solution.py:136
  207.0 6.4 fusion.82
  213.4 6.6 copy.63
  220.0 6.7 copy.61
  226.6 15.6 %fusion.55 = f32[16,256,2048]{2,1,0:T(8,128)} fusion(bf16[2048,16,64]{0,2,1:T(8,128)(2,1)} %bitcast.190, bf16[256,16,32]{0,2,1:T(8,128)(2,1)S(1)} %get-tuple-element.42, bf16[256,16,32]{0,2,1:T(8,128)(2,1)S(1)} %get-tuple-element.41), kind=kOutput, calls=%fused_computation.109 | convolution fusion | flops 1074790400 | bytes 38273024 | tf_op jit(solution)/shard_map/biuv,bfuv->buif/dot_general | solution.py:143
  242.2 38.3 %fusion.86 = (f32[16,256]{1,0:T(8,128)S(1)}, f32[16,256,2048]{2,1,0:T(8,128)}) fusion(f32[16,256,2048]{2,1,0:T(8,128)} %fusion.55, pred[256,2048]{1,0:T(8,128)(4,1)S(1)} %fusion.14), kind=kOutput, calls=%fused_computation.157 | output fusion | flops 50333696 | bytes 67649536 | tf_op jit(solution)/shard_map/sub | solution.py:153
  280.5 15.9 %fusion.24 = bf16[16,64,256]{2,1,0:T(8,128)(2,1)} fusion(bf16[2048,16,64]{0,2,1:T(8,128)(2,1)} %bitcast.224, f32[16,256,2048]{2,1,0:T(8,128)} %get-tuple-element.61, f32[16,256]{1,0:T(8,128)S(1)} %get-tuple-element.60), kind=kOutput, calls=%fused_computation.57 | convolution fusion | flops 1090781184 | bytes 38289408 | tf_op jit(solution)/shard_map/ytjo,yotv->yjtv/dot_general | solution.py:157
  296.4 2.0 multiply_reduce_fusion.1
  298.4 22.5 %all-gather.10.cloned.1.call-done = bf16[1024,8448]{1,0:T(8,128)(2,1)} async-done(((bf16[64,8448]{1,0:T(8,128)(2,1)}), bf16[1024,8448]{1,0:T(8,128)(2,1)}) %all-gather.10.cloned.1.call-update) | async-done | bytes 17301520 | tf_op jit(solution)/shard_map/all_gather | solution.py:115
  321.0 11.3 %fusion.80 = (bf16[16,64,2816]{2,1,0:T(8,128)(2,1)}, bf16[16,64,2816]{2,1,0:T(8,128)(2,1)}, bf16[16,64,2816]{2,1,0:T(8,128)(2,1)}) fusion(bf16[16,64,8448]{2,1,0:T(8,128)(2,1)} %bitcast.201), kind=kLoop, calls=%fused_computation.151 | loop fusion | bytes 34603008 | tf_op jit(solution)/shard_map/slice | solution.py:118
  332.2 12.1 %reshape_reshape.7 = bf16[2816,1024]{1,0:T(8,128)(2,1)} reshape(bf16[16,64,2816]{2,1,0:T(8,128)(2,1)} %get-tuple-element.20) | data formatting | bytes 11534336 | tf_op jit(solution)/shard_map/reshape;reshape | solution.py:118
  344.4 6.1 fusion.48
  350.5 3.3 fusion.50
  353.8 7.5 multiply_convert_fusion.2
  361.3 1.7 fusion.87
  363.0 1.8 fusion.39
  365.4 1.0 copy-done.2
  367.3 14.3 %fusion.11 = bf16[16,64,2048]{2,1,0:T(8,128)(2,1)} fusion(bf16[256,16,64]{0,2,1:T(8,128)(2,1)S(1)} %bitcast.232, f32[16,256,2048]{2,1,0:T(8,128)} %get-tuple-element.61, f32[16,256]{1,0:T(8,128)S(1)} %get-tuple-element.60), kind=kOutput, calls=%fused_computation.23 | convolution fusion | flops 1092616192 | bytes 38289408 | tf_op jit(solution)/shard_map/xtfk,xfty->kxty/dot_general | solution.py:238
  381.7 22.7 %multiply_reduce_fusion = (f32[16,256]{1,0:T(8,128)S(1)}, f32[16,256,2048]{2,1,0:T(8,128)}) fusion(f32[16,256,2048]{2,1,0:T(8,128)} %get-tuple-element.61, f32[16,256]{1,0:T(8,128)S(1)} %get-tuple-element.60, bf16[256,16,64]{0,2,1:T(8,128)(2,1)S(1)} %bitcast.233, bf16[2048,16,64]{0,2,1:T(8,128)(2,1)} %bitcast.225), kind=kOutput, calls=%fused_computation.2 | convolution fusion | flops 1098903552 | bytes 71860224 | tf_op jit(solution)/shard_map/biuv,bfuv->buif/dot_general | solution.py:215
  404.4 6.4 copy.66
  410.8 27.7 %multiply_convert_fusion = bf16[16,256,2048]{2,1,0:T(8,128)(2,1)} fusion(f32[16,256,2048]{2,1,0:T(8,128)} %get-tuple-element.66, f32[16,256]{1,0:T(8,128)S(1)} %get-tuple-element.65, f32[16,256,2048]{2,1,0:T(8,128)} %get-tuple-element.61, f32[16,256]{1,0:T(8,128)S(1)} %get-tuple-element.60), kind=kLoop, calls=%fused_computation.1 | loop fusion | flops 33554432 | bytes 83918848 | tf_op jit(solution)/shard_map/convert_element_type | solution.py:222
  438.5 10.8 %multiply_convert_fusion.1 = bf16[16,64,2048]{2,1,0:T(8,128)(2,1)} fusion(bf16[16,256,2048]{2,1,0:T(8,128)(2,1)} %multiply_convert_fusion, bf16[256,16,32]{0,2,1:T(8,128)(2,1)S(1)} %copy-done.24, bf16[256,16,32]{0,2,1:T(8,128)(2,1)S(1)} %copy-done.22), kind=kOutput, calls=%fused_computation.14 | convolution fusion | flops 1078984704 | bytes 21495808 | tf_op jit(solution)/shard_map/xtfk,xfty->kxty/dot_general | solution.py:230
  449.3 6.4 copy.65
  455.8 8.2 pad_maximum_fusion.1
  464.2 13.9 %fusion.17 = f32[1,256,16,64]{1,3,2,0:T(8,128)} fusion(bf16[2048,16,64]{0,2,1:T(8,128)(2,1)} %bitcast.191, bf16[16,256,2048]{2,1,0:T(8,128)(2,1)} %multiply_convert_fusion), kind=kOutput, calls=%fused_computation.46 | convolution fusion | flops 1074003968 | bytes 22020096 | tf_op jit(solution)/shard_map/ytjo,yotv->yjtv/dot_general | solution.py:224
  478.1 76.3 %reduce-scatter.4.cloned.1.call-done = bf16[256,1,2048]{2,0,1:T(8,128)(2,1)} async-done(((bf16[2048,1,2048]{2,0,1:T(8,128)(2,1)}), bf16[256,1,2048]{2,0,1:T(8,128)(2,1)}) %reduce-scatter.4.cloned.1.call-update) | async-done | bytes 1048592 | tf_op jit(solution)/shard_map/reduce_scatter | solution.py:244
  554.4 1.5 bitcast_convert_fusion
  555.9 1.3 slice_multiply_fusion
  557.1 3.0 copy.67
  560.1 2.0 subtract_convert_fusion
  565.0 1.0 copy-done.6
  569.1 3.4 fusion.10
  573.7 0.9 fusion.126
  574.7 1.2 copy.72
  576.0 5.4 convolution_convert_fusion
  581.4 12.1 %reshape_reshape.8 = bf16[16,64,2816]{2,1,0:T(8,128)(2,1)} reshape(bf16[2816,1024]{1,0:T(8,128)(2,1)} %convolution_convert_fusion) | data formatting | bytes 11534336 | tf_op jit(solution)/shard_map/reshape;reshape | solution.py:204
  593.5 3.2 convolution_convert_fusion.3
  596.8 4.2 convolution_convert_fusion.1
  601.0 5.4 convolution_convert_fusion.2
  606.4 13.3 %pad_maximum_fusion = bf16[16,64,9472]{2,1,0:T(8,128)(2,1)} fusion(bf16[16,64,1024]{2,1,0:T(8,128)(2,1)} %convolution_convert_fusion.3, bf16[16,64,2816]{2,1,0:T(8,128)(2,1)S(1)} %bitcast.194, bf16[16,64,2816]{2,1,0:T(8,128)(2,1)} %convolution_convert_fusion.1, bf16[16,64,2816]{2,1,0:T(8,128)(2,1)} %convolution_convert_fusion.2), kind=kLoop, calls=%fused_computation.6 | loop fusion | flops 77594624 | bytes 38797312 | tf_op jit(solution)/shard_map/concatenate | solution.py:200
  619.7 43.7 %reduce-scatter.6.cloned.1.call-done = bf16[1,208,1024]{2,1,0:T(8,128)(2,1)} async-done(((bf16[16,208,1024]{2,1,0:T(8,128)(2,1)}), bf16[1,208,1024]{2,1,0:T(8,128)(2,1)}) %reduce-scatter.6.cloned.1.call-update) | async-done | bytes 426000 | tf_op jit(solution)/shard_map/reduce_scatter | solution.py:299
  663.4 165.2 %reduce-scatter.8.cloned.1.call-done = bf16[1,64,9472]{2,1,0:T(8,128)(2,1)} async-done(((bf16[16,64,9472]{2,1,0:T(8,128)(2,1)}), bf16[1,64,9472]{2,1,0:T(8,128)(2,1)}) %reduce-scatter.8.cloned.1.call-update) | async-done | bytes 1212432 | tf_op jit(solution)/shard_map/reduce_scatter | solution.py:209
  828.6 5.7 fusion.23
  834.2 1.3 fusion.33
  835.6 73.4 %all-reduce.5.cloned.1.call-done = (bf16[208,1024]{1,0:T(8,128)(2,1)}, bf16[64,9472]{1,0:T(8,128)(2,1)}) async-done(((bf16[208,1024]{1,0:T(8,128)(2,1)}, bf16[64,9472]{1,0:T(8,128)(2,1)}), (bf16[208,1024]{1,0:T(8,128)(2,1)}, bf16[64,9472]{1,0:T(8,128)(2,1)})) %all-reduce.5.cloned.1.call-update) | async-done | bytes 1638416 | tf_op jit(solution)/shard_map/psum | solution.py:301
  909.0 2.0 fusion.84
  911.0 1.1 convert_element_type.215
  912.1 1.6 slice.144
  913.7 1.3 fusion.83
  915.6 1.1 reshape.649
  (166 shorter events, 18.3 us)
Async XLA Ops:
  7.2 83.5 %all-gather.8.cloned.1.call-start = ((), (), s32[]{:S(2)}) async-start(), calls=%async_computation.7 | async-start | bytes 9469952 | tf_op jit(solution)/shard_map/all_gather | solution.py:103
  12.2 0.8 copy-start.31
  13.0 194.0 %all-gather.6.cloned.1.call-start = ((), (), s32[]{:S(2)}) async-start(), calls=%async_computation.3 | async-start | bytes 9437184 | tf_op jit(solution)/shard_map/all_gather | solution.py:136
  14.3 99.3 %copy-start.40 = (f32[256]{0:T(256)}, f32[256]{0:T(256)S(1)}, u32[]{:S(2)}) copy-start(f32[256]{0:T(256)S(1)} %add_rsqrt_fusion.1) | copy-start | bytes 3076
  15.1 95.1 %copy-start.33 = (f32[256,32]{0,1:T(8,128)}, f32[256,32]{0,1:T(8,128)S(1)}, u32[]{:S(2)}) copy-start(f32[256,32]{0,1:T(8,128)S(1)} %get-tuple-element.59) | copy-start | bytes 98308
  97.5 16.1 %copy-start.36 = (f32[1024]{0:T(1024)}, f32[1024]{0:T(1024)S(1)}, u32[]{:S(2)}) copy-start(f32[1024]{0:T(1024)S(1)} %reshape.650) | copy-start | bytes 12292
  97.5 7.9 copy-start.9
  110.6 116.0 %copy-start.21 = (bf16[256,16,32]{0,2,1:T(8,128)(2,1)}, bf16[256,16,32]{0,2,1:T(8,128)(2,1)S(1)}, u32[]{:S(2)}) copy-start(bf16[256,16,32]{0,2,1:T(8,128)(2,1)S(1)} %get-tuple-element.41) | copy-start | bytes 786436
  110.6 116.0 %copy-start.23 = (bf16[256,16,32]{0,2,1:T(8,128)(2,1)}, bf16[256,16,32]{0,2,1:T(8,128)(2,1)S(1)}, u32[]{:S(2)}) copy-start(bf16[256,16,32]{0,2,1:T(8,128)(2,1)S(1)} %get-tuple-element.42) | copy-start | bytes 786436
  111.5 5.8 copy-start.32
  113.6 2.5 copy-start.26
  116.2 3.9 copy-start.47
  116.2 3.9 copy-start.48
  117.3 203.7 %all-gather.10.cloned.1.call-start = ((), (), s32[]{:S(2)}) async-start(), calls=%async_computation.8 | async-start | bytes 18382848 | tf_op jit(solution)/shard_map/all_gather | solution.py:115
  120.0 434.4 %reduce-scatter.4.cloned.1.call-start = ((), (), s32[]{:S(2)}) async-start(), calls=%async_computation.4 | async-start | bytes 9437184 | tf_op jit(solution)/shard_map/reduce_scatter | solution.py:244
  121.5 243.4 %copy-start.45 = (pred[256]{0:T(512)(128)(4,1)}, pred[256]{0:T(512)(128)(4,1)S(1)}, u32[]{:S(2)}) copy-start(pred[256]{0:T(512)(128)(4,1)S(1)} %fusion.69) | copy-start | bytes 772
  122.6 242.3 %copy-start.38 = (f32[1024]{0:T(1024)}, f32[1024]{0:T(1024)S(1)}, u32[]{:S(2)}) copy-start(f32[1024]{0:T(1024)S(1)} %reshape.651) | copy-start | bytes 12292
  298.4 66.5 %copy-start.4 = (f32[1,256,1024]{2,1,0:T(8,128)}, f32[1,256,1024]{2,1,0:T(8,128)S(1)}, u32[]{:S(2)}) copy-start(f32[1,256,1024]{2,1,0:T(8,128)S(1)} %get-tuple-element.63) | copy-start | bytes 3145732
  298.4 66.5 %copy-start.42 = (f32[256]{0:T(256)}, f32[256]{0:T(256)S(1)}, u32[]{:S(2)}) copy-start(f32[256]{0:T(256)S(1)} %add_rsqrt_fusion) | copy-start | bytes 3076
  344.3 6.1 copy-start.13
  344.3 9.4 %slice-start.2 = ((s8[5767168]{0:T(1024)(128)(4,1)}), s8[4194304]{0:T(1024)(128)(4,1)S(1)}, s32[]{:S(2)}) async-start(s8[5767168]{0:T(1024)(128)(4,1)} %bitcast.209), calls=%async_computation.12 | async-start | bytes 8388608
  350.5 3.3 slice-start.3
  350.5 3.3 copy-start.25
  350.5 12.5 %slice-start.4 = ((s8[5767168]{0:T(1024)(128)(4,1)}), s8[4194304]{0:T(1024)(128)(4,1)S(1)}, s32[]{:S(2)}) async-start(s8[5767168]{0:T(1024)(128)(4,1)} %bitcast.212), calls=%async_computation.14 | async-start | bytes 8388608
  353.8 9.2 slice-start.5
  361.3 1.7 copy-start.27
  361.3 1.7 copy-start.29
  365.3 1.0 copy-start.2
  410.8 27.7 %copy-start.22 = (bf16[256,16,32]{0,2,1:T(8,128)(2,1)S(1)}, bf16[256,16,32]{0,2,1:T(8,128)(2,1)}, u32[]{:S(2)}) copy-start(bf16[256,16,32]{0,2,1:T(8,128)(2,1)} %copy-done.21) | copy-start | bytes 786436
  410.8 27.7 %copy-start.24 = (bf16[256,16,32]{0,2,1:T(8,128)(2,1)S(1)}, bf16[256,16,32]{0,2,1:T(8,128)(2,1)}, u32[]{:S(2)}) copy-start(bf16[256,16,32]{0,2,1:T(8,128)(2,1)} %copy-done.23) | copy-start | bytes 786436
  464.0 199.3 %reduce-scatter.6.cloned.1.call-start = ((), (), s32[]{:S(2)}) async-start(), calls=%async_computation.5 | async-start | bytes 7241728 | tf_op jit(solution)/shard_map/reduce_scatter | solution.py:299
  478.1 82.0 %copy-start.34 = (f32[256,32]{0,1:T(8,128)S(1)}, f32[256,32]{0,1:T(8,128)}, u32[]{:S(2)}) copy-start(f32[256,32]{0,1:T(8,128)} %copy-done.33) | copy-start | bytes 98308
  478.1 82.0 %copy-start.35 = (f32[256,32]{0,1:T(8,128)S(1)}, f32[256,32]{0,1:T(8,128)}, u32[]{:S(2)}) copy-start(f32[256,32]{0,1:T(8,128)} %get-tuple-element.57) | copy-start | bytes 98308
  557.1 9.8 %copy-start.8 = (f32[1,256,1024]{2,1,0:T(8,128)}, f32[1,256,1024]{2,1,0:T(8,128)S(1)}, u32[]{:S(2)}) copy-start(f32[1,256,1024]{2,1,0:T(8,128)S(1)} %get-tuple-element.32) | copy-start | bytes 3145732
  557.1 5.1 copy-start.1
  560.1 3.0 copy-start
  562.2 1.7 copy-start.15
  562.2 0.8 copy-start.17
  562.3 1.9 copy-start.12
  563.1 2.9 copy-start.10
  563.1 2.9 copy-start.37
  563.1 2.9 copy-start.41
  563.9 2.6 copy-start.44
  565.0 1.0 copy-start.6
  566.0 1.7 copy-start.16
  566.4 1.9 copy-start.18
  572.5 1.2 copy-start.5
  572.5 1.2 copy-start.39
  572.5 1.2 copy-start.43
  572.5 3.4 copy-start.20
  572.5 3.4 copy-start.46
  572.6 256.0 %reduce-scatter.8.cloned.1.call-start = ((), (), s32[]{:S(2)}) async-start(), calls=%async_computation.6 | async-start | bytes 20611072 | tf_op jit(solution)/shard_map/reduce_scatter | solution.py:209
  575.9 20.8 %copy-start.19 = (bf16[1024,256]{1,0:T(8,128)(2,1)}, bf16[1024,256]{1,0:T(8,128)(2,1)S(1)}, u32[]{:S(2)}) copy-start(bf16[1024,256]{1,0:T(8,128)(2,1)S(1)} %copy.72) | copy-start | bytes 1572868
  581.4 12.1 %copy-start.3 = (f32[1,256,1024]{2,1,0:T(8,128)S(1)}, f32[1,256,1024]{2,1,0:T(8,128)}, u32[]{:S(2)}) copy-start(f32[1,256,1024]{2,1,0:T(8,128)} %copy-done.2) | copy-start | bytes 3145732
  593.5 3.2 copy-start.30
  596.8 4.2 copy-start.28
  596.8 9.6 %slice-start = ((s8[5767168]{0:T(1024)(128)(4,1)}), s8[4194304]{0:T(1024)(128)(4,1)S(1)}, s32[]{:S(2)}) async-start(s8[5767168]{0:T(1024)(128)(4,1)} %bitcast.193), calls=%async_computation.10 | async-start | bytes 8388608
  601.0 5.4 slice-start.1
  619.6 289.3 %all-reduce.5.cloned.1.call-start = ((), (), s32[]{:S(2)}) async-start(), calls=%async_computation.9 | async-start | bytes 3276800 | tf_op jit(solution)/shard_map/psum | solution.py:301
  828.5 5.7 copy-start.7
  828.6 5.7 copy-start.11
  909.0 4.7 copy-start.14
Sparse Core Ops, SparseCore 0:
  13.1 77.4 all-gather.7
  117.4 89.5 all-gather.5
  209.4 111.4 all-gather.9
  464.1 90.2 reduce-scatter.3
  572.7 90.6 reduce-scatter.5
  668.3 160.1 reduce-scatter.7
  831.3 77.6 all-reduce.4

commit v2 on v1

--- a/solution.py
+++ b/solution.py
@@ -1,8 +1,11 @@
+import functools
 import math
 
 import jax
 import jax.numpy as jnp
 from jax import lax
+from jax.experimental import pallas as pl
+from jax.experimental.pallas import tpu as pltpu
 from jax.sharding import PartitionSpec as P
 
 H = 16
@@ -11,6 +14,124 @@
 EPS = 1e-06
 MASKED = -1e30
 GAIN_ROWS = 16
+
+
+HEAD_BLOCK = 128
+NT_DIMS = (((1,), (1,)), ((), ()))
+TN_DIMS = (((0,), (0,)), ((), ()))
+
+
+def attention_shares(query, keys, first_row, slot_len, scale):
+    scores = lax.dot_general(query, keys, NT_DIMS, preferred_element_type=jnp.float32) * scale
+    shape = scores.shape
+    query_pos = first_row + lax.broadcasted_iota(jnp.int32, shape, 0)
+    key_pos = lax.broadcasted_iota(jnp.int32, shape, 1)
+    allowed = (key_pos <= query_pos) & (key_pos < slot_len)
+    scores = jnp.where(allowed, scores, MASKED)
+    peak = jnp.max(scores, axis=-1, keepdims=True)
+    raised = jnp.exp(scores - peak)
+    denominator = jnp.sum(raised, axis=-1, keepdims=True)
+    return raised / denominator
+
+
+def attn_fwd_kernel(head_dim, scale, meta_ref, q_ref, k_ref, v_ref, o_ref):
+    first_row = meta_ref[0]
+    slot_len = meta_ref[1]
+    for j in range(q_ref.shape[1] // head_dim):
+        cols = slice(j * head_dim, (j + 1) * head_dim)
+        shares = attention_shares(q_ref[:, cols], k_ref[:, cols], first_row, slot_len, scale)
+        mixed = jnp.dot(
+            shares.astype(jnp.bfloat16), v_ref[:, cols], preferred_element_type=jnp.float32
+        )
+        o_ref[:, cols] = mixed.astype(o_ref.dtype)
+
+
+def attn_bwd_kernel(head_dim, scale, meta_ref, q_ref, k_ref, v_ref, do_ref, dq_ref, dk_ref, dv_ref):
+    first_row = meta_ref[0]
+    slot_len = meta_ref[1]
+    for j in range(q_ref.shape[1] // head_dim):
+        cols = slice(j * head_dim, (j + 1) * head_dim)
+        query = q_ref[:, cols]
+        keys = k_ref[:, cols]
+        back = do_ref[:, cols]
+        shares = attention_shares(query, keys, first_row, slot_len, scale)
+        prob_back = lax.dot_general(back, v_ref[:, cols], NT_DIMS, preferred_element_type=jnp.float32)
+        inner = jnp.sum(shares * prob_back, axis=-1, keepdims=True)
+        score_back = (shares * (prob_back - inner)).astype(jnp.bfloat16)
+        dq_ref[:, cols] = (
+            jnp.dot(score_back, keys, preferred_element_type=jnp.float32) * scale
+        )
+        dk_ref[:, cols] = (
+            lax.dot_general(score_back, query, TN_DIMS, preferred_element_type=jnp.float32) * scale
+        ).astype(dk_ref.dtype)
+        dv_ref[:, cols] = lax.dot_general(
+            shares.astype(jnp.bfloat16), back, TN_DIMS, preferred_element_type=jnp.float32
+        ).astype(dv_ref.dtype)
+
+
+def attention_forward(meta, query_rows, kv_rows, head_dim, scale):
+    rows, width = query_rows.shape
+    keys = kv_rows.shape[0]
+    blocks = width // HEAD_BLOCK
+    return pl.pallas_call(
+        functools.partial(attn_fwd_kernel, head_dim, scale),
+        out_shape=jax.ShapeDtypeStruct((rows, width), jnp.bfloat16),
+        grid_spec=pltpu.PrefetchScalarGridSpec(
+            num_scalar_prefetch=1,
+            grid=(blocks,),
+            in_specs=[
+                pl.BlockSpec((rows, HEAD_BLOCK), lambda h, m: (0, h)),
+                pl.BlockSpec((keys, HEAD_BLOCK), lambda h, m: (0, h)),
+                pl.BlockSpec((keys, HEAD_BLOCK), lambda h, m: (0, h + blocks)),
+            ],
+            out_specs=pl.BlockSpec((rows, HEAD_BLOCK), lambda h, m: (0, h)),
+        ),
+        compiler_params=pltpu.CompilerParams(
+            dimension_semantics=("arbitrary",), vmem_limit_bytes=48 * 1024 * 1024
+        ),
+        cost_estimate=pl.CostEstimate(
+            flops=4 * rows * keys * width,
+            transcendentals=rows * keys * (width // head_dim),
+            bytes_accessed=2 * (2 * rows * width + 2 * keys * width),
+        ),
+    )(meta, query_rows, kv_rows, kv_rows)
+
+
+def attention_backward(meta, query_rows, kv_rows, back_rows, head_dim, scale):
+    rows, width = query_rows.shape
+    keys = kv_rows.shape[0]
+    blocks = width // HEAD_BLOCK
+    return pl.pallas_call(
+        functools.partial(attn_bwd_kernel, head_dim, scale),
+        out_shape=(
+            jax.ShapeDtypeStruct((rows, width), jnp.float32),
+            jax.ShapeDtypeStruct((keys, width), jnp.bfloat16),
+            jax.ShapeDtypeStruct((keys, width), jnp.bfloat16),
+        ),
+        grid_spec=pltpu.PrefetchScalarGridSpec(
+            num_scalar_prefetch=1,
+            grid=(blocks,),
+            in_specs=[
+                pl.BlockSpec((rows, HEAD_BLOCK), lambda h, m: (0, h)),
+                pl.BlockSpec((keys, HEAD_BLOCK), lambda h, m: (0, h)),
+                pl.BlockSpec((keys, HEAD_BLOCK), lambda h, m: (0, h + blocks)),
+                pl.BlockSpec((rows, HEAD_BLOCK), lambda h, m: (0, h)),
+            ],
+            out_specs=[
+                pl.BlockSpec((rows, HEAD_BLOCK), lambda h, m: (0, h)),
+                pl.BlockSpec((keys, HEAD_BLOCK), lambda h, m: (0, h)),
+                pl.BlockSpec((keys, HEAD_BLOCK), lambda h, m: (0, h)),
+            ],
+        ),
+        compiler_params=pltpu.CompilerParams(
+            dimension_semantics=("arbitrary",), vmem_limit_bytes=48 * 1024 * 1024
+        ),
+        cost_estimate=pl.CostEstimate(
+            flops=10 * rows * keys * width,
+            transcendentals=rows * keys * (width // head_dim),
+            bytes_accessed=2 * (3 * rows * width + 4 * keys * width) + 4 * rows * width,
+        ),
+    )(meta, query_rows, kv_rows, kv_rows, back_rows)
 
 
 def rope_tables(positions, half):
@@ -69,6 +190,7 @@
     assignment,
 ):
     slots, rows, width = tokens.shape
+    assert slots == 1
     head_count = H
     head_dim = width // head_count
     score_scale = head_dim ** (-0.5)
@@ -85,11 +207,7 @@
     lengths_all = jnp.sum(jnp.where(chosen, lengths[None, :], 0), axis=1)
     slot_lengths = lax.dynamic_slice_in_dim(lengths_all, lax.axis_index("fsdp") * slots, slots)
     query_places = lax.axis_index("ctx") * rows + jnp.arange(rows, dtype=jnp.int32)
-    key_places = jnp.arange(total_len, dtype=jnp.int32)
     valid = query_places[None, :] < slot_lengths[:, None]
-    allowed = (key_places[None, None, :] <= query_places[None, :, None]) & (
-        key_places[None, None, :] < slot_lengths[:, None, None]
-    )
     cosine, sine = rope_tables(query_places, head_dim // 2)
     cos_rows = cosine[None, :, None, :]
     sin_rows = sine[None, :, None, :]
@@ -135,32 +253,12 @@
 
     kv_all = lax.all_gather(
         jnp.concatenate([key_rot, value_mix], axis=-1), "ctx", axis=1, tiled=True
-    )
-    key_rows_per_head = kv_all[..., :width].reshape(slots, total_len, head_count, head_dim)
-    value_rows_per_head = kv_all[..., width:].reshape(slots, total_len, head_count, head_dim)
-
-    scores = (
-        jnp.einsum(
-            "biuv,bfuv->buif",
-            query_rotated_rows,
-            key_rows_per_head,
-            preferred_element_type=jnp.float32,
-        )
-        * score_scale
-    )
-    scores = jnp.where(allowed[:, None], scores, MASKED)
-    peak = jnp.max(scores, axis=-1, keepdims=True)
-    raised = jnp.exp(scores - peak)
-    denominator = jnp.sum(raised, axis=-1, keepdims=True)
-    shares = raised / denominator
-    attention_share_narrow = shares.astype(jnp.bfloat16)
-    mixed = jnp.einsum(
-        "ytjo,yotv->yjtv",
-        attention_share_narrow,
-        value_rows_per_head,
-        preferred_element_type=jnp.float32,
-    )
-    mixed_low = mixed.astype(jnp.bfloat16).reshape(slots, rows, width)
+    ).reshape(total_len, 2 * width)
+    meta = jnp.stack([lax.axis_index("ctx") * rows, slot_lengths[0]]).astype(jnp.int32)
+    query_flat = query_rotated_rows.reshape(rows, width)
+    mixed_low = attention_forward(
+        meta, query_flat, kv_all, head_dim, score_scale
+    ).reshape(slots, rows, width)
 
     middle = tokens_wide + jnp.dot(mixed_low, out_mat, preferred_element_type=jnp.float32)
     normed_two, inverse_two = norm_apply(middle, midnorm_full.astype(jnp.float32))
@@ -211,48 +309,15 @@
     blended_value_gradient = jnp.einsum(
         "sre,de->srd", middle_low, out_mat, preferred_element_type=jnp.float32
     ).astype(jnp.bfloat16)
-    blended_value_gradient = blended_value_gradient.reshape(slots, rows, head_count, head_dim)
-    prob_back = jnp.einsum(
-        "biuv,bfuv->buif",
-        blended_value_gradient,
-        value_rows_per_head,
-        preferred_element_type=jnp.float32,
-    )
-    inner = jnp.sum(shares * prob_back, axis=-1, keepdims=True)
-    score_gradient = (shares * (prob_back - inner)).astype(jnp.bfloat16)
-    query_rot_back = (
-        jnp.einsum(
-            "ytjo,yotv->yjtv", score_gradient, key_rows_per_head, preferred_element_type=jnp.float32
-        )
-        * score_scale
-    )
-    key_part = (
-        jnp.einsum(
-            "xtfk,xfty->kxty",
-            score_gradient,
-            query_rotated_rows,
-            preferred_element_type=jnp.float32,
-        )
-        * score_scale
-    )
-    value_part = jnp.einsum(
-        "xtfk,xfty->kxty",
-        attention_share_narrow,
-        blended_value_gradient,
-        preferred_element_type=jnp.float32,
-    )
+    query_rot_back, key_part, value_part = attention_backward(
+        meta, query_flat, kv_all, blended_value_gradient.reshape(rows, width), head_dim, score_scale
+    )
+    query_rot_back = query_rot_back.reshape(slots, rows, head_count, head_dim)
     key_value = lax.psum_scatter(
-        jnp.concatenate(
-            [key_part.reshape(total_len, slots, width), value_part.reshape(total_len, slots, width)],
-            axis=-1,
-        ).astype(jnp.bfloat16),
-        "ctx",
-        scatter_dimension=0,
-        tiled=True,
+        jnp.stack([key_part, value_part]), "ctx", scatter_dimension=1, tiled=True
     ).astype(jnp.float32)
-    key_value = jnp.swapaxes(key_value, 0, 1)
-    key_rot_back = key_value[..., :width].reshape(slots, rows, head_count, head_dim)
-    value_mix_back = key_value[..., width:]
+    key_rot_back = key_value[0].reshape(slots, rows, head_count, head_dim)
+    value_mix_back = key_value[1].reshape(slots, rows, width)
     first_grad = 0.5 * value_mix_back
     query_back = (
         rotate(query_rot_back, cos_rows, -sin_rows).reshape(slots, rows, width).astype(jnp.bfloat16)

time: 930 us -> 881 us (0.947)
  matrix products: 152 us -> 57.7 us
  waiting for transfers between devices: 541 us -> 619 us
  other arithmetic: 111 us -> 40.3 us
  Pallas kernels: 0 us -> 68.5 us
  local copies, waits for them, and re-layouts: 104 us -> 73.8 us
    dot_general x6 -> x0, matrix products: 93.3 us -> none  [the longest x1 22.7 us: body(): jnp.einsum('biuv,bfuv->buif', blended_value_gradient, value_rows_per_head...]
    pallas_call x0 -> x2, Pallas kernels: none -> 68.5 us  [the longest x1 44.2 us: attention_backward(): pl.pallas_call(functools.partial(attn_bwd_kernel, head_dim, scale), out_s...]
    all_gather x1, waiting for transfers between devices: 22.5 us -> 87.9 us  [body(): mlp_all = lax.all_gather(mlp_pack, 'fsdp', axis=0, tiled=False)]
    sub x1 -> x0, other arithmetic: 38.3 us -> none  [body(): raised = jnp.exp(scores - peak)]
    convert_element_type x1 -> x2, other arithmetic: 27.7 us -> 0.24 us  [the longest x1 0.23 us: body(): key_value = lax.psum_scatter(jnp.stack([key_part, value_part]), 'ctx', sc...]
    slice x4 -> x2, local copies, waits for them, and re-layouts: 22.6 us -> 4.76 us  [body(): key_rot_back = key_value[0].reshape(slots, rows, head_count, head_dim)]
    reduce_scatter x1, waiting for transfers between devices: 76.3 us -> 89.7 us  [body(): lax.psum_scatter(jnp.stack([key_part, value_part]), 'ctx', scatter_dimens...]
    concatenate x2 -> x0, local copies, waits for them, and re-layouts: 12.8 us -> none  [body(): jnp.concatenate([key_part.reshape(total_len, slots, width), value_part.re...]
  transfers between devices with their start and end apart: 7 -> 7, of which waited for: 7 -> 7; matrix products, arithmetic and copies ran while one was open for 18% -> 7% of each run, Pallas kernels for 0% -> 3%
where the time goes in v2:
time: 881 us; the launch traced here: 876 us
  waiting for transfers between devices  619 us (70%)
  local copies, waits for them, and re-layouts  73.8 us (8%)
  Pallas kernels  68.5 us (8%)
  matrix products  57.7 us (7%)
  other arithmetic  40.3 us (5%)
  between operations  15 us (2%)
    reduce_scatter x1, waiting for transfers between devices, body(): lax.psum_scatter(mlp_grads, 'fsdp', scatter_dimension=0, tiled=False)  165 us
    reduce_scatter x1, waiting for transfers between devices, body(): lax.psum_scatter(jnp.stack([key_part, value_part]), 'ctx', scatter_dimens...  89.7 us
    all_gather x1, waiting for transfers between devices, body(): mlp_all = lax.all_gather(mlp_pack, 'fsdp', axis=0, tiled=False)  87.9 us
    all_gather x1, waiting for transfers between devices, body(): lax.all_gather(jnp.concatenate([key_rot, value_mix], axis=-1), 'ctx', axi...  84 us
    all_gather x1, waiting for transfers between devices, body(): attn_all = lax.all_gather(attn_pack, 'fsdp', axis=0, tiled=False)  75.5 us
    psum x1, waiting for transfers between devices, body(): attn_share, mlp_share = lax.psum((attn_share, mlp_share), 'ctx')  73.4 us
    pallas_call x1, Pallas kernels, attention_backward(): pl.pallas_call(functools.partial(attn_bwd_kernel, head_dim, scale), out_s...  44.2 us
    reduce_scatter x1, waiting for transfers between devices, body(): lax.psum_scatter(attn_grads, 'fsdp', scatter_dimension=0, tiled=False)  43.6 us
  transfers between devices with their start and end apart: 7, of which 7 were waited for; matrix products, arithmetic and copies ran while one was open for 7% of the time, Pallas kernels for 3%

profile of v2, /device:TPU:0, one launch (start us, length us, event | category | flops | bytes accessed | tf_op | source)
XLA Modules:
  0.0 875.7 jit_solution(1862274457677083265)
XLA Ops:
  7.2 1.3 fusion.60
  8.5 0.9 constant_dynamic-update-slice_fusion.3
  9.4 0.9 constant_dynamic-update-slice_fusion.2
  10.3 0.9 constant_dynamic-update-slice_fusion.1
  11.3 0.9 constant_dynamic-update-slice_fusion
  12.2 0.8 copy-done.28
  13.1 1.2 fusion.17
  14.3 0.8 fusion.45
  15.2 75.5 %all-gather.8.cloned.1.call-done = bf16[4352,1024]{1,0:T(8,128)(2,1)} async-done(((bf16[272,1024]{1,0:T(8,128)(2,1)}), bf16[4352,1024]{1,0:T(8,128)(2,1)}) %all-gather.8.cloned.1.call-update) | async-done | bytes 8912912 | tf_op jit(solution)/shard_map/all_gather | solution.py:221
  90.7 0.9 fusion.46
  91.6 5.8 fusion.57
  97.4 3.9 copy.55
  101.4 4.0 copy.56
  105.4 2.6 convolution_bitcast_fusion.3
  108.0 0.8 convolution_bitcast_fusion.2
  109.1 0.9 pad_maximum_fusion.4
  110.0 1.0 copy.57
  111.0 2.5 fusion.8
  113.5 1.1 pad_maximum_fusion.3
  115.1 2.2 pad_maximum_fusion.2
  120.3 84.0 %all-gather.6.cloned.1.call-done = bf16[1,2048,2048]{2,1,0:T(8,128)(2,1)} async-done(((bf16[1,256,2048]{2,1,0:T(8,128)(2,1)}), bf16[1,2048,2048]{2,1,0:T(8,128)(2,1)}) %all-gather.6.cloned.1.call-update) | async-done | bytes 8388624 | tf_op jit(solution)/shard_map/all_gather | solution.py:254
  204.4 24.3 %shard_map.229 = bf16[256,1024]{1,0:T(8,128)(2,1)S(1)} custom-call(s32[2]{0:T(128)S(1)} %pad_add_fusion.meta_ref, bf16[256,1024]{1,0:T(8,128)(2,1)S(1)} %copy.58.q_ref, bf16[2048,2048]{1,0:T(8,128)(2,1)} %bitcast.158, bf16[2048,2048]{1,0:T(8,128)(2,1)} %bitcast.159), custom_call_target="tpu_custom_call" | custom-call | flops 2147483648 | bytes 9437184 | tf_op jit(solution)/shard_map/pallas_call | solution.py:76
  228.7 1.7 multiply_reduce_fusion
  230.4 87.9 %all-gather.10.cloned.1.call-done = bf16[1024,8448]{1,0:T(8,128)(2,1)} async-done(((bf16[64,8448]{1,0:T(8,128)(2,1)}), bf16[1024,8448]{1,0:T(8,128)(2,1)}) %all-gather.10.cloned.1.call-update) | async-done | bytes 17301520 | tf_op jit(solution)/shard_map/all_gather | solution.py:233
  318.3 11.4 %fusion.56 = (bf16[16,64,2816]{2,1,0:T(8,128)(2,1)}, bf16[16,64,2816]{2,1,0:T(8,128)(2,1)}, bf16[16,64,2816]{2,1,0:T(8,128)(2,1)}) fusion(bf16[16,64,8448]{2,1,0:T(8,128)(2,1)} %bitcast.170), kind=kLoop, calls=%fused_computation.122 | loop fusion | bytes 34603008 | tf_op jit(solution)/shard_map/slice | solution.py:236
  329.8 11.7 %reshape_reshape.7 = bf16[2816,1024]{1,0:T(8,128)(2,1)} reshape(bf16[16,64,2816]{2,1,0:T(8,128)(2,1)} %get-tuple-element.26) | data formatting | bytes 11534336 | tf_op jit(solution)/shard_map/reshape;reshape | solution.py:236
  341.5 6.4 fusion.31
  347.9 3.3 fusion.33
  351.2 7.6 multiply_convert_fusion
  358.9 1.7 fusion.61
  360.6 1.8 fusion.22
  362.9 0.8 convolution_convert_fusion.7.do_ref
  363.7 44.2 %shard_map.230 = (f32[256,1024]{1,0:T(8,128)S(1)}, bf16[2048,1024]{1,0:T(8,128)(2,1)}, bf16[2048,1024]{1,0:T(8,128)(2,1)}) custom-call(s32[2]{0:T(128)S(1)} %pad_add_fusion.meta_ref, bf16[256,1024]{1,0:T(8,128)(2,1)S(1)} %copy.58.q_ref, bf16[2048,2048]{1,0:T(8,128)(2,1)} %bitcast.160, bf16[2048,2048]{1,0:T(8,128)(2,1)} %bitcast.161, ...), custom_call_target="tpu_custom_call" | custom-call | flops 5368709120 | bytes 19398656 | tf_op jit(solution)/shard_map/pallas_call | solution.py:104
  407.9 7.5 pad_maximum_fusion.1
  416.1 89.7 %reduce-scatter.4.cloned.1.call-done = bf16[2,256,1024]{2,1,0:T(8,128)(2,1)} async-done(((bf16[2,2048,1024]{2,1,0:T(8,128)(2,1)}), bf16[2,256,1024]{2,1,0:T(8,128)(2,1)}) %reduce-scatter.4.cloned.1.call-update) | async-done | bytes 1048592 | tf_op jit(solution)/shard_map/reduce_scatter | solution.py:316
  505.8 2.2 slice.127
  508.0 2.5 copy.61
  511.0 0.8 copy-done.18
  512.2 0.8 copy-done.1
  513.0 0.8 fusion.62
  513.9 0.8 convolution_add_fusion.1
  515.4 0.8 convolution_add_fusion
  516.2 1.0 copy-done.7
  517.2 1.3 fusion.20
  518.7 1.2 copy.62
  522.2 3.4 fusion.1
  525.9 1.0 copy.67
  526.9 0.9 fusion.92
  527.8 1.2 copy.66
  529.1 5.4 convolution_convert_fusion
  534.6 12.1 %reshape_reshape.8 = bf16[16,64,2816]{2,1,0:T(8,128)(2,1)} reshape(bf16[2816,1024]{1,0:T(8,128)(2,1)} %convolution_convert_fusion) | data formatting | bytes 11534336 | tf_op jit(solution)/shard_map/reshape;reshape | solution.py:302
  546.7 3.2 convolution_convert_fusion.3
  549.9 4.2 convolution_convert_fusion.1
  554.1 5.3 convolution_convert_fusion.2
  559.5 13.3 %pad_maximum_fusion = bf16[16,64,9472]{2,1,0:T(8,128)(2,1)} fusion(bf16[16,64,1024]{2,1,0:T(8,128)(2,1)} %convolution_convert_fusion.3, bf16[16,64,2816]{2,1,0:T(8,128)(2,1)S(1)} %bitcast.163, bf16[16,64,2816]{2,1,0:T(8,128)(2,1)} %convolution_convert_fusion.1, bf16[16,64,2816]{2,1,0:T(8,128)(2,1)} %convolution_convert_fusion.2), kind=kLoop, calls=%fused_computation | loop fusion | flops 77594624 | bytes 38797312 | tf_op jit(solution)/shard_map/concatenate | solution.py:298
  572.8 43.6 %reduce-scatter.6.cloned.1.call-done = bf16[1,208,1024]{2,1,0:T(8,128)(2,1)} async-done(((bf16[16,208,1024]{2,1,0:T(8,128)(2,1)}), bf16[1,208,1024]{2,1,0:T(8,128)(2,1)}) %reduce-scatter.6.cloned.1.call-update) | async-done | bytes 426000 | tf_op jit(solution)/shard_map/reduce_scatter | solution.py:364
  616.4 164.9 %reduce-scatter.8.cloned.1.call-done = bf16[1,64,9472]{2,1,0:T(8,128)(2,1)} async-done(((bf16[16,64,9472]{2,1,0:T(8,128)(2,1)}), bf16[1,64,9472]{2,1,0:T(8,128)(2,1)}) %reduce-scatter.8.cloned.1.call-update) | async-done | bytes 1212432 | tf_op jit(solution)/shard_map/reduce_scatter | solution.py:307
  781.4 5.7 fusion.9
  787.1 1.3 fusion.16
  788.4 73.4 %all-reduce.5.cloned.1.call-done = (bf16[208,1024]{1,0:T(8,128)(2,1)}, bf16[64,9472]{1,0:T(8,128)(2,1)}) async-done(((bf16[208,1024]{1,0:T(8,128)(2,1)}, bf16[64,9472]{1,0:T(8,128)(2,1)}), (bf16[208,1024]{1,0:T(8,128)(2,1)}, bf16[64,9472]{1,0:T(8,128)(2,1)})) %all-reduce.5.cloned.1.call-update) | async-done | bytes 1638416 | tf_op jit(solution)/shard_map/psum | solution.py:366
  861.8 2.0 fusion.59
  863.9 1.1 convert_element_type.190
  865.7 1.3 fusion.58
  867.5 1.1 reshape.470
  (131 shorter events, 10.9 us)
Async XLA Ops:
  7.2 83.5 %all-gather.8.cloned.1.call-start = ((), (), s32[]{:S(2)}) async-start(), calls=%async_computation.7 | async-start | bytes 9469952 | tf_op jit(solution)/shard_map/all_gather | solution.py:221
  12.2 0.8 copy-start.28
  13.0 191.3 %all-gather.6.cloned.1.call-start = ((), (), s32[]{:S(2)}) async-start(), calls=%async_computation.3 | async-start | bytes 9437184 | tf_op jit(solution)/shard_map/all_gather | solution.py:254
  14.3 96.7 %copy-start.31 = (f32[256]{0:T(256)}, f32[256]{0:T(256)S(1)}, u32[]{:S(2)}) copy-start(f32[256]{0:T(256)S(1)} %add_rsqrt_fusion.1) | copy-start | bytes 3076
  101.4 4.0 copy-start.9
  105.4 2.6 copy-start.21
  111.0 2.5 copy-start.23
  111.0 3.7 copy-start.29
  114.6 3.3 copy-start.34
  114.6 3.3 copy-start.35
  114.6 5.5 copy-start.22
  114.6 203.7 %all-gather.10.cloned.1.call-start = ((), (), s32[]{:S(2)}) async-start(), calls=%async_computation.8 | async-start | bytes 18382848 | tf_op jit(solution)/shard_map/all_gather | solution.py:233
  117.3 388.5 %reduce-scatter.4.cloned.1.call-start = ((), (), s32[]{:S(2)}) async-start(), calls=%async_computation.4 | async-start | bytes 9437184 | tf_op jit(solution)/shard_map/reduce_scatter | solution.py:316
  204.4 24.3 %copy-start.10 = (bf16[1,256,1024]{2,1,0:T(8,128)(2,1)S(1)}, bf16[1,256,1024]{2,1,0:T(8,128)(2,1)}, u32[]{:S(2)}) copy-start(bf16[1,256,1024]{2,1,0:T(8,128)(2,1)} %param.14) | copy-start | bytes 1572868
  341.5 6.4 copy-start.4
  341.5 6.4 copy-start.14
  341.5 9.7 %slice-start.2 = ((s8[5767168]{0:T(1024)(128)(4,1)}), s8[4194304]{0:T(1024)(128)(4,1)S(1)}, s32[]{:S(2)}) async-start(s8[5767168]{0:T(1024)(128)(4,1)} %bitcast.178), calls=%async_computation.12 | async-start | bytes 8388608
  347.8 3.4 slice-start.3
  347.9 3.3 copy-start.20
  347.9 12.7 %slice-start.4 = ((s8[5767168]{0:T(1024)(128)(4,1)}), s8[4194304]{0:T(1024)(128)(4,1)S(1)}, s32[]{:S(2)}) async-start(s8[5767168]{0:T(1024)(128)(4,1)} %bitcast.181), calls=%async_computation.14 | async-start | bytes 8388608
  351.2 9.4 %slice-start.5 = ((s8[5767168]{0:T(1024)(128)(4,1)}), s8[1572864]{0:T(1024)(128)(4,1)S(1)}, s32[]{:S(2)}) async-start(s8[5767168]{0:T(1024)(128)(4,1)} %bitcast.181), calls=%async_computation.15 | async-start | bytes 3145728
  358.9 1.7 copy-start.24
  358.9 1.7 copy-start.26
  362.9 45.0 %copy-start.2 = (f32[1,256,1024]{2,1,0:T(8,128)}, f32[1,256,1024]{2,1,0:T(8,128)S(1)}, u32[]{:S(2)}) copy-start(f32[1,256,1024]{2,1,0:T(8,128)S(1)} %fusion.24) | copy-start | bytes 3145732
  415.5 201.0 %reduce-scatter.6.cloned.1.call-start = ((), (), s32[]{:S(2)}) async-start(), calls=%async_computation.5 | async-start | bytes 7241728 | tf_op jit(solution)/shard_map/reduce_scatter | solution.py:364
  505.8 4.8 copy-start.17
  510.6 1.2 copy-start.18
  510.6 1.2 copy-start.30
  511.0 9.0 %copy-start.6 = (f32[1,256,1024]{2,1,0:T(8,128)}, f32[1,256,1024]{2,1,0:T(8,128)S(1)}, u32[]{:S(2)}) copy-start(f32[1,256,1024]{2,1,0:T(8,128)S(1)} %slice_multiply_fusion) | copy-start | bytes 3145732
  511.0 2.1 copy-start.1
  512.1 1.7 copy-start
  513.8 1.6 copy-start.13
  515.4 1.8 copy-start.11
  515.4 1.8 copy-start.32
  515.4 3.2 copy-start.33
  516.2 1.0 copy-start.7
  525.6 1.3 copy-start.5
  525.6 3.5 copy-start.19
  525.6 255.8 %reduce-scatter.8.cloned.1.call-start = ((), (), s32[]{:S(2)}) async-start(), calls=%async_computation.6 | async-start | bytes 20611072 | tf_op jit(solution)/shard_map/reduce_scatter | solution.py:307
  529.1 20.8 %copy-start.16 = (bf16[1024,256]{1,0:T(8,128)(2,1)}, bf16[1024,256]{1,0:T(8,128)(2,1)S(1)}, u32[]{:S(2)}) copy-start(bf16[1024,256]{1,0:T(8,128)(2,1)S(1)} %copy.66) | copy-start | bytes 1572868
  534.6 12.1 %copy-start.3 = (f32[1,256,1024]{2,1,0:T(8,128)S(1)}, f32[1,256,1024]{2,1,0:T(8,128)}, u32[]{:S(2)}) copy-start(f32[1,256,1024]{2,1,0:T(8,128)} %copy-done.2) | copy-start | bytes 3145732
  546.7 3.2 copy-start.27
  549.9 4.2 copy-start.25
  549.9 9.5 %slice-start = ((s8[5767168]{0:T(1024)(128)(4,1)}), s8[4194304]{0:T(1024)(128)(4,1)S(1)}, s32[]{:S(2)}) async-start(s8[5767168]{0:T(1024)(128)(4,1)} %bitcast.162), calls=%async_computation.10 | async-start | bytes 8388608
  554.1 5.3 slice-start.1
  572.8 289.1 %all-reduce.5.cloned.1.call-start = ((), (), s32[]{:S(2)}) async-start(), calls=%async_computation.9 | async-start | bytes 3276800 | tf_op jit(solution)/shard_map/psum | solution.py:366
  781.4 5.7 copy-start.8
  781.4 5.7 copy-start.12
  861.8 3.1 copy-start.15
Sparse Core Ops, SparseCore 0:
  13.1 77.4 all-gather.7
  114.7 89.5 all-gather.5
  206.8 111.4 all-gather.9
  415.6 90.2 reduce-scatter.3
  525.7 90.6 reduce-scatter.5
  621.4 159.9 reduce-scatter.7
  784.1 77.6 all-reduce.4

commit v3 on v2

--- a/solution.py
+++ b/solution.py
@@ -24,9 +24,11 @@
 def attention_shares(query, keys, first_row, slot_len, scale):
     scores = lax.dot_general(query, keys, NT_DIMS, preferred_element_type=jnp.float32) * scale
     shape = scores.shape
+    rows = query.shape[0]
     query_pos = first_row + lax.broadcasted_iota(jnp.int32, shape, 0)
-    key_pos = lax.broadcasted_iota(jnp.int32, shape, 1)
-    allowed = (key_pos <= query_pos) & (key_pos < slot_len)
+    key_row = lax.broadcasted_iota(jnp.int32, shape, 1)
+    key_pos = first_row + key_row - 2 * rows * (key_row // rows)
+    allowed = (key_pos >= 0) & (key_pos <= query_pos) & (key_pos < slot_len)
     scores = jnp.where(allowed, scores, MASKED)
     peak = jnp.max(scores, axis=-1, keepdims=True)
     raised = jnp.exp(scores - peak)
@@ -46,7 +48,7 @@
         o_ref[:, cols] = mixed.astype(o_ref.dtype)
 
 
-def attn_bwd_kernel(head_dim, scale, meta_ref, q_ref, k_ref, v_ref, do_ref, dq_ref, dk_ref, dv_ref):
+def attn_bwd_kernel(head_dim, scale, meta_ref, q_ref, k_ref, v_ref, do_ref, dq_ref, dkv_ref):
     first_row = meta_ref[0]
     slot_len = meta_ref[1]
     for j in range(q_ref.shape[1] // head_dim):
@@ -61,12 +63,13 @@
         dq_ref[:, cols] = (
             jnp.dot(score_back, keys, preferred_element_type=jnp.float32) * scale
         )
-        dk_ref[:, cols] = (
+        dkv_ref[:, cols] = (
             lax.dot_general(score_back, query, TN_DIMS, preferred_element_type=jnp.float32) * scale
-        ).astype(dk_ref.dtype)
-        dv_ref[:, cols] = lax.dot_general(
+        ).astype(dkv_ref.dtype)
+        half = q_ref.shape[1]
+        dkv_ref[:, half + j * head_dim:half + (j + 1) * head_dim] = lax.dot_general(
             shares.astype(jnp.bfloat16), back, TN_DIMS, preferred_element_type=jnp.float32
-        ).astype(dv_ref.dtype)
+        ).astype(dkv_ref.dtype)
 
 
 def attention_forward(meta, query_rows, kv_rows, head_dim, scale):
@@ -105,8 +108,7 @@
         functools.partial(attn_bwd_kernel, head_dim, scale),
         out_shape=(
             jax.ShapeDtypeStruct((rows, width), jnp.float32),
-            jax.ShapeDtypeStruct((keys, width), jnp.bfloat16),
-            jax.ShapeDtypeStruct((keys, width), jnp.bfloat16),
+            jax.ShapeDtypeStruct((keys, 2 * width), jnp.bfloat16),
         ),
         grid_spec=pltpu.PrefetchScalarGridSpec(
             num_scalar_prefetch=1,
@@ -119,8 +121,7 @@
             ],
             out_specs=[
                 pl.BlockSpec((rows, HEAD_BLOCK), lambda h, m: (0, h)),
-                pl.BlockSpec((keys, HEAD_BLOCK), lambda h, m: (0, h)),
-                pl.BlockSpec((keys, HEAD_BLOCK), lambda h, m: (0, h)),
+                pl.BlockSpec((keys, 2 * HEAD_BLOCK), lambda h, m: (0, h)),
             ],
         ),
         compiler_params=pltpu.CompilerParams(
@@ -171,6 +172,16 @@
     row = row[..., None, :]
     pads = [(0, 0)] * len(leading) + [(0, GAIN_ROWS - 1), (0, 0)]
     return jnp.pad(row, pads)
+
+
+def ctx_allreduce(part, n_ctx):
+    total = part
+    step = 1
+    while step < n_ctx:
+        other = lax.ppermute(total, "ctx", [(j, j ^ step) for j in range(n_ctx)])
+        total = (total.astype(jnp.float32) + other.astype(jnp.float32)).astype(jnp.bfloat16)
+        step *= 2
+    return total.astype(jnp.float32)
 
 
 def body(
@@ -251,9 +262,15 @@
     )
     value_mix = (0.5 * own_value + 0.5 * first_wide).astype(jnp.bfloat16)
 
-    kv_all = lax.all_gather(
-        jnp.concatenate([key_rot, value_mix], axis=-1), "ctx", axis=1, tiled=True
-    ).reshape(total_len, 2 * width)
+    kv_own = jnp.concatenate([key_rot, value_mix], axis=-1).reshape(rows, 2 * width)
+    kv_all = jnp.concatenate(
+        [kv_own]
+        + [
+            lax.ppermute(kv_own, "ctx", [(j, j + b) for j in range(n_ctx - b)])
+            for b in range(1, n_ctx)
+        ],
+        axis=0,
+    )
     meta = jnp.stack([lax.axis_index("ctx") * rows, slot_lengths[0]]).astype(jnp.int32)
     query_flat = query_rotated_rows.reshape(rows, width)
     mixed_low = attention_forward(
@@ -309,15 +326,19 @@
     blended_value_gradient = jnp.einsum(
         "sre,de->srd", middle_low, out_mat, preferred_element_type=jnp.float32
     ).astype(jnp.bfloat16)
-    query_rot_back, key_part, value_part = attention_backward(
+    query_rot_back, kv_back = attention_backward(
         meta, query_flat, kv_all, blended_value_gradient.reshape(rows, width), head_dim, score_scale
     )
     query_rot_back = query_rot_back.reshape(slots, rows, head_count, head_dim)
-    key_value = lax.psum_scatter(
-        jnp.stack([key_part, value_part]), "ctx", scatter_dimension=1, tiled=True
-    ).astype(jnp.float32)
-    key_rot_back = key_value[0].reshape(slots, rows, head_count, head_dim)
-    value_mix_back = key_value[1].reshape(slots, rows, width)
+    kv_back = kv_back.reshape(n_ctx, rows, 2 * width)
+    key_value = kv_back[0].astype(jnp.float32)
+    for b_shift in range(1, n_ctx):
+        key_value = key_value + lax.ppermute(
+            kv_back[b_shift], "ctx", [(j, j - b_shift) for j in range(b_shift, n_ctx)]
+        ).astype(jnp.float32)
+    key_value = key_value.reshape(rows, width // HEAD_BLOCK, 2, HEAD_BLOCK)
+    key_rot_back = key_value[:, :, 0, :].reshape(slots, rows, head_count, head_dim)
+    value_mix_back = key_value[:, :, 1, :].reshape(slots, rows, width)
     first_grad = 0.5 * value_mix_back
     query_back = (
         rotate(query_rot_back, cos_rows, -sin_rows).reshape(slots, rows, width).astype(jnp.bfloat16)
@@ -361,11 +382,10 @@
         ],
         axis=1,
     ).astype(jnp.bfloat16)
+    attn_grads, mlp_share = lax.optimization_barrier((attn_grads, mlp_share))
+    mlp_share = ctx_allreduce(mlp_share, n_ctx)
     attn_share = lax.psum_scatter(attn_grads, "fsdp", scatter_dimension=0, tiled=False)
-
-    attn_share, mlp_share = lax.psum((attn_share, mlp_share), "ctx")
-    attn_share = attn_share.astype(jnp.float32)
-    mlp_share = mlp_share.astype(jnp.float32)
+    attn_share = ctx_allreduce(attn_share, n_ctx)
 
     def attn_grad(i):
         return attn_share[i * w_rows:(i + 1) * w_rows]

time: 881 us -> 760 us (0.86)
  waiting for transfers between devices: 619 us -> 416 us
  starting transfers between devices: 1.28 us -> 46.2 us
  local copies, waits for them, and re-layouts: 73.8 us -> 106 us
    ppermute x0 -> x20, waiting for transfers between devices: none -> 263 us  [the longest x7 115 us: body(): lax.ppermute(kv_back[b_shift], 'ctx', [(j, j - b_shift) for j in range(b_...]
    reduce_scatter x1, waiting for transfers between devices: 165 us -> 41 us  [body(): lax.psum_scatter(mlp_grads, 'fsdp', scatter_dimension=0, tiled=False)]
    reduce_scatter x1 -> x0, waiting for transfers between devices: 89.7 us -> none  [body(): lax.psum_scatter(jnp.stack([key_part, value_part]), 'ctx', scatter_dimens...]
    all_gather x1 -> x0, waiting for transfers between devices: 84 us -> none  [body(): lax.all_gather(jnp.concatenate([key_rot, value_mix], axis=-1), 'ctx', axi...]
    all_gather x1, waiting for transfers between devices: 87.9 us -> 5.49 us  [body(): mlp_all = lax.all_gather(mlp_pack, 'fsdp', axis=0, tiled=False)]
    psum x1 -> x0, waiting for transfers between devices: 73.4 us -> none  [body(): attn_share, mlp_share = lax.psum((attn_share, mlp_share), 'ctx')]
    ppermute x0 -> x20, starting transfers between devices: none -> 46.1 us  [the longest x7 25.1 us: body(): lax.ppermute(kv_own, 'ctx', [(j, j + b) for j in range(n_ctx - b)])]
    unnamed x88 -> x76, local copies, waits for them, and re-layouts: 8.03 us -> 28.2 us
  transfers between devices with their start and end apart: 7 -> 24, of which waited for: 7 -> 15; matrix products, arithmetic and copies ran while one was open for 7% -> 14% of each run, Pallas kernels for 3% -> 9%
where the time goes in v3:
time: 760 us; the launch traced here: 753 us
  waiting for transfers between devices  416 us (55%)
  local copies, waits for them, and re-layouts  106 us (14%)
  Pallas kernels  71.3 us (9%)
  matrix products  54.9 us (7%)
  starting transfers between devices  46.2 us (6%)
  other arithmetic  44.3 us (6%)
  between operations  15 us (2%)
    ppermute x7, waiting for transfers between devices, body(): lax.ppermute(kv_back[b_shift], 'ctx', [(j, j - b_shift) for j in range(b_...  115 us
    ppermute x7, waiting for transfers between devices, body(): lax.ppermute(kv_own, 'ctx', [(j, j + b) for j in range(n_ctx - b)])  80.1 us
    all_gather x1, waiting for transfers between devices, body(): attn_all = lax.all_gather(attn_pack, 'fsdp', axis=0, tiled=False)  74.6 us
    ppermute x6, waiting for transfers between devices, ctx_allreduce(): other = lax.ppermute(total, 'ctx', [(j, j ^ step) for j in range(n_ctx)])  67.8 us
    pallas_call x1, Pallas kernels, attention_backward(): pl.pallas_call(functools.partial(attn_bwd_kernel, head_dim, scale), out_s...  45 us
    reduce_scatter x1, waiting for transfers between devices, body(): lax.psum_scatter(mlp_grads, 'fsdp', scatter_dimension=0, tiled=False)  41 us
    reduce_scatter x1, waiting for transfers between devices, body(): lax.psum_scatter(attn_grads, 'fsdp', scatter_dimension=0, tiled=False)  31.6 us
    unnamed x76, local copies, waits for them, and re-layouts  28.2 us
  transfers between devices with their start and end apart: 24, of which 15 were waited for; matrix products, arithmetic and copies ran while one was open for 14% of the time, Pallas kernels for 9%

profile of v3, /device:TPU:0, one launch (start us, length us, event | category | flops | bytes accessed | tf_op | source)
XLA Modules:
  0.0 753.1 jit_solution(1549750325620794514)
XLA Ops:
  15.7 74.6 %all-gather.5.cloned.1.call-done = bf16[4352,1024]{1,0:T(8,128)(2,1)} async-done(((bf16[272,1024]{1,0:T(8,128)(2,1)}), bf16[4352,1024]{1,0:T(8,128)(2,1)}) %all-gather.5.cloned.1.call-update) | async-done | bytes 8912912 | tf_op jit(solution)/shard_map/all_gather | solution.py:232
  90.3 5.8 fusion.56
  96.0 3.9 copy.58
  101.0 4.0 copy.57
  105.0 2.6 convolution_bitcast_fusion.2
  111.1 2.4 fusion.8
  115.4 4.4 collective-permute-start
  119.8 4.5 collective-permute-start.1
  124.3 3.6 collective-permute-start.2
  129.4 2.2 collective-permute-start.3
  132.3 2.3 collective-permute-start.4
  134.6 2.2 constant_dynamic-update-slice_fusion.11
  138.1 4.4 collective-permute-done
  142.6 6.1 collective-permute-start.5
  148.7 2.4 constant_dynamic-update-slice_fusion.10
  151.0 14.0 %collective-permute-done.1 = bf16[256,2048]{1,0:T(8,128)(2,1)} collective-permute-done((bf16[256,2048]{1,0:T(8,128)(2,1)}, bf16[256,2048]{1,0:T(8,128)(2,1)}, u32[]{:S(2)}, u32[]{:S(2)}) %collective-permute-start.1) | collective-permute-done | bytes 1048608 | tf_op jit(solution)/shard_map/ppermute | solution.py:269
  165.1 1.9 collective-permute-start.6
  166.9 2.3 constant_dynamic-update-slice_fusion.9
  169.3 2.3 constant_dynamic-update-slice_fusion.8
  171.6 61.6 %collective-permute-done.3 = bf16[256,2048]{1,0:T(8,128)(2,1)} collective-permute-done((bf16[256,2048]{1,0:T(8,128)(2,1)}, bf16[256,2048]{1,0:T(8,128)(2,1)}, u32[]{:S(2)}, u32[]{:S(2)}) %collective-permute-start.3) | collective-permute-done | bytes 1048608 | tf_op jit(solution)/shard_map/ppermute | solution.py:269
  233.2 2.3 constant_dynamic-update-slice_fusion.7
  235.5 2.3 constant_dynamic-update-slice_fusion.6
  239.9 26.3 %shard_map.229 = bf16[256,1024]{1,0:T(8,128)(2,1)S(1)} custom-call(s32[2]{0:T(128)S(1)} %pad_add_fusion.meta_ref, bf16[256,1024]{1,0:T(8,128)(2,1)S(1)} %copy.60.q_ref, bf16[2048,2048]{1,0:T(8,128)(2,1)} %constant_dynamic-update-slice_fusion.4.k_ref.v_ref, bf16[2048,2048]{1,0:T(8,128)(2,1)} %constant_dynamic-update-slice_fusion.4.k_ref.v_ref), custom_call_target="tpu_custom_call" | custom-call | flops 2147483648 | bytes 9437184 | tf_op jit(solution)/shard_map/pallas_call | solution.py:79
  267.2 1.9 multiply_reduce_fusion
  272.4 5.5 all-gather.7.cloned.1.call-done
  277.9 8.7 %fusion.55 = (bf16[16,64,2816]{2,1,0:T(8,128)(2,1)}, bf16[16,64,2816]{2,1,0:T(8,128)(2,1)S(1)}, bf16[16,64,2816]{2,1,0:T(8,128)(2,1)S(1)}) fusion(bf16[16,64,8448]{2,1,0:T(8,128)(2,1)} %bitcast.166), kind=kLoop, calls=%fused_computation.135 | loop fusion | bytes 34603008 | tf_op jit(solution)/shard_map/slice | solution.py:247
  286.5 3.8 fusion.32
  291.6 3.3 fusion.30
  294.9 11.9 %reshape_reshape.7 = bf16[2816,1024]{1,0:T(8,128)(2,1)} reshape(bf16[16,64,2816]{2,1,0:T(8,128)(2,1)} %get-tuple-element.50) | data formatting | bytes 11534336 | tf_op jit(solution)/shard_map/reshape;reshape | solution.py:247
  306.8 7.2 multiply_convert_fusion
  314.0 4.9 fusion.62
  318.9 4.1 convolution_convert_fusion.2
  323.0 4.2 convolution_convert_fusion.1
  327.2 2.8 fusion.23
  330.0 4.3 convolution_convert_fusion
  334.3 11.9 %reshape_reshape.8 = bf16[16,64,2816]{2,1,0:T(8,128)(2,1)} reshape(bf16[2816,1024]{1,0:T(8,128)(2,1)} %convolution_convert_fusion) | data formatting | bytes 11534336 | tf_op jit(solution)/shard_map/reshape;reshape | solution.py:319
  346.2 2.0 fusion.25
  349.9 14.2 %pad_maximum_fusion = bf16[16,64,9472]{2,1,0:T(8,128)(2,1)} fusion(bf16[16,64,1024]{2,1,0:T(8,128)(2,1)S(1)} %convolution_convert_fusion.3, bf16[16,64,2816]{2,1,0:T(8,128)(2,1)} %reshape_reshape.8, bf16[16,64,2816]{2,1,0:T(8,128)(2,1)} %convolution_convert_fusion.1, bf16[16,64,2816]{2,1,0:T(8,128)(2,1)} %convolution_convert_fusion.2), kind=kLoop, calls=%fused_computation | loop fusion | flops 77594624 | bytes 38797312 | tf_op jit(solution)/shard_map/concatenate | solution.py:315
  364.2 2.0 convolution_convert_fusion.7.do_ref
  366.2 45.0 %shard_map.230 = (f32[256,1024]{1,0:T(8,128)S(1)}, bf16[2048,2048]{1,0:T(8,128)(2,1)}) custom-call(s32[2]{0:T(128)S(1)} %pad_add_fusion.meta_ref, bf16[256,1024]{1,0:T(8,128)(2,1)S(1)} %copy.60.q_ref, bf16[2048,2048]{1,0:T(8,128)(2,1)} %constant_dynamic-update-slice_fusion.4.k_ref.v_ref, bf16[2048,2048]{1,0:T(8,128)(2,1)} %constant_dynamic-update-slice_fusion.4.k_ref.v_ref, ...), custom_call_target="tpu_custom_call" | custom-call | flops 5368709120 | bytes 19398656 | tf_op jit(solution)/shard_map/pallas_call | solution.py:107
  411.2 6.5 fusion.57
  424.2 90.7 %collective-permute-done.13 = bf16[256,2048]{1,0:T(8,128)(2,1)S(1)} collective-permute-done((bf16[256,2048]{1,0:T(8,128)(2,1)S(1)}, bf16[256,2048]{1,0:T(8,128)(2,1)S(1)}, u32[]{:S(2)}, u32[]{:S(2)}) %collective-permute-start.13) | collective-permute-done | bytes 1048608 | tf_op jit(solution)/shard_map/ppermute | solution.py:336
  517.9 5.0 collective-permute-done.10
  522.9 19.5 %collective-permute-done.8 = bf16[256,2048]{1,0:T(8,128)(2,1)} collective-permute-done((bf16[256,2048]{1,0:T(8,128)(2,1)}, bf16[256,2048]{1,0:T(8,128)(2,1)}, u32[]{:S(2)}, u32[]{:S(2)}) %collective-permute-start.8) | collective-permute-done | bytes 1048608 | tf_op jit(solution)/shard_map/ppermute | solution.py:336
  542.4 5.1 convert_add_fusion
  547.5 3.1 reshape.505
  550.6 5.0 fusion.59
  555.6 2.4 copy.63
  558.0 2.1 copy.79
  571.2 3.3 fusion.1
  574.5 41.0 %reduce-scatter.3.cloned.1.call-done = bf16[1,64,9472]{2,1,0:T(8,128)(2,1)} async-done(((bf16[16,64,9472]{2,1,0:T(8,128)(2,1)}), bf16[1,64,9472]{2,1,0:T(8,128)(2,1)}) %reduce-scatter.3.cloned.1.call-update) | async-done | bytes 1212432 | tf_op jit(solution)/shard_map/reduce_scatter | solution.py:324
  617.0 26.7 %collective-permute-done.17 = bf16[64,9472]{1,0:T(8,128)(2,1)S(1)} collective-permute-done((bf16[64,9472]{1,0:T(8,128)(2,1)}, bf16[64,9472]{1,0:T(8,128)(2,1)S(1)}, u32[]{:S(2)}, u32[]{:S(2)}) %collective-permute-start.17) | collective-permute-done | bytes 1212448 | tf_op jit(solution)/shard_map/ppermute | solution.py:181
  645.3 3.0 collective-permute-start.18
  648.3 25.6 %collective-permute-done.18 = bf16[64,9472]{1,0:T(8,128)(2,1)S(1)} collective-permute-done((bf16[64,9472]{1,0:T(8,128)(2,1)S(1)}, bf16[64,9472]{1,0:T(8,128)(2,1)S(1)}, u32[]{:S(2)}, u32[]{:S(2)}) %collective-permute-start.18) | collective-permute-done | bytes 1212448 | tf_op jit(solution)/shard_map/ppermute | solution.py:181
  675.9 5.5 fusion.9
  681.4 31.6 %reduce-scatter.5.cloned.1.call-done = bf16[1,208,1024]{2,1,0:T(8,128)(2,1)} async-done(((bf16[16,208,1024]{2,1,0:T(8,128)(2,1)}), bf16[1,208,1024]{2,1,0:T(8,128)(2,1)}) %reduce-scatter.5.cloned.1.call-update) | async-done | bytes 426000 | tf_op jit(solution)/shard_map/reduce_scatter | solution.py:387
  713.0 1.8 collective-permute-start.14
  714.8 2.6 copy.72
  718.8 5.0 collective-permute-done.14
  724.0 3.1 collective-permute-start.15
  727.1 1.9 fusion.12
  729.7 5.5 collective-permute-done.15
  735.3 1.9 collective-permute-start.16
  739.5 5.0 collective-permute-done.16
  (156 shorter events, 59.4 us)
Async XLA Ops:
  7.2 7.0 copy-start.26
  7.2 7.0 copy-start.27
  7.2 83.1 %all-gather.5.cloned.1.call-start = ((), (), s32[]{:S(2)}) async-start(), calls=%async_computation.4 | async-start | bytes 9469952 | tf_op jit(solution)/shard_map/all_gather | solution.py:232
  10.8 4.5 copy-start.8
  11.8 0.8 copy-start.24
  12.7 265.2 %all-gather.7.cloned.1.call-start = ((), (), s32[]{:S(2)}) async-start(), calls=%async_computation.5 | async-start | bytes 18382848 | tf_op jit(solution)/shard_map/all_gather | solution.py:244
  15.2 600.3 %reduce-scatter.3.cloned.1.call-start = ((), (), s32[]{:S(2)}) async-start(), calls=%async_computation.2 | async-start | bytes 20611072 | tf_op jit(solution)/shard_map/reduce_scatter | solution.py:324
  105.0 2.6 copy-start.20
  111.0 16.8 %copy-start.28 = (s32[16]{0:T(128)S(1)}, s32[16]{0:T(128)}, u32[]{:S(2)}) copy-start(s32[16]{0:T(128)} %param.26) | copy-start | bytes 196
  111.1 16.8 %copy-start.29 = (s32[16]{0:T(128)S(1)}, s32[16]{0:T(128)}, u32[]{:S(2)}) copy-start(s32[16]{0:T(128)} %param.27) | copy-start | bytes 196
  113.5 0.8 copy-start.21
  115.4 27.2 %collective-permute-start = (bf16[256,2048]{1,0:T(8,128)(2,1)}, bf16[256,2048]{1,0:T(8,128)(2,1)}, u32[]{:S(2)}, u32[]{:S(2)}) collective-permute-start(bf16[256,2048]{1,0:T(8,128)(2,1)} %maximum_bitcast_fusion), channel_id=1, source_target_pairs={{0,1},{1,2},{2,3},{3,4},{4,5},{5,6},{6,7},{8,9},{9,10},{10,11},{11... | collective-permute-start | bytes 3145736 | tf_op jit(solution)/shard_map/ppermute | solution.py:269
  119.8 45.3 %collective-permute-start.1 = (bf16[256,2048]{1,0:T(8,128)(2,1)}, bf16[256,2048]{1,0:T(8,128)(2,1)}, u32[]{:S(2)}, u32[]{:S(2)}) collective-permute-start(bf16[256,2048]{1,0:T(8,128)(2,1)} %maximum_bitcast_fusion), channel_id=1, source_target_pairs={{0,2},{1,3},{2,4},{3,5},{4,6},{5,7},{8,10},{9,11},{10,12},{11,13},... | collective-permute-start | bytes 3145736 | tf_op jit(solution)/shard_map/ppermute | solution.py:269
  124.3 44.9 %collective-permute-start.2 = (bf16[256,2048]{1,0:T(8,128)(2,1)}, bf16[256,2048]{1,0:T(8,128)(2,1)}, u32[]{:S(2)}, u32[]{:S(2)}) collective-permute-start(bf16[256,2048]{1,0:T(8,128)(2,1)} %maximum_bitcast_fusion), channel_id=1, source_target_pairs={{0,3},{1,4},{2,5},{3,6},{4,7},{8,11},{9,12},{10,13},{11,14},{12,15... | collective-permute-start | bytes 3145736 | tf_op jit(solution)/shard_map/ppermute | solution.py:269
  129.4 103.8 %collective-permute-start.3 = (bf16[256,2048]{1,0:T(8,128)(2,1)}, bf16[256,2048]{1,0:T(8,128)(2,1)}, u32[]{:S(2)}, u32[]{:S(2)}) collective-permute-start(bf16[256,2048]{1,0:T(8,128)(2,1)} %maximum_bitcast_fusion), channel_id=1, source_target_pairs={{0,4},{1,5},{2,6},{3,7},{8,12},{9,13},{10,14},{11,15},{16,20},{17,... | collective-permute-start | bytes 3145736 | tf_op jit(solution)/shard_map/ppermute | solution.py:269
  132.3 103.2 %collective-permute-start.4 = (bf16[256,2048]{1,0:T(8,128)(2,1)}, bf16[256,2048]{1,0:T(8,128)(2,1)}, u32[]{:S(2)}, u32[]{:S(2)}) collective-permute-start(bf16[256,2048]{1,0:T(8,128)(2,1)} %maximum_bitcast_fusion), channel_id=1, source_target_pairs={{0,5},{1,6},{2,7},{8,13},{9,14},{10,15},{16,21},{17,22},{18,23},{2... | collective-permute-start | bytes 3145736 | tf_op jit(solution)/shard_map/ppermute | solution.py:269
  142.6 95.3 %collective-permute-start.5 = (bf16[256,2048]{1,0:T(8,128)(2,1)}, bf16[256,2048]{1,0:T(8,128)(2,1)S(1)}, u32[]{:S(2)}, u32[]{:S(2)}) collective-permute-start(bf16[256,2048]{1,0:T(8,128)(2,1)} %maximum_bitcast_fusion), channel_id=1, source_target_pairs={{0,6},{1,7},{8,14},{9,15},{16,22},{17,23},{24,30},{25,31},{32,38},... | collective-permute-start | bytes 3145736 | tf_op jit(solution)/shard_map/ppermute | solution.py:269
  165.1 73.8 %collective-permute-start.6 = (bf16[256,2048]{1,0:T(8,128)(2,1)}, bf16[256,2048]{1,0:T(8,128)(2,1)S(1)}, u32[]{:S(2)}, u32[]{:S(2)}) collective-permute-start(bf16[256,2048]{1,0:T(8,128)(2,1)} %maximum_bitcast_fusion), channel_id=1, source_target_pairs={{0,7},{8,15},{16,23},{24,31},{32,39},{40,47},{48,55},{56,63},{64,7... | collective-permute-start | bytes 3145736 | tf_op jit(solution)/shard_map/ppermute | solution.py:269
  269.1 1.0 copy-start.4
  277.9 8.7 %copy-start.5 = (f32[1,256,1024]{2,1,0:T(8,128)S(1)}, f32[1,256,1024]{2,1,0:T(8,128)}, u32[]{:S(2)}) copy-start(f32[1,256,1024]{2,1,0:T(8,128)} %copy-done.4) | copy-start | bytes 3145732
  286.5 3.8 copy-start.12
  286.5 5.1 copy-start.11
  314.0 16.0 %copy-start.16 = (bf16[256,2816]{1,0:T(8,128)(2,1)}, bf16[256,2816]{1,0:T(8,128)(2,1)S(1)}, u32[]{:S(2)}) copy-start(bf16[256,2816]{1,0:T(8,128)(2,1)S(1)} %get-tuple-element.66) | copy-start | bytes 4325380
  314.0 13.2 %slice-start = ((s8[5767168]{0:T(1024)(128)(4,1)}), s8[4194304]{0:T(1024)(128)(4,1)S(1)}, s32[]{:S(2)}) async-start(s8[5767168]{0:T(1024)(128)(4,1)} %bitcast.175), calls=%async_computation.6 | async-start | bytes 8388608
  318.8 8.3 %slice-start.1 = ((s8[5767168]{0:T(1024)(128)(4,1)}), s8[1572864]{0:T(1024)(128)(4,1)S(1)}, s32[]{:S(2)}) async-start(s8[5767168]{0:T(1024)(128)(4,1)} %bitcast.175), calls=%async_computation.7 | async-start | bytes 3145728
  323.0 4.2 copy-start.6
  327.2 2.8 copy-start.18
  346.2 3.0 copy-start.19
  348.2 1.0 copy-start.2
  364.1 348.9 %reduce-scatter.5.cloned.1.call-start = ((), (), s32[]{:S(2)}) async-start(), calls=%async_computation.3 | async-start | bytes 7241728 | tf_op jit(solution)/shard_map/reduce_scatter | solution.py:387
  417.7 97.2 %collective-permute-start.13 = (bf16[256,2048]{1,0:T(8,128)(2,1)S(1)}, bf16[256,2048]{1,0:T(8,128)(2,1)S(1)}, u32[]{:S(2)}, u32[]{:S(2)}) collective-permute-start(bf16[256,2048]{1,0:T(8,128)(2,1)S(1)} %get-tuple-element.58), channel_id=1, source_target_pairs={{7,0},{15,8},{23,16},{31,24},{39,32},{47,40},{55,48},{63,56},{71,6... | collective-permute-start | bytes 3145736 | tf_op jit(solution)/shard_map/ppermute | solution.py:336
  419.0 97.2 %collective-permute-start.12 = (bf16[256,2048]{1,0:T(8,128)(2,1)S(1)}, bf16[256,2048]{1,0:T(8,128)(2,1)S(1)}, u32[]{:S(2)}, u32[]{:S(2)}) collective-permute-start(bf16[256,2048]{1,0:T(8,128)(2,1)S(1)} %get-tuple-element.59), channel_id=1, source_target_pairs={{6,0},{7,1},{14,8},{15,9},{22,16},{23,17},{30,24},{31,25},{38,32},... | collective-permute-start | bytes 3145736 | tf_op jit(solution)/shard_map/ppermute | solution.py:336
  420.3 97.6 %collective-permute-start.11 = (bf16[256,2048]{1,0:T(8,128)(2,1)}, bf16[256,2048]{1,0:T(8,128)(2,1)}, u32[]{:S(2)}, u32[]{:S(2)}) collective-permute-start(bf16[256,2048]{1,0:T(8,128)(2,1)} %get-tuple-element.60), channel_id=1, source_target_pairs={{5,0},{6,1},{7,2},{13,8},{14,9},{15,10},{21,16},{22,17},{23,18},{2... | collective-permute-start | bytes 3145736 | tf_op jit(solution)/shard_map/ppermute | solution.py:336
  421.6 101.3 %collective-permute-start.10 = (bf16[256,2048]{1,0:T(8,128)(2,1)}, bf16[256,2048]{1,0:T(8,128)(2,1)}, u32[]{:S(2)}, u32[]{:S(2)}) collective-permute-start(bf16[256,2048]{1,0:T(8,128)(2,1)} %get-tuple-element.61), channel_id=1, source_target_pairs={{4,0},{5,1},{6,2},{7,3},{12,8},{13,9},{14,10},{15,11},{20,16},{21,... | collective-permute-start | bytes 3145736 | tf_op jit(solution)/shard_map/ppermute | solution.py:336
  422.9 100.0 %collective-permute-start.9 = (bf16[256,2048]{1,0:T(8,128)(2,1)}, bf16[256,2048]{1,0:T(8,128)(2,1)}, u32[]{:S(2)}, u32[]{:S(2)}) collective-permute-start(bf16[256,2048]{1,0:T(8,128)(2,1)} %get-tuple-element.62), channel_id=1, source_target_pairs={{3,0},{4,1},{5,2},{6,3},{7,4},{11,8},{12,9},{13,10},{14,11},{15,12... | collective-permute-start | bytes 3145736 | tf_op jit(solution)/shard_map/ppermute | solution.py:336
  514.9 2.6 copy-start.22
  514.9 27.6 %collective-permute-start.8 = (bf16[256,2048]{1,0:T(8,128)(2,1)}, bf16[256,2048]{1,0:T(8,128)(2,1)}, u32[]{:S(2)}, u32[]{:S(2)}) collective-permute-start(bf16[256,2048]{1,0:T(8,128)(2,1)} %get-tuple-element.63), channel_id=1, source_target_pairs={{2,0},{3,1},{4,2},{5,3},{6,4},{7,5},{10,8},{11,9},{12,10},{13,11},... | collective-permute-start | bytes 3145736 | tf_op jit(solution)/shard_map/ppermute | solution.py:336
  516.2 1.3 copy-start.23
  516.2 26.3 %collective-permute-start.7 = (bf16[256,2048]{1,0:T(8,128)(2,1)}, bf16[256,2048]{1,0:T(8,128)(2,1)}, u32[]{:S(2)}, u32[]{:S(2)}) collective-permute-start(bf16[256,2048]{1,0:T(8,128)(2,1)} %get-tuple-element.57), channel_id=1, source_target_pairs={{1,0},{2,1},{3,2},{4,3},{5,4},{6,5},{7,6},{9,8},{10,9},{11,10},{12... | collective-permute-start | bytes 3145736 | tf_op jit(solution)/shard_map/ppermute | solution.py:336
  560.1 1.2 copy-start.15
  560.4 2.0 copy-start.1
  561.3 1.9 copy-start.13
  562.5 1.6 copy-start
  563.2 1.7 copy-start.10
  564.8 1.1 copy-start.9
  568.7 1.0 copy-start.14
  615.5 28.2 %collective-permute-start.17 = (bf16[64,9472]{1,0:T(8,128)(2,1)}, bf16[64,9472]{1,0:T(8,128)(2,1)S(1)}, u32[]{:S(2)}, u32[]{:S(2)}) collective-permute-start(bf16[64,9472]{1,0:T(8,128)(2,1)} %bitcast.196), channel_id=1, source_target_pairs={{0,1},{1,0},{2,3},{3,2},{4,5},{5,4},{6,7},{7,6},{8,9},{9,8},{10,11... | collective-permute-start | bytes 3637256 | tf_op jit(solution)/shard_map/ppermute | solution.py:181
  645.3 30.6 %copy-start.7 = (f32[1,256,1024]{2,1,0:T(8,128)S(1)}, f32[1,256,1024]{2,1,0:T(8,128)}, u32[]{:S(2)}) copy-start(f32[1,256,1024]{2,1,0:T(8,128)} %copy-done.4) | copy-start | bytes 3145732
  645.3 30.6 %copy-start.17 = (bf16[256,2816]{1,0:T(8,128)(2,1)S(1)}, bf16[256,2816]{1,0:T(8,128)(2,1)}, u32[]{:S(2)}) copy-start(bf16[256,2816]{1,0:T(8,128)(2,1)} %copy-done.16) | copy-start | bytes 4325380
  645.3 28.6 %collective-permute-start.18 = (bf16[64,9472]{1,0:T(8,128)(2,1)S(1)}, bf16[64,9472]{1,0:T(8,128)(2,1)S(1)}, u32[]{:S(2)}, u32[]{:S(2)}) collective-permute-start(bf16[64,9472]{1,0:T(8,128)(2,1)S(1)} %add_convert_fusion.2), channel_id=1, source_target_pairs={{0,2},{1,3},{2,0},{3,1},{4,6},{5,7},{6,4},{7,5},{8,10},{9,11},{10,... | collective-permute-start | bytes 3637256 | tf_op jit(solution)/shard_map/ppermute | solution.py:181
  675.2 51.8 %collective-permute-start.19 = (bf16[64,9472]{1,0:T(8,128)(2,1)}, bf16[64,9472]{1,0:T(8,128)(2,1)}, u32[]{:S(2)}, u32[]{:S(2)}) collective-permute-start(bf16[64,9472]{1,0:T(8,128)(2,1)} %add_convert_fusion.1), channel_id=1, source_target_pairs={{0,4},{1,5},{2,6},{3,7},{4,0},{5,1},{6,2},{7,3},{8,12},{9,13},{10,... | collective-permute-start | bytes 3637256 | tf_op jit(solution)/shard_map/ppermute | solution.py:181
  681.4 36.0 %copy-start.3 = (f32[1,256,1024]{2,1,0:T(8,128)S(1)}, f32[1,256,1024]{2,1,0:T(8,128)}, u32[]{:S(2)}) copy-start(f32[1,256,1024]{2,1,0:T(8,128)} %copy-done.2) | copy-start | bytes 3145732
  713.0 10.7 %collective-permute-start.14 = (bf16[208,1024]{1,0:T(8,128)(2,1)}, bf16[208,1024]{1,0:T(8,128)(2,1)S(1)}, u32[]{:S(2)}, u32[]{:S(2)}) collective-permute-start(bf16[208,1024]{1,0:T(8,128)(2,1)} %bitcast.198), channel_id=1, source_target_pairs={{0,1},{1,0},{2,3},{3,2},{4,5},{5,4},{6,7},{7,6},{8,9},{9,8},{10,11... | collective-permute-start | bytes 1277960 | tf_op jit(solution)/shard_map/ppermute | solution.py:181
  714.8 9.0 %copy-start.25 = (bf16[1,208,1024]{2,1,0:T(8,128)(2,1)S(1)}, bf16[1,208,1024]{2,1,0:T(8,128)(2,1)}, u32[]{:S(2)}) copy-start(bf16[1,208,1024]{2,1,0:T(8,128)(2,1)} %reduce-scatter.5.cloned.1.call-done) | copy-start | bytes 1277956
  724.0 11.2 %collective-permute-start.15 = (bf16[208,1024]{1,0:T(8,128)(2,1)S(1)}, bf16[208,1024]{1,0:T(8,128)(2,1)S(1)}, u32[]{:S(2)}, u32[]{:S(2)}) collective-permute-start(bf16[208,1024]{1,0:T(8,128)(2,1)S(1)} %add_convert_fusion.5), channel_id=1, source_target_pairs={{0,2},{1,3},{2,0},{3,1},{4,6},{5,7},{6,4},{7,5},{8,10},{9,11},{10,... | collective-permute-start | bytes 1277960 | tf_op jit(solution)/shard_map/ppermute | solution.py:181
  735.3 9.2 %collective-permute-start.16 = (bf16[208,1024]{1,0:T(8,128)(2,1)S(1)}, bf16[208,1024]{1,0:T(8,128)(2,1)S(1)}, u32[]{:S(2)}, u32[]{:S(2)}) collective-permute-start(bf16[208,1024]{1,0:T(8,128)(2,1)S(1)} %add_convert_fusion.4), channel_id=1, source_target_pairs={{0,4},{1,5},{2,6},{3,7},{4,0},{5,1},{6,2},{7,3},{8,12},{9,13},{10,... | collective-permute-start | bytes 1277960 | tf_op jit(solution)/shard_map/ppermute | solution.py:181
Sparse Core Ops, SparseCore 0:
  12.8 77.4 all-gather.4
  92.7 185.0 all-gather.6
  364.3 251.1 reduce-scatter.2
  619.5 93.4 reduce-scatter.4

commit v4 on v3

--- a/solution.py
+++ b/solution.py
@@ -246,31 +246,42 @@
     upper_mat = mlp_all[:, :, ff:2 * ff].reshape(n_fsdp * w_rows, ff)
     down_mat = mlp_all[:, :, 2 * ff:].reshape(n_fsdp, d_rows, width).reshape(n_fsdp * d_rows, width)
 
+    raw_own = jnp.concatenate([tokens, first_value], axis=-1).reshape(rows, 2 * width)
+    raw_all = jnp.concatenate(
+        [raw_own]
+        + [
+            lax.ppermute(raw_own, "ctx", [(j, j + b) for j in range(n_ctx - b)])
+            for b in range(1, n_ctx)
+        ],
+        axis=0,
+    )
+    block_of = jnp.arange(total_len, dtype=jnp.int32) // rows
+    key_places = (
+        (lax.axis_index("ctx") - block_of) * rows + jnp.arange(total_len, dtype=jnp.int32) % rows
+    )
+    key_cos, key_sin = rope_tables(key_places, head_dim // 2)
+
     tokens_wide = tokens.astype(jnp.float32)
-    first_wide = first_value.astype(jnp.float32)
-    normed, inverse = norm_apply(tokens_wide, prenorm_full.astype(jnp.float32))
-    normed_low = normed.astype(jnp.bfloat16)
+    normed_all, inverse_all = norm_apply(
+        raw_all[:, :width].astype(jnp.float32), prenorm_full.astype(jnp.float32)
+    )
+    normed_all = normed_all.astype(jnp.bfloat16)
+    normed_low = normed_all[:rows].reshape(slots, rows, width)
+    inverse = inverse_all[:rows].reshape(slots, rows, 1)
     query = jnp.dot(normed_low, query_mat, preferred_element_type=jnp.float32)
-    keyed = jnp.dot(normed_low, key_mat, preferred_element_type=jnp.float32)
-    own_value = jnp.dot(normed_low, value_mat, preferred_element_type=jnp.float32)
+    keyed = jnp.dot(normed_all, key_mat, preferred_element_type=jnp.float32)
+    own_value = jnp.dot(normed_all, value_mat, preferred_element_type=jnp.float32)
     heads_shape = query.shape[:2] + (head_count, head_dim)
     query_rotated_rows = rotate(query.reshape(heads_shape), cos_rows, sin_rows).astype(jnp.bfloat16)
     key_rot = (
-        rotate(keyed.reshape(heads_shape), cos_rows, sin_rows)
+        rotate(
+            keyed.reshape(total_len, head_count, head_dim), key_cos[:, None, :], key_sin[:, None, :]
+        )
         .astype(jnp.bfloat16)
-        .reshape(query.shape)
-    )
-    value_mix = (0.5 * own_value + 0.5 * first_wide).astype(jnp.bfloat16)
-
-    kv_own = jnp.concatenate([key_rot, value_mix], axis=-1).reshape(rows, 2 * width)
-    kv_all = jnp.concatenate(
-        [kv_own]
-        + [
-            lax.ppermute(kv_own, "ctx", [(j, j + b) for j in range(n_ctx - b)])
-            for b in range(1, n_ctx)
-        ],
-        axis=0,
-    )
+        .reshape(total_len, width)
+    )
+    value_mix = (0.5 * own_value + 0.5 * raw_all[:, width:].astype(jnp.float32)).astype(jnp.bfloat16)
+    kv_all = jnp.concatenate([key_rot, value_mix], axis=-1)
     meta = jnp.stack([lax.axis_index("ctx") * rows, slot_lengths[0]]).astype(jnp.int32)
     query_flat = query_rotated_rows.reshape(rows, width)
     mixed_low = attention_forward(

time: 760 us -> 779 us (1.025)
  other arithmetic: 44.3 us -> 56.8 us
  matrix products: 54.9 us -> 66.3 us
    all_gather x1, waiting for transfers between devices: 74.6 us -> 3.49 us  [body(): attn_all = lax.all_gather(attn_pack, 'fsdp', axis=0, tiled=False)]
    all_gather x1, waiting for transfers between devices: 5.49 us -> 56.9 us  [body(): mlp_all = lax.all_gather(mlp_pack, 'fsdp', axis=0, tiled=False)]
    ppermute x7, waiting for transfers between devices: 80.1 us -> 106 us  [body(): lax.ppermute(raw_own, 'ctx', [(j, j + b) for j in range(n_ctx - b)])]
    dot_general x2, matrix products: 5 us -> 17.7 us  [the longest x1 10.7 us: body(): jnp.dot(normed_all, value_mat, preferred_element_type=jnp.float32)]
    ppermute x7, waiting for transfers between devices: 115 us -> 103 us  [body(): lax.ppermute(kv_back[b_shift], 'ctx', [(j, j - b_shift) for j in range(b_...]
    concatenate x0 -> x1, other arithmetic: none -> 8.31 us  [body(): kv_all = jnp.concatenate([key_rot, value_mix], axis=-1)]
    unnamed x76 -> x78, local copies, waits for them, and re-layouts: 28.2 us -> 23.3 us
  transfers between devices with their start and end apart: 24 -> 24, of which waited for: 15 -> 17; matrix products, arithmetic and copies ran while one was open for 14% -> 17% of each run, Pallas kernels for 9% -> 9%
where the time goes in v4:
time: 779 us; the launch traced here: 773 us
  waiting for transfers between devices  416 us (53%)
  local copies, waits for them, and re-layouts  107 us (14%)
  Pallas kernels  71.9 us (9%)
  matrix products  66.3 us (9%)
  other arithmetic  56.8 us (7%)
  starting transfers between devices  40.1 us (5%)
  between operations  15 us (2%)
    ppermute x7, waiting for transfers between devices, body(): lax.ppermute(raw_own, 'ctx', [(j, j + b) for j in range(n_ctx - b)])  106 us
    ppermute x7, waiting for transfers between devices, body(): lax.ppermute(kv_back[b_shift], 'ctx', [(j, j - b_shift) for j in range(b_...  103 us
    ppermute x6, waiting for transfers between devices, ctx_allreduce(): other = lax.ppermute(total, 'ctx', [(j, j ^ step) for j in range(n_ctx)])  68.8 us
    all_gather x1, waiting for transfers between devices, body(): mlp_all = lax.all_gather(mlp_pack, 'fsdp', axis=0, tiled=False)  56.9 us
    pallas_call x1, Pallas kernels, attention_backward(): pl.pallas_call(functools.partial(attn_bwd_kernel, head_dim, scale), out_s...  45.3 us
    reduce_scatter x1, waiting for transfers between devices, body(): lax.psum_scatter(mlp_grads, 'fsdp', scatter_dimension=0, tiled=False)  43.7 us
    reduce_scatter x1, waiting for transfers between devices, body(): lax.psum_scatter(attn_grads, 'fsdp', scatter_dimension=0, tiled=False)  34.1 us
    pallas_call x1, Pallas kernels, attention_forward(): pl.pallas_call(functools.partial(attn_fwd_kernel, head_dim, scale), out_s...  26.7 us
  transfers between devices with their start and end apart: 24, of which 17 were waited for; matrix products, arithmetic and copies ran while one was open for 17% of the time, Pallas kernels for 9%

profile of v4, /device:TPU:0, one launch (start us, length us, event | category | flops | bytes accessed | tf_op | source)
XLA Modules:
  0.0 773.2 jit_solution(10994270545492147225)
XLA Ops:
  14.1 2.2 pad_maximum_fusion.3
  16.5 4.9 collective-permute-start.4
  21.4 2.3 collective-permute-start.3
  23.7 4.6 collective-permute-start.2
  28.4 3.2 collective-permute-start.1
  31.6 2.4 collective-permute-start
  34.8 1.8 multiply_cosine_fusion
  38.3 66.6 %collective-permute-done = bf16[256,2048]{1,0:T(8,128)(2,1)} collective-permute-done((bf16[256,2048]{1,0:T(8,128)(2,1)S(1)}, bf16[256,2048]{1,0:T(8,128)(2,1)}, u32[]{:S(2)}, u32[]{:S(2)}) %collective-permute-start) | collective-permute-done | bytes 1048608 | tf_op jit(solution)/shard_map/ppermute | solution.py:253
  111.6 6.9 collective-permute-done.3
  119.9 8.0 %collective-permute-done.5 = bf16[256,2048]{1,0:T(8,128)(2,1)S(1)} collective-permute-done((bf16[256,2048]{1,0:T(8,128)(2,1)S(1)}, bf16[256,2048]{1,0:T(8,128)(2,1)S(1)}, u32[]{:S(2)}, u32[]{:S(2)}) %collective-permute-start.5) | collective-permute-done | bytes 1048608 | tf_op jit(solution)/shard_map/ppermute | solution.py:253
  128.0 24.5 %collective-permute-done.6 = bf16[256,2048]{1,0:T(8,128)(2,1)S(1)} collective-permute-done((bf16[256,2048]{1,0:T(8,128)(2,1)S(1)}, bf16[256,2048]{1,0:T(8,128)(2,1)S(1)}, u32[]{:S(2)}, u32[]{:S(2)}) %collective-permute-start.6) | collective-permute-done | bytes 1048608 | tf_op jit(solution)/shard_map/ppermute | solution.py:253
  152.6 3.2 copy-done.6
  156.7 3.5 all-gather.5.cloned.1.call-done
  161.2 6.0 fusion.61
  167.2 4.0 copy.59
  171.2 4.0 copy.60
  175.1 2.9 fusion.3
  180.4 7.0 fusion.5
  188.8 2.2 pad_maximum_fusion.2
  191.0 6.3 copy.62
  197.3 10.7 %multiply_convert_fusion = bf16[2048,1024]{1,0:T(8,128)(2,1)} fusion(bf16[2048,2048]{1,0:T(8,128)(2,1)} %copy-done.6, bf16[2048,1024]{1,0:T(8,128)(2,1)} %copy-done.12, bf16[1024,1024]{1,0:T(8,128)(2,1)} %bitcast.157), kind=kOutput, calls=%fused_computation.9 | convolution fusion | flops 4303355904 | bytes 14680064 | tf_op jit(solution)/shard_map/dot_general | solution.py:273
  208.0 8.3 %pad_maximum_fusion.1.k_ref.v_ref = bf16[2048,2048]{1,0:T(8,128)(2,1)} fusion(bf16[2048,1024]{1,0:T(8,128)(2,1)} %multiply_convert_fusion, bf16[2048,1024]{1,0:T(8,128)(2,1)} %copy.62), kind=kLoop, calls=%fused_computation.8 | loop fusion | flops 16777216 | bytes 16777216 | tf_op jit(solution)/shard_map/concatenate | solution.py:284
  216.3 26.7 %shard_map.229 = bf16[256,1024]{1,0:T(8,128)(2,1)S(1)} custom-call(s32[2]{0:T(128)S(1)} %pad_add_fusion.meta_ref, bf16[256,1024]{1,0:T(8,128)(2,1)S(1)} %copy.63.q_ref, bf16[2048,2048]{1,0:T(8,128)(2,1)} %pad_maximum_fusion.1.k_ref.v_ref, bf16[2048,2048]{1,0:T(8,128)(2,1)} %pad_maximum_fusion.1.k_ref.v_ref), custom_call_target="tpu_custom_call" | custom-call | flops 2147483648 | bytes 9437184 | tf_op jit(solution)/shard_map/pallas_call | solution.py:79
  244.0 1.9 multiply_reduce_fusion
  249.0 56.9 %all-gather.7.cloned.1.call-done = bf16[1024,8448]{1,0:T(8,128)(2,1)} async-done(((bf16[64,8448]{1,0:T(8,128)(2,1)}), bf16[1024,8448]{1,0:T(8,128)(2,1)}) %all-gather.7.cloned.1.call-update) | async-done | bytes 17301520 | tf_op jit(solution)/shard_map/all_gather | solution.py:244
  305.9 11.4 %fusion.60 = (bf16[16,64,2816]{2,1,0:T(8,128)(2,1)}, bf16[16,64,2816]{2,1,0:T(8,128)(2,1)}, bf16[16,64,2816]{2,1,0:T(8,128)(2,1)}) fusion(bf16[16,64,8448]{2,1,0:T(8,128)(2,1)} %bitcast.154), kind=kLoop, calls=%fused_computation.151 | loop fusion | bytes 34603008 | tf_op jit(solution)/shard_map/slice | solution.py:247
  317.3 11.7 %reshape_reshape.7 = bf16[2816,1024]{1,0:T(8,128)(2,1)} reshape(bf16[16,64,2816]{2,1,0:T(8,128)(2,1)} %get-tuple-element.50) | data formatting | bytes 11534336 | tf_op jit(solution)/shard_map/reshape;reshape | solution.py:247
  329.0 4.8 fusion.29
  333.9 3.3 fusion.31
  337.2 6.2 multiply_convert_fusion.1
  345.2 4.1 convolution_convert_fusion.2
  349.3 4.1 convolution_convert_fusion.1
  353.4 2.8 fusion.22
  356.2 4.2 convolution_convert_fusion
  360.4 11.8 %reshape_reshape.8 = bf16[16,64,2816]{2,1,0:T(8,128)(2,1)} reshape(bf16[2816,1024]{1,0:T(8,128)(2,1)} %convolution_convert_fusion) | data formatting | bytes 11534336 | tf_op jit(solution)/shard_map/reshape;reshape | solution.py:330
  372.1 2.0 fusion.24
  375.1 1.8 convolution_convert_fusion.3
  376.9 14.2 %pad_maximum_fusion = bf16[16,64,9472]{2,1,0:T(8,128)(2,1)} fusion(bf16[16,64,1024]{2,1,0:T(8,128)(2,1)S(1)} %convolution_convert_fusion.3, bf16[16,64,2816]{2,1,0:T(8,128)(2,1)} %reshape_reshape.8, bf16[16,64,2816]{2,1,0:T(8,128)(2,1)} %convolution_convert_fusion.1, bf16[16,64,2816]{2,1,0:T(8,128)(2,1)} %convolution_convert_fusion.2), kind=kLoop, calls=%fused_computation | loop fusion | flops 77594624 | bytes 38797312 | tf_op jit(solution)/shard_map/concatenate | solution.py:326
  391.1 2.0 convolution_convert_fusion.7.do_ref
  393.1 45.3 %shard_map.230 = (f32[256,1024]{1,0:T(8,128)S(1)}, bf16[2048,2048]{1,0:T(8,128)(2,1)}) custom-call(s32[2]{0:T(128)S(1)} %pad_add_fusion.meta_ref, bf16[256,1024]{1,0:T(8,128)(2,1)S(1)} %copy.63.q_ref, bf16[2048,2048]{1,0:T(8,128)(2,1)} %pad_maximum_fusion.1.k_ref.v_ref, bf16[2048,2048]{1,0:T(8,128)(2,1)} %pad_maximum_fusion.1.k_ref.v_ref, ...), custom_call_target="tpu_custom_call" | custom-call | flops 5368709120 | bytes 19398656 | tf_op jit(solution)/shard_map/pallas_call | solution.py:107
  438.4 5.7 fusion.62
  450.6 20.8 %collective-permute-done.7 = bf16[256,2048]{1,0:T(8,128)(2,1)S(1)} collective-permute-done((bf16[256,2048]{1,0:T(8,128)(2,1)S(1)}, bf16[256,2048]{1,0:T(8,128)(2,1)S(1)}, u32[]{:S(2)}, u32[]{:S(2)}) %collective-permute-start.7) | collective-permute-done | bytes 1048608 | tf_op jit(solution)/shard_map/ppermute | solution.py:347
  472.6 59.0 %collective-permute-done.13 = bf16[256,2048]{1,0:T(8,128)(2,1)S(1)} collective-permute-done((bf16[256,2048]{1,0:T(8,128)(2,1)S(1)}, bf16[256,2048]{1,0:T(8,128)(2,1)S(1)}, u32[]{:S(2)}, u32[]{:S(2)}) %collective-permute-start.13) | collective-permute-done | bytes 1048608 | tf_op jit(solution)/shard_map/ppermute | solution.py:347
  535.6 20.8 %collective-permute-done.10 = bf16[256,2048]{1,0:T(8,128)(2,1)} collective-permute-done((bf16[256,2048]{1,0:T(8,128)(2,1)}, bf16[256,2048]{1,0:T(8,128)(2,1)}, u32[]{:S(2)}, u32[]{:S(2)}) %collective-permute-start.10) | collective-permute-done | bytes 1048608 | tf_op jit(solution)/shard_map/ppermute | solution.py:347
  556.4 2.9 collective-permute-done.8
  559.3 5.1 convert_add_fusion
  564.4 3.1 reshape.574
  567.5 5.1 fusion.64
  572.6 2.1 copy.83
  574.7 2.4 copy.66
  581.3 1.9 fusion.20
  585.7 3.3 fusion.4
  589.0 43.7 %reduce-scatter.3.cloned.1.call-done = bf16[1,64,9472]{2,1,0:T(8,128)(2,1)} async-done(((bf16[16,64,9472]{2,1,0:T(8,128)(2,1)}), bf16[1,64,9472]{2,1,0:T(8,128)(2,1)}) %reduce-scatter.3.cloned.1.call-update) | async-done | bytes 1212432 | tf_op jit(solution)/shard_map/reduce_scatter | solution.py:335
  635.5 26.4 %collective-permute-done.17 = bf16[64,9472]{1,0:T(8,128)(2,1)S(1)} collective-permute-done((bf16[64,9472]{1,0:T(8,128)(2,1)S(1)}, bf16[64,9472]{1,0:T(8,128)(2,1)S(1)}, u32[]{:S(2)}, u32[]{:S(2)}) %collective-permute-start.17) | collective-permute-done | bytes 1212448 | tf_op jit(solution)/shard_map/ppermute | solution.py:181
  662.2 3.0 collective-permute-start.18
  665.2 25.5 %collective-permute-done.18 = bf16[64,9472]{1,0:T(8,128)(2,1)S(1)} collective-permute-done((bf16[64,9472]{1,0:T(8,128)(2,1)S(1)}, bf16[64,9472]{1,0:T(8,128)(2,1)S(1)}, u32[]{:S(2)}, u32[]{:S(2)}) %collective-permute-start.18) | collective-permute-done | bytes 1212448 | tf_op jit(solution)/shard_map/ppermute | solution.py:181
  691.8 5.3 fusion.11
  697.1 34.1 %reduce-scatter.5.cloned.1.call-done = bf16[1,208,1024]{2,1,0:T(8,128)(2,1)} async-done(((bf16[16,208,1024]{2,1,0:T(8,128)(2,1)}), bf16[1,208,1024]{2,1,0:T(8,128)(2,1)}) %reduce-scatter.5.cloned.1.call-update) | async-done | bytes 426000 | tf_op jit(solution)/shard_map/reduce_scatter | solution.py:398
  733.0 2.5 copy.75
  735.6 2.6 fusion.17
  738.1 4.6 collective-permute-done.14
  743.8 3.1 collective-permute-start.15
  749.1 6.2 collective-permute-done.15
  758.4 6.1 collective-permute-done.16
  (165 shorter events, 62.4 us)
Async XLA Ops:
  7.2 9.2 %copy-start.4 = (bf16[1,256,1024]{2,1,0:T(8,128)(2,1)S(1)}, bf16[1,256,1024]{2,1,0:T(8,128)(2,1)}, u32[]{:S(2)}) copy-start(bf16[1,256,1024]{2,1,0:T(8,128)(2,1)} %param.14) | copy-start | bytes 1572868
  7.2 9.2 %copy-start.20 = (bf16[1,256,1024]{2,1,0:T(8,128)(2,1)S(1)}, bf16[1,256,1024]{2,1,0:T(8,128)(2,1)}, u32[]{:S(2)}) copy-start(bf16[1,256,1024]{2,1,0:T(8,128)(2,1)} %param.15) | copy-start | bytes 1572868
  7.2 26.9 %copy-start.28 = (s32[16]{0:T(128)S(1)}, s32[16]{0:T(128)}, u32[]{:S(2)}) copy-start(s32[16]{0:T(128)} %param.27) | copy-start | bytes 196
  7.2 26.9 %copy-start.27 = (s32[16]{0:T(128)S(1)}, s32[16]{0:T(128)}, u32[]{:S(2)}) copy-start(s32[16]{0:T(128)} %param.26) | copy-start | bytes 196
  7.2 152.9 %all-gather.5.cloned.1.call-start = ((), (), s32[]{:S(2)}) async-start(), calls=%async_computation.4 | async-start | bytes 9469952 | tf_op jit(solution)/shard_map/all_gather | solution.py:232
  11.8 0.8 copy-start.25
  12.6 293.3 %all-gather.7.cloned.1.call-start = ((), (), s32[]{:S(2)}) async-start(), calls=%async_computation.5 | async-start | bytes 18382848 | tf_op jit(solution)/shard_map/all_gather | solution.py:244
  16.4 616.3 %reduce-scatter.3.cloned.1.call-start = ((), (), s32[]{:S(2)}) async-start(), calls=%async_computation.2 | async-start | bytes 20611072 | tf_op jit(solution)/shard_map/reduce_scatter | solution.py:335
  16.5 103.3 %collective-permute-start.4 = (bf16[256,2048]{1,0:T(8,128)(2,1)S(1)}, bf16[256,2048]{1,0:T(8,128)(2,1)S(1)}, u32[]{:S(2)}, u32[]{:S(2)}) collective-permute-start(bf16[256,2048]{1,0:T(8,128)(2,1)S(1)} %maximum_bitcast_fusion), channel_id=1, source_target_pairs={{0,5},{1,6},{2,7},{8,13},{9,14},{10,15},{16,21},{17,22},{18,23},{2... | collective-permute-start | bytes 3145736 | tf_op jit(solution)/shard_map/ppermute | solution.py:253
  21.4 97.1 %collective-permute-start.3 = (bf16[256,2048]{1,0:T(8,128)(2,1)S(1)}, bf16[256,2048]{1,0:T(8,128)(2,1)}, u32[]{:S(2)}, u32[]{:S(2)}) collective-permute-start(bf16[256,2048]{1,0:T(8,128)(2,1)S(1)} %maximum_bitcast_fusion), channel_id=1, source_target_pairs={{0,4},{1,5},{2,6},{3,7},{8,12},{9,13},{10,14},{11,15},{16,20},{17,... | collective-permute-start | bytes 3145736 | tf_op jit(solution)/shard_map/ppermute | solution.py:253
  23.7 86.5 %collective-permute-start.2 = (bf16[256,2048]{1,0:T(8,128)(2,1)S(1)}, bf16[256,2048]{1,0:T(8,128)(2,1)}, u32[]{:S(2)}, u32[]{:S(2)}) collective-permute-start(bf16[256,2048]{1,0:T(8,128)(2,1)S(1)} %maximum_bitcast_fusion), channel_id=1, source_target_pairs={{0,3},{1,4},{2,5},{3,6},{4,7},{8,11},{9,12},{10,13},{11,14},{12,15... | collective-permute-start | bytes 3145736 | tf_op jit(solution)/shard_map/ppermute | solution.py:253
  28.4 79.2 %collective-permute-start.1 = (bf16[256,2048]{1,0:T(8,128)(2,1)S(1)}, bf16[256,2048]{1,0:T(8,128)(2,1)}, u32[]{:S(2)}, u32[]{:S(2)}) collective-permute-start(bf16[256,2048]{1,0:T(8,128)(2,1)S(1)} %maximum_bitcast_fusion), channel_id=1, source_target_pairs={{0,2},{1,3},{2,4},{3,5},{4,6},{5,7},{8,10},{9,11},{10,12},{11,13},... | collective-permute-start | bytes 3145736 | tf_op jit(solution)/shard_map/ppermute | solution.py:253
  31.6 73.3 %collective-permute-start = (bf16[256,2048]{1,0:T(8,128)(2,1)S(1)}, bf16[256,2048]{1,0:T(8,128)(2,1)}, u32[]{:S(2)}, u32[]{:S(2)}) collective-permute-start(bf16[256,2048]{1,0:T(8,128)(2,1)S(1)} %maximum_bitcast_fusion), channel_id=1, source_target_pairs={{0,1},{1,2},{2,3},{3,4},{4,5},{5,6},{6,7},{8,9},{9,10},{10,11},{11... | collective-permute-start | bytes 3145736 | tf_op jit(solution)/shard_map/ppermute | solution.py:253
  104.9 23.1 %collective-permute-start.5 = (bf16[256,2048]{1,0:T(8,128)(2,1)S(1)}, bf16[256,2048]{1,0:T(8,128)(2,1)S(1)}, u32[]{:S(2)}, u32[]{:S(2)}) collective-permute-start(bf16[256,2048]{1,0:T(8,128)(2,1)S(1)} %maximum_bitcast_fusion), channel_id=1, source_target_pairs={{0,6},{1,7},{8,14},{9,15},{16,22},{17,23},{24,30},{25,31},{32,38},... | collective-permute-start | bytes 3145736 | tf_op jit(solution)/shard_map/ppermute | solution.py:253
  107.6 44.9 %collective-permute-start.6 = (bf16[256,2048]{1,0:T(8,128)(2,1)S(1)}, bf16[256,2048]{1,0:T(8,128)(2,1)S(1)}, u32[]{:S(2)}, u32[]{:S(2)}) collective-permute-start(bf16[256,2048]{1,0:T(8,128)(2,1)S(1)} %maximum_bitcast_fusion), channel_id=1, source_target_pairs={{0,7},{8,15},{16,23},{24,31},{32,39},{40,47},{48,55},{56,63},{64,7... | collective-permute-start | bytes 3145736 | tf_op jit(solution)/shard_map/ppermute | solution.py:253
  152.6 3.2 copy-start.6
  175.1 3.0 copy-start.7
  178.1 2.1 copy-start.12
  180.3 7.1 copy-start.24
  245.9 1.0 copy-start.8
  329.0 4.8 copy-start.9
  329.0 4.9 copy-start.13
  329.0 8.2 %slice-start = ((s8[5767168]{0:T(1024)(128)(4,1)}), s8[4194304]{0:T(1024)(128)(4,1)S(1)}, s32[]{:S(2)}) async-start(s8[5767168]{0:T(1024)(128)(4,1)} %bitcast.164), calls=%async_computation.6 | async-start | bytes 8388608
  333.8 3.4 slice-start.1
  333.9 3.3 copy-start.18
  343.5 12.7 %copy-start.16 = (bf16[256,2816]{1,0:T(8,128)(2,1)}, bf16[256,2816]{1,0:T(8,128)(2,1)S(1)}, u32[]{:S(2)}) copy-start(bf16[256,2816]{1,0:T(8,128)(2,1)S(1)} %get-tuple-element.68) | copy-start | bytes 4325380
  345.2 8.2 %slice-start.2 = ((s8[5767168]{0:T(1024)(128)(4,1)}), s8[4194304]{0:T(1024)(128)(4,1)S(1)}, s32[]{:S(2)}) async-start(s8[5767168]{0:T(1024)(128)(4,1)} %bitcast.167), calls=%async_computation.8 | async-start | bytes 8388608
  349.3 4.1 slice-start.3
  360.4 11.8 %copy-start.19 = (bf16[1,256,1024]{2,1,0:T(8,128)(2,1)S(1)}, bf16[1,256,1024]{2,1,0:T(8,128)(2,1)}, u32[]{:S(2)}) copy-start(bf16[1,256,1024]{2,1,0:T(8,128)(2,1)} %param.25) | copy-start | bytes 1572868
  374.1 1.0 copy-start.2
  391.1 340.2 %reduce-scatter.5.cloned.1.call-start = ((), (), s32[]{:S(2)}) async-start(), calls=%async_computation.3 | async-start | bytes 7241728 | tf_op jit(solution)/shard_map/reduce_scatter | solution.py:398
  444.1 27.2 %collective-permute-start.7 = (bf16[256,2048]{1,0:T(8,128)(2,1)S(1)}, bf16[256,2048]{1,0:T(8,128)(2,1)S(1)}, u32[]{:S(2)}, u32[]{:S(2)}) collective-permute-start(bf16[256,2048]{1,0:T(8,128)(2,1)S(1)} %get-tuple-element.59), channel_id=1, source_target_pairs={{1,0},{2,1},{3,2},{4,3},{5,4},{6,5},{7,6},{9,8},{10,9},{11,10},{12... | collective-permute-start | bytes 3145736 | tf_op jit(solution)/shard_map/ppermute | solution.py:347
  445.4 86.3 %collective-permute-start.13 = (bf16[256,2048]{1,0:T(8,128)(2,1)S(1)}, bf16[256,2048]{1,0:T(8,128)(2,1)S(1)}, u32[]{:S(2)}, u32[]{:S(2)}) collective-permute-start(bf16[256,2048]{1,0:T(8,128)(2,1)S(1)} %get-tuple-element.60), channel_id=1, source_target_pairs={{7,0},{15,8},{23,16},{31,24},{39,32},{47,40},{55,48},{63,56},{71,6... | collective-permute-start | bytes 3145736 | tf_op jit(solution)/shard_map/ppermute | solution.py:347
  446.7 89.0 %collective-permute-start.12 = (bf16[256,2048]{1,0:T(8,128)(2,1)}, bf16[256,2048]{1,0:T(8,128)(2,1)}, u32[]{:S(2)}, u32[]{:S(2)}) collective-permute-start(bf16[256,2048]{1,0:T(8,128)(2,1)} %get-tuple-element.61), channel_id=1, source_target_pairs={{6,0},{7,1},{14,8},{15,9},{22,16},{23,17},{30,24},{31,25},{38,32},... | collective-permute-start | bytes 3145736 | tf_op jit(solution)/shard_map/ppermute | solution.py:347
  448.0 87.7 %collective-permute-start.11 = (bf16[256,2048]{1,0:T(8,128)(2,1)}, bf16[256,2048]{1,0:T(8,128)(2,1)}, u32[]{:S(2)}, u32[]{:S(2)}) collective-permute-start(bf16[256,2048]{1,0:T(8,128)(2,1)} %get-tuple-element.62), channel_id=1, source_target_pairs={{5,0},{6,1},{7,2},{13,8},{14,9},{15,10},{21,16},{22,17},{23,18},{2... | collective-permute-start | bytes 3145736 | tf_op jit(solution)/shard_map/ppermute | solution.py:347
  449.3 107.1 %collective-permute-start.10 = (bf16[256,2048]{1,0:T(8,128)(2,1)}, bf16[256,2048]{1,0:T(8,128)(2,1)}, u32[]{:S(2)}, u32[]{:S(2)}) collective-permute-start(bf16[256,2048]{1,0:T(8,128)(2,1)} %get-tuple-element.63), channel_id=1, source_target_pairs={{4,0},{5,1},{6,2},{7,3},{12,8},{13,9},{14,10},{15,11},{20,16},{21,... | collective-permute-start | bytes 3145736 | tf_op jit(solution)/shard_map/ppermute | solution.py:347
  471.3 61.6 %copy-start.22 = (bf16[256,2048]{1,0:T(8,128)(2,1)}, bf16[256,2048]{1,0:T(8,128)(2,1)S(1)}, u32[]{:S(2)}) copy-start(bf16[256,2048]{1,0:T(8,128)(2,1)S(1)} %collective-permute-done.7) | copy-start | bytes 3145732
  471.3 85.1 %collective-permute-start.9 = (bf16[256,2048]{1,0:T(8,128)(2,1)}, bf16[256,2048]{1,0:T(8,128)(2,1)}, u32[]{:S(2)}, u32[]{:S(2)}) collective-permute-start(bf16[256,2048]{1,0:T(8,128)(2,1)} %get-tuple-element.64), channel_id=1, source_target_pairs={{3,0},{4,1},{5,2},{6,3},{7,4},{11,8},{12,9},{13,10},{14,11},{15,12... | collective-permute-start | bytes 3145736 | tf_op jit(solution)/shard_map/ppermute | solution.py:347
  531.6 1.3 copy-start.23
  531.6 27.6 %collective-permute-start.8 = (bf16[256,2048]{1,0:T(8,128)(2,1)}, bf16[256,2048]{1,0:T(8,128)(2,1)}, u32[]{:S(2)}, u32[]{:S(2)}) collective-permute-start(bf16[256,2048]{1,0:T(8,128)(2,1)} %get-tuple-element.65), channel_id=1, source_target_pairs={{2,0},{3,1},{4,2},{5,3},{6,4},{7,5},{10,8},{11,9},{12,10},{13,11},... | collective-permute-start | bytes 3145736 | tf_op jit(solution)/shard_map/ppermute | solution.py:347
  567.5 9.6 %copy-start.14 = (f32[256,1024]{0,1:T(8,128)S(1)}, f32[256,1024]{0,1:T(8,128)}, u32[]{:S(2)}) copy-start(f32[256,1024]{0,1:T(8,128)} %copy.65) | copy-start | bytes 3145732
  577.0 1.2 copy-start.15
  577.1 2.3 copy-start.1
  577.4 2.8 copy-start
  579.4 1.6 copy-start.5
  579.4 1.9 copy-start.11
  632.7 1.3 copy-start.21
  634.0 57.8 %copy-start.10 = (f32[1,256,1024]{2,1,0:T(8,128)S(1)}, f32[1,256,1024]{2,1,0:T(8,128)}, u32[]{:S(2)}) copy-start(f32[1,256,1024]{2,1,0:T(8,128)} %copy-done.8) | copy-start | bytes 3145732
  634.0 57.8 %copy-start.17 = (bf16[256,2816]{1,0:T(8,128)(2,1)S(1)}, bf16[256,2816]{1,0:T(8,128)(2,1)}, u32[]{:S(2)}) copy-start(bf16[256,2816]{1,0:T(8,128)(2,1)} %copy-done.16) | copy-start | bytes 4325380
  634.0 27.9 %collective-permute-start.17 = (bf16[64,9472]{1,0:T(8,128)(2,1)S(1)}, bf16[64,9472]{1,0:T(8,128)(2,1)S(1)}, u32[]{:S(2)}, u32[]{:S(2)}) collective-permute-start(bf16[64,9472]{1,0:T(8,128)(2,1)S(1)} %bitcast.186), channel_id=1, source_target_pairs={{0,1},{1,0},{2,3},{3,2},{4,5},{5,4},{6,7},{7,6},{8,9},{9,8},{10,11... | collective-permute-start | bytes 3637256 | tf_op jit(solution)/shard_map/ppermute | solution.py:181
  662.2 28.6 %collective-permute-start.18 = (bf16[64,9472]{1,0:T(8,128)(2,1)S(1)}, bf16[64,9472]{1,0:T(8,128)(2,1)S(1)}, u32[]{:S(2)}, u32[]{:S(2)}) collective-permute-start(bf16[64,9472]{1,0:T(8,128)(2,1)S(1)} %add_convert_fusion.3), channel_id=1, source_target_pairs={{0,2},{1,3},{2,0},{3,1},{4,6},{5,7},{6,4},{7,5},{8,10},{9,11},{10,... | collective-permute-start | bytes 3637256 | tf_op jit(solution)/shard_map/ppermute | solution.py:181
  691.0 44.5 %copy-start.3 = (f32[1,256,1024]{2,1,0:T(8,128)S(1)}, f32[1,256,1024]{2,1,0:T(8,128)}, u32[]{:S(2)}) copy-start(f32[1,256,1024]{2,1,0:T(8,128)} %copy-done.2) | copy-start | bytes 3145732
  691.0 55.9 %collective-permute-start.19 = (bf16[64,9472]{1,0:T(8,128)(2,1)S(1)}, bf16[64,9472]{1,0:T(8,128)(2,1)}, u32[]{:S(2)}, u32[]{:S(2)}) collective-permute-start(bf16[64,9472]{1,0:T(8,128)(2,1)S(1)} %add_convert_fusion.2), channel_id=1, source_target_pairs={{0,4},{1,5},{2,6},{3,7},{4,0},{5,1},{6,2},{7,3},{8,12},{9,13},{10,... | collective-permute-start | bytes 3637256 | tf_op jit(solution)/shard_map/ppermute | solution.py:181
  731.3 11.4 %copy-start.26 = (bf16[1,208,1024]{2,1,0:T(8,128)(2,1)S(1)}, bf16[1,208,1024]{2,1,0:T(8,128)(2,1)}, u32[]{:S(2)}) copy-start(bf16[1,208,1024]{2,1,0:T(8,128)(2,1)} %reduce-scatter.5.cloned.1.call-done) | copy-start | bytes 1277956
  731.3 11.4 %collective-permute-start.14 = (bf16[208,1024]{1,0:T(8,128)(2,1)}, bf16[208,1024]{1,0:T(8,128)(2,1)}, u32[]{:S(2)}, u32[]{:S(2)}) collective-permute-start(bf16[208,1024]{1,0:T(8,128)(2,1)} %bitcast.188), channel_id=1, source_target_pairs={{0,1},{1,0},{2,3},{3,2},{4,5},{5,4},{6,7},{7,6},{8,9},{9,8},{10,11... | collective-permute-start | bytes 1277960 | tf_op jit(solution)/shard_map/ppermute | solution.py:181
  743.8 11.5 %collective-permute-start.15 = (bf16[208,1024]{1,0:T(8,128)(2,1)S(1)}, bf16[208,1024]{1,0:T(8,128)(2,1)S(1)}, u32[]{:S(2)}, u32[]{:S(2)}) collective-permute-start(bf16[208,1024]{1,0:T(8,128)(2,1)S(1)} %add_convert_fusion.6), channel_id=1, source_target_pairs={{0,2},{1,3},{2,0},{3,1},{4,6},{5,7},{6,4},{7,5},{8,10},{9,11},{10,... | collective-permute-start | bytes 1277960 | tf_op jit(solution)/shard_map/ppermute | solution.py:181
  755.5 9.1 %collective-permute-start.16 = (bf16[208,1024]{1,0:T(8,128)(2,1)S(1)}, bf16[208,1024]{1,0:T(8,128)(2,1)S(1)}, u32[]{:S(2)}, u32[]{:S(2)}) collective-permute-start(bf16[208,1024]{1,0:T(8,128)(2,1)S(1)} %add_convert_fusion.5), channel_id=1, source_target_pairs={{0,4},{1,5},{2,6},{3,7},{4,0},{5,1},{6,2},{7,3},{8,12},{9,13},{10,... | collective-permute-start | bytes 1277960 | tf_op jit(solution)/shard_map/ppermute | solution.py:181
Sparse Core Ops, SparseCore 0:
  12.7 147.3 all-gather.4
  162.6 143.2 all-gather.6
  391.2 241.4 reduce-scatter.2
  636.7 94.5 reduce-scatter.4

commit v5 on v3

--- a/solution.py
+++ b/solution.py
@@ -24,11 +24,9 @@
 def attention_shares(query, keys, first_row, slot_len, scale):
     scores = lax.dot_general(query, keys, NT_DIMS, preferred_element_type=jnp.float32) * scale
     shape = scores.shape
-    rows = query.shape[0]
     query_pos = first_row + lax.broadcasted_iota(jnp.int32, shape, 0)
-    key_row = lax.broadcasted_iota(jnp.int32, shape, 1)
-    key_pos = first_row + key_row - 2 * rows * (key_row // rows)
-    allowed = (key_pos >= 0) & (key_pos <= query_pos) & (key_pos < slot_len)
+    key_pos = lax.broadcasted_iota(jnp.int32, shape, 1)
+    allowed = (key_pos <= query_pos) & (key_pos < slot_len)
     scores = jnp.where(allowed, scores, MASKED)
     peak = jnp.max(scores, axis=-1, keepdims=True)
     raised = jnp.exp(scores - peak)
@@ -263,14 +261,9 @@
     value_mix = (0.5 * own_value + 0.5 * first_wide).astype(jnp.bfloat16)
 
     kv_own = jnp.concatenate([key_rot, value_mix], axis=-1).reshape(rows, 2 * width)
-    kv_all = jnp.concatenate(
-        [kv_own]
-        + [
-            lax.ppermute(kv_own, "ctx", [(j, j + b) for j in range(n_ctx - b)])
-            for b in range(1, n_ctx)
-        ],
-        axis=0,
-    )
+    kv_all = lax.all_to_all(
+        jnp.broadcast_to(kv_own[None], (n_ctx, rows, 2 * width)), "ctx", 0, 0, tiled=False
+    ).reshape(total_len, 2 * width)
     meta = jnp.stack([lax.axis_index("ctx") * rows, slot_lengths[0]]).astype(jnp.int32)
     query_flat = query_rotated_rows.reshape(rows, width)
     mixed_low = attention_forward(
@@ -330,12 +323,12 @@
         meta, query_flat, kv_all, blended_value_gradient.reshape(rows, width), head_dim, score_scale
     )
     query_rot_back = query_rot_back.reshape(slots, rows, head_count, head_dim)
-    kv_back = kv_back.reshape(n_ctx, rows, 2 * width)
-    key_value = kv_back[0].astype(jnp.float32)
-    for b_shift in range(1, n_ctx):
-        key_value = key_value + lax.ppermute(
-            kv_back[b_shift], "ctx", [(j, j - b_shift) for j in range(b_shift, n_ctx)]
-        ).astype(jnp.float32)
+    key_value = jnp.sum(
+        lax.all_to_all(kv_back.reshape(n_ctx, rows, 2 * width), "ctx", 0, 0, tiled=False).astype(
+            jnp.float32
+        ),
+        axis=0,
+    )
     key_value = key_value.reshape(rows, width // HEAD_BLOCK, 2, HEAD_BLOCK)
     key_rot_back = key_value[:, :, 0, :].reshape(slots, rows, head_count, head_dim)
     value_mix_back = key_value[:, :, 1, :].reshape(slots, rows, width)

time: 760 us -> 752 us (0.989)
  waiting for transfers between devices: 416 us -> 466 us
  local copies, waits for them, and re-layouts: 106 us -> 79.4 us
  starting transfers between devices: 46.2 us -> 22.1 us
    all_to_all x0 -> x2, waiting for transfers between devices: none -> 209 us  [the longest x1 105 us: body(): lax.all_to_all(jnp.broadcast_to(kv_own[None], (n_ctx, rows, 2 * width)),...]
    ppermute x14 -> x0, waiting for transfers between devices: 195 us -> none  [the longest x7 115 us: body(): lax.ppermute(kv_back[b_shift], 'ctx', [(j, j - b_shift) for j in range(b_...]
    ppermute x14 -> x0, starting transfers between devices: 34.1 us -> none  [the longest x7 25.1 us: body(): lax.ppermute(kv_own, 'ctx', [(j, j + b) for j in range(n_ctx - b)])]
    reduce_scatter x1, waiting for transfers between devices: 41 us -> 63.4 us  [body(): lax.psum_scatter(mlp_grads, 'fsdp', scatter_dimension=0, tiled=False)]
    unnamed x76 -> x65, local copies, waits for them, and re-layouts: 28.2 us -> 11.4 us
    slice x3 -> x0, local copies, waits for them, and re-layouts: 13.9 us -> none  [the longest x1 6.5 us: body(): kv_back[b_shift]]
    all_gather x1, waiting for transfers between devices: 5.49 us -> 19.1 us  [body(): mlp_all = lax.all_gather(mlp_pack, 'fsdp', axis=0, tiled=False)]
    all_to_all x0 -> x2, starting transfers between devices: none -> 10.1 us  [the longest x1 5.1 us: body(): lax.all_to_all(jnp.broadcast_to(kv_own[None], (n_ctx, rows, 2 * width)),...]
  transfers between devices with their start and end apart: 24 -> 12, of which waited for: 15 -> 11; matrix products, arithmetic and copies ran while one was open for 14% -> 11% of each run, Pallas kernels for 9% -> 9%
where the time goes in v5:
time: 752 us; the launch traced here: 745 us
  waiting for transfers between devices  466 us (62%)
  local copies, waits for them, and re-layouts  79.4 us (11%)
  Pallas kernels  68 us (9%)
  matrix products  52 us (7%)
  other arithmetic  43.1 us (6%)
  starting transfers between devices  22.1 us (3%)
  between operations  14.6 us (2%)
    all_to_all x1, waiting for transfers between devices, body(): lax.all_to_all(jnp.broadcast_to(kv_own[None], (n_ctx, rows, 2 * width)),...  105 us
    all_to_all x1, waiting for transfers between devices, body(): lax.all_to_all(kv_back.reshape(n_ctx, rows, 2 * width), 'ctx', 0, 0, tile...  105 us
    all_gather x1, waiting for transfers between devices, body(): attn_all = lax.all_gather(attn_pack, 'fsdp', axis=0, tiled=False)  74.6 us
    ppermute x6, waiting for transfers between devices, ctx_allreduce(): other = lax.ppermute(total, 'ctx', [(j, j ^ step) for j in range(n_ctx)])  67.8 us
    reduce_scatter x1, waiting for transfers between devices, body(): lax.psum_scatter(mlp_grads, 'fsdp', scatter_dimension=0, tiled=False)  63.4 us
    pallas_call x1, Pallas kernels, attention_backward(): pl.pallas_call(functools.partial(attn_bwd_kernel, head_dim, scale), out_s...  43.6 us
    reduce_scatter x1, waiting for transfers between devices, body(): lax.psum_scatter(attn_grads, 'fsdp', scatter_dimension=0, tiled=False)  31.7 us
    pallas_call x1, Pallas kernels, attention_forward(): pl.pallas_call(functools.partial(attn_fwd_kernel, head_dim, scale), out_s...  24.4 us
  transfers between devices with their start and end apart: 12, of which 11 were waited for; matrix products, arithmetic and copies ran while one was open for 11% of the time, Pallas kernels for 9%

profile of v5, /device:TPU:0, one launch (start us, length us, event | category | flops | bytes accessed | tf_op | source)
XLA Modules:
  0.0 745.3 jit_solution(12464012200583934830)
XLA Ops:
  10.8 1.0 constant_dynamic-update-slice_fusion
  12.7 1.4 reshape.485
  14.1 1.1 pad_maximum_fusion.1
  15.7 74.6 %all-gather.5.cloned.1.call-done = bf16[4352,1024]{1,0:T(8,128)(2,1)} async-done(((bf16[272,1024]{1,0:T(8,128)(2,1)}), bf16[4352,1024]{1,0:T(8,128)(2,1)}) %all-gather.5.cloned.1.call-update) | async-done | bytes 8912912 | tf_op jit(solution)/shard_map/all_gather | solution.py:230
  91.3 5.8 fusion.56
  97.1 4.0 copy.71
  101.1 4.0 copy.72
  105.1 2.6 convolution_bitcast_fusion.3
  109.7 2.1 copy.73
  111.7 2.5 fusion.8
  114.3 4.3 broadcast_in_dim.72
  118.7 5.1 all-to-all-start
  126.5 104.9 %all-to-all-done = bf16[8,256,2048]{2,1,0:T(8,128)(2,1)} async-done(((bf16[8,256,2048]{2,1,0:T(8,128)(2,1)}), bf16[8,256,2048]{2,1,0:T(8,128)(2,1)}, u32[]{:S(2)}, u32[]{:S(2)}) %all-to-all-start) | async-done | bytes 8388640 | tf_op jit(solution)/shard_map/all_to_all | solution.py:264
  231.4 24.4 %shard_map.229 = bf16[256,1024]{1,0:T(8,128)(2,1)S(1)} custom-call(s32[2]{0:T(128)S(1)} %pad_add_fusion.meta_ref, bf16[256,1024]{1,0:T(8,128)(2,1)S(1)} %copy.74.q_ref, bf16[2048,2048]{1,0:T(8,128)(2,1)} %bitcast.18.k_ref.v_ref, bf16[2048,2048]{1,0:T(8,128)(2,1)} %bitcast.18.k_ref.v_ref), custom_call_target="tpu_custom_call" | custom-call | flops 2147483648 | bytes 9437184 | tf_op jit(solution)/shard_map/pallas_call | solution.py:77
  255.8 1.0 copy.84
  256.8 1.9 multiply_reduce_fusion
  258.7 1.0 copy-done.4
  260.6 1.2 copy.83
  261.8 19.1 %all-gather.7.cloned.1.call-done = bf16[1024,8448]{1,0:T(8,128)(2,1)} async-done(((bf16[64,8448]{1,0:T(8,128)(2,1)}), bf16[1024,8448]{1,0:T(8,128)(2,1)}) %all-gather.7.cloned.1.call-update) | async-done | bytes 17301520 | tf_op jit(solution)/shard_map/all_gather | solution.py:242
  281.0 11.4 %fusion.55 = (bf16[16,64,2816]{2,1,0:T(8,128)(2,1)}, bf16[16,64,2816]{2,1,0:T(8,128)(2,1)}, bf16[16,64,2816]{2,1,0:T(8,128)(2,1)}) fusion(bf16[16,64,8448]{2,1,0:T(8,128)(2,1)} %bitcast.168), kind=kLoop, calls=%fused_computation.127 | loop fusion | bytes 34603008 | tf_op jit(solution)/shard_map/slice | solution.py:245
  292.4 11.7 %reshape_reshape.7 = bf16[2816,1024]{1,0:T(8,128)(2,1)} reshape(bf16[16,64,2816]{2,1,0:T(8,128)(2,1)} %get-tuple-element.62) | data formatting | bytes 11534336 | tf_op jit(solution)/shard_map/reshape;reshape | solution.py:245
  304.1 4.8 fusion.30
  309.0 3.3 fusion.32
  312.3 6.3 multiply_convert_fusion
  318.6 1.7 fusion.60
  320.3 4.1 convolution_convert_fusion.2
  324.4 4.2 convolution_convert_fusion.1
  328.6 2.8 fusion.23
  331.4 4.2 convolution_convert_fusion
  335.7 11.8 %reshape_reshape.8 = bf16[16,64,2816]{2,1,0:T(8,128)(2,1)} reshape(bf16[2816,1024]{1,0:T(8,128)(2,1)} %convolution_convert_fusion) | data formatting | bytes 11534336 | tf_op jit(solution)/shard_map/reshape;reshape | solution.py:312
  347.5 2.0 fusion.25
  349.5 1.0 copy-done.2
  351.2 14.2 %pad_maximum_fusion = bf16[16,64,9472]{2,1,0:T(8,128)(2,1)} fusion(bf16[16,64,1024]{2,1,0:T(8,128)(2,1)S(1)} %convolution_convert_fusion.3, bf16[16,64,2816]{2,1,0:T(8,128)(2,1)} %reshape_reshape.8, bf16[16,64,2816]{2,1,0:T(8,128)(2,1)} %convolution_convert_fusion.1, bf16[16,64,2816]{2,1,0:T(8,128)(2,1)} %convolution_convert_fusion.2), kind=kLoop, calls=%fused_computation | loop fusion | flops 77594624 | bytes 38797312 | tf_op jit(solution)/shard_map/concatenate | solution.py:308
  365.4 2.0 convolution_convert_fusion.7.do_ref
  367.4 43.6 %shard_map.230 = (f32[256,1024]{1,0:T(8,128)S(1)}, bf16[2048,2048]{1,0:T(8,128)(2,1)}) custom-call(s32[2]{0:T(128)S(1)} %pad_add_fusion.meta_ref, bf16[256,1024]{1,0:T(8,128)(2,1)S(1)} %copy.74.q_ref, bf16[2048,2048]{1,0:T(8,128)(2,1)} %bitcast.18.k_ref.v_ref, bf16[2048,2048]{1,0:T(8,128)(2,1)} %bitcast.18.k_ref.v_ref, ...), custom_call_target="tpu_custom_call" | custom-call | flops 5368709120 | bytes 19398656 | tf_op jit(solution)/shard_map/pallas_call | solution.py:105
  411.1 5.0 all-to-all-start.1
  416.5 104.5 %all-to-all-done.1 = bf16[8,256,2048]{2,1,0:T(8,128)(2,1)} async-done(((bf16[8,256,2048]{2,1,0:T(8,128)(2,1)}), bf16[8,256,2048]{2,1,0:T(8,128)(2,1)}, u32[]{:S(2)}, u32[]{:S(2)}) %all-to-all-start.1) | async-done | bytes 8388640 | tf_op jit(solution)/shard_map/all_to_all | solution.py:327
  521.1 5.4 convert_reduce_fusion
  526.4 2.0 copy.77
  528.4 2.8 slice_multiply_fusion
  531.7 1.4 copy-done.1
  536.3 1.3 fusion.21
  537.8 1.3 copy.79
  541.3 3.4 fusion.1
  544.8 63.4 %reduce-scatter.3.cloned.1.call-done = bf16[1,64,9472]{2,1,0:T(8,128)(2,1)} async-done(((bf16[16,64,9472]{2,1,0:T(8,128)(2,1)}), bf16[1,64,9472]{2,1,0:T(8,128)(2,1)}) %reduce-scatter.3.cloned.1.call-update) | async-done | bytes 1212432 | tf_op jit(solution)/shard_map/reduce_scatter | solution.py:317
  608.2 1.5 collective-permute-start.3
  609.8 26.7 %collective-permute-done.3 = bf16[64,9472]{1,0:T(8,128)(2,1)S(1)} collective-permute-done((bf16[64,9472]{1,0:T(8,128)(2,1)}, bf16[64,9472]{1,0:T(8,128)(2,1)S(1)}, u32[]{:S(2)}, u32[]{:S(2)}) %collective-permute-start.3) | collective-permute-done | bytes 1212448 | tf_op jit(solution)/shard_map/ppermute | solution.py:179
  636.4 1.6 add_convert_fusion.2
  638.0 3.1 collective-permute-start.4
  641.1 25.5 %collective-permute-done.4 = bf16[64,9472]{1,0:T(8,128)(2,1)S(1)} collective-permute-done((bf16[64,9472]{1,0:T(8,128)(2,1)S(1)}, bf16[64,9472]{1,0:T(8,128)(2,1)S(1)}, u32[]{:S(2)}, u32[]{:S(2)}) %collective-permute-start.4) | collective-permute-done | bytes 1212448 | tf_op jit(solution)/shard_map/ppermute | solution.py:179
  666.6 1.3 add_convert_fusion.1
  668.6 5.5 fusion.9
  674.1 31.7 %reduce-scatter.5.cloned.1.call-done = bf16[1,208,1024]{2,1,0:T(8,128)(2,1)} async-done(((bf16[16,208,1024]{2,1,0:T(8,128)(2,1)}), bf16[1,208,1024]{2,1,0:T(8,128)(2,1)}) %reduce-scatter.5.cloned.1.call-update) | async-done | bytes 426000 | tf_op jit(solution)/shard_map/reduce_scatter | solution.py:380
  705.8 1.5 collective-permute-start
  707.2 2.6 copy.85
  709.8 1.3 fusion.17
  711.2 5.2 collective-permute-done
  716.5 3.1 collective-permute-start.1
  719.6 1.9 fusion.12
  722.2 5.4 collective-permute-done.1
  727.8 1.9 collective-permute-start.2
  729.7 1.3 fusion.57
  730.9 1.1 reshape.495
  732.0 5.0 collective-permute-done.2
  (118 shorter events, 22.2 us)
Async XLA Ops:
  7.2 7.0 copy-start.22
  7.2 7.0 copy-start.23
  7.2 83.1 %all-gather.5.cloned.1.call-start = ((), (), s32[]{:S(2)}) async-start(), calls=%async_computation.6 | async-start | bytes 9469952 | tf_op jit(solution)/shard_map/all_gather | solution.py:230
  10.8 4.5 copy-start.7
  11.8 0.8 copy-start.20
  12.7 268.3 %all-gather.7.cloned.1.call-start = ((), (), s32[]{:S(2)}) async-start(), calls=%async_computation.7 | async-start | bytes 18382848 | tf_op jit(solution)/shard_map/all_gather | solution.py:242
  105.1 2.6 copy-start.18
  111.7 2.5 copy-start.19
  118.7 5.3 copy-start.24
  118.7 5.4 copy-start.25
  118.7 112.7 %all-to-all-start = ((bf16[8,256,2048]{2,1,0:T(8,128)(2,1)}), bf16[8,256,2048]{2,1,0:T(8,128)(2,1)}, u32[]{:S(2)}, u32[]{:S(2)}) async-start(bf16[8,256,2048]{2,1,0:T(8,128)(2,1)} %broadcast_in_dim.72), calls=%async_computation | async-start | bytes 16777216 | tf_op jit(solution)/shard_map/all_to_all | solution.py:264
  123.8 484.4 %reduce-scatter.3.cloned.1.call-start = ((), (), s32[]{:S(2)}) async-start(), calls=%async_computation.4 | async-start | bytes 20611072 | tf_op jit(solution)/shard_map/reduce_scatter | solution.py:317
  258.7 1.0 copy-start.4
  304.1 4.8 copy-start.5
  304.1 4.9 copy-start.10
  304.1 8.2 %slice-start = ((s8[5767168]{0:T(1024)(128)(4,1)}), s8[4194304]{0:T(1024)(128)(4,1)S(1)}, s32[]{:S(2)}) async-start(s8[5767168]{0:T(1024)(128)(4,1)} %bitcast.178), calls=%async_computation.8 | async-start | bytes 8388608
  308.9 3.4 slice-start.1
  309.0 3.3 copy-start.15
  318.6 12.9 %copy-start.13 = (bf16[256,2816]{1,0:T(8,128)(2,1)}, bf16[256,2816]{1,0:T(8,128)(2,1)S(1)}, u32[]{:S(2)}) copy-start(bf16[256,2816]{1,0:T(8,128)(2,1)S(1)} %get-tuple-element.71) | copy-start | bytes 4325380
  320.3 8.4 %slice-start.2 = ((s8[5767168]{0:T(1024)(128)(4,1)}), s8[4194304]{0:T(1024)(128)(4,1)S(1)}, s32[]{:S(2)}) async-start(s8[5767168]{0:T(1024)(128)(4,1)} %bitcast.181), calls=%async_computation.10 | async-start | bytes 8388608
  324.4 4.2 slice-start.3
  335.7 11.8 %copy-start.16 = (bf16[1,256,1024]{2,1,0:T(8,128)(2,1)S(1)}, bf16[1,256,1024]{2,1,0:T(8,128)(2,1)}, u32[]{:S(2)}) copy-start(bf16[1,256,1024]{2,1,0:T(8,128)(2,1)} %param.25) | copy-start | bytes 1572868
  347.5 3.0 copy-start.17
  349.5 1.0 copy-start.2
  411.1 110.0 %all-to-all-start.1 = ((bf16[8,256,2048]{2,1,0:T(8,128)(2,1)}), bf16[8,256,2048]{2,1,0:T(8,128)(2,1)}, u32[]{:S(2)}, u32[]{:S(2)}) async-start(bf16[8,256,2048]{2,1,0:T(8,128)(2,1)} %bitcast.169), calls=%async_computation.1 | async-start | bytes 16777216 | tf_op jit(solution)/shard_map/all_to_all | solution.py:327
  416.0 289.7 %reduce-scatter.5.cloned.1.call-start = ((), (), s32[]{:S(2)}) async-start(), calls=%async_computation.5 | async-start | bytes 7241728 | tf_op jit(solution)/shard_map/reduce_scatter | solution.py:380
  531.3 1.9 copy-start.1
  531.7 2.3 copy-start
  531.7 3.0 copy-start.11
  533.9 1.6 copy-start.9
  534.7 1.6 copy-start.8
  539.1 1.5 copy-start.12
  608.2 28.2 %collective-permute-start.3 = (bf16[64,9472]{1,0:T(8,128)(2,1)}, bf16[64,9472]{1,0:T(8,128)(2,1)S(1)}, u32[]{:S(2)}, u32[]{:S(2)}) collective-permute-start(bf16[64,9472]{1,0:T(8,128)(2,1)} %bitcast.202), channel_id=1, source_target_pairs={{0,1},{1,0},{2,3},{3,2},{4,5},{5,4},{6,7},{7,6},{8,9},{9,8},{10,11... | collective-permute-start | bytes 3637256 | tf_op jit(solution)/shard_map/ppermute | solution.py:179
  638.0 30.6 %copy-start.6 = (f32[1,256,1024]{2,1,0:T(8,128)S(1)}, f32[1,256,1024]{2,1,0:T(8,128)}, u32[]{:S(2)}) copy-start(f32[1,256,1024]{2,1,0:T(8,128)} %copy-done.4) | copy-start | bytes 3145732
  638.0 30.6 %copy-start.14 = (bf16[256,2816]{1,0:T(8,128)(2,1)S(1)}, bf16[256,2816]{1,0:T(8,128)(2,1)}, u32[]{:S(2)}) copy-start(bf16[256,2816]{1,0:T(8,128)(2,1)} %copy-done.13) | copy-start | bytes 4325380
  638.0 28.6 %collective-permute-start.4 = (bf16[64,9472]{1,0:T(8,128)(2,1)S(1)}, bf16[64,9472]{1,0:T(8,128)(2,1)S(1)}, u32[]{:S(2)}, u32[]{:S(2)}) collective-permute-start(bf16[64,9472]{1,0:T(8,128)(2,1)S(1)} %add_convert_fusion.2), channel_id=1, source_target_pairs={{0,2},{1,3},{2,0},{3,1},{4,6},{5,7},{6,4},{7,5},{8,10},{9,11},{10,... | collective-permute-start | bytes 3637256 | tf_op jit(solution)/shard_map/ppermute | solution.py:179
  667.9 51.8 %collective-permute-start.5 = (bf16[64,9472]{1,0:T(8,128)(2,1)}, bf16[64,9472]{1,0:T(8,128)(2,1)}, u32[]{:S(2)}, u32[]{:S(2)}) collective-permute-start(bf16[64,9472]{1,0:T(8,128)(2,1)} %add_convert_fusion.1), channel_id=1, source_target_pairs={{0,4},{1,5},{2,6},{3,7},{4,0},{5,1},{6,2},{7,3},{8,12},{9,13},{10,... | collective-permute-start | bytes 3637256 | tf_op jit(solution)/shard_map/ppermute | solution.py:179
  674.1 35.7 %copy-start.3 = (f32[1,256,1024]{2,1,0:T(8,128)S(1)}, f32[1,256,1024]{2,1,0:T(8,128)}, u32[]{:S(2)}) copy-start(f32[1,256,1024]{2,1,0:T(8,128)} %copy-done.2) | copy-start | bytes 3145732
  705.8 10.6 %collective-permute-start = (bf16[208,1024]{1,0:T(8,128)(2,1)}, bf16[208,1024]{1,0:T(8,128)(2,1)S(1)}, u32[]{:S(2)}, u32[]{:S(2)}) collective-permute-start(bf16[208,1024]{1,0:T(8,128)(2,1)} %bitcast.204), channel_id=1, source_target_pairs={{0,1},{1,0},{2,3},{3,2},{4,5},{5,4},{6,7},{7,6},{8,9},{9,8},{10,11... | collective-permute-start | bytes 1277960 | tf_op jit(solution)/shard_map/ppermute | solution.py:179
  707.2 9.2 %copy-start.21 = (bf16[1,208,1024]{2,1,0:T(8,128)(2,1)S(1)}, bf16[1,208,1024]{2,1,0:T(8,128)(2,1)}, u32[]{:S(2)}) copy-start(bf16[1,208,1024]{2,1,0:T(8,128)(2,1)} %reduce-scatter.5.cloned.1.call-done) | copy-start | bytes 1277956
  716.5 11.1 %collective-permute-start.1 = (bf16[208,1024]{1,0:T(8,128)(2,1)S(1)}, bf16[208,1024]{1,0:T(8,128)(2,1)S(1)}, u32[]{:S(2)}, u32[]{:S(2)}) collective-permute-start(bf16[208,1024]{1,0:T(8,128)(2,1)S(1)} %add_convert_fusion.5), channel_id=1, source_target_pairs={{0,2},{1,3},{2,0},{3,1},{4,6},{5,7},{6,4},{7,5},{8,10},{9,11},{10,... | collective-permute-start | bytes 1277960 | tf_op jit(solution)/shard_map/ppermute | solution.py:179
  727.8 9.2 %collective-permute-start.2 = (bf16[208,1024]{1,0:T(8,128)(2,1)S(1)}, bf16[208,1024]{1,0:T(8,128)(2,1)S(1)}, u32[]{:S(2)}, u32[]{:S(2)}) collective-permute-start(bf16[208,1024]{1,0:T(8,128)(2,1)S(1)} %add_convert_fusion.4), channel_id=1, source_target_pairs={{0,4},{1,5},{2,6},{3,7},{4,0},{5,1},{6,2},{7,3},{8,12},{9,13},{10,... | collective-permute-start | bytes 1277960 | tf_op jit(solution)/shard_map/ppermute | solution.py:179
Sparse Core Ops, SparseCore 0:
  12.8 77.4 all-gather.4
  92.7 188.1 all-gather.6
  365.6 242.6 reduce-scatter.2
  612.2 93.4 reduce-scatter.4

commit v6 on v5

--- a/solution.py
+++ b/solution.py
@@ -305,15 +305,22 @@
     middle_low = middle_back.astype(jnp.bfloat16)
     out_total = jnp.einsum("srd,sre->de", mixed_low, middle_low, preferred_element_type=jnp.float32)
 
+    down_share = lax.psum_scatter(
+        down_total.astype(jnp.bfloat16).reshape(n_fsdp, d_rows, width),
+        "fsdp",
+        scatter_dimension=0,
+        tiled=False,
+    )
     mlp_grads = jnp.concatenate(
         [
             gate_total.reshape(n_fsdp, w_rows, ff),
             upper_total.reshape(n_fsdp, w_rows, ff),
-            down_total.reshape(n_fsdp, d_rows, width).reshape(n_fsdp, w_rows, ff),
             out_total.reshape(n_fsdp, w_rows, width),
         ],
         axis=2,
     ).astype(jnp.bfloat16)
+    mlp_grads, down_share = lax.optimization_barrier((mlp_grads, down_share))
+    down_share = ctx_allreduce(down_share, n_ctx)
     mlp_share = lax.psum_scatter(mlp_grads, "fsdp", scatter_dimension=0, tiled=False)
 
     blended_value_gradient = jnp.einsum(
@@ -388,8 +395,8 @@
     midnorm_grad = attn_share[3 * w_rows, g_len:2 * g_len]
     gate_grad = mlp_share[:, 0:ff]
     up_grad = mlp_share[:, ff:2 * ff]
-    down_grad = mlp_share[:, 2 * ff:3 * ff].reshape(d_rows, width)
-    out_grad = mlp_share[:, 3 * ff:]
+    down_grad = down_share
+    out_grad = mlp_share[:, 2 * ff:]
     return (
         layer_out,
         tokens_grad,

time: 752 us -> 765 us (1.017)
  waiting for transfers between devices: 466 us -> 499 us
  local copies, waits for them, and re-layouts: 79.4 us -> 66.1 us
    reduce_scatter x0 -> x1, waiting for transfers between devices: none -> 61.7 us  [body(): lax.psum_scatter(down_total.astype(jnp.bfloat16).reshape(n_fsdp, d_rows,...]
    reduce_scatter x1, waiting for transfers between devices: 63.4 us -> 34.6 us  [body(): lax.psum_scatter(mlp_grads, 'fsdp', scatter_dimension=0, tiled=False)]
    another operation x1 -> x0, local copies, waits for them, and re-layouts: 11.8 us -> none  [body(): down_total.reshape(n_fsdp, d_rows, width).reshape(n_fsdp, w_rows, ff)]
    concatenate x1, other arithmetic: 14.2 us -> 6.31 us  [body(): jnp.concatenate([gate_total.reshape(n_fsdp, w_rows, ff), upper_total.resh...]
    ppermute x6 -> x9, waiting for transfers between devices: 67.8 us -> 61.7 us  [ctx_allreduce(): other = lax.ppermute(total, 'ctx', [(j, j ^ step) for j in range(n_ctx)])]
    ppermute x6 -> x9, starting transfers between devices: 11.7 us -> 15.4 us  [ctx_allreduce(): other = lax.ppermute(total, 'ctx', [(j, j ^ step) for j in range(n_ctx)])]
  transfers between devices with their start and end apart: 12 -> 16, of which waited for: 11 -> 13; matrix products, arithmetic and copies ran while one was open for 11% -> 13% of each run, Pallas kernels for 9% -> 9%
where the time goes in v6:
time: 765 us; the launch traced here: 759 us
  waiting for transfers between devices  499 us (65%)
  Pallas kernels  67.5 us (9%)
  local copies, waits for them, and re-layouts  66.1 us (9%)
  matrix products  49.8 us (7%)
  other arithmetic  35.9 us (5%)
  starting transfers between devices  26.1 us (3%)
  between operations  14.6 us (2%)
    all_to_all x1, waiting for transfers between devices, body(): lax.all_to_all(jnp.broadcast_to(kv_own[None], (n_ctx, rows, 2 * width)),...  105 us
    all_to_all x1, waiting for transfers between devices, body(): lax.all_to_all(kv_back.reshape(n_ctx, rows, 2 * width), 'ctx', 0, 0, tile...  102 us
    all_gather x1, waiting for transfers between devices, body(): attn_all = lax.all_gather(attn_pack, 'fsdp', axis=0, tiled=False)  73.6 us
    ppermute x9, waiting for transfers between devices, ctx_allreduce(): other = lax.ppermute(total, 'ctx', [(j, j ^ step) for j in range(n_ctx)])  61.7 us
    reduce_scatter x1, waiting for transfers between devices, body(): lax.psum_scatter(down_total.astype(jnp.bfloat16).reshape(n_fsdp, d_rows,...  61.7 us
    pallas_call x1, Pallas kernels, attention_backward(): pl.pallas_call(functools.partial(attn_bwd_kernel, head_dim, scale), out_s...  43.2 us
    reduce_scatter x1, waiting for transfers between devices, body(): lax.psum_scatter(attn_grads, 'fsdp', scatter_dimension=0, tiled=False)  36.5 us
    reduce_scatter x1, waiting for transfers between devices, body(): lax.psum_scatter(mlp_grads, 'fsdp', scatter_dimension=0, tiled=False)  34.6 us
  transfers between devices with their start and end apart: 16, of which 13 were waited for; matrix products, arithmetic and copies ran while one was open for 13% of the time, Pallas kernels for 9%

profile of v6, /device:TPU:0, one launch (start us, length us, event | category | flops | bytes accessed | tf_op | source)
XLA Modules:
  0.0 758.8 jit_solution(13870640707578010051)
XLA Ops:
  9.0 0.9 constant_dynamic-update-slice_fusion.2
  12.6 1.4 reshape.485
  14.0 2.1 pad_maximum_fusion.1
  16.6 73.6 %all-gather.5.cloned.1.call-done = bf16[4352,1024]{1,0:T(8,128)(2,1)} async-done(((bf16[272,1024]{1,0:T(8,128)(2,1)}), bf16[4352,1024]{1,0:T(8,128)(2,1)}) %all-gather.5.cloned.1.call-update) | async-done | bytes 8912912 | tf_op jit(solution)/shard_map/all_gather | solution.py:230
  90.2 0.9 fusion.45
  91.2 5.8 fusion.57
  97.0 4.0 copy.71
  101.0 4.0 copy.72
  105.0 2.6 convolution_bitcast_fusion.3
  109.6 2.1 copy.73
  111.6 2.5 fusion.8
  114.2 4.4 broadcast_in_dim.72
  118.7 5.1 all-to-all-start
  126.4 105.1 %all-to-all-done = bf16[8,256,2048]{2,1,0:T(8,128)(2,1)} async-done(((bf16[8,256,2048]{2,1,0:T(8,128)(2,1)}), bf16[8,256,2048]{2,1,0:T(8,128)(2,1)}, u32[]{:S(2)}, u32[]{:S(2)}) %all-to-all-start) | async-done | bytes 8388640 | tf_op jit(solution)/shard_map/all_to_all | solution.py:264
  231.5 24.3 %shard_map.229 = bf16[256,1024]{1,0:T(8,128)(2,1)S(1)} custom-call(s32[2]{0:T(128)S(1)} %pad_add_fusion.meta_ref, bf16[256,1024]{1,0:T(8,128)(2,1)S(1)} %copy.74.q_ref, bf16[2048,2048]{1,0:T(8,128)(2,1)} %bitcast.18.k_ref.v_ref, bf16[2048,2048]{1,0:T(8,128)(2,1)} %bitcast.18.k_ref.v_ref), custom_call_target="tpu_custom_call" | custom-call | flops 2147483648 | bytes 9437184 | tf_op jit(solution)/shard_map/pallas_call | solution.py:77
  255.8 1.7 multiply_reduce_fusion
  257.5 23.4 %all-gather.7.cloned.1.call-done = bf16[1024,8448]{1,0:T(8,128)(2,1)} async-done(((bf16[64,8448]{1,0:T(8,128)(2,1)}), bf16[1024,8448]{1,0:T(8,128)(2,1)}) %all-gather.7.cloned.1.call-update) | async-done | bytes 17301520 | tf_op jit(solution)/shard_map/all_gather | solution.py:242
  281.0 11.3 %fusion.56 = (bf16[16,64,2816]{2,1,0:T(8,128)(2,1)}, bf16[16,64,2816]{2,1,0:T(8,128)(2,1)}, bf16[16,64,2816]{2,1,0:T(8,128)(2,1)}) fusion(bf16[16,64,8448]{2,1,0:T(8,128)(2,1)} %bitcast.171), kind=kLoop, calls=%fused_computation.131 | loop fusion | bytes 34603008 | tf_op jit(solution)/shard_map/slice | solution.py:245
  292.2 11.7 %reshape_reshape.3 = bf16[2816,1024]{1,0:T(8,128)(2,1)} reshape(bf16[16,64,2816]{2,1,0:T(8,128)(2,1)} %get-tuple-element.66) | data formatting | bytes 11534336 | tf_op jit(solution)/shard_map/reshape;reshape | solution.py:245
  303.9 4.8 fusion.30
  308.8 1.7 fusion.32
  310.7 5.8 multiply_convert_fusion
  316.5 4.2 convolution_convert_fusion
  321.0 1.0 copy.84
  322.0 2.2 fusion.94
  324.2 1.2 copy.83
  325.5 4.9 fusion.61
  330.4 5.0 fusion.22
  337.2 1.7 convolution_convert_fusion.1
  338.9 1.7 convolution_convert_fusion.2
  340.6 6.3 pad_maximum_fusion
  346.9 61.7 %reduce-scatter.4.cloned.1.call-done = bf16[1,176,1024]{2,1,0:T(8,128)(2,1)} async-done(((bf16[16,176,1024]{2,1,0:T(8,128)(2,1)}), bf16[1,176,1024]{2,1,0:T(8,128)(2,1)}) %reduce-scatter.4.cloned.1.call-update) | async-done | bytes 360464 | tf_op jit(solution)/shard_map/reduce_scatter | solution.py:308
  408.6 2.0 convolution_convert_fusion.7.do_ref
  410.6 43.2 %shard_map.230 = (f32[256,1024]{1,0:T(8,128)S(1)}, bf16[2048,2048]{1,0:T(8,128)(2,1)}) custom-call(s32[2]{0:T(128)S(1)} %pad_add_fusion.meta_ref, bf16[256,1024]{1,0:T(8,128)(2,1)S(1)} %copy.74.q_ref, bf16[2048,2048]{1,0:T(8,128)(2,1)} %bitcast.18.k_ref.v_ref, bf16[2048,2048]{1,0:T(8,128)(2,1)} %bitcast.18.k_ref.v_ref, ...), custom_call_target="tpu_custom_call" | custom-call | flops 5368709120 | bytes 19398656 | tf_op jit(solution)/shard_map/pallas_call | solution.py:105
  453.7 4.9 all-to-all-start.1
  459.2 102.2 %all-to-all-done.1 = bf16[8,256,2048]{2,1,0:T(8,128)(2,1)} async-done(((bf16[8,256,2048]{2,1,0:T(8,128)(2,1)}), bf16[8,256,2048]{2,1,0:T(8,128)(2,1)}, u32[]{:S(2)}, u32[]{:S(2)}) %all-to-all-start.1) | async-done | bytes 8388640 | tf_op jit(solution)/shard_map/all_to_all | solution.py:334
  561.4 5.4 convert_reduce_fusion
  566.8 2.0 copy.77
  568.8 2.9 slice_multiply_fusion
  572.1 1.3 copy-done.1
  576.6 1.3 fusion.20
  578.1 1.2 copy.79
  581.6 3.3 fusion.1
  585.0 34.6 %reduce-scatter.6.cloned.1.call-done = bf16[1,64,6656]{2,1,0:T(8,128)(2,1)} async-done(((bf16[16,64,6656]{2,1,0:T(8,128)(2,1)}), bf16[1,64,6656]{2,1,0:T(8,128)(2,1)}) %reduce-scatter.6.cloned.1.call-update) | async-done | bytes 851984 | tf_op jit(solution)/shard_map/reduce_scatter | solution.py:324
  619.6 1.1 copy-done.23
  620.7 1.5 collective-permute-start.3
  622.8 19.9 %collective-permute-done.3 = bf16[64,6656]{1,0:T(8,128)(2,1)S(1)} collective-permute-done((bf16[64,6656]{1,0:T(8,128)(2,1)S(1)}, bf16[64,6656]{1,0:T(8,128)(2,1)S(1)}, u32[]{:S(2)}, u32[]{:S(2)}) %collective-permute-start.3) | collective-permute-done | bytes 852000 | tf_op jit(solution)/shard_map/ppermute | solution.py:179
  642.8 3.0 collective-permute-start.4
  645.9 4.5 collective-permute-done.6
  650.5 3.0 collective-permute-start.7
  653.5 5.2 fusion.9
  658.7 17.9 %collective-permute-done.7 = bf16[176,1024]{1,0:T(8,128)(2,1)S(1)} collective-permute-done((bf16[176,1024]{1,0:T(8,128)(2,1)S(1)}, bf16[176,1024]{1,0:T(8,128)(2,1)S(1)}, u32[]{:S(2)}, u32[]{:S(2)}) %collective-permute-start.7) | collective-permute-done | bytes 360480 | tf_op jit(solution)/shard_map/ppermute | solution.py:179
  678.3 1.4 collective-permute-start.5
  679.8 2.5 copy.85
  682.3 36.5 %reduce-scatter.8.cloned.1.call-done = bf16[1,208,1024]{2,1,0:T(8,128)(2,1)} async-done(((bf16[16,208,1024]{2,1,0:T(8,128)(2,1)}), bf16[1,208,1024]{2,1,0:T(8,128)(2,1)}) %reduce-scatter.8.cloned.1.call-update) | async-done | bytes 426000 | tf_op jit(solution)/shard_map/reduce_scatter | solution.py:387
  718.8 1.5 collective-permute-start
  720.3 1.3 fusion.16
  721.6 2.0 fusion.38
  723.6 6.1 collective-permute-done
  729.9 3.1 collective-permute-start.1
  733.0 1.3 fusion.26
  735.0 6.3 collective-permute-done.1
  742.2 1.2 fusion.58
  743.3 7.1 collective-permute-done.2
  (129 shorter events, 24.4 us)
Async XLA Ops:
  7.2 9.1 %copy-start.7 = (bf16[1,256,1024]{2,1,0:T(8,128)(2,1)S(1)}, bf16[1,256,1024]{2,1,0:T(8,128)(2,1)}, u32[]{:S(2)}) copy-start(bf16[1,256,1024]{2,1,0:T(8,128)(2,1)} %param.14) | copy-start | bytes 1572868
  7.2 83.0 %all-gather.5.cloned.1.call-start = ((), (), s32[]{:S(2)}) async-start(), calls=%async_computation.8 | async-start | bytes 9469952 | tf_op jit(solution)/shard_map/all_gather | solution.py:230
  11.7 0.8 copy-start.24
  12.6 268.4 %all-gather.7.cloned.1.call-start = ((), (), s32[]{:S(2)}) async-start(), calls=%async_computation.9 | async-start | bytes 18382848 | tf_op jit(solution)/shard_map/all_gather | solution.py:242
  105.0 2.6 copy-start.19
  111.6 2.5 copy-start.20
  118.7 5.3 copy-start.27
  118.7 5.3 copy-start.28
  118.7 112.8 %all-to-all-start = ((bf16[8,256,2048]{2,1,0:T(8,128)(2,1)}), bf16[8,256,2048]{2,1,0:T(8,128)(2,1)}, u32[]{:S(2)}, u32[]{:S(2)}) async-start(bf16[8,256,2048]{2,1,0:T(8,128)(2,1)} %broadcast_in_dim.72), calls=%async_computation | async-start | bytes 16777216 | tf_op jit(solution)/shard_map/all_to_all | solution.py:264
  123.8 284.8 %reduce-scatter.4.cloned.1.call-start = ((), (), s32[]{:S(2)}) async-start(), calls=%async_computation.5 | async-start | bytes 6127616 | tf_op jit(solution)/shard_map/reduce_scatter | solution.py:308
  231.5 24.3 %copy-start.8 = (bf16[1,256,1024]{2,1,0:T(8,128)(2,1)S(1)}, bf16[1,256,1024]{2,1,0:T(8,128)(2,1)}, u32[]{:S(2)}) copy-start(bf16[1,256,1024]{2,1,0:T(8,128)(2,1)} %param.14) | copy-start | bytes 1572868
  303.9 4.8 copy-start.4
  303.9 4.9 copy-start.11
  303.9 6.7 slice-start
  308.7 1.9 slice-start.1
  308.8 1.9 copy-start.16
  316.5 4.2 copy-start.14
  320.8 298.8 %reduce-scatter.6.cloned.1.call-start = ((), (), s32[]{:S(2)}) async-start(), calls=%async_computation.6 | async-start | bytes 14483456 | tf_op jit(solution)/shard_map/reduce_scatter | solution.py:324
  325.4 4.9 copy-start.5
  325.5 4.9 copy-start.22
  330.4 5.0 copy-start.17
  335.4 1.1 copy-start.18
  335.9 1.3 copy-start.2
  337.2 1.7 copy-start.21
  453.7 107.6 %all-to-all-start.1 = ((bf16[8,256,2048]{2,1,0:T(8,128)(2,1)}), bf16[8,256,2048]{2,1,0:T(8,128)(2,1)}, u32[]{:S(2)}, u32[]{:S(2)}) async-start(bf16[8,256,2048]{2,1,0:T(8,128)(2,1)} %bitcast.172), calls=%async_computation.1 | async-start | bytes 16777216 | tf_op jit(solution)/shard_map/all_to_all | solution.py:334
  458.7 260.1 %reduce-scatter.8.cloned.1.call-start = ((), (), s32[]{:S(2)}) async-start(), calls=%async_computation.7 | async-start | bytes 7241728 | tf_op jit(solution)/shard_map/reduce_scatter | solution.py:387
  571.7 1.8 copy-start.1
  572.0 2.2 copy-start
  572.1 2.9 copy-start.12
  574.2 1.6 copy-start.10
  575.1 1.6 copy-start.9
  579.4 1.5 copy-start.13
  619.6 1.2 copy-start.23
  619.6 2.6 copy-start.26
  620.7 32.8 %copy-start.6 = (f32[1,256,1024]{2,1,0:T(8,128)S(1)}, f32[1,256,1024]{2,1,0:T(8,128)}, u32[]{:S(2)}) copy-start(f32[1,256,1024]{2,1,0:T(8,128)} %get-tuple-element.105) | copy-start | bytes 3145732
  620.7 32.8 %copy-start.15 = (bf16[256,2816]{1,0:T(8,128)(2,1)S(1)}, bf16[256,2816]{1,0:T(8,128)(2,1)}, u32[]{:S(2)}) copy-start(bf16[256,2816]{1,0:T(8,128)(2,1)} %copy-done.14) | copy-start | bytes 4325380
  620.7 21.9 %collective-permute-start.3 = (bf16[64,6656]{1,0:T(8,128)(2,1)S(1)}, bf16[64,6656]{1,0:T(8,128)(2,1)S(1)}, u32[]{:S(2)}, u32[]{:S(2)}) collective-permute-start(bf16[64,6656]{1,0:T(8,128)(2,1)S(1)} %bitcast.203), channel_id=1, source_target_pairs={{0,1},{1,0},{2,3},{3,2},{4,5},{5,4},{6,7},{7,6},{8,9},{9,8},{10,11... | collective-permute-start | bytes 2555912 | tf_op jit(solution)/shard_map/ppermute | solution.py:179
  622.2 28.2 %collective-permute-start.6 = (bf16[176,1024]{1,0:T(8,128)(2,1)S(1)}, bf16[176,1024]{1,0:T(8,128)(2,1)S(1)}, u32[]{:S(2)}, u32[]{:S(2)}) collective-permute-start(bf16[176,1024]{1,0:T(8,128)(2,1)S(1)} %bitcast.206), channel_id=1, source_target_pairs={{0,1},{1,0},{2,3},{3,2},{4,5},{5,4},{6,7},{7,6},{8,9},{9,8},{10,11... | collective-permute-start | bytes 1081352 | tf_op jit(solution)/shard_map/ppermute | solution.py:179
  642.8 35.3 %collective-permute-start.4 = (bf16[64,6656]{1,0:T(8,128)(2,1)S(1)}, bf16[64,6656]{1,0:T(8,128)(2,1)S(1)}, u32[]{:S(2)}, u32[]{:S(2)}) collective-permute-start(bf16[64,6656]{1,0:T(8,128)(2,1)S(1)} %add_convert_fusion.2), channel_id=1, source_target_pairs={{0,2},{1,3},{2,0},{3,1},{4,6},{5,7},{6,4},{7,5},{8,10},{9,11},{10,... | collective-permute-start | bytes 2555912 | tf_op jit(solution)/shard_map/ppermute | solution.py:179
  650.5 26.1 %collective-permute-start.7 = (bf16[176,1024]{1,0:T(8,128)(2,1)S(1)}, bf16[176,1024]{1,0:T(8,128)(2,1)S(1)}, u32[]{:S(2)}, u32[]{:S(2)}) collective-permute-start(bf16[176,1024]{1,0:T(8,128)(2,1)S(1)} %add_convert_fusion.8), channel_id=1, source_target_pairs={{0,2},{1,3},{2,0},{3,1},{4,6},{5,7},{6,4},{7,5},{8,10},{9,11},{10,... | collective-permute-start | bytes 1081352 | tf_op jit(solution)/shard_map/ppermute | solution.py:179
  658.7 61.5 %copy-start.3 = (f32[1,256,1024]{2,1,0:T(8,128)S(1)}, f32[1,256,1024]{2,1,0:T(8,128)}, u32[]{:S(2)}) copy-start(f32[1,256,1024]{2,1,0:T(8,128)} %copy-done.2) | copy-start | bytes 3145732
  677.5 44.1 %collective-permute-start.8 = (bf16[176,1024]{1,0:T(8,128)(2,1)}, bf16[176,1024]{1,0:T(8,128)(2,1)}, u32[]{:S(2)}, u32[]{:S(2)}) collective-permute-start(bf16[176,1024]{1,0:T(8,128)(2,1)} %add_convert_fusion.7), channel_id=1, source_target_pairs={{0,4},{1,5},{2,6},{3,7},{4,0},{5,1},{6,2},{7,3},{8,12},{9,13},{10,... | collective-permute-start | bytes 1081352 | tf_op jit(solution)/shard_map/ppermute | solution.py:179
  678.3 54.6 %collective-permute-start.5 = (bf16[64,6656]{1,0:T(8,128)(2,1)S(1)}, bf16[64,6656]{1,0:T(8,128)(2,1)}, u32[]{:S(2)}, u32[]{:S(2)}) collective-permute-start(bf16[64,6656]{1,0:T(8,128)(2,1)S(1)} %add_convert_fusion.1), channel_id=1, source_target_pairs={{0,4},{1,5},{2,6},{3,7},{4,0},{5,1},{6,2},{7,3},{8,12},{9,13},{10,... | collective-permute-start | bytes 2555912 | tf_op jit(solution)/shard_map/ppermute | solution.py:179
  718.8 11.0 %copy-start.25 = (bf16[1,208,1024]{2,1,0:T(8,128)(2,1)S(1)}, bf16[1,208,1024]{2,1,0:T(8,128)(2,1)}, u32[]{:S(2)}) copy-start(bf16[1,208,1024]{2,1,0:T(8,128)(2,1)} %reduce-scatter.8.cloned.1.call-done) | copy-start | bytes 1277956
  718.8 11.0 %collective-permute-start = (bf16[208,1024]{1,0:T(8,128)(2,1)}, bf16[208,1024]{1,0:T(8,128)(2,1)S(1)}, u32[]{:S(2)}, u32[]{:S(2)}) collective-permute-start(bf16[208,1024]{1,0:T(8,128)(2,1)} %bitcast.205), channel_id=1, source_target_pairs={{0,1},{1,0},{2,3},{3,2},{4,5},{5,4},{6,7},{7,6},{8,9},{9,8},{10,11... | collective-permute-start | bytes 1277960 | tf_op jit(solution)/shard_map/ppermute | solution.py:179
  729.9 11.4 %collective-permute-start.1 = (bf16[208,1024]{1,0:T(8,128)(2,1)S(1)}, bf16[208,1024]{1,0:T(8,128)(2,1)S(1)}, u32[]{:S(2)}, u32[]{:S(2)}) collective-permute-start(bf16[208,1024]{1,0:T(8,128)(2,1)S(1)} %add_convert_fusion.5), channel_id=1, source_target_pairs={{0,2},{1,3},{2,0},{3,1},{4,6},{5,7},{6,4},{7,5},{8,10},{9,11},{10,... | collective-permute-start | bytes 1277960 | tf_op jit(solution)/shard_map/ppermute | solution.py:179
  741.5 9.0 %collective-permute-start.2 = (bf16[208,1024]{1,0:T(8,128)(2,1)S(1)}, bf16[208,1024]{1,0:T(8,128)(2,1)S(1)}, u32[]{:S(2)}, u32[]{:S(2)}) collective-permute-start(bf16[208,1024]{1,0:T(8,128)(2,1)S(1)} %add_convert_fusion.4), channel_id=1, source_target_pairs={{0,4},{1,5},{2,6},{3,7},{4,0},{5,1},{6,2},{7,3},{8,12},{9,13},{10,... | collective-permute-start | bytes 1277960 | tf_op jit(solution)/shard_map/ppermute | solution.py:179
Sparse Core Ops, SparseCore 0:
  12.7 77.4 all-gather.4
  92.6 188.2 all-gather.6
  320.9 87.6 reduce-scatter.3
  412.8 206.6 reduce-scatter.5
  623.6 95.1 reduce-scatter.7

commit v7 on v5

--- a/solution.py
+++ b/solution.py
@@ -14,6 +14,9 @@
 EPS = 1e-06
 MASKED = -1e30
 GAIN_ROWS = 16
+FSDP = ("zh", "y", "core")
+CTX = ("zl", "x")
+Z_CROSS = [(0, 3), (3, 0), (1, 2), (2, 1)]
 
 
 HEAD_BLOCK = 128
@@ -172,11 +175,36 @@
     return jnp.pad(row, pads)
 
 
+def zh_pair(mine, other):
+    first = lax.axis_index("zh") == 0
+    return jnp.stack([jnp.where(first, mine, other), jnp.where(first, other, mine)])
+
+
+def fsdp_gather(pack):
+    other = lax.ppermute(pack, ("zh", "zl"), Z_CROSS)
+    both = lax.all_gather(zh_pair(pack, other), ("y", "core"), axis=0, tiled=False)
+    return jnp.swapaxes(both, 0, 1).reshape((-1,) + pack.shape)
+
+
+def fsdp_reduce_scatter(grads):
+    n_yc = grads.shape[0] // 2
+    by_yc = jnp.swapaxes(grads.reshape((2, n_yc) + grads.shape[1:]), 0, 1)
+    block = grads.shape[1:]
+    halves = lax.psum_scatter(
+        by_yc.reshape((n_yc, 2 * block[0]) + block[1:]), ("y", "core"), scatter_dimension=0, tiled=False
+    ).reshape((2,) + block)
+    zh = lax.axis_index("zh")
+    mine = lax.dynamic_index_in_dim(halves, zh, axis=0, keepdims=False)
+    theirs = lax.dynamic_index_in_dim(halves, 1 - zh, axis=0, keepdims=False)
+    got = lax.ppermute(theirs, ("zh", "zl"), Z_CROSS)
+    return (mine.astype(jnp.float32) + got.astype(jnp.float32)).astype(jnp.bfloat16)
+
+
 def ctx_allreduce(part, n_ctx):
     total = part
     step = 1
     while step < n_ctx:
-        other = lax.ppermute(total, "ctx", [(j, j ^ step) for j in range(n_ctx)])
+        other = lax.ppermute(total, CTX, [(j, j ^ step) for j in range(n_ctx)])
         total = (total.astype(jnp.float32) + other.astype(jnp.float32)).astype(jnp.bfloat16)
         step *= 2
     return total.astype(jnp.float32)
@@ -203,8 +231,8 @@
     head_count = H
     head_dim = width // head_count
     score_scale = head_dim ** (-0.5)
-    n_fsdp = lax.axis_size("fsdp")
-    n_ctx = lax.axis_size("ctx")
+    n_fsdp = lax.axis_size(FSDP)
+    n_ctx = lax.axis_size(CTX)
     total_len = rows * n_ctx
     w_rows = query_weight.shape[0]
     g_len = prenorm_gain.shape[0]
@@ -214,8 +242,8 @@
     slot_count = assignment.shape[0]
     chosen = assignment[:, None] == jnp.arange(slot_count, dtype=jnp.int32)[None, :]
     lengths_all = jnp.sum(jnp.where(chosen, lengths[None, :], 0), axis=1)
-    slot_lengths = lax.dynamic_slice_in_dim(lengths_all, lax.axis_index("fsdp") * slots, slots)
-    query_places = lax.axis_index("ctx") * rows + jnp.arange(rows, dtype=jnp.int32)
+    slot_lengths = lax.dynamic_slice_in_dim(lengths_all, lax.axis_index(FSDP) * slots, slots)
+    query_places = lax.axis_index(CTX) * rows + jnp.arange(rows, dtype=jnp.int32)
     valid = query_places[None, :] < slot_lengths[:, None]
     cosine, sine = rope_tables(query_places, head_dim // 2)
     cos_rows = cosine[None, :, None, :]
@@ -227,7 +255,7 @@
          gain_block(prenorm_gain, midnorm_gain, width)],
         axis=0,
     )
-    attn_all = lax.all_gather(attn_pack, "fsdp", axis=0, tiled=False)
+    attn_all = fsdp_gather(attn_pack)
 
     def attn_part(i):
         return attn_all[:, i * w_rows:(i + 1) * w_rows, :].reshape(n_fsdp * w_rows, width)
@@ -239,7 +267,7 @@
     mlp_pack = jnp.concatenate(
         [gate_weight, up_weight, down_weight.reshape(w_rows, ff)], axis=1
     )
-    mlp_all = lax.all_gather(mlp_pack, "fsdp", axis=0, tiled=False)
+    mlp_all = fsdp_gather(mlp_pack)
     gate_mat = mlp_all[:, :, 0:ff].reshape(n_fsdp * w_rows, ff)
     upper_mat = mlp_all[:, :, ff:2 * ff].reshape(n_fsdp * w_rows, ff)
     down_mat = mlp_all[:, :, 2 * ff:].reshape(n_fsdp, d_rows, width).reshape(n_fsdp * d_rows, width)
@@ -262,9 +290,9 @@
 
     kv_own = jnp.concatenate([key_rot, value_mix], axis=-1).reshape(rows, 2 * width)
     kv_all = lax.all_to_all(
-        jnp.broadcast_to(kv_own[None], (n_ctx, rows, 2 * width)), "ctx", 0, 0, tiled=False
+        jnp.broadcast_to(kv_own[None], (n_ctx, rows, 2 * width)), CTX, 0, 0, tiled=False
     ).reshape(total_len, 2 * width)
-    meta = jnp.stack([lax.axis_index("ctx") * rows, slot_lengths[0]]).astype(jnp.int32)
+    meta = jnp.stack([lax.axis_index(CTX) * rows, slot_lengths[0]]).astype(jnp.int32)
     query_flat = query_rotated_rows.reshape(rows, width)
     mixed_low = attention_forward(
         meta, query_flat, kv_all, head_dim, score_scale
@@ -314,7 +342,7 @@
         ],
         axis=2,
     ).astype(jnp.bfloat16)
-    mlp_share = lax.psum_scatter(mlp_grads, "fsdp", scatter_dimension=0, tiled=False)
+    mlp_share = fsdp_reduce_scatter(mlp_grads)
 
     blended_value_gradient = jnp.einsum(
         "sre,de->srd", middle_low, out_mat, preferred_element_type=jnp.float32
@@ -324,7 +352,7 @@
     )
     query_rot_back = query_rot_back.reshape(slots, rows, head_count, head_dim)
     key_value = jnp.sum(
-        lax.all_to_all(kv_back.reshape(n_ctx, rows, 2 * width), "ctx", 0, 0, tiled=False).astype(
+        lax.all_to_all(kv_back.reshape(n_ctx, rows, 2 * width), CTX, 0, 0, tiled=False).astype(
             jnp.float32
         ),
         axis=0,
@@ -377,7 +405,7 @@
     ).astype(jnp.bfloat16)
     attn_grads, mlp_share = lax.optimization_barrier((attn_grads, mlp_share))
     mlp_share = ctx_allreduce(mlp_share, n_ctx)
-    attn_share = lax.psum_scatter(attn_grads, "fsdp", scatter_dimension=0, tiled=False)
+    attn_share = fsdp_reduce_scatter(attn_grads)
     attn_share = ctx_allreduce(attn_share, n_ctx)
 
     def attn_grad(i):
@@ -407,39 +435,45 @@
 
 
 def solution(mesh):
+    zh = 2
+    zl = 2
+    n_f, n_c = mesh.devices.shape
+    fine = jax.sharding.Mesh(
+        mesh.devices.reshape(zh, n_f // (2 * zh), 2, zl, n_c // zl), FSDP + CTX
+    )
     placed = (
-        P("fsdp", "ctx", None),
-        P("fsdp", "ctx", None),
-        P("fsdp", None),
-        P("fsdp", None),
-        P("fsdp", None),
-        P("fsdp", None),
-        P("fsdp", None),
-        P("fsdp", None),
-        P("fsdp", None),
-        P("fsdp"),
-        P("fsdp"),
-        P("fsdp", "ctx", None),
+        P(FSDP, CTX, None),
+        P(FSDP, CTX, None),
+        P(FSDP, None),
+        P(FSDP, None),
+        P(FSDP, None),
+        P(FSDP, None),
+        P(FSDP, None),
+        P(FSDP, None),
+        P(FSDP, None),
+        P(FSDP),
+        P(FSDP),
+        P(FSDP, CTX, None),
         P(),
         P(),
     )
     return jax.shard_map(
         body,
-        mesh=mesh,
+        mesh=fine,
         in_specs=placed,
         out_specs=(
-            P("fsdp", "ctx", None),
-            P("fsdp", "ctx", None),
-            P("fsdp", "ctx", None),
-            P("fsdp", None),
-            P("fsdp", None),
-            P("fsdp", None),
-            P("fsdp", None),
-            P("fsdp", None),
-            P("fsdp", None),
-            P("fsdp", None),
-            P("fsdp"),
-            P("fsdp"),
+            P(FSDP, CTX, None),
+            P(FSDP, CTX, None),
+            P(FSDP, CTX, None),
+            P(FSDP, None),
+            P(FSDP, None),
+            P(FSDP, None),
+            P(FSDP, None),
+            P(FSDP, None),
+            P(FSDP, None),
+            P(FSDP, None),
+            P(FSDP),
+            P(FSDP),
         ),
         check_vma=False,
     )

time: 752 us -> 731 us (0.972)
  waiting for transfers between devices: 466 us -> 334 us
  starting transfers between devices: 22.1 us -> 90.7 us
  local copies, waits for them, and re-layouts: 79.4 us -> 113 us
    reduce_scatter x2, waiting for transfers between devices: 95.1 us -> 0.01 us  [fsdp_reduce_scatter(): lax.psum_scatter(by_yc.reshape((n_yc, 2 * block[0]) + block[1:]), ('y', '...]
    all_gather x2, waiting for transfers between devices: 93.7 us -> 24.2 us  [fsdp_gather(): lax.all_gather(zh_pair(pack, other), ('y', 'core'), axis=0, tiled=False)]
    ppermute x6 -> x10, waiting for transfers between devices: 67.8 us -> 125 us  [the longest x6 64.4 us: ctx_allreduce(): other = lax.ppermute(total, CTX, [(j, j ^ step) for j in range(n_ctx)])]
    ppermute x6 -> x10, starting transfers between devices: 11.7 us -> 49.3 us  [the longest x6 36.3 us: ctx_allreduce(): other = lax.ppermute(total, CTX, [(j, j ^ step) for j in range(n_ctx)])]
    transpose x0 -> x3, local copies, waits for them, and re-layouts: none -> 33 us  [the longest x2 16.5 us: fsdp_gather(): return jnp.swapaxes(both, 0, 1).reshape((-1,) + pack.shape)]
    all_to_all x1, starting transfers between devices: 4.95 us -> 35.3 us  [body(): lax.all_to_all(kv_back.reshape(n_ctx, rows, 2 * width), CTX, 0, 0, tiled=...]
    concatenate x2 -> x0, other arithmetic: 15.3 us -> none  [the longest x1 14.2 us: body(): jnp.concatenate([gate_total.reshape(n_fsdp, w_rows, ff), upper_total.resh...]
    transpose x0 -> x1, other arithmetic: none -> 14.3 us  [fsdp_reduce_scatter(): by_yc = jnp.swapaxes(grads.reshape((2, n_yc) + grads.shape[1:]), 0, 1)]
  transfers between devices with their start and end apart: 12 -> 16, of which waited for: 11 -> 13; matrix products, arithmetic and copies ran while one was open for 11% -> 13% of each run, Pallas kernels for 9% -> 9%
where the time goes in v7:
time: 731 us; the launch traced here: 723 us
  waiting for transfers between devices  334 us (46%)
  local copies, waits for them, and re-layouts  113 us (15%)
  starting transfers between devices  90.7 us (12%)
  Pallas kernels  67.8 us (9%)
  matrix products  55.8 us (8%)
  other arithmetic  46.1 us (6%)
  between operations  14.9 us (2%)
    all_to_all x1, waiting for transfers between devices, body(): lax.all_to_all(kv_back.reshape(n_ctx, rows, 2 * width), CTX, 0, 0, tiled=...  93 us
    all_to_all x1, waiting for transfers between devices, body(): lax.all_to_all(jnp.broadcast_to(kv_own[None], (n_ctx, rows, 2 * width)),...  91.7 us
    ppermute x6, waiting for transfers between devices, ctx_allreduce(): other = lax.ppermute(total, CTX, [(j, j ^ step) for j in range(n_ctx)])  64.4 us
    pallas_call x1, Pallas kernels, attention_backward(): pl.pallas_call(functools.partial(attn_bwd_kernel, head_dim, scale), out_s...  43.4 us
    ppermute x6, starting transfers between devices, ctx_allreduce(): other = lax.ppermute(total, CTX, [(j, j ^ step) for j in range(n_ctx)])  36.3 us
    ppermute x2, waiting for transfers between devices, fsdp_gather(): other = lax.ppermute(pack, ('zh', 'zl'), Z_CROSS)  35.9 us
    all_to_all x1, starting transfers between devices, body(): lax.all_to_all(kv_back.reshape(n_ctx, rows, 2 * width), CTX, 0, 0, tiled=...  35.3 us
    ppermute x2, waiting for transfers between devices, fsdp_reduce_scatter(): got = lax.ppermute(theirs, ('zh', 'zl'), Z_CROSS)  24.7 us
  transfers between devices with their start and end apart: 16, of which 13 were waited for; matrix products, arithmetic and copies ran while one was open for 13% of the time, Pallas kernels for 9%

profile of v7, /device:TPU:0, one launch (start us, length us, event | category | flops | bytes accessed | tf_op | source)
XLA Modules:
  0.0 722.5 jit_solution(10238883008610687366)
XLA Ops:
  11.7 4.2 collective-permute-start
  15.9 12.6 %collective-permute-done = bf16[272,1024]{1,0:T(8,128)(2,1)S(1)} collective-permute-done((bf16[272,1024]{1,0:T(8,128)(2,1)S(1)}, bf16[272,1024]{1,0:T(8,128)(2,1)S(1)}, u32[]{:S(2)}, u32[]{:S(2)}) %collective-permute-start) | collective-permute-done | bytes 557088 | tf_op jit(solution)/shard_map/ppermute | solution.py:184
  30.3 3.1 collective-permute-start.1
  33.4 23.3 %collective-permute-done.1 = bf16[64,8448]{1,0:T(8,128)(2,1)S(1)} collective-permute-done((bf16[64,8448]{1,0:T(8,128)(2,1)S(1)}, bf16[64,8448]{1,0:T(8,128)(2,1)S(1)}, u32[]{:S(2)}, u32[]{:S(2)}) %collective-permute-start.1) | collective-permute-done | bytes 1081376 | tf_op jit(solution)/shard_map/ppermute | solution.py:184
  56.8 1.6 pad_maximum_fusion
  58.9 24.2 %all-gather.5.cloned.1.call-done = bf16[16,272,1024]{2,1,0:T(8,128)(2,1)} async-done(((bf16[2,272,1024]{2,1,0:T(8,128)(2,1)}), bf16[16,272,1024]{2,1,0:T(8,128)(2,1)}) %all-gather.5.cloned.1.call-update) | async-done | bytes 8912912 | tf_op jit(solution)/shard_map/all_gather | solution.py:185
  83.1 8.4 %copy.93 = bf16[2,8,272,1024]{3,2,1,0:T(8,128)(2,1)} copy(bf16[2,8,272,1024]{3,2,0,1:T(8,128)(2,1)} %bitcast.212) | data formatting | bytes 17825792 | tf_op jit(solution)/shard_map/transpose | solution.py:186
  92.5 7.5 %fusion.58 = (bf16[16,64,1024]{2,1,0:T(8,128)(2,1)S(1)}, bf16[16,64,1024]{2,1,0:T(8,128)(2,1)}, bf16[16,64,1024]{2,1,0:T(8,128)(2,1)}, bf16[16,64,1024]{2,1,0:T(8,128)(2,1)}) fusion(bf16[16,272,1024]{2,1,0:T(8,128)(2,1)} %bitcast.202), kind=kLoop, calls=%fused_computation.142 | loop fusion | bytes 16777216 | tf_op jit(solution)/shard_map/slice | solution.py:261
  100.0 4.0 copy.94
  104.1 3.9 copy.95
  108.0 2.6 convolution_bitcast_fusion.3
  112.6 2.2 copy.96
  114.8 2.5 fusion.9
  117.4 4.4 broadcast_in_dim.72
  121.8 5.6 all-to-all-start
  130.4 91.7 %all-to-all-done = bf16[8,256,2048]{2,1,0:T(8,128)(2,1)} async-done(((bf16[8,256,2048]{2,1,0:T(8,128)(2,1)}), bf16[8,256,2048]{2,1,0:T(8,128)(2,1)}, u32[]{:S(2)}, u32[]{:S(2)}) %all-to-all-start) | async-done | bytes 8388640 | tf_op jit(solution)/shard_map/all_to_all | solution.py:292
  222.1 24.4 %shard_map.229 = bf16[256,1024]{1,0:T(8,128)(2,1)S(1)} custom-call(s32[2]{0:T(128)S(1)} %pad_add_fusion.meta_ref, bf16[256,1024]{1,0:T(8,128)(2,1)S(1)} %copy.97.q_ref, bf16[2048,2048]{1,0:T(8,128)(2,1)} %bitcast.22.k_ref.v_ref, bf16[2048,2048]{1,0:T(8,128)(2,1)} %bitcast.22.k_ref.v_ref), custom_call_target="tpu_custom_call" | custom-call | flops 2147483648 | bytes 9437184 | tf_op jit(solution)/shard_map/pallas_call | solution.py:80
  247.4 1.9 multiply_reduce_fusion
  252.5 8.1 %copy.98 = bf16[2,8,64,8448]{3,2,1,0:T(8,128)(2,1)S(1)} copy(bf16[2,8,64,8448]{3,2,0,1:T(8,128)(2,1)} %bitcast.211) | data formatting | bytes 34603008 | tf_op jit(solution)/shard_map/transpose | solution.py:186
  260.6 6.1 fusion.57
  266.7 11.7 %reshape_reshape.4 = bf16[2816,1024]{1,0:T(8,128)(2,1)} reshape(bf16[16,64,2816]{2,1,0:T(8,128)(2,1)} %get-tuple-element.74) | data formatting | bytes 11534336 | tf_op jit(solution)/shard_map/reshape;reshape | solution.py:273
  278.4 4.8 fusion.32
  283.4 3.3 fusion.34
  286.7 6.2 multiply_convert_fusion
  292.9 1.7 fusion.62
  294.6 4.1 convolution_convert_fusion.2
  298.8 4.1 convolution_convert_fusion.1
  302.9 2.8 fusion.24
  305.7 4.3 convolution_convert_fusion
  310.0 11.8 %concatenate.69 = bf16[2,8,64,2816]{3,2,1,0:T(8,128)(2,1)} reshape(bf16[2816,1024]{1,0:T(8,128)(2,1)} %convolution_convert_fusion) | data formatting | bytes 11534336 | tf_op jit(solution)/shard_map/concatenate | solution.py:336
  321.7 2.0 fusion.26
  325.4 14.3 %maximum_bitcast_fusion = bf16[8,2,64,9472]{3,2,0,1:T(8,128)(2,1)} fusion(bf16[2,8,64,1024]{3,2,1,0:T(8,128)(2,1)S(1)} %convolution_convert_fusion.3, bf16[2,8,64,2816]{3,2,1,0:T(8,128)(2,1)} %concatenate.69, bf16[2,8,64,2816]{3,2,1,0:T(8,128)(2,1)} %convolution_convert_fusion.1, bf16[2,8,64,2816]{3,2,1,0:T(8,128)(2,1)} %convolution_convert_fusion.2), kind=kLoop, calls=%fused_computation | loop fusion | flops 77594624 | bytes 38797312 | tf_op jit(solution)/shard_map/transpose | solution.py:191
  339.7 16.5 %copy.109 = bf16[8,2,64,9472]{3,2,1,0:T(8,128)(2,1)} copy(bf16[8,2,64,9472]{3,2,0,1:T(8,128)(2,1)} %maximum_bitcast_fusion) | data formatting | bytes 38797312 | tf_op jit(solution)/shard_map/transpose | solution.py:191
  356.2 2.0 convolution_convert_fusion.7.do_ref
  358.2 43.4 %shard_map.230 = (f32[256,1024]{1,0:T(8,128)S(1)}, bf16[2048,2048]{1,0:T(8,128)(2,1)}) custom-call(s32[2]{0:T(128)S(1)} %pad_add_fusion.meta_ref, bf16[256,1024]{1,0:T(8,128)(2,1)S(1)} %copy.97.q_ref, bf16[2048,2048]{1,0:T(8,128)(2,1)} %bitcast.22.k_ref.v_ref, bf16[2048,2048]{1,0:T(8,128)(2,1)} %bitcast.22.k_ref.v_ref, ...), custom_call_target="tpu_custom_call" | custom-call | flops 5368709120 | bytes 19398656 | tf_op jit(solution)/shard_map/pallas_call | solution.py:108
  401.6 35.3 %all-to-all-start.1 = ((bf16[8,256,2048]{2,1,0:T(8,128)(2,1)}), bf16[8,256,2048]{2,1,0:T(8,128)(2,1)}, u32[]{:S(2)}, u32[]{:S(2)}) async-start(bf16[8,256,2048]{2,1,0:T(8,128)(2,1)} %bitcast.213), calls=%async_computation.1 | async-start | bytes 16777216 | tf_op jit(solution)/shard_map/all_to_all | solution.py:355
  437.3 93.0 %all-to-all-done.1 = bf16[8,256,2048]{2,1,0:T(8,128)(2,1)} async-done(((bf16[8,256,2048]{2,1,0:T(8,128)(2,1)}), bf16[8,256,2048]{2,1,0:T(8,128)(2,1)}, u32[]{:S(2)}, u32[]{:S(2)}) %all-to-all-start.1) | async-done | bytes 8388640 | tf_op jit(solution)/shard_map/all_to_all | solution.py:355
  530.3 5.3 convert_reduce_fusion
  535.6 2.1 copy.101
  537.7 2.8 slice_multiply_fusion
  548.2 2.0 convolution_convert_fusion.4
  550.2 2.1 convolution_convert_fusion.5
  552.3 2.0 convolution_convert_fusion.6
  554.3 1.5 dynamic-slice_bitcast_fusion
  555.8 3.0 collective-permute-start.2
  558.8 3.1 fusion.1
  562.0 23.5 %collective-permute-done.2 = bf16[64,9472]{1,0:T(8,128)(2,1)S(1)} collective-permute-done((bf16[64,9472]{1,0:T(8,128)(2,1)S(1)}, bf16[64,9472]{1,0:T(8,128)(2,1)S(1)}, u32[]{:S(2)}, u32[]{:S(2)}) %collective-permute-start.2) | collective-permute-done | bytes 1212448 | tf_op jit(solution)/shard_map/ppermute | solution.py:199
  585.4 1.4 fusion.2
  586.8 3.6 copy.110
  590.4 27.9 %collective-permute-start.7 = (bf16[64,9472]{1,0:T(8,128)(2,1)}, bf16[64,9472]{1,0:T(8,128)(2,1)S(1)}, u32[]{:S(2)}, u32[]{:S(2)}) collective-permute-start(bf16[64,9472]{1,0:T(8,128)(2,1)} %fusion.2), channel_id=1, source_target_pairs={{0,1},{1,0},{2,3},{3,2},{4,5},{5,4},{6,7},{7,6},{8,9},{9,8},{10,11... | collective-permute-start | bytes 3637256 | tf_op jit(solution)/shard_map/ppermute | solution.py:207
  618.3 24.3 %collective-permute-done.7 = bf16[64,9472]{1,0:T(8,128)(2,1)S(1)} collective-permute-done((bf16[64,9472]{1,0:T(8,128)(2,1)}, bf16[64,9472]{1,0:T(8,128)(2,1)S(1)}, u32[]{:S(2)}, u32[]{:S(2)}) %collective-permute-start.7) | collective-permute-done | bytes 1212448 | tf_op jit(solution)/shard_map/ppermute | solution.py:207
  642.7 1.6 add_convert_fusion.2
  644.3 4.6 collective-permute-start.8
  648.9 24.0 %collective-permute-done.8 = bf16[64,9472]{1,0:T(8,128)(2,1)S(1)} collective-permute-done((bf16[64,9472]{1,0:T(8,128)(2,1)S(1)}, bf16[64,9472]{1,0:T(8,128)(2,1)S(1)}, u32[]{:S(2)}, u32[]{:S(2)}) %collective-permute-start.8) | collective-permute-done | bytes 1212448 | tf_op jit(solution)/shard_map/ppermute | solution.py:207
  672.9 1.4 add_convert_fusion.1
  675.3 2.7 collective-permute-start.3
  678.1 5.5 fusion.10
  685.4 2.5 copy.111
  687.9 1.3 fusion.18
  689.2 6.5 collective-permute-done.4
  695.9 2.7 collective-permute-start.5
  699.7 1.9 fusion.13
  702.3 3.3 collective-permute-done.5
  708.8 5.2 collective-permute-done.6
  (142 shorter events, 36.4 us)
Async XLA Ops:
  7.2 75.9 %all-gather.5.cloned.1.call-start = ((), (), s32[]{:S(2)}) async-start(), calls=%async_computation.6 | async-start | bytes 10027008 | tf_op jit(solution)/shard_map/all_gather | solution.py:185
  11.7 16.8 %collective-permute-start = (bf16[272,1024]{1,0:T(8,128)(2,1)S(1)}, bf16[272,1024]{1,0:T(8,128)(2,1)S(1)}, u32[]{:S(2)}, u32[]{:S(2)}) collective-permute-start(bf16[272,1024]{1,0:T(8,128)(2,1)S(1)} %pad_dynamic-update-slice_fusion), channel_id=1, source_target_pairs={{0,68},{68,0},{4,64},{64,4},{1,69},{69,1},{5,65},{65,5},{2,70},{70... | collective-permute-start | bytes 1671176 | tf_op jit(solution)/shard_map/ppermute | solution.py:184
  15.9 13.9 %copy-start.22 = (bf16[176,1024]{1,0:T(8,128)(2,1)S(1)}, bf16[176,1024]{1,0:T(8,128)(2,1)}, u32[]{:S(2)}) copy-start(bf16[176,1024]{1,0:T(8,128)(2,1)} %param.22) | copy-start | bytes 1081348
  28.6 1.6 copy-start.23
  28.6 1.7 copy-start.24
  29.7 222.8 %all-gather.7.cloned.1.call-start = ((), (), s32[]{:S(2)}) async-start(), calls=%async_computation.7 | async-start | bytes 19464192 | tf_op jit(solution)/shard_map/all_gather | solution.py:185
  30.3 26.3 %collective-permute-start.1 = (bf16[64,8448]{1,0:T(8,128)(2,1)S(1)}, bf16[64,8448]{1,0:T(8,128)(2,1)S(1)}, u32[]{:S(2)}, u32[]{:S(2)}) collective-permute-start(bf16[64,8448]{1,0:T(8,128)(2,1)S(1)} %constant_dynamic-update-slice_fusion.4), channel_id=1, source_target_pairs={{0,68},{68,0},{4,64},{64,4},{1,69},{69,1},{5,65},{65,5},{2,70},{70... | collective-permute-start | bytes 3244040 | tf_op jit(solution)/shard_map/ppermute | solution.py:184
  56.8 1.7 copy-start.8
  108.0 2.6 copy-start.19
  114.8 2.5 copy-start.20
  121.8 6.1 copy-start.25
  121.8 6.1 copy-start.26
  121.8 100.2 %all-to-all-start = ((bf16[8,256,2048]{2,1,0:T(8,128)(2,1)}), bf16[8,256,2048]{2,1,0:T(8,128)(2,1)}, u32[]{:S(2)}, u32[]{:S(2)}) async-start(bf16[8,256,2048]{2,1,0:T(8,128)(2,1)} %broadcast_in_dim.72), calls=%async_computation | async-start | bytes 16777216 | tf_op jit(solution)/shard_map/all_to_all | solution.py:292
  127.4 426.9 %reduce-scatter.3.cloned.1.call-start = ((), (), s32[]{:S(2)}) async-start(), calls=%async_computation.4 | async-start | bytes 21823488 | tf_op jit(solution)/shard_map/reduce_scatter | solution.py:193
  249.3 1.0 copy-start.4
  278.4 4.8 copy-start.5
  278.4 4.9 copy-start.11
  278.4 8.2 %slice-start = ((s8[5767168]{0:T(1024)(128)(4,1)}), s8[4194304]{0:T(1024)(128)(4,1)S(1)}, s32[]{:S(2)}) async-start(s8[5767168]{0:T(1024)(128)(4,1)} %bitcast.220), calls=%async_computation.8 | async-start | bytes 8388608
  283.3 3.4 slice-start.1
  283.4 3.3 copy-start.16
  292.9 12.8 %copy-start.14 = (bf16[256,2816]{1,0:T(8,128)(2,1)}, bf16[256,2816]{1,0:T(8,128)(2,1)S(1)}, u32[]{:S(2)}) copy-start(bf16[256,2816]{1,0:T(8,128)(2,1)S(1)} %get-tuple-element.83) | copy-start | bytes 4325380
  294.6 8.3 %slice-start.2 = ((s8[5767168]{0:T(1024)(128)(4,1)}), s8[4194304]{0:T(1024)(128)(4,1)S(1)}, s32[]{:S(2)}) async-start(s8[5767168]{0:T(1024)(128)(4,1)} %bitcast.223), calls=%async_computation.10 | async-start | bytes 8388608
  298.7 4.2 slice-start.3
  310.0 11.8 %copy-start.17 = (bf16[1,256,1024]{2,1,0:T(8,128)(2,1)S(1)}, bf16[1,256,1024]{2,1,0:T(8,128)(2,1)}, u32[]{:S(2)}) copy-start(bf16[1,256,1024]{2,1,0:T(8,128)(2,1)} %param.25) | copy-start | bytes 1572868
  321.7 3.0 copy-start.18
  323.8 1.0 copy-start.2
  401.6 128.7 %all-to-all-start.1 = ((bf16[8,256,2048]{2,1,0:T(8,128)(2,1)}), bf16[8,256,2048]{2,1,0:T(8,128)(2,1)}, u32[]{:S(2)}, u32[]{:S(2)}) async-start(bf16[8,256,2048]{2,1,0:T(8,128)(2,1)} %bitcast.213), calls=%async_computation.1 | async-start | bytes 16777216 | tf_op jit(solution)/shard_map/all_to_all | solution.py:355
  436.9 237.4 %reduce-scatter.5.cloned.1.call-start = ((), (), s32[]{:S(2)}) async-start(), calls=%async_computation.5 | async-start | bytes 7667712 | tf_op jit(solution)/shard_map/reduce_scatter | solution.py:193
  540.5 1.8 copy-start.1
  540.9 2.2 copy-start
  540.9 2.9 copy-start.12
  543.0 1.6 copy-start.10
  543.9 1.5 copy-start.9
  548.1 4.1 copy-start.13
  554.3 4.6 copy-start.7
  555.8 29.7 %copy-start.15 = (bf16[1,128,9472]{2,1,0:T(8,128)(2,1)S(1)}, bf16[1,128,9472]{2,1,0:T(8,128)(2,1)}, u32[]{:S(2)}) copy-start(bf16[1,128,9472]{2,1,0:T(8,128)(2,1)} %reduce-scatter.3.cloned.1.call-done) | copy-start | bytes 7274500
  555.8 29.6 %collective-permute-start.2 = (bf16[64,9472]{1,0:T(8,128)(2,1)S(1)}, bf16[64,9472]{1,0:T(8,128)(2,1)S(1)}, u32[]{:S(2)}, u32[]{:S(2)}) collective-permute-start(bf16[64,9472]{1,0:T(8,128)(2,1)S(1)} %dynamic-slice_bitcast_fusion), channel_id=1, source_target_pairs={{0,68},{68,0},{4,64},{64,4},{1,69},{69,1},{5,65},{65,5},{2,70},{70... | collective-permute-start | bytes 3637256 | tf_op jit(solution)/shard_map/ppermute | solution.py:199
  590.4 52.2 %collective-permute-start.7 = (bf16[64,9472]{1,0:T(8,128)(2,1)}, bf16[64,9472]{1,0:T(8,128)(2,1)S(1)}, u32[]{:S(2)}, u32[]{:S(2)}) collective-permute-start(bf16[64,9472]{1,0:T(8,128)(2,1)} %fusion.2), channel_id=1, source_target_pairs={{0,1},{1,0},{2,3},{3,2},{4,5},{5,4},{6,7},{7,6},{8,9},{9,8},{10,11... | collective-permute-start | bytes 3637256 | tf_op jit(solution)/shard_map/ppermute | solution.py:207
  644.2 33.8 %copy-start.6 = (f32[1,256,1024]{2,1,0:T(8,128)S(1)}, f32[1,256,1024]{2,1,0:T(8,128)}, u32[]{:S(2)}) copy-start(f32[1,256,1024]{2,1,0:T(8,128)} %copy-done.4) | copy-start | bytes 3145732
  644.3 28.6 %collective-permute-start.8 = (bf16[64,9472]{1,0:T(8,128)(2,1)S(1)}, bf16[64,9472]{1,0:T(8,128)(2,1)S(1)}, u32[]{:S(2)}, u32[]{:S(2)}) collective-permute-start(bf16[64,9472]{1,0:T(8,128)(2,1)S(1)} %add_convert_fusion.2), channel_id=1, source_target_pairs={{0,2},{1,3},{2,0},{3,1},{4,6},{5,7},{6,4},{7,5},{8,10},{9,11},{10,... | collective-permute-start | bytes 3637256 | tf_op jit(solution)/shard_map/ppermute | solution.py:207
  674.3 25.4 %collective-permute-start.9 = (bf16[64,9472]{1,0:T(8,128)(2,1)}, bf16[64,9472]{1,0:T(8,128)(2,1)}, u32[]{:S(2)}, u32[]{:S(2)}) collective-permute-start(bf16[64,9472]{1,0:T(8,128)(2,1)} %add_convert_fusion.1), channel_id=1, source_target_pairs={{0,4},{1,5},{2,6},{3,7},{4,0},{5,1},{6,2},{7,3},{8,12},{9,13},{10,... | collective-permute-start | bytes 3637256 | tf_op jit(solution)/shard_map/ppermute | solution.py:207
  675.3 9.6 %copy-start.21 = (bf16[1,416,1024]{2,1,0:T(8,128)(2,1)S(1)}, bf16[1,416,1024]{2,1,0:T(8,128)(2,1)}, u32[]{:S(2)}) copy-start(bf16[1,416,1024]{2,1,0:T(8,128)(2,1)} %reduce-scatter.5.cloned.1.call-done) | copy-start | bytes 2555908
  675.3 9.5 %collective-permute-start.3 = (bf16[208,1024]{1,0:T(8,128)(2,1)S(1)}, bf16[208,1024]{1,0:T(8,128)(2,1)S(1)}, u32[]{:S(2)}, u32[]{:S(2)}) collective-permute-start(bf16[208,1024]{1,0:T(8,128)(2,1)S(1)} %dynamic-slice_bitcast_fusion.1), channel_id=1, source_target_pairs={{0,68},{68,0},{4,64},{64,4},{1,69},{69,1},{5,65},{65,5},{2,70},{70... | collective-permute-start | bytes 1277960 | tf_op jit(solution)/shard_map/ppermute | solution.py:199
  683.6 4.3 copy-start.3
  685.0 10.7 %collective-permute-start.4 = (bf16[208,1024]{1,0:T(8,128)(2,1)S(1)}, bf16[208,1024]{1,0:T(8,128)(2,1)S(1)}, u32[]{:S(2)}, u32[]{:S(2)}) collective-permute-start(bf16[208,1024]{1,0:T(8,128)(2,1)S(1)} %fusion.28), channel_id=1, source_target_pairs={{0,1},{1,0},{2,3},{3,2},{4,5},{5,4},{6,7},{7,6},{8,9},{9,8},{10,11... | collective-permute-start | bytes 1277960 | tf_op jit(solution)/shard_map/ppermute | solution.py:207
  695.9 9.7 %collective-permute-start.5 = (bf16[208,1024]{1,0:T(8,128)(2,1)S(1)}, bf16[208,1024]{1,0:T(8,128)(2,1)S(1)}, u32[]{:S(2)}, u32[]{:S(2)}) collective-permute-start(bf16[208,1024]{1,0:T(8,128)(2,1)S(1)} %add_convert_fusion.5), channel_id=1, source_target_pairs={{0,2},{1,3},{2,0},{3,1},{4,6},{5,7},{6,4},{7,5},{8,10},{9,11},{10,... | collective-permute-start | bytes 1277960 | tf_op jit(solution)/shard_map/ppermute | solution.py:207
  705.7 8.2 %collective-permute-start.6 = (bf16[208,1024]{1,0:T(8,128)(2,1)S(1)}, bf16[208,1024]{1,0:T(8,128)(2,1)S(1)}, u32[]{:S(2)}, u32[]{:S(2)}) collective-permute-start(bf16[208,1024]{1,0:T(8,128)(2,1)S(1)} %add_convert_fusion.4), channel_id=1, source_target_pairs={{0,4},{1,5},{2,6},{3,7},{4,0},{5,1},{6,2},{7,3},{8,12},{9,13},{10,... | collective-permute-start | bytes 1277960 | tf_op jit(solution)/shard_map/ppermute | solution.py:207
Sparse Core Ops, SparseCore 0:
  29.8 53.2 all-gather.4
  84.8 87.3 all-gather.6
  356.3 134.1 reduce-scatter.2
  590.6 72.5 reduce-scatter.4

commit v8 on v7

--- a/solution.py
+++ b/solution.py
@@ -175,6 +175,16 @@
     return jnp.pad(row, pads)
 
 
+def to_gathered(rows, block):
+    lead = rows.shape[:-1]
+    return jnp.swapaxes(rows.reshape(lead + (2, -1, block)), -3, -2).reshape(rows.shape)
+
+
+def from_gathered(rows, block):
+    lead = rows.shape[:-1]
+    return jnp.swapaxes(rows.reshape(lead + (-1, 2, block)), -3, -2).reshape(rows.shape)
+
+
 def zh_pair(mine, other):
     first = lax.axis_index("zh") == 0
     return jnp.stack([jnp.where(first, mine, other), jnp.where(first, other, mine)])
@@ -183,12 +193,12 @@
 def fsdp_gather(pack):
     other = lax.ppermute(pack, ("zh", "zl"), Z_CROSS)
     both = lax.all_gather(zh_pair(pack, other), ("y", "core"), axis=0, tiled=False)
-    return jnp.swapaxes(both, 0, 1).reshape((-1,) + pack.shape)
+    return both.reshape((-1,) + pack.shape)
 
 
 def fsdp_reduce_scatter(grads):
     n_yc = grads.shape[0] // 2
-    by_yc = jnp.swapaxes(grads.reshape((2, n_yc) + grads.shape[1:]), 0, 1)
+    by_yc = grads
     block = grads.shape[1:]
     halves = lax.psum_scatter(
         by_yc.reshape((n_yc, 2 * block[0]) + block[1:]), ("y", "core"), scatter_dimension=0, tiled=False
@@ -261,8 +271,10 @@
         return attn_all[:, i * w_rows:(i + 1) * w_rows, :].reshape(n_fsdp * w_rows, width)
 
     query_mat, key_mat, value_mat, out_mat = (attn_part(i) for i in range(4))
-    prenorm_full = attn_all[:, 4 * w_rows, 0:g_len].reshape(n_fsdp * g_len)
-    midnorm_full = attn_all[:, 4 * w_rows, g_len:2 * g_len].reshape(n_fsdp * g_len)
+    prenorm_full = from_gathered(attn_all[:, 4 * w_rows, 0:g_len].reshape(n_fsdp * g_len), g_len)
+    midnorm_full = from_gathered(
+        attn_all[:, 4 * w_rows, g_len:2 * g_len].reshape(n_fsdp * g_len), g_len
+    )
 
     mlp_pack = jnp.concatenate(
         [gate_weight, up_weight, down_weight.reshape(w_rows, ff)], axis=1
@@ -276,9 +288,10 @@
     first_wide = first_value.astype(jnp.float32)
     normed, inverse = norm_apply(tokens_wide, prenorm_full.astype(jnp.float32))
     normed_low = normed.astype(jnp.bfloat16)
-    query = jnp.dot(normed_low, query_mat, preferred_element_type=jnp.float32)
-    keyed = jnp.dot(normed_low, key_mat, preferred_element_type=jnp.float32)
-    own_value = jnp.dot(normed_low, value_mat, preferred_element_type=jnp.float32)
+    normed_low_g = to_gathered(normed_low, w_rows)
+    query = jnp.dot(normed_low_g, query_mat, preferred_element_type=jnp.float32)
+    keyed = jnp.dot(normed_low_g, key_mat, preferred_element_type=jnp.float32)
+    own_value = jnp.dot(normed_low_g, value_mat, preferred_element_type=jnp.float32)
     heads_shape = query.shape[:2] + (head_count, head_dim)
     query_rotated_rows = rotate(query.reshape(heads_shape), cos_rows, sin_rows).astype(jnp.bfloat16)
     key_rot = (
@@ -298,27 +311,32 @@
         meta, query_flat, kv_all, head_dim, score_scale
     ).reshape(slots, rows, width)
 
-    middle = tokens_wide + jnp.dot(mixed_low, out_mat, preferred_element_type=jnp.float32)
+    mixed_low_g = to_gathered(mixed_low, w_rows)
+    middle = tokens_wide + jnp.dot(mixed_low_g, out_mat, preferred_element_type=jnp.float32)
     normed_two, inverse_two = norm_apply(middle, midnorm_full.astype(jnp.float32))
     normed_two = normed_two.astype(jnp.bfloat16)
-    gate = jnp.dot(normed_two, gate_mat, preferred_element_type=jnp.float32)
-    upper = jnp.dot(normed_two, upper_mat, preferred_element_type=jnp.float32)
+    normed_two_g = to_gathered(normed_two, w_rows)
+    gate = jnp.dot(normed_two_g, gate_mat, preferred_element_type=jnp.float32)
+    upper = jnp.dot(normed_two_g, upper_mat, preferred_element_type=jnp.float32)
     hidden = (jax.nn.silu(gate) * upper).astype(jnp.bfloat16)
-    branch = jnp.dot(hidden, down_mat, preferred_element_type=jnp.float32)
+    hidden_g = to_gathered(hidden, d_rows)
+    branch = jnp.dot(hidden_g, down_mat, preferred_element_type=jnp.float32)
     layer_out = jnp.where(valid_wide, middle + branch, 0.0).astype(jnp.bfloat16)
 
     cot_wide = jnp.where(valid_wide, cotangent.astype(jnp.float32), 0.0)
     cot_low = cot_wide.astype(jnp.bfloat16)
-    down_total = jnp.einsum("srf,sre->fe", hidden, cot_low, preferred_element_type=jnp.float32)
-    hidden_back = jnp.einsum("sre,fe->srf", cot_low, down_mat, preferred_element_type=jnp.float32)
+    down_total = jnp.einsum("srf,sre->fe", hidden_g, cot_low, preferred_element_type=jnp.float32)
+    hidden_back = from_gathered(
+        jnp.einsum("sre,fe->srf", cot_low, down_mat, preferred_element_type=jnp.float32), d_rows
+    )
     sigma = jax.nn.sigmoid(gate)
     gate_back = (hidden_back * upper * sigma * (1.0 + gate * (1.0 - sigma))).astype(jnp.bfloat16)
     upper_back = (hidden_back * gate * sigma).astype(jnp.bfloat16)
     gate_total = jnp.einsum(
-        "srd,srf->df", normed_two, gate_back, preferred_element_type=jnp.float32
+        "srd,srf->df", normed_two_g, gate_back, preferred_element_type=jnp.float32
     )
     upper_total = jnp.einsum(
-        "srd,srf->df", normed_two, upper_back, preferred_element_type=jnp.float32
+        "srd,srf->df", normed_two_g, upper_back, preferred_element_type=jnp.float32
     )
     normed_two_back = jnp.einsum(
         "srf,df->srd", gate_back, gate_mat, preferred_element_type=jnp.float32
@@ -326,12 +344,13 @@
     normed_two_back = normed_two_back + jnp.einsum(
         "srf,df->srd", upper_back, upper_mat, preferred_element_type=jnp.float32
     )
+    normed_two_back = from_gathered(normed_two_back, w_rows)
     middle_norm_back, midnorm_total = norm_back(
         middle, inverse_two, midnorm_full.astype(jnp.float32), normed_two_back
     )
     middle_back = cot_wide + middle_norm_back
     middle_low = middle_back.astype(jnp.bfloat16)
-    out_total = jnp.einsum("srd,sre->de", mixed_low, middle_low, preferred_element_type=jnp.float32)
+    out_total = jnp.einsum("srd,sre->de", mixed_low_g, middle_low, preferred_element_type=jnp.float32)
 
     mlp_grads = jnp.concatenate(
         [
@@ -344,9 +363,12 @@
     ).astype(jnp.bfloat16)
     mlp_share = fsdp_reduce_scatter(mlp_grads)
 
-    blended_value_gradient = jnp.einsum(
-        "sre,de->srd", middle_low, out_mat, preferred_element_type=jnp.float32
-    ).astype(jnp.bfloat16)
+    blended_value_gradient = from_gathered(
+        jnp.einsum("sre,de->srd", middle_low, out_mat, preferred_element_type=jnp.float32).astype(
+            jnp.bfloat16
+        ),
+        w_rows,
+    )
     query_rot_back, kv_back = attention_backward(
         meta, query_flat, kv_all, blended_value_gradient.reshape(rows, width), head_dim, score_scale
     )
@@ -369,11 +391,11 @@
     )
     value_back = (0.5 * value_mix_back).astype(jnp.bfloat16)
     query_total = jnp.einsum(
-        "srd,sre->de", normed_low, query_back, preferred_element_type=jnp.float32
-    )
-    key_total = jnp.einsum("srd,sre->de", normed_low, key_back, preferred_element_type=jnp.float32)
+        "srd,sre->de", normed_low_g, query_back, preferred_element_type=jnp.float32
+    )
+    key_total = jnp.einsum("srd,sre->de", normed_low_g, key_back, preferred_element_type=jnp.float32)
     value_total = jnp.einsum(
-        "srd,sre->de", normed_low, value_back, preferred_element_type=jnp.float32
+        "srd,sre->de", normed_low_g, value_back, preferred_element_type=jnp.float32
     )
     normed_back = jnp.einsum(
         "sre,de->srd", query_back, query_mat, preferred_element_type=jnp.float32
@@ -384,6 +406,7 @@
     normed_back = normed_back + jnp.einsum(
         "sre,de->srd", value_back, value_mat, preferred_element_type=jnp.float32
     )
+    normed_back = from_gathered(normed_back, w_rows)
     tokens_norm_back, prenorm_total = norm_back(
         tokens_wide, inverse, prenorm_full.astype(jnp.float32), normed_back
     )
@@ -395,8 +418,8 @@
             key_total.reshape(n_fsdp, w_rows, width),
             value_total.reshape(n_fsdp, w_rows, width),
             gain_block(
-                prenorm_total.reshape(n_fsdp, g_len),
-                midnorm_total.reshape(n_fsdp, g_len),
+                to_gathered(prenorm_total, g_len).reshape(n_fsdp, g_len),
+                to_gathered(midnorm_total, g_len).reshape(n_fsdp, g_len),
                 width,
                 leading=(n_fsdp,),
             ),

time: 731 us -> 732 us (level)
  waiting for transfers between devices: 334 us -> 318 us
    transpose x3 -> x10, local copies, waits for them, and re-layouts: 33 us -> 9.98 us  [the longest x4 5.19 us: from_gathered(): jnp.swapaxes(rows.reshape(lead + (-1, 2, block)), -3, -2)]
    ppermute x6, waiting for transfers between devices: 64.4 us -> 50.1 us  [ctx_allreduce(): other = lax.ppermute(total, CTX, [(j, j ^ step) for j in range(n_ctx)])]
    transpose x1 -> x0, other arithmetic: 14.3 us -> none  [fsdp_reduce_scatter(): by_yc = jnp.swapaxes(grads.reshape((2, n_yc) + grads.shape[1:]), 0, 1)]
    concatenate x0 -> x1, other arithmetic: none -> 14.3 us  [body(): jnp.concatenate([gate_total.reshape(n_fsdp, w_rows, ff), upper_total.resh...]
    reshape x3 -> x7, local copies, waits for them, and re-layouts: 3.76 us -> 15.8 us  [the longest x2 8.08 us: attn_part(): attn_all[:, i * w_rows:(i + 1) * w_rows, :].reshape(n_fsdp * w_rows, width)]
  transfers between devices with their start and end apart: 16 -> 16, of which waited for: 13 -> 12; matrix products, arithmetic and copies ran while one was open for 13% -> 15% of each run, Pallas kernels for 9% -> 9%
where the time goes in v8:
time: 732 us; the launch traced here: 722 us
  waiting for transfers between devices  318 us (43%)
  local copies, waits for them, and re-layouts  115 us (16%)
  starting transfers between devices  93.8 us (13%)
  Pallas kernels  67.7 us (9%)
  matrix products  61.2 us (8%)
  other arithmetic  51.7 us (7%)
  between operations  15 us (2%)
    all_to_all x1, waiting for transfers between devices, body(): lax.all_to_all(kv_back.reshape(n_ctx, rows, 2 * width), CTX, 0, 0, tiled=...  93.3 us
    all_to_all x1, waiting for transfers between devices, body(): lax.all_to_all(jnp.broadcast_to(kv_own[None], (n_ctx, rows, 2 * width)),...  91.9 us
    ppermute x6, waiting for transfers between devices, ctx_allreduce(): other = lax.ppermute(total, CTX, [(j, j ^ step) for j in range(n_ctx)])  50.1 us
    pallas_call x1, Pallas kernels, attention_backward(): pl.pallas_call(functools.partial(attn_bwd_kernel, head_dim, scale), out_s...  43.3 us
    ppermute x6, starting transfers between devices, ctx_allreduce(): other = lax.ppermute(total, CTX, [(j, j ^ step) for j in range(n_ctx)])  39.9 us
    ppermute x2, waiting for transfers between devices, fsdp_gather(): other = lax.ppermute(pack, ('zh', 'zl'), Z_CROSS)  35.9 us
    all_to_all x1, starting transfers between devices, body(): lax.all_to_all(kv_back.reshape(n_ctx, rows, 2 * width), CTX, 0, 0, tiled=...  35.6 us
    pallas_call x1, Pallas kernels, attention_forward(): pl.pallas_call(functools.partial(attn_fwd_kernel, head_dim, scale), out_s...  24.4 us
  transfers between devices with their start and end apart: 16, of which 12 were waited for; matrix products, arithmetic and copies ran while one was open for 15% of the time, Pallas kernels for 9%

profile of v8, /device:TPU:0, one launch (start us, length us, event | category | flops | bytes accessed | tf_op | source)
XLA Modules:
  0.0 722.4 jit_solution(15852297280089125888)
XLA Ops:
  11.7 4.2 collective-permute-start
  15.9 12.6 %collective-permute-done = bf16[272,1024]{1,0:T(8,128)(2,1)S(1)} collective-permute-done((bf16[272,1024]{1,0:T(8,128)(2,1)S(1)}, bf16[272,1024]{1,0:T(8,128)(2,1)S(1)}, u32[]{:S(2)}, u32[]{:S(2)}) %collective-permute-start) | collective-permute-done | bytes 557088 | tf_op jit(solution)/shard_map/ppermute | solution.py:194
  30.4 3.1 collective-permute-start.1
  33.4 23.3 %collective-permute-done.1 = bf16[64,8448]{1,0:T(8,128)(2,1)S(1)} collective-permute-done((bf16[64,8448]{1,0:T(8,128)(2,1)S(1)}, bf16[64,8448]{1,0:T(8,128)(2,1)S(1)}, u32[]{:S(2)}, u32[]{:S(2)}) %collective-permute-start.1) | collective-permute-done | bytes 1081376 | tf_op jit(solution)/shard_map/ppermute | solution.py:194
  58.9 24.2 %all-gather.5.cloned.1.call-done = bf16[16,272,1024]{2,1,0:T(8,128)(2,1)} async-done(((bf16[2,272,1024]{2,1,0:T(8,128)(2,1)}), bf16[16,272,1024]{2,1,0:T(8,128)(2,1)}) %all-gather.5.cloned.1.call-update) | async-done | bytes 8912912 | tf_op jit(solution)/shard_map/all_gather | solution.py:195
  84.6 6.0 fusion.41
  90.5 3.9 copy.163
  94.5 4.1 copy.161
  98.6 2.8 convolution_bitcast_fusion.3
  104.4 2.5 fusion.9
  107.0 4.4 broadcast_in_dim.72
  111.4 5.3 all-to-all-start
  119.8 91.9 %all-to-all-done = bf16[8,256,2048]{2,1,0:T(8,128)(2,1)} async-done(((bf16[8,256,2048]{2,1,0:T(8,128)(2,1)}), bf16[8,256,2048]{2,1,0:T(8,128)(2,1)}, u32[]{:S(2)}, u32[]{:S(2)}) %all-to-all-start) | async-done | bytes 8388640 | tf_op jit(solution)/shard_map/all_to_all | solution.py:305
  211.7 24.4 %shard_map.229 = bf16[256,1024]{1,0:T(8,128)(2,1)S(1)} custom-call(s32[2]{0:T(128)S(1)} %pad_add_fusion.meta_ref, bf16[256,1024]{1,0:T(8,128)(2,1)S(1)} %copy.166.q_ref, bf16[2048,2048]{1,0:T(8,128)(2,1)} %bitcast.24.k_ref.v_ref, bf16[2048,2048]{1,0:T(8,128)(2,1)} %bitcast.24.k_ref.v_ref), custom_call_target="tpu_custom_call" | custom-call | flops 2147483648 | bytes 9437184 | tf_op jit(solution)/shard_map/pallas_call | solution.py:80
  238.1 2.1 multiply_reduce_fusion.2
  242.1 2.0 copy.170
  245.3 11.3 %fusion.40 = (bf16[16,64,2816]{2,1,0:T(8,128)(2,1)}, bf16[16,64,2816]{2,1,0:T(8,128)(2,1)}, bf16[16,64,2816]{2,1,0:T(8,128)(2,1)}) fusion(bf16[16,64,8448]{2,1,0:T(8,128)(2,1)} %all-gather.7.cloned.1.call-done), kind=kLoop, calls=%fused_computation.130 | loop fusion | bytes 34603008 | tf_op jit(solution)/shard_map/slice | solution.py:285
  256.6 11.7 %dot_general.113 = bf16[8,2,176,1024]{3,2,1,0:T(8,128)(2,1)} reshape(bf16[16,64,2816]{2,1,0:T(8,128)(2,1)} %get-tuple-element.72) | data formatting | bytes 11534336 | tf_op jit(solution)/shard_map/sre,fe->srf/dot_general | solution.py:330
  268.3 4.6 convolution_bitcast_fusion
  272.9 1.8 copy.174
  274.7 3.4 copy.175
  278.1 4.5 fusion.45
  282.6 7.0 multiply_convert_fusion
  291.3 4.2 convolution_convert_fusion.2
  295.5 4.1 convolution_convert_fusion.1
  299.6 2.7 convolution_add_fusion.2
  302.2 2.5 copy.172
  304.8 2.6 copy.173
  307.4 2.6 copy.177
  309.9 2.3 copy.178
  312.2 2.6 copy.179
  314.8 2.0 multiply_reduce_fusion
  318.4 4.3 convolution_convert_fusion
  322.7 11.8 %concatenate.69 = bf16[8,128,2816]{2,1,0:T(8,128)(2,1)} reshape(bf16[2816,1024]{1,0:T(8,128)(2,1)} %convolution_convert_fusion) | data formatting | bytes 11534336 | tf_op jit(solution)/shard_map/concatenate | solution.py:355
  334.5 1.9 convolution_convert_fusion.3
  336.4 14.3 %pad_maximum_fusion = bf16[8,128,9472]{2,1,0:T(8,128)(2,1)} fusion(bf16[8,128,1024]{2,1,0:T(8,128)(2,1)S(1)} %convolution_convert_fusion.3, bf16[8,128,2816]{2,1,0:T(8,128)(2,1)} %concatenate.69, bf16[8,128,2816]{2,1,0:T(8,128)(2,1)} %convolution_convert_fusion.1, bf16[8,128,2816]{2,1,0:T(8,128)(2,1)} %convolution_convert_fusion.2), kind=kLoop, calls=%fused_computation | loop fusion | flops 77594624 | bytes 38797312 | tf_op jit(solution)/shard_map/concatenate | solution.py:355
  350.7 2.0 convolution_convert_fusion.7
  353.2 43.3 %shard_map.230 = (f32[256,1024]{1,0:T(8,128)S(1)}, bf16[2048,2048]{1,0:T(8,128)(2,1)}) custom-call(s32[2]{0:T(128)S(1)} %pad_add_fusion.meta_ref, bf16[256,1024]{1,0:T(8,128)(2,1)S(1)} %copy.166.q_ref, bf16[2048,2048]{1,0:T(8,128)(2,1)} %bitcast.24.k_ref.v_ref, bf16[2048,2048]{1,0:T(8,128)(2,1)} %bitcast.24.k_ref.v_ref, bf16[256,1024]{1,0:T(8,128)(2,1)S(1)} %copy.183.do_ref), custom_call_target="tpu_custom_call" | custom-call | flops 5368709120 | bytes 19398656 | tf_op jit(solution)/shard_map/pallas_call | solution.py:108
  396.5 35.6 %all-to-all-start.1 = ((bf16[8,256,2048]{2,1,0:T(8,128)(2,1)}), bf16[8,256,2048]{2,1,0:T(8,128)(2,1)}, u32[]{:S(2)}, u32[]{:S(2)}) async-start(bf16[8,256,2048]{2,1,0:T(8,128)(2,1)} %bitcast.228), calls=%async_computation.1 | async-start | bytes 16777216 | tf_op jit(solution)/shard_map/all_to_all | solution.py:377
  432.6 93.3 %all-to-all-done.1 = bf16[8,256,2048]{2,1,0:T(8,128)(2,1)} async-done(((bf16[8,256,2048]{2,1,0:T(8,128)(2,1)}), bf16[8,256,2048]{2,1,0:T(8,128)(2,1)}, u32[]{:S(2)}, u32[]{:S(2)}) %all-to-all-start.1) | async-done | bytes 8388640 | tf_op jit(solution)/shard_map/all_to_all | solution.py:377
  525.9 5.3 convert_reduce_fusion
  531.2 2.1 copy.185
  533.3 2.7 slice_multiply_fusion
  546.8 3.1 convolution_convert_fusion.6
  549.9 2.1 convolution_convert_fusion.5
  552.0 2.1 convolution_convert_fusion.4
  555.6 2.6 collective-permute-start.2
  558.3 5.5 fusion.1
  563.8 21.5 %collective-permute-done.2 = bf16[64,9472]{1,0:T(8,128)(2,1)S(1)} collective-permute-done((bf16[64,9472]{1,0:T(8,128)(2,1)S(1)}, bf16[64,9472]{1,0:T(8,128)(2,1)S(1)}, u32[]{:S(2)}, u32[]{:S(2)}) %collective-permute-start.2) | collective-permute-done | bytes 1212448 | tf_op jit(solution)/shard_map/ppermute | solution.py:209
  586.7 28.0 %collective-permute-start.7 = (bf16[64,9472]{1,0:T(8,128)(2,1)}, bf16[64,9472]{1,0:T(8,128)(2,1)S(1)}, u32[]{:S(2)}, u32[]{:S(2)}) collective-permute-start(bf16[64,9472]{1,0:T(8,128)(2,1)} %fusion.2), channel_id=1, source_target_pairs={{0,1},{1,0},{2,3},{3,2},{4,5},{5,4},{6,7},{7,6},{8,9},{9,8},{10,11... | collective-permute-start | bytes 3637256 | tf_op jit(solution)/shard_map/ppermute | solution.py:217
  614.6 24.5 %collective-permute-done.7 = bf16[64,9472]{1,0:T(8,128)(2,1)S(1)} collective-permute-done((bf16[64,9472]{1,0:T(8,128)(2,1)}, bf16[64,9472]{1,0:T(8,128)(2,1)S(1)}, u32[]{:S(2)}, u32[]{:S(2)}) %collective-permute-start.7) | collective-permute-done | bytes 1212448 | tf_op jit(solution)/shard_map/ppermute | solution.py:217
  639.2 2.6 add_convert_fusion.2
  641.8 4.5 collective-permute-start.8
  646.3 11.8 %reshape_reshape.19 = bf16[2816,1024]{1,0:T(8,128)(2,1)} reshape(bf16[16,64,2816]{2,1,0:T(8,128)(2,1)} %get-tuple-element.72) | data formatting | bytes 11534336 | tf_op jit(solution)/shard_map/reshape;reshape | solution.py:285
  658.1 12.3 %collective-permute-done.8 = bf16[64,9472]{1,0:T(8,128)(2,1)} collective-permute-done((bf16[64,9472]{1,0:T(8,128)(2,1)}, bf16[64,9472]{1,0:T(8,128)(2,1)}, u32[]{:S(2)}, u32[]{:S(2)}) %collective-permute-start.8) | collective-permute-done | bytes 1212448 | tf_op jit(solution)/shard_map/ppermute | solution.py:217
  670.3 3.0 add_convert_fusion.1
  674.3 2.5 collective-permute-start.3
  676.8 5.6 fusion.10
  685.1 2.5 copy.197
  689.0 4.7 collective-permute-done.4
  693.8 5.5 collective-permute-start.5
  699.3 1.9 fusion.13
  701.9 3.5 collective-permute-done.5
  708.6 5.1 collective-permute-done.6
  (165 shorter events, 49.4 us)
Async XLA Ops:
  7.2 75.9 %all-gather.5.cloned.1.call-start = ((), (), s32[]{:S(2)}) async-start(), calls=%async_computation.6 | async-start | bytes 10027008 | tf_op jit(solution)/shard_map/all_gather | solution.py:195
  11.7 16.8 %collective-permute-start = (bf16[272,1024]{1,0:T(8,128)(2,1)S(1)}, bf16[272,1024]{1,0:T(8,128)(2,1)S(1)}, u32[]{:S(2)}, u32[]{:S(2)}) collective-permute-start(bf16[272,1024]{1,0:T(8,128)(2,1)S(1)} %pad_dynamic-update-slice_fusion), channel_id=1, source_target_pairs={{0,68},{68,0},{4,64},{64,4},{1,69},{69,1},{5,65},{65,5},{2,70},{70... | collective-permute-start | bytes 1671176 | tf_op jit(solution)/shard_map/ppermute | solution.py:194
  15.9 13.9 %copy-start.24 = (bf16[176,1024]{1,0:T(8,128)(2,1)S(1)}, bf16[176,1024]{1,0:T(8,128)(2,1)}, u32[]{:S(2)}) copy-start(bf16[176,1024]{1,0:T(8,128)(2,1)} %param.22) | copy-start | bytes 1081348
  28.6 1.6 copy-start.25
  28.6 1.7 copy-start.26
  29.7 215.5 %all-gather.7.cloned.1.call-start = ((), (), s32[]{:S(2)}) async-start(), calls=%async_computation.7 | async-start | bytes 19464192 | tf_op jit(solution)/shard_map/all_gather | solution.py:195
  30.4 26.3 %collective-permute-start.1 = (bf16[64,8448]{1,0:T(8,128)(2,1)S(1)}, bf16[64,8448]{1,0:T(8,128)(2,1)S(1)}, u32[]{:S(2)}, u32[]{:S(2)}) collective-permute-start(bf16[64,8448]{1,0:T(8,128)(2,1)S(1)} %constant_dynamic-update-slice_fusion.4), channel_id=1, source_target_pairs={{0,68},{68,0},{4,64},{64,4},{1,69},{69,1},{5,65},{65,5},{2,70},{70... | collective-permute-start | bytes 3244040 | tf_op jit(solution)/shard_map/ppermute | solution.py:194
  56.8 1.6 copy-start.7
  84.6 19.9 %copy-start.9 = (bf16[1,256,8,2,64]{1,4,3,2,0:T(8,128)(2,1)}, bf16[1,256,8,2,64]{1,4,3,2,0:T(8,128)(2,1)S(1)}, u32[]{:S(2)}) copy-start(bf16[1,256,8,2,64]{1,4,3,2,0:T(8,128)(2,1)S(1)} %copy.160) | copy-start | bytes 1572868
  98.6 2.8 copy-start.19
  104.4 2.5 copy-start.22
  111.4 5.9 copy-start.27
  111.4 5.9 copy-start.28
  111.4 8.2 %copy-start.21 = (bf16[1,256,16,64]{1,3,2,0:T(8,128)(2,1)S(1)}, bf16[1,256,16,64]{1,3,2,0:T(8,128)(2,1)}, u32[]{:S(2)}) copy-start(bf16[1,256,16,64]{1,3,2,0:T(8,128)(2,1)} %get-tuple-element.118) | copy-start | bytes 1572868
  111.4 100.2 %all-to-all-start = ((bf16[8,256,2048]{2,1,0:T(8,128)(2,1)}), bf16[8,256,2048]{2,1,0:T(8,128)(2,1)}, u32[]{:S(2)}, u32[]{:S(2)}) async-start(bf16[8,256,2048]{2,1,0:T(8,128)(2,1)} %broadcast_in_dim.72), calls=%async_computation | async-start | bytes 16777216 | tf_op jit(solution)/shard_map/all_to_all | solution.py:305
  116.7 437.4 %reduce-scatter.3.cloned.1.call-start = ((), (), s32[]{:S(2)}) async-start(), calls=%async_computation.4 | async-start | bytes 21823488 | tf_op jit(solution)/shard_map/reduce_scatter | solution.py:203
  238.1 4.0 copy-start.14
  240.2 1.0 copy-start.3
  278.1 4.5 copy-start.17
  278.1 11.5 %slice-start.2 = ((s8[5767168]{0:T(1024)(128)(4,1)}), s8[4194304]{0:T(1024)(128)(4,1)S(1)}, s32[]{:S(2)}) async-start(s8[5767168]{0:T(1024)(128)(4,1)} %bitcast.232), calls=%async_computation.10 | async-start | bytes 8388608
  282.6 7.0 slice-start.3
  291.3 8.3 %slice-start = ((s8[5767168]{0:T(1024)(128)(4,1)}), s8[4194304]{0:T(1024)(128)(4,1)S(1)}, s32[]{:S(2)}) async-start(s8[5767168]{0:T(1024)(128)(4,1)} %bitcast.203), calls=%async_computation.8 | async-start | bytes 8388608
  295.5 4.1 slice-start.1
  312.2 4.6 copy-start.20
  314.8 2.0 copy-start.4
  314.8 2.2 copy-start.11
  314.8 3.6 copy-start.12
  322.7 11.8 %copy-start.15 = (bf16[1,256,8,2,64]{1,4,3,2,0:T(8,128)(2,1)S(1)}, bf16[1,256,8,2,64]{1,4,3,2,0:T(8,128)(2,1)}, u32[]{:S(2)}) copy-start(bf16[1,256,8,2,64]{1,4,3,2,0:T(8,128)(2,1)} %copy-done.14) | copy-start | bytes 1572868
  396.5 129.3 %all-to-all-start.1 = ((bf16[8,256,2048]{2,1,0:T(8,128)(2,1)}), bf16[8,256,2048]{2,1,0:T(8,128)(2,1)}, u32[]{:S(2)}, u32[]{:S(2)}) async-start(bf16[8,256,2048]{2,1,0:T(8,128)(2,1)} %bitcast.228), calls=%async_computation.1 | async-start | bytes 16777216 | tf_op jit(solution)/shard_map/all_to_all | solution.py:377
  432.1 241.2 %reduce-scatter.5.cloned.1.call-start = ((), (), s32[]{:S(2)}) async-start(), calls=%async_computation.5 | async-start | bytes 7667712 | tf_op jit(solution)/shard_map/reduce_scatter | solution.py:203
  536.0 1.8 copy-start.2
  536.4 2.2 copy-start.1
  536.5 2.9 copy-start.16
  538.6 1.6 copy-start
  543.5 2.7 copy-start.8
  544.6 2.2 copy-start.10
  554.1 4.2 copy-start.13
  555.6 29.7 %copy-start.18 = (bf16[1,128,9472]{2,1,0:T(8,128)(2,1)S(1)}, bf16[1,128,9472]{2,1,0:T(8,128)(2,1)}, u32[]{:S(2)}) copy-start(bf16[1,128,9472]{2,1,0:T(8,128)(2,1)} %reduce-scatter.3.cloned.1.call-done) | copy-start | bytes 7274500
  555.6 29.7 %collective-permute-start.2 = (bf16[64,9472]{1,0:T(8,128)(2,1)S(1)}, bf16[64,9472]{1,0:T(8,128)(2,1)S(1)}, u32[]{:S(2)}, u32[]{:S(2)}) collective-permute-start(bf16[64,9472]{1,0:T(8,128)(2,1)S(1)} %dynamic-slice_bitcast_fusion), channel_id=1, source_target_pairs={{0,68},{68,0},{4,64},{64,4},{1,69},{69,1},{5,65},{65,5},{2,70},{70... | collective-permute-start | bytes 3637256 | tf_op jit(solution)/shard_map/ppermute | solution.py:209
  586.7 52.5 %collective-permute-start.7 = (bf16[64,9472]{1,0:T(8,128)(2,1)}, bf16[64,9472]{1,0:T(8,128)(2,1)S(1)}, u32[]{:S(2)}, u32[]{:S(2)}) collective-permute-start(bf16[64,9472]{1,0:T(8,128)(2,1)} %fusion.2), channel_id=1, source_target_pairs={{0,1},{1,0},{2,3},{3,2},{4,5},{5,4},{6,7},{7,6},{8,9},{9,8},{10,11... | collective-permute-start | bytes 3637256 | tf_op jit(solution)/shard_map/ppermute | solution.py:217
  641.8 28.6 %collective-permute-start.8 = (bf16[64,9472]{1,0:T(8,128)(2,1)}, bf16[64,9472]{1,0:T(8,128)(2,1)}, u32[]{:S(2)}, u32[]{:S(2)}) collective-permute-start(bf16[64,9472]{1,0:T(8,128)(2,1)} %add_convert_fusion.2), channel_id=1, source_target_pairs={{0,2},{1,3},{2,0},{3,1},{4,6},{5,7},{6,4},{7,5},{8,10},{9,11},{10,... | collective-permute-start | bytes 3637256 | tf_op jit(solution)/shard_map/ppermute | solution.py:217
  658.1 18.7 %copy-start.5 = (f32[1,256,1024]{2,1,0:T(8,128)S(1)}, f32[1,256,1024]{2,1,0:T(8,128)}, u32[]{:S(2)}) copy-start(f32[1,256,1024]{2,1,0:T(8,128)} %copy-done.3) | copy-start | bytes 3145732
  673.3 26.0 %collective-permute-start.9 = (bf16[64,9472]{1,0:T(8,128)(2,1)}, bf16[64,9472]{1,0:T(8,128)(2,1)}, u32[]{:S(2)}, u32[]{:S(2)}) collective-permute-start(bf16[64,9472]{1,0:T(8,128)(2,1)} %add_convert_fusion.1), channel_id=1, source_target_pairs={{0,4},{1,5},{2,6},{3,7},{4,0},{5,1},{6,2},{7,3},{8,12},{9,13},{10,... | collective-permute-start | bytes 3637256 | tf_op jit(solution)/shard_map/ppermute | solution.py:217
  674.3 9.4 %copy-start.23 = (bf16[1,416,1024]{2,1,0:T(8,128)(2,1)S(1)}, bf16[1,416,1024]{2,1,0:T(8,128)(2,1)}, u32[]{:S(2)}) copy-start(bf16[1,416,1024]{2,1,0:T(8,128)(2,1)} %reduce-scatter.5.cloned.1.call-done) | copy-start | bytes 2555908
  674.3 9.4 %collective-permute-start.3 = (bf16[208,1024]{1,0:T(8,128)(2,1)S(1)}, bf16[208,1024]{1,0:T(8,128)(2,1)S(1)}, u32[]{:S(2)}, u32[]{:S(2)}) collective-permute-start(bf16[208,1024]{1,0:T(8,128)(2,1)S(1)} %dynamic-slice_bitcast_fusion.1), channel_id=1, source_target_pairs={{0,68},{68,0},{4,64},{64,4},{1,69},{69,1},{5,65},{65,5},{2,70},{70... | collective-permute-start | bytes 1277960 | tf_op jit(solution)/shard_map/ppermute | solution.py:209
  682.4 5.3 copy-start.6
  683.9 9.8 %collective-permute-start.4 = (bf16[208,1024]{1,0:T(8,128)(2,1)S(1)}, bf16[208,1024]{1,0:T(8,128)(2,1)S(1)}, u32[]{:S(2)}, u32[]{:S(2)}) collective-permute-start(bf16[208,1024]{1,0:T(8,128)(2,1)S(1)} %fusion.24), channel_id=1, source_target_pairs={{0,1},{1,0},{2,3},{3,2},{4,5},{5,4},{6,7},{7,6},{8,9},{9,8},{10,11... | collective-permute-start | bytes 1277960 | tf_op jit(solution)/shard_map/ppermute | solution.py:217
  693.8 11.6 %collective-permute-start.5 = (bf16[208,1024]{1,0:T(8,128)(2,1)S(1)}, bf16[208,1024]{1,0:T(8,128)(2,1)S(1)}, u32[]{:S(2)}, u32[]{:S(2)}) collective-permute-start(bf16[208,1024]{1,0:T(8,128)(2,1)S(1)} %add_convert_fusion.5), channel_id=1, source_target_pairs={{0,2},{1,3},{2,0},{3,1},{4,6},{5,7},{6,4},{7,5},{8,10},{9,11},{10,... | collective-permute-start | bytes 1277960 | tf_op jit(solution)/shard_map/ppermute | solution.py:217
  705.6 8.2 %collective-permute-start.6 = (bf16[208,1024]{1,0:T(8,128)(2,1)S(1)}, bf16[208,1024]{1,0:T(8,128)(2,1)S(1)}, u32[]{:S(2)}, u32[]{:S(2)}) collective-permute-start(bf16[208,1024]{1,0:T(8,128)(2,1)S(1)} %add_convert_fusion.4), channel_id=1, source_target_pairs={{0,4},{1,5},{2,6},{3,7},{4,0},{5,1},{6,2},{7,3},{8,12},{9,13},{10,... | collective-permute-start | bytes 1277960 | tf_op jit(solution)/shard_map/ppermute | solution.py:217
Sparse Core Ops, SparseCore 0:
  29.9 53.2 all-gather.4
  84.8 87.3 all-gather.6
  350.8 135.3 reduce-scatter.2
  586.8 73.5 reduce-scatter.4

commit v9 on v8

--- a/solution.py
+++ b/solution.py
@@ -197,12 +197,20 @@
 
 
 def fsdp_reduce_scatter(grads):
+    return z_combine(yc_reduce_scatter(grads))
+
+
+def yc_reduce_scatter(grads):
     n_yc = grads.shape[0] // 2
     by_yc = grads
     block = grads.shape[1:]
     halves = lax.psum_scatter(
         by_yc.reshape((n_yc, 2 * block[0]) + block[1:]), ("y", "core"), scatter_dimension=0, tiled=False
     ).reshape((2,) + block)
+    return halves
+
+
+def z_combine(halves):
     zh = lax.axis_index("zh")
     mine = lax.dynamic_index_in_dim(halves, zh, axis=0, keepdims=False)
     theirs = lax.dynamic_index_in_dim(halves, 1 - zh, axis=0, keepdims=False)
@@ -352,27 +360,34 @@
     middle_low = middle_back.astype(jnp.bfloat16)
     out_total = jnp.einsum("srd,sre->de", mixed_low_g, middle_low, preferred_element_type=jnp.float32)
 
+    blended_value_gradient = from_gathered(
+        jnp.einsum("sre,de->srd", middle_low, out_mat, preferred_element_type=jnp.float32).astype(
+            jnp.bfloat16
+        ),
+        w_rows,
+    )
+    query_rot_back, kv_back = attention_backward(
+        meta, query_flat, kv_all, blended_value_gradient.reshape(rows, width), head_dim, score_scale
+    )
+    query_rot_back = query_rot_back.reshape(slots, rows, head_count, head_dim)
+    query_back = (
+        rotate(query_rot_back, cos_rows, -sin_rows).reshape(slots, rows, width).astype(jnp.bfloat16)
+    )
+    query_total = jnp.einsum(
+        "srd,sre->de", normed_low_g, query_back, preferred_element_type=jnp.float32
+    )
     mlp_grads = jnp.concatenate(
         [
             gate_total.reshape(n_fsdp, w_rows, ff),
             upper_total.reshape(n_fsdp, w_rows, ff),
             down_total.reshape(n_fsdp, d_rows, width).reshape(n_fsdp, w_rows, ff),
             out_total.reshape(n_fsdp, w_rows, width),
+            query_total.reshape(n_fsdp, w_rows, width),
         ],
         axis=2,
     ).astype(jnp.bfloat16)
-    mlp_share = fsdp_reduce_scatter(mlp_grads)
-
-    blended_value_gradient = from_gathered(
-        jnp.einsum("sre,de->srd", middle_low, out_mat, preferred_element_type=jnp.float32).astype(
-            jnp.bfloat16
-        ),
-        w_rows,
-    )
-    query_rot_back, kv_back = attention_backward(
-        meta, query_flat, kv_all, blended_value_gradient.reshape(rows, width), head_dim, score_scale
-    )
-    query_rot_back = query_rot_back.reshape(slots, rows, head_count, head_dim)
+    mlp_halves = yc_reduce_scatter(mlp_grads)
+
     key_value = jnp.sum(
         lax.all_to_all(kv_back.reshape(n_ctx, rows, 2 * width), CTX, 0, 0, tiled=False).astype(
             jnp.float32
@@ -383,16 +398,10 @@
     key_rot_back = key_value[:, :, 0, :].reshape(slots, rows, head_count, head_dim)
     value_mix_back = key_value[:, :, 1, :].reshape(slots, rows, width)
     first_grad = 0.5 * value_mix_back
-    query_back = (
-        rotate(query_rot_back, cos_rows, -sin_rows).reshape(slots, rows, width).astype(jnp.bfloat16)
-    )
     key_back = (
         rotate(key_rot_back, cos_rows, -sin_rows).reshape(slots, rows, width).astype(jnp.bfloat16)
     )
     value_back = (0.5 * value_mix_back).astype(jnp.bfloat16)
-    query_total = jnp.einsum(
-        "srd,sre->de", normed_low_g, query_back, preferred_element_type=jnp.float32
-    )
     key_total = jnp.einsum("srd,sre->de", normed_low_g, key_back, preferred_element_type=jnp.float32)
     value_total = jnp.einsum(
         "srd,sre->de", normed_low_g, value_back, preferred_element_type=jnp.float32
@@ -414,7 +423,6 @@
 
     attn_grads = jnp.concatenate(
         [
-            query_total.reshape(n_fsdp, w_rows, width),
             key_total.reshape(n_fsdp, w_rows, width),
             value_total.reshape(n_fsdp, w_rows, width),
             gain_block(
@@ -426,21 +434,22 @@
         ],
         axis=1,
     ).astype(jnp.bfloat16)
-    attn_grads, mlp_share = lax.optimization_barrier((attn_grads, mlp_share))
-    mlp_share = ctx_allreduce(mlp_share, n_ctx)
+    attn_grads, mlp_halves = lax.optimization_barrier((attn_grads, mlp_halves))
+    mlp_share = ctx_allreduce(z_combine(mlp_halves), n_ctx)
     attn_share = fsdp_reduce_scatter(attn_grads)
     attn_share = ctx_allreduce(attn_share, n_ctx)
 
     def attn_grad(i):
         return attn_share[i * w_rows:(i + 1) * w_rows]
 
-    query_grad, key_grad, value_grad = (attn_grad(i) for i in range(3))
-    prenorm_grad = attn_share[3 * w_rows, 0:g_len]
-    midnorm_grad = attn_share[3 * w_rows, g_len:2 * g_len]
+    key_grad, value_grad = (attn_grad(i) for i in range(2))
+    prenorm_grad = attn_share[2 * w_rows, 0:g_len]
+    midnorm_grad = attn_share[2 * w_rows, g_len:2 * g_len]
     gate_grad = mlp_share[:, 0:ff]
     up_grad = mlp_share[:, ff:2 * ff]
     down_grad = mlp_share[:, 2 * ff:3 * ff].reshape(d_rows, width)
-    out_grad = mlp_share[:, 3 * ff:]
+    out_grad = mlp_share[:, 3 * ff:3 * ff + width]
+    query_grad = mlp_share[:, 3 * ff + width:]
     return (
         layer_out,
         tokens_grad,

time: 732 us -> 800 us (1.093)
  waiting for transfers between devices: 318 us -> 425 us
  starting transfers between devices: 93.8 us -> 66.1 us
  other arithmetic: 51.7 us -> 37.7 us
    reduce_scatter x2, waiting for transfers between devices: 0.01 us -> 130 us  [yc_reduce_scatter(): lax.psum_scatter(by_yc.reshape((n_yc, 2 * block[0]) + block[1:]), ('y', '...]
    all_to_all x1, waiting for transfers between devices: 93.3 us -> 58.2 us  [body(): lax.all_to_all(kv_back.reshape(n_ctx, rows, 2 * width), CTX, 0, 0, tiled=...]
    ppermute x6, starting transfers between devices: 39.9 us -> 11.2 us  [ctx_allreduce(): other = lax.ppermute(total, CTX, [(j, j ^ step) for j in range(n_ctx)])]
    concatenate x2 -> x1, other arithmetic: 19.8 us -> 2.4 us  [body(): jnp.concatenate([key_total.reshape(n_fsdp, w_rows, width), value_total.re...]
  transfers between devices with their start and end apart: 16 -> 16, of which waited for: 12 -> 12; matrix products, arithmetic and copies ran while one was open for 15% -> 16% of each run, Pallas kernels for 9% -> 3%
where the time goes in v9:
time: 800 us; the launch traced here: 788 us
  waiting for transfers between devices  425 us (53%)
  local copies, waits for them, and re-layouts  117 us (15%)
  Pallas kernels  67.5 us (8%)
  starting transfers between devices  66.1 us (8%)
  matrix products  59.4 us (7%)
  other arithmetic  37.7 us (5%)
  between operations  15.1 us (2%)
    reduce_scatter x2, waiting for transfers between devices, yc_reduce_scatter(): lax.psum_scatter(by_yc.reshape((n_yc, 2 * block[0]) + block[1:]), ('y', '...  130 us
    all_to_all x1, waiting for transfers between devices, body(): lax.all_to_all(jnp.broadcast_to(kv_own[None], (n_ctx, rows, 2 * width)),...  92.4 us
    all_to_all x1, waiting for transfers between devices, body(): lax.all_to_all(kv_back.reshape(n_ctx, rows, 2 * width), CTX, 0, 0, tiled=...  58.2 us
    ppermute x6, waiting for transfers between devices, ctx_allreduce(): other = lax.ppermute(total, CTX, [(j, j ^ step) for j in range(n_ctx)])  55.3 us
    pallas_call x1, Pallas kernels, attention_backward(): pl.pallas_call(functools.partial(attn_bwd_kernel, head_dim, scale), out_s...  43.2 us
    ppermute x2, waiting for transfers between devices, fsdp_gather(): other = lax.ppermute(pack, ('zh', 'zl'), Z_CROSS)  35.9 us
    all_to_all x1, starting transfers between devices, body(): lax.all_to_all(kv_back.reshape(n_ctx, rows, 2 * width), CTX, 0, 0, tiled=...  35.8 us
    ppermute x2, waiting for transfers between devices, z_combine(): got = lax.ppermute(theirs, ('zh', 'zl'), Z_CROSS)  29.2 us
  transfers between devices with their start and end apart: 16, of which 12 were waited for; matrix products, arithmetic and copies ran while one was open for 16% of the time, Pallas kernels for 3%

profile of v9, /device:TPU:0, one launch (start us, length us, event | category | flops | bytes accessed | tf_op | source)
XLA Modules:
  0.0 788.1 jit_solution(11765824643101043085)
XLA Ops:
  11.7 4.2 collective-permute-start
  15.9 12.6 %collective-permute-done = bf16[272,1024]{1,0:T(8,128)(2,1)S(1)} collective-permute-done((bf16[272,1024]{1,0:T(8,128)(2,1)S(1)}, bf16[272,1024]{1,0:T(8,128)(2,1)S(1)}, u32[]{:S(2)}, u32[]{:S(2)}) %collective-permute-start) | collective-permute-done | bytes 557088 | tf_op jit(solution)/shard_map/ppermute | solution.py:194
  30.4 3.1 collective-permute-start.1
  33.4 23.3 %collective-permute-done.1 = bf16[64,8448]{1,0:T(8,128)(2,1)S(1)} collective-permute-done((bf16[64,8448]{1,0:T(8,128)(2,1)S(1)}, bf16[64,8448]{1,0:T(8,128)(2,1)S(1)}, u32[]{:S(2)}, u32[]{:S(2)}) %collective-permute-start.1) | collective-permute-done | bytes 1081376 | tf_op jit(solution)/shard_map/ppermute | solution.py:194
  58.9 24.3 %all-gather.5.cloned.1.call-done = bf16[16,272,1024]{2,1,0:T(8,128)(2,1)} async-done(((bf16[2,272,1024]{2,1,0:T(8,128)(2,1)}), bf16[16,272,1024]{2,1,0:T(8,128)(2,1)}) %all-gather.5.cloned.1.call-update) | async-done | bytes 8912912 | tf_op jit(solution)/shard_map/all_gather | solution.py:195
  84.6 6.0 fusion.41
  90.5 3.9 copy.164
  94.5 4.1 copy.162
  98.6 2.8 convolution_bitcast_fusion.3
  104.4 2.5 fusion.10
  107.0 4.3 broadcast_in_dim.72
  111.3 5.8 all-to-all-start
  119.7 92.4 %all-to-all-done = bf16[8,256,2048]{2,1,0:T(8,128)(2,1)} async-done(((bf16[8,256,2048]{2,1,0:T(8,128)(2,1)}), bf16[8,256,2048]{2,1,0:T(8,128)(2,1)}, u32[]{:S(2)}, u32[]{:S(2)}) %all-to-all-start) | async-done | bytes 8388640 | tf_op jit(solution)/shard_map/all_to_all | solution.py:313
  212.1 24.3 %shard_map.229 = bf16[256,1024]{1,0:T(8,128)(2,1)S(1)} custom-call(s32[2]{0:T(128)S(1)} %pad_add_fusion.meta_ref, bf16[256,1024]{1,0:T(8,128)(2,1)S(1)} %copy.167.q_ref, bf16[2048,2048]{1,0:T(8,128)(2,1)} %bitcast.24.k_ref.v_ref, bf16[2048,2048]{1,0:T(8,128)(2,1)} %bitcast.24.k_ref.v_ref), custom_call_target="tpu_custom_call" | custom-call | flops 2147483648 | bytes 9437184 | tf_op jit(solution)/shard_map/pallas_call | solution.py:80
  238.5 2.1 multiply_reduce_fusion.2
  242.5 2.0 copy.171
  245.7 11.4 %fusion.40 = (bf16[16,64,2816]{2,1,0:T(8,128)(2,1)}, bf16[16,64,2816]{2,1,0:T(8,128)(2,1)}, bf16[16,64,2816]{2,1,0:T(8,128)(2,1)}) fusion(bf16[16,64,8448]{2,1,0:T(8,128)(2,1)} %all-gather.7.cloned.1.call-done), kind=kLoop, calls=%fused_computation.130 | loop fusion | bytes 34603008 | tf_op jit(solution)/shard_map/slice | solution.py:293
  257.1 11.7 %dot_general.115 = bf16[8,2,176,1024]{3,2,1,0:T(8,128)(2,1)} reshape(bf16[16,64,2816]{2,1,0:T(8,128)(2,1)} %get-tuple-element.72) | data formatting | bytes 11534336 | tf_op jit(solution)/shard_map/sre,fe->srf/dot_general | solution.py:338
  268.7 4.6 convolution_bitcast_fusion
  273.4 1.8 copy.175
  275.2 3.4 copy.176
  278.6 4.5 fusion.46
  283.2 7.3 multiply_convert_fusion
  290.6 1.7 fusion.47
  292.3 2.7 convolution_add_fusion.2
  295.0 2.6 copy.178
  297.5 2.3 copy.179
  299.8 2.6 copy.180
  302.4 2.0 multiply_reduce_fusion
  307.3 43.2 %shard_map.230 = (f32[256,1024]{1,0:T(8,128)S(1)}, bf16[2048,2048]{1,0:T(8,128)(2,1)}) custom-call(s32[2]{0:T(128)S(1)} %pad_add_fusion.meta_ref, bf16[256,1024]{1,0:T(8,128)(2,1)S(1)} %copy.167.q_ref, bf16[2048,2048]{1,0:T(8,128)(2,1)} %bitcast.24.k_ref.v_ref, bf16[2048,2048]{1,0:T(8,128)(2,1)} %bitcast.24.k_ref.v_ref, bf16[256,1024]{1,0:T(8,128)(2,1)S(1)} %copy.184.do_ref), custom_call_target="tpu_custom_call" | custom-call | flops 5368709120 | bytes 19398656 | tf_op jit(solution)/shard_map/pallas_call | solution.py:108
  350.5 35.8 %all-to-all-start.1 = ((bf16[8,256,2048]{2,1,0:T(8,128)(2,1)}), bf16[8,256,2048]{2,1,0:T(8,128)(2,1)}, u32[]{:S(2)}, u32[]{:S(2)}) async-start(bf16[8,256,2048]{2,1,0:T(8,128)(2,1)} %bitcast.228), calls=%async_computation.1 | async-start | bytes 16777216 | tf_op jit(solution)/shard_map/all_to_all | solution.py:392
  386.3 1.8 copy.173
  391.0 4.2 convolution_convert_fusion
  395.2 11.8 %concatenate.69 = bf16[8,128,2816]{2,1,0:T(8,128)(2,1)} reshape(bf16[2816,1024]{1,0:T(8,128)(2,1)} %convolution_convert_fusion) | data formatting | bytes 11534336 | tf_op jit(solution)/shard_map/concatenate | solution.py:379
  407.0 5.7 convert_dynamic-update-slice_fusion.1
  412.7 4.1 convert_dynamic-update-slice_fusion
  416.9 2.8 constant_dynamic-update-slice_fusion.7
  419.7 2.1 convert_dynamic-update-slice_fusion.3
  421.8 58.2 %all-to-all-done.1 = bf16[8,256,2048]{2,1,0:T(8,128)(2,1)} async-done(((bf16[8,256,2048]{2,1,0:T(8,128)(2,1)}), bf16[8,256,2048]{2,1,0:T(8,128)(2,1)}, u32[]{:S(2)}, u32[]{:S(2)}) %all-to-all-start.1) | async-done | bytes 8388640 | tf_op jit(solution)/shard_map/all_to_all | solution.py:392
  479.9 5.3 convert_reduce_fusion
  485.3 1.9 copy.186
  487.1 3.0 slice_multiply_fusion
  492.0 2.1 convert_dynamic-update-slice_fusion.2
  495.8 1.9 fusion.48
  503.8 1.8 convolution_convert_fusion.1
  506.3 2.4 fusion.1
  508.7 130.1 %reduce-scatter.3.cloned.1.call-done = bf16[1,128,10496]{2,1,0:T(8,128)(2,1)} async-done(((bf16[8,128,10496]{2,1,0:T(8,128)(2,1)}), bf16[1,128,10496]{2,1,0:T(8,128)(2,1)}) %reduce-scatter.3.cloned.1.call-update) | async-done | bytes 2686992 | tf_op jit(solution)/shard_map/reduce_scatter | solution.py:207
  638.8 2.5 dynamic-slice_bitcast_fusion
  641.3 3.0 collective-permute-start.2
  644.3 29.2 %collective-permute-done.2 = bf16[64,10496]{1,0:T(8,128)(2,1)} collective-permute-done((bf16[64,10496]{1,0:T(8,128)(2,1)}, bf16[64,10496]{1,0:T(8,128)(2,1)}, u32[]{:S(2)}, u32[]{:S(2)}) %collective-permute-start.2) | collective-permute-done | bytes 1343520 | tf_op jit(solution)/shard_map/ppermute | solution.py:217
  673.5 2.1 fusion.2
  677.1 28.3 %collective-permute-done.3 = bf16[64,10496]{1,0:T(8,128)(2,1)S(1)} collective-permute-done((bf16[64,10496]{1,0:T(8,128)(2,1)S(1)}, bf16[64,10496]{1,0:T(8,128)(2,1)S(1)}, u32[]{:S(2)}, u32[]{:S(2)}) %collective-permute-start.3) | collective-permute-done | bytes 1343520 | tf_op jit(solution)/shard_map/ppermute | solution.py:225
  706.8 3.0 collective-permute-start.4
  709.8 11.7 %reshape_reshape.19 = bf16[2816,1024]{1,0:T(8,128)(2,1)} reshape(bf16[16,64,2816]{2,1,0:T(8,128)(2,1)} %get-tuple-element.72) | data formatting | bytes 11534336 | tf_op jit(solution)/shard_map/reshape;reshape | solution.py:293
  721.5 15.9 %collective-permute-done.4 = bf16[64,10496]{1,0:T(8,128)(2,1)} collective-permute-done((bf16[64,10496]{1,0:T(8,128)(2,1)}, bf16[64,10496]{1,0:T(8,128)(2,1)}, u32[]{:S(2)}, u32[]{:S(2)}) %collective-permute-start.4) | collective-permute-done | bytes 1343520 | tf_op jit(solution)/shard_map/ppermute | solution.py:225
  737.4 3.1 add_convert_fusion.1
  741.9 2.6 collective-permute-start.6
  744.5 5.6 fusion.11
  750.1 2.6 copy.198
  756.7 4.0 collective-permute-done.7
  760.8 4.1 collective-permute-start.8
  764.9 3.8 collective-permute-done.5
  768.7 2.0 fusion.5
  775.3 3.3 collective-permute-done.9
  (194 shorter events, 51.8 us)
Async XLA Ops:
  7.2 76.0 %all-gather.5.cloned.1.call-start = ((), (), s32[]{:S(2)}) async-start(), calls=%async_computation.6 | async-start | bytes 10027008 | tf_op jit(solution)/shard_map/all_gather | solution.py:195
  11.7 16.8 %collective-permute-start = (bf16[272,1024]{1,0:T(8,128)(2,1)S(1)}, bf16[272,1024]{1,0:T(8,128)(2,1)S(1)}, u32[]{:S(2)}, u32[]{:S(2)}) collective-permute-start(bf16[272,1024]{1,0:T(8,128)(2,1)S(1)} %pad_dynamic-update-slice_fusion), channel_id=1, source_target_pairs={{0,68},{68,0},{4,64},{64,4},{1,69},{69,1},{5,65},{65,5},{2,70},{70... | collective-permute-start | bytes 1671176 | tf_op jit(solution)/shard_map/ppermute | solution.py:194
  15.9 13.9 %copy-start.33 = (bf16[176,1024]{1,0:T(8,128)(2,1)S(1)}, bf16[176,1024]{1,0:T(8,128)(2,1)}, u32[]{:S(2)}) copy-start(bf16[176,1024]{1,0:T(8,128)(2,1)} %param.22) | copy-start | bytes 1081348
  28.6 1.7 copy-start.34
  28.6 1.7 copy-start.35
  29.7 215.9 %all-gather.7.cloned.1.call-start = ((), (), s32[]{:S(2)}) async-start(), calls=%async_computation.7 | async-start | bytes 19464192 | tf_op jit(solution)/shard_map/all_gather | solution.py:195
  30.4 26.3 %collective-permute-start.1 = (bf16[64,8448]{1,0:T(8,128)(2,1)S(1)}, bf16[64,8448]{1,0:T(8,128)(2,1)S(1)}, u32[]{:S(2)}, u32[]{:S(2)}) collective-permute-start(bf16[64,8448]{1,0:T(8,128)(2,1)S(1)} %constant_dynamic-update-slice_fusion.4), channel_id=1, source_target_pairs={{0,68},{68,0},{4,64},{64,4},{1,69},{69,1},{5,65},{65,5},{2,70},{70... | collective-permute-start | bytes 3244040 | tf_op jit(solution)/shard_map/ppermute | solution.py:194
  56.9 1.6 copy-start.8
  84.6 19.9 %copy-start.10 = (bf16[1,256,8,2,64]{1,4,3,2,0:T(8,128)(2,1)}, bf16[1,256,8,2,64]{1,4,3,2,0:T(8,128)(2,1)S(1)}, u32[]{:S(2)}) copy-start(bf16[1,256,8,2,64]{1,4,3,2,0:T(8,128)(2,1)S(1)} %copy.161) | copy-start | bytes 1572868
  98.6 2.8 copy-start.27
  104.4 2.5 copy-start.31
  111.3 5.9 copy-start.36
  111.3 5.9 copy-start.37
  111.3 8.0 %copy-start.30 = (bf16[1,256,16,64]{1,3,2,0:T(8,128)(2,1)S(1)}, bf16[1,256,16,64]{1,3,2,0:T(8,128)(2,1)}, u32[]{:S(2)}) copy-start(bf16[1,256,16,64]{1,3,2,0:T(8,128)(2,1)} %get-tuple-element.119) | copy-start | bytes 1572868
  111.3 100.7 %all-to-all-start = ((bf16[8,256,2048]{2,1,0:T(8,128)(2,1)}), bf16[8,256,2048]{2,1,0:T(8,128)(2,1)}, u32[]{:S(2)}, u32[]{:S(2)}) async-start(bf16[8,256,2048]{2,1,0:T(8,128)(2,1)} %broadcast_in_dim.72), calls=%async_computation | async-start | bytes 16777216 | tf_op jit(solution)/shard_map/all_to_all | solution.py:313
  238.5 4.0 copy-start.17
  240.6 1.0 copy-start.3
  245.6 37.5 %copy-start.24 = (bf16[1,256,8,2,64]{1,4,3,2,0:T(8,128)(2,1)}, bf16[1,256,8,2,64]{1,4,3,2,0:T(8,128)(2,1)S(1)}, u32[]{:S(2)}) copy-start(bf16[1,256,8,2,64]{1,4,3,2,0:T(8,128)(2,1)S(1)} %copy.172) | copy-start | bytes 1572868
  278.6 4.5 copy-start.26
  278.6 11.9 %slice-start.4 = ((s8[5767168]{0:T(1024)(128)(4,1)}), s8[4194304]{0:T(1024)(128)(4,1)S(1)}, s32[]{:S(2)}) async-start(s8[5767168]{0:T(1024)(128)(4,1)} %bitcast.232), calls=%async_computation.12 | async-start | bytes 8388608
  278.6 13.6 %slice-start = ((s8[5767168]{0:T(1024)(128)(4,1)}), s8[4194304]{0:T(1024)(128)(4,1)S(1)}, s32[]{:S(2)}) async-start(s8[5767168]{0:T(1024)(128)(4,1)} %bitcast.205), calls=%async_computation.8 | async-start | bytes 8388608
  283.2 7.4 slice-start.5
  283.2 9.1 %slice-start.1 = ((s8[5767168]{0:T(1024)(128)(4,1)}), s8[1572864]{0:T(1024)(128)(4,1)S(1)}, s32[]{:S(2)}) async-start(s8[5767168]{0:T(1024)(128)(4,1)} %bitcast.205), calls=%async_computation.9 | async-start | bytes 3145728
  290.5 1.7 copy-start.40
  290.5 1.7 copy-start.38
  299.8 4.6 copy-start.28
  302.4 2.0 copy-start.4
  302.4 2.2 copy-start.15
  305.0 1.0 copy-start.6
  350.5 35.8 %copy-start.32 = (bf16[256,2816]{1,0:T(8,128)(2,1)S(1)}, bf16[256,2816]{1,0:T(8,128)(2,1)}, u32[]{:S(2)}) copy-start(bf16[256,2816]{1,0:T(8,128)(2,1)} %get-tuple-element.83) | copy-start | bytes 4325380
  350.5 129.5 %all-to-all-start.1 = ((bf16[8,256,2048]{2,1,0:T(8,128)(2,1)}), bf16[8,256,2048]{2,1,0:T(8,128)(2,1)}, u32[]{:S(2)}, u32[]{:S(2)}) async-start(bf16[8,256,2048]{2,1,0:T(8,128)(2,1)} %bitcast.228), calls=%async_computation.1 | async-start | bytes 16777216 | tf_op jit(solution)/shard_map/all_to_all | solution.py:392
  386.2 252.6 %reduce-scatter.3.cloned.1.call-start = ((), (), s32[]{:S(2)}) async-start(), calls=%async_computation.4 | async-start | bytes 24182784 | tf_op jit(solution)/shard_map/reduce_scatter | solution.py:207
  388.1 2.9 copy-start.29
  389.6 5.6 copy-start.16
  395.2 11.8 %copy-start.25 = (bf16[1,256,8,2,64]{1,4,3,2,0:T(8,128)(2,1)S(1)}, bf16[1,256,8,2,64]{1,4,3,2,0:T(8,128)(2,1)}, u32[]{:S(2)}) copy-start(bf16[1,256,8,2,64]{1,4,3,2,0:T(8,128)(2,1)} %copy-done.24) | copy-start | bytes 1572868
  407.0 5.8 copy-start.39
  407.0 9.9 %slice-start.2 = ((s8[5767168]{0:T(1024)(128)(4,1)}), s8[4194304]{0:T(1024)(128)(4,1)S(1)}, s32[]{:S(2)}) async-start(s8[5767168]{0:T(1024)(128)(4,1)} %bitcast.208), calls=%async_computation.10 | async-start | bytes 8388608
  412.7 4.2 slice-start.3
  416.9 2.8 copy-start.7
  416.9 2.8 copy-start.18
  487.1 3.0 copy-start.23
  490.1 1.9 copy-start.11
  491.2 0.8 copy-start.22
  494.1 1.7 copy-start.2
  494.1 246.7 %reduce-scatter.5.cloned.1.call-start = ((), (), s32[]{:S(2)}) async-start(), calls=%async_computation.5 | async-start | bytes 5308416 | tf_op jit(solution)/shard_map/reduce_scatter | solution.py:207
  494.5 3.2 copy-start.1
  495.7 2.8 copy-start.20
  497.7 1.6 copy-start
  497.7 1.7 copy-start.19
  500.5 2.7 copy-start.9
  501.6 2.2 copy-start.12
  503.2 2.4 copy-start.13
  503.6 2.0 copy-start.21
  641.3 32.2 %collective-permute-start.2 = (bf16[64,10496]{1,0:T(8,128)(2,1)}, bf16[64,10496]{1,0:T(8,128)(2,1)}, u32[]{:S(2)}, u32[]{:S(2)}) collective-permute-start(bf16[64,10496]{1,0:T(8,128)(2,1)} %dynamic-slice_bitcast_fusion), channel_id=1, source_target_pairs={{0,68},{68,0},{4,64},{64,4},{1,69},{69,1},{5,65},{65,5},{2,70},{70... | collective-permute-start | bytes 4030472 | tf_op jit(solution)/shard_map/ppermute | solution.py:217
  675.6 29.8 %collective-permute-start.3 = (bf16[64,10496]{1,0:T(8,128)(2,1)S(1)}, bf16[64,10496]{1,0:T(8,128)(2,1)S(1)}, u32[]{:S(2)}, u32[]{:S(2)}) collective-permute-start(bf16[64,10496]{1,0:T(8,128)(2,1)S(1)} %fusion.2), channel_id=1, source_target_pairs={{0,1},{1,0},{2,3},{3,2},{4,5},{5,4},{6,7},{7,6},{8,9},{9,8},{10,11... | collective-permute-start | bytes 4030472 | tf_op jit(solution)/shard_map/ppermute | solution.py:225
  706.8 30.6 %collective-permute-start.4 = (bf16[64,10496]{1,0:T(8,128)(2,1)}, bf16[64,10496]{1,0:T(8,128)(2,1)}, u32[]{:S(2)}, u32[]{:S(2)}) collective-permute-start(bf16[64,10496]{1,0:T(8,128)(2,1)} %add_convert_fusion.2), channel_id=1, source_target_pairs={{0,2},{1,3},{2,0},{3,1},{4,6},{5,7},{6,4},{7,5},{8,10},{9,11},{10,... | collective-permute-start | bytes 4030472 | tf_op jit(solution)/shard_map/ppermute | solution.py:225
  721.5 23.0 %copy-start.5 = (f32[1,256,1024]{2,1,0:T(8,128)S(1)}, f32[1,256,1024]{2,1,0:T(8,128)}, u32[]{:S(2)}) copy-start(f32[1,256,1024]{2,1,0:T(8,128)} %copy-done.3) | copy-start | bytes 3145732
  740.5 28.2 %collective-permute-start.5 = (bf16[64,10496]{1,0:T(8,128)(2,1)}, bf16[64,10496]{1,0:T(8,128)(2,1)}, u32[]{:S(2)}, u32[]{:S(2)}) collective-permute-start(bf16[64,10496]{1,0:T(8,128)(2,1)} %add_convert_fusion.1), channel_id=1, source_target_pairs={{0,4},{1,5},{2,6},{3,7},{4,0},{5,1},{6,2},{7,3},{8,12},{9,13},{10,... | collective-permute-start | bytes 4030472 | tf_op jit(solution)/shard_map/ppermute | solution.py:225
  741.9 10.8 %collective-permute-start.6 = (bf16[144,1024]{1,0:T(8,128)(2,1)S(1)}, bf16[144,1024]{1,0:T(8,128)(2,1)S(1)}, u32[]{:S(2)}, u32[]{:S(2)}) collective-permute-start(bf16[144,1024]{1,0:T(8,128)(2,1)S(1)} %dynamic-slice_bitcast_fusion.1), channel_id=1, source_target_pairs={{0,68},{68,0},{4,64},{64,4},{1,69},{69,1},{5,65},{65,5},{2,70},{70... | collective-permute-start | bytes 884744 | tf_op jit(solution)/shard_map/ppermute | solution.py:217
  750.1 5.3 copy-start.14
  753.7 7.0 collective-permute-start.7
  760.8 10.0 %collective-permute-start.8 = (bf16[144,1024]{1,0:T(8,128)(2,1)S(1)}, bf16[144,1024]{1,0:T(8,128)(2,1)S(1)}, u32[]{:S(2)}, u32[]{:S(2)}) collective-permute-start(bf16[144,1024]{1,0:T(8,128)(2,1)S(1)} %add_convert_fusion.5), channel_id=1, source_target_pairs={{0,2},{1,3},{2,0},{3,1},{4,6},{5,7},{6,4},{7,5},{8,10},{9,11},{10,... | collective-permute-start | bytes 884744 | tf_op jit(solution)/shard_map/ppermute | solution.py:225
  771.5 7.0 collective-permute-start.9
Sparse Core Ops, SparseCore 0:
  29.9 53.2 all-gather.4
  84.8 87.3 all-gather.6
  494.3 144.5 reduce-scatter.2
  644.4 36.4 reduce-scatter.4

commit v10 on v8

--- a/solution.py
+++ b/solution.py
@@ -197,12 +197,20 @@
 
 
 def fsdp_reduce_scatter(grads):
+    return z_combine(yc_reduce_scatter(grads))
+
+
+def yc_reduce_scatter(grads):
     n_yc = grads.shape[0] // 2
     by_yc = grads
     block = grads.shape[1:]
     halves = lax.psum_scatter(
         by_yc.reshape((n_yc, 2 * block[0]) + block[1:]), ("y", "core"), scatter_dimension=0, tiled=False
     ).reshape((2,) + block)
+    return halves
+
+
+def z_combine(halves):
     zh = lax.axis_index("zh")
     mine = lax.dynamic_index_in_dim(halves, zh, axis=0, keepdims=False)
     theirs = lax.dynamic_index_in_dim(halves, 1 - zh, axis=0, keepdims=False)
@@ -361,7 +369,7 @@
         ],
         axis=2,
     ).astype(jnp.bfloat16)
-    mlp_share = fsdp_reduce_scatter(mlp_grads)
+    mlp_halves = yc_reduce_scatter(mlp_grads)
 
     blended_value_gradient = from_gathered(
         jnp.einsum("sre,de->srd", middle_low, out_mat, preferred_element_type=jnp.float32).astype(
@@ -426,8 +434,8 @@
         ],
         axis=1,
     ).astype(jnp.bfloat16)
-    attn_grads, mlp_share = lax.optimization_barrier((attn_grads, mlp_share))
-    mlp_share = ctx_allreduce(mlp_share, n_ctx)
+    attn_grads, mlp_halves = lax.optimization_barrier((attn_grads, mlp_halves))
+    mlp_share = ctx_allreduce(z_combine(mlp_halves), n_ctx)
     attn_share = fsdp_reduce_scatter(attn_grads)
     attn_share = ctx_allreduce(attn_share, n_ctx)
 

time: 732 us -> 730 us (level)
  waiting for transfers between devices: 318 us -> 327 us
  transfers between devices with their start and end apart: 16 -> 16, of which waited for: 12 -> 13; matrix products, arithmetic and copies ran while one was open for 15% -> 15% of each run, Pallas kernels for 9% -> 9%
where the time goes in v10:
time: 730 us; the launch traced here: 722 us
  waiting for transfers between devices  327 us (45%)
  local copies, waits for them, and re-layouts  116 us (16%)
  starting transfers between devices  91 us (12%)
  Pallas kernels  67.7 us (9%)
  matrix products  57.1 us (8%)
  other arithmetic  48.8 us (7%)
  between operations  15 us (2%)
    all_to_all x1, waiting for transfers between devices, body(): lax.all_to_all(kv_back.reshape(n_ctx, rows, 2 * width), CTX, 0, 0, tiled=...  93.4 us
    all_to_all x1, waiting for transfers between devices, body(): lax.all_to_all(jnp.broadcast_to(kv_own[None], (n_ctx, rows, 2 * width)),...  91.9 us
    ppermute x6, waiting for transfers between devices, ctx_allreduce(): other = lax.ppermute(total, CTX, [(j, j ^ step) for j in range(n_ctx)])  53 us
    pallas_call x1, Pallas kernels, attention_backward(): pl.pallas_call(functools.partial(attn_bwd_kernel, head_dim, scale), out_s...  43.3 us
    ppermute x6, starting transfers between devices, ctx_allreduce(): other = lax.ppermute(total, CTX, [(j, j ^ step) for j in range(n_ctx)])  36.8 us
    ppermute x2, waiting for transfers between devices, fsdp_gather(): other = lax.ppermute(pack, ('zh', 'zl'), Z_CROSS)  35.9 us
    all_to_all x1, starting transfers between devices, body(): lax.all_to_all(kv_back.reshape(n_ctx, rows, 2 * width), CTX, 0, 0, tiled=...  35.6 us
    ppermute x2, waiting for transfers between devices, z_combine(): got = lax.ppermute(theirs, ('zh', 'zl'), Z_CROSS)  28.6 us
  transfers between devices with their start and end apart: 16, of which 13 were waited for; matrix products, arithmetic and copies ran while one was open for 15% of the time, Pallas kernels for 9%

profile of v10, /device:TPU:0, one launch (start us, length us, event | category | flops | bytes accessed | tf_op | source)
XLA Modules:
  0.0 722.3 jit_solution(11806541547017406336)
XLA Ops:
  11.7 4.2 collective-permute-start
  15.9 12.6 %collective-permute-done = bf16[272,1024]{1,0:T(8,128)(2,1)S(1)} collective-permute-done((bf16[272,1024]{1,0:T(8,128)(2,1)S(1)}, bf16[272,1024]{1,0:T(8,128)(2,1)S(1)}, u32[]{:S(2)}, u32[]{:S(2)}) %collective-permute-start) | collective-permute-done | bytes 557088 | tf_op jit(solution)/shard_map/ppermute | solution.py:194
  30.4 3.1 collective-permute-start.1
  33.4 23.3 %collective-permute-done.1 = bf16[64,8448]{1,0:T(8,128)(2,1)S(1)} collective-permute-done((bf16[64,8448]{1,0:T(8,128)(2,1)S(1)}, bf16[64,8448]{1,0:T(8,128)(2,1)S(1)}, u32[]{:S(2)}, u32[]{:S(2)}) %collective-permute-start.1) | collective-permute-done | bytes 1081376 | tf_op jit(solution)/shard_map/ppermute | solution.py:194
  58.9 24.3 %all-gather.5.cloned.1.call-done = bf16[16,272,1024]{2,1,0:T(8,128)(2,1)} async-done(((bf16[2,272,1024]{2,1,0:T(8,128)(2,1)}), bf16[16,272,1024]{2,1,0:T(8,128)(2,1)}) %all-gather.5.cloned.1.call-update) | async-done | bytes 8912912 | tf_op jit(solution)/shard_map/all_gather | solution.py:195
  84.6 6.0 fusion.41
  90.5 3.9 copy.163
  94.5 4.1 copy.161
  98.6 2.8 convolution_bitcast_fusion.3
  104.4 2.5 fusion.9
  107.0 4.4 broadcast_in_dim.72
  111.4 5.3 all-to-all-start
  119.8 91.9 %all-to-all-done = bf16[8,256,2048]{2,1,0:T(8,128)(2,1)} async-done(((bf16[8,256,2048]{2,1,0:T(8,128)(2,1)}), bf16[8,256,2048]{2,1,0:T(8,128)(2,1)}, u32[]{:S(2)}, u32[]{:S(2)}) %all-to-all-start) | async-done | bytes 8388640 | tf_op jit(solution)/shard_map/all_to_all | solution.py:313
  211.7 24.4 %shard_map.229 = bf16[256,1024]{1,0:T(8,128)(2,1)S(1)} custom-call(s32[2]{0:T(128)S(1)} %pad_add_fusion.meta_ref, bf16[256,1024]{1,0:T(8,128)(2,1)S(1)} %copy.166.q_ref, bf16[2048,2048]{1,0:T(8,128)(2,1)} %bitcast.24.k_ref.v_ref, bf16[2048,2048]{1,0:T(8,128)(2,1)} %bitcast.24.k_ref.v_ref), custom_call_target="tpu_custom_call" | custom-call | flops 2147483648 | bytes 9437184 | tf_op jit(solution)/shard_map/pallas_call | solution.py:80
  238.1 2.1 multiply_reduce_fusion.2
  242.1 2.0 copy.170
  245.3 11.4 %fusion.40 = (bf16[16,64,2816]{2,1,0:T(8,128)(2,1)}, bf16[16,64,2816]{2,1,0:T(8,128)(2,1)}, bf16[16,64,2816]{2,1,0:T(8,128)(2,1)}) fusion(bf16[16,64,8448]{2,1,0:T(8,128)(2,1)} %all-gather.7.cloned.1.call-done), kind=kLoop, calls=%fused_computation.130 | loop fusion | bytes 34603008 | tf_op jit(solution)/shard_map/slice | solution.py:293
  256.6 11.7 %dot_general.113 = bf16[8,2,176,1024]{3,2,1,0:T(8,128)(2,1)} reshape(bf16[16,64,2816]{2,1,0:T(8,128)(2,1)} %get-tuple-element.72) | data formatting | bytes 11534336 | tf_op jit(solution)/shard_map/sre,fe->srf/dot_general | solution.py:338
  268.4 4.6 convolution_bitcast_fusion
  273.0 1.8 copy.174
  274.8 3.4 copy.175
  278.2 4.5 fusion.45
  282.7 7.0 multiply_convert_fusion
  291.4 4.2 convolution_convert_fusion.2
  295.6 4.1 convolution_convert_fusion.1
  299.7 2.7 convolution_add_fusion.2
  302.3 2.6 copy.172
  304.9 2.6 copy.173
  307.5 2.6 copy.177
  310.0 2.3 copy.178
  312.3 2.6 copy.179
  314.9 2.0 multiply_reduce_fusion
  318.5 4.3 convolution_convert_fusion
  322.8 11.8 %concatenate.69 = bf16[8,128,2816]{2,1,0:T(8,128)(2,1)} reshape(bf16[2816,1024]{1,0:T(8,128)(2,1)} %convolution_convert_fusion) | data formatting | bytes 11534336 | tf_op jit(solution)/shard_map/concatenate | solution.py:363
  334.5 1.9 convolution_convert_fusion.3
  336.5 14.2 %pad_maximum_fusion = bf16[8,128,9472]{2,1,0:T(8,128)(2,1)} fusion(bf16[8,128,1024]{2,1,0:T(8,128)(2,1)S(1)} %convolution_convert_fusion.3, bf16[8,128,2816]{2,1,0:T(8,128)(2,1)} %concatenate.69, bf16[8,128,2816]{2,1,0:T(8,128)(2,1)} %convolution_convert_fusion.1, bf16[8,128,2816]{2,1,0:T(8,128)(2,1)} %convolution_convert_fusion.2), kind=kLoop, calls=%fused_computation | loop fusion | flops 77594624 | bytes 38797312 | tf_op jit(solution)/shard_map/concatenate | solution.py:363
  350.8 2.0 convolution_convert_fusion.7
  353.2 43.3 %shard_map.230 = (f32[256,1024]{1,0:T(8,128)S(1)}, bf16[2048,2048]{1,0:T(8,128)(2,1)}) custom-call(s32[2]{0:T(128)S(1)} %pad_add_fusion.meta_ref, bf16[256,1024]{1,0:T(8,128)(2,1)S(1)} %copy.166.q_ref, bf16[2048,2048]{1,0:T(8,128)(2,1)} %bitcast.24.k_ref.v_ref, bf16[2048,2048]{1,0:T(8,128)(2,1)} %bitcast.24.k_ref.v_ref, bf16[256,1024]{1,0:T(8,128)(2,1)S(1)} %copy.183.do_ref), custom_call_target="tpu_custom_call" | custom-call | flops 5368709120 | bytes 19398656 | tf_op jit(solution)/shard_map/pallas_call | solution.py:108
  396.6 35.6 %all-to-all-start.1 = ((bf16[8,256,2048]{2,1,0:T(8,128)(2,1)}), bf16[8,256,2048]{2,1,0:T(8,128)(2,1)}, u32[]{:S(2)}, u32[]{:S(2)}) async-start(bf16[8,256,2048]{2,1,0:T(8,128)(2,1)} %bitcast.228), calls=%async_computation.1 | async-start | bytes 16777216 | tf_op jit(solution)/shard_map/all_to_all | solution.py:385
  432.6 93.4 %all-to-all-done.1 = bf16[8,256,2048]{2,1,0:T(8,128)(2,1)} async-done(((bf16[8,256,2048]{2,1,0:T(8,128)(2,1)}), bf16[8,256,2048]{2,1,0:T(8,128)(2,1)}, u32[]{:S(2)}, u32[]{:S(2)}) %all-to-all-start.1) | async-done | bytes 8388640 | tf_op jit(solution)/shard_map/all_to_all | solution.py:385
  526.0 5.3 convert_reduce_fusion
  531.4 2.1 copy.185
  533.4 2.8 slice_multiply_fusion
  540.4 1.8 convolution_add_fusion
  547.0 1.8 convolution_convert_fusion.6
  550.3 3.3 fusion.1
  553.6 2.5 dynamic-slice_bitcast_fusion
  556.1 2.6 collective-permute-start.6
  558.7 27.3 %collective-permute-done.6 = bf16[64,9472]{1,0:T(8,128)(2,1)} collective-permute-done((bf16[64,9472]{1,0:T(8,128)(2,1)}, bf16[64,9472]{1,0:T(8,128)(2,1)}, u32[]{:S(2)}, u32[]{:S(2)}) %collective-permute-start.6) | collective-permute-done | bytes 1212448 | tf_op jit(solution)/shard_map/ppermute | solution.py:217
  586.0 1.9 fusion.2
  587.9 28.1 %collective-permute-start.7 = (bf16[64,9472]{1,0:T(8,128)(2,1)S(1)}, bf16[64,9472]{1,0:T(8,128)(2,1)S(1)}, u32[]{:S(2)}, u32[]{:S(2)}) collective-permute-start(bf16[64,9472]{1,0:T(8,128)(2,1)S(1)} %fusion.2), channel_id=1, source_target_pairs={{0,1},{1,0},{2,3},{3,2},{4,5},{5,4},{6,7},{7,6},{8,9},{9,8},{10,11... | collective-permute-start | bytes 3637256 | tf_op jit(solution)/shard_map/ppermute | solution.py:225
  616.1 24.3 %collective-permute-done.7 = bf16[64,9472]{1,0:T(8,128)(2,1)S(1)} collective-permute-done((bf16[64,9472]{1,0:T(8,128)(2,1)S(1)}, bf16[64,9472]{1,0:T(8,128)(2,1)S(1)}, u32[]{:S(2)}, u32[]{:S(2)}) %collective-permute-start.7) | collective-permute-done | bytes 1212448 | tf_op jit(solution)/shard_map/ppermute | solution.py:225
  641.8 4.6 collective-permute-start.8
  646.3 11.7 %reshape_reshape.19 = bf16[2816,1024]{1,0:T(8,128)(2,1)} reshape(bf16[16,64,2816]{2,1,0:T(8,128)(2,1)} %get-tuple-element.72) | data formatting | bytes 11534336 | tf_op jit(solution)/shard_map/reshape;reshape | solution.py:293
  658.0 12.7 %collective-permute-done.8 = bf16[64,9472]{1,0:T(8,128)(2,1)} collective-permute-done((bf16[64,9472]{1,0:T(8,128)(2,1)}, bf16[64,9472]{1,0:T(8,128)(2,1)}, u32[]{:S(2)}, u32[]{:S(2)}) %collective-permute-start.8) | collective-permute-done | bytes 1212448 | tf_op jit(solution)/shard_map/ppermute | solution.py:225
  670.8 3.0 add_convert_fusion.1
  674.8 2.8 collective-permute-start.2
  677.6 5.6 fusion.10
  685.2 2.5 copy.197
  689.1 6.4 collective-permute-done.3
  695.6 2.6 collective-permute-start.4
  699.3 1.9 fusion.13
  701.9 3.4 collective-permute-done.4
  708.7 5.0 collective-permute-done.5
  (161 shorter events, 48.1 us)
Async XLA Ops:
  7.2 75.9 %all-gather.5.cloned.1.call-start = ((), (), s32[]{:S(2)}) async-start(), calls=%async_computation.6 | async-start | bytes 10027008 | tf_op jit(solution)/shard_map/all_gather | solution.py:195
  11.7 16.8 %collective-permute-start = (bf16[272,1024]{1,0:T(8,128)(2,1)S(1)}, bf16[272,1024]{1,0:T(8,128)(2,1)S(1)}, u32[]{:S(2)}, u32[]{:S(2)}) collective-permute-start(bf16[272,1024]{1,0:T(8,128)(2,1)S(1)} %pad_dynamic-update-slice_fusion), channel_id=1, source_target_pairs={{0,68},{68,0},{4,64},{64,4},{1,69},{69,1},{5,65},{65,5},{2,70},{70... | collective-permute-start | bytes 1671176 | tf_op jit(solution)/shard_map/ppermute | solution.py:194
  15.9 13.9 %copy-start.22 = (bf16[176,1024]{1,0:T(8,128)(2,1)S(1)}, bf16[176,1024]{1,0:T(8,128)(2,1)}, u32[]{:S(2)}) copy-start(bf16[176,1024]{1,0:T(8,128)(2,1)} %param.22) | copy-start | bytes 1081348
  28.6 1.6 copy-start.23
  28.6 1.7 copy-start.24
  29.7 215.5 %all-gather.7.cloned.1.call-start = ((), (), s32[]{:S(2)}) async-start(), calls=%async_computation.7 | async-start | bytes 19464192 | tf_op jit(solution)/shard_map/all_gather | solution.py:195
  30.4 26.3 %collective-permute-start.1 = (bf16[64,8448]{1,0:T(8,128)(2,1)S(1)}, bf16[64,8448]{1,0:T(8,128)(2,1)S(1)}, u32[]{:S(2)}, u32[]{:S(2)}) collective-permute-start(bf16[64,8448]{1,0:T(8,128)(2,1)S(1)} %constant_dynamic-update-slice_fusion.4), channel_id=1, source_target_pairs={{0,68},{68,0},{4,64},{64,4},{1,69},{69,1},{5,65},{65,5},{2,70},{70... | collective-permute-start | bytes 3244040 | tf_op jit(solution)/shard_map/ppermute | solution.py:194
  56.8 1.6 copy-start.7
  84.6 19.9 %copy-start.9 = (bf16[1,256,8,2,64]{1,4,3,2,0:T(8,128)(2,1)}, bf16[1,256,8,2,64]{1,4,3,2,0:T(8,128)(2,1)S(1)}, u32[]{:S(2)}) copy-start(bf16[1,256,8,2,64]{1,4,3,2,0:T(8,128)(2,1)S(1)} %copy.160) | copy-start | bytes 1572868
  98.6 2.8 copy-start.17
  104.4 2.5 copy-start.20
  111.4 5.9 copy-start.25
  111.4 5.9 copy-start.26
  111.4 8.2 %copy-start.19 = (bf16[1,256,16,64]{1,3,2,0:T(8,128)(2,1)S(1)}, bf16[1,256,16,64]{1,3,2,0:T(8,128)(2,1)}, u32[]{:S(2)}) copy-start(bf16[1,256,16,64]{1,3,2,0:T(8,128)(2,1)} %get-tuple-element.118) | copy-start | bytes 1572868
  111.4 100.2 %all-to-all-start = ((bf16[8,256,2048]{2,1,0:T(8,128)(2,1)}), bf16[8,256,2048]{2,1,0:T(8,128)(2,1)}, u32[]{:S(2)}, u32[]{:S(2)}) async-start(bf16[8,256,2048]{2,1,0:T(8,128)(2,1)} %broadcast_in_dim.72), calls=%async_computation | async-start | bytes 16777216 | tf_op jit(solution)/shard_map/all_to_all | solution.py:313
  116.7 436.8 %reduce-scatter.3.cloned.1.call-start = ((), (), s32[]{:S(2)}) async-start(), calls=%async_computation.4 | async-start | bytes 21823488 | tf_op jit(solution)/shard_map/reduce_scatter | solution.py:207
  238.1 4.0 copy-start.13
  240.2 1.0 copy-start.3
  278.1 4.5 copy-start.16
  278.1 11.5 %slice-start.2 = ((s8[5767168]{0:T(1024)(128)(4,1)}), s8[4194304]{0:T(1024)(128)(4,1)S(1)}, s32[]{:S(2)}) async-start(s8[5767168]{0:T(1024)(128)(4,1)} %bitcast.232), calls=%async_computation.10 | async-start | bytes 8388608
  282.7 7.0 slice-start.3
  291.4 8.3 %slice-start = ((s8[5767168]{0:T(1024)(128)(4,1)}), s8[4194304]{0:T(1024)(128)(4,1)S(1)}, s32[]{:S(2)}) async-start(s8[5767168]{0:T(1024)(128)(4,1)} %bitcast.203), calls=%async_computation.8 | async-start | bytes 8388608
  295.6 4.1 slice-start.1
  312.3 4.6 copy-start.18
  314.9 2.0 copy-start.4
  314.9 2.2 copy-start.11
  314.9 3.6 copy-start.12
  322.8 11.8 %copy-start.14 = (bf16[1,256,8,2,64]{1,4,3,2,0:T(8,128)(2,1)S(1)}, bf16[1,256,8,2,64]{1,4,3,2,0:T(8,128)(2,1)}, u32[]{:S(2)}) copy-start(bf16[1,256,8,2,64]{1,4,3,2,0:T(8,128)(2,1)} %copy-done.13) | copy-start | bytes 1572868
  396.6 129.4 %all-to-all-start.1 = ((bf16[8,256,2048]{2,1,0:T(8,128)(2,1)}), bf16[8,256,2048]{2,1,0:T(8,128)(2,1)}, u32[]{:S(2)}, u32[]{:S(2)}) async-start(bf16[8,256,2048]{2,1,0:T(8,128)(2,1)} %bitcast.228), calls=%async_computation.1 | async-start | bytes 16777216 | tf_op jit(solution)/shard_map/all_to_all | solution.py:385
  432.2 241.6 %reduce-scatter.5.cloned.1.call-start = ((), (), s32[]{:S(2)}) async-start(), calls=%async_computation.5 | async-start | bytes 7667712 | tf_op jit(solution)/shard_map/reduce_scatter | solution.py:207
  536.2 1.8 copy-start.2
  536.6 2.2 copy-start.1
  536.7 2.9 copy-start.15
  538.8 1.6 copy-start
  543.7 2.7 copy-start.8
  544.8 2.2 copy-start.10
  556.1 29.9 %collective-permute-start.6 = (bf16[64,9472]{1,0:T(8,128)(2,1)}, bf16[64,9472]{1,0:T(8,128)(2,1)}, u32[]{:S(2)}, u32[]{:S(2)}) collective-permute-start(bf16[64,9472]{1,0:T(8,128)(2,1)} %dynamic-slice_bitcast_fusion), channel_id=1, source_target_pairs={{0,68},{68,0},{4,64},{64,4},{1,69},{69,1},{5,65},{65,5},{2,70},{70... | collective-permute-start | bytes 3637256 | tf_op jit(solution)/shard_map/ppermute | solution.py:217
  587.9 52.5 %collective-permute-start.7 = (bf16[64,9472]{1,0:T(8,128)(2,1)S(1)}, bf16[64,9472]{1,0:T(8,128)(2,1)S(1)}, u32[]{:S(2)}, u32[]{:S(2)}) collective-permute-start(bf16[64,9472]{1,0:T(8,128)(2,1)S(1)} %fusion.2), channel_id=1, source_target_pairs={{0,1},{1,0},{2,3},{3,2},{4,5},{5,4},{6,7},{7,6},{8,9},{9,8},{10,11... | collective-permute-start | bytes 3637256 | tf_op jit(solution)/shard_map/ppermute | solution.py:225
  641.8 29.0 %collective-permute-start.8 = (bf16[64,9472]{1,0:T(8,128)(2,1)}, bf16[64,9472]{1,0:T(8,128)(2,1)}, u32[]{:S(2)}, u32[]{:S(2)}) collective-permute-start(bf16[64,9472]{1,0:T(8,128)(2,1)} %add_convert_fusion.2), channel_id=1, source_target_pairs={{0,2},{1,3},{2,0},{3,1},{4,6},{5,7},{6,4},{7,5},{8,10},{9,11},{10,... | collective-permute-start | bytes 3637256 | tf_op jit(solution)/shard_map/ppermute | solution.py:225
  658.0 19.6 %copy-start.5 = (f32[1,256,1024]{2,1,0:T(8,128)S(1)}, f32[1,256,1024]{2,1,0:T(8,128)}, u32[]{:S(2)}) copy-start(f32[1,256,1024]{2,1,0:T(8,128)} %copy-done.3) | copy-start | bytes 3145732
  673.8 25.5 %collective-permute-start.9 = (bf16[64,9472]{1,0:T(8,128)(2,1)}, bf16[64,9472]{1,0:T(8,128)(2,1)}, u32[]{:S(2)}, u32[]{:S(2)}) collective-permute-start(bf16[64,9472]{1,0:T(8,128)(2,1)} %add_convert_fusion.1), channel_id=1, source_target_pairs={{0,4},{1,5},{2,6},{3,7},{4,0},{5,1},{6,2},{7,3},{8,12},{9,13},{10,... | collective-permute-start | bytes 3637256 | tf_op jit(solution)/shard_map/ppermute | solution.py:225
  674.8 9.7 %copy-start.21 = (bf16[1,416,1024]{2,1,0:T(8,128)(2,1)S(1)}, bf16[1,416,1024]{2,1,0:T(8,128)(2,1)}, u32[]{:S(2)}) copy-start(bf16[1,416,1024]{2,1,0:T(8,128)(2,1)} %reduce-scatter.5.cloned.1.call-done) | copy-start | bytes 2555908
  674.8 9.7 %collective-permute-start.2 = (bf16[208,1024]{1,0:T(8,128)(2,1)S(1)}, bf16[208,1024]{1,0:T(8,128)(2,1)S(1)}, u32[]{:S(2)}, u32[]{:S(2)}) collective-permute-start(bf16[208,1024]{1,0:T(8,128)(2,1)S(1)} %dynamic-slice_bitcast_fusion.1), channel_id=1, source_target_pairs={{0,68},{68,0},{4,64},{64,4},{1,69},{69,1},{5,65},{65,5},{2,70},{70... | collective-permute-start | bytes 1277960 | tf_op jit(solution)/shard_map/ppermute | solution.py:217
  683.2 4.6 copy-start.6
  684.6 10.8 %collective-permute-start.3 = (bf16[208,1024]{1,0:T(8,128)(2,1)S(1)}, bf16[208,1024]{1,0:T(8,128)(2,1)S(1)}, u32[]{:S(2)}, u32[]{:S(2)}) collective-permute-start(bf16[208,1024]{1,0:T(8,128)(2,1)S(1)} %fusion.24), channel_id=1, source_target_pairs={{0,1},{1,0},{2,3},{3,2},{4,5},{5,4},{6,7},{7,6},{8,9},{9,8},{10,11... | collective-permute-start | bytes 1277960 | tf_op jit(solution)/shard_map/ppermute | solution.py:225
  695.6 9.7 %collective-permute-start.4 = (bf16[208,1024]{1,0:T(8,128)(2,1)S(1)}, bf16[208,1024]{1,0:T(8,128)(2,1)S(1)}, u32[]{:S(2)}, u32[]{:S(2)}) collective-permute-start(bf16[208,1024]{1,0:T(8,128)(2,1)S(1)} %add_convert_fusion.5), channel_id=1, source_target_pairs={{0,2},{1,3},{2,0},{3,1},{4,6},{5,7},{6,4},{7,5},{8,10},{9,11},{10,... | collective-permute-start | bytes 1277960 | tf_op jit(solution)/shard_map/ppermute | solution.py:225
  705.5 8.2 %collective-permute-start.5 = (bf16[208,1024]{1,0:T(8,128)(2,1)S(1)}, bf16[208,1024]{1,0:T(8,128)(2,1)S(1)}, u32[]{:S(2)}, u32[]{:S(2)}) collective-permute-start(bf16[208,1024]{1,0:T(8,128)(2,1)S(1)} %add_convert_fusion.4), channel_id=1, source_target_pairs={{0,4},{1,5},{2,6},{3,7},{4,0},{5,1},{6,2},{7,3},{8,12},{9,13},{10,... | collective-permute-start | bytes 1277960 | tf_op jit(solution)/shard_map/ppermute | solution.py:225
Sparse Core Ops, SparseCore 0:
  29.9 53.2 all-gather.4
  84.8 87.3 all-gather.6
  350.9 135.4 reduce-scatter.2
  553.7 75.4 reduce-scatter.4

commit v11 on v10

--- a/solution.py
+++ b/solution.py
@@ -434,8 +434,11 @@
         ],
         axis=1,
     ).astype(jnp.bfloat16)
-    attn_grads, mlp_halves = lax.optimization_barrier((attn_grads, mlp_halves))
-    mlp_share = ctx_allreduce(z_combine(mlp_halves), n_ctx)
+    mlp_sum = lax.psum(mlp_halves, ("zh",) + CTX)
+    attn_grads, mlp_sum = lax.optimization_barrier((attn_grads, mlp_sum))
+    mlp_share = lax.dynamic_index_in_dim(
+        mlp_sum, lax.axis_index("zh"), axis=0, keepdims=False
+    ).astype(jnp.float32)
     attn_share = fsdp_reduce_scatter(attn_grads)
     attn_share = ctx_allreduce(attn_share, n_ctx)
 

time: 730 us -> 779 us (1.067)
  waiting for transfers between devices: 327 us -> 416 us
  starting transfers between devices: 91 us -> 57.1 us
  other arithmetic: 48.8 us -> 40.8 us
    psum x0 -> x1, waiting for transfers between devices: none -> 115 us  [body(): mlp_sum = lax.psum(mlp_halves, ('zh',) + CTX)]
    ppermute x6 -> x3, waiting for transfers between devices: 53 us -> 17.8 us  [ctx_allreduce(): other = lax.ppermute(total, CTX, [(j, j ^ step) for j in range(n_ctx)])]
    reduce_scatter x2, waiting for transfers between devices: 0.01 us -> 34.3 us  [yc_reduce_scatter(): lax.psum_scatter(by_yc.reshape((n_yc, 2 * block[0]) + block[1:]), ('y', '...]
    ppermute x6 -> x3, starting transfers between devices: 36.8 us -> 5.05 us  [ctx_allreduce(): other = lax.ppermute(total, CTX, [(j, j ^ step) for j in range(n_ctx)])]
    ppermute x2 -> x1, waiting for transfers between devices: 28.6 us -> 3.68 us  [z_combine(): got = lax.ppermute(theirs, ('zh', 'zl'), Z_CROSS)]
  transfers between devices with their start and end apart: 16 -> 13, of which waited for: 13 -> 11; matrix products, arithmetic and copies ran while one was open for 15% -> 12% of each run, Pallas kernels for 9% -> 9%
where the time goes in v11:
time: 779 us; the launch traced here: 767 us
  waiting for transfers between devices  416 us (53%)
  local copies, waits for them, and re-layouts  113 us (15%)
  Pallas kernels  67.8 us (9%)
  matrix products  57.2 us (7%)
  starting transfers between devices  57.1 us (7%)
  other arithmetic  40.8 us (5%)
  between operations  14.9 us (2%)
    psum x1, waiting for transfers between devices, body(): mlp_sum = lax.psum(mlp_halves, ('zh',) + CTX)  115 us
    all_to_all x1, waiting for transfers between devices, body(): lax.all_to_all(kv_back.reshape(n_ctx, rows, 2 * width), CTX, 0, 0, tiled=...  93.4 us
    all_to_all x1, waiting for transfers between devices, body(): lax.all_to_all(jnp.broadcast_to(kv_own[None], (n_ctx, rows, 2 * width)),...  91.8 us
    pallas_call x1, Pallas kernels, attention_backward(): pl.pallas_call(functools.partial(attn_bwd_kernel, head_dim, scale), out_s...  43.4 us
    ppermute x2, waiting for transfers between devices, fsdp_gather(): other = lax.ppermute(pack, ('zh', 'zl'), Z_CROSS)  35.9 us
    all_to_all x1, starting transfers between devices, body(): lax.all_to_all(kv_back.reshape(n_ctx, rows, 2 * width), CTX, 0, 0, tiled=...  35.4 us
    reduce_scatter x2, waiting for transfers between devices, yc_reduce_scatter(): lax.psum_scatter(by_yc.reshape((n_yc, 2 * block[0]) + block[1:]), ('y', '...  34.3 us
    pallas_call x1, Pallas kernels, attention_forward(): pl.pallas_call(functools.partial(attn_fwd_kernel, head_dim, scale), out_s...  24.4 us
  transfers between devices with their start and end apart: 13, of which 11 were waited for; matrix products, arithmetic and copies ran while one was open for 12% of the time, Pallas kernels for 9%

profile of v11, /device:TPU:0, one launch (start us, length us, event | category | flops | bytes accessed | tf_op | source)
XLA Modules:
  0.0 767.2 jit_solution(6058302683792610711)
XLA Ops:
  11.7 4.2 collective-permute-start
  15.9 12.6 %collective-permute-done = bf16[272,1024]{1,0:T(8,128)(2,1)S(1)} collective-permute-done((bf16[272,1024]{1,0:T(8,128)(2,1)S(1)}, bf16[272,1024]{1,0:T(8,128)(2,1)S(1)}, u32[]{:S(2)}, u32[]{:S(2)}) %collective-permute-start) | collective-permute-done | bytes 557088 | tf_op jit(solution)/shard_map/ppermute | solution.py:194
  30.4 3.1 collective-permute-start.1
  33.4 23.3 %collective-permute-done.1 = bf16[64,8448]{1,0:T(8,128)(2,1)S(1)} collective-permute-done((bf16[64,8448]{1,0:T(8,128)(2,1)S(1)}, bf16[64,8448]{1,0:T(8,128)(2,1)S(1)}, u32[]{:S(2)}, u32[]{:S(2)}) %collective-permute-start.1) | collective-permute-done | bytes 1081376 | tf_op jit(solution)/shard_map/ppermute | solution.py:194
  56.9 1.6 pad_maximum_fusion.1
  58.9 24.2 %all-gather.5.cloned.1.call-done = bf16[16,272,1024]{2,1,0:T(8,128)(2,1)} async-done(((bf16[2,272,1024]{2,1,0:T(8,128)(2,1)}), bf16[16,272,1024]{2,1,0:T(8,128)(2,1)}) %all-gather.5.cloned.1.call-update) | async-done | bytes 8912912 | tf_op jit(solution)/shard_map/all_gather | solution.py:195
  84.6 5.9 fusion.39
  90.5 3.9 copy.163
  94.4 4.1 copy.161
  98.6 2.8 convolution_bitcast_fusion.3
  104.3 2.5 fusion.8
  106.9 4.4 broadcast_in_dim.72
  111.3 5.4 all-to-all-start
  119.7 91.8 %all-to-all-done = bf16[8,256,2048]{2,1,0:T(8,128)(2,1)} async-done(((bf16[8,256,2048]{2,1,0:T(8,128)(2,1)}), bf16[8,256,2048]{2,1,0:T(8,128)(2,1)}, u32[]{:S(2)}, u32[]{:S(2)}) %all-to-all-start) | async-done | bytes 8388640 | tf_op jit(solution)/shard_map/all_to_all | solution.py:313
  211.6 24.4 %shard_map.229 = bf16[256,1024]{1,0:T(8,128)(2,1)S(1)} custom-call(s32[2]{0:T(128)S(1)} %pad_add_fusion.meta_ref, bf16[256,1024]{1,0:T(8,128)(2,1)S(1)} %copy.166.q_ref, bf16[2048,2048]{1,0:T(8,128)(2,1)} %bitcast.24.k_ref.v_ref, bf16[2048,2048]{1,0:T(8,128)(2,1)} %bitcast.24.k_ref.v_ref), custom_call_target="tpu_custom_call" | custom-call | flops 2147483648 | bytes 9437184 | tf_op jit(solution)/shard_map/pallas_call | solution.py:80
  238.0 2.1 multiply_reduce_fusion.2
  242.0 2.0 copy.170
  245.2 11.3 %fusion.38 = (bf16[16,64,2816]{2,1,0:T(8,128)(2,1)}, bf16[16,64,2816]{2,1,0:T(8,128)(2,1)}, bf16[16,64,2816]{2,1,0:T(8,128)(2,1)}) fusion(bf16[16,64,8448]{2,1,0:T(8,128)(2,1)} %all-gather.7.cloned.1.call-done), kind=kLoop, calls=%fused_computation.124 | loop fusion | bytes 34603008 | tf_op jit(solution)/shard_map/slice | solution.py:293
  256.5 11.7 %dot_general.113 = bf16[8,2,176,1024]{3,2,1,0:T(8,128)(2,1)} reshape(bf16[16,64,2816]{2,1,0:T(8,128)(2,1)} %get-tuple-element.72) | data formatting | bytes 11534336 | tf_op jit(solution)/shard_map/sre,fe->srf/dot_general | solution.py:338
  268.2 4.6 convolution_bitcast_fusion
  272.8 1.8 copy.174
  274.6 3.4 copy.175
  278.0 4.5 fusion.43
  282.5 7.0 multiply_convert_fusion
  289.5 1.7 fusion.44
  291.2 4.1 convolution_convert_fusion.2
  295.3 4.2 convolution_convert_fusion.1
  299.5 2.7 convolution_add_fusion.2
  302.2 2.6 copy.172
  304.8 2.6 copy.173
  307.3 2.6 copy.177
  309.9 2.3 copy.178
  312.2 2.6 copy.179
  314.8 2.0 multiply_reduce_fusion
  317.0 1.4 subtract_add_fusion
  318.4 4.3 convolution_convert_fusion
  322.7 11.8 %concatenate.69 = bf16[8,128,2816]{2,1,0:T(8,128)(2,1)} reshape(bf16[2816,1024]{1,0:T(8,128)(2,1)} %convolution_convert_fusion) | data formatting | bytes 11534336 | tf_op jit(solution)/shard_map/concatenate | solution.py:363
  334.5 1.9 convolution_convert_fusion.3
  336.4 14.2 %pad_maximum_fusion = bf16[8,128,9472]{2,1,0:T(8,128)(2,1)} fusion(bf16[8,128,1024]{2,1,0:T(8,128)(2,1)S(1)} %convolution_convert_fusion.3, bf16[8,128,2816]{2,1,0:T(8,128)(2,1)} %concatenate.69, bf16[8,128,2816]{2,1,0:T(8,128)(2,1)} %convolution_convert_fusion.1, bf16[8,128,2816]{2,1,0:T(8,128)(2,1)} %convolution_convert_fusion.2), kind=kLoop, calls=%fused_computation | loop fusion | flops 77594624 | bytes 38797312 | tf_op jit(solution)/shard_map/concatenate | solution.py:363
  350.7 2.0 convolution_convert_fusion.7
  353.2 43.4 %shard_map.230 = (f32[256,1024]{1,0:T(8,128)S(1)}, bf16[2048,2048]{1,0:T(8,128)(2,1)}) custom-call(s32[2]{0:T(128)S(1)} %pad_add_fusion.meta_ref, bf16[256,1024]{1,0:T(8,128)(2,1)S(1)} %copy.166.q_ref, bf16[2048,2048]{1,0:T(8,128)(2,1)} %bitcast.24.k_ref.v_ref, bf16[2048,2048]{1,0:T(8,128)(2,1)} %bitcast.24.k_ref.v_ref, bf16[256,1024]{1,0:T(8,128)(2,1)S(1)} %copy.183.do_ref), custom_call_target="tpu_custom_call" | custom-call | flops 5368709120 | bytes 19398656 | tf_op jit(solution)/shard_map/pallas_call | solution.py:108
  396.5 35.4 %all-to-all-start.1 = ((bf16[8,256,2048]{2,1,0:T(8,128)(2,1)}), bf16[8,256,2048]{2,1,0:T(8,128)(2,1)}, u32[]{:S(2)}, u32[]{:S(2)}) async-start(bf16[8,256,2048]{2,1,0:T(8,128)(2,1)} %bitcast.226), calls=%async_computation.1 | async-start | bytes 16777216 | tf_op jit(solution)/shard_map/all_to_all | solution.py:385
  432.5 93.4 %all-to-all-done.1 = bf16[8,256,2048]{2,1,0:T(8,128)(2,1)} async-done(((bf16[8,256,2048]{2,1,0:T(8,128)(2,1)}), bf16[8,256,2048]{2,1,0:T(8,128)(2,1)}, u32[]{:S(2)}, u32[]{:S(2)}) %all-to-all-start.1) | async-done | bytes 8388640 | tf_op jit(solution)/shard_map/all_to_all | solution.py:385
  525.8 5.3 convert_reduce_fusion
  531.1 1.8 copy.185
  533.0 2.8 slice_multiply_fusion
  539.9 1.8 convolution_add_fusion
  541.7 1.6 copy.187
  544.4 1.6 copy.189
  547.0 1.8 convolution_convert_fusion.6
  550.3 3.3 fusion.1
  553.5 115.2 %all-reduce.4.cloned.1.call-done = bf16[2,64,9472]{2,1,0:T(8,128)(2,1)} async-done(((bf16[2,64,9472]{2,1,0:T(8,128)(2,1)}), bf16[2,64,9472]{2,1,0:T(8,128)(2,1)}) %all-reduce.4.cloned.1.call-update) | async-done | bytes 2424848 | tf_op jit(solution)/shard_map/psum | solution.py:437
  668.8 11.8 %reshape_reshape.19 = bf16[2816,1024]{1,0:T(8,128)(2,1)} reshape(bf16[16,64,2816]{2,1,0:T(8,128)(2,1)} %get-tuple-element.72) | data formatting | bytes 11534336 | tf_op jit(solution)/shard_map/reshape;reshape | solution.py:293
  680.6 34.3 %reduce-scatter.5.cloned.1.call-done = bf16[1,416,1024]{2,1,0:T(8,128)(2,1)} async-done(((bf16[8,416,1024]{2,1,0:T(8,128)(2,1)}), bf16[1,416,1024]{2,1,0:T(8,128)(2,1)}) %reduce-scatter.5.cloned.1.call-update) | async-done | bytes 851984 | tf_op jit(solution)/shard_map/reduce_scatter | solution.py:207
  716.0 3.0 collective-permute-start.2
  719.0 5.6 fusion.9
  724.6 3.7 collective-permute-done.2
  728.4 1.6 collective-permute-start.3
  730.0 2.5 copy.197
  732.5 1.3 fusion.16
  733.8 4.7 collective-permute-done.3
  738.7 3.1 collective-permute-start.4
  742.7 7.2 collective-permute-done.4
  752.7 5.9 collective-permute-done.5
  (154 shorter events, 34.8 us)
Async XLA Ops:
  7.2 75.9 %all-gather.5.cloned.1.call-start = ((), (), s32[]{:S(2)}) async-start(), calls=%async_computation.7 | async-start | bytes 10027008 | tf_op jit(solution)/shard_map/all_gather | solution.py:195
  11.7 16.8 %collective-permute-start = (bf16[272,1024]{1,0:T(8,128)(2,1)S(1)}, bf16[272,1024]{1,0:T(8,128)(2,1)S(1)}, u32[]{:S(2)}, u32[]{:S(2)}) collective-permute-start(bf16[272,1024]{1,0:T(8,128)(2,1)S(1)} %pad_dynamic-update-slice_fusion), channel_id=1, source_target_pairs={{0,68},{68,0},{4,64},{64,4},{1,69},{69,1},{5,65},{65,5},{2,70},{70... | collective-permute-start | bytes 1671176 | tf_op jit(solution)/shard_map/ppermute | solution.py:194
  15.9 13.9 %copy-start.23 = (bf16[176,1024]{1,0:T(8,128)(2,1)S(1)}, bf16[176,1024]{1,0:T(8,128)(2,1)}, u32[]{:S(2)}) copy-start(bf16[176,1024]{1,0:T(8,128)(2,1)} %param.22) | copy-start | bytes 1081348
  28.6 1.6 copy-start.24
  28.6 1.7 copy-start.25
  29.7 215.4 %all-gather.7.cloned.1.call-start = ((), (), s32[]{:S(2)}) async-start(), calls=%async_computation.8 | async-start | bytes 19464192 | tf_op jit(solution)/shard_map/all_gather | solution.py:195
  30.4 26.3 %collective-permute-start.1 = (bf16[64,8448]{1,0:T(8,128)(2,1)S(1)}, bf16[64,8448]{1,0:T(8,128)(2,1)S(1)}, u32[]{:S(2)}, u32[]{:S(2)}) collective-permute-start(bf16[64,8448]{1,0:T(8,128)(2,1)S(1)} %constant_dynamic-update-slice_fusion.4), channel_id=1, source_target_pairs={{0,68},{68,0},{4,64},{64,4},{1,69},{69,1},{5,65},{65,5},{2,70},{70... | collective-permute-start | bytes 3244040 | tf_op jit(solution)/shard_map/ppermute | solution.py:194
  56.8 1.7 copy-start.7
  84.6 19.8 %copy-start.9 = (bf16[1,256,8,2,64]{1,4,3,2,0:T(8,128)(2,1)}, bf16[1,256,8,2,64]{1,4,3,2,0:T(8,128)(2,1)S(1)}, u32[]{:S(2)}) copy-start(bf16[1,256,8,2,64]{1,4,3,2,0:T(8,128)(2,1)S(1)} %copy.160) | copy-start | bytes 1572868
  98.6 2.8 copy-start.17
  104.3 2.5 copy-start.20
  111.3 5.9 copy-start.26
  111.3 5.9 copy-start.27
  111.3 8.2 %copy-start.19 = (bf16[1,256,16,64]{1,3,2,0:T(8,128)(2,1)S(1)}, bf16[1,256,16,64]{1,3,2,0:T(8,128)(2,1)}, u32[]{:S(2)}) copy-start(bf16[1,256,16,64]{1,3,2,0:T(8,128)(2,1)} %get-tuple-element.118) | copy-start | bytes 1572868
  111.3 100.2 %all-to-all-start = ((bf16[8,256,2048]{2,1,0:T(8,128)(2,1)}), bf16[8,256,2048]{2,1,0:T(8,128)(2,1)}, u32[]{:S(2)}, u32[]{:S(2)}) async-start(bf16[8,256,2048]{2,1,0:T(8,128)(2,1)} %broadcast_in_dim.72), calls=%async_computation | async-start | bytes 16777216 | tf_op jit(solution)/shard_map/all_to_all | solution.py:313
  116.7 429.6 %reduce-scatter.3.cloned.1.call-start = ((), (), s32[]{:S(2)}) async-start(), calls=%async_computation.4 | async-start | bytes 21823488 | tf_op jit(solution)/shard_map/reduce_scatter | solution.py:207
  238.0 4.0 copy-start.13
  240.1 1.0 copy-start.3
  278.0 4.5 copy-start.16
  278.0 11.5 %slice-start.2 = ((s8[5767168]{0:T(1024)(128)(4,1)}), s8[4194304]{0:T(1024)(128)(4,1)S(1)}, s32[]{:S(2)}) async-start(s8[5767168]{0:T(1024)(128)(4,1)} %bitcast.230), calls=%async_computation.11 | async-start | bytes 8388608
  282.5 7.0 slice-start.3
  291.2 8.3 %slice-start = ((s8[5767168]{0:T(1024)(128)(4,1)}), s8[4194304]{0:T(1024)(128)(4,1)S(1)}, s32[]{:S(2)}) async-start(s8[5767168]{0:T(1024)(128)(4,1)} %bitcast.201), calls=%async_computation.9 | async-start | bytes 8388608
  295.3 4.2 slice-start.1
  312.2 4.6 copy-start.18
  314.8 2.0 copy-start.4
  314.8 2.2 copy-start.11
  314.8 3.6 copy-start.12
  322.7 11.8 %copy-start.14 = (bf16[1,256,8,2,64]{1,4,3,2,0:T(8,128)(2,1)S(1)}, bf16[1,256,8,2,64]{1,4,3,2,0:T(8,128)(2,1)}, u32[]{:S(2)}) copy-start(bf16[1,256,8,2,64]{1,4,3,2,0:T(8,128)(2,1)} %copy-done.13) | copy-start | bytes 1572868
  396.5 129.3 %all-to-all-start.1 = ((bf16[8,256,2048]{2,1,0:T(8,128)(2,1)}), bf16[8,256,2048]{2,1,0:T(8,128)(2,1)}, u32[]{:S(2)}, u32[]{:S(2)}) async-start(bf16[8,256,2048]{2,1,0:T(8,128)(2,1)} %bitcast.226), calls=%async_computation.1 | async-start | bytes 16777216 | tf_op jit(solution)/shard_map/all_to_all | solution.py:385
  432.0 236.8 %all-reduce.4.cloned.1.call-start = ((), (), s32[]{:S(2)}) async-start(), calls=%async_computation.5 | async-start | bytes 4849664 | tf_op jit(solution)/shard_map/psum | solution.py:437
  535.7 1.8 copy-start.2
  536.1 2.2 copy-start.1
  536.2 2.9 copy-start.15
  538.3 1.6 copy-start
  543.2 2.7 copy-start.8
  545.9 1.0 copy-start.10
  546.4 168.6 %reduce-scatter.5.cloned.1.call-start = ((), (), s32[]{:S(2)}) async-start(), calls=%async_computation.6 | async-start | bytes 7667712 | tf_op jit(solution)/shard_map/reduce_scatter | solution.py:207
  668.8 50.2 %copy-start.5 = (f32[1,256,1024]{2,1,0:T(8,128)S(1)}, f32[1,256,1024]{2,1,0:T(8,128)}, u32[]{:S(2)}) copy-start(f32[1,256,1024]{2,1,0:T(8,128)} %copy-done.3) | copy-start | bytes 3145732
  716.0 12.3 %copy-start.21 = (bf16[1,416,1024]{2,1,0:T(8,128)(2,1)S(1)}, bf16[1,416,1024]{2,1,0:T(8,128)(2,1)}, u32[]{:S(2)}) copy-start(bf16[1,416,1024]{2,1,0:T(8,128)(2,1)} %reduce-scatter.5.cloned.1.call-done) | copy-start | bytes 2555908
  716.0 12.3 %collective-permute-start.2 = (bf16[208,1024]{1,0:T(8,128)(2,1)S(1)}, bf16[208,1024]{1,0:T(8,128)(2,1)S(1)}, u32[]{:S(2)}, u32[]{:S(2)}) collective-permute-start(bf16[208,1024]{1,0:T(8,128)(2,1)S(1)} %dynamic-slice_bitcast_fusion), channel_id=1, source_target_pairs={{0,68},{68,0},{4,64},{64,4},{1,69},{69,1},{5,65},{65,5},{2,70},{70... | collective-permute-start | bytes 1277960 | tf_op jit(solution)/shard_map/ppermute | solution.py:217
  724.6 7.9 %copy-start.6 = (f32[1,256,1024]{2,1,0:T(8,128)S(1)}, f32[1,256,1024]{2,1,0:T(8,128)}, u32[]{:S(2)}) copy-start(f32[1,256,1024]{2,1,0:T(8,128)} %subtract_add_fusion) | copy-start | bytes 3145732
  728.4 10.1 %collective-permute-start.3 = (bf16[208,1024]{1,0:T(8,128)(2,1)S(1)}, bf16[208,1024]{1,0:T(8,128)(2,1)S(1)}, u32[]{:S(2)}, u32[]{:S(2)}) collective-permute-start(bf16[208,1024]{1,0:T(8,128)(2,1)S(1)} %fusion.22), channel_id=1, source_target_pairs={{0,1},{1,0},{2,3},{3,2},{4,5},{5,4},{6,7},{7,6},{8,9},{9,8},{10,11... | collective-permute-start | bytes 1277960 | tf_op jit(solution)/shard_map/ppermute | solution.py:225
  732.5 9.3 %copy-start.22 = (bf16[2,64,9472]{2,1,0:T(8,128)(2,1)S(1)}, bf16[2,64,9472]{2,1,0:T(8,128)(2,1)}, u32[]{:S(2)}) copy-start(bf16[2,64,9472]{2,1,0:T(8,128)(2,1)} %all-reduce.4.cloned.1.call-done) | copy-start | bytes 7274500
  738.7 11.1 %collective-permute-start.4 = (bf16[208,1024]{1,0:T(8,128)(2,1)S(1)}, bf16[208,1024]{1,0:T(8,128)(2,1)S(1)}, u32[]{:S(2)}, u32[]{:S(2)}) collective-permute-start(bf16[208,1024]{1,0:T(8,128)(2,1)S(1)} %add_convert_fusion.2), channel_id=1, source_target_pairs={{0,2},{1,3},{2,0},{3,1},{4,6},{5,7},{6,4},{7,5},{8,10},{9,11},{10,... | collective-permute-start | bytes 1277960 | tf_op jit(solution)/shard_map/ppermute | solution.py:225
  750.0 8.7 %collective-permute-start.5 = (bf16[208,1024]{1,0:T(8,128)(2,1)S(1)}, bf16[208,1024]{1,0:T(8,128)(2,1)S(1)}, u32[]{:S(2)}, u32[]{:S(2)}) collective-permute-start(bf16[208,1024]{1,0:T(8,128)(2,1)S(1)} %add_convert_fusion.1), channel_id=1, source_target_pairs={{0,4},{1,5},{2,6},{3,7},{4,0},{5,1},{6,2},{7,3},{8,12},{9,13},{10,... | collective-permute-start | bytes 1277960 | tf_op jit(solution)/shard_map/ppermute | solution.py:225
Sparse Core Ops, SparseCore 0:
  29.9 53.2 all-gather.4
  84.8 87.3 all-gather.6
  350.8 135.4 reduce-scatter.2
  546.5 122.2 all-reduce.3
  671.0 43.8 reduce-scatter.4

commit v12 on v10

--- a/solution.py
+++ b/solution.py
@@ -360,11 +360,14 @@
     middle_low = middle_back.astype(jnp.bfloat16)
     out_total = jnp.einsum("srd,sre->de", mixed_low_g, middle_low, preferred_element_type=jnp.float32)
 
+    down_share = ctx_allreduce(
+        z_combine(yc_reduce_scatter(down_total.astype(jnp.bfloat16).reshape(n_fsdp, d_rows, width))),
+        n_ctx,
+    )
     mlp_grads = jnp.concatenate(
         [
             gate_total.reshape(n_fsdp, w_rows, ff),
             upper_total.reshape(n_fsdp, w_rows, ff),
-            down_total.reshape(n_fsdp, d_rows, width).reshape(n_fsdp, w_rows, ff),
             out_total.reshape(n_fsdp, w_rows, width),
         ],
         axis=2,
@@ -447,8 +450,8 @@
     midnorm_grad = attn_share[3 * w_rows, g_len:2 * g_len]
     gate_grad = mlp_share[:, 0:ff]
     up_grad = mlp_share[:, ff:2 * ff]
-    down_grad = mlp_share[:, 2 * ff:3 * ff].reshape(d_rows, width)
-    out_grad = mlp_share[:, 3 * ff:]
+    down_grad = down_share
+    out_grad = mlp_share[:, 2 * ff:]
     return (
         layer_out,
         tokens_grad,

time: 730 us -> 691 us (0.947)
  waiting for transfers between devices: 327 us -> 294 us
  local copies, waits for them, and re-layouts: 116 us -> 105 us
    ppermute x6 -> x9, waiting for transfers between devices: 53 us -> 39.6 us  [ctx_allreduce(): other = lax.ppermute(total, CTX, [(j, j ^ step) for j in range(n_ctx)])]
    concatenate x1 -> x0, local copies, waits for them, and re-layouts: 11.8 us -> none  [body(): jnp.concatenate([gate_total.reshape(n_fsdp, w_rows, ff), upper_total.resh...]
    ppermute x2 -> x3, waiting for transfers between devices: 28.6 us -> 19 us  [z_combine(): got = lax.ppermute(theirs, ('zh', 'zl'), Z_CROSS)]
    all_to_all x1, waiting for transfers between devices: 93.4 us -> 84.8 us  [body(): lax.all_to_all(kv_back.reshape(n_ctx, rows, 2 * width), CTX, 0, 0, tiled=...]
    ppermute x6 -> x9, starting transfers between devices: 36.8 us -> 40.6 us  [ctx_allreduce(): other = lax.ppermute(total, CTX, [(j, j ^ step) for j in range(n_ctx)])]
  transfers between devices with their start and end apart: 16 -> 21, of which waited for: 13 -> 12; matrix products, arithmetic and copies ran while one was open for 15% -> 17% of each run, Pallas kernels for 9% -> 10%
where the time goes in v12:
time: 691 us; the launch traced here: 683 us
  waiting for transfers between devices  294 us (43%)
  local copies, waits for them, and re-layouts  105 us (15%)
  starting transfers between devices  96.5 us (14%)
  Pallas kernels  67.7 us (10%)
  matrix products  55.3 us (8%)
  other arithmetic  49.4 us (7%)
  between operations  15.2 us (2%)
    all_to_all x1, waiting for transfers between devices, body(): lax.all_to_all(jnp.broadcast_to(kv_own[None], (n_ctx, rows, 2 * width)),...  91.9 us
    all_to_all x1, waiting for transfers between devices, body(): lax.all_to_all(kv_back.reshape(n_ctx, rows, 2 * width), CTX, 0, 0, tiled=...  84.8 us
    pallas_call x1, Pallas kernels, attention_backward(): pl.pallas_call(functools.partial(attn_bwd_kernel, head_dim, scale), out_s...  43.4 us
    ppermute x9, starting transfers between devices, ctx_allreduce(): other = lax.ppermute(total, CTX, [(j, j ^ step) for j in range(n_ctx)])  40.6 us
    ppermute x9, waiting for transfers between devices, ctx_allreduce(): other = lax.ppermute(total, CTX, [(j, j ^ step) for j in range(n_ctx)])  39.6 us
    ppermute x2, waiting for transfers between devices, fsdp_gather(): other = lax.ppermute(pack, ('zh', 'zl'), Z_CROSS)  35.9 us
    all_to_all x1, starting transfers between devices, body(): lax.all_to_all(kv_back.reshape(n_ctx, rows, 2 * width), CTX, 0, 0, tiled=...  35.7 us
    pallas_call x1, Pallas kernels, attention_forward(): pl.pallas_call(functools.partial(attn_fwd_kernel, head_dim, scale), out_s...  24.4 us
  transfers between devices with their start and end apart: 21, of which 12 were waited for; matrix products, arithmetic and copies ran while one was open for 17% of the time, Pallas kernels for 10%

profile of v12, /device:TPU:0, one launch (start us, length us, event | category | flops | bytes accessed | tf_op | source)
XLA Modules:
  0.0 682.9 jit_solution(12046516725057412327)
XLA Ops:
  12.2 4.2 collective-permute-start
  16.4 12.6 %collective-permute-done = bf16[272,1024]{1,0:T(8,128)(2,1)S(1)} collective-permute-done((bf16[272,1024]{1,0:T(8,128)(2,1)S(1)}, bf16[272,1024]{1,0:T(8,128)(2,1)S(1)}, u32[]{:S(2)}, u32[]{:S(2)}) %collective-permute-start) | collective-permute-done | bytes 557088 | tf_op jit(solution)/shard_map/ppermute | solution.py:194
  30.9 3.1 collective-permute-start.1
  33.9 23.3 %collective-permute-done.1 = bf16[64,8448]{1,0:T(8,128)(2,1)S(1)} collective-permute-done((bf16[64,8448]{1,0:T(8,128)(2,1)S(1)}, bf16[64,8448]{1,0:T(8,128)(2,1)S(1)}, u32[]{:S(2)}, u32[]{:S(2)}) %collective-permute-start.1) | collective-permute-done | bytes 1081376 | tf_op jit(solution)/shard_map/ppermute | solution.py:194
  61.0 22.7 %all-gather.5.cloned.1.call-done = bf16[16,272,1024]{2,1,0:T(8,128)(2,1)} async-done(((bf16[2,272,1024]{2,1,0:T(8,128)(2,1)}), bf16[16,272,1024]{2,1,0:T(8,128)(2,1)}) %all-gather.5.cloned.1.call-update) | async-done | bytes 8912912 | tf_op jit(solution)/shard_map/all_gather | solution.py:195
  85.1 6.0 fusion.43
  91.1 3.9 copy.163
  95.0 4.1 copy.161
  99.1 2.8 convolution_bitcast_fusion.3
  105.0 2.5 fusion.9
  107.5 4.3 broadcast_in_dim.72
  111.8 5.3 all-to-all-start
  120.2 91.9 %all-to-all-done = bf16[8,256,2048]{2,1,0:T(8,128)(2,1)} async-done(((bf16[8,256,2048]{2,1,0:T(8,128)(2,1)}), bf16[8,256,2048]{2,1,0:T(8,128)(2,1)}, u32[]{:S(2)}, u32[]{:S(2)}) %all-to-all-start) | async-done | bytes 8388640 | tf_op jit(solution)/shard_map/all_to_all | solution.py:313
  212.1 24.4 %shard_map.229 = bf16[256,1024]{1,0:T(8,128)(2,1)S(1)} custom-call(s32[2]{0:T(128)S(1)} %pad_add_fusion.meta_ref, bf16[256,1024]{1,0:T(8,128)(2,1)S(1)} %copy.166.q_ref, bf16[2048,2048]{1,0:T(8,128)(2,1)} %bitcast.24.k_ref.v_ref, bf16[2048,2048]{1,0:T(8,128)(2,1)} %bitcast.24.k_ref.v_ref), custom_call_target="tpu_custom_call" | custom-call | flops 2147483648 | bytes 9437184 | tf_op jit(solution)/shard_map/pallas_call | solution.py:80
  238.6 2.1 multiply_reduce_fusion.2
  243.9 11.3 %fusion.42 = (bf16[16,64,2816]{2,1,0:T(8,128)(2,1)}, bf16[16,64,2816]{2,1,0:T(8,128)(2,1)}, bf16[16,64,2816]{2,1,0:T(8,128)(2,1)}) fusion(bf16[16,64,8448]{2,1,0:T(8,128)(2,1)} %all-gather.7.cloned.1.call-done), kind=kLoop, calls=%fused_computation.137 | loop fusion | bytes 34603008 | tf_op jit(solution)/shard_map/slice | solution.py:293
  255.2 11.7 %dot_general.113 = bf16[8,2,176,1024]{3,2,1,0:T(8,128)(2,1)} reshape(bf16[16,64,2816]{2,1,0:T(8,128)(2,1)} %get-tuple-element.72) | data formatting | bytes 11534336 | tf_op jit(solution)/shard_map/sre,fe->srf/dot_general | solution.py:338
  266.9 4.6 convolution_bitcast_fusion
  271.6 1.9 copy.174
  273.4 3.4 copy.175
  276.8 4.5 fusion.47
  281.3 7.0 %multiply_convert_fusion = (bf16[256,2816]{1,0:T(8,128)(2,1)S(1)}, bf16[256,2816]{1,0:T(8,128)(2,1)S(1)}, bf16[256,2816]{1,0:T(8,128)(2,1)}) fusion(f32[256,2816]{1,0:T(8,128)S(1)} %copy-done.21, f32[256,2816]{1,0:T(8,128)S(1)} %fusion.47, bf16[256,1024]{0,1:T(8,128)(2,1)S(1)} %bitcast.231, bf16[1024,2816]{1,0:T(8,128)(2,1)} %bitcast.239), kind=kOutput, calls=%fused_computation.8 | convolution fusion | flops 1487929344 | bytes 16384000 | tf_op jit(solution)/shard_map/dot_general | solution.py:327
  288.3 1.7 fusion.48
  290.0 4.1 convolution_convert_fusion.2
  294.2 4.1 convolution_convert_fusion.1
  298.3 2.7 convolution_add_fusion.2
  300.9 2.5 copy.177
  303.5 2.3 copy.178
  305.8 2.5 copy.179
  308.3 2.0 multiply_reduce_fusion
  313.7 11.0 %pad_maximum_fusion = bf16[8,128,6656]{2,1,0:T(8,128)(2,1)} fusion(bf16[8,128,1024]{2,1,0:T(8,128)(2,1)S(1)} %convolution_convert_fusion.3, bf16[8,128,2816]{2,1,0:T(8,128)(2,1)} %convolution_convert_fusion.1, bf16[8,128,2816]{2,1,0:T(8,128)(2,1)} %convolution_convert_fusion.2), kind=kLoop, calls=%fused_computation.2 | loop fusion | flops 40894464 | bytes 27262976 | tf_op jit(solution)/shard_map/concatenate | solution.py:367
  324.7 2.0 convolution_convert_fusion.7
  327.2 43.4 %shard_map.230 = (f32[256,1024]{1,0:T(8,128)S(1)}, bf16[2048,2048]{1,0:T(8,128)(2,1)}) custom-call(s32[2]{0:T(128)S(1)} %pad_add_fusion.meta_ref, bf16[256,1024]{1,0:T(8,128)(2,1)S(1)} %copy.166.q_ref, bf16[2048,2048]{1,0:T(8,128)(2,1)} %bitcast.24.k_ref.v_ref, bf16[2048,2048]{1,0:T(8,128)(2,1)} %bitcast.24.k_ref.v_ref, bf16[256,1024]{1,0:T(8,128)(2,1)S(1)} %copy.183.do_ref), custom_call_target="tpu_custom_call" | custom-call | flops 5368709120 | bytes 19398656 | tf_op jit(solution)/shard_map/pallas_call | solution.py:108
  370.6 35.7 %all-to-all-start.1 = ((bf16[8,256,2048]{2,1,0:T(8,128)(2,1)}), bf16[8,256,2048]{2,1,0:T(8,128)(2,1)}, u32[]{:S(2)}, u32[]{:S(2)}) async-start(bf16[8,256,2048]{2,1,0:T(8,128)(2,1)} %bitcast.236), calls=%async_computation.1 | async-start | bytes 16777216 | tf_op jit(solution)/shard_map/all_to_all | solution.py:388
  406.4 1.6 copy.172
  407.9 1.6 copy.173
  409.5 4.2 convolution_convert_fusion
  415.2 84.8 %all-to-all-done.1 = bf16[8,256,2048]{2,1,0:T(8,128)(2,1)} async-done(((bf16[8,256,2048]{2,1,0:T(8,128)(2,1)}), bf16[8,256,2048]{2,1,0:T(8,128)(2,1)}, u32[]{:S(2)}, u32[]{:S(2)}) %all-to-all-start.1) | async-done | bytes 8388640 | tf_op jit(solution)/shard_map/all_to_all | solution.py:388
  500.0 5.3 convert_reduce_fusion
  505.4 2.1 copy.185
  507.5 2.8 slice_multiply_fusion
  510.8 1.7 copy-done.2
  514.8 1.7 convolution_add_fusion
  519.2 1.6 copy.189
  523.3 1.8 convolution_convert_fusion.6
  526.9 3.3 fusion.1
  530.2 2.2 dynamic-slice_bitcast_fusion
  532.4 2.9 collective-permute-start.6
  536.8 19.0 %collective-permute-done.6 = bf16[64,6656]{1,0:T(8,128)(2,1)} collective-permute-done((bf16[64,6656]{1,0:T(8,128)(2,1)}, bf16[64,6656]{1,0:T(8,128)(2,1)}, u32[]{:S(2)}, u32[]{:S(2)}) %collective-permute-start.6) | collective-permute-done | bytes 852000 | tf_op jit(solution)/shard_map/ppermute | solution.py:217
  555.7 2.6 fusion.2
  558.3 29.6 %collective-permute-start.7 = (bf16[64,6656]{1,0:T(8,128)(2,1)}, bf16[64,6656]{1,0:T(8,128)(2,1)}, u32[]{:S(2)}, u32[]{:S(2)}) collective-permute-start(bf16[64,6656]{1,0:T(8,128)(2,1)} %fusion.2), channel_id=1, source_target_pairs={{0,1},{1,0},{2,3},{3,2},{4,5},{5,4},{6,7},{7,6},{8,9},{9,8},{10,11... | collective-permute-start | bytes 2555912 | tf_op jit(solution)/shard_map/ppermute | solution.py:225
  588.0 2.5 collective-permute-start.11
  590.5 11.8 %reshape_reshape.21 = bf16[2816,1024]{1,0:T(8,128)(2,1)} reshape(bf16[16,64,2816]{2,1,0:T(8,128)(2,1)} %get-tuple-element.72) | data formatting | bytes 11534336 | tf_op jit(solution)/shard_map/reshape;reshape | solution.py:293
  602.3 7.6 %collective-permute-done.11 = bf16[176,1024]{1,0:T(8,128)(2,1)} collective-permute-done((bf16[176,1024]{1,0:T(8,128)(2,1)S(1)}, bf16[176,1024]{1,0:T(8,128)(2,1)}, u32[]{:S(2)}, u32[]{:S(2)}) %collective-permute-start.11) | collective-permute-done | bytes 360480 | tf_op jit(solution)/shard_map/ppermute | solution.py:225
  611.1 7.0 %collective-permute-start.12 = (bf16[176,1024]{1,0:T(8,128)(2,1)S(1)}, bf16[176,1024]{1,0:T(8,128)(2,1)}, u32[]{:S(2)}, u32[]{:S(2)}) collective-permute-start(bf16[176,1024]{1,0:T(8,128)(2,1)S(1)} %add_convert_fusion.8), channel_id=1, source_target_pairs={{0,2},{1,3},{2,0},{3,1},{4,6},{5,7},{6,4},{7,5},{8,10},{9,11},{10,... | collective-permute-start | bytes 1081352 | tf_op jit(solution)/shard_map/ppermute | solution.py:225
  618.1 2.6 add_convert_fusion.2
  620.7 5.1 fusion.10
  625.8 2.5 copy.197
  630.8 3.6 collective-permute-start.2
  634.3 8.8 %collective-permute-done.8 = bf16[64,6656]{1,0:T(8,128)(2,1)} collective-permute-done((bf16[64,6656]{1,0:T(8,128)(2,1)}, bf16[64,6656]{1,0:T(8,128)(2,1)}, u32[]{:S(2)}, u32[]{:S(2)}) %collective-permute-start.8) | collective-permute-done | bytes 852000 | tf_op jit(solution)/shard_map/ppermute | solution.py:225
  643.2 1.6 add_convert_fusion.1
  647.5 8.6 %collective-permute-done.3 = bf16[208,1024]{1,0:T(8,128)(2,1)S(1)} collective-permute-done((bf16[208,1024]{1,0:T(8,128)(2,1)S(1)}, bf16[208,1024]{1,0:T(8,128)(2,1)S(1)}, u32[]{:S(2)}, u32[]{:S(2)}) %collective-permute-start.3) | collective-permute-done | bytes 426016 | tf_op jit(solution)/shard_map/ppermute | solution.py:225
  658.4 7.5 %collective-permute-done.4 = bf16[208,1024]{1,0:T(8,128)(2,1)S(1)} collective-permute-done((bf16[208,1024]{1,0:T(8,128)(2,1)S(1)}, bf16[208,1024]{1,0:T(8,128)(2,1)S(1)}, u32[]{:S(2)}, u32[]{:S(2)}) %collective-permute-start.4) | collective-permute-done | bytes 426016 | tf_op jit(solution)/shard_map/ppermute | solution.py:225
  667.3 6.9 %collective-permute-done.5 = bf16[208,1024]{1,0:T(8,128)(2,1)S(1)} collective-permute-done((bf16[208,1024]{1,0:T(8,128)(2,1)S(1)}, bf16[208,1024]{1,0:T(8,128)(2,1)S(1)}, u32[]{:S(2)}, u32[]{:S(2)}) %collective-permute-start.5) | collective-permute-done | bytes 426016 | tf_op jit(solution)/shard_map/ppermute | solution.py:225
  (205 shorter events, 51.5 us)
Async XLA Ops:
  7.2 76.5 %all-gather.5.cloned.1.call-start = ((), (), s32[]{:S(2)}) async-start(), calls=%async_computation.8 | async-start | bytes 10027008 | tf_op jit(solution)/shard_map/all_gather | solution.py:195
  12.2 16.8 %collective-permute-start = (bf16[272,1024]{1,0:T(8,128)(2,1)S(1)}, bf16[272,1024]{1,0:T(8,128)(2,1)S(1)}, u32[]{:S(2)}, u32[]{:S(2)}) collective-permute-start(bf16[272,1024]{1,0:T(8,128)(2,1)S(1)} %pad_dynamic-update-slice_fusion), channel_id=1, source_target_pairs={{0,68},{68,0},{4,64},{64,4},{1,69},{69,1},{5,65},{65,5},{2,70},{70... | collective-permute-start | bytes 1671176 | tf_op jit(solution)/shard_map/ppermute | solution.py:194
  29.1 1.2 copy-start.30
  29.1 1.7 copy-start.31
  29.1 1.7 copy-start.32
  30.3 213.6 %all-gather.7.cloned.1.call-start = ((), (), s32[]{:S(2)}) async-start(), calls=%async_computation.9 | async-start | bytes 19464192 | tf_op jit(solution)/shard_map/all_gather | solution.py:195
  30.9 26.3 %collective-permute-start.1 = (bf16[64,8448]{1,0:T(8,128)(2,1)S(1)}, bf16[64,8448]{1,0:T(8,128)(2,1)S(1)}, u32[]{:S(2)}, u32[]{:S(2)}) collective-permute-start(bf16[64,8448]{1,0:T(8,128)(2,1)S(1)} %constant_dynamic-update-slice_fusion.4), channel_id=1, source_target_pairs={{0,68},{68,0},{4,64},{64,4},{1,69},{69,1},{5,65},{65,5},{2,70},{70... | collective-permute-start | bytes 3244040 | tf_op jit(solution)/shard_map/ppermute | solution.py:194
  58.9 1.1 copy-start.8
  61.0 41.8 %copy-start.33 = (f32[256,32]{0,1:T(8,128)}, f32[256,32]{0,1:T(8,128)S(1)}, u32[]{:S(2)}) copy-start(f32[256,32]{0,1:T(8,128)S(1)} %get-tuple-element.114) | copy-start | bytes 98308
  85.1 19.9 %copy-start.10 = (bf16[1,256,8,2,64]{1,4,3,2,0:T(8,128)(2,1)}, bf16[1,256,8,2,64]{1,4,3,2,0:T(8,128)(2,1)S(1)}, u32[]{:S(2)}) copy-start(bf16[1,256,8,2,64]{1,4,3,2,0:T(8,128)(2,1)S(1)} %copy.160) | copy-start | bytes 1572868
  99.1 2.8 copy-start.22
  105.0 2.5 copy-start.25
  111.8 5.9 copy-start.40
  111.8 5.9 copy-start.41
  111.8 8.2 %copy-start.24 = (bf16[1,256,16,64]{1,3,2,0:T(8,128)(2,1)S(1)}, bf16[1,256,16,64]{1,3,2,0:T(8,128)(2,1)}, u32[]{:S(2)}) copy-start(bf16[1,256,16,64]{1,3,2,0:T(8,128)(2,1)} %get-tuple-element.117) | copy-start | bytes 1572868
  111.8 100.3 %all-to-all-start = ((bf16[8,256,2048]{2,1,0:T(8,128)(2,1)}), bf16[8,256,2048]{2,1,0:T(8,128)(2,1)}, u32[]{:S(2)}, u32[]{:S(2)}) async-start(bf16[8,256,2048]{2,1,0:T(8,128)(2,1)} %broadcast_in_dim.72), calls=%async_computation | async-start | bytes 16777216 | tf_op jit(solution)/shard_map/all_to_all | solution.py:313
  117.1 413.0 %reduce-scatter.4.cloned.1.call-start = ((), (), s32[]{:S(2)}) async-start(), calls=%async_computation.5 | async-start | bytes 15335424 | tf_op jit(solution)/shard_map/reduce_scatter | solution.py:207
  119.2 191.2 %copy-start.37 = (pred[256]{0:T(512)(128)(4,1)}, pred[256]{0:T(512)(128)(4,1)S(1)}, u32[]{:S(2)}) copy-start(pred[256]{0:T(512)(128)(4,1)S(1)} %fusion.38) | copy-start | bytes 772
  238.5 2.1 copy-start.13
  276.8 4.5 copy-start.21
  276.8 11.5 %slice-start.2 = ((s8[5767168]{0:T(1024)(128)(4,1)}), s8[4194304]{0:T(1024)(128)(4,1)S(1)}, s32[]{:S(2)}) async-start(s8[5767168]{0:T(1024)(128)(4,1)} %bitcast.240), calls=%async_computation.12 | async-start | bytes 8388608
  281.3 7.0 %slice-start.3 = ((s8[5767168]{0:T(1024)(128)(4,1)}), s8[1572864]{0:T(1024)(128)(4,1)S(1)}, s32[]{:S(2)}) async-start(s8[5767168]{0:T(1024)(128)(4,1)} %bitcast.240), calls=%async_computation.13 | async-start | bytes 3145728
  290.0 8.3 %slice-start = ((s8[5767168]{0:T(1024)(128)(4,1)}), s8[4194304]{0:T(1024)(128)(4,1)S(1)}, s32[]{:S(2)}) async-start(s8[5767168]{0:T(1024)(128)(4,1)} %bitcast.210), calls=%async_computation.10 | async-start | bytes 8388608
  294.2 4.1 slice-start.1
  308.3 2.0 copy-start.4
  308.3 2.2 copy-start.12
  310.3 2.7 copy-start.14
  370.6 35.8 %copy-start.26 = (bf16[256,2816]{1,0:T(8,128)(2,1)S(1)}, bf16[256,2816]{1,0:T(8,128)(2,1)}, u32[]{:S(2)}) copy-start(bf16[256,2816]{1,0:T(8,128)(2,1)} %get-tuple-element.83) | copy-start | bytes 4325380
  370.6 129.5 %all-to-all-start.1 = ((bf16[8,256,2048]{2,1,0:T(8,128)(2,1)}), bf16[8,256,2048]{2,1,0:T(8,128)(2,1)}, u32[]{:S(2)}, u32[]{:S(2)}) async-start(bf16[8,256,2048]{2,1,0:T(8,128)(2,1)} %bitcast.236), calls=%async_computation.1 | async-start | bytes 16777216 | tf_op jit(solution)/shard_map/all_to_all | solution.py:388
  406.3 128.9 %reduce-scatter.8.cloned.1.call-start = ((), (), s32[]{:S(2)}) async-start(), calls=%async_computation.7 | async-start | bytes 6488064 | tf_op jit(solution)/shard_map/reduce_scatter | solution.py:207
  407.9 1.6 copy-start.23
  407.9 1.6 copy-start.38
  413.8 215.8 %reduce-scatter.6.cloned.1.call-start = ((), (), s32[]{:S(2)}) async-start(), calls=%async_computation.6 | async-start | bytes 7667712 | tf_op jit(solution)/shard_map/reduce_scatter | solution.py:207
  507.5 2.8 copy-start.20
  507.5 2.8 copy-start.34
  507.5 2.8 copy-start.35
  510.3 3.7 copy-start.15
  510.3 2.2 copy-start.2
  510.7 2.5 copy-start.17
  510.7 3.2 copy-start.19
  510.8 2.4 copy-start.1
  513.2 1.6 copy-start
  518.1 2.7 copy-start.9
  519.1 4.2 copy-start.11
  522.4 2.7 copy-start.18
  532.4 23.4 %collective-permute-start.6 = (bf16[64,6656]{1,0:T(8,128)(2,1)}, bf16[64,6656]{1,0:T(8,128)(2,1)}, u32[]{:S(2)}, u32[]{:S(2)}) collective-permute-start(bf16[64,6656]{1,0:T(8,128)(2,1)} %dynamic-slice_bitcast_fusion), channel_id=1, source_target_pairs={{0,68},{68,0},{4,64},{64,4},{1,69},{69,1},{5,65},{65,5},{2,70},{70... | collective-permute-start | bytes 2555912 | tf_op jit(solution)/shard_map/ppermute | solution.py:217
  535.2 52.6 %copy-start.29 = (bf16[1,352,1024]{2,1,0:T(8,128)(2,1)S(1)}, bf16[1,352,1024]{2,1,0:T(8,128)(2,1)}, u32[]{:S(2)}) copy-start(bf16[1,352,1024]{2,1,0:T(8,128)(2,1)} %reduce-scatter.8.cloned.1.call-done) | copy-start | bytes 2162692
  536.3 51.5 %collective-permute-start.10 = (bf16[176,1024]{1,0:T(8,128)(2,1)S(1)}, bf16[176,1024]{1,0:T(8,128)(2,1)S(1)}, u32[]{:S(2)}, u32[]{:S(2)}) collective-permute-start(bf16[176,1024]{1,0:T(8,128)(2,1)S(1)} %dynamic-slice_bitcast_fusion.2), channel_id=1, source_target_pairs={{0,68},{68,0},{4,64},{64,4},{1,69},{69,1},{5,65},{65,5},{2,70},{70... | collective-permute-start | bytes 1081352 | tf_op jit(solution)/shard_map/ppermute | solution.py:217
  558.3 59.8 %collective-permute-start.7 = (bf16[64,6656]{1,0:T(8,128)(2,1)}, bf16[64,6656]{1,0:T(8,128)(2,1)}, u32[]{:S(2)}, u32[]{:S(2)}) collective-permute-start(bf16[64,6656]{1,0:T(8,128)(2,1)} %fusion.2), channel_id=1, source_target_pairs={{0,1},{1,0},{2,3},{3,2},{4,5},{5,4},{6,7},{7,6},{8,9},{9,8},{10,11... | collective-permute-start | bytes 2555912 | tf_op jit(solution)/shard_map/ppermute | solution.py:225
  588.0 14.3 %copy-start.27 = (bf16[176,1024]{1,0:T(8,128)(2,1)}, bf16[176,1024]{1,0:T(8,128)(2,1)S(1)}, u32[]{:S(2)}) copy-start(bf16[176,1024]{1,0:T(8,128)(2,1)S(1)} %fusion.25) | copy-start | bytes 1081348
  588.0 21.9 %collective-permute-start.11 = (bf16[176,1024]{1,0:T(8,128)(2,1)S(1)}, bf16[176,1024]{1,0:T(8,128)(2,1)}, u32[]{:S(2)}, u32[]{:S(2)}) collective-permute-start(bf16[176,1024]{1,0:T(8,128)(2,1)S(1)} %fusion.25), channel_id=1, source_target_pairs={{0,1},{1,0},{2,3},{3,2},{4,5},{5,4},{6,7},{7,6},{8,9},{9,8},{10,11... | collective-permute-start | bytes 1081352 | tf_op jit(solution)/shard_map/ppermute | solution.py:225
  602.3 18.5 %copy-start.5 = (f32[1,256,1024]{2,1,0:T(8,128)S(1)}, f32[1,256,1024]{2,1,0:T(8,128)}, u32[]{:S(2)}) copy-start(f32[1,256,1024]{2,1,0:T(8,128)} %copy-done.3) | copy-start | bytes 3145732
  602.3 18.5 %copy-start.39 = (pred[256]{0:T(512)(128)(4,1)S(1)}, pred[256]{0:T(512)(128)(4,1)}, u32[]{:S(2)}) copy-start(pred[256]{0:T(512)(128)(4,1)} %copy-done.37) | copy-start | bytes 772
  611.1 17.3 %collective-permute-start.12 = (bf16[176,1024]{1,0:T(8,128)(2,1)S(1)}, bf16[176,1024]{1,0:T(8,128)(2,1)}, u32[]{:S(2)}, u32[]{:S(2)}) collective-permute-start(bf16[176,1024]{1,0:T(8,128)(2,1)S(1)} %add_convert_fusion.8), channel_id=1, source_target_pairs={{0,2},{1,3},{2,0},{3,1},{4,6},{5,7},{6,4},{7,5},{8,10},{9,11},{10,... | collective-permute-start | bytes 1081352 | tf_op jit(solution)/shard_map/ppermute | solution.py:225
  620.7 22.5 %collective-permute-start.8 = (bf16[64,6656]{1,0:T(8,128)(2,1)}, bf16[64,6656]{1,0:T(8,128)(2,1)}, u32[]{:S(2)}, u32[]{:S(2)}) collective-permute-start(bf16[64,6656]{1,0:T(8,128)(2,1)} %add_convert_fusion.2), channel_id=1, source_target_pairs={{0,2},{1,3},{2,0},{3,1},{4,6},{5,7},{6,4},{7,5},{8,10},{9,11},{10,... | collective-permute-start | bytes 2555912 | tf_op jit(solution)/shard_map/ppermute | solution.py:225
  625.8 2.5 copy-start.36
  629.5 17.0 %collective-permute-start.13 = (bf16[176,1024]{1,0:T(8,128)(2,1)S(1)}, bf16[176,1024]{1,0:T(8,128)(2,1)S(1)}, u32[]{:S(2)}, u32[]{:S(2)}) collective-permute-start(bf16[176,1024]{1,0:T(8,128)(2,1)S(1)} %add_convert_fusion.7), channel_id=1, source_target_pairs={{0,4},{1,5},{2,6},{3,7},{4,0},{5,1},{6,2},{7,3},{8,12},{9,13},{10,... | collective-permute-start | bytes 1081352 | tf_op jit(solution)/shard_map/ppermute | solution.py:225
  629.6 15.3 %copy-start.28 = (bf16[1,416,1024]{2,1,0:T(8,128)(2,1)S(1)}, bf16[1,416,1024]{2,1,0:T(8,128)(2,1)}, u32[]{:S(2)}) copy-start(bf16[1,416,1024]{2,1,0:T(8,128)(2,1)} %reduce-scatter.6.cloned.1.call-done) | copy-start | bytes 2555908
  630.7 14.4 %copy-start.7 = (f32[1,256,1024]{2,1,0:T(8,128)S(1)}, f32[1,256,1024]{2,1,0:T(8,128)}, u32[]{:S(2)}) copy-start(f32[1,256,1024]{2,1,0:T(8,128)} %copy-done.6) | copy-start | bytes 3145732
  630.8 14.1 %collective-permute-start.2 = (bf16[208,1024]{1,0:T(8,128)(2,1)S(1)}, bf16[208,1024]{1,0:T(8,128)(2,1)S(1)}, u32[]{:S(2)}, u32[]{:S(2)}) collective-permute-start(bf16[208,1024]{1,0:T(8,128)(2,1)S(1)} %dynamic-slice_bitcast_fusion.1), channel_id=1, source_target_pairs={{0,68},{68,0},{4,64},{64,4},{1,69},{69,1},{5,65},{65,5},{2,70},{70... | collective-permute-start | bytes 1277960 | tf_op jit(solution)/shard_map/ppermute | solution.py:217
  644.8 12.8 %collective-permute-start.9 = (bf16[64,6656]{1,0:T(8,128)(2,1)S(1)}, bf16[64,6656]{1,0:T(8,128)(2,1)S(1)}, u32[]{:S(2)}, u32[]{:S(2)}) collective-permute-start(bf16[64,6656]{1,0:T(8,128)(2,1)S(1)} %add_convert_fusion.1), channel_id=1, source_target_pairs={{0,4},{1,5},{2,6},{3,7},{4,0},{5,1},{6,2},{7,3},{8,12},{9,13},{10,... | collective-permute-start | bytes 2555912 | tf_op jit(solution)/shard_map/ppermute | solution.py:225
  645.1 11.0 %collective-permute-start.3 = (bf16[208,1024]{1,0:T(8,128)(2,1)S(1)}, bf16[208,1024]{1,0:T(8,128)(2,1)S(1)}, u32[]{:S(2)}, u32[]{:S(2)}) collective-permute-start(bf16[208,1024]{1,0:T(8,128)(2,1)S(1)} %fusion.24), channel_id=1, source_target_pairs={{0,1},{1,0},{2,3},{3,2},{4,5},{5,4},{6,7},{7,6},{8,9},{9,8},{10,11... | collective-permute-start | bytes 1277960 | tf_op jit(solution)/shard_map/ppermute | solution.py:225
  656.2 9.7 %collective-permute-start.4 = (bf16[208,1024]{1,0:T(8,128)(2,1)S(1)}, bf16[208,1024]{1,0:T(8,128)(2,1)S(1)}, u32[]{:S(2)}, u32[]{:S(2)}) collective-permute-start(bf16[208,1024]{1,0:T(8,128)(2,1)S(1)} %add_convert_fusion.5), channel_id=1, source_target_pairs={{0,2},{1,3},{2,0},{3,1},{4,6},{5,7},{6,4},{7,5},{8,10},{9,11},{10,... | collective-permute-start | bytes 1277960 | tf_op jit(solution)/shard_map/ppermute | solution.py:225
  666.1 8.2 %collective-permute-start.5 = (bf16[208,1024]{1,0:T(8,128)(2,1)S(1)}, bf16[208,1024]{1,0:T(8,128)(2,1)S(1)}, u32[]{:S(2)}, u32[]{:S(2)}) collective-permute-start(bf16[208,1024]{1,0:T(8,128)(2,1)S(1)} %add_convert_fusion.4), channel_id=1, source_target_pairs={{0,4},{1,5},{2,6},{3,7},{4,0},{5,1},{6,2},{7,3},{8,12},{9,13},{10,... | collective-permute-start | bytes 1277960 | tf_op jit(solution)/shard_map/ppermute | solution.py:225
  (3 other events, 3.0 us)
Sparse Core Ops, SparseCore 0:
  30.4 53.2 all-gather.4
  85.3 87.3 all-gather.6
  324.9 108.7 reduce-scatter.3
  435.9 41.9 reduce-scatter.7
  530.3 75.5 reduce-scatter.5

commit v13 on v12

--- a/solution.py
+++ b/solution.py
@@ -360,10 +360,6 @@
     middle_low = middle_back.astype(jnp.bfloat16)
     out_total = jnp.einsum("srd,sre->de", mixed_low_g, middle_low, preferred_element_type=jnp.float32)
 
-    down_share = ctx_allreduce(
-        z_combine(yc_reduce_scatter(down_total.astype(jnp.bfloat16).reshape(n_fsdp, d_rows, width))),
-        n_ctx,
-    )
     mlp_grads = jnp.concatenate(
         [
             gate_total.reshape(n_fsdp, w_rows, ff),
@@ -372,7 +368,10 @@
         ],
         axis=2,
     ).astype(jnp.bfloat16)
+    down_grads = down_total.astype(jnp.bfloat16).reshape(n_fsdp, d_rows, width)
+    mlp_grads, down_grads = lax.optimization_barrier((mlp_grads, down_grads))
     mlp_halves = yc_reduce_scatter(mlp_grads)
+    down_share = ctx_allreduce(z_combine(yc_reduce_scatter(down_grads)), n_ctx)
 
     blended_value_gradient = from_gathered(
         jnp.einsum("sre,de->srd", middle_low, out_mat, preferred_element_type=jnp.float32).astype(
@@ -384,6 +383,15 @@
         meta, query_flat, kv_all, blended_value_gradient.reshape(rows, width), head_dim, score_scale
     )
     query_rot_back = query_rot_back.reshape(slots, rows, head_count, head_dim)
+    query_back = (
+        rotate(query_rot_back, cos_rows, -sin_rows).reshape(slots, rows, width).astype(jnp.bfloat16)
+    )
+    query_total = jnp.einsum(
+        "srd,sre->de", normed_low_g, query_back, preferred_element_type=jnp.float32
+    )
+    query_grads = query_total.astype(jnp.bfloat16).reshape(n_fsdp, w_rows, width)
+    query_grads, kv_back = lax.optimization_barrier((query_grads, kv_back))
+    query_share = ctx_allreduce(z_combine(yc_reduce_scatter(query_grads)), n_ctx)
     key_value = jnp.sum(
         lax.all_to_all(kv_back.reshape(n_ctx, rows, 2 * width), CTX, 0, 0, tiled=False).astype(
             jnp.float32
@@ -394,16 +402,10 @@
     key_rot_back = key_value[:, :, 0, :].reshape(slots, rows, head_count, head_dim)
     value_mix_back = key_value[:, :, 1, :].reshape(slots, rows, width)
     first_grad = 0.5 * value_mix_back
-    query_back = (
-        rotate(query_rot_back, cos_rows, -sin_rows).reshape(slots, rows, width).astype(jnp.bfloat16)
-    )
     key_back = (
         rotate(key_rot_back, cos_rows, -sin_rows).reshape(slots, rows, width).astype(jnp.bfloat16)
     )
     value_back = (0.5 * value_mix_back).astype(jnp.bfloat16)
-    query_total = jnp.einsum(
-        "srd,sre->de", normed_low_g, query_back, preferred_element_type=jnp.float32
-    )
     key_total = jnp.einsum("srd,sre->de", normed_low_g, key_back, preferred_element_type=jnp.float32)
     value_total = jnp.einsum(
         "srd,sre->de", normed_low_g, value_back, preferred_element_type=jnp.float32
@@ -425,7 +427,6 @@
 
     attn_grads = jnp.concatenate(
         [
-            query_total.reshape(n_fsdp, w_rows, width),
             key_total.reshape(n_fsdp, w_rows, width),
             value_total.reshape(n_fsdp, w_rows, width),
             gain_block(
@@ -445,9 +446,10 @@
     def attn_grad(i):
         return attn_share[i * w_rows:(i + 1) * w_rows]
 
-    query_grad, key_grad, value_grad = (attn_grad(i) for i in range(3))
-    prenorm_grad = attn_share[3 * w_rows, 0:g_len]
-    midnorm_grad = attn_share[3 * w_rows, g_len:2 * g_len]
+    query_grad = query_share
+    key_grad, value_grad = (attn_grad(i) for i in range(2))
+    prenorm_grad = attn_share[2 * w_rows, 0:g_len]
+    midnorm_grad = attn_share[2 * w_rows, g_len:2 * g_len]
     gate_grad = mlp_share[:, 0:ff]
     up_grad = mlp_share[:, ff:2 * ff]
     down_grad = down_share

time: 691 us -> 713 us (1.032)
  waiting for transfers between devices: 294 us -> 316 us
  other arithmetic: 49.4 us -> 40.2 us
    ppermute x9 -> x12, waiting for transfers between devices: 39.6 us -> 50 us  [ctx_allreduce(): other = lax.ppermute(total, CTX, [(j, j ^ step) for j in range(n_ctx)])]
    all_to_all x1, waiting for transfers between devices: 84.8 us -> 92 us  [body(): lax.all_to_all(kv_back.reshape(n_ctx, rows, 2 * width), CTX, 0, 0, tiled=...]
    ppermute x3 -> x4, waiting for transfers between devices: 19 us -> 22.6 us  [z_combine(): got = lax.ppermute(theirs, ('zh', 'zl'), Z_CROSS)]
    ppermute x9 -> x12, starting transfers between devices: 40.6 us -> 43.4 us  [ctx_allreduce(): other = lax.ppermute(total, CTX, [(j, j ^ step) for j in range(n_ctx)])]
  transfers between devices with their start and end apart: 21 -> 26, of which waited for: 12 -> 13; matrix products, arithmetic and copies ran while one was open for 17% -> 15% of each run, Pallas kernels for 10% -> 10%
where the time goes in v13:
time: 713 us; the launch traced here: 705 us
  waiting for transfers between devices  316 us (44%)
  local copies, waits for them, and re-layouts  107 us (15%)
  starting transfers between devices  101 us (14%)
  Pallas kernels  67.8 us (10%)
  matrix products  57.2 us (8%)
  other arithmetic  40.2 us (6%)
  between operations  15.5 us (2%)
    all_to_all x1, waiting for transfers between devices, body(): lax.all_to_all(kv_back.reshape(n_ctx, rows, 2 * width), CTX, 0, 0, tiled=...  92 us
    all_to_all x1, waiting for transfers between devices, body(): lax.all_to_all(jnp.broadcast_to(kv_own[None], (n_ctx, rows, 2 * width)),...  91.9 us
    ppermute x12, waiting for transfers between devices, ctx_allreduce(): other = lax.ppermute(total, CTX, [(j, j ^ step) for j in range(n_ctx)])  50 us
    ppermute x12, starting transfers between devices, ctx_allreduce(): other = lax.ppermute(total, CTX, [(j, j ^ step) for j in range(n_ctx)])  43.4 us
    pallas_call x1, Pallas kernels, attention_backward(): pl.pallas_call(functools.partial(attn_bwd_kernel, head_dim, scale), out_s...  43.4 us
    ppermute x2, waiting for transfers between devices, fsdp_gather(): other = lax.ppermute(pack, ('zh', 'zl'), Z_CROSS)  35.9 us
    all_to_all x1, starting transfers between devices, body(): lax.all_to_all(kv_back.reshape(n_ctx, rows, 2 * width), CTX, 0, 0, tiled=...  35.7 us
    pallas_call x1, Pallas kernels, attention_forward(): pl.pallas_call(functools.partial(attn_fwd_kernel, head_dim, scale), out_s...  24.4 us
  transfers between devices with their start and end apart: 26, of which 13 were waited for; matrix products, arithmetic and copies ran while one was open for 15% of the time, Pallas kernels for 10%

profile of v13, /device:TPU:0, one launch (start us, length us, event | category | flops | bytes accessed | tf_op | source)
XLA Modules:
  0.0 705.1 jit_solution(14646734954250844230)
XLA Ops:
  11.7 4.2 collective-permute-start
  15.9 12.6 %collective-permute-done = bf16[272,1024]{1,0:T(8,128)(2,1)S(1)} collective-permute-done((bf16[272,1024]{1,0:T(8,128)(2,1)S(1)}, bf16[272,1024]{1,0:T(8,128)(2,1)S(1)}, u32[]{:S(2)}, u32[]{:S(2)}) %collective-permute-start) | collective-permute-done | bytes 557088 | tf_op jit(solution)/shard_map/ppermute | solution.py:194
  30.4 3.1 collective-permute-start.1
  33.4 23.3 %collective-permute-done.1 = bf16[64,8448]{1,0:T(8,128)(2,1)S(1)} collective-permute-done((bf16[64,8448]{1,0:T(8,128)(2,1)S(1)}, bf16[64,8448]{1,0:T(8,128)(2,1)S(1)}, u32[]{:S(2)}, u32[]{:S(2)}) %collective-permute-start.1) | collective-permute-done | bytes 1081376 | tf_op jit(solution)/shard_map/ppermute | solution.py:194
  59.9 23.3 %all-gather.5.cloned.1.call-done = bf16[16,272,1024]{2,1,0:T(8,128)(2,1)} async-done(((bf16[2,272,1024]{2,1,0:T(8,128)(2,1)}), bf16[16,272,1024]{2,1,0:T(8,128)(2,1)}) %all-gather.5.cloned.1.call-update) | async-done | bytes 8912912 | tf_op jit(solution)/shard_map/all_gather | solution.py:195
  84.6 6.0 fusion.45
  90.6 3.9 copy.159
  94.5 4.1 copy.157
  98.6 2.8 convolution_bitcast_fusion.3
  103.4 2.0 copy.161
  105.5 2.5 fusion.9
  108.0 4.3 broadcast_in_dim.72
  112.3 5.3 all-to-all-start
  120.7 91.9 %all-to-all-done = bf16[8,256,2048]{2,1,0:T(8,128)(2,1)} async-done(((bf16[8,256,2048]{2,1,0:T(8,128)(2,1)}), bf16[8,256,2048]{2,1,0:T(8,128)(2,1)}, u32[]{:S(2)}, u32[]{:S(2)}) %all-to-all-start) | async-done | bytes 8388640 | tf_op jit(solution)/shard_map/all_to_all | solution.py:313
  212.6 24.4 %shard_map.229 = bf16[256,1024]{1,0:T(8,128)(2,1)S(1)} custom-call(s32[2]{0:T(128)S(1)} %pad_add_fusion.meta_ref, bf16[256,1024]{1,0:T(8,128)(2,1)S(1)} %copy.162.q_ref, bf16[2048,2048]{1,0:T(8,128)(2,1)} %bitcast.24.k_ref.v_ref, bf16[2048,2048]{1,0:T(8,128)(2,1)} %bitcast.24.k_ref.v_ref), custom_call_target="tpu_custom_call" | custom-call | flops 2147483648 | bytes 9437184 | tf_op jit(solution)/shard_map/pallas_call | solution.py:80
  239.1 2.1 multiply_reduce_fusion.2
  244.4 11.3 %fusion.44 = (bf16[16,64,2816]{2,1,0:T(8,128)(2,1)}, bf16[16,64,2816]{2,1,0:T(8,128)(2,1)}, bf16[16,64,2816]{2,1,0:T(8,128)(2,1)}) fusion(bf16[16,64,8448]{2,1,0:T(8,128)(2,1)} %all-gather.7.cloned.1.call-done), kind=kLoop, calls=%fused_computation.144 | loop fusion | bytes 34603008 | tf_op jit(solution)/shard_map/slice | solution.py:293
  255.7 11.7 %dot_general.113 = bf16[8,2,176,1024]{3,2,1,0:T(8,128)(2,1)} reshape(bf16[16,64,2816]{2,1,0:T(8,128)(2,1)} %get-tuple-element.80) | data formatting | bytes 11534336 | tf_op jit(solution)/shard_map/sre,fe->srf/dot_general | solution.py:338
  267.5 4.6 convolution_bitcast_fusion
  272.1 1.7 copy.170
  273.8 3.4 copy.171
  277.3 4.5 fusion.49
  281.8 7.0 multiply_convert_fusion
  290.5 4.1 convolution_convert_fusion.2
  294.6 4.2 convolution_convert_fusion.1
  298.8 2.7 convolution_add_fusion.2
  301.5 2.6 copy.168
  304.0 2.6 copy.169
  306.6 2.5 copy.173
  309.1 2.3 copy.174
  311.4 2.6 copy.175
  313.9 2.0 multiply_reduce_fusion
  317.3 4.7 convolution_convert_fusion
  323.4 5.9 pad_maximum_fusion
  329.4 2.0 convolution_convert_fusion.7
  331.9 43.4 %shard_map.230 = (f32[256,1024]{1,0:T(8,128)S(1)}, bf16[2048,2048]{1,0:T(8,128)(2,1)}) custom-call(s32[2]{0:T(128)S(1)} %pad_add_fusion.meta_ref, bf16[256,1024]{1,0:T(8,128)(2,1)S(1)} %copy.162.q_ref, bf16[2048,2048]{1,0:T(8,128)(2,1)} %bitcast.24.k_ref.v_ref, bf16[2048,2048]{1,0:T(8,128)(2,1)} %bitcast.24.k_ref.v_ref, bf16[256,1024]{1,0:T(8,128)(2,1)S(1)} %copy.179.do_ref), custom_call_target="tpu_custom_call" | custom-call | flops 5368709120 | bytes 19398656 | tf_op jit(solution)/shard_map/pallas_call | solution.py:108
  376.3 2.1 convolution_convert_fusion.6
  379.0 35.7 %all-to-all-start.1 = ((bf16[8,256,2048]{2,1,0:T(8,128)(2,1)}), bf16[8,256,2048]{2,1,0:T(8,128)(2,1)}, u32[]{:S(2)}, u32[]{:S(2)}) async-start(bf16[8,256,2048]{2,1,0:T(8,128)(2,1)} %bitcast.249), calls=%async_computation.1 | async-start | bytes 16777216 | tf_op jit(solution)/shard_map/all_to_all | solution.py:396
  414.8 1.7 fusion.51
  416.6 92.0 %all-to-all-done.1 = bf16[8,256,2048]{2,1,0:T(8,128)(2,1)} async-done(((bf16[8,256,2048]{2,1,0:T(8,128)(2,1)}), bf16[8,256,2048]{2,1,0:T(8,128)(2,1)}, u32[]{:S(2)}, u32[]{:S(2)}) %all-to-all-start.1) | async-done | bytes 8388640 | tf_op jit(solution)/shard_map/all_to_all | solution.py:396
  508.6 5.5 convert_reduce_fusion
  514.1 2.1 copy.181
  516.2 2.8 slice_multiply_fusion
  522.2 1.8 convolution_add_fusion
  530.2 2.4 fusion.1
  535.1 2.5 collective-permute-start.10
  539.3 20.6 %collective-permute-done.2 = bf16[64,1024]{1,0:T(8,128)(2,1)S(1)} collective-permute-done((bf16[64,1024]{1,0:T(8,128)(2,1)S(1)}, bf16[64,1024]{1,0:T(8,128)(2,1)S(1)}, u32[]{:S(2)}, u32[]{:S(2)}) %collective-permute-start.2) | collective-permute-done | bytes 131104 | tf_op jit(solution)/shard_map/ppermute | solution.py:217
  560.8 27.8 %collective-permute-start.3 = (bf16[64,1024]{1,0:T(8,128)(2,1)S(1)}, bf16[64,1024]{1,0:T(8,128)(2,1)S(1)}, u32[]{:S(2)}, u32[]{:S(2)}) collective-permute-start(bf16[64,1024]{1,0:T(8,128)(2,1)S(1)} %fusion.32), channel_id=1, source_target_pairs={{0,1},{1,0},{2,3},{3,2},{4,5},{5,4},{6,7},{7,6},{8,9},{9,8},{10,11... | collective-permute-start | bytes 393224 | tf_op jit(solution)/shard_map/ppermute | solution.py:225
  588.7 11.8 %reshape_reshape.18 = bf16[2816,1024]{1,0:T(8,128)(2,1)} reshape(bf16[16,64,2816]{2,1,0:T(8,128)(2,1)} %get-tuple-element.80) | data formatting | bytes 11534336 | tf_op jit(solution)/shard_map/reshape;reshape | solution.py:293
  600.5 4.7 collective-permute-start.4
  606.2 3.0 collective-permute-start.14
  611.0 5.2 fusion.10
  616.4 2.0 collective-permute-start.15
  618.4 14.4 %collective-permute-done.11 = bf16[64,6656]{1,0:T(8,128)(2,1)S(1)} collective-permute-done((bf16[64,6656]{1,0:T(8,128)(2,1)S(1)}, bf16[64,6656]{1,0:T(8,128)(2,1)S(1)}, u32[]{:S(2)}, u32[]{:S(2)}) %collective-permute-start.11) | collective-permute-done | bytes 852000 | tf_op jit(solution)/shard_map/ppermute | solution.py:225
  633.3 7.3 %collective-permute-done.15 = bf16[176,1024]{1,0:T(8,128)(2,1)S(1)} collective-permute-done((bf16[176,1024]{1,0:T(8,128)(2,1)S(1)}, bf16[176,1024]{1,0:T(8,128)(2,1)S(1)}, u32[]{:S(2)}, u32[]{:S(2)}) %collective-permute-start.15) | collective-permute-done | bytes 360480 | tf_op jit(solution)/shard_map/ppermute | solution.py:225
  641.7 19.0 %collective-permute-done.16 = bf16[176,1024]{1,0:T(8,128)(2,1)S(1)} collective-permute-done((bf16[176,1024]{1,0:T(8,128)(2,1)S(1)}, bf16[176,1024]{1,0:T(8,128)(2,1)S(1)}, u32[]{:S(2)}, u32[]{:S(2)}) %collective-permute-start.16) | collective-permute-done | bytes 360480 | tf_op jit(solution)/shard_map/ppermute | solution.py:225
  662.7 2.0 collective-permute-start.6
  664.8 2.3 add_convert_fusion.1
  668.7 2.1 collective-permute-done.6
  673.4 2.5 copy.192
  675.9 2.0 fusion.30
  678.1 5.3 collective-permute-start.8
  683.5 4.1 collective-permute-done.13
  691.2 5.1 collective-permute-done.9
  (212 shorter events, 58.3 us)
Async XLA Ops:
  7.2 76.0 %all-gather.5.cloned.1.call-start = ((), (), s32[]{:S(2)}) async-start(), calls=%async_computation.10 | async-start | bytes 10027008 | tf_op jit(solution)/shard_map/all_gather | solution.py:195
  11.7 16.8 %collective-permute-start = (bf16[272,1024]{1,0:T(8,128)(2,1)S(1)}, bf16[272,1024]{1,0:T(8,128)(2,1)S(1)}, u32[]{:S(2)}, u32[]{:S(2)}) collective-permute-start(bf16[272,1024]{1,0:T(8,128)(2,1)S(1)} %pad_dynamic-update-slice_fusion), channel_id=1, source_target_pairs={{0,68},{68,0},{4,64},{64,4},{1,69},{69,1},{5,65},{65,5},{2,70},{70... | collective-permute-start | bytes 1671176 | tf_op jit(solution)/shard_map/ppermute | solution.py:194
  28.6 1.2 copy-start.27
  28.6 1.7 copy-start.28
  28.6 1.7 copy-start.29
  29.8 214.7 %all-gather.7.cloned.1.call-start = ((), (), s32[]{:S(2)}) async-start(), calls=%async_computation.11 | async-start | bytes 19464192 | tf_op jit(solution)/shard_map/all_gather | solution.py:195
  30.4 26.3 %collective-permute-start.1 = (bf16[64,8448]{1,0:T(8,128)(2,1)S(1)}, bf16[64,8448]{1,0:T(8,128)(2,1)S(1)}, u32[]{:S(2)}, u32[]{:S(2)}) collective-permute-start(bf16[64,8448]{1,0:T(8,128)(2,1)S(1)} %constant_dynamic-update-slice_fusion.4), channel_id=1, source_target_pairs={{0,68},{68,0},{4,64},{64,4},{1,69},{69,1},{5,65},{65,5},{2,70},{70... | collective-permute-start | bytes 3244040 | tf_op jit(solution)/shard_map/ppermute | solution.py:194
  84.6 20.9 %copy-start.10 = (bf16[1,256,8,2,64]{1,4,3,2,0:T(8,128)(2,1)}, bf16[1,256,8,2,64]{1,4,3,2,0:T(8,128)(2,1)S(1)}, u32[]{:S(2)}) copy-start(bf16[1,256,8,2,64]{1,4,3,2,0:T(8,128)(2,1)S(1)} %copy.156) | copy-start | bytes 1572868
  98.6 2.9 copy-start.21
  105.5 2.5 copy-start.23
  112.3 5.9 copy-start.30
  112.3 5.9 copy-start.31
  112.3 100.3 %all-to-all-start = ((bf16[8,256,2048]{2,1,0:T(8,128)(2,1)}), bf16[8,256,2048]{2,1,0:T(8,128)(2,1)}, u32[]{:S(2)}, u32[]{:S(2)}) async-start(bf16[8,256,2048]{2,1,0:T(8,128)(2,1)} %broadcast_in_dim.72), calls=%async_computation | async-start | bytes 16777216 | tf_op jit(solution)/shard_map/all_to_all | solution.py:313
  117.7 415.0 %reduce-scatter.7.cloned.1.call-start = ((), (), s32[]{:S(2)}) async-start(), calls=%async_computation.7 | async-start | bytes 15335424 | tf_op jit(solution)/shard_map/reduce_scatter | solution.py:207
  239.1 2.1 copy-start.17
  277.3 4.5 copy-start.20
  277.3 11.5 %slice-start.6 = ((s8[5767168]{0:T(1024)(128)(4,1)}), s8[4194304]{0:T(1024)(128)(4,1)S(1)}, s32[]{:S(2)}) async-start(s8[5767168]{0:T(1024)(128)(4,1)} %bitcast.254), calls=%async_computation.18 | async-start | bytes 8388608
  281.8 7.0 slice-start.7
  290.5 8.3 %slice-start = ((s8[5767168]{0:T(1024)(128)(4,1)}), s8[4194304]{0:T(1024)(128)(4,1)S(1)}, s32[]{:S(2)}) async-start(s8[5767168]{0:T(1024)(128)(4,1)} %bitcast.219), calls=%async_computation.12 | async-start | bytes 8388608
  294.6 4.2 slice-start.1
  311.4 4.6 copy-start.22
  313.9 2.0 copy-start.6
  313.9 2.2 copy-start.14
  315.9 1.4 copy-start.15
  316.1 6.6 slice-start.4
  316.6 5.5 copy-start.3
  316.6 6.2 slice-start.2
  317.3 4.7 copy-start.18
  317.3 5.4 slice-start.3
  317.3 6.1 slice-start.5
  329.4 208.3 %reduce-scatter.5.cloned.1.call-start = ((), (), s32[]{:S(2)}) async-start(), calls=%async_computation.6 | async-start | bytes 2359296 | tf_op jit(solution)/shard_map/reduce_scatter | solution.py:207
  375.2 1.1 copy-start.11
  378.4 226.8 %reduce-scatter.11.cloned.1.call-start = ((), (), s32[]{:S(2)}) async-start(), calls=%async_computation.9 | async-start | bytes 6488064 | tf_op jit(solution)/shard_map/reduce_scatter | solution.py:207
  379.0 35.8 %copy-start.2 = (bf16[16,64,1024]{2,1,0:T(8,128)(2,1)S(1)}, bf16[16,64,1024]{2,1,0:T(8,128)(2,1)}, u32[]{:S(2)}) copy-start(bf16[16,64,1024]{2,1,0:T(8,128)(2,1)} %get-tuple-element.88) | copy-start | bytes 6291460
  379.0 129.6 %all-to-all-start.1 = ((bf16[8,256,2048]{2,1,0:T(8,128)(2,1)}), bf16[8,256,2048]{2,1,0:T(8,128)(2,1)}, u32[]{:S(2)}, u32[]{:S(2)}) async-start(bf16[8,256,2048]{2,1,0:T(8,128)(2,1)} %bitcast.249), calls=%async_computation.1 | async-start | bytes 16777216 | tf_op jit(solution)/shard_map/all_to_all | solution.py:396
  414.7 246.9 %reduce-scatter.9.cloned.1.call-start = ((), (), s32[]{:S(2)}) async-start(), calls=%async_computation.8 | async-start | bytes 5308416 | tf_op jit(solution)/shard_map/reduce_scatter | solution.py:207
  516.2 3.0 copy-start.19
  519.0 1.6 copy-start.1
  520.6 1.6 copy-start
  525.5 2.7 copy-start.9
  528.2 1.3 copy-start.12
  532.7 1.5 copy-start.24
  535.1 74.1 %collective-permute-start.10 = (bf16[64,6656]{1,0:T(8,128)(2,1)}, bf16[64,6656]{1,0:T(8,128)(2,1)}, u32[]{:S(2)}, u32[]{:S(2)}) collective-permute-start(bf16[64,6656]{1,0:T(8,128)(2,1)} %dynamic-slice_bitcast_fusion), channel_id=1, source_target_pairs={{0,68},{68,0},{4,64},{64,4},{1,69},{69,1},{5,65},{65,5},{2,70},{70... | collective-permute-start | bytes 2555912 | tf_op jit(solution)/shard_map/ppermute | solution.py:217
  538.6 21.3 %collective-permute-start.2 = (bf16[64,1024]{1,0:T(8,128)(2,1)S(1)}, bf16[64,1024]{1,0:T(8,128)(2,1)S(1)}, u32[]{:S(2)}, u32[]{:S(2)}) collective-permute-start(bf16[64,1024]{1,0:T(8,128)(2,1)S(1)} %dynamic-slice_bitcast_fusion.3), channel_id=1, source_target_pairs={{0,68},{68,0},{4,64},{64,4},{1,69},{69,1},{5,65},{65,5},{2,70},{70... | collective-permute-start | bytes 393224 | tf_op jit(solution)/shard_map/ppermute | solution.py:217
  560.8 39.6 %collective-permute-start.3 = (bf16[64,1024]{1,0:T(8,128)(2,1)S(1)}, bf16[64,1024]{1,0:T(8,128)(2,1)S(1)}, u32[]{:S(2)}, u32[]{:S(2)}) collective-permute-start(bf16[64,1024]{1,0:T(8,128)(2,1)S(1)} %fusion.32), channel_id=1, source_target_pairs={{0,1},{1,0},{2,3},{3,2},{4,5},{5,4},{6,7},{7,6},{8,9},{9,8},{10,11... | collective-permute-start | bytes 393224 | tf_op jit(solution)/shard_map/ppermute | solution.py:225
  600.5 10.5 %copy-start.7 = (f32[1,256,1024]{2,1,0:T(8,128)S(1)}, f32[1,256,1024]{2,1,0:T(8,128)}, u32[]{:S(2)}) copy-start(f32[1,256,1024]{2,1,0:T(8,128)} %copy-done.5) | copy-start | bytes 3145732
  600.5 10.5 %copy-start.16 = (bf16[1,256,8,2,176]{1,4,3,2,0:T(8,128)(2,1)S(1)}, bf16[1,256,8,2,176]{1,4,3,2,0:T(8,128)(2,1)}, u32[]{:S(2)}) copy-start(bf16[1,256,8,2,176]{1,4,3,2,0:T(8,128)(2,1)} %copy.169) | copy-start | bytes 4325380
  600.5 15.6 %collective-permute-start.4 = (bf16[64,1024]{1,0:T(8,128)(2,1)S(1)}, bf16[64,1024]{1,0:T(8,128)(2,1)S(1)}, u32[]{:S(2)}, u32[]{:S(2)}) collective-permute-start(bf16[64,1024]{1,0:T(8,128)(2,1)S(1)} %add_convert_fusion.15), channel_id=1, source_target_pairs={{0,2},{1,3},{2,0},{3,1},{4,6},{5,7},{6,4},{7,5},{8,10},{9,11},{10,... | collective-permute-start | bytes 393224 | tf_op jit(solution)/shard_map/ppermute | solution.py:225
  606.2 10.1 %collective-permute-start.14 = (bf16[176,1024]{1,0:T(8,128)(2,1)S(1)}, bf16[176,1024]{1,0:T(8,128)(2,1)S(1)}, u32[]{:S(2)}, u32[]{:S(2)}) collective-permute-start(bf16[176,1024]{1,0:T(8,128)(2,1)S(1)} %dynamic-slice_bitcast_fusion.1), channel_id=1, source_target_pairs={{0,68},{68,0},{4,64},{64,4},{1,69},{69,1},{5,65},{65,5},{2,70},{70... | collective-permute-start | bytes 1081352 | tf_op jit(solution)/shard_map/ppermute | solution.py:217
  610.8 5.5 copy-start.25
  610.8 22.0 %collective-permute-start.11 = (bf16[64,6656]{1,0:T(8,128)(2,1)S(1)}, bf16[64,6656]{1,0:T(8,128)(2,1)S(1)}, u32[]{:S(2)}, u32[]{:S(2)}) collective-permute-start(bf16[64,6656]{1,0:T(8,128)(2,1)S(1)} %fusion.2), channel_id=1, source_target_pairs={{0,1},{1,0},{2,3},{3,2},{4,5},{5,4},{6,7},{7,6},{8,9},{9,8},{10,11... | collective-permute-start | bytes 2555912 | tf_op jit(solution)/shard_map/ppermute | solution.py:225
  616.2 24.7 %collective-permute-start.5 = (bf16[64,1024]{1,0:T(8,128)(2,1)S(1)}, bf16[64,1024]{1,0:T(8,128)(2,1)S(1)}, u32[]{:S(2)}, u32[]{:S(2)}) collective-permute-start(bf16[64,1024]{1,0:T(8,128)(2,1)S(1)} %add_convert_fusion.14), channel_id=1, source_target_pairs={{0,4},{1,5},{2,6},{3,7},{4,0},{5,1},{6,2},{7,3},{8,12},{9,13},{10,... | collective-permute-start | bytes 393224 | tf_op jit(solution)/shard_map/ppermute | solution.py:225
  616.4 24.1 %collective-permute-start.15 = (bf16[176,1024]{1,0:T(8,128)(2,1)S(1)}, bf16[176,1024]{1,0:T(8,128)(2,1)S(1)}, u32[]{:S(2)}, u32[]{:S(2)}) collective-permute-start(bf16[176,1024]{1,0:T(8,128)(2,1)S(1)} %fusion.24), channel_id=1, source_target_pairs={{0,1},{1,0},{2,3},{3,2},{4,5},{5,4},{6,7},{7,6},{8,9},{9,8},{10,11... | collective-permute-start | bytes 1081352 | tf_op jit(solution)/shard_map/ppermute | solution.py:225
  633.0 31.8 %collective-permute-start.12 = (bf16[64,6656]{1,0:T(8,128)(2,1)S(1)}, bf16[64,6656]{1,0:T(8,128)(2,1)}, u32[]{:S(2)}, u32[]{:S(2)}) collective-permute-start(bf16[64,6656]{1,0:T(8,128)(2,1)S(1)} %add_convert_fusion.2), channel_id=1, source_target_pairs={{0,2},{1,3},{2,0},{3,1},{4,6},{5,7},{6,4},{7,5},{8,10},{9,11},{10,... | collective-permute-start | bytes 2555912 | tf_op jit(solution)/shard_map/ppermute | solution.py:225
  640.7 20.0 %collective-permute-start.16 = (bf16[176,1024]{1,0:T(8,128)(2,1)S(1)}, bf16[176,1024]{1,0:T(8,128)(2,1)S(1)}, u32[]{:S(2)}, u32[]{:S(2)}) collective-permute-start(bf16[176,1024]{1,0:T(8,128)(2,1)S(1)} %add_convert_fusion.5), channel_id=1, source_target_pairs={{0,2},{1,3},{2,0},{3,1},{4,6},{5,7},{6,4},{7,5},{8,10},{9,11},{10,... | collective-permute-start | bytes 1081352 | tf_op jit(solution)/shard_map/ppermute | solution.py:225
  661.5 10.5 %copy-start.4 = (f32[1,256,1024]{2,1,0:T(8,128)S(1)}, f32[1,256,1024]{2,1,0:T(8,128)}, u32[]{:S(2)}) copy-start(f32[1,256,1024]{2,1,0:T(8,128)} %copy-done.3) | copy-start | bytes 3145732
  661.5 10.5 %copy-start.13 = (f32[1,256,1024]{2,1,0:T(8,128)S(1)}, f32[1,256,1024]{2,1,0:T(8,128)}, u32[]{:S(2)}) copy-start(f32[1,256,1024]{2,1,0:T(8,128)} %copy-done.12) | copy-start | bytes 3145732
  661.5 14.3 %collective-permute-start.17 = (bf16[176,1024]{1,0:T(8,128)(2,1)}, bf16[176,1024]{1,0:T(8,128)(2,1)}, u32[]{:S(2)}, u32[]{:S(2)}) collective-permute-start(bf16[176,1024]{1,0:T(8,128)(2,1)} %add_convert_fusion.4), channel_id=1, source_target_pairs={{0,4},{1,5},{2,6},{3,7},{4,0},{5,1},{6,2},{7,3},{8,12},{9,13},{10,... | collective-permute-start | bytes 1081352 | tf_op jit(solution)/shard_map/ppermute | solution.py:225
  661.6 9.2 %copy-start.26 = (bf16[1,288,1024]{2,1,0:T(8,128)(2,1)S(1)}, bf16[1,288,1024]{2,1,0:T(8,128)(2,1)}, u32[]{:S(2)}) copy-start(bf16[1,288,1024]{2,1,0:T(8,128)(2,1)} %reduce-scatter.9.cloned.1.call-done) | copy-start | bytes 1769476
  662.7 8.0 %collective-permute-start.6 = (bf16[144,1024]{1,0:T(8,128)(2,1)S(1)}, bf16[144,1024]{1,0:T(8,128)(2,1)S(1)}, u32[]{:S(2)}, u32[]{:S(2)}) collective-permute-start(bf16[144,1024]{1,0:T(8,128)(2,1)S(1)} %dynamic-slice_bitcast_fusion.2), channel_id=1, source_target_pairs={{0,68},{68,0},{4,64},{64,4},{1,69},{69,1},{5,65},{65,5},{2,70},{70... | collective-permute-start | bytes 884744 | tf_op jit(solution)/shard_map/ppermute | solution.py:217
  667.1 20.5 %collective-permute-start.13 = (bf16[64,6656]{1,0:T(8,128)(2,1)}, bf16[64,6656]{1,0:T(8,128)(2,1)}, u32[]{:S(2)}, u32[]{:S(2)}) collective-permute-start(bf16[64,6656]{1,0:T(8,128)(2,1)} %add_convert_fusion.1), channel_id=1, source_target_pairs={{0,4},{1,5},{2,6},{3,7},{4,0},{5,1},{6,2},{7,3},{8,12},{9,13},{10,... | collective-permute-start | bytes 2555912 | tf_op jit(solution)/shard_map/ppermute | solution.py:225
  670.8 7.2 %collective-permute-start.7 = (bf16[144,1024]{1,0:T(8,128)(2,1)S(1)}, bf16[144,1024]{1,0:T(8,128)(2,1)S(1)}, u32[]{:S(2)}, u32[]{:S(2)}) collective-permute-start(bf16[144,1024]{1,0:T(8,128)(2,1)S(1)} %fusion.25), channel_id=1, source_target_pairs={{0,1},{1,0},{2,3},{3,2},{4,5},{5,4},{6,7},{7,6},{8,9},{9,8},{10,11... | collective-permute-start | bytes 884744 | tf_op jit(solution)/shard_map/ppermute | solution.py:225
  678.1 11.0 %collective-permute-start.8 = (bf16[144,1024]{1,0:T(8,128)(2,1)S(1)}, bf16[144,1024]{1,0:T(8,128)(2,1)S(1)}, u32[]{:S(2)}, u32[]{:S(2)}) collective-permute-start(bf16[144,1024]{1,0:T(8,128)(2,1)S(1)} %add_convert_fusion.8), channel_id=1, source_target_pairs={{0,2},{1,3},{2,0},{3,1},{4,6},{5,7},{6,4},{7,5},{8,10},{9,11},{10,... | collective-permute-start | bytes 884744 | tf_op jit(solution)/shard_map/ppermute | solution.py:225
  689.2 7.1 %collective-permute-start.9 = (bf16[144,1024]{1,0:T(8,128)(2,1)S(1)}, bf16[144,1024]{1,0:T(8,128)(2,1)S(1)}, u32[]{:S(2)}, u32[]{:S(2)}) collective-permute-start(bf16[144,1024]{1,0:T(8,128)(2,1)S(1)} %add_convert_fusion.7), channel_id=1, source_target_pairs={{0,4},{1,5},{2,6},{3,7},{4,0},{5,1},{6,2},{7,3},{8,12},{9,13},{10,... | collective-permute-start | bytes 884744 | tf_op jit(solution)/shard_map/ppermute | solution.py:225
  (2 other events, 2.0 us)
Sparse Core Ops, SparseCore 0:
  29.9 53.2 all-gather.4
  84.8 87.3 all-gather.6
  329.5 108.3 reduce-scatter.6
  440.1 34.3 reduce-scatter.4
  476.8 39.9 reduce-scatter.10
  532.8 68.3 reduce-scatter.8

commit v14 on v12

--- a/solution.py
+++ b/solution.py
@@ -191,9 +191,16 @@
 
 
 def fsdp_gather(pack):
-    other = lax.ppermute(pack, ("zh", "zl"), Z_CROSS)
-    both = lax.all_gather(zh_pair(pack, other), ("y", "core"), axis=0, tiled=False)
-    return both.reshape((-1,) + pack.shape)
+    return yc_gather(z_exchange(pack))
+
+
+def z_exchange(pack):
+    return zh_pair(pack, lax.ppermute(pack, ("zh", "zl"), Z_CROSS))
+
+
+def yc_gather(pair):
+    both = lax.all_gather(pair, ("y", "core"), axis=0, tiled=False)
+    return both.reshape((-1,) + pair.shape[1:])
 
 
 def fsdp_reduce_scatter(grads):
@@ -268,44 +275,53 @@
     sin_rows = sine[None, :, None, :]
     valid_wide = valid[:, :, None]
 
-    attn_pack = jnp.concatenate(
-        [query_weight, key_weight, value_weight, out_weight,
-         gain_block(prenorm_gain, midnorm_gain, width)],
-        axis=0,
-    )
-    attn_all = fsdp_gather(attn_pack)
-
-    def attn_part(i):
-        return attn_all[:, i * w_rows:(i + 1) * w_rows, :].reshape(n_fsdp * w_rows, width)
-
-    query_mat, key_mat, value_mat, out_mat = (attn_part(i) for i in range(4))
-    prenorm_full = from_gathered(attn_all[:, 4 * w_rows, 0:g_len].reshape(n_fsdp * g_len), g_len)
+    kv_pair = z_exchange(
+        jnp.concatenate(
+            [key_weight, value_weight, gain_block(prenorm_gain, midnorm_gain, width)], axis=0
+        )
+    )
+    rest_pair = z_exchange(
+        jnp.concatenate(
+            [
+                gate_weight,
+                up_weight,
+                down_weight.reshape(w_rows, ff),
+                query_weight,
+                out_weight,
+            ],
+            axis=1,
+        )
+    )
+    kv_wall = yc_gather(kv_pair)
+    rest_pair, kv_wall = lax.optimization_barrier((rest_pair, kv_wall))
+    rest_wall = yc_gather(rest_pair)
+
+    key_mat = kv_wall[:, 0:w_rows, :].reshape(n_fsdp * w_rows, width)
+    value_mat = kv_wall[:, w_rows:2 * w_rows, :].reshape(n_fsdp * w_rows, width)
+    prenorm_full = from_gathered(kv_wall[:, 2 * w_rows, 0:g_len].reshape(n_fsdp * g_len), g_len)
     midnorm_full = from_gathered(
-        attn_all[:, 4 * w_rows, g_len:2 * g_len].reshape(n_fsdp * g_len), g_len
-    )
-
-    mlp_pack = jnp.concatenate(
-        [gate_weight, up_weight, down_weight.reshape(w_rows, ff)], axis=1
-    )
-    mlp_all = fsdp_gather(mlp_pack)
-    gate_mat = mlp_all[:, :, 0:ff].reshape(n_fsdp * w_rows, ff)
-    upper_mat = mlp_all[:, :, ff:2 * ff].reshape(n_fsdp * w_rows, ff)
-    down_mat = mlp_all[:, :, 2 * ff:].reshape(n_fsdp, d_rows, width).reshape(n_fsdp * d_rows, width)
+        kv_wall[:, 2 * w_rows, g_len:2 * g_len].reshape(n_fsdp * g_len), g_len
+    )
+    gate_mat = rest_wall[:, :, 0:ff].reshape(n_fsdp * w_rows, ff)
+    upper_mat = rest_wall[:, :, ff:2 * ff].reshape(n_fsdp * w_rows, ff)
+    down_mat = (
+        rest_wall[:, :, 2 * ff:3 * ff].reshape(n_fsdp, d_rows, width).reshape(n_fsdp * d_rows, width)
+    )
+    query_mat = rest_wall[:, :, 3 * ff:3 * ff + width].reshape(n_fsdp * w_rows, width)
+    out_mat = rest_wall[:, :, 3 * ff + width:].reshape(n_fsdp * w_rows, width)
 
     tokens_wide = tokens.astype(jnp.float32)
     first_wide = first_value.astype(jnp.float32)
     normed, inverse = norm_apply(tokens_wide, prenorm_full.astype(jnp.float32))
     normed_low = normed.astype(jnp.bfloat16)
     normed_low_g = to_gathered(normed_low, w_rows)
-    query = jnp.dot(normed_low_g, query_mat, preferred_element_type=jnp.float32)
     keyed = jnp.dot(normed_low_g, key_mat, preferred_element_type=jnp.float32)
     own_value = jnp.dot(normed_low_g, value_mat, preferred_element_type=jnp.float32)
-    heads_shape = query.shape[:2] + (head_count, head_dim)
-    query_rotated_rows = rotate(query.reshape(heads_shape), cos_rows, sin_rows).astype(jnp.bfloat16)
+    heads_shape = keyed.shape[:2] + (head_count, head_dim)
     key_rot = (
         rotate(keyed.reshape(heads_shape), cos_rows, sin_rows)
         .astype(jnp.bfloat16)
-        .reshape(query.shape)
+        .reshape(keyed.shape)
     )
     value_mix = (0.5 * own_value + 0.5 * first_wide).astype(jnp.bfloat16)
 
@@ -313,6 +329,9 @@
     kv_all = lax.all_to_all(
         jnp.broadcast_to(kv_own[None], (n_ctx, rows, 2 * width)), CTX, 0, 0, tiled=False
     ).reshape(total_len, 2 * width)
+    query_in, kv_all = lax.optimization_barrier((normed_low_g, kv_all))
+    query = jnp.dot(query_in, query_mat, preferred_element_type=jnp.float32)
+    query_rotated_rows = rotate(query.reshape(heads_shape), cos_rows, sin_rows).astype(jnp.bfloat16)
     meta = jnp.stack([lax.axis_index(CTX) * rows, slot_lengths[0]]).astype(jnp.int32)
     query_flat = query_rotated_rows.reshape(rows, width)
     mixed_low = attention_forward(

time: 691 us -> 668 us (0.967)
  waiting for transfers between devices: 294 us -> 274 us
    all_gather x2, waiting for transfers between devices: 22.7 us -> 1 us  [yc_gather(): both = lax.all_gather(pair, ('y', 'core'), axis=0, tiled=False)]
    slice x2 -> x3, local copies, waits for them, and re-layouts: 17.3 us -> 19.9 us  [the longest x1 11.4 us: body(): rest_wall[:, :, 2 * ff:3 * ff].reshape(n_fsdp, d_rows, width)]
  transfers between devices with their start and end apart: 21 -> 21, of which waited for: 12 -> 12; matrix products, arithmetic and copies ran while one was open for 17% -> 15% of each run, Pallas kernels for 10% -> 7%
where the time goes in v14:
time: 668 us; the launch traced here: 661 us
  waiting for transfers between devices  274 us (41%)
  local copies, waits for them, and re-layouts  104 us (16%)
  starting transfers between devices  95.3 us (14%)
  Pallas kernels  67.8 us (10%)
  matrix products  53.4 us (8%)
  other arithmetic  50.8 us (8%)
  between operations  15.3 us (2%)
    all_to_all x1, waiting for transfers between devices, body(): lax.all_to_all(jnp.broadcast_to(kv_own[None], (n_ctx, rows, 2 * width)),...  92.7 us
    all_to_all x1, waiting for transfers between devices, body(): lax.all_to_all(kv_back.reshape(n_ctx, rows, 2 * width), CTX, 0, 0, tiled=...  85 us
    pallas_call x1, Pallas kernels, attention_backward(): pl.pallas_call(functools.partial(attn_bwd_kernel, head_dim, scale), out_s...  43.4 us
    ppermute x9, waiting for transfers between devices, ctx_allreduce(): other = lax.ppermute(total, CTX, [(j, j ^ step) for j in range(n_ctx)])  40.4 us
    ppermute x9, starting transfers between devices, ctx_allreduce(): other = lax.ppermute(total, CTX, [(j, j ^ step) for j in range(n_ctx)])  39.9 us
    ppermute x2, waiting for transfers between devices, z_exchange(): return zh_pair(pack, lax.ppermute(pack, ('zh', 'zl'), Z_CROSS))  35.9 us
    all_to_all x1, starting transfers between devices, body(): lax.all_to_all(kv_back.reshape(n_ctx, rows, 2 * width), CTX, 0, 0, tiled=...  35.9 us
    pallas_call x1, Pallas kernels, attention_forward(): pl.pallas_call(functools.partial(attn_fwd_kernel, head_dim, scale), out_s...  24.4 us
  transfers between devices with their start and end apart: 21, of which 12 were waited for; matrix products, arithmetic and copies ran while one was open for 15% of the time, Pallas kernels for 7%

profile of v14, /device:TPU:0, one launch (start us, length us, event | category | flops | bytes accessed | tf_op | source)
XLA Modules:
  0.0 660.8 jit_solution(17904668077887631607)
XLA Ops:
  9.6 4.2 collective-permute-start.1
  13.8 7.0 %collective-permute-done.1 = bf16[144,1024]{1,0:T(8,128)(2,1)S(1)} collective-permute-done((bf16[144,1024]{1,0:T(8,128)(2,1)S(1)}, bf16[144,1024]{1,0:T(8,128)(2,1)S(1)}, u32[]{:S(2)}, u32[]{:S(2)}) %collective-permute-start.1) | collective-permute-done | bytes 294944 | tf_op jit(solution)/shard_map/ppermute | solution.py:198
  23.7 3.0 collective-permute-start
  26.7 28.9 %collective-permute-done = bf16[64,10496]{1,0:T(8,128)(2,1)S(1)} collective-permute-done((bf16[64,10496]{1,0:T(8,128)(2,1)S(1)}, bf16[64,10496]{1,0:T(8,128)(2,1)S(1)}, u32[]{:S(2)}, u32[]{:S(2)}) %collective-permute-start) | collective-permute-done | bytes 1343520 | tf_op jit(solution)/shard_map/ppermute | solution.py:198
  55.8 1.7 pad_maximum_fusion.1
  61.1 4.4 fusion.47
  65.5 4.5 copy.166
  70.1 2.6 convolution_bitcast_fusion.4
  73.9 2.0 fusion.9
  76.0 4.3 broadcast_in_dim.72
  80.4 5.1 all-to-all-start
  87.8 92.7 %all-to-all-done = bf16[8,256,2048]{2,1,0:T(8,128)(2,1)} async-done(((bf16[8,256,2048]{2,1,0:T(8,128)(2,1)}), bf16[8,256,2048]{2,1,0:T(8,128)(2,1)}, u32[]{:S(2)}, u32[]{:S(2)}) %all-to-all-start) | async-done | bytes 8388640 | tf_op jit(solution)/shard_map/all_to_all | solution.py:329
  180.6 4.1 fusion.46
  184.7 4.5 copy.169
  189.2 11.4 %fusion.45 = (bf16[16,64,2816]{2,1,0:T(8,128)(2,1)}, bf16[16,64,2816]{2,1,0:T(8,128)(2,1)}, bf16[16,64,2816]{2,1,0:T(8,128)(2,1)}) fusion(bf16[16,64,10496]{2,1,0:T(8,128)(2,1)} %all-gather.7.cloned.1.call-done), kind=kLoop, calls=%fused_computation.138 | loop fusion | bytes 34603008 | tf_op jit(solution)/shard_map/slice | solution.py:308
  200.5 11.8 %dot_general.113 = bf16[8,2,176,1024]{3,2,1,0:T(8,128)(2,1)} reshape(bf16[16,64,2816]{2,1,0:T(8,128)(2,1)} %get-tuple-element.80) | data formatting | bytes 11534336 | tf_op jit(solution)/shard_map/sre,fe->srf/dot_general | solution.py:357
  212.3 4.5 convolution_bitcast_fusion
  216.8 1.8 copy.179
  218.6 3.4 copy.180
  222.0 2.3 convolution_bitcast_fusion.2
  224.8 24.4 %shard_map.229 = bf16[256,1024]{1,0:T(8,128)(2,1)S(1)} custom-call(s32[2]{0:T(128)S(1)} %pad_add_fusion.meta_ref, bf16[256,1024]{1,0:T(8,128)(2,1)S(1)} %copy.171.q_ref, bf16[2048,2048]{1,0:T(8,128)(2,1)} %bitcast.22.k_ref.v_ref, bf16[2048,2048]{1,0:T(8,128)(2,1)} %bitcast.22.k_ref.v_ref), custom_call_target="tpu_custom_call" | custom-call | flops 2147483648 | bytes 9437184 | tf_op jit(solution)/shard_map/pallas_call | solution.py:80
  251.3 2.1 multiply_reduce_fusion.2
  256.7 4.6 fusion.51
  261.3 4.2 multiply_convert_fusion
  265.6 1.7 fusion.52
  267.2 4.1 convolution_convert_fusion.2
  271.4 4.1 convolution_convert_fusion.1
  275.5 2.7 convolution_add_fusion.2
  278.2 2.6 copy.182
  280.7 2.3 copy.183
  283.0 2.6 copy.184
  285.6 2.0 multiply_reduce_fusion
  290.9 11.1 %pad_maximum_fusion = bf16[8,128,6656]{2,1,0:T(8,128)(2,1)} fusion(bf16[8,128,1024]{2,1,0:T(8,128)(2,1)S(1)} %convolution_convert_fusion.3, bf16[8,128,2816]{2,1,0:T(8,128)(2,1)} %convolution_convert_fusion.1, bf16[8,128,2816]{2,1,0:T(8,128)(2,1)} %convolution_convert_fusion.2), kind=kLoop, calls=%fused_computation.2 | loop fusion | flops 40894464 | bytes 27262976 | tf_op jit(solution)/shard_map/concatenate | solution.py:386
  302.0 2.0 convolution_convert_fusion.7
  304.5 43.4 %shard_map.230 = (f32[256,1024]{1,0:T(8,128)S(1)}, bf16[2048,2048]{1,0:T(8,128)(2,1)}) custom-call(s32[2]{0:T(128)S(1)} %pad_add_fusion.meta_ref, bf16[256,1024]{1,0:T(8,128)(2,1)S(1)} %copy.171.q_ref, bf16[2048,2048]{1,0:T(8,128)(2,1)} %bitcast.22.k_ref.v_ref, bf16[2048,2048]{1,0:T(8,128)(2,1)} %bitcast.22.k_ref.v_ref, bf16[256,1024]{1,0:T(8,128)(2,1)S(1)} %copy.188.do_ref), custom_call_target="tpu_custom_call" | custom-call | flops 5368709120 | bytes 19398656 | tf_op jit(solution)/shard_map/pallas_call | solution.py:108
  347.9 35.9 %all-to-all-start.1 = ((bf16[8,256,2048]{2,1,0:T(8,128)(2,1)}), bf16[8,256,2048]{2,1,0:T(8,128)(2,1)}, u32[]{:S(2)}, u32[]{:S(2)}) async-start(bf16[8,256,2048]{2,1,0:T(8,128)(2,1)} %bitcast.240), calls=%async_computation.1 | async-start | bytes 16777216 | tf_op jit(solution)/shard_map/all_to_all | solution.py:407
  387.0 4.2 convolution_convert_fusion
  392.7 85.0 %all-to-all-done.1 = bf16[8,256,2048]{2,1,0:T(8,128)(2,1)} async-done(((bf16[8,256,2048]{2,1,0:T(8,128)(2,1)}), bf16[8,256,2048]{2,1,0:T(8,128)(2,1)}, u32[]{:S(2)}, u32[]{:S(2)}) %all-to-all-start.1) | async-done | bytes 8388640 | tf_op jit(solution)/shard_map/all_to_all | solution.py:407
  477.8 5.3 convert_reduce_fusion
  483.1 2.1 copy.190
  485.2 2.8 slice_multiply_fusion
  488.5 1.7 copy-done.3
  492.6 1.7 convolution_add_fusion
  496.9 1.6 copy.194
  501.1 1.8 convolution_convert_fusion.5
  504.7 3.3 fusion.1
  508.0 2.1 dynamic-slice_bitcast_fusion
  510.1 2.4 collective-permute-start.6
  514.5 19.0 %collective-permute-done.6 = bf16[64,6656]{1,0:T(8,128)(2,1)} collective-permute-done((bf16[64,6656]{1,0:T(8,128)(2,1)}, bf16[64,6656]{1,0:T(8,128)(2,1)}, u32[]{:S(2)}, u32[]{:S(2)}) %collective-permute-start.6) | collective-permute-done | bytes 852000 | tf_op jit(solution)/shard_map/ppermute | solution.py:224
  533.5 2.5 fusion.2
  536.0 29.4 %collective-permute-start.7 = (bf16[64,6656]{1,0:T(8,128)(2,1)}, bf16[64,6656]{1,0:T(8,128)(2,1)}, u32[]{:S(2)}, u32[]{:S(2)}) collective-permute-start(bf16[64,6656]{1,0:T(8,128)(2,1)} %fusion.2), channel_id=1, source_target_pairs={{0,1},{1,0},{2,3},{3,2},{4,5},{5,4},{6,7},{7,6},{8,9},{9,8},{10,11... | collective-permute-start | bytes 2555912 | tf_op jit(solution)/shard_map/ppermute | solution.py:232
  565.6 2.6 collective-permute-start.11
  568.2 11.8 %reshape_reshape.21 = bf16[2816,1024]{1,0:T(8,128)(2,1)} reshape(bf16[16,64,2816]{2,1,0:T(8,128)(2,1)} %get-tuple-element.80) | data formatting | bytes 11534336 | tf_op jit(solution)/shard_map/reshape;reshape | solution.py:308
  580.0 7.7 %collective-permute-done.11 = bf16[176,1024]{1,0:T(8,128)(2,1)} collective-permute-done((bf16[176,1024]{1,0:T(8,128)(2,1)S(1)}, bf16[176,1024]{1,0:T(8,128)(2,1)}, u32[]{:S(2)}, u32[]{:S(2)}) %collective-permute-start.11) | collective-permute-done | bytes 360480 | tf_op jit(solution)/shard_map/ppermute | solution.py:232
  589.0 6.8 %collective-permute-start.12 = (bf16[176,1024]{1,0:T(8,128)(2,1)S(1)}, bf16[176,1024]{1,0:T(8,128)(2,1)}, u32[]{:S(2)}, u32[]{:S(2)}) collective-permute-start(bf16[176,1024]{1,0:T(8,128)(2,1)S(1)} %add_convert_fusion.8), channel_id=1, source_target_pairs={{0,2},{1,3},{2,0},{3,1},{4,6},{5,7},{6,4},{7,5},{8,10},{9,11},{10,... | collective-permute-start | bytes 1081352 | tf_op jit(solution)/shard_map/ppermute | solution.py:232
  595.7 2.5 add_convert_fusion.2
  598.3 5.1 fusion.10
  603.4 2.5 copy.202
  608.3 3.6 collective-permute-start.2
  611.9 8.8 %collective-permute-done.8 = bf16[64,6656]{1,0:T(8,128)(2,1)} collective-permute-done((bf16[64,6656]{1,0:T(8,128)(2,1)}, bf16[64,6656]{1,0:T(8,128)(2,1)}, u32[]{:S(2)}, u32[]{:S(2)}) %collective-permute-start.8) | collective-permute-done | bytes 852000 | tf_op jit(solution)/shard_map/ppermute | solution.py:232
  620.7 1.6 add_convert_fusion.1
  625.0 8.9 %collective-permute-done.3 = bf16[208,1024]{1,0:T(8,128)(2,1)S(1)} collective-permute-done((bf16[208,1024]{1,0:T(8,128)(2,1)S(1)}, bf16[208,1024]{1,0:T(8,128)(2,1)S(1)}, u32[]{:S(2)}, u32[]{:S(2)}) %collective-permute-start.3) | collective-permute-done | bytes 426016 | tf_op jit(solution)/shard_map/ppermute | solution.py:232
  636.1 7.7 %collective-permute-done.4 = bf16[208,1024]{1,0:T(8,128)(2,1)S(1)} collective-permute-done((bf16[208,1024]{1,0:T(8,128)(2,1)S(1)}, bf16[208,1024]{1,0:T(8,128)(2,1)S(1)}, u32[]{:S(2)}, u32[]{:S(2)}) %collective-permute-start.4) | collective-permute-done | bytes 426016 | tf_op jit(solution)/shard_map/ppermute | solution.py:232
  645.2 6.9 %collective-permute-done.5 = bf16[208,1024]{1,0:T(8,128)(2,1)S(1)} collective-permute-done((bf16[208,1024]{1,0:T(8,128)(2,1)S(1)}, bf16[208,1024]{1,0:T(8,128)(2,1)S(1)}, u32[]{:S(2)}, u32[]{:S(2)}) %collective-permute-start.5) | collective-permute-done | bytes 426016 | tf_op jit(solution)/shard_map/ppermute | solution.py:232
  (211 shorter events, 49.9 us)
Async XLA Ops:
  7.2 15.7 %copy-start.33 = (bf16[176,1024]{1,0:T(8,128)(2,1)S(1)}, bf16[176,1024]{1,0:T(8,128)(2,1)}, u32[]{:S(2)}) copy-start(bf16[176,1024]{1,0:T(8,128)(2,1)} %param.22) | copy-start | bytes 1081348
  7.2 51.4 %all-gather.5.cloned.1.call-start = ((), (), s32[]{:S(2)}) async-start(), calls=%async_computation.8 | async-start | bytes 5308416 | tf_op jit(solution)/shard_map/all_gather | solution.py:202
  8.5 14.8 %copy-start.34 = (bf16[64,2816]{1,0:T(8,128)(2,1)S(1)}, bf16[64,2816]{1,0:T(8,128)(2,1)}, u32[]{:S(2)}) copy-start(bf16[64,2816]{1,0:T(8,128)(2,1)} %param.20) | copy-start | bytes 1081348
  9.6 11.2 %collective-permute-start.1 = (bf16[144,1024]{1,0:T(8,128)(2,1)S(1)}, bf16[144,1024]{1,0:T(8,128)(2,1)S(1)}, u32[]{:S(2)}, u32[]{:S(2)}) collective-permute-start(bf16[144,1024]{1,0:T(8,128)(2,1)S(1)} %fusion.34), channel_id=1, source_target_pairs={{0,68},{68,0},{4,64},{64,4},{1,69},{69,1},{5,65},{65,5},{2,70},{70... | collective-permute-start | bytes 884744 | tf_op jit(solution)/shard_map/ppermute | solution.py:198
  13.8 9.6 %copy-start.35 = (bf16[64,2816]{1,0:T(8,128)(2,1)S(1)}, bf16[64,2816]{1,0:T(8,128)(2,1)}, u32[]{:S(2)}) copy-start(bf16[64,2816]{1,0:T(8,128)(2,1)} %param.21) | copy-start | bytes 1081348
  22.8 157.8 %all-gather.7.cloned.1.call-start = ((), (), s32[]{:S(2)}) async-start(), calls=%async_computation.9 | async-start | bytes 24182784 | tf_op jit(solution)/shard_map/all_gather | solution.py:202
  23.7 32.0 %collective-permute-start = (bf16[64,10496]{1,0:T(8,128)(2,1)S(1)}, bf16[64,10496]{1,0:T(8,128)(2,1)S(1)}, u32[]{:S(2)}, u32[]{:S(2)}) collective-permute-start(bf16[64,10496]{1,0:T(8,128)(2,1)S(1)} %constant_dynamic-update-slice_fusion), channel_id=1, source_target_pairs={{0,68},{68,0},{4,64},{64,4},{1,69},{69,1},{5,65},{65,5},{2,70},{70... | collective-permute-start | bytes 4030472 | tf_op jit(solution)/shard_map/ppermute | solution.py:198
  59.7 164.7 %copy-start.31 = (f32[256,32]{0,1:T(8,128)}, f32[256,32]{0,1:T(8,128)S(1)}, u32[]{:S(2)}) copy-start(f32[256,32]{0,1:T(8,128)S(1)} %get-tuple-element.120) | copy-start | bytes 98308
  61.1 12.8 %copy-start.11 = (bf16[1,256,8,2,64]{1,4,3,2,0:T(8,128)(2,1)}, bf16[1,256,8,2,64]{1,4,3,2,0:T(8,128)(2,1)S(1)}, u32[]{:S(2)}) copy-start(bf16[1,256,8,2,64]{1,4,3,2,0:T(8,128)(2,1)S(1)} %copy.164) | copy-start | bytes 1572868
  65.5 8.4 %copy-start = (bf16[16,64,1024]{2,1,0:T(8,128)(2,1)}, bf16[16,64,1024]{2,1,0:T(8,128)(2,1)S(1)}, u32[]{:S(2)}) copy-start(bf16[16,64,1024]{2,1,0:T(8,128)(2,1)S(1)} %get-tuple-element.91) | copy-start | bytes 6291460
  73.9 2.0 copy-start.26
  80.4 5.2 copy-start.43
  80.4 5.2 copy-start.44
  80.4 100.2 %all-to-all-start = ((bf16[8,256,2048]{2,1,0:T(8,128)(2,1)}), bf16[8,256,2048]{2,1,0:T(8,128)(2,1)}, u32[]{:S(2)}, u32[]{:S(2)}) async-start(bf16[8,256,2048]{2,1,0:T(8,128)(2,1)} %broadcast_in_dim.72), calls=%async_computation | async-start | bytes 16777216 | tf_op jit(solution)/shard_map/all_to_all | solution.py:329
  85.5 422.4 %reduce-scatter.4.cloned.1.call-start = ((), (), s32[]{:S(2)}) async-start(), calls=%async_computation.5 | async-start | bytes 15335424 | tf_op jit(solution)/shard_map/reduce_scatter | solution.py:214
  87.0 200.5 %copy-start.40 = (pred[256]{0:T(512)(128)(4,1)}, pred[256]{0:T(512)(128)(4,1)S(1)}, u32[]{:S(2)}) copy-start(pred[256]{0:T(512)(128)(4,1)S(1)} %fusion.41) | copy-start | bytes 772
  200.5 11.8 %copy-start.24 = (bf16[1,256,1024]{2,1,0:T(8,128)(2,1)S(1)}, bf16[1,256,1024]{2,1,0:T(8,128)(2,1)}, u32[]{:S(2)}) copy-start(bf16[1,256,1024]{2,1,0:T(8,128)(2,1)} %param.25) | copy-start | bytes 1572868
  218.6 3.4 copy-start.12
  251.3 2.1 copy-start.15
  255.5 5.8 slice-start.2
  256.7 4.6 slice-start.3
  256.7 4.6 copy-start.23
  267.2 8.3 %slice-start = ((s8[5767168]{0:T(1024)(128)(4,1)}), s8[4194304]{0:T(1024)(128)(4,1)S(1)}, s32[]{:S(2)}) async-start(s8[5767168]{0:T(1024)(128)(4,1)} %bitcast.214), calls=%async_computation.10 | async-start | bytes 8388608
  271.4 4.1 slice-start.1
  285.6 2.0 copy-start.7
  285.6 2.2 copy-start.14
  287.5 2.7 copy-start.16
  347.9 35.9 %copy-start.27 = (bf16[256,2816]{1,0:T(8,128)(2,1)S(1)}, bf16[256,2816]{1,0:T(8,128)(2,1)}, u32[]{:S(2)}) copy-start(bf16[256,2816]{1,0:T(8,128)(2,1)} %get-tuple-element.87) | copy-start | bytes 4325380
  347.9 129.9 %all-to-all-start.1 = ((bf16[8,256,2048]{2,1,0:T(8,128)(2,1)}), bf16[8,256,2048]{2,1,0:T(8,128)(2,1)}, u32[]{:S(2)}, u32[]{:S(2)}) async-start(bf16[8,256,2048]{2,1,0:T(8,128)(2,1)} %bitcast.240), calls=%async_computation.1 | async-start | bytes 16777216 | tf_op jit(solution)/shard_map/all_to_all | solution.py:407
  383.8 128.8 %reduce-scatter.8.cloned.1.call-start = ((), (), s32[]{:S(2)}) async-start(), calls=%async_computation.7 | async-start | bytes 6488064 | tf_op jit(solution)/shard_map/reduce_scatter | solution.py:214
  385.4 1.6 copy-start.25
  385.4 1.6 copy-start.41
  391.2 215.9 %reduce-scatter.6.cloned.1.call-start = ((), (), s32[]{:S(2)}) async-start(), calls=%async_computation.6 | async-start | bytes 7667712 | tf_op jit(solution)/shard_map/reduce_scatter | solution.py:214
  485.2 2.8 copy-start.22
  485.2 2.8 copy-start.32
  485.2 2.8 copy-start.36
  488.0 3.7 copy-start.17
  488.1 2.2 copy-start.3
  488.5 3.2 copy-start.19
  488.5 3.2 copy-start.21
  488.5 2.4 copy-start.2
  491.0 1.6 copy-start.1
  495.9 2.7 copy-start.10
  496.9 4.2 copy-start.13
  500.2 2.7 copy-start.20
  510.1 23.4 %collective-permute-start.6 = (bf16[64,6656]{1,0:T(8,128)(2,1)}, bf16[64,6656]{1,0:T(8,128)(2,1)}, u32[]{:S(2)}, u32[]{:S(2)}) collective-permute-start(bf16[64,6656]{1,0:T(8,128)(2,1)} %dynamic-slice_bitcast_fusion), channel_id=1, source_target_pairs={{0,68},{68,0},{4,64},{64,4},{1,69},{69,1},{5,65},{65,5},{2,70},{70... | collective-permute-start | bytes 2555912 | tf_op jit(solution)/shard_map/ppermute | solution.py:224
  512.6 52.9 %copy-start.30 = (bf16[1,352,1024]{2,1,0:T(8,128)(2,1)S(1)}, bf16[1,352,1024]{2,1,0:T(8,128)(2,1)}, u32[]{:S(2)}) copy-start(bf16[1,352,1024]{2,1,0:T(8,128)(2,1)} %reduce-scatter.8.cloned.1.call-done) | copy-start | bytes 2162692
  513.7 51.8 %collective-permute-start.10 = (bf16[176,1024]{1,0:T(8,128)(2,1)S(1)}, bf16[176,1024]{1,0:T(8,128)(2,1)S(1)}, u32[]{:S(2)}, u32[]{:S(2)}) collective-permute-start(bf16[176,1024]{1,0:T(8,128)(2,1)S(1)} %dynamic-slice_bitcast_fusion.2), channel_id=1, source_target_pairs={{0,68},{68,0},{4,64},{64,4},{1,69},{69,1},{5,65},{65,5},{2,70},{70... | collective-permute-start | bytes 1081352 | tf_op jit(solution)/shard_map/ppermute | solution.py:224
  536.0 59.7 %collective-permute-start.7 = (bf16[64,6656]{1,0:T(8,128)(2,1)}, bf16[64,6656]{1,0:T(8,128)(2,1)}, u32[]{:S(2)}, u32[]{:S(2)}) collective-permute-start(bf16[64,6656]{1,0:T(8,128)(2,1)} %fusion.2), channel_id=1, source_target_pairs={{0,1},{1,0},{2,3},{3,2},{4,5},{5,4},{6,7},{7,6},{8,9},{9,8},{10,11... | collective-permute-start | bytes 2555912 | tf_op jit(solution)/shard_map/ppermute | solution.py:232
  565.6 14.4 %copy-start.28 = (bf16[176,1024]{1,0:T(8,128)(2,1)}, bf16[176,1024]{1,0:T(8,128)(2,1)S(1)}, u32[]{:S(2)}) copy-start(bf16[176,1024]{1,0:T(8,128)(2,1)S(1)} %fusion.25) | copy-start | bytes 1081348
  565.6 22.2 %collective-permute-start.11 = (bf16[176,1024]{1,0:T(8,128)(2,1)S(1)}, bf16[176,1024]{1,0:T(8,128)(2,1)}, u32[]{:S(2)}, u32[]{:S(2)}) collective-permute-start(bf16[176,1024]{1,0:T(8,128)(2,1)S(1)} %fusion.25), channel_id=1, source_target_pairs={{0,1},{1,0},{2,3},{3,2},{4,5},{5,4},{6,7},{7,6},{8,9},{9,8},{10,11... | collective-permute-start | bytes 1081352 | tf_op jit(solution)/shard_map/ppermute | solution.py:232
  580.0 18.3 %copy-start.8 = (f32[1,256,1024]{2,1,0:T(8,128)S(1)}, f32[1,256,1024]{2,1,0:T(8,128)}, u32[]{:S(2)}) copy-start(f32[1,256,1024]{2,1,0:T(8,128)} %copy-done.6) | copy-start | bytes 3145732
  580.0 18.3 %copy-start.42 = (pred[256]{0:T(512)(128)(4,1)S(1)}, pred[256]{0:T(512)(128)(4,1)}, u32[]{:S(2)}) copy-start(pred[256]{0:T(512)(128)(4,1)} %copy-done.40) | copy-start | bytes 772
  589.0 17.0 %collective-permute-start.12 = (bf16[176,1024]{1,0:T(8,128)(2,1)S(1)}, bf16[176,1024]{1,0:T(8,128)(2,1)}, u32[]{:S(2)}, u32[]{:S(2)}) collective-permute-start(bf16[176,1024]{1,0:T(8,128)(2,1)S(1)} %add_convert_fusion.8), channel_id=1, source_target_pairs={{0,2},{1,3},{2,0},{3,1},{4,6},{5,7},{6,4},{7,5},{8,10},{9,11},{10,... | collective-permute-start | bytes 1081352 | tf_op jit(solution)/shard_map/ppermute | solution.py:232
  598.2 22.5 %collective-permute-start.8 = (bf16[64,6656]{1,0:T(8,128)(2,1)}, bf16[64,6656]{1,0:T(8,128)(2,1)}, u32[]{:S(2)}, u32[]{:S(2)}) collective-permute-start(bf16[64,6656]{1,0:T(8,128)(2,1)} %add_convert_fusion.2), channel_id=1, source_target_pairs={{0,2},{1,3},{2,0},{3,1},{4,6},{5,7},{6,4},{7,5},{8,10},{9,11},{10,... | collective-permute-start | bytes 2555912 | tf_op jit(solution)/shard_map/ppermute | solution.py:232
  603.4 2.5 copy-start.39
  607.0 17.0 %collective-permute-start.13 = (bf16[176,1024]{1,0:T(8,128)(2,1)S(1)}, bf16[176,1024]{1,0:T(8,128)(2,1)S(1)}, u32[]{:S(2)}, u32[]{:S(2)}) collective-permute-start(bf16[176,1024]{1,0:T(8,128)(2,1)S(1)} %add_convert_fusion.7), channel_id=1, source_target_pairs={{0,4},{1,5},{2,6},{3,7},{4,0},{5,1},{6,2},{7,3},{8,12},{9,13},{10,... | collective-permute-start | bytes 1081352 | tf_op jit(solution)/shard_map/ppermute | solution.py:232
  607.2 15.3 %copy-start.29 = (bf16[1,416,1024]{2,1,0:T(8,128)(2,1)S(1)}, bf16[1,416,1024]{2,1,0:T(8,128)(2,1)}, u32[]{:S(2)}) copy-start(bf16[1,416,1024]{2,1,0:T(8,128)(2,1)} %reduce-scatter.6.cloned.1.call-done) | copy-start | bytes 2555908
  608.3 14.4 %copy-start.5 = (f32[1,256,1024]{2,1,0:T(8,128)S(1)}, f32[1,256,1024]{2,1,0:T(8,128)}, u32[]{:S(2)}) copy-start(f32[1,256,1024]{2,1,0:T(8,128)} %copy-done.4) | copy-start | bytes 3145732
  608.3 14.1 %collective-permute-start.2 = (bf16[208,1024]{1,0:T(8,128)(2,1)S(1)}, bf16[208,1024]{1,0:T(8,128)(2,1)S(1)}, u32[]{:S(2)}, u32[]{:S(2)}) collective-permute-start(bf16[208,1024]{1,0:T(8,128)(2,1)S(1)} %dynamic-slice_bitcast_fusion.1), channel_id=1, source_target_pairs={{0,68},{68,0},{4,64},{64,4},{1,69},{69,1},{5,65},{65,5},{2,70},{70... | collective-permute-start | bytes 1277960 | tf_op jit(solution)/shard_map/ppermute | solution.py:224
  622.4 12.9 %collective-permute-start.9 = (bf16[64,6656]{1,0:T(8,128)(2,1)S(1)}, bf16[64,6656]{1,0:T(8,128)(2,1)S(1)}, u32[]{:S(2)}, u32[]{:S(2)}) collective-permute-start(bf16[64,6656]{1,0:T(8,128)(2,1)S(1)} %add_convert_fusion.1), channel_id=1, source_target_pairs={{0,4},{1,5},{2,6},{3,7},{4,0},{5,1},{6,2},{7,3},{8,12},{9,13},{10,... | collective-permute-start | bytes 2555912 | tf_op jit(solution)/shard_map/ppermute | solution.py:232
  622.6 11.3 %collective-permute-start.3 = (bf16[208,1024]{1,0:T(8,128)(2,1)S(1)}, bf16[208,1024]{1,0:T(8,128)(2,1)S(1)}, u32[]{:S(2)}, u32[]{:S(2)}) collective-permute-start(bf16[208,1024]{1,0:T(8,128)(2,1)S(1)} %fusion.24), channel_id=1, source_target_pairs={{0,1},{1,0},{2,3},{3,2},{4,5},{5,4},{6,7},{7,6},{8,9},{9,8},{10,11... | collective-permute-start | bytes 1277960 | tf_op jit(solution)/shard_map/ppermute | solution.py:232
  634.1 9.7 %collective-permute-start.4 = (bf16[208,1024]{1,0:T(8,128)(2,1)S(1)}, bf16[208,1024]{1,0:T(8,128)(2,1)S(1)}, u32[]{:S(2)}, u32[]{:S(2)}) collective-permute-start(bf16[208,1024]{1,0:T(8,128)(2,1)S(1)} %add_convert_fusion.5), channel_id=1, source_target_pairs={{0,2},{1,3},{2,0},{3,1},{4,6},{5,7},{6,4},{7,5},{8,10},{9,11},{10,... | collective-permute-start | bytes 1277960 | tf_op jit(solution)/shard_map/ppermute | solution.py:232
  643.9 8.2 %collective-permute-start.5 = (bf16[208,1024]{1,0:T(8,128)(2,1)S(1)}, bf16[208,1024]{1,0:T(8,128)(2,1)S(1)}, u32[]{:S(2)}, u32[]{:S(2)}) collective-permute-start(bf16[208,1024]{1,0:T(8,128)(2,1)S(1)} %add_convert_fusion.4), channel_id=1, source_target_pairs={{0,4},{1,5},{2,6},{3,7},{4,0},{5,1},{6,2},{7,3},{8,12},{9,13},{10,... | collective-permute-start | bytes 1277960 | tf_op jit(solution)/shard_map/ppermute | solution.py:232
  (6 other events, 6.5 us)
Sparse Core Ops, SparseCore 0:
  22.9 35.6 all-gather.4
  60.3 104.7 all-gather.6
  302.2 106.8 reduce-scatter.3
  411.3 41.7 reduce-scatter.7
  508.1 73.3 reduce-scatter.5

commit v15 on v14

--- a/solution.py
+++ b/solution.py
@@ -280,21 +280,12 @@
             [key_weight, value_weight, gain_block(prenorm_gain, midnorm_gain, width)], axis=0
         )
     )
-    rest_pair = z_exchange(
-        jnp.concatenate(
-            [
-                gate_weight,
-                up_weight,
-                down_weight.reshape(w_rows, ff),
-                query_weight,
-                out_weight,
-            ],
-            axis=1,
-        )
-    )
+    qod_pair = z_exchange(jnp.concatenate([query_weight, out_weight, down_weight], axis=0))
+    gate_up_pair = z_exchange(jnp.concatenate([gate_weight, up_weight], axis=1))
     kv_wall = yc_gather(kv_pair)
-    rest_pair, kv_wall = lax.optimization_barrier((rest_pair, kv_wall))
-    rest_wall = yc_gather(rest_pair)
+    qod_pair, gate_up_pair, kv_wall = lax.optimization_barrier((qod_pair, gate_up_pair, kv_wall))
+    qod_wall = yc_gather(qod_pair)
+    gate_up_mat = yc_gather(gate_up_pair).reshape(n_fsdp * w_rows, 2 * ff)
 
     key_mat = kv_wall[:, 0:w_rows, :].reshape(n_fsdp * w_rows, width)
     value_mat = kv_wall[:, w_rows:2 * w_rows, :].reshape(n_fsdp * w_rows, width)
@@ -302,13 +293,9 @@
     midnorm_full = from_gathered(
         kv_wall[:, 2 * w_rows, g_len:2 * g_len].reshape(n_fsdp * g_len), g_len
     )
-    gate_mat = rest_wall[:, :, 0:ff].reshape(n_fsdp * w_rows, ff)
-    upper_mat = rest_wall[:, :, ff:2 * ff].reshape(n_fsdp * w_rows, ff)
-    down_mat = (
-        rest_wall[:, :, 2 * ff:3 * ff].reshape(n_fsdp, d_rows, width).reshape(n_fsdp * d_rows, width)
-    )
-    query_mat = rest_wall[:, :, 3 * ff:3 * ff + width].reshape(n_fsdp * w_rows, width)
-    out_mat = rest_wall[:, :, 3 * ff + width:].reshape(n_fsdp * w_rows, width)
+    query_mat = qod_wall[:, 0:w_rows, :].reshape(n_fsdp * w_rows, width)
+    out_mat = qod_wall[:, w_rows:2 * w_rows, :].reshape(n_fsdp * w_rows, width)
+    down_mat = qod_wall[:, 2 * w_rows:, :].reshape(n_fsdp * d_rows, width)
 
     tokens_wide = tokens.astype(jnp.float32)
     first_wide = first_value.astype(jnp.float32)
@@ -343,8 +330,9 @@
     normed_two, inverse_two = norm_apply(middle, midnorm_full.astype(jnp.float32))
     normed_two = normed_two.astype(jnp.bfloat16)
     normed_two_g = to_gathered(normed_two, w_rows)
-    gate = jnp.dot(normed_two_g, gate_mat, preferred_element_type=jnp.float32)
-    upper = jnp.dot(normed_two_g, upper_mat, preferred_element_type=jnp.float32)
+    gate_up = jnp.dot(normed_two_g, gate_up_mat, preferred_element_type=jnp.float32)
+    gate = gate_up[..., :ff]
+    upper = gate_up[..., ff:]
     hidden = (jax.nn.silu(gate) * upper).astype(jnp.bfloat16)
     hidden_g = to_gathered(hidden, d_rows)
     branch = jnp.dot(hidden_g, down_mat, preferred_element_type=jnp.float32)
@@ -359,17 +347,12 @@
     sigma = jax.nn.sigmoid(gate)
     gate_back = (hidden_back * upper * sigma * (1.0 + gate * (1.0 - sigma))).astype(jnp.bfloat16)
     upper_back = (hidden_back * gate * sigma).astype(jnp.bfloat16)
-    gate_total = jnp.einsum(
-        "srd,srf->df", normed_two_g, gate_back, preferred_element_type=jnp.float32
-    )
-    upper_total = jnp.einsum(
-        "srd,srf->df", normed_two_g, upper_back, preferred_element_type=jnp.float32
+    gate_up_back = jnp.concatenate([gate_back, upper_back], axis=-1)
+    gate_up_total = jnp.einsum(
+        "srd,srf->df", normed_two_g, gate_up_back, preferred_element_type=jnp.float32
     )
     normed_two_back = jnp.einsum(
-        "srf,df->srd", gate_back, gate_mat, preferred_element_type=jnp.float32
-    )
-    normed_two_back = normed_two_back + jnp.einsum(
-        "srf,df->srd", upper_back, upper_mat, preferred_element_type=jnp.float32
+        "srf,df->srd", gate_up_back, gate_up_mat, preferred_element_type=jnp.float32
     )
     normed_two_back = from_gathered(normed_two_back, w_rows)
     middle_norm_back, midnorm_total = norm_back(
@@ -385,8 +368,7 @@
     )
     mlp_grads = jnp.concatenate(
         [
-            gate_total.reshape(n_fsdp, w_rows, ff),
-            upper_total.reshape(n_fsdp, w_rows, ff),
+            gate_up_total.reshape(n_fsdp, w_rows, 2 * ff),
             out_total.reshape(n_fsdp, w_rows, width),
         ],
         axis=2,

time: 668 us -> 635 us (0.951)
  local copies, waits for them, and re-layouts: 104 us -> 67.4 us
  waiting for transfers between devices: 274 us -> 285 us
  matrix products: 53.4 us -> 44.2 us
    another operation x1 -> x0, local copies, waits for them, and re-layouts: 11.8 us -> none  [body(): rest_wall[:, :, 2 * ff:3 * ff].reshape(n_fsdp, d_rows, width)]
    dot_general x1 -> x0, local copies, waits for them, and re-layouts: 11.8 us -> none  [body(): jnp.einsum('sre,fe->srf', cot_low, down_mat, preferred_element_type=jnp.f...]
    ppermute x9, waiting for transfers between devices: 40.4 us -> 51.7 us  [ctx_allreduce(): other = lax.ppermute(total, CTX, [(j, j ^ step) for j in range(n_ctx)])]
    slice x2, local copies, waits for them, and re-layouts: 15.5 us -> 7.51 us  [the longest x1 4.13 us: body(): out_mat = qod_wall[:, w_rows:2 * w_rows, :].reshape(n_fsdp * w_rows, width)]
    dot_general x6 -> x3, matrix products: 21.4 us -> 15.5 us  [the longest x1 6.37 us: body(): jnp.dot(normed_two_g, gate_up_mat, preferred_element_type=jnp.float32)]
    ppermute x2 -> x3, waiting for transfers between devices: 35.9 us -> 34.3 us  [z_exchange(): return zh_pair(pack, lax.ppermute(pack, ('zh', 'zl'), Z_CROSS))]
  transfers between devices with their start and end apart: 21 -> 23, of which waited for: 12 -> 13; matrix products, arithmetic and copies ran while one was open for 15% -> 18% of each run, Pallas kernels for 7% -> 11%
where the time goes in v15:
time: 635 us; the launch traced here: 628 us
  waiting for transfers between devices  285 us (45%)
  starting transfers between devices  99.1 us (16%)
  Pallas kernels  67.6 us (11%)
  local copies, waits for them, and re-layouts  67.4 us (11%)
  other arithmetic  49.7 us (8%)
  matrix products  44.2 us (7%)
  between operations  15.3 us (2%)
    all_to_all x1, waiting for transfers between devices, body(): lax.all_to_all(jnp.broadcast_to(kv_own[None], (n_ctx, rows, 2 * width)),...  92.4 us
    all_to_all x1, waiting for transfers between devices, body(): lax.all_to_all(kv_back.reshape(n_ctx, rows, 2 * width), CTX, 0, 0, tiled=...  84.8 us
    ppermute x9, waiting for transfers between devices, ctx_allreduce(): other = lax.ppermute(total, CTX, [(j, j ^ step) for j in range(n_ctx)])  51.7 us
    ppermute x9, starting transfers between devices, ctx_allreduce(): other = lax.ppermute(total, CTX, [(j, j ^ step) for j in range(n_ctx)])  43.3 us
    pallas_call x1, Pallas kernels, attention_backward(): pl.pallas_call(functools.partial(attn_bwd_kernel, head_dim, scale), out_s...  43.2 us
    all_to_all x1, starting transfers between devices, body(): lax.all_to_all(kv_back.reshape(n_ctx, rows, 2 * width), CTX, 0, 0, tiled=...  35.7 us
    ppermute x3, waiting for transfers between devices, z_exchange(): return zh_pair(pack, lax.ppermute(pack, ('zh', 'zl'), Z_CROSS))  34.3 us
    pallas_call x1, Pallas kernels, attention_forward(): pl.pallas_call(functools.partial(attn_fwd_kernel, head_dim, scale), out_s...  24.4 us
  transfers between devices with their start and end apart: 23, of which 13 were waited for; matrix products, arithmetic and copies ran while one was open for 18% of the time, Pallas kernels for 11%

profile of v15, /device:TPU:0, one launch (start us, length us, event | category | flops | bytes accessed | tf_op | source)
XLA Modules:
  0.0 628.2 jit_solution(11419195306591604996)
XLA Ops:
  9.1 4.2 collective-permute-start.2
  13.3 7.0 %collective-permute-done.2 = bf16[144,1024]{1,0:T(8,128)(2,1)S(1)} collective-permute-done((bf16[144,1024]{1,0:T(8,128)(2,1)S(1)}, bf16[144,1024]{1,0:T(8,128)(2,1)S(1)}, u32[]{:S(2)}, u32[]{:S(2)}) %collective-permute-start.2) | collective-permute-done | bytes 294944 | tf_op jit(solution)/shard_map/ppermute | solution.py:198
  22.5 3.0 collective-permute-start
  26.0 14.8 %collective-permute-done = bf16[304,1024]{1,0:T(8,128)(2,1)S(1)} collective-permute-done((bf16[304,1024]{1,0:T(8,128)(2,1)S(1)}, bf16[304,1024]{1,0:T(8,128)(2,1)S(1)}, u32[]{:S(2)}, u32[]{:S(2)}) %collective-permute-start) | collective-permute-done | bytes 622624 | tf_op jit(solution)/shard_map/ppermute | solution.py:198
  42.0 12.5 %collective-permute-done.1 = bf16[64,5632]{1,0:T(8,128)(2,1)S(1)} collective-permute-done((bf16[64,5632]{1,0:T(8,128)(2,1)S(1)}, bf16[64,5632]{1,0:T(8,128)(2,1)S(1)}, u32[]{:S(2)}, u32[]{:S(2)}) %collective-permute-start.1) | collective-permute-done | bytes 720928 | tf_op jit(solution)/shard_map/ppermute | solution.py:198
  55.8 2.3 all-gather.7.cloned.1.call-done
  60.8 4.4 fusion.52
  65.2 4.5 copy.163
  69.7 2.5 convolution_bitcast_fusion.5
  73.4 1.8 fusion.13
  75.4 4.3 broadcast_in_dim.72
  79.7 5.4 all-to-all-start
  87.6 92.4 %all-to-all-done = bf16[8,256,2048]{2,1,0:T(8,128)(2,1)} async-done(((bf16[8,256,2048]{2,1,0:T(8,128)(2,1)}), bf16[8,256,2048]{2,1,0:T(8,128)(2,1)}, u32[]{:S(2)}, u32[]{:S(2)}) %all-to-all-start) | async-done | bytes 8388640 | tf_op jit(solution)/shard_map/all_to_all | solution.py:316
  180.0 4.1 fusion.51
  184.1 3.9 copy.166
  188.0 2.3 convolution_bitcast_fusion.3
  190.8 24.4 %shard_map.229 = bf16[256,1024]{1,0:T(8,128)(2,1)S(1)} custom-call(s32[2]{0:T(128)S(1)} %pad_add_fusion.meta_ref, bf16[256,1024]{1,0:T(8,128)(2,1)S(1)} %copy.168.q_ref, bf16[2048,2048]{1,0:T(8,128)(2,1)} %bitcast.24.k_ref.v_ref, bf16[2048,2048]{1,0:T(8,128)(2,1)} %bitcast.24.k_ref.v_ref), custom_call_target="tpu_custom_call" | custom-call | flops 2147483648 | bytes 9437184 | tf_op jit(solution)/shard_map/pallas_call | solution.py:80
  216.2 1.9 copy.170
  218.1 3.4 slice.116
  221.5 1.8 convolution_bitcast_fusion.1
  223.9 1.8 copy.176
  225.7 3.4 copy.177
  229.1 1.9 multiply_reduce_fusion.2
  232.9 2.0 copy.172
  234.9 1.9 copy.173
  236.8 6.4 %convolution_bitcast_fusion = f32[1,256,5632]{2,1,0:T(8,128)S(1)} fusion(bf16[256,1024]{0,1:T(8,128)(2,1)} %bitcast.247, bf16[1024,5632]{1,0:T(8,128)(2,1)} %bitcast.238), kind=kOutput, calls=%fused_computation.5 | convolution fusion | flops 2952790016 | bytes 17825792 | tf_op jit(solution)/shard_map/dot_general | solution.py:333
  243.2 3.1 multiply_convert_fusion.1
  246.4 3.2 fusion.6
  250.6 2.5 copy.180
  253.1 2.0 multiply_reduce_fusion
  255.3 1.6 subtract_add_fusion
  257.3 6.0 convolution_convert_fusion
  264.0 11.2 %pad_maximum_fusion = bf16[8,128,6656]{2,1,0:T(8,128)(2,1)} fusion(bf16[8,128,1024]{2,1,0:T(8,128)(2,1)S(1)} %convolution_convert_fusion.2, bf16[8,128,5632]{2,1,0:T(8,128)(2,1)} %convolution_convert_fusion), kind=kLoop, calls=%fused_computation.2 | loop fusion | flops 27262976 | bytes 27262976 | tf_op jit(solution)/shard_map/concatenate | solution.py:369
  275.2 2.8 convolution_convert_fusion.6
  279.5 43.2 %shard_map.230 = (f32[256,1024]{1,0:T(8,128)S(1)}, bf16[2048,2048]{1,0:T(8,128)(2,1)}) custom-call(s32[2]{0:T(128)S(1)} %pad_add_fusion.meta_ref, bf16[256,1024]{1,0:T(8,128)(2,1)S(1)} %copy.168.q_ref, bf16[2048,2048]{1,0:T(8,128)(2,1)} %bitcast.24.k_ref.v_ref, bf16[2048,2048]{1,0:T(8,128)(2,1)} %bitcast.24.k_ref.v_ref, bf16[256,1024]{1,0:T(8,128)(2,1)S(1)} %copy.184.do_ref), custom_call_target="tpu_custom_call" | custom-call | flops 5368709120 | bytes 19398656 | tf_op jit(solution)/shard_map/pallas_call | solution.py:108
  322.7 35.7 %all-to-all-start.1 = ((bf16[8,256,2048]{2,1,0:T(8,128)(2,1)}), bf16[8,256,2048]{2,1,0:T(8,128)(2,1)}, u32[]{:S(2)}, u32[]{:S(2)}) async-start(bf16[8,256,2048]{2,1,0:T(8,128)(2,1)} %bitcast.245), calls=%async_computation.1 | async-start | bytes 16777216 | tf_op jit(solution)/shard_map/all_to_all | solution.py:389
  358.4 1.7 copy.174
  360.2 1.5 copy.175
  361.7 4.2 convolution_convert_fusion.1
  367.4 84.8 %all-to-all-done.1 = bf16[8,256,2048]{2,1,0:T(8,128)(2,1)} async-done(((bf16[8,256,2048]{2,1,0:T(8,128)(2,1)}), bf16[8,256,2048]{2,1,0:T(8,128)(2,1)}, u32[]{:S(2)}, u32[]{:S(2)}) %all-to-all-start.1) | async-done | bytes 8388640 | tf_op jit(solution)/shard_map/all_to_all | solution.py:389
  452.2 5.3 convert_reduce_fusion
  457.5 1.8 copy.186
  459.3 2.8 slice_multiply_fusion
  466.3 1.7 convolution_add_fusion
  468.0 1.6 copy.188
  470.6 1.6 copy.190
  475.2 3.3 fusion.1
  479.8 2.5 collective-permute-start.7
  484.2 18.8 %collective-permute-done.7 = bf16[64,6656]{1,0:T(8,128)(2,1)} collective-permute-done((bf16[64,6656]{1,0:T(8,128)(2,1)S(1)}, bf16[64,6656]{1,0:T(8,128)(2,1)}, u32[]{:S(2)}, u32[]{:S(2)}) %collective-permute-start.7) | collective-permute-done | bytes 852000 | tf_op jit(solution)/shard_map/ppermute | solution.py:224
  503.0 1.6 fusion.5
  504.6 29.2 %collective-permute-start.8 = (bf16[64,6656]{1,0:T(8,128)(2,1)S(1)}, bf16[64,6656]{1,0:T(8,128)(2,1)S(1)}, u32[]{:S(2)}, u32[]{:S(2)}) collective-permute-start(bf16[64,6656]{1,0:T(8,128)(2,1)S(1)} %fusion.5), channel_id=1, source_target_pairs={{0,1},{1,0},{2,3},{3,2},{4,5},{5,4},{6,7},{7,6},{8,9},{9,8},{10,11... | collective-permute-start | bytes 2555912 | tf_op jit(solution)/shard_map/ppermute | solution.py:232
  533.9 3.4 collective-permute-start.12
  537.4 18.0 %collective-permute-done.12 = bf16[176,1024]{1,0:T(8,128)(2,1)S(1)} collective-permute-done((bf16[176,1024]{1,0:T(8,128)(2,1)S(1)}, bf16[176,1024]{1,0:T(8,128)(2,1)S(1)}, u32[]{:S(2)}, u32[]{:S(2)}) %collective-permute-start.12) | collective-permute-done | bytes 360480 | tf_op jit(solution)/shard_map/ppermute | solution.py:232
  555.5 8.4 %collective-permute-start.13 = (bf16[176,1024]{1,0:T(8,128)(2,1)S(1)}, bf16[176,1024]{1,0:T(8,128)(2,1)}, u32[]{:S(2)}, u32[]{:S(2)}) collective-permute-start(bf16[176,1024]{1,0:T(8,128)(2,1)S(1)} %add_convert_fusion.8), channel_id=1, source_target_pairs={{0,2},{1,3},{2,0},{3,1},{4,6},{5,7},{6,4},{7,5},{8,10},{9,11},{10,... | collective-permute-start | bytes 1081352 | tf_op jit(solution)/shard_map/ppermute | solution.py:232
  565.0 5.2 fusion.14
  571.5 1.8 collective-permute-done.13
  575.7 3.3 collective-permute-start.3
  579.0 9.9 %collective-permute-done.9 = bf16[64,6656]{1,0:T(8,128)(2,1)} collective-permute-done((bf16[64,6656]{1,0:T(8,128)(2,1)}, bf16[64,6656]{1,0:T(8,128)(2,1)}, u32[]{:S(2)}, u32[]{:S(2)}) %collective-permute-start.9) | collective-permute-done | bytes 852000 | tf_op jit(solution)/shard_map/ppermute | solution.py:232
  588.9 1.6 add_convert_fusion.1
  590.9 1.4 fusion.21
  593.2 8.1 %collective-permute-done.4 = bf16[208,1024]{1,0:T(8,128)(2,1)S(1)} collective-permute-done((bf16[208,1024]{1,0:T(8,128)(2,1)S(1)}, bf16[208,1024]{1,0:T(8,128)(2,1)S(1)}, u32[]{:S(2)}, u32[]{:S(2)}) %collective-permute-start.4) | collective-permute-done | bytes 426016 | tf_op jit(solution)/shard_map/ppermute | solution.py:232
  601.5 1.8 collective-permute-start.5
  604.2 7.0 %collective-permute-done.5 = bf16[208,1024]{1,0:T(8,128)(2,1)S(1)} collective-permute-done((bf16[208,1024]{1,0:T(8,128)(2,1)S(1)}, bf16[208,1024]{1,0:T(8,128)(2,1)S(1)}, u32[]{:S(2)}, u32[]{:S(2)}) %collective-permute-start.5) | collective-permute-done | bytes 426016 | tf_op jit(solution)/shard_map/ppermute | solution.py:232
  612.7 6.9 %collective-permute-done.6 = bf16[208,1024]{1,0:T(8,128)(2,1)S(1)} collective-permute-done((bf16[208,1024]{1,0:T(8,128)(2,1)S(1)}, bf16[208,1024]{1,0:T(8,128)(2,1)S(1)}, u32[]{:S(2)}, u32[]{:S(2)}) %collective-permute-start.6) | collective-permute-done | bytes 426016 | tf_op jit(solution)/shard_map/ppermute | solution.py:232
  (201 shorter events, 44.3 us)
Async XLA Ops:
  7.2 15.2 %copy-start.37 = (bf16[64,1024]{1,0:T(8,128)(2,1)S(1)}, bf16[64,1024]{1,0:T(8,128)(2,1)}, u32[]{:S(2)}) copy-start(bf16[64,1024]{1,0:T(8,128)(2,1)} %param.16) | copy-start | bytes 393220
  7.2 15.2 %copy-start.38 = (bf16[64,1024]{1,0:T(8,128)(2,1)S(1)}, bf16[64,1024]{1,0:T(8,128)(2,1)}, u32[]{:S(2)}) copy-start(bf16[64,1024]{1,0:T(8,128)(2,1)} %param.19) | copy-start | bytes 393220
  7.2 15.2 %copy-start.34 = (bf16[176,1024]{1,0:T(8,128)(2,1)S(1)}, bf16[176,1024]{1,0:T(8,128)(2,1)}, u32[]{:S(2)}) copy-start(bf16[176,1024]{1,0:T(8,128)(2,1)} %param.22) | copy-start | bytes 1081348
  7.2 50.9 %all-gather.7.cloned.1.call-start = ((), (), s32[]{:S(2)}) async-start(), calls=%async_computation.8 | async-start | bytes 5308416 | tf_op jit(solution)/shard_map/all_gather | solution.py:202
  9.1 16.4 %copy-start.35 = (bf16[64,2816]{1,0:T(8,128)(2,1)S(1)}, bf16[64,2816]{1,0:T(8,128)(2,1)}, u32[]{:S(2)}) copy-start(bf16[64,2816]{1,0:T(8,128)(2,1)} %param.20) | copy-start | bytes 1081348
  9.1 11.2 %collective-permute-start.2 = (bf16[144,1024]{1,0:T(8,128)(2,1)S(1)}, bf16[144,1024]{1,0:T(8,128)(2,1)S(1)}, u32[]{:S(2)}, u32[]{:S(2)}) collective-permute-start(bf16[144,1024]{1,0:T(8,128)(2,1)S(1)} %fusion.38), channel_id=1, source_target_pairs={{0,68},{68,0},{4,64},{64,4},{1,69},{69,1},{5,65},{65,5},{2,70},{70... | collective-permute-start | bytes 884744 | tf_op jit(solution)/shard_map/ppermute | solution.py:198
  21.4 4.1 copy-start.36
  22.3 157.7 %all-gather.9.cloned.1.call-start = ((), (), s32[]{:S(2)}) async-start(), calls=%async_computation.9 | async-start | bytes 11206656 | tf_op jit(solution)/shard_map/all_gather | solution.py:202
  22.5 18.3 %collective-permute-start = (bf16[304,1024]{1,0:T(8,128)(2,1)S(1)}, bf16[304,1024]{1,0:T(8,128)(2,1)S(1)}, u32[]{:S(2)}, u32[]{:S(2)}) collective-permute-start(bf16[304,1024]{1,0:T(8,128)(2,1)S(1)} %constant_dynamic-update-slice_fusion), channel_id=1, source_target_pairs={{0,68},{68,0},{4,64},{64,4},{1,69},{69,1},{5,65},{65,5},{2,70},{70... | collective-permute-start | bytes 1867784 | tf_op jit(solution)/shard_map/ppermute | solution.py:198
  25.6 28.9 %collective-permute-start.1 = (bf16[64,5632]{1,0:T(8,128)(2,1)S(1)}, bf16[64,5632]{1,0:T(8,128)(2,1)S(1)}, u32[]{:S(2)}, u32[]{:S(2)}) collective-permute-start(bf16[64,5632]{1,0:T(8,128)(2,1)S(1)} %constant_dynamic-update-slice_fusion.3), channel_id=1, source_target_pairs={{0,68},{68,0},{4,64},{64,4},{1,69},{69,1},{5,65},{65,5},{2,70},{70... | collective-permute-start | bytes 2162696 | tf_op jit(solution)/shard_map/ppermute | solution.py:198
  54.5 4.4 copy-start.9
  58.1 178.7 %all-gather.11.cloned.1.call-start = ((), (), s32[]{:S(2)}) async-start(), calls=%async_computation.10 | async-start | bytes 12976128 | tf_op jit(solution)/shard_map/all_gather | solution.py:202
  60.8 127.3 %copy-start.11 = (bf16[1,256,8,2,64]{1,4,3,2,0:T(8,128)(2,1)}, bf16[1,256,8,2,64]{1,4,3,2,0:T(8,128)(2,1)S(1)}, u32[]{:S(2)}) copy-start(bf16[1,256,8,2,64]{1,4,3,2,0:T(8,128)(2,1)S(1)} %copy.161) | copy-start | bytes 1572868
  65.2 8.3 %copy-start = (bf16[16,64,1024]{2,1,0:T(8,128)(2,1)}, bf16[16,64,1024]{2,1,0:T(8,128)(2,1)S(1)}, u32[]{:S(2)}) copy-start(bf16[16,64,1024]{2,1,0:T(8,128)(2,1)S(1)} %get-tuple-element.90) | copy-start | bytes 6291460
  73.4 1.8 copy-start.31
  79.7 5.7 copy-start.39
  79.7 5.7 copy-start.40
  79.7 100.3 %all-to-all-start = ((bf16[8,256,2048]{2,1,0:T(8,128)(2,1)}), bf16[8,256,2048]{2,1,0:T(8,128)(2,1)}, u32[]{:S(2)}, u32[]{:S(2)}) async-start(bf16[8,256,2048]{2,1,0:T(8,128)(2,1)} %broadcast_in_dim.72), calls=%async_computation | async-start | bytes 16777216 | tf_op jit(solution)/shard_map/all_to_all | solution.py:316
  85.1 393.4 %reduce-scatter.4.cloned.1.call-start = ((), (), s32[]{:S(2)}) async-start(), calls=%async_computation.5 | async-start | bytes 15335424 | tf_op jit(solution)/shard_map/reduce_scatter | solution.py:214
  218.1 3.4 copy-start.29
  221.5 2.5 copy-start.23
  225.7 3.4 copy-start.10
  236.8 6.4 %copy-start.13 = (f32[1,256,2816]{2,1,0:T(8,128)S(1)}, f32[1,256,2816]{2,1,0:T(8,128)}, u32[]{:S(2)}) copy-start(f32[1,256,2816]{2,1,0:T(8,128)} %copy.177) | copy-start | bytes 8650756
  236.8 9.5 %slice-start = ((s8[11534336]{0:T(1024)(128)(4,1)}), s8[4194304]{0:T(1024)(128)(4,1)S(1)}, s32[]{:S(2)}) async-start(s8[11534336]{0:T(1024)(128)(4,1)} %bitcast.239), calls=%async_computation.11 | async-start | bytes 8388608
  236.8 9.5 %slice-start.1 = ((s8[11534336]{0:T(1024)(128)(4,1)}), s8[4194304]{0:T(1024)(128)(4,1)S(1)}, s32[]{:S(2)}) async-start(s8[11534336]{0:T(1024)(128)(4,1)} %bitcast.239), calls=%async_computation.12 | async-start | bytes 8388608
  243.2 3.1 slice-start.2
  246.3 3.2 copy-start.19
  246.3 3.2 copy-start.21
  253.1 2.0 copy-start.7
  253.1 2.2 copy-start.14
  255.1 1.8 copy-start.17
  255.1 1.8 copy-start.20
  255.1 2.1 copy-start.22
  256.9 6.4 %copy-start.4 = (f32[1,256,1024]{2,1,0:T(8,128)}, f32[1,256,1024]{2,1,0:T(8,128)S(1)}, u32[]{:S(2)}) copy-start(f32[1,256,1024]{2,1,0:T(8,128)S(1)} %subtract_add_fusion) | copy-start | bytes 3145732
  257.3 6.0 copy-start.24
  322.7 35.7 %copy-start.18 = (bf16[1,256,2816]{2,1,0:T(8,128)(2,1)S(1)}, bf16[1,256,2816]{2,1,0:T(8,128)(2,1)}, u32[]{:S(2)}) copy-start(bf16[1,256,2816]{2,1,0:T(8,128)(2,1)} %get-tuple-element.86) | copy-start | bytes 4325380
  322.7 129.4 %all-to-all-start.1 = ((bf16[8,256,2048]{2,1,0:T(8,128)(2,1)}), bf16[8,256,2048]{2,1,0:T(8,128)(2,1)}, u32[]{:S(2)}, u32[]{:S(2)}) async-start(bf16[8,256,2048]{2,1,0:T(8,128)(2,1)} %bitcast.245), calls=%async_computation.1 | async-start | bytes 16777216 | tf_op jit(solution)/shard_map/all_to_all | solution.py:389
  358.4 123.9 %reduce-scatter.8.cloned.1.call-start = ((), (), s32[]{:S(2)}) async-start(), calls=%async_computation.7 | async-start | bytes 6488064 | tf_op jit(solution)/shard_map/reduce_scatter | solution.py:214
  361.7 4.2 copy-start.15
  365.9 208.6 %reduce-scatter.6.cloned.1.call-start = ((), (), s32[]{:S(2)}) async-start(), calls=%async_computation.6 | async-start | bytes 7667712 | tf_op jit(solution)/shard_map/reduce_scatter | solution.py:214
  459.3 2.8 copy-start.27
  462.1 1.8 copy-start.3
  462.6 2.9 copy-start.25
  462.6 2.1 copy-start.2
  464.7 1.6 copy-start.1
  470.6 2.2 copy-start.12
  479.8 23.2 %collective-permute-start.7 = (bf16[64,6656]{1,0:T(8,128)(2,1)S(1)}, bf16[64,6656]{1,0:T(8,128)(2,1)}, u32[]{:S(2)}, u32[]{:S(2)}) collective-permute-start(bf16[64,6656]{1,0:T(8,128)(2,1)S(1)} %dynamic-slice_bitcast_fusion), channel_id=1, source_target_pairs={{0,68},{68,0},{4,64},{64,4},{1,69},{69,1},{5,65},{65,5},{2,70},{70... | collective-permute-start | bytes 2555912 | tf_op jit(solution)/shard_map/ppermute | solution.py:224
  482.2 51.6 %copy-start.33 = (bf16[1,352,1024]{2,1,0:T(8,128)(2,1)S(1)}, bf16[1,352,1024]{2,1,0:T(8,128)(2,1)}, u32[]{:S(2)}) copy-start(bf16[1,352,1024]{2,1,0:T(8,128)(2,1)} %reduce-scatter.8.cloned.1.call-done) | copy-start | bytes 2162692
  483.3 50.5 %collective-permute-start.11 = (bf16[176,1024]{1,0:T(8,128)(2,1)S(1)}, bf16[176,1024]{1,0:T(8,128)(2,1)S(1)}, u32[]{:S(2)}, u32[]{:S(2)}) collective-permute-start(bf16[176,1024]{1,0:T(8,128)(2,1)S(1)} %dynamic-slice_bitcast_fusion.2), channel_id=1, source_target_pairs={{0,68},{68,0},{4,64},{64,4},{1,69},{69,1},{5,65},{65,5},{2,70},{70... | collective-permute-start | bytes 1081352 | tf_op jit(solution)/shard_map/ppermute | solution.py:224
  504.6 60.4 %copy-start.8 = (f32[1,256,1024]{2,1,0:T(8,128)S(1)}, f32[1,256,1024]{2,1,0:T(8,128)}, u32[]{:S(2)}) copy-start(f32[1,256,1024]{2,1,0:T(8,128)} %copy-done.6) | copy-start | bytes 3145732
  504.6 60.4 %copy-start.16 = (bf16[1,256,8,2,176]{1,4,3,2,0:T(8,128)(2,1)S(1)}, bf16[1,256,8,2,176]{1,4,3,2,0:T(8,128)(2,1)}, u32[]{:S(2)}) copy-start(bf16[1,256,8,2,176]{1,4,3,2,0:T(8,128)(2,1)} %copy-done.15) | copy-start | bytes 4325380
  504.6 59.3 %collective-permute-start.8 = (bf16[64,6656]{1,0:T(8,128)(2,1)S(1)}, bf16[64,6656]{1,0:T(8,128)(2,1)S(1)}, u32[]{:S(2)}, u32[]{:S(2)}) collective-permute-start(bf16[64,6656]{1,0:T(8,128)(2,1)S(1)} %fusion.5), channel_id=1, source_target_pairs={{0,1},{1,0},{2,3},{3,2},{4,5},{5,4},{6,7},{7,6},{8,9},{9,8},{10,11... | collective-permute-start | bytes 2555912 | tf_op jit(solution)/shard_map/ppermute | solution.py:232
  533.9 21.4 %collective-permute-start.12 = (bf16[176,1024]{1,0:T(8,128)(2,1)S(1)}, bf16[176,1024]{1,0:T(8,128)(2,1)S(1)}, u32[]{:S(2)}, u32[]{:S(2)}) collective-permute-start(bf16[176,1024]{1,0:T(8,128)(2,1)S(1)} %fusion.29), channel_id=1, source_target_pairs={{0,1},{1,0},{2,3},{3,2},{4,5},{5,4},{6,7},{7,6},{8,9},{9,8},{10,11... | collective-permute-start | bytes 1081352 | tf_op jit(solution)/shard_map/ppermute | solution.py:232
  555.5 17.8 %collective-permute-start.13 = (bf16[176,1024]{1,0:T(8,128)(2,1)S(1)}, bf16[176,1024]{1,0:T(8,128)(2,1)}, u32[]{:S(2)}, u32[]{:S(2)}) collective-permute-start(bf16[176,1024]{1,0:T(8,128)(2,1)S(1)} %add_convert_fusion.8), channel_id=1, source_target_pairs={{0,2},{1,3},{2,0},{3,1},{4,6},{5,7},{6,4},{7,5},{8,10},{9,11},{10,... | collective-permute-start | bytes 1081352 | tf_op jit(solution)/shard_map/ppermute | solution.py:232
  565.0 24.0 %collective-permute-start.9 = (bf16[64,6656]{1,0:T(8,128)(2,1)}, bf16[64,6656]{1,0:T(8,128)(2,1)}, u32[]{:S(2)}, u32[]{:S(2)}) collective-permute-start(bf16[64,6656]{1,0:T(8,128)(2,1)} %add_convert_fusion.2), channel_id=1, source_target_pairs={{0,2},{1,3},{2,0},{3,1},{4,6},{5,7},{6,4},{7,5},{8,10},{9,11},{10,... | collective-permute-start | bytes 2555912 | tf_op jit(solution)/shard_map/ppermute | solution.py:232
  565.0 5.2 copy-start.28
  574.4 17.9 %collective-permute-start.14 = (bf16[176,1024]{1,0:T(8,128)(2,1)S(1)}, bf16[176,1024]{1,0:T(8,128)(2,1)S(1)}, u32[]{:S(2)}, u32[]{:S(2)}) collective-permute-start(bf16[176,1024]{1,0:T(8,128)(2,1)S(1)} %add_convert_fusion.7), channel_id=1, source_target_pairs={{0,4},{1,5},{2,6},{3,7},{4,0},{5,1},{6,2},{7,3},{8,12},{9,13},{10,... | collective-permute-start | bytes 1081352 | tf_op jit(solution)/shard_map/ppermute | solution.py:232
  574.6 16.1 %copy-start.32 = (bf16[1,416,1024]{2,1,0:T(8,128)(2,1)S(1)}, bf16[1,416,1024]{2,1,0:T(8,128)(2,1)}, u32[]{:S(2)}) copy-start(bf16[1,416,1024]{2,1,0:T(8,128)(2,1)} %reduce-scatter.6.cloned.1.call-done) | copy-start | bytes 2555908
  575.7 15.2 %copy-start.5 = (f32[1,256,1024]{2,1,0:T(8,128)S(1)}, f32[1,256,1024]{2,1,0:T(8,128)}, u32[]{:S(2)}) copy-start(f32[1,256,1024]{2,1,0:T(8,128)} %copy-done.4) | copy-start | bytes 3145732
  575.7 15.0 %collective-permute-start.3 = (bf16[208,1024]{1,0:T(8,128)(2,1)S(1)}, bf16[208,1024]{1,0:T(8,128)(2,1)S(1)}, u32[]{:S(2)}, u32[]{:S(2)}) collective-permute-start(bf16[208,1024]{1,0:T(8,128)(2,1)S(1)} %dynamic-slice_bitcast_fusion.1), channel_id=1, source_target_pairs={{0,68},{68,0},{4,64},{64,4},{1,69},{69,1},{5,65},{65,5},{2,70},{70... | collective-permute-start | bytes 1277960 | tf_op jit(solution)/shard_map/ppermute | solution.py:224
  590.5 12.8 %collective-permute-start.10 = (bf16[64,6656]{1,0:T(8,128)(2,1)S(1)}, bf16[64,6656]{1,0:T(8,128)(2,1)S(1)}, u32[]{:S(2)}, u32[]{:S(2)}) collective-permute-start(bf16[64,6656]{1,0:T(8,128)(2,1)S(1)} %add_convert_fusion.1), channel_id=1, source_target_pairs={{0,4},{1,5},{2,6},{3,7},{4,0},{5,1},{6,2},{7,3},{8,12},{9,13},{10,... | collective-permute-start | bytes 2555912 | tf_op jit(solution)/shard_map/ppermute | solution.py:232
  590.8 10.5 %collective-permute-start.4 = (bf16[208,1024]{1,0:T(8,128)(2,1)S(1)}, bf16[208,1024]{1,0:T(8,128)(2,1)S(1)}, u32[]{:S(2)}, u32[]{:S(2)}) collective-permute-start(bf16[208,1024]{1,0:T(8,128)(2,1)S(1)} %fusion.28), channel_id=1, source_target_pairs={{0,1},{1,0},{2,3},{3,2},{4,5},{5,4},{6,7},{7,6},{8,9},{9,8},{10,11... | collective-permute-start | bytes 1277960 | tf_op jit(solution)/shard_map/ppermute | solution.py:232
  601.5 9.7 %collective-permute-start.5 = (bf16[208,1024]{1,0:T(8,128)(2,1)S(1)}, bf16[208,1024]{1,0:T(8,128)(2,1)S(1)}, u32[]{:S(2)}, u32[]{:S(2)}) collective-permute-start(bf16[208,1024]{1,0:T(8,128)(2,1)S(1)} %add_convert_fusion.5), channel_id=1, source_target_pairs={{0,2},{1,3},{2,0},{3,1},{4,6},{5,7},{6,4},{7,5},{8,10},{9,11},{10,... | collective-permute-start | bytes 1277960 | tf_op jit(solution)/shard_map/ppermute | solution.py:232
  611.4 8.2 %collective-permute-start.6 = (bf16[208,1024]{1,0:T(8,128)(2,1)S(1)}, bf16[208,1024]{1,0:T(8,128)(2,1)S(1)}, u32[]{:S(2)}, u32[]{:S(2)}) collective-permute-start(bf16[208,1024]{1,0:T(8,128)(2,1)S(1)} %add_convert_fusion.4), channel_id=1, source_target_pairs={{0,4},{1,5},{2,6},{3,7},{4,0},{5,1},{6,2},{7,3},{8,12},{9,13},{10,... | collective-permute-start | bytes 1277960 | tf_op jit(solution)/shard_map/ppermute | solution.py:232
  (3 other events, 3.6 us)
Sparse Core Ops, SparseCore 0:
  22.5 35.6 all-gather.6
  59.8 56.3 all-gather.8
  117.8 63.1 all-gather.10
  275.3 107.6 reduce-scatter.3
  385.3 41.8 reduce-scatter.7
  478.7 74.0 reduce-scatter.5

commit v16 on v15

--- a/solution.py
+++ b/solution.py
@@ -223,6 +223,20 @@
     theirs = lax.dynamic_index_in_dim(halves, 1 - zh, axis=0, keepdims=False)
     got = lax.ppermute(theirs, ("zh", "zl"), Z_CROSS)
     return (mine.astype(jnp.float32) + got.astype(jnp.float32)).astype(jnp.bfloat16)
+
+
+def xor_sum(value, axes, partners):
+    got = [lax.ppermute(value[k], axes, [(j, j ^ (k + 1)) for j in range(partners)]) for k in range(3)]
+    wide = [v.astype(jnp.float32) for v in [value[3]] + got]
+    return (wide[0] + wide[1]) + (wide[2] + wide[3])
+
+
+def group_sum(halves):
+    across_x = xor_sum([halves] * 4, "x", 4).astype(jnp.bfloat16)
+    zh = lax.axis_index("zh")
+    mine = lax.dynamic_index_in_dim(across_x, zh, axis=0, keepdims=False)
+    theirs = lax.dynamic_index_in_dim(across_x, 1 - zh, axis=0, keepdims=False)
+    return xor_sum([mine, theirs, theirs, mine], ("zh", "zl"), 4)
 
 
 def ctx_allreduce(part, n_ctx):
@@ -362,9 +376,8 @@
     middle_low = middle_back.astype(jnp.bfloat16)
     out_total = jnp.einsum("srd,sre->de", mixed_low_g, middle_low, preferred_element_type=jnp.float32)
 
-    down_share = ctx_allreduce(
-        z_combine(yc_reduce_scatter(down_total.astype(jnp.bfloat16).reshape(n_fsdp, d_rows, width))),
-        n_ctx,
+    down_share = group_sum(
+        yc_reduce_scatter(down_total.astype(jnp.bfloat16).reshape(n_fsdp, d_rows, width))
     )
     mlp_grads = jnp.concatenate(
         [
@@ -439,9 +452,8 @@
         axis=1,
     ).astype(jnp.bfloat16)
     attn_grads, mlp_halves = lax.optimization_barrier((attn_grads, mlp_halves))
-    mlp_share = ctx_allreduce(z_combine(mlp_halves), n_ctx)
-    attn_share = fsdp_reduce_scatter(attn_grads)
-    attn_share = ctx_allreduce(attn_share, n_ctx)
+    mlp_share = group_sum(mlp_halves)
+    attn_share = group_sum(yc_reduce_scatter(attn_grads))
 
     def attn_grad(i):
         return attn_share[i * w_rows:(i + 1) * w_rows]

time: 635 us -> 757 us (1.19)
  waiting for transfers between devices: 285 us -> 402 us
    ppermute x12 -> x18, waiting for transfers between devices: 70.4 us -> 188 us  [xor_sum(): lax.ppermute(value[k], axes, [(j, j ^ k + 1) for j in range(partners)])]
    ppermute x12 -> x18, starting transfers between devices: 50 us -> 53.9 us  [xor_sum(): lax.ppermute(value[k], axes, [(j, j ^ k + 1) for j in range(partners)])]
  transfers between devices with their start and end apart: 23 -> 29, of which waited for: 13 -> 16; matrix products, arithmetic and copies ran while one was open for 18% -> 15% of each run, Pallas kernels for 11% -> 9%
where the time goes in v16:
time: 757 us; the launch traced here: 751 us
  waiting for transfers between devices  402 us (53%)
  starting transfers between devices  103 us (14%)
  local copies, waits for them, and re-layouts  67.7 us (9%)
  Pallas kernels  67.6 us (9%)
  other arithmetic  53.2 us (7%)
  matrix products  41.5 us (5%)
  between operations  15.5 us (2%)
    ppermute x18, waiting for transfers between devices, xor_sum(): lax.ppermute(value[k], axes, [(j, j ^ k + 1) for j in range(partners)])  188 us
    all_to_all x1, waiting for transfers between devices, body(): lax.all_to_all(jnp.broadcast_to(kv_own[None], (n_ctx, rows, 2 * width)),...  92.1 us
    all_to_all x1, waiting for transfers between devices, body(): lax.all_to_all(kv_back.reshape(n_ctx, rows, 2 * width), CTX, 0, 0, tiled=...  84.7 us
    ppermute x18, starting transfers between devices, xor_sum(): lax.ppermute(value[k], axes, [(j, j ^ k + 1) for j in range(partners)])  53.9 us
    pallas_call x1, Pallas kernels, attention_backward(): pl.pallas_call(functools.partial(attn_bwd_kernel, head_dim, scale), out_s...  43.2 us
    all_to_all x1, starting transfers between devices, body(): lax.all_to_all(kv_back.reshape(n_ctx, rows, 2 * width), CTX, 0, 0, tiled=...  35.6 us
    ppermute x3, waiting for transfers between devices, z_exchange(): return zh_pair(pack, lax.ppermute(pack, ('zh', 'zl'), Z_CROSS))  34.2 us
    pallas_call x1, Pallas kernels, attention_forward(): pl.pallas_call(functools.partial(attn_fwd_kernel, head_dim, scale), out_s...  24.4 us
  transfers between devices with their start and end apart: 29, of which 16 were waited for; matrix products, arithmetic and copies ran while one was open for 15% of the time, Pallas kernels for 9%

profile of v16, /device:TPU:0, one launch (start us, length us, event | category | flops | bytes accessed | tf_op | source)
XLA Modules:
  0.0 750.9 jit_solution(6887119833813005098)
XLA Ops:
  9.1 4.2 collective-permute-start.2
  13.3 7.0 collective-permute-done.2
  22.5 3.0 collective-permute-start
  26.0 14.8 %collective-permute-done = bf16[304,1024]{1,0:T(8,128)(2,1)S(1)} collective-permute-done((bf16[304,1024]{1,0:T(8,128)(2,1)S(1)}, bf16[304,1024]{1,0:T(8,128)(2,1)S(1)}, u32[]{:S(2)}, u32[]{:S(2)}) %collective-permute-start) | collective-permute-done | bytes 622624 | tf_op jit(solution)/shard_map/ppermute | solution.py:198
  42.0 12.5 %collective-permute-done.1 = bf16[64,5632]{1,0:T(8,128)(2,1)S(1)} collective-permute-done((bf16[64,5632]{1,0:T(8,128)(2,1)S(1)}, bf16[64,5632]{1,0:T(8,128)(2,1)S(1)}, u32[]{:S(2)}, u32[]{:S(2)}) %collective-permute-start.1) | collective-permute-done | bytes 720928 | tf_op jit(solution)/shard_map/ppermute | solution.py:198
  55.8 2.3 all-gather.7.cloned.1.call-done
  60.8 4.4 fusion.46
  65.2 4.5 copy.163
  69.7 2.5 convolution_bitcast_fusion.5
  73.5 1.8 fusion.12
  75.4 4.4 broadcast_in_dim.72
  79.8 5.4 all-to-all-start
  87.9 92.1 %all-to-all-done = bf16[8,256,2048]{2,1,0:T(8,128)(2,1)} async-done(((bf16[8,256,2048]{2,1,0:T(8,128)(2,1)}), bf16[8,256,2048]{2,1,0:T(8,128)(2,1)}, u32[]{:S(2)}, u32[]{:S(2)}) %all-to-all-start) | async-done | bytes 8388640 | tf_op jit(solution)/shard_map/all_to_all | solution.py:330
  180.0 4.1 fusion.45
  184.1 3.9 copy.166
  188.0 2.3 convolution_bitcast_fusion.3
  190.8 24.4 %shard_map.229 = bf16[256,1024]{1,0:T(8,128)(2,1)S(1)} custom-call(s32[2]{0:T(128)S(1)} %pad_add_fusion.meta_ref, bf16[256,1024]{1,0:T(8,128)(2,1)S(1)} %copy.168.q_ref, bf16[2048,2048]{1,0:T(8,128)(2,1)} %bitcast.24.k_ref.v_ref, bf16[2048,2048]{1,0:T(8,128)(2,1)} %bitcast.24.k_ref.v_ref), custom_call_target="tpu_custom_call" | custom-call | flops 2147483648 | bytes 9437184 | tf_op jit(solution)/shard_map/pallas_call | solution.py:80
  216.2 1.9 copy.170
  218.1 3.4 slice.116
  221.5 1.8 convolution_bitcast_fusion.1
  223.9 1.8 copy.176
  225.7 3.4 copy.177
  229.1 1.9 multiply_reduce_fusion.2
  232.9 2.0 copy.172
  234.9 1.9 copy.173
  236.8 6.4 convolution_bitcast_fusion
  243.2 2.9 multiply_convert_fusion.1
  246.2 3.2 fusion.5
  250.4 2.5 copy.180
  253.0 2.0 multiply_reduce_fusion
  257.1 6.0 convolution_convert_fusion
  263.8 11.2 %pad_maximum_fusion = bf16[8,128,6656]{2,1,0:T(8,128)(2,1)} fusion(bf16[8,128,1024]{2,1,0:T(8,128)(2,1)S(1)} %convolution_convert_fusion.2, bf16[8,128,5632]{2,1,0:T(8,128)(2,1)} %convolution_convert_fusion), kind=kLoop, calls=%fused_computation.2 | loop fusion | flops 27262976 | bytes 27262976 | tf_op jit(solution)/shard_map/concatenate | solution.py:382
  275.0 2.8 convolution_convert_fusion.6
  279.4 43.2 %shard_map.230 = (f32[256,1024]{1,0:T(8,128)S(1)}, bf16[2048,2048]{1,0:T(8,128)(2,1)}) custom-call(s32[2]{0:T(128)S(1)} %pad_add_fusion.meta_ref, bf16[256,1024]{1,0:T(8,128)(2,1)S(1)} %copy.168.q_ref, bf16[2048,2048]{1,0:T(8,128)(2,1)} %bitcast.24.k_ref.v_ref, bf16[2048,2048]{1,0:T(8,128)(2,1)} %bitcast.24.k_ref.v_ref, bf16[256,1024]{1,0:T(8,128)(2,1)S(1)} %copy.184.do_ref), custom_call_target="tpu_custom_call" | custom-call | flops 5368709120 | bytes 19398656 | tf_op jit(solution)/shard_map/pallas_call | solution.py:108
  322.5 35.6 %all-to-all-start.1 = ((bf16[8,256,2048]{2,1,0:T(8,128)(2,1)}), bf16[8,256,2048]{2,1,0:T(8,128)(2,1)}, u32[]{:S(2)}, u32[]{:S(2)}) async-start(bf16[8,256,2048]{2,1,0:T(8,128)(2,1)} %bitcast.242), calls=%async_computation.1 | async-start | bytes 16777216 | tf_op jit(solution)/shard_map/all_to_all | solution.py:402
  358.2 1.8 copy.174
  361.6 4.2 convolution_convert_fusion.1
  367.2 84.7 %all-to-all-done.1 = bf16[8,256,2048]{2,1,0:T(8,128)(2,1)} async-done(((bf16[8,256,2048]{2,1,0:T(8,128)(2,1)}), bf16[8,256,2048]{2,1,0:T(8,128)(2,1)}, u32[]{:S(2)}, u32[]{:S(2)}) %all-to-all-start.1) | async-done | bytes 8388640 | tf_op jit(solution)/shard_map/all_to_all | solution.py:402
  451.9 5.3 convert_reduce_fusion
  457.2 1.8 copy.186
  459.0 2.8 slice_multiply_fusion
  466.0 1.8 convolution_add_fusion
  475.0 3.3 fusion.1
  478.4 31.8 %collective-permute-start.17 = (bf16[2,176,1024]{2,1,0:T(8,128)(2,1)}, bf16[2,176,1024]{2,1,0:T(8,128)(2,1)S(1)}, u32[]{:S(2)}, u32[]{:S(2)}) collective-permute-start(bf16[2,176,1024]{2,1,0:T(8,128)(2,1)} %bitcast.282), channel_id=1, source_target_pairs={{0,3},{1,2},{2,1},{3,0},{4,7},{5,6},{6,5},{7,4},{8,11},{9,10},{10,... | collective-permute-start | bytes 2162696 | tf_op jit(solution)/shard_map/ppermute | solution.py:229
  510.3 4.0 collective-permute-start.9
  514.9 49.1 %collective-permute-done.17 = bf16[2,176,1024]{2,1,0:T(8,128)(2,1)S(1)} collective-permute-done((bf16[2,176,1024]{2,1,0:T(8,128)(2,1)}, bf16[2,176,1024]{2,1,0:T(8,128)(2,1)S(1)}, u32[]{:S(2)}, u32[]{:S(2)}) %collective-permute-start.17) | collective-permute-done | bytes 720928 | tf_op jit(solution)/shard_map/ppermute | solution.py:229
  564.2 40.0 %collective-permute-done.16 = bf16[2,176,1024]{2,1,0:T(8,128)(2,1)} collective-permute-done((bf16[2,176,1024]{2,1,0:T(8,128)(2,1)}, bf16[2,176,1024]{2,1,0:T(8,128)(2,1)}, u32[]{:S(2)}, u32[]{:S(2)}) %collective-permute-start.16) | collective-permute-done | bytes 720928 | tf_op jit(solution)/shard_map/ppermute | solution.py:229
  604.3 12.2 %collective-permute-done.15 = bf16[2,176,1024]{2,1,0:T(8,128)(2,1)} collective-permute-done((bf16[2,176,1024]{2,1,0:T(8,128)(2,1)}, bf16[2,176,1024]{2,1,0:T(8,128)(2,1)}, u32[]{:S(2)}, u32[]{:S(2)}) %collective-permute-start.15) | collective-permute-done | bytes 720928 | tf_op jit(solution)/shard_map/ppermute | solution.py:229
  616.4 2.2 add_convert_fusion.2
  619.5 4.2 collective-permute-start.20
  623.7 3.3 add_convert_fusion
  628.5 1.9 collective-permute-start.13
  630.4 2.1 collective-permute-start.12
  632.5 2.5 fusion.13
  635.6 13.5 %collective-permute-done.20 = bf16[176,1024]{1,0:T(8,128)(2,1)S(1)} collective-permute-done((bf16[176,1024]{1,0:T(8,128)(2,1)}, bf16[176,1024]{1,0:T(8,128)(2,1)S(1)}, u32[]{:S(2)}, u32[]{:S(2)}) %collective-permute-start.20) | collective-permute-done | bytes 360480 | tf_op jit(solution)/shard_map/ppermute | solution.py:229
  649.0 2.5 copy.198
  652.9 24.4 %collective-permute-done.19 = bf16[176,1024]{1,0:T(8,128)(2,1)} collective-permute-done((bf16[176,1024]{1,0:T(8,128)(2,1)}, bf16[176,1024]{1,0:T(8,128)(2,1)}, u32[]{:S(2)}, u32[]{:S(2)}) %collective-permute-start.19) | collective-permute-done | bytes 360480 | tf_op jit(solution)/shard_map/ppermute | solution.py:229
  677.4 4.0 collective-permute-done.18
  681.4 2.2 add_add_fusion.2
  685.2 2.5 collective-permute-start.3
  687.7 2.3 add_add_fusion
  690.7 28.5 %collective-permute-done.5 = bf16[2,208,1024]{2,1,0:T(8,128)(2,1)S(1)} collective-permute-done((bf16[2,208,1024]{2,1,0:T(8,128)(2,1)}, bf16[2,208,1024]{2,1,0:T(8,128)(2,1)S(1)}, u32[]{:S(2)}, u32[]{:S(2)}) %collective-permute-start.5) | collective-permute-done | bytes 852000 | tf_op jit(solution)/shard_map/ppermute | solution.py:229
  722.8 2.1 collective-permute-start.6
  726.1 15.2 %collective-permute-done.8 = bf16[208,1024]{1,0:T(8,128)(2,1)S(1)} collective-permute-done((bf16[208,1024]{1,0:T(8,128)(2,1)S(1)}, bf16[208,1024]{1,0:T(8,128)(2,1)S(1)}, u32[]{:S(2)}, u32[]{:S(2)}) %collective-permute-start.8) | collective-permute-done | bytes 426016 | tf_op jit(solution)/shard_map/ppermute | solution.py:229
  (210 shorter events, 51.9 us)
Async XLA Ops:
  7.2 15.2 %copy-start.36 = (bf16[64,1024]{1,0:T(8,128)(2,1)S(1)}, bf16[64,1024]{1,0:T(8,128)(2,1)}, u32[]{:S(2)}) copy-start(bf16[64,1024]{1,0:T(8,128)(2,1)} %param.16) | copy-start | bytes 393220
  7.2 15.2 %copy-start.37 = (bf16[64,1024]{1,0:T(8,128)(2,1)S(1)}, bf16[64,1024]{1,0:T(8,128)(2,1)}, u32[]{:S(2)}) copy-start(bf16[64,1024]{1,0:T(8,128)(2,1)} %param.19) | copy-start | bytes 393220
  7.2 15.2 %copy-start.33 = (bf16[176,1024]{1,0:T(8,128)(2,1)S(1)}, bf16[176,1024]{1,0:T(8,128)(2,1)}, u32[]{:S(2)}) copy-start(bf16[176,1024]{1,0:T(8,128)(2,1)} %param.22) | copy-start | bytes 1081348
  7.2 50.9 %all-gather.7.cloned.1.call-start = ((), (), s32[]{:S(2)}) async-start(), calls=%async_computation.8 | async-start | bytes 5308416 | tf_op jit(solution)/shard_map/all_gather | solution.py:202
  9.1 16.4 %copy-start.34 = (bf16[64,2816]{1,0:T(8,128)(2,1)S(1)}, bf16[64,2816]{1,0:T(8,128)(2,1)}, u32[]{:S(2)}) copy-start(bf16[64,2816]{1,0:T(8,128)(2,1)} %param.20) | copy-start | bytes 1081348
  9.1 11.2 %collective-permute-start.2 = (bf16[144,1024]{1,0:T(8,128)(2,1)S(1)}, bf16[144,1024]{1,0:T(8,128)(2,1)S(1)}, u32[]{:S(2)}, u32[]{:S(2)}) collective-permute-start(bf16[144,1024]{1,0:T(8,128)(2,1)S(1)} %fusion.32), channel_id=1, source_target_pairs={{0,68},{68,0},{4,64},{64,4},{1,69},{69,1},{5,65},{65,5},{2,70},{70... | collective-permute-start | bytes 884744 | tf_op jit(solution)/shard_map/ppermute | solution.py:198
  21.4 4.1 copy-start.35
  22.3 157.7 %all-gather.9.cloned.1.call-start = ((), (), s32[]{:S(2)}) async-start(), calls=%async_computation.9 | async-start | bytes 11206656 | tf_op jit(solution)/shard_map/all_gather | solution.py:202
  22.5 18.3 %collective-permute-start = (bf16[304,1024]{1,0:T(8,128)(2,1)S(1)}, bf16[304,1024]{1,0:T(8,128)(2,1)S(1)}, u32[]{:S(2)}, u32[]{:S(2)}) collective-permute-start(bf16[304,1024]{1,0:T(8,128)(2,1)S(1)} %constant_dynamic-update-slice_fusion), channel_id=1, source_target_pairs={{0,68},{68,0},{4,64},{64,4},{1,69},{69,1},{5,65},{65,5},{2,70},{70... | collective-permute-start | bytes 1867784 | tf_op jit(solution)/shard_map/ppermute | solution.py:198
  25.6 28.9 %collective-permute-start.1 = (bf16[64,5632]{1,0:T(8,128)(2,1)S(1)}, bf16[64,5632]{1,0:T(8,128)(2,1)S(1)}, u32[]{:S(2)}, u32[]{:S(2)}) collective-permute-start(bf16[64,5632]{1,0:T(8,128)(2,1)S(1)} %constant_dynamic-update-slice_fusion.3), channel_id=1, source_target_pairs={{0,68},{68,0},{4,64},{64,4},{1,69},{69,1},{5,65},{65,5},{2,70},{70... | collective-permute-start | bytes 2162696 | tf_op jit(solution)/shard_map/ppermute | solution.py:198
  54.5 4.4 copy-start.9
  58.1 178.7 %all-gather.11.cloned.1.call-start = ((), (), s32[]{:S(2)}) async-start(), calls=%async_computation.10 | async-start | bytes 12976128 | tf_op jit(solution)/shard_map/all_gather | solution.py:202
  60.8 127.3 %copy-start.11 = (bf16[1,256,8,2,64]{1,4,3,2,0:T(8,128)(2,1)}, bf16[1,256,8,2,64]{1,4,3,2,0:T(8,128)(2,1)S(1)}, u32[]{:S(2)}) copy-start(bf16[1,256,8,2,64]{1,4,3,2,0:T(8,128)(2,1)S(1)} %copy.161) | copy-start | bytes 1572868
  65.2 8.3 %copy-start = (bf16[16,64,1024]{2,1,0:T(8,128)(2,1)}, bf16[16,64,1024]{2,1,0:T(8,128)(2,1)S(1)}, u32[]{:S(2)}) copy-start(bf16[16,64,1024]{2,1,0:T(8,128)(2,1)S(1)} %get-tuple-element.90) | copy-start | bytes 6291460
  79.8 5.9 copy-start.38
  79.8 5.9 copy-start.39
  79.8 100.2 %all-to-all-start = ((bf16[8,256,2048]{2,1,0:T(8,128)(2,1)}), bf16[8,256,2048]{2,1,0:T(8,128)(2,1)}, u32[]{:S(2)}, u32[]{:S(2)}) async-start(bf16[8,256,2048]{2,1,0:T(8,128)(2,1)} %broadcast_in_dim.72), calls=%async_computation | async-start | bytes 16777216 | tf_op jit(solution)/shard_map/all_to_all | solution.py:330
  85.1 393.2 %reduce-scatter.4.cloned.1.call-start = ((), (), s32[]{:S(2)}) async-start(), calls=%async_computation.5 | async-start | bytes 15335424 | tf_op jit(solution)/shard_map/reduce_scatter | solution.py:214
  218.1 3.4 copy-start.28
  221.4 2.5 copy-start.23
  225.7 3.4 copy-start.10
  236.8 6.4 copy-start.13
  236.8 9.3 %slice-start = ((s8[11534336]{0:T(1024)(128)(4,1)}), s8[4194304]{0:T(1024)(128)(4,1)S(1)}, s32[]{:S(2)}) async-start(s8[11534336]{0:T(1024)(128)(4,1)} %bitcast.236), calls=%async_computation.11 | async-start | bytes 8388608
  236.8 9.3 %slice-start.1 = ((s8[11534336]{0:T(1024)(128)(4,1)}), s8[4194304]{0:T(1024)(128)(4,1)S(1)}, s32[]{:S(2)}) async-start(s8[11534336]{0:T(1024)(128)(4,1)} %bitcast.236), calls=%async_computation.12 | async-start | bytes 8388608
  243.2 2.9 slice-start.2
  246.1 3.2 copy-start.19
  246.1 3.2 copy-start.21
  253.0 2.2 copy-start.14
  255.0 2.1 copy-start.22
  256.7 6.3 copy-start.7
  257.1 6.0 copy-start.24
  322.5 35.7 %copy-start.18 = (bf16[1,256,2816]{2,1,0:T(8,128)(2,1)S(1)}, bf16[1,256,2816]{2,1,0:T(8,128)(2,1)}, u32[]{:S(2)}) copy-start(bf16[1,256,2816]{2,1,0:T(8,128)(2,1)} %get-tuple-element.86) | copy-start | bytes 4325380
  322.5 129.4 %all-to-all-start.1 = ((bf16[8,256,2048]{2,1,0:T(8,128)(2,1)}), bf16[8,256,2048]{2,1,0:T(8,128)(2,1)}, u32[]{:S(2)}, u32[]{:S(2)}) async-start(bf16[8,256,2048]{2,1,0:T(8,128)(2,1)} %bitcast.242), calls=%async_computation.1 | async-start | bytes 16777216 | tf_op jit(solution)/shard_map/all_to_all | solution.py:402
  358.1 120.3 %reduce-scatter.8.cloned.1.call-start = ((), (), s32[]{:S(2)}) async-start(), calls=%async_computation.7 | async-start | bytes 6488064 | tf_op jit(solution)/shard_map/reduce_scatter | solution.py:214
  361.5 4.2 copy-start.15
  365.7 317.8 %reduce-scatter.6.cloned.1.call-start = ((), (), s32[]{:S(2)}) async-start(), calls=%async_computation.6 | async-start | bytes 7667712 | tf_op jit(solution)/shard_map/reduce_scatter | solution.py:214
  459.0 2.8 copy-start.27
  462.3 2.9 copy-start.25
  470.5 2.2 copy-start.12
  478.4 85.6 %collective-permute-start.17 = (bf16[2,176,1024]{2,1,0:T(8,128)(2,1)}, bf16[2,176,1024]{2,1,0:T(8,128)(2,1)S(1)}, u32[]{:S(2)}, u32[]{:S(2)}) collective-permute-start(bf16[2,176,1024]{2,1,0:T(8,128)(2,1)} %bitcast.282), channel_id=1, source_target_pairs={{0,3},{1,2},{2,1},{3,0},{4,7},{5,6},{6,5},{7,4},{8,11},{9,10},{10,... | collective-permute-start | bytes 2162696 | tf_op jit(solution)/shard_map/ppermute | solution.py:229
  510.2 113.4 %collective-permute-start.11 = (bf16[2,64,6656]{2,1,0:T(8,128)(2,1)}, bf16[2,64,6656]{2,1,0:T(8,128)(2,1)}, u32[]{:S(2)}, u32[]{:S(2)}) collective-permute-start(bf16[2,64,6656]{2,1,0:T(8,128)(2,1)} %bitcast.274), channel_id=1, source_target_pairs={{0,3},{1,2},{2,1},{3,0},{4,7},{5,6},{6,5},{7,4},{8,11},{9,10},{10,... | collective-permute-start | bytes 5111816 | tf_op jit(solution)/shard_map/ppermute | solution.py:229
  510.3 113.4 %collective-permute-start.10 = (bf16[2,64,6656]{2,1,0:T(8,128)(2,1)}, bf16[2,64,6656]{2,1,0:T(8,128)(2,1)}, u32[]{:S(2)}, u32[]{:S(2)}) collective-permute-start(bf16[2,64,6656]{2,1,0:T(8,128)(2,1)} %bitcast.275), channel_id=1, source_target_pairs={{0,2},{1,3},{2,0},{3,1},{4,6},{5,7},{6,4},{7,5},{8,10},{9,11},{10,... | collective-permute-start | bytes 5111816 | tf_op jit(solution)/shard_map/ppermute | solution.py:229
  510.3 113.4 %collective-permute-start.9 = (bf16[2,64,6656]{2,1,0:T(8,128)(2,1)}, bf16[2,64,6656]{2,1,0:T(8,128)(2,1)}, u32[]{:S(2)}, u32[]{:S(2)}) collective-permute-start(bf16[2,64,6656]{2,1,0:T(8,128)(2,1)} %bitcast.276), channel_id=1, source_target_pairs={{0,1},{1,0},{2,3},{3,2},{4,5},{5,4},{6,7},{7,6},{8,9},{9,8},{10,11... | collective-permute-start | bytes 5111816 | tf_op jit(solution)/shard_map/ppermute | solution.py:229
  514.3 90.0 %collective-permute-start.16 = (bf16[2,176,1024]{2,1,0:T(8,128)(2,1)}, bf16[2,176,1024]{2,1,0:T(8,128)(2,1)}, u32[]{:S(2)}, u32[]{:S(2)}) collective-permute-start(bf16[2,176,1024]{2,1,0:T(8,128)(2,1)} %bitcast.283), channel_id=1, source_target_pairs={{0,2},{1,3},{2,0},{3,1},{4,6},{5,7},{6,4},{7,5},{8,10},{9,11},{10,... | collective-permute-start | bytes 2162696 | tf_op jit(solution)/shard_map/ppermute | solution.py:229
  564.0 52.4 %collective-permute-start.15 = (bf16[2,176,1024]{2,1,0:T(8,128)(2,1)}, bf16[2,176,1024]{2,1,0:T(8,128)(2,1)}, u32[]{:S(2)}, u32[]{:S(2)}) collective-permute-start(bf16[2,176,1024]{2,1,0:T(8,128)(2,1)} %bitcast.284), channel_id=1, source_target_pairs={{0,1},{1,0},{2,3},{3,2},{4,5},{5,4},{6,7},{7,6},{8,9},{9,8},{10,11... | collective-permute-start | bytes 2162696 | tf_op jit(solution)/shard_map/ppermute | solution.py:229
  564.2 59.4 %copy-start.31 = (bf16[1,128,6656]{2,1,0:T(8,128)(2,1)S(1)}, bf16[1,128,6656]{2,1,0:T(8,128)(2,1)}, u32[]{:S(2)}) copy-start(bf16[1,128,6656]{2,1,0:T(8,128)(2,1)} %reduce-scatter.4.cloned.1.call-done) | copy-start | bytes 5111812
  616.4 16.1 %slice-start.3 = ((s8[5767168]{0:T(1024)(128)(4,1)}), s8[4194304]{0:T(1024)(128)(4,1)S(1)}, s32[]{:S(2)}) async-start(s8[5767168]{0:T(1024)(128)(4,1)} %bitcast.247), calls=%async_computation.14 | async-start | bytes 8388608
  619.5 13.0 %slice-start.4 = ((s8[5767168]{0:T(1024)(128)(4,1)}), s8[1572864]{0:T(1024)(128)(4,1)S(1)}, s32[]{:S(2)}) async-start(s8[5767168]{0:T(1024)(128)(4,1)} %bitcast.247), calls=%async_computation.15 | async-start | bytes 3145728
  619.5 29.6 %collective-permute-start.20 = (bf16[176,1024]{1,0:T(8,128)(2,1)}, bf16[176,1024]{1,0:T(8,128)(2,1)S(1)}, u32[]{:S(2)}, u32[]{:S(2)}) collective-permute-start(bf16[176,1024]{1,0:T(8,128)(2,1)} %get-tuple-element.118), channel_id=1, source_target_pairs={{0,68},{4,64},{64,4},{68,0},{1,69},{5,65},{65,5},{69,1},{2,70},{6,... | collective-permute-start | bytes 1081352 | tf_op jit(solution)/shard_map/ppermute | solution.py:229
  627.0 5.5 copy-start.6
  627.0 5.5 copy-start.16
  628.4 56.8 %collective-permute-start.14 = (bf16[64,6656]{1,0:T(8,128)(2,1)}, bf16[64,6656]{1,0:T(8,128)(2,1)}, u32[]{:S(2)}, u32[]{:S(2)}) collective-permute-start(bf16[64,6656]{1,0:T(8,128)(2,1)} %get-tuple-element.97), channel_id=1, source_target_pairs={{0,68},{4,64},{64,4},{68,0},{1,69},{5,65},{65,5},{69,1},{2,70},{6,... | collective-permute-start | bytes 2555912 | tf_op jit(solution)/shard_map/ppermute | solution.py:229
  628.5 59.2 %collective-permute-start.13 = (bf16[64,6656]{1,0:T(8,128)(2,1)}, bf16[64,6656]{1,0:T(8,128)(2,1)}, u32[]{:S(2)}, u32[]{:S(2)}) collective-permute-start(bf16[64,6656]{1,0:T(8,128)(2,1)} %get-tuple-element.97), channel_id=1, source_target_pairs={{0,64},{4,68},{64,0},{68,4},{1,65},{5,69},{65,1},{69,5},{2,66},{6,... | collective-permute-start | bytes 2555912 | tf_op jit(solution)/shard_map/ppermute | solution.py:229
  630.4 57.3 %collective-permute-start.12 = (bf16[64,6656]{1,0:T(8,128)(2,1)}, bf16[64,6656]{1,0:T(8,128)(2,1)}, u32[]{:S(2)}, u32[]{:S(2)}) collective-permute-start(bf16[64,6656]{1,0:T(8,128)(2,1)} %get-tuple-element.96), channel_id=1, source_target_pairs={{0,4},{4,0},{64,68},{68,64},{1,5},{5,1},{65,69},{69,65},{2,6},{6,2... | collective-permute-start | bytes 2555912 | tf_op jit(solution)/shard_map/ppermute | solution.py:229
  635.0 16.6 %copy-start.8 = (f32[1,256,1024]{2,1,0:T(8,128)S(1)}, f32[1,256,1024]{2,1,0:T(8,128)}, u32[]{:S(2)}) copy-start(f32[1,256,1024]{2,1,0:T(8,128)} %copy-done.7) | copy-start | bytes 3145732
  635.0 42.4 %collective-permute-start.19 = (bf16[176,1024]{1,0:T(8,128)(2,1)}, bf16[176,1024]{1,0:T(8,128)(2,1)}, u32[]{:S(2)}, u32[]{:S(2)}) collective-permute-start(bf16[176,1024]{1,0:T(8,128)(2,1)} %get-tuple-element.118), channel_id=1, source_target_pairs={{0,64},{4,68},{64,0},{68,4},{1,65},{5,69},{65,1},{69,5},{2,66},{6,... | collective-permute-start | bytes 1081352 | tf_op jit(solution)/shard_map/ppermute | solution.py:229
  649.0 32.4 %collective-permute-start.18 = (bf16[176,1024]{1,0:T(8,128)(2,1)S(1)}, bf16[176,1024]{1,0:T(8,128)(2,1)}, u32[]{:S(2)}, u32[]{:S(2)}) collective-permute-start(bf16[176,1024]{1,0:T(8,128)(2,1)S(1)} %get-tuple-element.117), channel_id=1, source_target_pairs={{0,4},{4,0},{64,68},{68,64},{1,5},{5,1},{65,69},{69,65},{2,6},{6,2... | collective-permute-start | bytes 1081352 | tf_op jit(solution)/shard_map/ppermute | solution.py:229
  683.6 36.3 %copy-start.32 = (bf16[1,416,1024]{2,1,0:T(8,128)(2,1)S(1)}, bf16[1,416,1024]{2,1,0:T(8,128)(2,1)}, u32[]{:S(2)}) copy-start(bf16[1,416,1024]{2,1,0:T(8,128)(2,1)} %reduce-scatter.6.cloned.1.call-done) | copy-start | bytes 2555908
  683.6 35.7 %collective-permute-start.5 = (bf16[2,208,1024]{2,1,0:T(8,128)(2,1)}, bf16[2,208,1024]{2,1,0:T(8,128)(2,1)S(1)}, u32[]{:S(2)}, u32[]{:S(2)}) collective-permute-start(bf16[2,208,1024]{2,1,0:T(8,128)(2,1)} %bitcast.278), channel_id=1, source_target_pairs={{0,3},{1,2},{2,1},{3,0},{4,7},{5,6},{6,5},{7,4},{8,11},{9,10},{10,... | collective-permute-start | bytes 2555912 | tf_op jit(solution)/shard_map/ppermute | solution.py:229
  684.2 35.0 %collective-permute-start.4 = (bf16[2,208,1024]{2,1,0:T(8,128)(2,1)}, bf16[2,208,1024]{2,1,0:T(8,128)(2,1)S(1)}, u32[]{:S(2)}, u32[]{:S(2)}) collective-permute-start(bf16[2,208,1024]{2,1,0:T(8,128)(2,1)} %bitcast.279), channel_id=1, source_target_pairs={{0,2},{1,3},{2,0},{3,1},{4,6},{5,7},{6,4},{7,5},{8,10},{9,11},{10,... | collective-permute-start | bytes 2555912 | tf_op jit(solution)/shard_map/ppermute | solution.py:229
  685.2 34.7 %collective-permute-start.3 = (bf16[2,208,1024]{2,1,0:T(8,128)(2,1)}, bf16[2,208,1024]{2,1,0:T(8,128)(2,1)S(1)}, u32[]{:S(2)}, u32[]{:S(2)}) collective-permute-start(bf16[2,208,1024]{2,1,0:T(8,128)(2,1)} %bitcast.280), channel_id=1, source_target_pairs={{0,1},{1,0},{2,3},{3,2},{4,5},{5,4},{6,7},{7,6},{8,9},{9,8},{10,11... | collective-permute-start | bytes 2555912 | tf_op jit(solution)/shard_map/ppermute | solution.py:229
  720.7 20.5 %collective-permute-start.8 = (bf16[208,1024]{1,0:T(8,128)(2,1)S(1)}, bf16[208,1024]{1,0:T(8,128)(2,1)S(1)}, u32[]{:S(2)}, u32[]{:S(2)}) collective-permute-start(bf16[208,1024]{1,0:T(8,128)(2,1)S(1)} %get-tuple-element.116), channel_id=1, source_target_pairs={{0,68},{4,64},{64,4},{68,0},{1,69},{5,65},{65,5},{69,1},{2,70},{6,... | collective-permute-start | bytes 1277960 | tf_op jit(solution)/shard_map/ppermute | solution.py:229
  721.5 19.8 %collective-permute-start.7 = (bf16[208,1024]{1,0:T(8,128)(2,1)S(1)}, bf16[208,1024]{1,0:T(8,128)(2,1)S(1)}, u32[]{:S(2)}, u32[]{:S(2)}) collective-permute-start(bf16[208,1024]{1,0:T(8,128)(2,1)S(1)} %get-tuple-element.116), channel_id=1, source_target_pairs={{0,64},{4,68},{64,0},{68,4},{1,65},{5,69},{65,1},{69,5},{2,66},{6,... | collective-permute-start | bytes 1277960 | tf_op jit(solution)/shard_map/ppermute | solution.py:229
  722.8 19.0 %collective-permute-start.6 = (bf16[208,1024]{1,0:T(8,128)(2,1)S(1)}, bf16[208,1024]{1,0:T(8,128)(2,1)S(1)}, u32[]{:S(2)}, u32[]{:S(2)}) collective-permute-start(bf16[208,1024]{1,0:T(8,128)(2,1)S(1)} %get-tuple-element.115), channel_id=1, source_target_pairs={{0,4},{4,0},{64,68},{68,64},{1,5},{5,1},{65,69},{69,65},{2,6},{6,2... | collective-permute-start | bytes 1277960 | tf_op jit(solution)/shard_map/ppermute | solution.py:229
  (10 other events, 16.6 us)
Sparse Core Ops, SparseCore 0:
  22.5 35.6 all-gather.6
  59.8 56.3 all-gather.8
  117.8 63.1 all-gather.10
  275.2 107.7 reduce-scatter.3
  385.2 41.9 reduce-scatter.7
  478.5 74.4 reduce-scatter.5

commit v17 on v15

--- a/solution.py
+++ b/solution.py
@@ -19,30 +19,31 @@
 Z_CROSS = [(0, 3), (3, 0), (1, 2), (2, 1)]
 
 
-HEAD_BLOCK = 128
+HEAD_BLOCK = 256
 NT_DIMS = (((1,), (1,)), ((), ()))
 TN_DIMS = (((0,), (0,)), ((), ()))
 
 
-def attention_shares(query, keys, first_row, slot_len, scale):
+def allowed_keys(rows, keys, first_row, slot_len):
+    query_pos = first_row + lax.broadcasted_iota(jnp.int32, (rows, keys), 0)
+    key_pos = lax.broadcasted_iota(jnp.int32, (rows, keys), 1)
+    return (key_pos <= query_pos) & (key_pos < slot_len)
+
+
+def attention_shares(query, keys, allowed, scale):
     scores = lax.dot_general(query, keys, NT_DIMS, preferred_element_type=jnp.float32) * scale
-    shape = scores.shape
-    query_pos = first_row + lax.broadcasted_iota(jnp.int32, shape, 0)
-    key_pos = lax.broadcasted_iota(jnp.int32, shape, 1)
-    allowed = (key_pos <= query_pos) & (key_pos < slot_len)
     scores = jnp.where(allowed, scores, MASKED)
     peak = jnp.max(scores, axis=-1, keepdims=True)
     raised = jnp.exp(scores - peak)
     denominator = jnp.sum(raised, axis=-1, keepdims=True)
-    return raised / denominator
+    return raised * (1.0 / denominator)
 
 
 def attn_fwd_kernel(head_dim, scale, meta_ref, q_ref, k_ref, v_ref, o_ref):
-    first_row = meta_ref[0]
-    slot_len = meta_ref[1]
+    allowed = allowed_keys(q_ref.shape[0], k_ref.shape[0], meta_ref[0], meta_ref[1])
     for j in range(q_ref.shape[1] // head_dim):
         cols = slice(j * head_dim, (j + 1) * head_dim)
-        shares = attention_shares(q_ref[:, cols], k_ref[:, cols], first_row, slot_len, scale)
+        shares = attention_shares(q_ref[:, cols], k_ref[:, cols], allowed, scale)
         mixed = jnp.dot(
             shares.astype(jnp.bfloat16), v_ref[:, cols], preferred_element_type=jnp.float32
         )
@@ -50,14 +51,13 @@
 
 
 def attn_bwd_kernel(head_dim, scale, meta_ref, q_ref, k_ref, v_ref, do_ref, dq_ref, dkv_ref):
-    first_row = meta_ref[0]
-    slot_len = meta_ref[1]
+    allowed = allowed_keys(q_ref.shape[0], k_ref.shape[0], meta_ref[0], meta_ref[1])
     for j in range(q_ref.shape[1] // head_dim):
         cols = slice(j * head_dim, (j + 1) * head_dim)
         query = q_ref[:, cols]
         keys = k_ref[:, cols]
         back = do_ref[:, cols]
-        shares = attention_shares(query, keys, first_row, slot_len, scale)
+        shares = attention_shares(query, keys, allowed, scale)
         prob_back = lax.dot_general(back, v_ref[:, cols], NT_DIMS, preferred_element_type=jnp.float32)
         inner = jnp.sum(shares * prob_back, axis=-1, keepdims=True)
         score_back = (shares * (prob_back - inner)).astype(jnp.bfloat16)

time: 635 us -> 632 us (level)
  transfers between devices with their start and end apart: 23 -> 23, of which waited for: 13 -> 14; matrix products, arithmetic and copies ran while one was open for 18% -> 18% of each run, Pallas kernels for 11% -> 10%
where the time goes in v17:
time: 632 us; the launch traced here: 625 us
  waiting for transfers between devices  285 us (45%)
  starting transfers between devices  99.2 us (16%)
  local copies, waits for them, and re-layouts  67.8 us (11%)
  Pallas kernels  63.9 us (10%)
  other arithmetic  49.5 us (8%)
  matrix products  44.2 us (7%)
  between operations  15.6 us (2%)
    all_to_all x1, waiting for transfers between devices, body(): lax.all_to_all(jnp.broadcast_to(kv_own[None], (n_ctx, rows, 2 * width)),...  92.6 us
    all_to_all x1, waiting for transfers between devices, body(): lax.all_to_all(kv_back.reshape(n_ctx, rows, 2 * width), CTX, 0, 0, tiled=...  84.6 us
    ppermute x9, waiting for transfers between devices, ctx_allreduce(): other = lax.ppermute(total, CTX, [(j, j ^ step) for j in range(n_ctx)])  51.7 us
    ppermute x9, starting transfers between devices, ctx_allreduce(): other = lax.ppermute(total, CTX, [(j, j ^ step) for j in range(n_ctx)])  43.4 us
    pallas_call x1, Pallas kernels, attention_backward(): pl.pallas_call(functools.partial(attn_bwd_kernel, head_dim, scale), out_s...  41.4 us
    all_to_all x1, starting transfers between devices, body(): lax.all_to_all(kv_back.reshape(n_ctx, rows, 2 * width), CTX, 0, 0, tiled=...  35.7 us
    ppermute x3, waiting for transfers between devices, z_exchange(): return zh_pair(pack, lax.ppermute(pack, ('zh', 'zl'), Z_CROSS))  34.3 us
    pallas_call x1, Pallas kernels, attention_forward(): pl.pallas_call(functools.partial(attn_fwd_kernel, head_dim, scale), out_s...  22.4 us
  transfers between devices with their start and end apart: 23, of which 14 were waited for; matrix products, arithmetic and copies ran while one was open for 18% of the time, Pallas kernels for 10%

profile of v17, /device:TPU:0, one launch (start us, length us, event | category | flops | bytes accessed | tf_op | source)
XLA Modules:
  0.0 625.1 jit_solution(12903678850952938022)
XLA Ops:
  9.1 4.2 collective-permute-start.2
  13.3 7.0 %collective-permute-done.2 = bf16[144,1024]{1,0:T(8,128)(2,1)S(1)} collective-permute-done((bf16[144,1024]{1,0:T(8,128)(2,1)S(1)}, bf16[144,1024]{1,0:T(8,128)(2,1)S(1)}, u32[]{:S(2)}, u32[]{:S(2)}) %collective-permute-start.2) | collective-permute-done | bytes 294944 | tf_op jit(solution)/shard_map/ppermute | solution.py:198
  22.5 3.0 collective-permute-start
  26.0 14.8 %collective-permute-done = bf16[304,1024]{1,0:T(8,128)(2,1)S(1)} collective-permute-done((bf16[304,1024]{1,0:T(8,128)(2,1)S(1)}, bf16[304,1024]{1,0:T(8,128)(2,1)S(1)}, u32[]{:S(2)}, u32[]{:S(2)}) %collective-permute-start) | collective-permute-done | bytes 622624 | tf_op jit(solution)/shard_map/ppermute | solution.py:198
  42.0 12.5 %collective-permute-done.1 = bf16[64,5632]{1,0:T(8,128)(2,1)S(1)} collective-permute-done((bf16[64,5632]{1,0:T(8,128)(2,1)S(1)}, bf16[64,5632]{1,0:T(8,128)(2,1)S(1)}, u32[]{:S(2)}, u32[]{:S(2)}) %collective-permute-start.1) | collective-permute-done | bytes 720928 | tf_op jit(solution)/shard_map/ppermute | solution.py:198
  55.8 2.3 all-gather.7.cloned.1.call-done
  60.8 4.4 fusion.52
  65.2 4.5 copy.163
  69.7 2.5 convolution_bitcast_fusion.5
  73.4 1.8 fusion.13
  75.4 4.3 broadcast_in_dim.72
  79.7 5.4 all-to-all-start
  87.4 92.6 %all-to-all-done = bf16[8,256,2048]{2,1,0:T(8,128)(2,1)} async-done(((bf16[8,256,2048]{2,1,0:T(8,128)(2,1)}), bf16[8,256,2048]{2,1,0:T(8,128)(2,1)}, u32[]{:S(2)}, u32[]{:S(2)}) %all-to-all-start) | async-done | bytes 8388640 | tf_op jit(solution)/shard_map/all_to_all | solution.py:316
  180.0 4.1 fusion.51
  184.1 4.4 copy.166
  188.5 2.3 convolution_bitcast_fusion.3
  191.3 22.4 %shard_map.229 = bf16[256,1024]{1,0:T(8,128)(2,1)S(1)} custom-call(s32[2]{0:T(128)S(1)} %pad_add_fusion.meta_ref, bf16[256,1024]{1,0:T(8,128)(2,1)S(1)} %copy.168.q_ref, bf16[2048,2048]{1,0:T(8,128)(2,1)} %bitcast.24.k_ref.v_ref, bf16[2048,2048]{1,0:T(8,128)(2,1)} %bitcast.24.k_ref.v_ref), custom_call_target="tpu_custom_call" | custom-call | flops 2147483648 | bytes 9437184 | tf_op jit(solution)/shard_map/pallas_call | solution.py:80
  214.7 1.9 copy.170
  216.6 3.4 slice.116
  220.0 1.8 convolution_bitcast_fusion.1
  222.5 1.8 copy.176
  224.2 3.4 copy.177
  227.7 1.9 multiply_reduce_fusion.2
  231.4 2.0 copy.172
  233.5 1.9 copy.173
  235.4 6.4 %convolution_bitcast_fusion = f32[1,256,5632]{2,1,0:T(8,128)S(1)} fusion(bf16[256,1024]{0,1:T(8,128)(2,1)} %bitcast.247, bf16[1024,5632]{1,0:T(8,128)(2,1)} %bitcast.238), kind=kOutput, calls=%fused_computation.5 | convolution fusion | flops 2952790016 | bytes 17825792 | tf_op jit(solution)/shard_map/dot_general | solution.py:333
  241.8 2.9 multiply_convert_fusion.1
  244.7 3.2 fusion.6
  248.9 2.5 copy.180
  251.4 2.0 multiply_reduce_fusion
  253.6 1.6 subtract_add_fusion
  255.6 6.0 convolution_convert_fusion
  262.3 11.2 %pad_maximum_fusion = bf16[8,128,6656]{2,1,0:T(8,128)(2,1)} fusion(bf16[8,128,1024]{2,1,0:T(8,128)(2,1)S(1)} %convolution_convert_fusion.2, bf16[8,128,5632]{2,1,0:T(8,128)(2,1)} %convolution_convert_fusion), kind=kLoop, calls=%fused_computation.2 | loop fusion | flops 27262976 | bytes 27262976 | tf_op jit(solution)/shard_map/concatenate | solution.py:369
  273.5 2.8 convolution_convert_fusion.6
  277.8 41.4 %shard_map.230 = (f32[256,1024]{1,0:T(8,128)S(1)}, bf16[2048,2048]{1,0:T(8,128)(2,1)}) custom-call(s32[2]{0:T(128)S(1)} %pad_add_fusion.meta_ref, bf16[256,1024]{1,0:T(8,128)(2,1)S(1)} %copy.168.q_ref, bf16[2048,2048]{1,0:T(8,128)(2,1)} %bitcast.24.k_ref.v_ref, bf16[2048,2048]{1,0:T(8,128)(2,1)} %bitcast.24.k_ref.v_ref, bf16[256,1024]{1,0:T(8,128)(2,1)S(1)} %copy.184.do_ref), custom_call_target="tpu_custom_call" | custom-call | flops 5368709120 | bytes 19398656 | tf_op jit(solution)/shard_map/pallas_call | solution.py:108
  319.3 35.7 %all-to-all-start.1 = ((bf16[8,256,2048]{2,1,0:T(8,128)(2,1)}), bf16[8,256,2048]{2,1,0:T(8,128)(2,1)}, u32[]{:S(2)}, u32[]{:S(2)}) async-start(bf16[8,256,2048]{2,1,0:T(8,128)(2,1)} %bitcast.245), calls=%async_computation.1 | async-start | bytes 16777216 | tf_op jit(solution)/shard_map/all_to_all | solution.py:389
  355.0 1.6 copy.174
  356.6 1.5 copy.175
  358.1 4.2 convolution_convert_fusion.1
  364.0 84.6 %all-to-all-done.1 = bf16[8,256,2048]{2,1,0:T(8,128)(2,1)} async-done(((bf16[8,256,2048]{2,1,0:T(8,128)(2,1)}), bf16[8,256,2048]{2,1,0:T(8,128)(2,1)}, u32[]{:S(2)}, u32[]{:S(2)}) %all-to-all-start.1) | async-done | bytes 8388640 | tf_op jit(solution)/shard_map/all_to_all | solution.py:389
  448.7 5.3 convert_reduce_fusion
  454.0 1.8 copy.186
  455.8 2.8 slice_multiply_fusion
  462.8 1.7 convolution_add_fusion
  464.5 1.6 copy.188
  467.2 1.6 copy.190
  471.7 3.3 fusion.1
  476.3 2.6 collective-permute-start.7
  480.7 18.8 %collective-permute-done.7 = bf16[64,6656]{1,0:T(8,128)(2,1)} collective-permute-done((bf16[64,6656]{1,0:T(8,128)(2,1)S(1)}, bf16[64,6656]{1,0:T(8,128)(2,1)}, u32[]{:S(2)}, u32[]{:S(2)}) %collective-permute-start.7) | collective-permute-done | bytes 852000 | tf_op jit(solution)/shard_map/ppermute | solution.py:224
  499.5 1.6 fusion.5
  501.1 29.3 %collective-permute-start.8 = (bf16[64,6656]{1,0:T(8,128)(2,1)S(1)}, bf16[64,6656]{1,0:T(8,128)(2,1)S(1)}, u32[]{:S(2)}, u32[]{:S(2)}) collective-permute-start(bf16[64,6656]{1,0:T(8,128)(2,1)S(1)} %fusion.5), channel_id=1, source_target_pairs={{0,1},{1,0},{2,3},{3,2},{4,5},{5,4},{6,7},{7,6},{8,9},{9,8},{10,11... | collective-permute-start | bytes 2555912 | tf_op jit(solution)/shard_map/ppermute | solution.py:232
  530.5 3.3 collective-permute-start.12
  533.8 18.2 %collective-permute-done.12 = bf16[176,1024]{1,0:T(8,128)(2,1)S(1)} collective-permute-done((bf16[176,1024]{1,0:T(8,128)(2,1)S(1)}, bf16[176,1024]{1,0:T(8,128)(2,1)S(1)}, u32[]{:S(2)}, u32[]{:S(2)}) %collective-permute-start.12) | collective-permute-done | bytes 360480 | tf_op jit(solution)/shard_map/ppermute | solution.py:232
  552.1 8.4 %collective-permute-start.13 = (bf16[176,1024]{1,0:T(8,128)(2,1)S(1)}, bf16[176,1024]{1,0:T(8,128)(2,1)}, u32[]{:S(2)}, u32[]{:S(2)}) collective-permute-start(bf16[176,1024]{1,0:T(8,128)(2,1)S(1)} %add_convert_fusion.8), channel_id=1, source_target_pairs={{0,2},{1,3},{2,0},{3,1},{4,6},{5,7},{6,4},{7,5},{8,10},{9,11},{10,... | collective-permute-start | bytes 1081352 | tf_op jit(solution)/shard_map/ppermute | solution.py:232
  561.9 5.2 fusion.14
  568.4 1.5 collective-permute-done.13
  572.3 3.3 collective-permute-start.3
  575.6 9.9 %collective-permute-done.9 = bf16[64,6656]{1,0:T(8,128)(2,1)} collective-permute-done((bf16[64,6656]{1,0:T(8,128)(2,1)}, bf16[64,6656]{1,0:T(8,128)(2,1)}, u32[]{:S(2)}, u32[]{:S(2)}) %collective-permute-start.9) | collective-permute-done | bytes 852000 | tf_op jit(solution)/shard_map/ppermute | solution.py:232
  585.5 1.6 add_convert_fusion.1
  587.5 1.4 fusion.21
  589.8 8.1 %collective-permute-done.4 = bf16[208,1024]{1,0:T(8,128)(2,1)S(1)} collective-permute-done((bf16[208,1024]{1,0:T(8,128)(2,1)S(1)}, bf16[208,1024]{1,0:T(8,128)(2,1)S(1)}, u32[]{:S(2)}, u32[]{:S(2)}) %collective-permute-start.4) | collective-permute-done | bytes 426016 | tf_op jit(solution)/shard_map/ppermute | solution.py:232
  598.1 1.7 collective-permute-start.5
  600.8 7.0 %collective-permute-done.5 = bf16[208,1024]{1,0:T(8,128)(2,1)S(1)} collective-permute-done((bf16[208,1024]{1,0:T(8,128)(2,1)S(1)}, bf16[208,1024]{1,0:T(8,128)(2,1)S(1)}, u32[]{:S(2)}, u32[]{:S(2)}) %collective-permute-start.5) | collective-permute-done | bytes 426016 | tf_op jit(solution)/shard_map/ppermute | solution.py:232
  609.3 6.8 %collective-permute-done.6 = bf16[208,1024]{1,0:T(8,128)(2,1)S(1)} collective-permute-done((bf16[208,1024]{1,0:T(8,128)(2,1)S(1)}, bf16[208,1024]{1,0:T(8,128)(2,1)S(1)}, u32[]{:S(2)}, u32[]{:S(2)}) %collective-permute-start.6) | collective-permute-done | bytes 426016 | tf_op jit(solution)/shard_map/ppermute | solution.py:232
  (201 shorter events, 44.6 us)
Async XLA Ops:
  7.2 15.2 %copy-start.37 = (bf16[64,1024]{1,0:T(8,128)(2,1)S(1)}, bf16[64,1024]{1,0:T(8,128)(2,1)}, u32[]{:S(2)}) copy-start(bf16[64,1024]{1,0:T(8,128)(2,1)} %param.16) | copy-start | bytes 393220
  7.2 15.2 %copy-start.38 = (bf16[64,1024]{1,0:T(8,128)(2,1)S(1)}, bf16[64,1024]{1,0:T(8,128)(2,1)}, u32[]{:S(2)}) copy-start(bf16[64,1024]{1,0:T(8,128)(2,1)} %param.19) | copy-start | bytes 393220
  7.2 15.2 %copy-start.34 = (bf16[176,1024]{1,0:T(8,128)(2,1)S(1)}, bf16[176,1024]{1,0:T(8,128)(2,1)}, u32[]{:S(2)}) copy-start(bf16[176,1024]{1,0:T(8,128)(2,1)} %param.22) | copy-start | bytes 1081348
  7.2 50.9 %all-gather.7.cloned.1.call-start = ((), (), s32[]{:S(2)}) async-start(), calls=%async_computation.8 | async-start | bytes 5308416 | tf_op jit(solution)/shard_map/all_gather | solution.py:202
  9.1 16.4 %copy-start.35 = (bf16[64,2816]{1,0:T(8,128)(2,1)S(1)}, bf16[64,2816]{1,0:T(8,128)(2,1)}, u32[]{:S(2)}) copy-start(bf16[64,2816]{1,0:T(8,128)(2,1)} %param.20) | copy-start | bytes 1081348
  9.1 11.2 %collective-permute-start.2 = (bf16[144,1024]{1,0:T(8,128)(2,1)S(1)}, bf16[144,1024]{1,0:T(8,128)(2,1)S(1)}, u32[]{:S(2)}, u32[]{:S(2)}) collective-permute-start(bf16[144,1024]{1,0:T(8,128)(2,1)S(1)} %fusion.38), channel_id=1, source_target_pairs={{0,68},{68,0},{4,64},{64,4},{1,69},{69,1},{5,65},{65,5},{2,70},{70... | collective-permute-start | bytes 884744 | tf_op jit(solution)/shard_map/ppermute | solution.py:198
  21.4 4.1 copy-start.36
  22.3 157.6 %all-gather.9.cloned.1.call-start = ((), (), s32[]{:S(2)}) async-start(), calls=%async_computation.9 | async-start | bytes 11206656 | tf_op jit(solution)/shard_map/all_gather | solution.py:202
  22.5 18.3 %collective-permute-start = (bf16[304,1024]{1,0:T(8,128)(2,1)S(1)}, bf16[304,1024]{1,0:T(8,128)(2,1)S(1)}, u32[]{:S(2)}, u32[]{:S(2)}) collective-permute-start(bf16[304,1024]{1,0:T(8,128)(2,1)S(1)} %constant_dynamic-update-slice_fusion), channel_id=1, source_target_pairs={{0,68},{68,0},{4,64},{64,4},{1,69},{69,1},{5,65},{65,5},{2,70},{70... | collective-permute-start | bytes 1867784 | tf_op jit(solution)/shard_map/ppermute | solution.py:198
  25.6 28.9 %collective-permute-start.1 = (bf16[64,5632]{1,0:T(8,128)(2,1)S(1)}, bf16[64,5632]{1,0:T(8,128)(2,1)S(1)}, u32[]{:S(2)}, u32[]{:S(2)}) collective-permute-start(bf16[64,5632]{1,0:T(8,128)(2,1)S(1)} %constant_dynamic-update-slice_fusion.3), channel_id=1, source_target_pairs={{0,68},{68,0},{4,64},{64,4},{1,69},{69,1},{5,65},{65,5},{2,70},{70... | collective-permute-start | bytes 2162696 | tf_op jit(solution)/shard_map/ppermute | solution.py:198
  54.5 4.4 copy-start.9
  58.1 177.2 %all-gather.11.cloned.1.call-start = ((), (), s32[]{:S(2)}) async-start(), calls=%async_computation.10 | async-start | bytes 12976128 | tf_op jit(solution)/shard_map/all_gather | solution.py:202
  60.8 127.8 %copy-start.11 = (bf16[1,256,8,2,64]{1,4,3,2,0:T(8,128)(2,1)}, bf16[1,256,8,2,64]{1,4,3,2,0:T(8,128)(2,1)S(1)}, u32[]{:S(2)}) copy-start(bf16[1,256,8,2,64]{1,4,3,2,0:T(8,128)(2,1)S(1)} %copy.161) | copy-start | bytes 1572868
  65.2 8.3 %copy-start = (bf16[16,64,1024]{2,1,0:T(8,128)(2,1)}, bf16[16,64,1024]{2,1,0:T(8,128)(2,1)S(1)}, u32[]{:S(2)}) copy-start(bf16[16,64,1024]{2,1,0:T(8,128)(2,1)S(1)} %get-tuple-element.90) | copy-start | bytes 6291460
  73.4 1.8 copy-start.31
  79.7 5.5 copy-start.39
  79.7 5.5 copy-start.40
  79.7 100.3 %all-to-all-start = ((bf16[8,256,2048]{2,1,0:T(8,128)(2,1)}), bf16[8,256,2048]{2,1,0:T(8,128)(2,1)}, u32[]{:S(2)}, u32[]{:S(2)}) async-start(bf16[8,256,2048]{2,1,0:T(8,128)(2,1)} %broadcast_in_dim.72), calls=%async_computation | async-start | bytes 16777216 | tf_op jit(solution)/shard_map/all_to_all | solution.py:316
  85.1 389.9 %reduce-scatter.4.cloned.1.call-start = ((), (), s32[]{:S(2)}) async-start(), calls=%async_computation.5 | async-start | bytes 15335424 | tf_op jit(solution)/shard_map/reduce_scatter | solution.py:214
  216.6 3.4 copy-start.29
  220.0 2.5 copy-start.23
  224.2 3.4 copy-start.10
  235.4 6.4 %copy-start.13 = (f32[1,256,2816]{2,1,0:T(8,128)S(1)}, f32[1,256,2816]{2,1,0:T(8,128)}, u32[]{:S(2)}) copy-start(f32[1,256,2816]{2,1,0:T(8,128)} %copy.177) | copy-start | bytes 8650756
  235.4 9.3 %slice-start = ((s8[11534336]{0:T(1024)(128)(4,1)}), s8[4194304]{0:T(1024)(128)(4,1)S(1)}, s32[]{:S(2)}) async-start(s8[11534336]{0:T(1024)(128)(4,1)} %bitcast.239), calls=%async_computation.11 | async-start | bytes 8388608
  235.4 9.3 %slice-start.1 = ((s8[11534336]{0:T(1024)(128)(4,1)}), s8[4194304]{0:T(1024)(128)(4,1)S(1)}, s32[]{:S(2)}) async-start(s8[11534336]{0:T(1024)(128)(4,1)} %bitcast.239), calls=%async_computation.12 | async-start | bytes 8388608
  241.8 2.9 slice-start.2
  244.6 3.2 copy-start.19
  244.6 3.2 copy-start.21
  251.4 2.0 copy-start.7
  251.4 2.2 copy-start.14
  253.4 1.8 copy-start.17
  253.4 1.8 copy-start.20
  253.4 2.1 copy-start.22
  255.2 6.4 %copy-start.4 = (f32[1,256,1024]{2,1,0:T(8,128)}, f32[1,256,1024]{2,1,0:T(8,128)S(1)}, u32[]{:S(2)}) copy-start(f32[1,256,1024]{2,1,0:T(8,128)S(1)} %subtract_add_fusion) | copy-start | bytes 3145732
  255.6 6.0 copy-start.24
  319.3 35.7 %copy-start.18 = (bf16[1,256,2816]{2,1,0:T(8,128)(2,1)S(1)}, bf16[1,256,2816]{2,1,0:T(8,128)(2,1)}, u32[]{:S(2)}) copy-start(bf16[1,256,2816]{2,1,0:T(8,128)(2,1)} %get-tuple-element.86) | copy-start | bytes 4325380
  319.3 129.4 %all-to-all-start.1 = ((bf16[8,256,2048]{2,1,0:T(8,128)(2,1)}), bf16[8,256,2048]{2,1,0:T(8,128)(2,1)}, u32[]{:S(2)}, u32[]{:S(2)}) async-start(bf16[8,256,2048]{2,1,0:T(8,128)(2,1)} %bitcast.245), calls=%async_computation.1 | async-start | bytes 16777216 | tf_op jit(solution)/shard_map/all_to_all | solution.py:389
  355.0 123.9 %reduce-scatter.8.cloned.1.call-start = ((), (), s32[]{:S(2)}) async-start(), calls=%async_computation.7 | async-start | bytes 6488064 | tf_op jit(solution)/shard_map/reduce_scatter | solution.py:214
  358.1 4.2 copy-start.15
  362.3 208.8 %reduce-scatter.6.cloned.1.call-start = ((), (), s32[]{:S(2)}) async-start(), calls=%async_computation.6 | async-start | bytes 7667712 | tf_op jit(solution)/shard_map/reduce_scatter | solution.py:214
  455.8 2.8 copy-start.27
  458.6 1.8 copy-start.3
  459.1 2.9 copy-start.25
  459.1 2.1 copy-start.2
  461.2 1.6 copy-start.1
  467.1 2.2 copy-start.12
  476.3 23.3 %collective-permute-start.7 = (bf16[64,6656]{1,0:T(8,128)(2,1)S(1)}, bf16[64,6656]{1,0:T(8,128)(2,1)}, u32[]{:S(2)}, u32[]{:S(2)}) collective-permute-start(bf16[64,6656]{1,0:T(8,128)(2,1)S(1)} %dynamic-slice_bitcast_fusion), channel_id=1, source_target_pairs={{0,68},{68,0},{4,64},{64,4},{1,69},{69,1},{5,65},{65,5},{2,70},{70... | collective-permute-start | bytes 2555912 | tf_op jit(solution)/shard_map/ppermute | solution.py:224
  478.8 51.6 %copy-start.33 = (bf16[1,352,1024]{2,1,0:T(8,128)(2,1)S(1)}, bf16[1,352,1024]{2,1,0:T(8,128)(2,1)}, u32[]{:S(2)}) copy-start(bf16[1,352,1024]{2,1,0:T(8,128)(2,1)} %reduce-scatter.8.cloned.1.call-done) | copy-start | bytes 2162692
  479.9 50.5 %collective-permute-start.11 = (bf16[176,1024]{1,0:T(8,128)(2,1)S(1)}, bf16[176,1024]{1,0:T(8,128)(2,1)S(1)}, u32[]{:S(2)}, u32[]{:S(2)}) collective-permute-start(bf16[176,1024]{1,0:T(8,128)(2,1)S(1)} %dynamic-slice_bitcast_fusion.2), channel_id=1, source_target_pairs={{0,68},{68,0},{4,64},{64,4},{1,69},{69,1},{5,65},{65,5},{2,70},{70... | collective-permute-start | bytes 1081352 | tf_op jit(solution)/shard_map/ppermute | solution.py:224
  501.1 60.8 %copy-start.8 = (f32[1,256,1024]{2,1,0:T(8,128)S(1)}, f32[1,256,1024]{2,1,0:T(8,128)}, u32[]{:S(2)}) copy-start(f32[1,256,1024]{2,1,0:T(8,128)} %copy-done.6) | copy-start | bytes 3145732
  501.1 60.7 %copy-start.16 = (bf16[1,256,8,2,176]{1,4,3,2,0:T(8,128)(2,1)S(1)}, bf16[1,256,8,2,176]{1,4,3,2,0:T(8,128)(2,1)}, u32[]{:S(2)}) copy-start(bf16[1,256,8,2,176]{1,4,3,2,0:T(8,128)(2,1)} %copy-done.15) | copy-start | bytes 4325380
  501.1 59.3 %collective-permute-start.8 = (bf16[64,6656]{1,0:T(8,128)(2,1)S(1)}, bf16[64,6656]{1,0:T(8,128)(2,1)S(1)}, u32[]{:S(2)}, u32[]{:S(2)}) collective-permute-start(bf16[64,6656]{1,0:T(8,128)(2,1)S(1)} %fusion.5), channel_id=1, source_target_pairs={{0,1},{1,0},{2,3},{3,2},{4,5},{5,4},{6,7},{7,6},{8,9},{9,8},{10,11... | collective-permute-start | bytes 2555912 | tf_op jit(solution)/shard_map/ppermute | solution.py:232
  530.5 21.5 %collective-permute-start.12 = (bf16[176,1024]{1,0:T(8,128)(2,1)S(1)}, bf16[176,1024]{1,0:T(8,128)(2,1)S(1)}, u32[]{:S(2)}, u32[]{:S(2)}) collective-permute-start(bf16[176,1024]{1,0:T(8,128)(2,1)S(1)} %fusion.29), channel_id=1, source_target_pairs={{0,1},{1,0},{2,3},{3,2},{4,5},{5,4},{6,7},{7,6},{8,9},{9,8},{10,11... | collective-permute-start | bytes 1081352 | tf_op jit(solution)/shard_map/ppermute | solution.py:232
  552.1 17.8 %collective-permute-start.13 = (bf16[176,1024]{1,0:T(8,128)(2,1)S(1)}, bf16[176,1024]{1,0:T(8,128)(2,1)}, u32[]{:S(2)}, u32[]{:S(2)}) collective-permute-start(bf16[176,1024]{1,0:T(8,128)(2,1)S(1)} %add_convert_fusion.8), channel_id=1, source_target_pairs={{0,2},{1,3},{2,0},{3,1},{4,6},{5,7},{6,4},{7,5},{8,10},{9,11},{10,... | collective-permute-start | bytes 1081352 | tf_op jit(solution)/shard_map/ppermute | solution.py:232
  561.6 24.0 %collective-permute-start.9 = (bf16[64,6656]{1,0:T(8,128)(2,1)}, bf16[64,6656]{1,0:T(8,128)(2,1)}, u32[]{:S(2)}, u32[]{:S(2)}) collective-permute-start(bf16[64,6656]{1,0:T(8,128)(2,1)} %add_convert_fusion.2), channel_id=1, source_target_pairs={{0,2},{1,3},{2,0},{3,1},{4,6},{5,7},{6,4},{7,5},{8,10},{9,11},{10,... | collective-permute-start | bytes 2555912 | tf_op jit(solution)/shard_map/ppermute | solution.py:232
  561.9 5.2 copy-start.28
  571.0 17.9 %collective-permute-start.14 = (bf16[176,1024]{1,0:T(8,128)(2,1)S(1)}, bf16[176,1024]{1,0:T(8,128)(2,1)S(1)}, u32[]{:S(2)}, u32[]{:S(2)}) collective-permute-start(bf16[176,1024]{1,0:T(8,128)(2,1)S(1)} %add_convert_fusion.7), channel_id=1, source_target_pairs={{0,4},{1,5},{2,6},{3,7},{4,0},{5,1},{6,2},{7,3},{8,12},{9,13},{10,... | collective-permute-start | bytes 1081352 | tf_op jit(solution)/shard_map/ppermute | solution.py:232
  571.1 16.1 %copy-start.32 = (bf16[1,416,1024]{2,1,0:T(8,128)(2,1)S(1)}, bf16[1,416,1024]{2,1,0:T(8,128)(2,1)}, u32[]{:S(2)}) copy-start(bf16[1,416,1024]{2,1,0:T(8,128)(2,1)} %reduce-scatter.6.cloned.1.call-done) | copy-start | bytes 2555908
  572.3 15.2 %copy-start.5 = (f32[1,256,1024]{2,1,0:T(8,128)S(1)}, f32[1,256,1024]{2,1,0:T(8,128)}, u32[]{:S(2)}) copy-start(f32[1,256,1024]{2,1,0:T(8,128)} %copy-done.4) | copy-start | bytes 3145732
  572.3 15.0 %collective-permute-start.3 = (bf16[208,1024]{1,0:T(8,128)(2,1)S(1)}, bf16[208,1024]{1,0:T(8,128)(2,1)S(1)}, u32[]{:S(2)}, u32[]{:S(2)}) collective-permute-start(bf16[208,1024]{1,0:T(8,128)(2,1)S(1)} %dynamic-slice_bitcast_fusion.1), channel_id=1, source_target_pairs={{0,68},{68,0},{4,64},{64,4},{1,69},{69,1},{5,65},{65,5},{2,70},{70... | collective-permute-start | bytes 1277960 | tf_op jit(solution)/shard_map/ppermute | solution.py:224
  587.1 12.8 %collective-permute-start.10 = (bf16[64,6656]{1,0:T(8,128)(2,1)S(1)}, bf16[64,6656]{1,0:T(8,128)(2,1)S(1)}, u32[]{:S(2)}, u32[]{:S(2)}) collective-permute-start(bf16[64,6656]{1,0:T(8,128)(2,1)S(1)} %add_convert_fusion.1), channel_id=1, source_target_pairs={{0,4},{1,5},{2,6},{3,7},{4,0},{5,1},{6,2},{7,3},{8,12},{9,13},{10,... | collective-permute-start | bytes 2555912 | tf_op jit(solution)/shard_map/ppermute | solution.py:232
  587.4 10.5 %collective-permute-start.4 = (bf16[208,1024]{1,0:T(8,128)(2,1)S(1)}, bf16[208,1024]{1,0:T(8,128)(2,1)S(1)}, u32[]{:S(2)}, u32[]{:S(2)}) collective-permute-start(bf16[208,1024]{1,0:T(8,128)(2,1)S(1)} %fusion.28), channel_id=1, source_target_pairs={{0,1},{1,0},{2,3},{3,2},{4,5},{5,4},{6,7},{7,6},{8,9},{9,8},{10,11... | collective-permute-start | bytes 1277960 | tf_op jit(solution)/shard_map/ppermute | solution.py:232
  598.1 9.7 %collective-permute-start.5 = (bf16[208,1024]{1,0:T(8,128)(2,1)S(1)}, bf16[208,1024]{1,0:T(8,128)(2,1)S(1)}, u32[]{:S(2)}, u32[]{:S(2)}) collective-permute-start(bf16[208,1024]{1,0:T(8,128)(2,1)S(1)} %add_convert_fusion.5), channel_id=1, source_target_pairs={{0,2},{1,3},{2,0},{3,1},{4,6},{5,7},{6,4},{7,5},{8,10},{9,11},{10,... | collective-permute-start | bytes 1277960 | tf_op jit(solution)/shard_map/ppermute | solution.py:232
  608.0 8.2 %collective-permute-start.6 = (bf16[208,1024]{1,0:T(8,128)(2,1)S(1)}, bf16[208,1024]{1,0:T(8,128)(2,1)S(1)}, u32[]{:S(2)}, u32[]{:S(2)}) collective-permute-start(bf16[208,1024]{1,0:T(8,128)(2,1)S(1)} %add_convert_fusion.4), channel_id=1, source_target_pairs={{0,4},{1,5},{2,6},{3,7},{4,0},{5,1},{6,2},{7,3},{8,12},{9,13},{10,... | collective-permute-start | bytes 1277960 | tf_op jit(solution)/shard_map/ppermute | solution.py:232
  (3 other events, 3.6 us)
Sparse Core Ops, SparseCore 0:
  22.5 35.6 all-gather.6
  59.8 56.3 all-gather.8
  117.8 63.1 all-gather.10
  273.6 107.7 reduce-scatter.3
  383.7 41.9 reduce-scatter.7
  475.2 74.1 reduce-scatter.5

commit v18 on v17

--- a/solution.py
+++ b/solution.py
@@ -101,24 +101,25 @@
     )(meta, query_rows, kv_rows, kv_rows)
 
 
-def attention_backward(meta, query_rows, kv_rows, back_rows, head_dim, scale):
+def attention_backward(meta, query_rows, kv_rows, back_rows, head_dim, scale, first, count):
     rows, width = query_rows.shape
     keys = kv_rows.shape[0]
     blocks = width // HEAD_BLOCK
+    part = count * HEAD_BLOCK
     return pl.pallas_call(
         functools.partial(attn_bwd_kernel, head_dim, scale),
         out_shape=(
-            jax.ShapeDtypeStruct((rows, width), jnp.float32),
-            jax.ShapeDtypeStruct((keys, 2 * width), jnp.bfloat16),
+            jax.ShapeDtypeStruct((rows, part), jnp.float32),
+            jax.ShapeDtypeStruct((keys, 2 * part), jnp.bfloat16),
         ),
         grid_spec=pltpu.PrefetchScalarGridSpec(
             num_scalar_prefetch=1,
-            grid=(blocks,),
+            grid=(count,),
             in_specs=[
-                pl.BlockSpec((rows, HEAD_BLOCK), lambda h, m: (0, h)),
-                pl.BlockSpec((keys, HEAD_BLOCK), lambda h, m: (0, h)),
-                pl.BlockSpec((keys, HEAD_BLOCK), lambda h, m: (0, h + blocks)),
-                pl.BlockSpec((rows, HEAD_BLOCK), lambda h, m: (0, h)),
+                pl.BlockSpec((rows, HEAD_BLOCK), lambda h, m: (0, h + first)),
+                pl.BlockSpec((keys, HEAD_BLOCK), lambda h, m: (0, h + first)),
+                pl.BlockSpec((keys, HEAD_BLOCK), lambda h, m: (0, h + first + blocks)),
+                pl.BlockSpec((rows, HEAD_BLOCK), lambda h, m: (0, h + first)),
             ],
             out_specs=[
                 pl.BlockSpec((rows, HEAD_BLOCK), lambda h, m: (0, h)),
@@ -129,9 +130,9 @@
             dimension_semantics=("arbitrary",), vmem_limit_bytes=48 * 1024 * 1024
         ),
         cost_estimate=pl.CostEstimate(
-            flops=10 * rows * keys * width,
-            transcendentals=rows * keys * (width // head_dim),
-            bytes_accessed=2 * (3 * rows * width + 4 * keys * width) + 4 * rows * width,
+            flops=10 * rows * keys * part,
+            transcendentals=rows * keys * (part // head_dim),
+            bytes_accessed=2 * (3 * rows * part + 4 * keys * part) + 4 * rows * part,
         ),
     )(meta, query_rows, kv_rows, kv_rows, back_rows)
 
@@ -381,17 +382,26 @@
         ),
         w_rows,
     )
-    query_rot_back, kv_back = attention_backward(
-        meta, query_flat, kv_all, blended_value_gradient.reshape(rows, width), head_dim, score_scale
-    )
-    query_rot_back = query_rot_back.reshape(slots, rows, head_count, head_dim)
-    key_value = jnp.sum(
-        lax.all_to_all(kv_back.reshape(n_ctx, rows, 2 * width), CTX, 0, 0, tiled=False).astype(
-            jnp.float32
-        ),
-        axis=0,
-    )
-    key_value = key_value.reshape(rows, width // HEAD_BLOCK, 2, HEAD_BLOCK)
+    n_head_blocks = width // HEAD_BLOCK
+    half_blocks = n_head_blocks // 2
+    back_flat = blended_value_gradient.reshape(rows, width)
+    dq_parts = []
+    kv_parts = []
+    for first in (0, half_blocks):
+        dq_part, kv_back = attention_backward(
+            meta, query_flat, kv_all, back_flat, head_dim, score_scale, first, half_blocks
+        )
+        dq_parts.append(dq_part)
+        kv_parts.append(
+            jnp.sum(
+                lax.all_to_all(
+                    kv_back.reshape(n_ctx, rows, kv_back.shape[1]), CTX, 0, 0, tiled=False
+                ).astype(jnp.float32),
+                axis=0,
+            ).reshape(rows, half_blocks, 2, HEAD_BLOCK)
+        )
+    query_rot_back = jnp.concatenate(dq_parts, axis=-1).reshape(slots, rows, head_count, head_dim)
+    key_value = jnp.concatenate(kv_parts, axis=1)
     key_rot_back = key_value[:, :, 0, :].reshape(slots, rows, head_count, head_dim)
     value_mix_back = key_value[:, :, 1, :].reshape(slots, rows, width)
     first_grad = 0.5 * value_mix_back

time: 632 us -> 600 us (0.949)
  waiting for transfers between devices: 285 us -> 261 us
  starting transfers between devices: 99.2 us -> 88 us
    ppermute x9, starting transfers between devices: 43.4 us -> 17.4 us  [ctx_allreduce(): other = lax.ppermute(total, CTX, [(j, j ^ step) for j in range(n_ctx)])]
    all_to_all x1 -> x2, waiting for transfers between devices: 84.6 us -> 61 us  [body(): lax.all_to_all(kv_back.reshape(n_ctx, rows, kv_back.shape[1]), CTX, 0, 0,...]
    all_to_all x1 -> x2, starting transfers between devices: 35.7 us -> 50.7 us  [body(): lax.all_to_all(kv_back.reshape(n_ctx, rows, kv_back.shape[1]), CTX, 0, 0,...]
    pallas_call x1 -> x2, Pallas kernels: 41.4 us -> 43 us  [attention_backward(): pl.pallas_call(functools.partial(attn_bwd_kernel, head_dim, scale), out_s...]
  transfers between devices with their start and end apart: 23 -> 24, of which waited for: 14 -> 15; matrix products, arithmetic and copies ran while one was open for 18% -> 19% of each run, Pallas kernels for 10% -> 11%
where the time goes in v18:
time: 600 us; the launch traced here: 593 us
  waiting for transfers between devices  261 us (44%)
  starting transfers between devices  88 us (15%)
  local copies, waits for them, and re-layouts  67.4 us (11%)
  Pallas kernels  65.4 us (11%)
  other arithmetic  52.3 us (9%)
  matrix products  43.5 us (7%)
  between operations  15.4 us (3%)
    all_to_all x1, waiting for transfers between devices, body(): lax.all_to_all(jnp.broadcast_to(kv_own[None], (n_ctx, rows, 2 * width)),...  92.6 us
    all_to_all x2, waiting for transfers between devices, body(): lax.all_to_all(kv_back.reshape(n_ctx, rows, kv_back.shape[1]), CTX, 0, 0,...  61 us
    ppermute x9, waiting for transfers between devices, ctx_allreduce(): other = lax.ppermute(total, CTX, [(j, j ^ step) for j in range(n_ctx)])  51.2 us
    all_to_all x2, starting transfers between devices, body(): lax.all_to_all(kv_back.reshape(n_ctx, rows, kv_back.shape[1]), CTX, 0, 0,...  50.7 us
    pallas_call x2, Pallas kernels, attention_backward(): pl.pallas_call(functools.partial(attn_bwd_kernel, head_dim, scale), out_s...  43 us
    ppermute x3, waiting for transfers between devices, z_exchange(): return zh_pair(pack, lax.ppermute(pack, ('zh', 'zl'), Z_CROSS))  34.3 us
    pallas_call x1, Pallas kernels, attention_forward(): pl.pallas_call(functools.partial(attn_fwd_kernel, head_dim, scale), out_s...  22.4 us
    ppermute x3, waiting for transfers between devices, z_combine(): got = lax.ppermute(theirs, ('zh', 'zl'), Z_CROSS)  18.6 us
  transfers between devices with their start and end apart: 24, of which 15 were waited for; matrix products, arithmetic and copies ran while one was open for 19% of the time, Pallas kernels for 11%

profile of v18, /device:TPU:0, one launch (start us, length us, event | category | flops | bytes accessed | tf_op | source)
XLA Modules:
  0.0 592.8 jit_solution(10444628918935811880)
XLA Ops:
  9.1 4.2 collective-permute-start.2
  13.3 7.0 %collective-permute-done.2 = bf16[144,1024]{1,0:T(8,128)(2,1)S(1)} collective-permute-done((bf16[144,1024]{1,0:T(8,128)(2,1)S(1)}, bf16[144,1024]{1,0:T(8,128)(2,1)S(1)}, u32[]{:S(2)}, u32[]{:S(2)}) %collective-permute-start.2) | collective-permute-done | bytes 294944 | tf_op jit(solution)/shard_map/ppermute | solution.py:199
  22.5 3.0 collective-permute-start
  26.0 14.8 %collective-permute-done = bf16[304,1024]{1,0:T(8,128)(2,1)S(1)} collective-permute-done((bf16[304,1024]{1,0:T(8,128)(2,1)S(1)}, bf16[304,1024]{1,0:T(8,128)(2,1)S(1)}, u32[]{:S(2)}, u32[]{:S(2)}) %collective-permute-start) | collective-permute-done | bytes 622624 | tf_op jit(solution)/shard_map/ppermute | solution.py:199
  42.0 12.5 %collective-permute-done.1 = bf16[64,5632]{1,0:T(8,128)(2,1)S(1)} collective-permute-done((bf16[64,5632]{1,0:T(8,128)(2,1)S(1)}, bf16[64,5632]{1,0:T(8,128)(2,1)S(1)}, u32[]{:S(2)}, u32[]{:S(2)}) %collective-permute-start.1) | collective-permute-done | bytes 720928 | tf_op jit(solution)/shard_map/ppermute | solution.py:199
  55.8 2.3 all-gather.7.cloned.1.call-done
  61.4 4.5 fusion.55
  65.9 4.6 copy.170
  70.4 2.5 convolution_bitcast_fusion.5
  74.2 1.8 fusion.13
  76.2 4.4 broadcast_in_dim.72
  80.5 5.3 all-to-all-start
  88.2 92.6 %all-to-all-done = bf16[8,256,2048]{2,1,0:T(8,128)(2,1)} async-done(((bf16[8,256,2048]{2,1,0:T(8,128)(2,1)}), bf16[8,256,2048]{2,1,0:T(8,128)(2,1)}, u32[]{:S(2)}, u32[]{:S(2)}) %all-to-all-start) | async-done | bytes 8388640 | tf_op jit(solution)/shard_map/all_to_all | solution.py:317
  180.8 4.2 fusion.54
  185.0 4.1 copy.173
  189.1 2.3 convolution_bitcast_fusion.3
  191.8 22.4 %shard_map.229 = bf16[256,1024]{1,0:T(8,128)(2,1)S(1)} custom-call(s32[2]{0:T(128)S(1)} %pad_add_fusion.meta_ref, bf16[256,1024]{1,0:T(8,128)(2,1)S(1)} %copy.175.q_ref, bf16[2048,2048]{1,0:T(8,128)(2,1)} %bitcast.24.k_ref.v_ref, bf16[2048,2048]{1,0:T(8,128)(2,1)} %bitcast.24.k_ref.v_ref), custom_call_target="tpu_custom_call" | custom-call | flops 2147483648 | bytes 9437184 | tf_op jit(solution)/shard_map/pallas_call | solution.py:80
  215.3 1.9 copy.177
  217.1 3.4 slice.116
  220.6 1.8 convolution_bitcast_fusion.1
  223.1 1.8 copy.183
  224.8 3.5 copy.184
  228.3 1.9 multiply_reduce_fusion.2
  233.5 6.3 %convolution_bitcast_fusion = f32[1,256,5632]{2,1,0:T(8,128)S(1)} fusion(bf16[256,1024]{0,1:T(8,128)(2,1)S(1)} %bitcast.249, bf16[1024,5632]{1,0:T(8,128)(2,1)} %bitcast.242), kind=kOutput, calls=%fused_computation.6 | convolution fusion | flops 2952790016 | bytes 17825792 | tf_op jit(solution)/shard_map/dot_general | solution.py:334
  239.7 2.9 multiply_convert_fusion.1
  242.7 3.2 fusion.6
  246.9 2.6 copy.187
  249.5 2.5 multiply_reduce_fusion
  252.0 2.1 subtract_add_fusion
  254.2 6.1 %convolution_convert_fusion = bf16[8,128,5632]{2,1,0:T(8,128)(2,1)} fusion(bf16[8,128,256]{2,1,0:T(8,128)(2,1)S(1)} %bitcast.250, bf16[1,256,2816]{2,1,0:T(8,128)(2,1)S(1)} %copy-done.23, bf16[1,256,2816]{2,1,0:T(8,128)(2,1)S(1)} %copy-done.21), kind=kOutput, calls=%fused_computation.3 | convolution fusion | flops 2964324352 | bytes 14942208 | tf_op jit(solution)/shard_map/srd,srf->df/dot_general | solution.py:352
  261.0 11.1 %pad_maximum_fusion = bf16[8,128,6656]{2,1,0:T(8,128)(2,1)} fusion(bf16[8,128,1024]{2,1,0:T(8,128)(2,1)S(1)} %convolution_convert_fusion.2, bf16[8,128,5632]{2,1,0:T(8,128)(2,1)} %convolution_convert_fusion), kind=kLoop, calls=%fused_computation.1 | loop fusion | flops 27262976 | bytes 27262976 | tf_op jit(solution)/shard_map/concatenate | solution.py:370
  272.1 2.0 convolution_convert_fusion.6
  274.6 21.7 %shard_map.231 = (f32[256,512]{1,0:T(8,128)S(1)}, bf16[2048,1024]{1,0:T(8,128)(2,1)S(1)}) custom-call(s32[2]{0:T(128)S(1)} %pad_add_fusion.meta_ref, bf16[256,1024]{1,0:T(8,128)(2,1)S(1)} %copy.175.q_ref, bf16[2048,2048]{1,0:T(8,128)(2,1)} %bitcast.24.k_ref.v_ref, bf16[2048,2048]{1,0:T(8,128)(2,1)} %bitcast.24.k_ref.v_ref, bf16[256,1024]{1,0:T(8,128)(2,1)S(1)} %copy.191.do_ref), custom_call_target="tpu_custom_call" | custom-call | flops 2684354560 | bytes 9699328 | tf_op jit(solution)/shard_map/pallas_call | solution.py:109
  296.3 1.9 copy-done.1
  298.2 35.7 %all-to-all-start.2 = ((bf16[8,256,1024]{2,1,0:T(8,128)(2,1)}), bf16[8,256,1024]{2,1,0:T(8,128)(2,1)}, u32[]{:S(2)}, u32[]{:S(2)}) async-start(bf16[8,256,1024]{2,1,0:T(8,128)(2,1)} %bitcast.225), calls=%async_computation.2 | async-start | bytes 8388608 | tf_op jit(solution)/shard_map/all_to_all | solution.py:397
  334.0 1.7 copy.181
  337.3 4.2 convolution_convert_fusion.1
  341.5 21.3 %shard_map.230 = (f32[256,512]{1,0:T(8,128)S(1)}, bf16[2048,1024]{1,0:T(8,128)(2,1)S(1)}) custom-call(s32[2]{0:T(128)S(1)} %pad_add_fusion.meta_ref, bf16[256,1024]{1,0:T(8,128)(2,1)S(1)} %copy.175.q_ref, bf16[2048,2048]{1,0:T(8,128)(2,1)} %bitcast.24.k_ref.v_ref, bf16[2048,2048]{1,0:T(8,128)(2,1)} %bitcast.24.k_ref.v_ref, bf16[256,1024]{1,0:T(8,128)(2,1)S(1)} %copy.191.do_ref), custom_call_target="tpu_custom_call" | custom-call | flops 2684354560 | bytes 9699328 | tf_op jit(solution)/shard_map/pallas_call | solution.py:109
  362.9 1.9 copy-done
  364.8 17.9 %all-to-all-done.2 = bf16[8,256,1024]{2,1,0:T(8,128)(2,1)} async-done(((bf16[8,256,1024]{2,1,0:T(8,128)(2,1)}), bf16[8,256,1024]{2,1,0:T(8,128)(2,1)}, u32[]{:S(2)}, u32[]{:S(2)}) %all-to-all-start.2) | async-done | bytes 4194336 | tf_op jit(solution)/shard_map/all_to_all | solution.py:397
  382.7 15.0 %all-to-all-start.1 = ((bf16[8,256,1024]{2,1,0:T(8,128)(2,1)}), bf16[8,256,1024]{2,1,0:T(8,128)(2,1)}, u32[]{:S(2)}, u32[]{:S(2)}) async-start(bf16[8,256,1024]{2,1,0:T(8,128)(2,1)} %bitcast.224), calls=%async_computation.1 | async-start | bytes 8388608 | tf_op jit(solution)/shard_map/all_to_all | solution.py:397
  398.5 3.3 convert_reduce_fusion
  402.1 43.1 %all-to-all-done.1 = bf16[8,256,1024]{2,1,0:T(8,128)(2,1)} async-done(((bf16[8,256,1024]{2,1,0:T(8,128)(2,1)}), bf16[8,256,1024]{2,1,0:T(8,128)(2,1)}, u32[]{:S(2)}, u32[]{:S(2)}) %all-to-all-start.1) | async-done | bytes 4194336 | tf_op jit(solution)/shard_map/all_to_all | solution.py:397
  445.2 3.2 convert_reduce_fusion.1
  449.6 2.4 fusion.52
  456.2 1.7 convolution_add_fusion
  458.0 1.6 copy.198
  465.2 3.3 fusion.1
  469.7 3.5 collective-permute-start.7
  474.4 18.6 %collective-permute-done.7 = bf16[64,6656]{1,0:T(8,128)(2,1)S(1)} collective-permute-done((bf16[64,6656]{1,0:T(8,128)(2,1)S(1)}, bf16[64,6656]{1,0:T(8,128)(2,1)S(1)}, u32[]{:S(2)}, u32[]{:S(2)}) %collective-permute-start.7) | collective-permute-done | bytes 852000 | tf_op jit(solution)/shard_map/ppermute | solution.py:225
  494.3 6.5 %collective-permute-start.8 = (bf16[64,6656]{1,0:T(8,128)(2,1)S(1)}, bf16[64,6656]{1,0:T(8,128)(2,1)S(1)}, u32[]{:S(2)}, u32[]{:S(2)}) collective-permute-start(bf16[64,6656]{1,0:T(8,128)(2,1)S(1)} %fusion.5), channel_id=1, source_target_pairs={{0,1},{1,0},{2,3},{3,2},{4,5},{5,4},{6,7},{7,6},{8,9},{9,8},{10,11... | collective-permute-start | bytes 2555912 | tf_op jit(solution)/shard_map/ppermute | solution.py:233
  500.9 2.4 collective-permute-start.12
  503.4 20.0 %collective-permute-done.12 = bf16[176,1024]{1,0:T(8,128)(2,1)S(1)} collective-permute-done((bf16[176,1024]{1,0:T(8,128)(2,1)S(1)}, bf16[176,1024]{1,0:T(8,128)(2,1)S(1)}, u32[]{:S(2)}, u32[]{:S(2)}) %collective-permute-start.12) | collective-permute-done | bytes 360480 | tf_op jit(solution)/shard_map/ppermute | solution.py:233
  524.2 5.9 %collective-permute-start.13 = (bf16[176,1024]{1,0:T(8,128)(2,1)}, bf16[176,1024]{1,0:T(8,128)(2,1)}, u32[]{:S(2)}, u32[]{:S(2)}) collective-permute-start(bf16[176,1024]{1,0:T(8,128)(2,1)} %add_convert_fusion.8), channel_id=1, source_target_pairs={{0,2},{1,3},{2,0},{3,1},{4,6},{5,7},{6,4},{7,5},{8,10},{9,11},{10,... | collective-permute-start | bytes 1081352 | tf_op jit(solution)/shard_map/ppermute | solution.py:233
  530.8 5.2 fusion.14
  537.3 2.5 collective-permute-done.13
  539.8 1.9 add_convert_fusion.7
  542.9 3.0 collective-permute-start.3
  545.9 9.0 %collective-permute-done.9 = bf16[64,6656]{1,0:T(8,128)(2,1)} collective-permute-done((bf16[64,6656]{1,0:T(8,128)(2,1)S(1)}, bf16[64,6656]{1,0:T(8,128)(2,1)}, u32[]{:S(2)}, u32[]{:S(2)}) %collective-permute-start.9) | collective-permute-done | bytes 852000 | tf_op jit(solution)/shard_map/ppermute | solution.py:233
  558.0 2.0 fusion.39
  560.1 5.8 collective-permute-done.4
  567.0 4.0 collective-permute-done.10
  571.8 3.9 collective-permute-done.5
  578.1 6.0 %collective-permute-done.6 = bf16[208,1024]{1,0:T(8,128)(2,1)S(1)} collective-permute-done((bf16[208,1024]{1,0:T(8,128)(2,1)S(1)}, bf16[208,1024]{1,0:T(8,128)(2,1)S(1)}, u32[]{:S(2)}, u32[]{:S(2)}) %collective-permute-start.6) | collective-permute-done | bytes 426016 | tf_op jit(solution)/shard_map/ppermute | solution.py:233
  (221 shorter events, 51.7 us)
Async XLA Ops:
  7.2 15.2 %copy-start.40 = (bf16[64,1024]{1,0:T(8,128)(2,1)S(1)}, bf16[64,1024]{1,0:T(8,128)(2,1)}, u32[]{:S(2)}) copy-start(bf16[64,1024]{1,0:T(8,128)(2,1)} %param.16) | copy-start | bytes 393220
  7.2 15.2 %copy-start.41 = (bf16[64,1024]{1,0:T(8,128)(2,1)S(1)}, bf16[64,1024]{1,0:T(8,128)(2,1)}, u32[]{:S(2)}) copy-start(bf16[64,1024]{1,0:T(8,128)(2,1)} %param.19) | copy-start | bytes 393220
  7.2 15.3 %copy-start.36 = (bf16[176,1024]{1,0:T(8,128)(2,1)S(1)}, bf16[176,1024]{1,0:T(8,128)(2,1)}, u32[]{:S(2)}) copy-start(bf16[176,1024]{1,0:T(8,128)(2,1)} %param.22) | copy-start | bytes 1081348
  7.2 18.3 %copy-start.37 = (bf16[64,2816]{1,0:T(8,128)(2,1)S(1)}, bf16[64,2816]{1,0:T(8,128)(2,1)}, u32[]{:S(2)}) copy-start(bf16[64,2816]{1,0:T(8,128)(2,1)} %param.20) | copy-start | bytes 1081348
  7.2 18.3 %copy-start.38 = (bf16[64,2816]{1,0:T(8,128)(2,1)S(1)}, bf16[64,2816]{1,0:T(8,128)(2,1)}, u32[]{:S(2)}) copy-start(bf16[64,2816]{1,0:T(8,128)(2,1)} %param.21) | copy-start | bytes 1081348
  7.2 50.9 %all-gather.7.cloned.1.call-start = ((), (), s32[]{:S(2)}) async-start(), calls=%async_computation.9 | async-start | bytes 5308416 | tf_op jit(solution)/shard_map/all_gather | solution.py:203
  9.1 11.2 %collective-permute-start.2 = (bf16[144,1024]{1,0:T(8,128)(2,1)S(1)}, bf16[144,1024]{1,0:T(8,128)(2,1)S(1)}, u32[]{:S(2)}, u32[]{:S(2)}) collective-permute-start(bf16[144,1024]{1,0:T(8,128)(2,1)S(1)} %fusion.40), channel_id=1, source_target_pairs={{0,68},{68,0},{4,64},{64,4},{1,69},{69,1},{5,65},{65,5},{2,70},{70... | collective-permute-start | bytes 884744 | tf_op jit(solution)/shard_map/ppermute | solution.py:199
  22.3 158.4 %all-gather.9.cloned.1.call-start = ((), (), s32[]{:S(2)}) async-start(), calls=%async_computation.10 | async-start | bytes 11206656 | tf_op jit(solution)/shard_map/all_gather | solution.py:203
  22.5 18.3 %collective-permute-start = (bf16[304,1024]{1,0:T(8,128)(2,1)S(1)}, bf16[304,1024]{1,0:T(8,128)(2,1)S(1)}, u32[]{:S(2)}, u32[]{:S(2)}) collective-permute-start(bf16[304,1024]{1,0:T(8,128)(2,1)S(1)} %constant_dynamic-update-slice_fusion), channel_id=1, source_target_pairs={{0,68},{68,0},{4,64},{64,4},{1,69},{69,1},{5,65},{65,5},{2,70},{70... | collective-permute-start | bytes 1867784 | tf_op jit(solution)/shard_map/ppermute | solution.py:199
  25.6 28.9 %collective-permute-start.1 = (bf16[64,5632]{1,0:T(8,128)(2,1)S(1)}, bf16[64,5632]{1,0:T(8,128)(2,1)S(1)}, u32[]{:S(2)}, u32[]{:S(2)}) collective-permute-start(bf16[64,5632]{1,0:T(8,128)(2,1)S(1)} %constant_dynamic-update-slice_fusion.3), channel_id=1, source_target_pairs={{0,68},{68,0},{4,64},{64,4},{1,69},{69,1},{5,65},{65,5},{2,70},{70... | collective-permute-start | bytes 2162696 | tf_op jit(solution)/shard_map/ppermute | solution.py:199
  54.6 4.4 copy-start.10
  58.1 175.3 %all-gather.11.cloned.1.call-start = ((), (), s32[]{:S(2)}) async-start(), calls=%async_computation.11 | async-start | bytes 12976128 | tf_op jit(solution)/shard_map/all_gather | solution.py:203
  59.9 131.4 %copy-start.34 = (f32[256,32]{0,1:T(8,128)}, f32[256,32]{0,1:T(8,128)S(1)}, u32[]{:S(2)}) copy-start(f32[256,32]{0,1:T(8,128)S(1)} %get-tuple-element.125) | copy-start | bytes 98308
  61.4 12.8 %copy-start.13 = (bf16[1,256,8,2,64]{1,4,3,2,0:T(8,128)(2,1)}, bf16[1,256,8,2,64]{1,4,3,2,0:T(8,128)(2,1)S(1)}, u32[]{:S(2)}) copy-start(bf16[1,256,8,2,64]{1,4,3,2,0:T(8,128)(2,1)S(1)} %copy.168) | copy-start | bytes 1572868
  65.9 8.4 %copy-start.2 = (bf16[16,64,1024]{2,1,0:T(8,128)(2,1)}, bf16[16,64,1024]{2,1,0:T(8,128)(2,1)S(1)}, u32[]{:S(2)}) copy-start(bf16[16,64,1024]{2,1,0:T(8,128)(2,1)S(1)} %get-tuple-element.96) | copy-start | bytes 6291460
  80.5 5.4 copy-start.46
  80.5 5.4 copy-start.47
  80.5 100.2 %all-to-all-start = ((bf16[8,256,2048]{2,1,0:T(8,128)(2,1)}), bf16[8,256,2048]{2,1,0:T(8,128)(2,1)}, u32[]{:S(2)}, u32[]{:S(2)}) async-start(bf16[8,256,2048]{2,1,0:T(8,128)(2,1)} %broadcast_in_dim.72), calls=%async_computation | async-start | bytes 16777216 | tf_op jit(solution)/shard_map/all_to_all | solution.py:317
  85.9 382.6 %reduce-scatter.4.cloned.1.call-start = ((), (), s32[]{:S(2)}) async-start(), calls=%async_computation.6 | async-start | bytes 15335424 | tf_op jit(solution)/shard_map/reduce_scatter | solution.py:215
  88.1 164.0 %copy-start.43 = (pred[256]{0:T(512)(128)(4,1)}, pred[256]{0:T(512)(128)(4,1)S(1)}, u32[]{:S(2)}) copy-start(pred[256]{0:T(512)(128)(4,1)S(1)} %fusion.47) | copy-start | bytes 772
  184.9 4.1 copy-start.14
  217.1 3.4 copy-start.29
  220.5 2.5 copy-start.24
  224.8 3.5 copy-start.11
  233.4 6.3 %copy-start.16 = (f32[1,256,2816]{2,1,0:T(8,128)S(1)}, f32[1,256,2816]{2,1,0:T(8,128)}, u32[]{:S(2)}) copy-start(f32[1,256,2816]{2,1,0:T(8,128)} %copy.184) | copy-start | bytes 8650756
  233.4 9.2 %slice-start = ((s8[11534336]{0:T(1024)(128)(4,1)}), s8[4194304]{0:T(1024)(128)(4,1)S(1)}, s32[]{:S(2)}) async-start(s8[11534336]{0:T(1024)(128)(4,1)} %bitcast.243), calls=%async_computation.12 | async-start | bytes 8388608
  233.4 9.2 %slice-start.1 = ((s8[11534336]{0:T(1024)(128)(4,1)}), s8[4194304]{0:T(1024)(128)(4,1)S(1)}, s32[]{:S(2)}) async-start(s8[11534336]{0:T(1024)(128)(4,1)} %bitcast.243), calls=%async_computation.13 | async-start | bytes 8388608
  239.7 2.9 slice-start.2
  242.7 3.2 copy-start.20
  242.7 3.2 copy-start.22
  249.5 4.7 copy-start.21
  249.5 4.7 copy-start.23
  254.2 6.1 %copy-start.6 = (f32[1,256,1024]{2,1,0:T(8,128)}, f32[1,256,1024]{2,1,0:T(8,128)S(1)}, u32[]{:S(2)}) copy-start(f32[1,256,1024]{2,1,0:T(8,128)S(1)} %subtract_add_fusion) | copy-start | bytes 3145732
  254.2 6.1 %copy-start.25 = (bf16[1,256,8,2,64]{1,4,3,2,0:T(8,128)(2,1)S(1)}, bf16[1,256,8,2,64]{1,4,3,2,0:T(8,128)(2,1)}, u32[]{:S(2)}) copy-start(bf16[1,256,8,2,64]{1,4,3,2,0:T(8,128)(2,1)} %copy.177) | copy-start | bytes 1572868
  298.2 35.7 %copy-start.19 = (bf16[1,256,2816]{2,1,0:T(8,128)(2,1)S(1)}, bf16[1,256,2816]{2,1,0:T(8,128)(2,1)}, u32[]{:S(2)}) copy-start(bf16[1,256,2816]{2,1,0:T(8,128)(2,1)} %get-tuple-element.92) | copy-start | bytes 4325380
  298.2 84.4 %all-to-all-start.2 = ((bf16[8,256,1024]{2,1,0:T(8,128)(2,1)}), bf16[8,256,1024]{2,1,0:T(8,128)(2,1)}, u32[]{:S(2)}, u32[]{:S(2)}) async-start(bf16[8,256,1024]{2,1,0:T(8,128)(2,1)} %bitcast.225), calls=%async_computation.2 | async-start | bytes 8388608 | tf_op jit(solution)/shard_map/all_to_all | solution.py:397
  333.9 139.3 %reduce-scatter.8.cloned.1.call-start = ((), (), s32[]{:S(2)}) async-start(), calls=%async_computation.8 | async-start | bytes 6488064 | tf_op jit(solution)/shard_map/reduce_scatter | solution.py:215
  333.9 3.3 copy-start.30
  337.2 4.2 copy-start.17
  382.7 62.5 %all-to-all-start.1 = ((bf16[8,256,1024]{2,1,0:T(8,128)(2,1)}), bf16[8,256,1024]{2,1,0:T(8,128)(2,1)}, u32[]{:S(2)}, u32[]{:S(2)}) async-start(bf16[8,256,1024]{2,1,0:T(8,128)(2,1)} %bitcast.224), calls=%async_computation.1 | async-start | bytes 8388608 | tf_op jit(solution)/shard_map/all_to_all | solution.py:397
  397.7 144.1 %reduce-scatter.6.cloned.1.call-start = ((), (), s32[]{:S(2)}) async-start(), calls=%async_computation.7 | async-start | bytes 7667712 | tf_op jit(solution)/shard_map/reduce_scatter | solution.py:215
  449.6 2.4 copy-start.39
  452.5 2.9 copy-start.26
  458.0 4.3 copy-start.12
  459.6 3.2 copy-start.15
  469.7 23.3 %collective-permute-start.7 = (bf16[64,6656]{1,0:T(8,128)(2,1)S(1)}, bf16[64,6656]{1,0:T(8,128)(2,1)S(1)}, u32[]{:S(2)}, u32[]{:S(2)}) collective-permute-start(bf16[64,6656]{1,0:T(8,128)(2,1)S(1)} %dynamic-slice_bitcast_fusion), channel_id=1, source_target_pairs={{0,68},{68,0},{4,64},{64,4},{1,69},{69,1},{5,65},{65,5},{2,70},{70... | collective-permute-start | bytes 2555912 | tf_op jit(solution)/shard_map/ppermute | solution.py:225
  473.1 27.7 %copy-start.33 = (bf16[1,352,1024]{2,1,0:T(8,128)(2,1)S(1)}, bf16[1,352,1024]{2,1,0:T(8,128)(2,1)}, u32[]{:S(2)}) copy-start(bf16[1,352,1024]{2,1,0:T(8,128)(2,1)} %reduce-scatter.8.cloned.1.call-done) | copy-start | bytes 2162692
  474.2 26.6 %collective-permute-start.11 = (bf16[176,1024]{1,0:T(8,128)(2,1)S(1)}, bf16[176,1024]{1,0:T(8,128)(2,1)S(1)}, u32[]{:S(2)}, u32[]{:S(2)}) collective-permute-start(bf16[176,1024]{1,0:T(8,128)(2,1)S(1)} %dynamic-slice_bitcast_fusion.2), channel_id=1, source_target_pairs={{0,68},{68,0},{4,64},{64,4},{1,69},{69,1},{5,65},{65,5},{2,70},{70... | collective-permute-start | bytes 1081352 | tf_op jit(solution)/shard_map/ppermute | solution.py:225
  494.3 36.4 %copy-start.9 = (f32[1,256,1024]{2,1,0:T(8,128)S(1)}, f32[1,256,1024]{2,1,0:T(8,128)}, u32[]{:S(2)}) copy-start(f32[1,256,1024]{2,1,0:T(8,128)} %copy-done.8) | copy-start | bytes 3145732
  494.3 36.4 %copy-start.18 = (bf16[1,256,8,2,176]{1,4,3,2,0:T(8,128)(2,1)S(1)}, bf16[1,256,8,2,176]{1,4,3,2,0:T(8,128)(2,1)}, u32[]{:S(2)}) copy-start(bf16[1,256,8,2,176]{1,4,3,2,0:T(8,128)(2,1)} %copy-done.17) | copy-start | bytes 4325380
  494.3 36.4 %copy-start.45 = (pred[256]{0:T(512)(128)(4,1)S(1)}, pred[256]{0:T(512)(128)(4,1)}, u32[]{:S(2)}) copy-start(pred[256]{0:T(512)(128)(4,1)} %copy-done.43) | copy-start | bytes 772
  494.3 35.8 %collective-permute-start.8 = (bf16[64,6656]{1,0:T(8,128)(2,1)S(1)}, bf16[64,6656]{1,0:T(8,128)(2,1)S(1)}, u32[]{:S(2)}, u32[]{:S(2)}) collective-permute-start(bf16[64,6656]{1,0:T(8,128)(2,1)S(1)} %fusion.5), channel_id=1, source_target_pairs={{0,1},{1,0},{2,3},{3,2},{4,5},{5,4},{6,7},{7,6},{8,9},{9,8},{10,11... | collective-permute-start | bytes 2555912 | tf_op jit(solution)/shard_map/ppermute | solution.py:233
  500.9 22.4 %collective-permute-start.12 = (bf16[176,1024]{1,0:T(8,128)(2,1)S(1)}, bf16[176,1024]{1,0:T(8,128)(2,1)S(1)}, u32[]{:S(2)}, u32[]{:S(2)}) collective-permute-start(bf16[176,1024]{1,0:T(8,128)(2,1)S(1)} %fusion.31), channel_id=1, source_target_pairs={{0,1},{1,0},{2,3},{3,2},{4,5},{5,4},{6,7},{7,6},{8,9},{9,8},{10,11... | collective-permute-start | bytes 1081352 | tf_op jit(solution)/shard_map/ppermute | solution.py:233
  524.2 15.6 %collective-permute-start.13 = (bf16[176,1024]{1,0:T(8,128)(2,1)}, bf16[176,1024]{1,0:T(8,128)(2,1)}, u32[]{:S(2)}, u32[]{:S(2)}) collective-permute-start(bf16[176,1024]{1,0:T(8,128)(2,1)} %add_convert_fusion.8), channel_id=1, source_target_pairs={{0,2},{1,3},{2,0},{3,1},{4,6},{5,7},{6,4},{7,5},{8,10},{9,11},{10,... | collective-permute-start | bytes 1081352 | tf_op jit(solution)/shard_map/ppermute | solution.py:233
  530.4 24.6 %collective-permute-start.9 = (bf16[64,6656]{1,0:T(8,128)(2,1)S(1)}, bf16[64,6656]{1,0:T(8,128)(2,1)}, u32[]{:S(2)}, u32[]{:S(2)}) collective-permute-start(bf16[64,6656]{1,0:T(8,128)(2,1)S(1)} %add_convert_fusion.2), channel_id=1, source_target_pairs={{0,2},{1,3},{2,0},{3,1},{4,6},{5,7},{6,4},{7,5},{8,10},{9,11},{10,... | collective-permute-start | bytes 2555912 | tf_op jit(solution)/shard_map/ppermute | solution.py:233
  530.7 5.2 copy-start.28
  537.3 19.4 %copy-start.7 = (f32[1,256,1024]{2,1,0:T(8,128)S(1)}, f32[1,256,1024]{2,1,0:T(8,128)}, u32[]{:S(2)}) copy-start(f32[1,256,1024]{2,1,0:T(8,128)} %copy-done.6) | copy-start | bytes 3145732
  541.8 16.3 %collective-permute-start.14 = (bf16[176,1024]{1,0:T(8,128)(2,1)}, bf16[176,1024]{1,0:T(8,128)(2,1)}, u32[]{:S(2)}, u32[]{:S(2)}) collective-permute-start(bf16[176,1024]{1,0:T(8,128)(2,1)} %add_convert_fusion.7), channel_id=1, source_target_pairs={{0,4},{1,5},{2,6},{3,7},{4,0},{5,1},{6,2},{7,3},{8,12},{9,13},{10,... | collective-permute-start | bytes 1081352 | tf_op jit(solution)/shard_map/ppermute | solution.py:233
  541.8 14.7 %copy-start.32 = (bf16[1,416,1024]{2,1,0:T(8,128)(2,1)S(1)}, bf16[1,416,1024]{2,1,0:T(8,128)(2,1)}, u32[]{:S(2)}) copy-start(bf16[1,416,1024]{2,1,0:T(8,128)(2,1)} %reduce-scatter.6.cloned.1.call-done) | copy-start | bytes 2555908
  542.9 13.5 %collective-permute-start.3 = (bf16[208,1024]{1,0:T(8,128)(2,1)S(1)}, bf16[208,1024]{1,0:T(8,128)(2,1)S(1)}, u32[]{:S(2)}, u32[]{:S(2)}) collective-permute-start(bf16[208,1024]{1,0:T(8,128)(2,1)S(1)} %dynamic-slice_bitcast_fusion.1), channel_id=1, source_target_pairs={{0,68},{68,0},{4,64},{64,4},{1,69},{69,1},{5,65},{65,5},{2,70},{70... | collective-permute-start | bytes 1277960 | tf_op jit(solution)/shard_map/ppermute | solution.py:225
  556.3 14.6 %collective-permute-start.10 = (bf16[64,6656]{1,0:T(8,128)(2,1)S(1)}, bf16[64,6656]{1,0:T(8,128)(2,1)S(1)}, u32[]{:S(2)}, u32[]{:S(2)}) collective-permute-start(bf16[64,6656]{1,0:T(8,128)(2,1)S(1)} %add_convert_fusion.1), channel_id=1, source_target_pairs={{0,4},{1,5},{2,6},{3,7},{4,0},{5,1},{6,2},{7,3},{8,12},{9,13},{10,... | collective-permute-start | bytes 2555912 | tf_op jit(solution)/shard_map/ppermute | solution.py:233
  556.6 9.3 %collective-permute-start.4 = (bf16[208,1024]{1,0:T(8,128)(2,1)S(1)}, bf16[208,1024]{1,0:T(8,128)(2,1)S(1)}, u32[]{:S(2)}, u32[]{:S(2)}) collective-permute-start(bf16[208,1024]{1,0:T(8,128)(2,1)S(1)} %fusion.30), channel_id=1, source_target_pairs={{0,1},{1,0},{2,3},{3,2},{4,5},{5,4},{6,7},{7,6},{8,9},{9,8},{10,11... | collective-permute-start | bytes 1277960 | tf_op jit(solution)/shard_map/ppermute | solution.py:233
  566.0 9.7 %collective-permute-start.5 = (bf16[208,1024]{1,0:T(8,128)(2,1)S(1)}, bf16[208,1024]{1,0:T(8,128)(2,1)S(1)}, u32[]{:S(2)}, u32[]{:S(2)}) collective-permute-start(bf16[208,1024]{1,0:T(8,128)(2,1)S(1)} %add_convert_fusion.5), channel_id=1, source_target_pairs={{0,2},{1,3},{2,0},{3,1},{4,6},{5,7},{6,4},{7,5},{8,10},{9,11},{10,... | collective-permute-start | bytes 1277960 | tf_op jit(solution)/shard_map/ppermute | solution.py:233
  575.9 8.2 %collective-permute-start.6 = (bf16[208,1024]{1,0:T(8,128)(2,1)S(1)}, bf16[208,1024]{1,0:T(8,128)(2,1)S(1)}, u32[]{:S(2)}, u32[]{:S(2)}) collective-permute-start(bf16[208,1024]{1,0:T(8,128)(2,1)S(1)} %add_convert_fusion.4), channel_id=1, source_target_pairs={{0,4},{1,5},{2,6},{3,7},{4,0},{5,1},{6,2},{7,3},{8,12},{9,13},{10,... | collective-permute-start | bytes 1277960 | tf_op jit(solution)/shard_map/ppermute | solution.py:233
  (11 other events, 18.0 us)
Sparse Core Ops, SparseCore 0:
  22.5 35.6 all-gather.6
  59.8 56.3 all-gather.8
  117.9 63.1 all-gather.10
  272.2 107.7 reduce-scatter.3
  382.3 41.6 reduce-scatter.7
  468.6 51.6 reduce-scatter.5

commit v19 on v18

--- a/solution.py
+++ b/solution.py
@@ -383,11 +383,11 @@
         w_rows,
     )
     n_head_blocks = width // HEAD_BLOCK
-    half_blocks = n_head_blocks // 2
+    half_blocks = 1
     back_flat = blended_value_gradient.reshape(rows, width)
     dq_parts = []
     kv_parts = []
-    for first in (0, half_blocks):
+    for first in range(0, n_head_blocks, half_blocks):
         dq_part, kv_back = attention_backward(
             meta, query_flat, kv_all, back_flat, head_dim, score_scale, first, half_blocks
         )

time: 600 us -> 601 us (level)
  Pallas kernels: 65.4 us -> 75 us
  waiting for transfers between devices: 261 us -> 253 us
  starting transfers between devices: 88 us -> 81.5 us
    all_to_all x2 -> x4, waiting for transfers between devices: 61 us -> 47.9 us  [body(): lax.all_to_all(kv_back.reshape(n_ctx, rows, kv_back.shape[1]), CTX, 0, 0,...]
    pallas_call x2 -> x4, Pallas kernels: 43 us -> 52.5 us  [attention_backward(): pl.pallas_call(functools.partial(attn_bwd_kernel, head_dim, scale), out_s...]
    ppermute x9, starting transfers between devices: 17.4 us -> 11 us  [ctx_allreduce(): other = lax.ppermute(total, CTX, [(j, j ^ step) for j in range(n_ctx)])]
    all_to_all x2 -> x4, starting transfers between devices: 50.7 us -> 51.2 us  [body(): lax.all_to_all(kv_back.reshape(n_ctx, rows, kv_back.shape[1]), CTX, 0, 0,...]
  transfers between devices with their start and end apart: 24 -> 26, of which waited for: 15 -> 18; matrix products, arithmetic and copies ran while one was open for 19% -> 20% of each run, Pallas kernels for 11% -> 13%
where the time goes in v19:
time: 601 us; the launch traced here: 592 us
  waiting for transfers between devices  253 us (42%)
  starting transfers between devices  81.5 us (14%)
  Pallas kernels  75 us (12%)
  local copies, waits for them, and re-layouts  69.7 us (12%)
  other arithmetic  53 us (9%)
  matrix products  44.2 us (7%)
  between operations  15.3 us (3%)
    all_to_all x1, waiting for transfers between devices, body(): lax.all_to_all(jnp.broadcast_to(kv_own[None], (n_ctx, rows, 2 * width)),...  92.6 us
    ppermute x9, waiting for transfers between devices, ctx_allreduce(): other = lax.ppermute(total, CTX, [(j, j ^ step) for j in range(n_ctx)])  53.4 us
    pallas_call x4, Pallas kernels, attention_backward(): pl.pallas_call(functools.partial(attn_bwd_kernel, head_dim, scale), out_s...  52.5 us
    all_to_all x4, starting transfers between devices, body(): lax.all_to_all(kv_back.reshape(n_ctx, rows, kv_back.shape[1]), CTX, 0, 0,...  51.2 us
    all_to_all x4, waiting for transfers between devices, body(): lax.all_to_all(kv_back.reshape(n_ctx, rows, kv_back.shape[1]), CTX, 0, 0,...  47.9 us
    ppermute x3, waiting for transfers between devices, z_exchange(): return zh_pair(pack, lax.ppermute(pack, ('zh', 'zl'), Z_CROSS))  34.3 us
    pallas_call x1, Pallas kernels, attention_forward(): pl.pallas_call(functools.partial(attn_fwd_kernel, head_dim, scale), out_s...  22.4 us
    ppermute x3, waiting for transfers between devices, z_combine(): got = lax.ppermute(theirs, ('zh', 'zl'), Z_CROSS)  21.9 us
  transfers between devices with their start and end apart: 26, of which 18 were waited for; matrix products, arithmetic and copies ran while one was open for 20% of the time, Pallas kernels for 13%

profile of v19, /device:TPU:0, one launch (start us, length us, event | category | flops | bytes accessed | tf_op | source)
XLA Modules:
  0.0 591.8 jit_solution(12717378184572715644)
XLA Ops:
  9.1 4.2 collective-permute-start.2
  13.3 7.0 %collective-permute-done.2 = bf16[144,1024]{1,0:T(8,128)(2,1)S(1)} collective-permute-done((bf16[144,1024]{1,0:T(8,128)(2,1)S(1)}, bf16[144,1024]{1,0:T(8,128)(2,1)S(1)}, u32[]{:S(2)}, u32[]{:S(2)}) %collective-permute-start.2) | collective-permute-done | bytes 294944 | tf_op jit(solution)/shard_map/ppermute | solution.py:199
  22.5 3.0 collective-permute-start
  26.0 14.8 %collective-permute-done = bf16[304,1024]{1,0:T(8,128)(2,1)S(1)} collective-permute-done((bf16[304,1024]{1,0:T(8,128)(2,1)S(1)}, bf16[304,1024]{1,0:T(8,128)(2,1)S(1)}, u32[]{:S(2)}, u32[]{:S(2)}) %collective-permute-start) | collective-permute-done | bytes 622624 | tf_op jit(solution)/shard_map/ppermute | solution.py:199
  42.0 12.5 %collective-permute-done.1 = bf16[64,5632]{1,0:T(8,128)(2,1)S(1)} collective-permute-done((bf16[64,5632]{1,0:T(8,128)(2,1)S(1)}, bf16[64,5632]{1,0:T(8,128)(2,1)S(1)}, u32[]{:S(2)}, u32[]{:S(2)}) %collective-permute-start.1) | collective-permute-done | bytes 720928 | tf_op jit(solution)/shard_map/ppermute | solution.py:199
  55.8 2.3 all-gather.7.cloned.1.call-done
  60.8 4.5 fusion.52
  65.2 4.5 copy.184
  69.8 2.5 convolution_bitcast_fusion.5
  73.5 1.8 fusion.13
  75.5 4.4 broadcast_in_dim.72
  79.8 5.4 all-to-all-start
  87.5 92.6 %all-to-all-done = bf16[8,256,2048]{2,1,0:T(8,128)(2,1)} async-done(((bf16[8,256,2048]{2,1,0:T(8,128)(2,1)}), bf16[8,256,2048]{2,1,0:T(8,128)(2,1)}, u32[]{:S(2)}, u32[]{:S(2)}) %all-to-all-start) | async-done | bytes 8388640 | tf_op jit(solution)/shard_map/all_to_all | solution.py:317
  180.1 4.1 fusion.51
  184.2 4.2 copy.187
  188.4 2.3 convolution_bitcast_fusion.3
  191.1 22.4 %shard_map.229 = bf16[256,1024]{1,0:T(8,128)(2,1)S(1)} custom-call(s32[2]{0:T(128)S(1)} %pad_add_fusion.meta_ref, bf16[256,1024]{1,0:T(8,128)(2,1)S(1)} %copy.189.q_ref, bf16[2048,2048]{1,0:T(8,128)(2,1)} %bitcast.24.k_ref.v_ref, bf16[2048,2048]{1,0:T(8,128)(2,1)} %bitcast.24.k_ref.v_ref), custom_call_target="tpu_custom_call" | custom-call | flops 2147483648 | bytes 9437184 | tf_op jit(solution)/shard_map/pallas_call | solution.py:80
  214.6 1.9 copy.191
  216.4 3.4 slice.116
  219.9 1.8 convolution_bitcast_fusion.1
  224.1 3.5 copy.198
  227.6 1.9 multiply_reduce_fusion.2
  231.3 2.0 copy.193
  233.4 1.9 copy.194
  235.3 6.4 %convolution_bitcast_fusion = f32[1,256,5632]{2,1,0:T(8,128)S(1)} fusion(bf16[256,1024]{0,1:T(8,128)(2,1)} %bitcast.251, bf16[1024,5632]{1,0:T(8,128)(2,1)} %bitcast.244), kind=kOutput, calls=%fused_computation.4 | convolution fusion | flops 2952790016 | bytes 17825792 | tf_op jit(solution)/shard_map/dot_general | solution.py:334
  241.7 3.1 multiply_convert_fusion.1
  244.8 3.2 fusion.6
  249.1 2.5 copy.201
  251.6 2.0 multiply_reduce_fusion
  255.7 5.9 %convolution_convert_fusion = bf16[8,128,5632]{2,1,0:T(8,128)(2,1)} fusion(bf16[8,128,256]{2,1,0:T(8,128)(2,1)S(1)} %bitcast.252, bf16[1,256,2816]{2,1,0:T(8,128)(2,1)S(1)} %copy-done.21, bf16[1,256,2816]{2,1,0:T(8,128)(2,1)S(1)} %copy-done.19), kind=kOutput, calls=%fused_computation.3 | convolution fusion | flops 2964324352 | bytes 14942208 | tf_op jit(solution)/shard_map/srd,srf->df/dot_general | solution.py:352
  262.4 11.2 %pad_maximum_fusion = bf16[8,128,6656]{2,1,0:T(8,128)(2,1)} fusion(bf16[8,128,1024]{2,1,0:T(8,128)(2,1)S(1)} %convolution_convert_fusion.2, bf16[8,128,5632]{2,1,0:T(8,128)(2,1)} %convolution_convert_fusion), kind=kLoop, calls=%fused_computation.1 | loop fusion | flops 27262976 | bytes 27262976 | tf_op jit(solution)/shard_map/concatenate | solution.py:370
  273.6 2.8 convolution_convert_fusion.6
  277.9 13.0 %shard_map.233 = (f32[256,256]{1,0:T(8,128)S(1)}, bf16[2048,512]{1,0:T(8,128)(2,1)}) custom-call(s32[2]{0:T(128)S(1)} %pad_add_fusion.meta_ref, bf16[256,1024]{1,0:T(8,128)(2,1)S(1)} %copy.189.q_ref, bf16[2048,2048]{1,0:T(8,128)(2,1)} %bitcast.24.k_ref.v_ref, bf16[2048,2048]{1,0:T(8,128)(2,1)} %bitcast.24.k_ref.v_ref, bf16[256,1024]{1,0:T(8,128)(2,1)S(1)} %copy.205.do_ref), custom_call_target="tpu_custom_call" | custom-call | flops 1342177280 | bytes 4849664 | tf_op jit(solution)/shard_map/pallas_call | solution.py:109
  290.9 35.5 %all-to-all-start.4 = ((bf16[8,256,512]{2,1,0:T(8,128)(2,1)}), bf16[8,256,512]{2,1,0:T(8,128)(2,1)}, u32[]{:S(2)}, u32[]{:S(2)}) async-start(bf16[8,256,512]{2,1,0:T(8,128)(2,1)} %bitcast.75), calls=%async_computation.4 | async-start | bytes 4194304 | tf_op jit(solution)/shard_map/all_to_all | solution.py:397
  326.5 2.7 copy.195
  330.8 4.2 convolution_convert_fusion.1
  335.0 13.0 %shard_map.232 = (f32[256,256]{1,0:T(8,128)S(1)}, bf16[2048,512]{1,0:T(8,128)(2,1)}) custom-call(s32[2]{0:T(128)S(1)} %pad_add_fusion.meta_ref, bf16[256,1024]{1,0:T(8,128)(2,1)S(1)} %copy.189.q_ref, bf16[2048,2048]{1,0:T(8,128)(2,1)} %bitcast.24.k_ref.v_ref, bf16[2048,2048]{1,0:T(8,128)(2,1)} %bitcast.24.k_ref.v_ref, bf16[256,1024]{1,0:T(8,128)(2,1)S(1)} %copy.205.do_ref), custom_call_target="tpu_custom_call" | custom-call | flops 1342177280 | bytes 4849664 | tf_op jit(solution)/shard_map/pallas_call | solution.py:109
  348.1 4.7 all-to-all-done.4
  352.7 4.6 all-to-all-start.3
  357.3 13.1 %shard_map.231 = (f32[256,256]{1,0:T(8,128)S(1)}, bf16[2048,512]{1,0:T(8,128)(2,1)}) custom-call(s32[2]{0:T(128)S(1)} %pad_add_fusion.meta_ref, bf16[256,1024]{1,0:T(8,128)(2,1)S(1)} %copy.189.q_ref, bf16[2048,2048]{1,0:T(8,128)(2,1)} %bitcast.24.k_ref.v_ref, bf16[2048,2048]{1,0:T(8,128)(2,1)} %bitcast.24.k_ref.v_ref, bf16[256,1024]{1,0:T(8,128)(2,1)S(1)} %copy.205.do_ref), custom_call_target="tpu_custom_call" | custom-call | flops 1342177280 | bytes 4849664 | tf_op jit(solution)/shard_map/pallas_call | solution.py:109
  370.4 14.0 %all-to-all-done.3 = bf16[8,256,512]{2,1,0:T(8,128)(2,1)} async-done(((bf16[8,256,512]{2,1,0:T(8,128)(2,1)}), bf16[8,256,512]{2,1,0:T(8,128)(2,1)}, u32[]{:S(2)}, u32[]{:S(2)}) %all-to-all-start.3) | async-done | bytes 2097184 | tf_op jit(solution)/shard_map/all_to_all | solution.py:397
  384.4 6.7 %all-to-all-start.2 = ((bf16[8,256,512]{2,1,0:T(8,128)(2,1)}), bf16[8,256,512]{2,1,0:T(8,128)(2,1)}, u32[]{:S(2)}, u32[]{:S(2)}) async-start(bf16[8,256,512]{2,1,0:T(8,128)(2,1)} %bitcast.71), calls=%async_computation.2 | async-start | bytes 4194304 | tf_op jit(solution)/shard_map/all_to_all | solution.py:397
  391.1 13.4 %shard_map.230 = (f32[256,256]{1,0:T(8,128)S(1)}, bf16[2048,512]{1,0:T(8,128)(2,1)}) custom-call(s32[2]{0:T(128)S(1)} %pad_add_fusion.meta_ref, bf16[256,1024]{1,0:T(8,128)(2,1)S(1)} %copy.189.q_ref, bf16[2048,2048]{1,0:T(8,128)(2,1)} %bitcast.24.k_ref.v_ref, bf16[2048,2048]{1,0:T(8,128)(2,1)} %bitcast.24.k_ref.v_ref, bf16[256,1024]{1,0:T(8,128)(2,1)S(1)} %copy.205.do_ref), custom_call_target="tpu_custom_call" | custom-call | flops 1342177280 | bytes 4849664 | tf_op jit(solution)/shard_map/pallas_call | solution.py:109
  404.5 12.5 %all-to-all-done.2 = bf16[8,256,512]{2,1,0:T(8,128)(2,1)} async-done(((bf16[8,256,512]{2,1,0:T(8,128)(2,1)}), bf16[8,256,512]{2,1,0:T(8,128)(2,1)}, u32[]{:S(2)}, u32[]{:S(2)}) %all-to-all-start.2) | async-done | bytes 2097184 | tf_op jit(solution)/shard_map/all_to_all | solution.py:397
  416.9 4.4 all-to-all-start.1
  424.3 2.0 convert_reduce_fusion
  426.5 1.9 convert_reduce_fusion.1
  428.7 1.9 convert_reduce_fusion.2
  431.6 16.8 %all-to-all-done.1 = bf16[8,256,512]{2,1,0:T(8,128)(2,1)} async-done(((bf16[8,256,512]{2,1,0:T(8,128)(2,1)}), bf16[8,256,512]{2,1,0:T(8,128)(2,1)}, u32[]{:S(2)}, u32[]{:S(2)}) %all-to-all-start.1) | async-done | bytes 2097184 | tf_op jit(solution)/shard_map/all_to_all | solution.py:397
  448.4 1.9 convert_reduce_fusion.3
  466.9 3.2 fusion.1
  471.4 2.8 collective-permute-start.7
  475.9 18.8 %collective-permute-done.7 = bf16[64,6656]{1,0:T(8,128)(2,1)} collective-permute-done((bf16[64,6656]{1,0:T(8,128)(2,1)S(1)}, bf16[64,6656]{1,0:T(8,128)(2,1)}, u32[]{:S(2)}, u32[]{:S(2)}) %collective-permute-start.7) | collective-permute-done | bytes 852000 | tf_op jit(solution)/shard_map/ppermute | solution.py:225
  497.9 3.1 collective-permute-done.11
  502.0 20.5 %collective-permute-done.12 = bf16[176,1024]{1,0:T(8,128)(2,1)S(1)} collective-permute-done((bf16[176,1024]{1,0:T(8,128)(2,1)S(1)}, bf16[176,1024]{1,0:T(8,128)(2,1)S(1)}, u32[]{:S(2)}, u32[]{:S(2)}) %collective-permute-start.12) | collective-permute-done | bytes 360480 | tf_op jit(solution)/shard_map/ppermute | solution.py:233
  522.6 4.9 collective-permute-start.13
  528.8 5.2 fusion.14
  540.0 2.6 collective-permute-start.3
  542.6 8.6 %collective-permute-done.9 = bf16[64,6656]{1,0:T(8,128)(2,1)} collective-permute-done((bf16[64,6656]{1,0:T(8,128)(2,1)}, bf16[64,6656]{1,0:T(8,128)(2,1)}, u32[]{:S(2)}, u32[]{:S(2)}) %collective-permute-start.9) | collective-permute-done | bytes 852000 | tf_op jit(solution)/shard_map/ppermute | solution.py:233
  555.5 9.1 %collective-permute-done.4 = bf16[208,1024]{1,0:T(8,128)(2,1)S(1)} collective-permute-done((bf16[208,1024]{1,0:T(8,128)(2,1)S(1)}, bf16[208,1024]{1,0:T(8,128)(2,1)S(1)}, u32[]{:S(2)}, u32[]{:S(2)}) %collective-permute-start.4) | collective-permute-done | bytes 426016 | tf_op jit(solution)/shard_map/ppermute | solution.py:233
  564.9 5.9 collective-permute-done.10
  571.7 2.8 collective-permute-done.5
  574.6 2.4 collective-permute-start.6
  578.2 4.9 collective-permute-done.6
  (214 shorter events, 69.3 us)
Async XLA Ops:
  7.2 15.2 %copy-start.35 = (bf16[64,1024]{1,0:T(8,128)(2,1)S(1)}, bf16[64,1024]{1,0:T(8,128)(2,1)}, u32[]{:S(2)}) copy-start(bf16[64,1024]{1,0:T(8,128)(2,1)} %param.16) | copy-start | bytes 393220
  7.2 15.2 %copy-start.36 = (bf16[64,1024]{1,0:T(8,128)(2,1)S(1)}, bf16[64,1024]{1,0:T(8,128)(2,1)}, u32[]{:S(2)}) copy-start(bf16[64,1024]{1,0:T(8,128)(2,1)} %param.19) | copy-start | bytes 393220
  7.2 15.2 %copy-start.32 = (bf16[176,1024]{1,0:T(8,128)(2,1)S(1)}, bf16[176,1024]{1,0:T(8,128)(2,1)}, u32[]{:S(2)}) copy-start(bf16[176,1024]{1,0:T(8,128)(2,1)} %param.22) | copy-start | bytes 1081348
  7.2 50.9 %all-gather.7.cloned.1.call-start = ((), (), s32[]{:S(2)}) async-start(), calls=%async_computation.11 | async-start | bytes 5308416 | tf_op jit(solution)/shard_map/all_gather | solution.py:203
  9.1 16.4 %copy-start.33 = (bf16[64,2816]{1,0:T(8,128)(2,1)S(1)}, bf16[64,2816]{1,0:T(8,128)(2,1)}, u32[]{:S(2)}) copy-start(bf16[64,2816]{1,0:T(8,128)(2,1)} %param.20) | copy-start | bytes 1081348
  9.1 11.2 %collective-permute-start.2 = (bf16[144,1024]{1,0:T(8,128)(2,1)S(1)}, bf16[144,1024]{1,0:T(8,128)(2,1)S(1)}, u32[]{:S(2)}, u32[]{:S(2)}) collective-permute-start(bf16[144,1024]{1,0:T(8,128)(2,1)S(1)} %fusion.38), channel_id=1, source_target_pairs={{0,68},{68,0},{4,64},{64,4},{1,69},{69,1},{5,65},{65,5},{2,70},{70... | collective-permute-start | bytes 884744 | tf_op jit(solution)/shard_map/ppermute | solution.py:199
  21.4 4.1 copy-start.34
  22.3 157.7 %all-gather.9.cloned.1.call-start = ((), (), s32[]{:S(2)}) async-start(), calls=%async_computation.12 | async-start | bytes 11206656 | tf_op jit(solution)/shard_map/all_gather | solution.py:203
  22.5 18.3 %collective-permute-start = (bf16[304,1024]{1,0:T(8,128)(2,1)S(1)}, bf16[304,1024]{1,0:T(8,128)(2,1)S(1)}, u32[]{:S(2)}, u32[]{:S(2)}) collective-permute-start(bf16[304,1024]{1,0:T(8,128)(2,1)S(1)} %constant_dynamic-update-slice_fusion), channel_id=1, source_target_pairs={{0,68},{68,0},{4,64},{64,4},{1,69},{69,1},{5,65},{65,5},{2,70},{70... | collective-permute-start | bytes 1867784 | tf_op jit(solution)/shard_map/ppermute | solution.py:199
  25.6 28.9 %collective-permute-start.1 = (bf16[64,5632]{1,0:T(8,128)(2,1)S(1)}, bf16[64,5632]{1,0:T(8,128)(2,1)S(1)}, u32[]{:S(2)}, u32[]{:S(2)}) collective-permute-start(bf16[64,5632]{1,0:T(8,128)(2,1)S(1)} %constant_dynamic-update-slice_fusion.3), channel_id=1, source_target_pairs={{0,68},{68,0},{4,64},{64,4},{1,69},{69,1},{5,65},{65,5},{2,70},{70... | collective-permute-start | bytes 2162696 | tf_op jit(solution)/shard_map/ppermute | solution.py:199
  54.5 4.4 copy-start.9
  58.1 177.1 %all-gather.11.cloned.1.call-start = ((), (), s32[]{:S(2)}) async-start(), calls=%async_computation.13 | async-start | bytes 12976128 | tf_op jit(solution)/shard_map/all_gather | solution.py:203
  60.8 127.6 %copy-start.11 = (bf16[1,256,8,2,64]{1,4,3,2,0:T(8,128)(2,1)}, bf16[1,256,8,2,64]{1,4,3,2,0:T(8,128)(2,1)S(1)}, u32[]{:S(2)}) copy-start(bf16[1,256,8,2,64]{1,4,3,2,0:T(8,128)(2,1)S(1)} %copy.182) | copy-start | bytes 1572868
  65.2 8.3 %copy-start = (bf16[16,64,1024]{2,1,0:T(8,128)(2,1)}, bf16[16,64,1024]{2,1,0:T(8,128)(2,1)S(1)}, u32[]{:S(2)}) copy-start(bf16[16,64,1024]{2,1,0:T(8,128)(2,1)S(1)} %get-tuple-element.54) | copy-start | bytes 6291460
  73.5 1.9 copy-start.29
  79.8 5.4 copy-start.37
  79.8 5.4 copy-start.38
  79.8 100.2 %all-to-all-start = ((bf16[8,256,2048]{2,1,0:T(8,128)(2,1)}), bf16[8,256,2048]{2,1,0:T(8,128)(2,1)}, u32[]{:S(2)}, u32[]{:S(2)}) async-start(bf16[8,256,2048]{2,1,0:T(8,128)(2,1)} %broadcast_in_dim.72), calls=%async_computation | async-start | bytes 16777216 | tf_op jit(solution)/shard_map/all_to_all | solution.py:317
  85.2 385.0 %reduce-scatter.4.cloned.1.call-start = ((), (), s32[]{:S(2)}) async-start(), calls=%async_computation.8 | async-start | bytes 15335424 | tf_op jit(solution)/shard_map/reduce_scatter | solution.py:215
  216.4 3.4 copy-start.27
  219.8 2.5 copy-start.22
  224.1 3.5 copy-start.10
  235.3 6.4 %copy-start.13 = (f32[1,256,2816]{2,1,0:T(8,128)S(1)}, f32[1,256,2816]{2,1,0:T(8,128)}, u32[]{:S(2)}) copy-start(f32[1,256,2816]{2,1,0:T(8,128)} %copy.198) | copy-start | bytes 8650756
  235.3 9.6 %slice-start = ((s8[11534336]{0:T(1024)(128)(4,1)}), s8[4194304]{0:T(1024)(128)(4,1)S(1)}, s32[]{:S(2)}) async-start(s8[11534336]{0:T(1024)(128)(4,1)} %bitcast.245), calls=%async_computation.14 | async-start | bytes 8388608
  235.3 9.6 %slice-start.1 = ((s8[11534336]{0:T(1024)(128)(4,1)}), s8[4194304]{0:T(1024)(128)(4,1)S(1)}, s32[]{:S(2)}) async-start(s8[11534336]{0:T(1024)(128)(4,1)} %bitcast.245), calls=%async_computation.15 | async-start | bytes 8388608
  241.7 3.2 slice-start.2
  244.8 3.2 copy-start.18
  244.8 3.2 copy-start.20
  251.6 2.0 copy-start.7
  251.6 2.2 copy-start.14
  253.6 1.8 copy-start.17
  253.6 1.8 copy-start.19
  253.6 2.1 copy-start.21
  255.4 6.3 %copy-start.4 = (f32[1,256,1024]{2,1,0:T(8,128)}, f32[1,256,1024]{2,1,0:T(8,128)S(1)}, u32[]{:S(2)}) copy-start(f32[1,256,1024]{2,1,0:T(8,128)S(1)} %subtract_add_fusion) | copy-start | bytes 3145732
  255.7 5.9 %copy-start.23 = (bf16[1,256,8,2,64]{1,4,3,2,0:T(8,128)(2,1)S(1)}, bf16[1,256,8,2,64]{1,4,3,2,0:T(8,128)(2,1)}, u32[]{:S(2)}) copy-start(bf16[1,256,8,2,64]{1,4,3,2,0:T(8,128)(2,1)} %copy.191) | copy-start | bytes 1572868
  290.9 61.8 %all-to-all-start.4 = ((bf16[8,256,512]{2,1,0:T(8,128)(2,1)}), bf16[8,256,512]{2,1,0:T(8,128)(2,1)}, u32[]{:S(2)}, u32[]{:S(2)}) async-start(bf16[8,256,512]{2,1,0:T(8,128)(2,1)} %bitcast.75), calls=%async_computation.4 | async-start | bytes 4194304 | tf_op jit(solution)/shard_map/all_to_all | solution.py:397
  326.5 147.8 %reduce-scatter.8.cloned.1.call-start = ((), (), s32[]{:S(2)}) async-start(), calls=%async_computation.10 | async-start | bytes 6488064 | tf_op jit(solution)/shard_map/reduce_scatter | solution.py:215
  330.8 4.2 copy-start.15
  352.7 31.6 %all-to-all-start.3 = ((bf16[8,256,512]{2,1,0:T(8,128)(2,1)}), bf16[8,256,512]{2,1,0:T(8,128)(2,1)}, u32[]{:S(2)}, u32[]{:S(2)}) async-start(bf16[8,256,512]{2,1,0:T(8,128)(2,1)} %bitcast.73), calls=%async_computation.3 | async-start | bytes 4194304 | tf_op jit(solution)/shard_map/all_to_all | solution.py:397
  384.4 32.6 %all-to-all-start.2 = ((bf16[8,256,512]{2,1,0:T(8,128)(2,1)}), bf16[8,256,512]{2,1,0:T(8,128)(2,1)}, u32[]{:S(2)}, u32[]{:S(2)}) async-start(bf16[8,256,512]{2,1,0:T(8,128)(2,1)} %bitcast.71), calls=%async_computation.2 | async-start | bytes 4194304 | tf_op jit(solution)/shard_map/all_to_all | solution.py:397
  416.9 31.5 %all-to-all-start.1 = ((bf16[8,256,512]{2,1,0:T(8,128)(2,1)}), bf16[8,256,512]{2,1,0:T(8,128)(2,1)}, u32[]{:S(2)}, u32[]{:S(2)}) async-start(bf16[8,256,512]{2,1,0:T(8,128)(2,1)} %bitcast.69), calls=%async_computation.1 | async-start | bytes 4194304 | tf_op jit(solution)/shard_map/all_to_all | solution.py:397
  421.3 117.5 %reduce-scatter.6.cloned.1.call-start = ((), (), s32[]{:S(2)}) async-start(), calls=%async_computation.9 | async-start | bytes 7667712 | tf_op jit(solution)/shard_map/reduce_scatter | solution.py:215
  453.8 1.8 copy-start.3
  454.3 2.9 copy-start.24
  454.3 2.1 copy-start.2
  462.4 2.2 copy-start.12
  471.4 23.3 %collective-permute-start.7 = (bf16[64,6656]{1,0:T(8,128)(2,1)S(1)}, bf16[64,6656]{1,0:T(8,128)(2,1)}, u32[]{:S(2)}, u32[]{:S(2)}) collective-permute-start(bf16[64,6656]{1,0:T(8,128)(2,1)S(1)} %dynamic-slice_bitcast_fusion), channel_id=1, source_target_pairs={{0,68},{68,0},{4,64},{64,4},{1,69},{69,1},{5,65},{65,5},{2,70},{70... | collective-permute-start | bytes 2555912 | tf_op jit(solution)/shard_map/ppermute | solution.py:225
  474.2 26.8 %copy-start.31 = (bf16[1,352,1024]{2,1,0:T(8,128)(2,1)S(1)}, bf16[1,352,1024]{2,1,0:T(8,128)(2,1)}, u32[]{:S(2)}) copy-start(bf16[1,352,1024]{2,1,0:T(8,128)(2,1)} %reduce-scatter.8.cloned.1.call-done) | copy-start | bytes 2162692
  475.3 25.7 %collective-permute-start.11 = (bf16[176,1024]{1,0:T(8,128)(2,1)S(1)}, bf16[176,1024]{1,0:T(8,128)(2,1)S(1)}, u32[]{:S(2)}, u32[]{:S(2)}) collective-permute-start(bf16[176,1024]{1,0:T(8,128)(2,1)S(1)} %dynamic-slice_bitcast_fusion.2), channel_id=1, source_target_pairs={{0,68},{68,0},{4,64},{64,4},{1,69},{69,1},{5,65},{65,5},{2,70},{70... | collective-permute-start | bytes 1081352 | tf_op jit(solution)/shard_map/ppermute | solution.py:225
  496.3 32.5 %copy-start.8 = (f32[1,256,1024]{2,1,0:T(8,128)S(1)}, f32[1,256,1024]{2,1,0:T(8,128)}, u32[]{:S(2)}) copy-start(f32[1,256,1024]{2,1,0:T(8,128)} %copy-done.6) | copy-start | bytes 3145732
  496.4 32.5 %copy-start.16 = (bf16[1,256,8,2,176]{1,4,3,2,0:T(8,128)(2,1)S(1)}, bf16[1,256,8,2,176]{1,4,3,2,0:T(8,128)(2,1)}, u32[]{:S(2)}) copy-start(bf16[1,256,8,2,176]{1,4,3,2,0:T(8,128)(2,1)} %copy-done.15) | copy-start | bytes 4325380
  496.4 31.1 %collective-permute-start.8 = (bf16[64,6656]{1,0:T(8,128)(2,1)S(1)}, bf16[64,6656]{1,0:T(8,128)(2,1)S(1)}, u32[]{:S(2)}, u32[]{:S(2)}) collective-permute-start(bf16[64,6656]{1,0:T(8,128)(2,1)S(1)} %fusion.5), channel_id=1, source_target_pairs={{0,1},{1,0},{2,3},{3,2},{4,5},{5,4},{6,7},{7,6},{8,9},{9,8},{10,11... | collective-permute-start | bytes 2555912 | tf_op jit(solution)/shard_map/ppermute | solution.py:233
  501.1 21.4 %collective-permute-start.12 = (bf16[176,1024]{1,0:T(8,128)(2,1)S(1)}, bf16[176,1024]{1,0:T(8,128)(2,1)S(1)}, u32[]{:S(2)}, u32[]{:S(2)}) collective-permute-start(bf16[176,1024]{1,0:T(8,128)(2,1)S(1)} %fusion.29), channel_id=1, source_target_pairs={{0,1},{1,0},{2,3},{3,2},{4,5},{5,4},{6,7},{7,6},{8,9},{9,8},{10,11... | collective-permute-start | bytes 1081352 | tf_op jit(solution)/shard_map/ppermute | solution.py:233
  522.6 14.3 %collective-permute-start.13 = (bf16[176,1024]{1,0:T(8,128)(2,1)S(1)}, bf16[176,1024]{1,0:T(8,128)(2,1)}, u32[]{:S(2)}, u32[]{:S(2)}) collective-permute-start(bf16[176,1024]{1,0:T(8,128)(2,1)S(1)} %add_convert_fusion.8), channel_id=1, source_target_pairs={{0,2},{1,3},{2,0},{3,1},{4,6},{5,7},{6,4},{7,5},{8,10},{9,11},{10,... | collective-permute-start | bytes 1081352 | tf_op jit(solution)/shard_map/ppermute | solution.py:233
  528.6 22.6 %collective-permute-start.9 = (bf16[64,6656]{1,0:T(8,128)(2,1)}, bf16[64,6656]{1,0:T(8,128)(2,1)}, u32[]{:S(2)}, u32[]{:S(2)}) collective-permute-start(bf16[64,6656]{1,0:T(8,128)(2,1)} %add_convert_fusion.2), channel_id=1, source_target_pairs={{0,2},{1,3},{2,0},{3,1},{4,6},{5,7},{6,4},{7,5},{8,10},{9,11},{10,... | collective-permute-start | bytes 2555912 | tf_op jit(solution)/shard_map/ppermute | solution.py:233
  528.8 5.2 copy-start.26
  538.0 16.5 %collective-permute-start.14 = (bf16[176,1024]{1,0:T(8,128)(2,1)S(1)}, bf16[176,1024]{1,0:T(8,128)(2,1)S(1)}, u32[]{:S(2)}, u32[]{:S(2)}) collective-permute-start(bf16[176,1024]{1,0:T(8,128)(2,1)S(1)} %add_convert_fusion.7), channel_id=1, source_target_pairs={{0,4},{1,5},{2,6},{3,7},{4,0},{5,1},{6,2},{7,3},{8,12},{9,13},{10,... | collective-permute-start | bytes 1081352 | tf_op jit(solution)/shard_map/ppermute | solution.py:233
  538.9 14.1 %copy-start.30 = (bf16[1,416,1024]{2,1,0:T(8,128)(2,1)S(1)}, bf16[1,416,1024]{2,1,0:T(8,128)(2,1)}, u32[]{:S(2)}) copy-start(bf16[1,416,1024]{2,1,0:T(8,128)(2,1)} %reduce-scatter.6.cloned.1.call-done) | copy-start | bytes 2555908
  540.0 13.2 %copy-start.5 = (f32[1,256,1024]{2,1,0:T(8,128)S(1)}, f32[1,256,1024]{2,1,0:T(8,128)}, u32[]{:S(2)}) copy-start(f32[1,256,1024]{2,1,0:T(8,128)} %copy-done.4) | copy-start | bytes 3145732
  540.0 12.9 %collective-permute-start.3 = (bf16[208,1024]{1,0:T(8,128)(2,1)S(1)}, bf16[208,1024]{1,0:T(8,128)(2,1)S(1)}, u32[]{:S(2)}, u32[]{:S(2)}) collective-permute-start(bf16[208,1024]{1,0:T(8,128)(2,1)S(1)} %dynamic-slice_bitcast_fusion.1), channel_id=1, source_target_pairs={{0,68},{68,0},{4,64},{64,4},{1,69},{69,1},{5,65},{65,5},{2,70},{70... | collective-permute-start | bytes 1277960 | tf_op jit(solution)/shard_map/ppermute | solution.py:225
  552.8 17.9 %collective-permute-start.10 = (bf16[64,6656]{1,0:T(8,128)(2,1)S(1)}, bf16[64,6656]{1,0:T(8,128)(2,1)S(1)}, u32[]{:S(2)}, u32[]{:S(2)}) collective-permute-start(bf16[64,6656]{1,0:T(8,128)(2,1)S(1)} %add_convert_fusion.1), channel_id=1, source_target_pairs={{0,4},{1,5},{2,6},{3,7},{4,0},{5,1},{6,2},{7,3},{8,12},{9,13},{10,... | collective-permute-start | bytes 2555912 | tf_op jit(solution)/shard_map/ppermute | solution.py:233
  553.1 11.5 %collective-permute-start.4 = (bf16[208,1024]{1,0:T(8,128)(2,1)S(1)}, bf16[208,1024]{1,0:T(8,128)(2,1)S(1)}, u32[]{:S(2)}, u32[]{:S(2)}) collective-permute-start(bf16[208,1024]{1,0:T(8,128)(2,1)S(1)} %fusion.28), channel_id=1, source_target_pairs={{0,1},{1,0},{2,3},{3,2},{4,5},{5,4},{6,7},{7,6},{8,9},{9,8},{10,11... | collective-permute-start | bytes 1277960 | tf_op jit(solution)/shard_map/ppermute | solution.py:233
  564.8 9.7 %collective-permute-start.5 = (bf16[208,1024]{1,0:T(8,128)(2,1)S(1)}, bf16[208,1024]{1,0:T(8,128)(2,1)S(1)}, u32[]{:S(2)}, u32[]{:S(2)}) collective-permute-start(bf16[208,1024]{1,0:T(8,128)(2,1)S(1)} %add_convert_fusion.5), channel_id=1, source_target_pairs={{0,2},{1,3},{2,0},{3,1},{4,6},{5,7},{6,4},{7,5},{8,10},{9,11},{10,... | collective-permute-start | bytes 1277960 | tf_op jit(solution)/shard_map/ppermute | solution.py:233
  574.6 8.5 %collective-permute-start.6 = (bf16[208,1024]{1,0:T(8,128)(2,1)S(1)}, bf16[208,1024]{1,0:T(8,128)(2,1)S(1)}, u32[]{:S(2)}, u32[]{:S(2)}) collective-permute-start(bf16[208,1024]{1,0:T(8,128)(2,1)S(1)} %add_convert_fusion.4), channel_id=1, source_target_pairs={{0,4},{1,5},{2,6},{3,7},{4,0},{5,1},{6,2},{7,3},{8,12},{9,13},{10,... | collective-permute-start | bytes 1277960 | tf_op jit(solution)/shard_map/ppermute | solution.py:233
  (4 other events, 5.1 us)
Sparse Core Ops, SparseCore 0:
  22.5 35.6 all-gather.6
  59.8 56.3 all-gather.8
  117.8 63.1 all-gather.10
  273.7 107.7 reduce-scatter.3
  383.8 41.4 reduce-scatter.7
  470.3 46.4 reduce-scatter.5

commit v20 on v18

--- a/solution.py
+++ b/solution.py
@@ -313,17 +313,32 @@
     )
     value_mix = (0.5 * own_value + 0.5 * first_wide).astype(jnp.bfloat16)
 
-    kv_own = jnp.concatenate([key_rot, value_mix], axis=-1).reshape(rows, 2 * width)
-    kv_all = lax.all_to_all(
-        jnp.broadcast_to(kv_own[None], (n_ctx, rows, 2 * width)), CTX, 0, 0, tiled=False
-    ).reshape(total_len, 2 * width)
-    query_in, kv_all = lax.optimization_barrier((normed_low_g, kv_all))
+    half_width = width // 2
+    key_rot = key_rot.reshape(rows, width)
+    value_mix = value_mix.reshape(rows, width)
+    kv_halves = []
+    for part in range(2):
+        cols = slice(part * half_width, (part + 1) * half_width)
+        kv_own = jnp.concatenate([key_rot[:, cols], value_mix[:, cols]], axis=-1)
+        kv_halves.append(
+            lax.all_to_all(
+                jnp.broadcast_to(kv_own[None], (n_ctx, rows, width)), CTX, 0, 0, tiled=False
+            ).reshape(total_len, width)
+        )
+    query_in, kv_halves[0] = lax.optimization_barrier((normed_low_g, kv_halves[0]))
     query = jnp.dot(query_in, query_mat, preferred_element_type=jnp.float32)
     query_rotated_rows = rotate(query.reshape(heads_shape), cos_rows, sin_rows).astype(jnp.bfloat16)
     meta = jnp.stack([lax.axis_index(CTX) * rows, slot_lengths[0]]).astype(jnp.int32)
     query_flat = query_rotated_rows.reshape(rows, width)
-    mixed_low = attention_forward(
-        meta, query_flat, kv_all, head_dim, score_scale
+    query_halves = [query_flat[:, :half_width], query_flat[:, half_width:]]
+    mixed_first = attention_forward(meta, query_halves[0], kv_halves[0], head_dim, score_scale)
+    mixed_first, kv_halves[1] = lax.optimization_barrier((mixed_first, kv_halves[1]))
+    mixed_low = jnp.concatenate(
+        [
+            mixed_first,
+            attention_forward(meta, query_halves[1], kv_halves[1], head_dim, score_scale),
+        ],
+        axis=-1,
     ).reshape(slots, rows, width)
 
     mixed_low_g = to_gathered(mixed_low, w_rows)
@@ -385,11 +400,19 @@
     n_head_blocks = width // HEAD_BLOCK
     half_blocks = n_head_blocks // 2
     back_flat = blended_value_gradient.reshape(rows, width)
+    back_halves = [back_flat[:, :half_width], back_flat[:, half_width:]]
     dq_parts = []
     kv_parts = []
-    for first in (0, half_blocks):
+    for part in range(2):
         dq_part, kv_back = attention_backward(
-            meta, query_flat, kv_all, back_flat, head_dim, score_scale, first, half_blocks
+            meta,
+            query_halves[part],
+            kv_halves[part],
+            back_halves[part],
+            head_dim,
+            score_scale,
+            0,
+            half_blocks,
         )
         dq_parts.append(dq_part)
         kv_parts.append(

time: 600 us -> 576 us (0.960)
  waiting for transfers between devices: 261 us -> 236 us
  starting transfers between devices: 88 us -> 70.4 us
  local copies, waits for them, and re-layouts: 67.4 us -> 79.3 us
    all_to_all x2, starting transfers between devices: 50.7 us -> 24.9 us  [body(): lax.all_to_all(kv_back.reshape(n_ctx, rows, kv_back.shape[1]), CTX, 0, 0,...]
    all_to_all x1 -> x2, waiting for transfers between devices: 92.6 us -> 70.9 us  [body(): lax.all_to_all(jnp.broadcast_to(kv_own[None], (n_ctx, rows, width)), CTX,...]
    all_to_all x1 -> x2, starting transfers between devices: 5.31 us -> 23 us  [body(): lax.all_to_all(jnp.broadcast_to(kv_own[None], (n_ctx, rows, width)), CTX,...]
    ppermute x9, starting transfers between devices: 17.4 us -> 8.16 us  [ctx_allreduce(): other = lax.ppermute(total, CTX, [(j, j ^ step) for j in range(n_ctx)])]
    all_to_all x2, waiting for transfers between devices: 61 us -> 53.8 us  [body(): lax.all_to_all(kv_back.reshape(n_ctx, rows, kv_back.shape[1]), CTX, 0, 0,...]
    unnamed x106 -> x96, local copies, waits for them, and re-layouts: 9.29 us -> 13.7 us
    pallas_call x1 -> x2, Pallas kernels: 22.4 us -> 25 us  [attention_forward(): pl.pallas_call(functools.partial(attn_fwd_kernel, head_dim, scale), out_s...]
  transfers between devices with their start and end apart: 24 -> 25, of which waited for: 15 -> 17; matrix products, arithmetic and copies ran while one was open for 19% -> 22% of each run, Pallas kernels for 11% -> 12%
where the time goes in v20:
time: 576 us; the launch traced here: 567 us
  waiting for transfers between devices  236 us (41%)
  local copies, waits for them, and re-layouts  79.3 us (14%)
  starting transfers between devices  70.4 us (12%)
  Pallas kernels  67.5 us (12%)
  other arithmetic  54 us (9%)
  matrix products  44.4 us (8%)
  between operations  15.3 us (3%)
    all_to_all x2, waiting for transfers between devices, body(): lax.all_to_all(jnp.broadcast_to(kv_own[None], (n_ctx, rows, width)), CTX,...  70.9 us
    all_to_all x2, waiting for transfers between devices, body(): lax.all_to_all(kv_back.reshape(n_ctx, rows, kv_back.shape[1]), CTX, 0, 0,...  53.8 us
    ppermute x9, waiting for transfers between devices, ctx_allreduce(): other = lax.ppermute(total, CTX, [(j, j ^ step) for j in range(n_ctx)])  51.1 us
    pallas_call x2, Pallas kernels, attention_backward(): pl.pallas_call(functools.partial(attn_bwd_kernel, head_dim, scale), out_s...  42.5 us
    ppermute x3, waiting for transfers between devices, z_exchange(): return zh_pair(pack, lax.ppermute(pack, ('zh', 'zl'), Z_CROSS))  34.2 us
    pallas_call x2, Pallas kernels, attention_forward(): pl.pallas_call(functools.partial(attn_fwd_kernel, head_dim, scale), out_s...  25 us
    all_to_all x2, starting transfers between devices, body(): lax.all_to_all(kv_back.reshape(n_ctx, rows, kv_back.shape[1]), CTX, 0, 0,...  24.9 us
    all_to_all x2, starting transfers between devices, body(): lax.all_to_all(jnp.broadcast_to(kv_own[None], (n_ctx, rows, width)), CTX,...  23 us
  transfers between devices with their start and end apart: 25, of which 17 were waited for; matrix products, arithmetic and copies ran while one was open for 22% of the time, Pallas kernels for 12%

profile of v20, /device:TPU:0, one launch (start us, length us, event | category | flops | bytes accessed | tf_op | source)
XLA Modules:
  0.0 566.9 jit_solution(16800576103711379251)
XLA Ops:
  9.1 4.2 collective-permute-start.2
  13.3 7.0 %collective-permute-done.2 = bf16[144,1024]{1,0:T(8,128)(2,1)S(1)} collective-permute-done((bf16[144,1024]{1,0:T(8,128)(2,1)S(1)}, bf16[144,1024]{1,0:T(8,128)(2,1)S(1)}, u32[]{:S(2)}, u32[]{:S(2)}) %collective-permute-start.2) | collective-permute-done | bytes 294944 | tf_op jit(solution)/shard_map/ppermute | solution.py:199
  22.5 3.0 collective-permute-start
  26.0 14.8 %collective-permute-done = bf16[304,1024]{1,0:T(8,128)(2,1)S(1)} collective-permute-done((bf16[304,1024]{1,0:T(8,128)(2,1)S(1)}, bf16[304,1024]{1,0:T(8,128)(2,1)S(1)}, u32[]{:S(2)}, u32[]{:S(2)}) %collective-permute-start) | collective-permute-done | bytes 622624 | tf_op jit(solution)/shard_map/ppermute | solution.py:199
  42.0 12.4 %collective-permute-done.1 = bf16[64,5632]{1,0:T(8,128)(2,1)S(1)} collective-permute-done((bf16[64,5632]{1,0:T(8,128)(2,1)S(1)}, bf16[64,5632]{1,0:T(8,128)(2,1)S(1)}, u32[]{:S(2)}, u32[]{:S(2)}) %collective-permute-start.1) | collective-permute-done | bytes 720928 | tf_op jit(solution)/shard_map/ppermute | solution.py:199
  55.8 2.3 all-gather.7.cloned.1.call-done
  60.8 4.4 fusion.56
  65.2 4.5 copy.171
  69.7 2.5 convolution_bitcast_fusion.5
  77.0 2.5 broadcast_in_dim.76
  79.5 5.3 all-to-all-start
  85.0 49.7 %all-to-all-done = bf16[8,256,1024]{2,1,0:T(8,128)(2,1)} async-done(((bf16[8,256,1024]{2,1,0:T(8,128)(2,1)}), bf16[8,256,1024]{2,1,0:T(8,128)(2,1)}, u32[]{:S(2)}, u32[]{:S(2)}) %all-to-all-start) | async-done | bytes 4194336 | tf_op jit(solution)/shard_map/all_to_all | solution.py:324
  134.7 2.5 broadcast_in_dim.77
  137.2 17.7 %all-to-all-start.1 = ((bf16[8,256,1024]{2,1,0:T(8,128)(2,1)}), bf16[8,256,1024]{2,1,0:T(8,128)(2,1)}, u32[]{:S(2)}, u32[]{:S(2)}) async-start(bf16[8,256,1024]{2,1,0:T(8,128)(2,1)} %broadcast_in_dim.77), calls=%async_computation.1 | async-start | bytes 8388608 | tf_op jit(solution)/shard_map/all_to_all | solution.py:324
  157.6 4.2 fusion.55
  161.8 4.0 copy.174
  165.7 2.3 convolution_bitcast_fusion.3
  170.3 12.3 %shard_map.229 = bf16[256,512]{1,0:T(8,128)(2,1)S(1)} custom-call(s32[2]{0:T(128)S(1)} %pad_add_fusion.meta_ref, bf16[256,512]{1,0:T(8,128)(2,1)S(1)} %copy.222.q_ref, bf16[2048,1024]{1,0:T(8,128)(2,1)} %bitcast.24.k_ref.v_ref, bf16[2048,1024]{1,0:T(8,128)(2,1)} %bitcast.24.k_ref.v_ref), custom_call_target="tpu_custom_call" | custom-call | flops 1073741824 | bytes 4718592 | tf_op jit(solution)/shard_map/pallas_call | solution.py:80
  182.5 21.2 %all-to-all-done.1 = bf16[8,256,1024]{2,1,0:T(8,128)(2,1)} async-done(((bf16[8,256,1024]{2,1,0:T(8,128)(2,1)}), bf16[8,256,1024]{2,1,0:T(8,128)(2,1)}, u32[]{:S(2)}, u32[]{:S(2)}) %all-to-all-start.1) | async-done | bytes 4194336 | tf_op jit(solution)/shard_map/all_to_all | solution.py:324
  203.7 12.8 %shard_map.230 = bf16[256,512]{1,0:T(8,128)(2,1)S(1)} custom-call(s32[2]{0:T(128)S(1)} %pad_add_fusion.meta_ref, bf16[256,512]{1,0:T(8,128)(2,1)S(1)} %copy.224.q_ref, bf16[2048,1024]{1,0:T(8,128)(2,1)} %bitcast.32.k_ref.v_ref, bf16[2048,1024]{1,0:T(8,128)(2,1)} %bitcast.32.k_ref.v_ref), custom_call_target="tpu_custom_call" | custom-call | flops 1073741824 | bytes 4718592 | tf_op jit(solution)/shard_map/pallas_call | solution.py:80
  217.3 2.0 copy.179
  219.4 1.9 copy.180
  221.3 3.4 slice.154
  224.7 1.8 convolution_bitcast_fusion.1
  228.9 3.4 copy.187
  232.3 1.9 multiply_reduce_fusion.2
  236.1 2.0 copy.182
  238.1 1.9 copy.183
  240.0 6.4 %convolution_bitcast_fusion = f32[1,256,5632]{2,1,0:T(8,128)S(1)} fusion(bf16[256,1024]{0,1:T(8,128)(2,1)} %bitcast.252, bf16[1024,5632]{1,0:T(8,128)(2,1)} %bitcast.245), kind=kOutput, calls=%fused_computation.6 | convolution fusion | flops 2952790016 | bytes 17825792 | tf_op jit(solution)/shard_map/dot_general | solution.py:349
  246.4 2.7 multiply_convert_fusion.1
  249.2 3.2 fusion.6
  253.4 2.6 copy.190
  256.0 2.0 multiply_reduce_fusion
  258.0 2.1 subtract_add_fusion
  260.2 6.0 %convolution_convert_fusion = bf16[8,128,5632]{2,1,0:T(8,128)(2,1)} fusion(bf16[8,128,256]{2,1,0:T(8,128)(2,1)S(1)} %bitcast.253, bf16[1,256,2816]{2,1,0:T(8,128)(2,1)S(1)} %copy-done.21, bf16[1,256,2816]{2,1,0:T(8,128)(2,1)S(1)} %copy-done.19), kind=kOutput, calls=%fused_computation.3 | convolution fusion | flops 2964324352 | bytes 14942208 | tf_op jit(solution)/shard_map/srd,srf->df/dot_general | solution.py:367
  266.9 11.3 %pad_maximum_fusion = bf16[8,128,6656]{2,1,0:T(8,128)(2,1)} fusion(bf16[8,128,1024]{2,1,0:T(8,128)(2,1)S(1)} %convolution_convert_fusion.2, bf16[8,128,5632]{2,1,0:T(8,128)(2,1)} %convolution_convert_fusion), kind=kLoop, calls=%fused_computation.1 | loop fusion | flops 27262976 | bytes 27262976 | tf_op jit(solution)/shard_map/concatenate | solution.py:385
  278.2 2.8 convolution_convert_fusion.6
  283.2 21.3 %shard_map.232 = (f32[256,512]{1,0:T(8,128)S(1)}, bf16[2048,1024]{1,0:T(8,128)(2,1)S(1)}) custom-call(s32[2]{0:T(128)S(1)} %pad_add_fusion.meta_ref, bf16[256,512]{1,0:T(8,128)(2,1)S(1)} %copy.224.q_ref, bf16[2048,1024]{1,0:T(8,128)(2,1)} %bitcast.32.k_ref.v_ref, bf16[2048,1024]{1,0:T(8,128)(2,1)} %bitcast.32.k_ref.v_ref, bf16[256,512]{1,0:T(8,128)(2,1)S(1)} %copy.226.do_ref), custom_call_target="tpu_custom_call" | custom-call | flops 2684354560 | bytes 9699328 | tf_op jit(solution)/shard_map/pallas_call | solution.py:109
  304.5 2.0 copy-done
  306.5 15.0 %all-to-all-start.3 = ((bf16[8,256,1024]{2,1,0:T(8,128)(2,1)}), bf16[8,256,1024]{2,1,0:T(8,128)(2,1)}, u32[]{:S(2)}, u32[]{:S(2)}) async-start(bf16[8,256,1024]{2,1,0:T(8,128)(2,1)} %bitcast.227), calls=%async_computation.3 | async-start | bytes 8388608 | tf_op jit(solution)/shard_map/all_to_all | solution.py:420
  321.5 1.8 copy.184
  324.9 4.3 convolution_convert_fusion.1
  330.3 21.3 %shard_map.231 = (f32[256,512]{1,0:T(8,128)S(1)}, bf16[2048,1024]{1,0:T(8,128)(2,1)S(1)}) custom-call(s32[2]{0:T(128)S(1)} %pad_add_fusion.meta_ref, bf16[256,512]{1,0:T(8,128)(2,1)S(1)} %copy.222.q_ref, bf16[2048,1024]{1,0:T(8,128)(2,1)} %bitcast.24.k_ref.v_ref, bf16[2048,1024]{1,0:T(8,128)(2,1)} %bitcast.24.k_ref.v_ref, bf16[256,512]{1,0:T(8,128)(2,1)S(1)} %copy.225.do_ref), custom_call_target="tpu_custom_call" | custom-call | flops 2684354560 | bytes 9699328 | tf_op jit(solution)/shard_map/pallas_call | solution.py:109
  351.6 1.9 copy-done.1
  353.5 15.4 %all-to-all-done.3 = bf16[8,256,1024]{2,1,0:T(8,128)(2,1)} async-done(((bf16[8,256,1024]{2,1,0:T(8,128)(2,1)}), bf16[8,256,1024]{2,1,0:T(8,128)(2,1)}, u32[]{:S(2)}, u32[]{:S(2)}) %all-to-all-start.3) | async-done | bytes 4194336 | tf_op jit(solution)/shard_map/all_to_all | solution.py:420
  368.9 10.0 %all-to-all-start.2 = ((bf16[8,256,1024]{2,1,0:T(8,128)(2,1)}), bf16[8,256,1024]{2,1,0:T(8,128)(2,1)}, u32[]{:S(2)}, u32[]{:S(2)}) async-start(bf16[8,256,1024]{2,1,0:T(8,128)(2,1)} %bitcast.228), calls=%async_computation.2 | async-start | bytes 8388608 | tf_op jit(solution)/shard_map/all_to_all | solution.py:420
  382.1 3.3 convert_reduce_fusion
  386.7 38.4 %all-to-all-done.2 = bf16[8,256,1024]{2,1,0:T(8,128)(2,1)} async-done(((bf16[8,256,1024]{2,1,0:T(8,128)(2,1)}), bf16[8,256,1024]{2,1,0:T(8,128)(2,1)}, u32[]{:S(2)}, u32[]{:S(2)}) %all-to-all-start.2) | async-done | bytes 4194336 | tf_op jit(solution)/shard_map/all_to_all | solution.py:420
  425.1 3.2 convert_reduce_fusion.1
  429.6 2.8 fusion.53
  445.4 3.3 fusion.1
  450.0 2.0 collective-permute-start.7
  454.4 18.8 %collective-permute-done.7 = bf16[64,6656]{1,0:T(8,128)(2,1)} collective-permute-done((bf16[64,6656]{1,0:T(8,128)(2,1)S(1)}, bf16[64,6656]{1,0:T(8,128)(2,1)}, u32[]{:S(2)}, u32[]{:S(2)}) %collective-permute-start.7) | collective-permute-done | bytes 852000 | tf_op jit(solution)/shard_map/ppermute | solution.py:225
  475.4 4.1 collective-permute-done.11
  479.7 23.5 %collective-permute-done.12 = bf16[176,1024]{1,0:T(8,128)(2,1)S(1)} collective-permute-done((bf16[176,1024]{1,0:T(8,128)(2,1)S(1)}, bf16[176,1024]{1,0:T(8,128)(2,1)S(1)}, u32[]{:S(2)}, u32[]{:S(2)}) %collective-permute-start.12) | collective-permute-done | bytes 360480 | tf_op jit(solution)/shard_map/ppermute | solution.py:233
  504.6 3.7 collective-permute-start.9
  508.2 5.2 fusion.14
  518.7 2.4 collective-permute-start.3
  521.1 6.7 %collective-permute-done.9 = bf16[64,6656]{1,0:T(8,128)(2,1)} collective-permute-done((bf16[64,6656]{1,0:T(8,128)(2,1)}, bf16[64,6656]{1,0:T(8,128)(2,1)}, u32[]{:S(2)}, u32[]{:S(2)}) %collective-permute-start.9) | collective-permute-done | bytes 852000 | tf_op jit(solution)/shard_map/ppermute | solution.py:233
  531.8 1.9 fusion.40
  533.8 6.3 %collective-permute-done.4 = bf16[208,1024]{1,0:T(8,128)(2,1)S(1)} collective-permute-done((bf16[208,1024]{1,0:T(8,128)(2,1)S(1)}, bf16[208,1024]{1,0:T(8,128)(2,1)S(1)}, u32[]{:S(2)}, u32[]{:S(2)}) %collective-permute-start.4) | collective-permute-done | bytes 426016 | tf_op jit(solution)/shard_map/ppermute | solution.py:233
  540.2 1.9 collective-permute-start.5
  544.5 5.4 collective-permute-done.5
  552.2 6.1 %collective-permute-done.6 = bf16[208,1024]{1,0:T(8,128)(2,1)S(1)} collective-permute-done((bf16[208,1024]{1,0:T(8,128)(2,1)S(1)}, bf16[208,1024]{1,0:T(8,128)(2,1)S(1)}, u32[]{:S(2)}, u32[]{:S(2)}) %collective-permute-start.6) | collective-permute-done | bytes 426016 | tf_op jit(solution)/shard_map/ppermute | solution.py:233
  (218 shorter events, 73.0 us)
Async XLA Ops:
  7.2 15.2 %copy-start.36 = (bf16[64,1024]{1,0:T(8,128)(2,1)S(1)}, bf16[64,1024]{1,0:T(8,128)(2,1)}, u32[]{:S(2)}) copy-start(bf16[64,1024]{1,0:T(8,128)(2,1)} %param.16) | copy-start | bytes 393220
  7.2 15.2 %copy-start.37 = (bf16[64,1024]{1,0:T(8,128)(2,1)S(1)}, bf16[64,1024]{1,0:T(8,128)(2,1)}, u32[]{:S(2)}) copy-start(bf16[64,1024]{1,0:T(8,128)(2,1)} %param.19) | copy-start | bytes 393220
  7.2 15.3 %copy-start.33 = (bf16[176,1024]{1,0:T(8,128)(2,1)S(1)}, bf16[176,1024]{1,0:T(8,128)(2,1)}, u32[]{:S(2)}) copy-start(bf16[176,1024]{1,0:T(8,128)(2,1)} %param.22) | copy-start | bytes 1081348
  7.2 18.3 %copy-start.34 = (bf16[64,2816]{1,0:T(8,128)(2,1)S(1)}, bf16[64,2816]{1,0:T(8,128)(2,1)}, u32[]{:S(2)}) copy-start(bf16[64,2816]{1,0:T(8,128)(2,1)} %param.20) | copy-start | bytes 1081348
  7.2 18.3 %copy-start.35 = (bf16[64,2816]{1,0:T(8,128)(2,1)S(1)}, bf16[64,2816]{1,0:T(8,128)(2,1)}, u32[]{:S(2)}) copy-start(bf16[64,2816]{1,0:T(8,128)(2,1)} %param.21) | copy-start | bytes 1081348
  7.2 50.9 %all-gather.7.cloned.1.call-start = ((), (), s32[]{:S(2)}) async-start(), calls=%async_computation.10 | async-start | bytes 5308416 | tf_op jit(solution)/shard_map/all_gather | solution.py:203
  9.1 11.2 %collective-permute-start.2 = (bf16[144,1024]{1,0:T(8,128)(2,1)S(1)}, bf16[144,1024]{1,0:T(8,128)(2,1)S(1)}, u32[]{:S(2)}, u32[]{:S(2)}) collective-permute-start(bf16[144,1024]{1,0:T(8,128)(2,1)S(1)} %fusion.41), channel_id=1, source_target_pairs={{0,68},{68,0},{4,64},{64,4},{1,69},{69,1},{5,65},{65,5},{2,70},{70... | collective-permute-start | bytes 884744 | tf_op jit(solution)/shard_map/ppermute | solution.py:199
  22.3 135.2 %all-gather.9.cloned.1.call-start = ((), (), s32[]{:S(2)}) async-start(), calls=%async_computation.11 | async-start | bytes 11206656 | tf_op jit(solution)/shard_map/all_gather | solution.py:203
  22.5 18.3 %collective-permute-start = (bf16[304,1024]{1,0:T(8,128)(2,1)S(1)}, bf16[304,1024]{1,0:T(8,128)(2,1)S(1)}, u32[]{:S(2)}, u32[]{:S(2)}) collective-permute-start(bf16[304,1024]{1,0:T(8,128)(2,1)S(1)} %constant_dynamic-update-slice_fusion), channel_id=1, source_target_pairs={{0,68},{68,0},{4,64},{64,4},{1,69},{69,1},{5,65},{65,5},{2,70},{70... | collective-permute-start | bytes 1867784 | tf_op jit(solution)/shard_map/ppermute | solution.py:199
  25.6 28.9 %collective-permute-start.1 = (bf16[64,5632]{1,0:T(8,128)(2,1)S(1)}, bf16[64,5632]{1,0:T(8,128)(2,1)S(1)}, u32[]{:S(2)}, u32[]{:S(2)}) collective-permute-start(bf16[64,5632]{1,0:T(8,128)(2,1)S(1)} %constant_dynamic-update-slice_fusion.3), channel_id=1, source_target_pairs={{0,68},{68,0},{4,64},{64,4},{1,69},{69,1},{5,65},{65,5},{2,70},{70... | collective-permute-start | bytes 2162696 | tf_op jit(solution)/shard_map/ppermute | solution.py:199
  54.6 4.4 copy-start.10
  58.1 181.9 %all-gather.11.cloned.1.call-start = ((), (), s32[]{:S(2)}) async-start(), calls=%async_computation.12 | async-start | bytes 12976128 | tf_op jit(solution)/shard_map/all_gather | solution.py:203
  60.8 105.0 %copy-start.11 = (bf16[1,256,8,2,64]{1,4,3,2,0:T(8,128)(2,1)}, bf16[1,256,8,2,64]{1,4,3,2,0:T(8,128)(2,1)S(1)}, u32[]{:S(2)}) copy-start(bf16[1,256,8,2,64]{1,4,3,2,0:T(8,128)(2,1)S(1)} %copy.169) | copy-start | bytes 1572868
  65.2 9.8 %copy-start.2 = (bf16[16,64,1024]{2,1,0:T(8,128)(2,1)}, bf16[16,64,1024]{2,1,0:T(8,128)(2,1)S(1)}, u32[]{:S(2)}) copy-start(bf16[16,64,1024]{2,1,0:T(8,128)(2,1)S(1)} %get-tuple-element.100) | copy-start | bytes 6291460
  75.0 1.9 copy-start.30
  79.5 55.2 %all-to-all-start = ((bf16[8,256,1024]{2,1,0:T(8,128)(2,1)}), bf16[8,256,1024]{2,1,0:T(8,128)(2,1)}, u32[]{:S(2)}, u32[]{:S(2)}) async-start(bf16[8,256,1024]{2,1,0:T(8,128)(2,1)} %broadcast_in_dim.76), calls=%async_computation | async-start | bytes 8388608 | tf_op jit(solution)/shard_map/all_to_all | solution.py:324
  137.2 18.1 %copy-start.38 = (s32[16]{0:T(128)S(1)}, s32[16]{0:T(128)}, u32[]{:S(2)}) copy-start(s32[16]{0:T(128)} %param.26) | copy-start | bytes 196
  137.2 18.1 %copy-start.39 = (s32[16]{0:T(128)S(1)}, s32[16]{0:T(128)}, u32[]{:S(2)}) copy-start(s32[16]{0:T(128)} %param.27) | copy-start | bytes 196
  137.2 66.5 %all-to-all-start.1 = ((bf16[8,256,1024]{2,1,0:T(8,128)(2,1)}), bf16[8,256,1024]{2,1,0:T(8,128)(2,1)}, u32[]{:S(2)}, u32[]{:S(2)}) async-start(bf16[8,256,1024]{2,1,0:T(8,128)(2,1)} %broadcast_in_dim.77), calls=%async_computation.1 | async-start | bytes 8388608 | tf_op jit(solution)/shard_map/all_to_all | solution.py:324
  155.0 293.7 %reduce-scatter.4.cloned.1.call-start = ((), (), s32[]{:S(2)}) async-start(), calls=%async_computation.7 | async-start | bytes 15335424 | tf_op jit(solution)/shard_map/reduce_scatter | solution.py:215
  221.3 3.4 copy-start.27
  224.6 2.5 copy-start.22
  240.0 6.4 %copy-start.13 = (f32[1,256,2816]{2,1,0:T(8,128)S(1)}, f32[1,256,2816]{2,1,0:T(8,128)}, u32[]{:S(2)}) copy-start(f32[1,256,2816]{2,1,0:T(8,128)} %copy.187) | copy-start | bytes 8650756
  240.0 9.1 %slice-start = ((s8[11534336]{0:T(1024)(128)(4,1)}), s8[4194304]{0:T(1024)(128)(4,1)S(1)}, s32[]{:S(2)}) async-start(s8[11534336]{0:T(1024)(128)(4,1)} %bitcast.246), calls=%async_computation.13 | async-start | bytes 8388608
  240.0 9.1 %slice-start.1 = ((s8[11534336]{0:T(1024)(128)(4,1)}), s8[4194304]{0:T(1024)(128)(4,1)S(1)}, s32[]{:S(2)}) async-start(s8[11534336]{0:T(1024)(128)(4,1)} %bitcast.246), calls=%async_computation.14 | async-start | bytes 8388608
  246.4 2.7 slice-start.2
  249.2 3.2 copy-start.18
  249.2 3.2 copy-start.20
  256.0 4.1 copy-start.16
  256.0 4.1 copy-start.19
  256.0 4.1 copy-start.21
  260.1 6.0 %copy-start.6 = (f32[1,256,1024]{2,1,0:T(8,128)}, f32[1,256,1024]{2,1,0:T(8,128)S(1)}, u32[]{:S(2)}) copy-start(f32[1,256,1024]{2,1,0:T(8,128)S(1)} %subtract_add_fusion) | copy-start | bytes 3145732
  260.1 6.0 %copy-start.23 = (bf16[1,256,8,2,64]{1,4,3,2,0:T(8,128)(2,1)S(1)}, bf16[1,256,8,2,64]{1,4,3,2,0:T(8,128)(2,1)}, u32[]{:S(2)}) copy-start(bf16[1,256,8,2,64]{1,4,3,2,0:T(8,128)(2,1)} %copy.180) | copy-start | bytes 1572868
  304.5 2.0 copy-start
  306.5 15.0 %copy-start.17 = (bf16[1,256,2816]{2,1,0:T(8,128)(2,1)S(1)}, bf16[1,256,2816]{2,1,0:T(8,128)(2,1)}, u32[]{:S(2)}) copy-start(bf16[1,256,2816]{2,1,0:T(8,128)(2,1)} %get-tuple-element.96) | copy-start | bytes 4325380
  306.5 62.4 %all-to-all-start.3 = ((bf16[8,256,1024]{2,1,0:T(8,128)(2,1)}), bf16[8,256,1024]{2,1,0:T(8,128)(2,1)}, u32[]{:S(2)}, u32[]{:S(2)}) async-start(bf16[8,256,1024]{2,1,0:T(8,128)(2,1)} %bitcast.227), calls=%async_computation.3 | async-start | bytes 8388608 | tf_op jit(solution)/shard_map/all_to_all | solution.py:420
  321.4 130.5 %reduce-scatter.8.cloned.1.call-start = ((), (), s32[]{:S(2)}) async-start(), calls=%async_computation.9 | async-start | bytes 6488064 | tf_op jit(solution)/shard_map/reduce_scatter | solution.py:215
  321.5 3.4 copy-start.28
  324.9 4.3 copy-start.14
  351.6 2.0 copy-start.1
  368.9 56.2 %all-to-all-start.2 = ((bf16[8,256,1024]{2,1,0:T(8,128)(2,1)}), bf16[8,256,1024]{2,1,0:T(8,128)(2,1)}, u32[]{:S(2)}, u32[]{:S(2)}) async-start(bf16[8,256,1024]{2,1,0:T(8,128)(2,1)} %bitcast.228), calls=%async_computation.2 | async-start | bytes 8388608 | tf_op jit(solution)/shard_map/all_to_all | solution.py:420
  378.9 138.7 %reduce-scatter.6.cloned.1.call-start = ((), (), s32[]{:S(2)}) async-start(), calls=%async_computation.8 | async-start | bytes 7667712 | tf_op jit(solution)/shard_map/reduce_scatter | solution.py:215
  432.3 1.8 copy-start.5
  432.7 2.2 copy-start.4
  432.8 2.9 copy-start.24
  439.8 3.2 copy-start.12
  450.0 23.3 %collective-permute-start.7 = (bf16[64,6656]{1,0:T(8,128)(2,1)S(1)}, bf16[64,6656]{1,0:T(8,128)(2,1)}, u32[]{:S(2)}, u32[]{:S(2)}) collective-permute-start(bf16[64,6656]{1,0:T(8,128)(2,1)S(1)} %dynamic-slice_bitcast_fusion), channel_id=1, source_target_pairs={{0,68},{68,0},{4,64},{64,4},{1,69},{69,1},{5,65},{65,5},{2,70},{70... | collective-permute-start | bytes 2555912 | tf_op jit(solution)/shard_map/ppermute | solution.py:225
  451.9 27.5 %copy-start.32 = (bf16[1,352,1024]{2,1,0:T(8,128)(2,1)S(1)}, bf16[1,352,1024]{2,1,0:T(8,128)(2,1)}, u32[]{:S(2)}) copy-start(bf16[1,352,1024]{2,1,0:T(8,128)(2,1)} %reduce-scatter.8.cloned.1.call-done) | copy-start | bytes 2162692
  453.0 26.4 %collective-permute-start.11 = (bf16[176,1024]{1,0:T(8,128)(2,1)S(1)}, bf16[176,1024]{1,0:T(8,128)(2,1)S(1)}, u32[]{:S(2)}, u32[]{:S(2)}) collective-permute-start(bf16[176,1024]{1,0:T(8,128)(2,1)S(1)} %dynamic-slice_bitcast_fusion.2), channel_id=1, source_target_pairs={{0,68},{68,0},{4,64},{64,4},{1,69},{69,1},{5,65},{65,5},{2,70},{70... | collective-permute-start | bytes 1081352 | tf_op jit(solution)/shard_map/ppermute | solution.py:225
  474.9 33.4 %copy-start.9 = (f32[1,256,1024]{2,1,0:T(8,128)S(1)}, f32[1,256,1024]{2,1,0:T(8,128)}, u32[]{:S(2)}) copy-start(f32[1,256,1024]{2,1,0:T(8,128)} %copy-done.8) | copy-start | bytes 3145732
  474.9 33.4 %copy-start.15 = (bf16[1,256,8,2,176]{1,4,3,2,0:T(8,128)(2,1)S(1)}, bf16[1,256,8,2,176]{1,4,3,2,0:T(8,128)(2,1)}, u32[]{:S(2)}) copy-start(bf16[1,256,8,2,176]{1,4,3,2,0:T(8,128)(2,1)} %copy-done.14) | copy-start | bytes 4325380
  474.9 28.6 %collective-permute-start.8 = (bf16[64,6656]{1,0:T(8,128)(2,1)S(1)}, bf16[64,6656]{1,0:T(8,128)(2,1)S(1)}, u32[]{:S(2)}, u32[]{:S(2)}) collective-permute-start(bf16[64,6656]{1,0:T(8,128)(2,1)S(1)} %fusion.5), channel_id=1, source_target_pairs={{0,1},{1,0},{2,3},{3,2},{4,5},{5,4},{6,7},{7,6},{8,9},{9,8},{10,11... | collective-permute-start | bytes 2555912 | tf_op jit(solution)/shard_map/ppermute | solution.py:233
  479.6 23.6 %collective-permute-start.12 = (bf16[176,1024]{1,0:T(8,128)(2,1)S(1)}, bf16[176,1024]{1,0:T(8,128)(2,1)S(1)}, u32[]{:S(2)}, u32[]{:S(2)}) collective-permute-start(bf16[176,1024]{1,0:T(8,128)(2,1)S(1)} %fusion.32), channel_id=1, source_target_pairs={{0,1},{1,0},{2,3},{3,2},{4,5},{5,4},{6,7},{7,6},{8,9},{9,8},{10,11... | collective-permute-start | bytes 1081352 | tf_op jit(solution)/shard_map/ppermute | solution.py:233
  503.3 13.0 %collective-permute-start.13 = (bf16[176,1024]{1,0:T(8,128)(2,1)S(1)}, bf16[176,1024]{1,0:T(8,128)(2,1)}, u32[]{:S(2)}, u32[]{:S(2)}) collective-permute-start(bf16[176,1024]{1,0:T(8,128)(2,1)S(1)} %add_convert_fusion.8), channel_id=1, source_target_pairs={{0,2},{1,3},{2,0},{3,1},{4,6},{5,7},{6,4},{7,5},{8,10},{9,11},{10,... | collective-permute-start | bytes 1081352 | tf_op jit(solution)/shard_map/ppermute | solution.py:233
  504.6 23.2 %collective-permute-start.9 = (bf16[64,6656]{1,0:T(8,128)(2,1)}, bf16[64,6656]{1,0:T(8,128)(2,1)}, u32[]{:S(2)}, u32[]{:S(2)}) collective-permute-start(bf16[64,6656]{1,0:T(8,128)(2,1)} %add_convert_fusion.2), channel_id=1, source_target_pairs={{0,2},{1,3},{2,0},{3,1},{4,6},{5,7},{6,4},{7,5},{8,10},{9,11},{10,... | collective-permute-start | bytes 2555912 | tf_op jit(solution)/shard_map/ppermute | solution.py:233
  508.2 5.2 copy-start.26
  514.8 15.7 %copy-start.7 = (f32[1,256,1024]{2,1,0:T(8,128)S(1)}, f32[1,256,1024]{2,1,0:T(8,128)}, u32[]{:S(2)}) copy-start(f32[1,256,1024]{2,1,0:T(8,128)} %copy-done.6) | copy-start | bytes 3145732
  517.5 14.4 %collective-permute-start.14 = (bf16[176,1024]{1,0:T(8,128)(2,1)S(1)}, bf16[176,1024]{1,0:T(8,128)(2,1)}, u32[]{:S(2)}, u32[]{:S(2)}) collective-permute-start(bf16[176,1024]{1,0:T(8,128)(2,1)S(1)} %add_convert_fusion.7), channel_id=1, source_target_pairs={{0,4},{1,5},{2,6},{3,7},{4,0},{5,1},{6,2},{7,3},{8,12},{9,13},{10,... | collective-permute-start | bytes 1081352 | tf_op jit(solution)/shard_map/ppermute | solution.py:233
  517.6 12.6 %copy-start.31 = (bf16[1,416,1024]{2,1,0:T(8,128)(2,1)S(1)}, bf16[1,416,1024]{2,1,0:T(8,128)(2,1)}, u32[]{:S(2)}) copy-start(bf16[1,416,1024]{2,1,0:T(8,128)(2,1)} %reduce-scatter.6.cloned.1.call-done) | copy-start | bytes 2555908
  518.7 11.5 %collective-permute-start.3 = (bf16[208,1024]{1,0:T(8,128)(2,1)S(1)}, bf16[208,1024]{1,0:T(8,128)(2,1)S(1)}, u32[]{:S(2)}, u32[]{:S(2)}) collective-permute-start(bf16[208,1024]{1,0:T(8,128)(2,1)S(1)} %dynamic-slice_bitcast_fusion.1), channel_id=1, source_target_pairs={{0,68},{68,0},{4,64},{64,4},{1,69},{69,1},{5,65},{65,5},{2,70},{70... | collective-permute-start | bytes 1277960 | tf_op jit(solution)/shard_map/ppermute | solution.py:225
  529.4 14.2 %collective-permute-start.10 = (bf16[64,6656]{1,0:T(8,128)(2,1)S(1)}, bf16[64,6656]{1,0:T(8,128)(2,1)S(1)}, u32[]{:S(2)}, u32[]{:S(2)}) collective-permute-start(bf16[64,6656]{1,0:T(8,128)(2,1)S(1)} %add_convert_fusion.1), channel_id=1, source_target_pairs={{0,4},{1,5},{2,6},{3,7},{4,0},{5,1},{6,2},{7,3},{8,12},{9,13},{10,... | collective-permute-start | bytes 2555912 | tf_op jit(solution)/shard_map/ppermute | solution.py:233
  530.4 9.7 %collective-permute-start.4 = (bf16[208,1024]{1,0:T(8,128)(2,1)S(1)}, bf16[208,1024]{1,0:T(8,128)(2,1)S(1)}, u32[]{:S(2)}, u32[]{:S(2)}) collective-permute-start(bf16[208,1024]{1,0:T(8,128)(2,1)S(1)} %fusion.31), channel_id=1, source_target_pairs={{0,1},{1,0},{2,3},{3,2},{4,5},{5,4},{6,7},{7,6},{8,9},{9,8},{10,11... | collective-permute-start | bytes 1277960 | tf_op jit(solution)/shard_map/ppermute | solution.py:233
  540.2 9.7 %collective-permute-start.5 = (bf16[208,1024]{1,0:T(8,128)(2,1)S(1)}, bf16[208,1024]{1,0:T(8,128)(2,1)S(1)}, u32[]{:S(2)}, u32[]{:S(2)}) collective-permute-start(bf16[208,1024]{1,0:T(8,128)(2,1)S(1)} %add_convert_fusion.5), channel_id=1, source_target_pairs={{0,2},{1,3},{2,0},{3,1},{4,6},{5,7},{6,4},{7,5},{8,10},{9,11},{10,... | collective-permute-start | bytes 1277960 | tf_op jit(solution)/shard_map/ppermute | solution.py:233
  550.1 8.2 %collective-permute-start.6 = (bf16[208,1024]{1,0:T(8,128)(2,1)S(1)}, bf16[208,1024]{1,0:T(8,128)(2,1)S(1)}, u32[]{:S(2)}, u32[]{:S(2)}) collective-permute-start(bf16[208,1024]{1,0:T(8,128)(2,1)S(1)} %add_convert_fusion.4), channel_id=1, source_target_pairs={{0,4},{1,5},{2,6},{3,7},{4,0},{5,1},{6,2},{7,3},{8,12},{9,13},{10,... | collective-permute-start | bytes 1277960 | tf_op jit(solution)/shard_map/ppermute | solution.py:233
  (4 other events, 4.6 us)
Sparse Core Ops, SparseCore 0:
  22.5 35.6 all-gather.6
  59.8 56.3 all-gather.8
  117.9 63.1 all-gather.10
  278.3 86.6 reduce-scatter.3
  367.3 41.8 reduce-scatter.7
  448.9 43.8 reduce-scatter.5

commit v21 on v20

--- a/solution.py
+++ b/solution.py
@@ -424,33 +424,43 @@
             ).reshape(rows, half_blocks, 2, HEAD_BLOCK)
         )
     query_rot_back = jnp.concatenate(dq_parts, axis=-1).reshape(slots, rows, head_count, head_dim)
-    key_value = jnp.concatenate(kv_parts, axis=1)
-    key_rot_back = key_value[:, :, 0, :].reshape(slots, rows, head_count, head_dim)
-    value_mix_back = key_value[:, :, 1, :].reshape(slots, rows, width)
-    first_grad = 0.5 * value_mix_back
+    key_totals, value_totals, value_mix_backs, kv_normed_back = [], [], [], []
+    for part, key_value in enumerate(kv_parts):
+        cols = slice(part * half_width, (part + 1) * half_width)
+        key_rot_back = key_value[:, :, 0, :].reshape(slots, rows, head_count // 2, head_dim)
+        value_mix_back = key_value[:, :, 1, :].reshape(slots, rows, half_width)
+        key_back = (
+            rotate(key_rot_back, cos_rows, -sin_rows)
+            .reshape(slots, rows, half_width)
+            .astype(jnp.bfloat16)
+        )
+        value_back = (0.5 * value_mix_back).astype(jnp.bfloat16)
+        key_totals.append(
+            jnp.einsum("srd,sre->de", normed_low_g, key_back, preferred_element_type=jnp.float32)
+        )
+        value_totals.append(
+            jnp.einsum("srd,sre->de", normed_low_g, value_back, preferred_element_type=jnp.float32)
+        )
+        value_mix_backs.append(value_mix_back)
+        kv_normed_back.append(
+            jnp.einsum("sre,de->srd", key_back, key_mat[:, cols], preferred_element_type=jnp.float32)
+            + jnp.einsum(
+                "sre,de->srd", value_back, value_mat[:, cols], preferred_element_type=jnp.float32
+            )
+        )
+    first_grad = 0.5 * jnp.concatenate(value_mix_backs, axis=-1)
     query_back = (
         rotate(query_rot_back, cos_rows, -sin_rows).reshape(slots, rows, width).astype(jnp.bfloat16)
     )
-    key_back = (
-        rotate(key_rot_back, cos_rows, -sin_rows).reshape(slots, rows, width).astype(jnp.bfloat16)
-    )
-    value_back = (0.5 * value_mix_back).astype(jnp.bfloat16)
     query_total = jnp.einsum(
         "srd,sre->de", normed_low_g, query_back, preferred_element_type=jnp.float32
     )
-    key_total = jnp.einsum("srd,sre->de", normed_low_g, key_back, preferred_element_type=jnp.float32)
-    value_total = jnp.einsum(
-        "srd,sre->de", normed_low_g, value_back, preferred_element_type=jnp.float32
-    )
+    key_total = jnp.concatenate(key_totals, axis=1)
+    value_total = jnp.concatenate(value_totals, axis=1)
     normed_back = jnp.einsum(
         "sre,de->srd", query_back, query_mat, preferred_element_type=jnp.float32
     )
-    normed_back = normed_back + jnp.einsum(
-        "sre,de->srd", key_back, key_mat, preferred_element_type=jnp.float32
-    )
-    normed_back = normed_back + jnp.einsum(
-        "sre,de->srd", value_back, value_mat, preferred_element_type=jnp.float32
-    )
+    normed_back = normed_back + (kv_normed_back[0] + kv_normed_back[1])
     normed_back = from_gathered(normed_back, w_rows)
     tokens_norm_back, prenorm_total = norm_back(
         tokens_wide, inverse, prenorm_full.astype(jnp.float32), normed_back

time: 576 us -> 587 us (1.019)
  other arithmetic: 54 us -> 64.9 us
    concatenate x0 -> x4, local copies, waits for them, and re-layouts: none -> 9.37 us  [the longest x1 3.98 us: body(): value_total = jnp.concatenate(value_totals, axis=1)]
    unnamed x96 -> x115, local copies, waits for them, and re-layouts: 13.7 us -> 8.51 us
  transfers between devices with their start and end apart: 25 -> 25, of which waited for: 17 -> 17; matrix products, arithmetic and copies ran while one was open for 22% -> 24% of each run, Pallas kernels for 12% -> 12%
where the time goes in v21:
time: 587 us; the launch traced here: 580 us
  waiting for transfers between devices  234 us (40%)
  local copies, waits for them, and re-layouts  80.9 us (14%)
  starting transfers between devices  70.2 us (12%)
  Pallas kernels  67.2 us (11%)
  other arithmetic  64.9 us (11%)
  matrix products  46.9 us (8%)
  between operations  15.7 us (3%)
    all_to_all x2, waiting for transfers between devices, body(): lax.all_to_all(jnp.broadcast_to(kv_own[None], (n_ctx, rows, width)), CTX,...  72.5 us
    all_to_all x2, waiting for transfers between devices, body(): lax.all_to_all(kv_back.reshape(n_ctx, rows, kv_back.shape[1]), CTX, 0, 0,...  53 us
    ppermute x9, waiting for transfers between devices, ctx_allreduce(): other = lax.ppermute(total, CTX, [(j, j ^ step) for j in range(n_ctx)])  48.5 us
    pallas_call x2, Pallas kernels, attention_backward(): pl.pallas_call(functools.partial(attn_bwd_kernel, head_dim, scale), out_s...  42.5 us
    ppermute x3, waiting for transfers between devices, z_exchange(): return zh_pair(pack, lax.ppermute(pack, ('zh', 'zl'), Z_CROSS))  34.2 us
    all_to_all x2, starting transfers between devices, body(): lax.all_to_all(kv_back.reshape(n_ctx, rows, kv_back.shape[1]), CTX, 0, 0,...  24.9 us
    pallas_call x2, Pallas kernels, attention_forward(): pl.pallas_call(functools.partial(attn_fwd_kernel, head_dim, scale), out_s...  24.7 us
    all_to_all x2, starting transfers between devices, body(): lax.all_to_all(jnp.broadcast_to(kv_own[None], (n_ctx, rows, width)), CTX,...  23 us
  transfers between devices with their start and end apart: 25, of which 17 were waited for; matrix products, arithmetic and copies ran while one was open for 24% of the time, Pallas kernels for 12%

profile of v21, /device:TPU:0, one launch (start us, length us, event | category | flops | bytes accessed | tf_op | source)
XLA Modules:
  0.0 579.8 jit_solution(10000996485785775929)
XLA Ops:
  9.1 4.2 collective-permute-start.2
  13.3 7.0 %collective-permute-done.2 = bf16[144,1024]{1,0:T(8,128)(2,1)S(1)} collective-permute-done((bf16[144,1024]{1,0:T(8,128)(2,1)S(1)}, bf16[144,1024]{1,0:T(8,128)(2,1)S(1)}, u32[]{:S(2)}, u32[]{:S(2)}) %collective-permute-start.2) | collective-permute-done | bytes 294944 | tf_op jit(solution)/shard_map/ppermute | solution.py:199
  22.5 3.0 collective-permute-start
  26.0 14.8 %collective-permute-done = bf16[304,1024]{1,0:T(8,128)(2,1)S(1)} collective-permute-done((bf16[304,1024]{1,0:T(8,128)(2,1)S(1)}, bf16[304,1024]{1,0:T(8,128)(2,1)S(1)}, u32[]{:S(2)}, u32[]{:S(2)}) %collective-permute-start) | collective-permute-done | bytes 622624 | tf_op jit(solution)/shard_map/ppermute | solution.py:199
  42.0 12.5 %collective-permute-done.1 = bf16[64,5632]{1,0:T(8,128)(2,1)S(1)} collective-permute-done((bf16[64,5632]{1,0:T(8,128)(2,1)S(1)}, bf16[64,5632]{1,0:T(8,128)(2,1)S(1)}, u32[]{:S(2)}, u32[]{:S(2)}) %collective-permute-start.1) | collective-permute-done | bytes 720928 | tf_op jit(solution)/shard_map/ppermute | solution.py:199
  55.8 2.3 all-gather.7.cloned.1.call-done
  61.4 4.3 fusion.60
  65.6 4.5 copy.175
  70.2 2.5 convolution_bitcast_fusion.5
  74.9 2.6 broadcast_in_dim.76
  77.5 5.3 all-to-all-start
  83.0 49.7 %all-to-all-done = bf16[8,256,1024]{2,1,0:T(8,128)(2,1)} async-done(((bf16[8,256,1024]{2,1,0:T(8,128)(2,1)}), bf16[8,256,1024]{2,1,0:T(8,128)(2,1)}, u32[]{:S(2)}, u32[]{:S(2)}) %all-to-all-start) | async-done | bytes 4194336 | tf_op jit(solution)/shard_map/all_to_all | solution.py:324
  132.7 2.5 broadcast_in_dim.77
  135.2 17.7 %all-to-all-start.1 = ((bf16[8,256,1024]{2,1,0:T(8,128)(2,1)}), bf16[8,256,1024]{2,1,0:T(8,128)(2,1)}, u32[]{:S(2)}, u32[]{:S(2)}) async-start(bf16[8,256,1024]{2,1,0:T(8,128)(2,1)} %broadcast_in_dim.77), calls=%async_computation.1 | async-start | bytes 8388608 | tf_op jit(solution)/shard_map/all_to_all | solution.py:324
  155.5 4.3 fusion.59
  159.8 3.9 copy.178
  163.7 2.4 convolution_bitcast_fusion.3
  166.7 12.3 %shard_map.229 = bf16[256,512]{1,0:T(8,128)(2,1)S(1)} custom-call(s32[2]{0:T(128)S(1)} %pad_add_fusion.meta_ref, bf16[256,512]{1,0:T(8,128)(2,1)S(1)} %copy.226.q_ref, bf16[2048,1024]{1,0:T(8,128)(2,1)} %bitcast.24.k_ref.v_ref, bf16[2048,1024]{1,0:T(8,128)(2,1)} %bitcast.24.k_ref.v_ref), custom_call_target="tpu_custom_call" | custom-call | flops 1073741824 | bytes 4718592 | tf_op jit(solution)/shard_map/pallas_call | solution.py:80
  178.9 22.8 %all-to-all-done.1 = bf16[8,256,1024]{2,1,0:T(8,128)(2,1)} async-done(((bf16[8,256,1024]{2,1,0:T(8,128)(2,1)}), bf16[8,256,1024]{2,1,0:T(8,128)(2,1)}, u32[]{:S(2)}, u32[]{:S(2)}) %all-to-all-start.1) | async-done | bytes 4194336 | tf_op jit(solution)/shard_map/all_to_all | solution.py:324
  201.7 12.5 %shard_map.230 = bf16[256,512]{1,0:T(8,128)(2,1)S(1)} custom-call(s32[2]{0:T(128)S(1)} %pad_add_fusion.meta_ref, bf16[256,512]{1,0:T(8,128)(2,1)S(1)} %copy.228.q_ref, bf16[2048,1024]{1,0:T(8,128)(2,1)} %bitcast.32.k_ref.v_ref, bf16[2048,1024]{1,0:T(8,128)(2,1)} %bitcast.32.k_ref.v_ref), custom_call_target="tpu_custom_call" | custom-call | flops 1073741824 | bytes 4718592 | tf_op jit(solution)/shard_map/pallas_call | solution.py:80
  215.0 2.0 copy.183
  219.0 3.4 slice.186
  226.6 3.4 copy.191
  230.0 2.0 multiply_reduce_fusion.2
  234.0 2.0 copy.186
  237.9 6.4 %convolution_bitcast_fusion = f32[1,256,5632]{2,1,0:T(8,128)S(1)} fusion(bf16[256,1024]{0,1:T(8,128)(2,1)} %bitcast.263, bf16[1024,5632]{1,0:T(8,128)(2,1)} %bitcast.254), kind=kOutput, calls=%fused_computation.6 | convolution fusion | flops 2952790016 | bytes 17825792 | tf_op jit(solution)/shard_map/dot_general | solution.py:349
  244.3 2.7 multiply_convert_fusion.1
  247.0 3.2 fusion.6
  251.3 2.5 copy.194
  253.8 2.5 multiply_reduce_fusion
  256.4 2.1 subtract_add_fusion
  258.5 6.1 %convolution_convert_fusion = bf16[8,128,5632]{2,1,0:T(8,128)(2,1)} fusion(bf16[8,128,256]{2,1,0:T(8,128)(2,1)S(1)} %bitcast.264, bf16[1,256,2816]{2,1,0:T(8,128)(2,1)S(1)} %copy-done.20, bf16[1,256,2816]{2,1,0:T(8,128)(2,1)S(1)} %copy-done.18), kind=kOutput, calls=%fused_computation.3 | convolution fusion | flops 2964324352 | bytes 14942208 | tf_op jit(solution)/shard_map/srd,srf->df/dot_general | solution.py:367
  265.3 11.6 %pad_maximum_fusion = bf16[8,128,6656]{2,1,0:T(8,128)(2,1)} fusion(bf16[8,128,1024]{2,1,0:T(8,128)(2,1)S(1)} %convolution_convert_fusion.2, bf16[8,128,5632]{2,1,0:T(8,128)(2,1)} %convolution_convert_fusion), kind=kLoop, calls=%fused_computation.1 | loop fusion | flops 27262976 | bytes 27262976 | tf_op jit(solution)/shard_map/concatenate | solution.py:385
  277.0 2.8 convolution_convert_fusion.8
  281.9 21.3 %shard_map.232 = (f32[256,512]{1,0:T(8,128)S(1)}, bf16[2048,1024]{1,0:T(8,128)(2,1)S(1)}) custom-call(s32[2]{0:T(128)S(1)} %pad_add_fusion.meta_ref, bf16[256,512]{1,0:T(8,128)(2,1)S(1)} %copy.228.q_ref, bf16[2048,1024]{1,0:T(8,128)(2,1)} %bitcast.32.k_ref.v_ref, bf16[2048,1024]{1,0:T(8,128)(2,1)} %bitcast.32.k_ref.v_ref, bf16[256,512]{1,0:T(8,128)(2,1)S(1)} %copy.230.do_ref), custom_call_target="tpu_custom_call" | custom-call | flops 2684354560 | bytes 9699328 | tf_op jit(solution)/shard_map/pallas_call | solution.py:109
  303.2 2.0 copy-done.1
  305.2 15.0 %all-to-all-start.3 = ((bf16[8,256,1024]{2,1,0:T(8,128)(2,1)}), bf16[8,256,1024]{2,1,0:T(8,128)(2,1)}, u32[]{:S(2)}, u32[]{:S(2)}) async-start(bf16[8,256,1024]{2,1,0:T(8,128)(2,1)} %bitcast.233), calls=%async_computation.3 | async-start | bytes 8388608 | tf_op jit(solution)/shard_map/all_to_all | solution.py:420
  323.6 4.3 convolution_convert_fusion.1
  329.0 21.3 %shard_map.231 = (f32[256,512]{1,0:T(8,128)S(1)}, bf16[2048,1024]{1,0:T(8,128)(2,1)S(1)}) custom-call(s32[2]{0:T(128)S(1)} %pad_add_fusion.meta_ref, bf16[256,512]{1,0:T(8,128)(2,1)S(1)} %copy.226.q_ref, bf16[2048,1024]{1,0:T(8,128)(2,1)} %bitcast.24.k_ref.v_ref, bf16[2048,1024]{1,0:T(8,128)(2,1)} %bitcast.24.k_ref.v_ref, bf16[256,512]{1,0:T(8,128)(2,1)S(1)} %copy.229.do_ref), custom_call_target="tpu_custom_call" | custom-call | flops 2684354560 | bytes 9699328 | tf_op jit(solution)/shard_map/pallas_call | solution.py:109
  350.3 2.0 copy-done
  352.3 15.4 %all-to-all-done.3 = bf16[8,256,1024]{2,1,0:T(8,128)(2,1)} async-done(((bf16[8,256,1024]{2,1,0:T(8,128)(2,1)}), bf16[8,256,1024]{2,1,0:T(8,128)(2,1)}, u32[]{:S(2)}, u32[]{:S(2)}) %all-to-all-start.3) | async-done | bytes 4194336 | tf_op jit(solution)/shard_map/all_to_all | solution.py:420
  367.7 9.9 %all-to-all-start.2 = ((bf16[8,256,1024]{2,1,0:T(8,128)(2,1)}), bf16[8,256,1024]{2,1,0:T(8,128)(2,1)}, u32[]{:S(2)}, u32[]{:S(2)}) async-start(bf16[8,256,1024]{2,1,0:T(8,128)(2,1)} %bitcast.232), calls=%async_computation.2 | async-start | bytes 8388608 | tf_op jit(solution)/shard_map/all_to_all | solution.py:420
  378.7 2.1 convolution_convert_fusion.3
  381.6 3.3 convert_reduce_fusion
  386.3 37.5 %all-to-all-done.2 = bf16[8,256,1024]{2,1,0:T(8,128)(2,1)} async-done(((bf16[8,256,1024]{2,1,0:T(8,128)(2,1)}), bf16[8,256,1024]{2,1,0:T(8,128)(2,1)}, u32[]{:S(2)}, u32[]{:S(2)}) %all-to-all-start.2) | async-done | bytes 4194336 | tf_op jit(solution)/shard_map/all_to_all | solution.py:420
  423.8 3.2 convert_reduce_fusion.1
  428.4 2.2 fusion.63
  443.1 4.0 copy.209
  449.5 4.0 copy.208
  453.5 6.1 %fusion.1 = bf16[16,208,1024]{2,1,0:T(8,128)(2,1)} fusion(bf16[16,1,1024]{2,1,0:T(2,128)(2,1)S(1)} %copy.214, bf16[16,64,1024]{2,1,0:T(8,128)(2,1)} %bitcast.261, bf16[16,64,1024]{2,1,0:T(8,128)(2,1)} %bitcast.262, bf16[16,64,1024]{2,1,0:T(8,128)(2,1)} %convolution_convert_fusion.3), kind=kLoop, calls=%fused_computation.7 | loop fusion | flops 34078720 | bytes 13139968 | tf_op jit(solution)/shard_map/concatenate | solution.py:470
  460.8 2.0 collective-permute-start.7
  465.3 18.8 %collective-permute-done.7 = bf16[64,6656]{1,0:T(8,128)(2,1)} collective-permute-done((bf16[64,6656]{1,0:T(8,128)(2,1)S(1)}, bf16[64,6656]{1,0:T(8,128)(2,1)}, u32[]{:S(2)}, u32[]{:S(2)}) %collective-permute-start.7) | collective-permute-done | bytes 852000 | tf_op jit(solution)/shard_map/ppermute | solution.py:225
  486.3 4.0 collective-permute-done.11
  490.8 23.2 %collective-permute-done.12 = bf16[176,1024]{1,0:T(8,128)(2,1)S(1)} collective-permute-done((bf16[176,1024]{1,0:T(8,128)(2,1)S(1)}, bf16[176,1024]{1,0:T(8,128)(2,1)S(1)}, u32[]{:S(2)}, u32[]{:S(2)}) %collective-permute-start.12) | collective-permute-done | bytes 360480 | tf_op jit(solution)/shard_map/ppermute | solution.py:233
  515.3 3.5 collective-permute-start.9
  518.9 5.1 fusion.16
  524.0 3.1 collective-permute-done.13
  528.4 2.5 collective-permute-start.3
  530.9 7.7 %collective-permute-done.9 = bf16[64,6656]{1,0:T(8,128)(2,1)} collective-permute-done((bf16[64,6656]{1,0:T(8,128)(2,1)}, bf16[64,6656]{1,0:T(8,128)(2,1)}, u32[]{:S(2)}, u32[]{:S(2)}) %collective-permute-start.9) | collective-permute-done | bytes 852000 | tf_op jit(solution)/shard_map/ppermute | solution.py:233
  538.7 2.5 add_convert_fusion.1
  546.8 2.0 fusion.46
  548.7 2.8 collective-permute-done.4
  558.0 4.6 collective-permute-done.5
  565.0 5.9 %collective-permute-done.6 = bf16[208,1024]{1,0:T(8,128)(2,1)S(1)} collective-permute-done((bf16[208,1024]{1,0:T(8,128)(2,1)S(1)}, bf16[208,1024]{1,0:T(8,128)(2,1)S(1)}, u32[]{:S(2)}, u32[]{:S(2)}) %collective-permute-start.6) | collective-permute-done | bytes 426016 | tf_op jit(solution)/shard_map/ppermute | solution.py:233
  (251 shorter events, 79.1 us)
Async XLA Ops:
  7.2 15.2 %copy-start.42 = (bf16[64,1024]{1,0:T(8,128)(2,1)S(1)}, bf16[64,1024]{1,0:T(8,128)(2,1)}, u32[]{:S(2)}) copy-start(bf16[64,1024]{1,0:T(8,128)(2,1)} %param.16) | copy-start | bytes 393220
  7.2 15.2 %copy-start.43 = (bf16[64,1024]{1,0:T(8,128)(2,1)S(1)}, bf16[64,1024]{1,0:T(8,128)(2,1)}, u32[]{:S(2)}) copy-start(bf16[64,1024]{1,0:T(8,128)(2,1)} %param.19) | copy-start | bytes 393220
  7.2 15.3 %copy-start.38 = (bf16[176,1024]{1,0:T(8,128)(2,1)S(1)}, bf16[176,1024]{1,0:T(8,128)(2,1)}, u32[]{:S(2)}) copy-start(bf16[176,1024]{1,0:T(8,128)(2,1)} %param.22) | copy-start | bytes 1081348
  7.2 18.3 %copy-start.39 = (bf16[64,2816]{1,0:T(8,128)(2,1)S(1)}, bf16[64,2816]{1,0:T(8,128)(2,1)}, u32[]{:S(2)}) copy-start(bf16[64,2816]{1,0:T(8,128)(2,1)} %param.20) | copy-start | bytes 1081348
  7.2 18.3 %copy-start.40 = (bf16[64,2816]{1,0:T(8,128)(2,1)S(1)}, bf16[64,2816]{1,0:T(8,128)(2,1)}, u32[]{:S(2)}) copy-start(bf16[64,2816]{1,0:T(8,128)(2,1)} %param.21) | copy-start | bytes 1081348
  7.2 50.9 %all-gather.7.cloned.1.call-start = ((), (), s32[]{:S(2)}) async-start(), calls=%async_computation.10 | async-start | bytes 5308416 | tf_op jit(solution)/shard_map/all_gather | solution.py:203
  9.1 11.2 %collective-permute-start.2 = (bf16[144,1024]{1,0:T(8,128)(2,1)S(1)}, bf16[144,1024]{1,0:T(8,128)(2,1)S(1)}, u32[]{:S(2)}, u32[]{:S(2)}) collective-permute-start(bf16[144,1024]{1,0:T(8,128)(2,1)S(1)} %fusion.47), channel_id=1, source_target_pairs={{0,68},{68,0},{4,64},{64,4},{1,69},{69,1},{5,65},{65,5},{2,70},{70... | collective-permute-start | bytes 884744 | tf_op jit(solution)/shard_map/ppermute | solution.py:199
  22.3 133.1 %all-gather.9.cloned.1.call-start = ((), (), s32[]{:S(2)}) async-start(), calls=%async_computation.11 | async-start | bytes 11206656 | tf_op jit(solution)/shard_map/all_gather | solution.py:203
  22.5 18.3 %collective-permute-start = (bf16[304,1024]{1,0:T(8,128)(2,1)S(1)}, bf16[304,1024]{1,0:T(8,128)(2,1)S(1)}, u32[]{:S(2)}, u32[]{:S(2)}) collective-permute-start(bf16[304,1024]{1,0:T(8,128)(2,1)S(1)} %constant_dynamic-update-slice_fusion), channel_id=1, source_target_pairs={{0,68},{68,0},{4,64},{64,4},{1,69},{69,1},{5,65},{65,5},{2,70},{70... | collective-permute-start | bytes 1867784 | tf_op jit(solution)/shard_map/ppermute | solution.py:199
  25.6 28.9 %collective-permute-start.1 = (bf16[64,5632]{1,0:T(8,128)(2,1)S(1)}, bf16[64,5632]{1,0:T(8,128)(2,1)S(1)}, u32[]{:S(2)}, u32[]{:S(2)}) collective-permute-start(bf16[64,5632]{1,0:T(8,128)(2,1)S(1)} %constant_dynamic-update-slice_fusion.3), channel_id=1, source_target_pairs={{0,68},{68,0},{4,64},{64,4},{1,69},{69,1},{5,65},{65,5},{2,70},{70... | collective-permute-start | bytes 2162696 | tf_op jit(solution)/shard_map/ppermute | solution.py:199
  54.5 4.4 copy-start.10
  58.1 179.7 %all-gather.11.cloned.1.call-start = ((), (), s32[]{:S(2)}) async-start(), calls=%async_computation.12 | async-start | bytes 12976128 | tf_op jit(solution)/shard_map/all_gather | solution.py:203
  59.9 106.2 %copy-start.35 = (f32[256,32]{0,1:T(8,128)}, f32[256,32]{0,1:T(8,128)S(1)}, u32[]{:S(2)}) copy-start(f32[256,32]{0,1:T(8,128)S(1)} %get-tuple-element.94) | copy-start | bytes 98308
  65.6 7.4 %copy-start.2 = (bf16[16,64,1024]{2,1,0:T(8,128)(2,1)}, bf16[16,64,1024]{2,1,0:T(8,128)(2,1)S(1)}, u32[]{:S(2)}) copy-start(bf16[16,64,1024]{2,1,0:T(8,128)(2,1)S(1)} %get-tuple-element.50) | copy-start | bytes 6291460
  77.5 55.2 %all-to-all-start = ((bf16[8,256,1024]{2,1,0:T(8,128)(2,1)}), bf16[8,256,1024]{2,1,0:T(8,128)(2,1)}, u32[]{:S(2)}, u32[]{:S(2)}) async-start(bf16[8,256,1024]{2,1,0:T(8,128)(2,1)} %broadcast_in_dim.76), calls=%async_computation | async-start | bytes 8388608 | tf_op jit(solution)/shard_map/all_to_all | solution.py:324
  135.2 18.0 %copy-start.48 = (s32[16]{0:T(128)S(1)}, s32[16]{0:T(128)}, u32[]{:S(2)}) copy-start(s32[16]{0:T(128)} %param.26) | copy-start | bytes 196
  135.2 18.0 %copy-start.49 = (s32[16]{0:T(128)S(1)}, s32[16]{0:T(128)}, u32[]{:S(2)}) copy-start(s32[16]{0:T(128)} %param.27) | copy-start | bytes 196
  135.2 66.5 %all-to-all-start.1 = ((bf16[8,256,1024]{2,1,0:T(8,128)(2,1)}), bf16[8,256,1024]{2,1,0:T(8,128)(2,1)}, u32[]{:S(2)}, u32[]{:S(2)}) async-start(bf16[8,256,1024]{2,1,0:T(8,128)(2,1)} %broadcast_in_dim.77), calls=%async_computation.1 | async-start | bytes 8388608 | tf_op jit(solution)/shard_map/all_to_all | solution.py:324
  153.0 306.6 %reduce-scatter.4.cloned.1.call-start = ((), (), s32[]{:S(2)}) async-start(), calls=%async_computation.7 | async-start | bytes 15335424 | tf_op jit(solution)/shard_map/reduce_scatter | solution.py:215
  155.4 101.0 %copy-start.45 = (pred[256]{0:T(512)(128)(4,1)}, pred[256]{0:T(512)(128)(4,1)S(1)}, u32[]{:S(2)}) copy-start(pred[256]{0:T(512)(128)(4,1)S(1)} %fusion.54) | copy-start | bytes 772
  219.0 3.4 copy-start.30
  222.3 2.5 copy-start.21
  237.9 6.4 %copy-start.12 = (f32[1,256,2816]{2,1,0:T(8,128)S(1)}, f32[1,256,2816]{2,1,0:T(8,128)}, u32[]{:S(2)}) copy-start(f32[1,256,2816]{2,1,0:T(8,128)} %copy.191) | copy-start | bytes 8650756
  237.9 9.1 %slice-start = ((s8[11534336]{0:T(1024)(128)(4,1)}), s8[4194304]{0:T(1024)(128)(4,1)S(1)}, s32[]{:S(2)}) async-start(s8[11534336]{0:T(1024)(128)(4,1)} %bitcast.255), calls=%async_computation.13 | async-start | bytes 8388608
  237.9 9.1 %slice-start.1 = ((s8[11534336]{0:T(1024)(128)(4,1)}), s8[4194304]{0:T(1024)(128)(4,1)S(1)}, s32[]{:S(2)}) async-start(s8[11534336]{0:T(1024)(128)(4,1)} %bitcast.255), calls=%async_computation.14 | async-start | bytes 8388608
  244.3 2.7 slice-start.2
  247.0 3.2 copy-start.17
  247.0 3.2 copy-start.19
  253.8 4.7 copy-start.15
  253.8 4.7 copy-start.18
  253.8 4.7 copy-start.20
  258.5 6.1 %copy-start.6 = (f32[1,256,1024]{2,1,0:T(8,128)}, f32[1,256,1024]{2,1,0:T(8,128)S(1)}, u32[]{:S(2)}) copy-start(f32[1,256,1024]{2,1,0:T(8,128)S(1)} %subtract_add_fusion) | copy-start | bytes 3145732
  258.5 6.1 %copy-start.22 = (bf16[1,256,8,2,64]{1,4,3,2,0:T(8,128)(2,1)S(1)}, bf16[1,256,8,2,64]{1,4,3,2,0:T(8,128)(2,1)}, u32[]{:S(2)}) copy-start(bf16[1,256,8,2,64]{1,4,3,2,0:T(8,128)(2,1)} %copy.184) | copy-start | bytes 1572868
  305.2 15.0 %copy-start.16 = (bf16[1,256,2816]{2,1,0:T(8,128)(2,1)S(1)}, bf16[1,256,2816]{2,1,0:T(8,128)(2,1)}, u32[]{:S(2)}) copy-start(bf16[1,256,2816]{2,1,0:T(8,128)(2,1)} %get-tuple-element.46) | copy-start | bytes 4325380
  305.2 62.5 %all-to-all-start.3 = ((bf16[8,256,1024]{2,1,0:T(8,128)(2,1)}), bf16[8,256,1024]{2,1,0:T(8,128)(2,1)}, u32[]{:S(2)}, u32[]{:S(2)}) async-start(bf16[8,256,1024]{2,1,0:T(8,128)(2,1)} %bitcast.233), calls=%async_computation.3 | async-start | bytes 8388608 | tf_op jit(solution)/shard_map/all_to_all | solution.py:420
  320.2 142.6 %reduce-scatter.8.cloned.1.call-start = ((), (), s32[]{:S(2)}) async-start(), calls=%async_computation.9 | async-start | bytes 6488064 | tf_op jit(solution)/shard_map/reduce_scatter | solution.py:215
  320.3 3.3 copy-start.31
  320.3 3.3 copy-start.46
  323.6 4.4 copy-start.13
  367.7 56.1 %all-to-all-start.2 = ((bf16[8,256,1024]{2,1,0:T(8,128)(2,1)}), bf16[8,256,1024]{2,1,0:T(8,128)(2,1)}, u32[]{:S(2)}, u32[]{:S(2)}) async-start(bf16[8,256,1024]{2,1,0:T(8,128)(2,1)} %bitcast.232), calls=%async_computation.2 | async-start | bytes 8388608 | tf_op jit(solution)/shard_map/all_to_all | solution.py:420
  377.7 149.6 %reduce-scatter.6.cloned.1.call-start = ((), (), s32[]{:S(2)}) async-start(), calls=%async_computation.8 | async-start | bytes 7667712 | tf_op jit(solution)/shard_map/reduce_scatter | solution.py:215
  430.6 3.4 copy-start.28
  435.6 4.4 copy-start.11
  438.4 2.7 copy-start.27
  443.1 4.0 copy-start.25
  460.8 23.3 %collective-permute-start.7 = (bf16[64,6656]{1,0:T(8,128)(2,1)S(1)}, bf16[64,6656]{1,0:T(8,128)(2,1)}, u32[]{:S(2)}, u32[]{:S(2)}) collective-permute-start(bf16[64,6656]{1,0:T(8,128)(2,1)S(1)} %dynamic-slice_bitcast_fusion), channel_id=1, source_target_pairs={{0,68},{68,0},{4,64},{64,4},{1,69},{69,1},{5,65},{65,5},{2,70},{70... | collective-permute-start | bytes 2555912 | tf_op jit(solution)/shard_map/ppermute | solution.py:225
  462.8 27.5 %copy-start.37 = (bf16[1,352,1024]{2,1,0:T(8,128)(2,1)S(1)}, bf16[1,352,1024]{2,1,0:T(8,128)(2,1)}, u32[]{:S(2)}) copy-start(bf16[1,352,1024]{2,1,0:T(8,128)(2,1)} %reduce-scatter.8.cloned.1.call-done) | copy-start | bytes 2162692
  463.9 26.4 %collective-permute-start.11 = (bf16[176,1024]{1,0:T(8,128)(2,1)S(1)}, bf16[176,1024]{1,0:T(8,128)(2,1)S(1)}, u32[]{:S(2)}, u32[]{:S(2)}) collective-permute-start(bf16[176,1024]{1,0:T(8,128)(2,1)S(1)} %dynamic-slice_bitcast_fusion.2), channel_id=1, source_target_pairs={{0,68},{68,0},{4,64},{64,4},{1,69},{69,1},{5,65},{65,5},{2,70},{70... | collective-permute-start | bytes 1081352 | tf_op jit(solution)/shard_map/ppermute | solution.py:225
  485.7 33.1 %copy-start.9 = (f32[1,256,1024]{2,1,0:T(8,128)S(1)}, f32[1,256,1024]{2,1,0:T(8,128)}, u32[]{:S(2)}) copy-start(f32[1,256,1024]{2,1,0:T(8,128)} %copy-done.8) | copy-start | bytes 3145732
  485.7 33.1 %copy-start.14 = (bf16[1,256,8,2,176]{1,4,3,2,0:T(8,128)(2,1)S(1)}, bf16[1,256,8,2,176]{1,4,3,2,0:T(8,128)(2,1)}, u32[]{:S(2)}) copy-start(bf16[1,256,8,2,176]{1,4,3,2,0:T(8,128)(2,1)} %copy-done.13) | copy-start | bytes 4325380
  485.7 33.1 %copy-start.47 = (pred[256]{0:T(512)(128)(4,1)S(1)}, pred[256]{0:T(512)(128)(4,1)}, u32[]{:S(2)}) copy-start(pred[256]{0:T(512)(128)(4,1)} %copy-done.45) | copy-start | bytes 772
  485.7 28.5 %collective-permute-start.8 = (bf16[64,6656]{1,0:T(8,128)(2,1)S(1)}, bf16[64,6656]{1,0:T(8,128)(2,1)S(1)}, u32[]{:S(2)}, u32[]{:S(2)}) collective-permute-start(bf16[64,6656]{1,0:T(8,128)(2,1)S(1)} %fusion.5), channel_id=1, source_target_pairs={{0,1},{1,0},{2,3},{3,2},{4,5},{5,4},{6,7},{7,6},{8,9},{9,8},{10,11... | collective-permute-start | bytes 2555912 | tf_op jit(solution)/shard_map/ppermute | solution.py:233
  490.4 23.6 %collective-permute-start.12 = (bf16[176,1024]{1,0:T(8,128)(2,1)S(1)}, bf16[176,1024]{1,0:T(8,128)(2,1)S(1)}, u32[]{:S(2)}, u32[]{:S(2)}) collective-permute-start(bf16[176,1024]{1,0:T(8,128)(2,1)S(1)} %fusion.38), channel_id=1, source_target_pairs={{0,1},{1,0},{2,3},{3,2},{4,5},{5,4},{6,7},{7,6},{8,9},{9,8},{10,11... | collective-permute-start | bytes 1081352 | tf_op jit(solution)/shard_map/ppermute | solution.py:233
  514.1 12.9 %collective-permute-start.13 = (bf16[176,1024]{1,0:T(8,128)(2,1)S(1)}, bf16[176,1024]{1,0:T(8,128)(2,1)S(1)}, u32[]{:S(2)}, u32[]{:S(2)}) collective-permute-start(bf16[176,1024]{1,0:T(8,128)(2,1)S(1)} %add_convert_fusion.8), channel_id=1, source_target_pairs={{0,2},{1,3},{2,0},{3,1},{4,6},{5,7},{6,4},{7,5},{8,10},{9,11},{10,... | collective-permute-start | bytes 1081352 | tf_op jit(solution)/shard_map/ppermute | solution.py:233
  515.3 23.3 %collective-permute-start.9 = (bf16[64,6656]{1,0:T(8,128)(2,1)}, bf16[64,6656]{1,0:T(8,128)(2,1)}, u32[]{:S(2)}, u32[]{:S(2)}) collective-permute-start(bf16[64,6656]{1,0:T(8,128)(2,1)} %add_convert_fusion.2), channel_id=1, source_target_pairs={{0,2},{1,3},{2,0},{3,1},{4,6},{5,7},{6,4},{7,5},{8,10},{9,11},{10,... | collective-permute-start | bytes 2555912 | tf_op jit(solution)/shard_map/ppermute | solution.py:233
  524.0 18.9 %copy-start.7 = (f32[1,256,1024]{2,1,0:T(8,128)S(1)}, f32[1,256,1024]{2,1,0:T(8,128)}, u32[]{:S(2)}) copy-start(f32[1,256,1024]{2,1,0:T(8,128)} %copy-done.6) | copy-start | bytes 3145732
  527.2 19.6 %collective-permute-start.14 = (bf16[176,1024]{1,0:T(8,128)(2,1)S(1)}, bf16[176,1024]{1,0:T(8,128)(2,1)}, u32[]{:S(2)}, u32[]{:S(2)}) collective-permute-start(bf16[176,1024]{1,0:T(8,128)(2,1)S(1)} %add_convert_fusion.7), channel_id=1, source_target_pairs={{0,4},{1,5},{2,6},{3,7},{4,0},{5,1},{6,2},{7,3},{8,12},{9,13},{10,... | collective-permute-start | bytes 1081352 | tf_op jit(solution)/shard_map/ppermute | solution.py:233
  527.3 14.7 %copy-start.34 = (bf16[1,416,1024]{2,1,0:T(8,128)(2,1)S(1)}, bf16[1,416,1024]{2,1,0:T(8,128)(2,1)}, u32[]{:S(2)}) copy-start(bf16[1,416,1024]{2,1,0:T(8,128)(2,1)} %reduce-scatter.6.cloned.1.call-done) | copy-start | bytes 2555908
  528.4 13.5 %collective-permute-start.3 = (bf16[208,1024]{1,0:T(8,128)(2,1)S(1)}, bf16[208,1024]{1,0:T(8,128)(2,1)S(1)}, u32[]{:S(2)}, u32[]{:S(2)}) collective-permute-start(bf16[208,1024]{1,0:T(8,128)(2,1)S(1)} %dynamic-slice_bitcast_fusion.1), channel_id=1, source_target_pairs={{0,68},{68,0},{4,64},{64,4},{1,69},{69,1},{5,65},{65,5},{2,70},{70... | collective-permute-start | bytes 1277960 | tf_op jit(solution)/shard_map/ppermute | solution.py:225
  541.2 3.1 copy-start.32
  541.2 14.5 %collective-permute-start.10 = (bf16[64,6656]{1,0:T(8,128)(2,1)}, bf16[64,6656]{1,0:T(8,128)(2,1)}, u32[]{:S(2)}, u32[]{:S(2)}) collective-permute-start(bf16[64,6656]{1,0:T(8,128)(2,1)} %add_convert_fusion.1), channel_id=1, source_target_pairs={{0,4},{1,5},{2,6},{3,7},{4,0},{5,1},{6,2},{7,3},{8,12},{9,13},{10,... | collective-permute-start | bytes 2555912 | tf_op jit(solution)/shard_map/ppermute | solution.py:233
  542.9 8.7 %collective-permute-start.4 = (bf16[208,1024]{1,0:T(8,128)(2,1)}, bf16[208,1024]{1,0:T(8,128)(2,1)}, u32[]{:S(2)}, u32[]{:S(2)}) collective-permute-start(bf16[208,1024]{1,0:T(8,128)(2,1)} %fusion.37), channel_id=1, source_target_pairs={{0,1},{1,0},{2,3},{3,2},{4,5},{5,4},{6,7},{7,6},{8,9},{9,8},{10,11... | collective-permute-start | bytes 1277960 | tf_op jit(solution)/shard_map/ppermute | solution.py:233
  552.9 9.7 %collective-permute-start.5 = (bf16[208,1024]{1,0:T(8,128)(2,1)S(1)}, bf16[208,1024]{1,0:T(8,128)(2,1)S(1)}, u32[]{:S(2)}, u32[]{:S(2)}) collective-permute-start(bf16[208,1024]{1,0:T(8,128)(2,1)S(1)} %add_convert_fusion.5), channel_id=1, source_target_pairs={{0,2},{1,3},{2,0},{3,1},{4,6},{5,7},{6,4},{7,5},{8,10},{9,11},{10,... | collective-permute-start | bytes 1277960 | tf_op jit(solution)/shard_map/ppermute | solution.py:233
  562.7 8.2 %collective-permute-start.6 = (bf16[208,1024]{1,0:T(8,128)(2,1)S(1)}, bf16[208,1024]{1,0:T(8,128)(2,1)S(1)}, u32[]{:S(2)}, u32[]{:S(2)}) collective-permute-start(bf16[208,1024]{1,0:T(8,128)(2,1)S(1)} %add_convert_fusion.4), channel_id=1, source_target_pairs={{0,4},{1,5},{2,6},{3,7},{4,0},{5,1},{6,2},{7,3},{8,12},{9,13},{10,... | collective-permute-start | bytes 1277960 | tf_op jit(solution)/shard_map/ppermute | solution.py:233
  (14 other events, 23.0 us)
Sparse Core Ops, SparseCore 0:
  22.5 35.6 all-gather.6
  59.8 56.3 all-gather.8
  117.8 63.1 all-gather.10
  277.1 86.7 reduce-scatter.3
  366.2 41.8 reduce-scatter.7
  459.7 44.5 reduce-scatter.5

commit v22 on v20

--- a/solution.py
+++ b/solution.py
@@ -303,23 +303,21 @@
     normed, inverse = norm_apply(tokens_wide, prenorm_full.astype(jnp.float32))
     normed_low = normed.astype(jnp.bfloat16)
     normed_low_g = to_gathered(normed_low, w_rows)
-    keyed = jnp.dot(normed_low_g, key_mat, preferred_element_type=jnp.float32)
-    own_value = jnp.dot(normed_low_g, value_mat, preferred_element_type=jnp.float32)
-    heads_shape = keyed.shape[:2] + (head_count, head_dim)
-    key_rot = (
-        rotate(keyed.reshape(heads_shape), cos_rows, sin_rows)
-        .astype(jnp.bfloat16)
-        .reshape(keyed.shape)
-    )
-    value_mix = (0.5 * own_value + 0.5 * first_wide).astype(jnp.bfloat16)
+    heads_shape = (slots, rows, head_count, head_dim)
 
     half_width = width // 2
-    key_rot = key_rot.reshape(rows, width)
-    value_mix = value_mix.reshape(rows, width)
     kv_halves = []
     for part in range(2):
         cols = slice(part * half_width, (part + 1) * half_width)
-        kv_own = jnp.concatenate([key_rot[:, cols], value_mix[:, cols]], axis=-1)
+        keyed = jnp.dot(normed_low_g, key_mat[:, cols], preferred_element_type=jnp.float32)
+        own_value = jnp.dot(normed_low_g, value_mat[:, cols], preferred_element_type=jnp.float32)
+        key_rot = (
+            rotate(keyed.reshape(slots, rows, head_count // 2, head_dim), cos_rows, sin_rows)
+            .astype(jnp.bfloat16)
+            .reshape(rows, half_width)
+        )
+        value_mix = (0.5 * own_value + 0.5 * first_wide[..., cols]).astype(jnp.bfloat16)
+        kv_own = jnp.concatenate([key_rot, value_mix.reshape(rows, half_width)], axis=-1)
         kv_halves.append(
             lax.all_to_all(
                 jnp.broadcast_to(kv_own[None], (n_ctx, rows, width)), CTX, 0, 0, tiled=False

time: 576 us -> 578 us (level)
    unnamed x96 -> x98, local copies, waits for them, and re-layouts: 13.7 us -> 17.8 us
where the time goes in v22:
time: 578 us; the launch traced here: 571 us
  waiting for transfers between devices  241 us (42%)
  local copies, waits for them, and re-layouts  77.5 us (13%)
  starting transfers between devices  68.5 us (12%)
  Pallas kernels  67.7 us (12%)
  other arithmetic  54.3 us (9%)
  matrix products  46.7 us (8%)
  between operations  15.3 us (3%)
    all_to_all x2, waiting for transfers between devices, body(): lax.all_to_all(jnp.broadcast_to(kv_own[None], (n_ctx, rows, width)), CTX,...  69.3 us
    all_to_all x2, waiting for transfers between devices, body(): lax.all_to_all(kv_back.reshape(n_ctx, rows, kv_back.shape[1]), CTX, 0, 0,...  56.1 us
    ppermute x9, waiting for transfers between devices, ctx_allreduce(): other = lax.ppermute(total, CTX, [(j, j ^ step) for j in range(n_ctx)])  55 us
    pallas_call x2, Pallas kernels, attention_backward(): pl.pallas_call(functools.partial(attn_bwd_kernel, head_dim, scale), out_s...  42.5 us
    ppermute x3, waiting for transfers between devices, z_exchange(): return zh_pair(pack, lax.ppermute(pack, ('zh', 'zl'), Z_CROSS))  34.2 us
    all_to_all x2, starting transfers between devices, body(): lax.all_to_all(kv_back.reshape(n_ctx, rows, kv_back.shape[1]), CTX, 0, 0,...  25.2 us
    pallas_call x2, Pallas kernels, attention_forward(): pl.pallas_call(functools.partial(attn_fwd_kernel, head_dim, scale), out_s...  25.2 us
    ppermute x3, waiting for transfers between devices, z_combine(): got = lax.ppermute(theirs, ('zh', 'zl'), Z_CROSS)  23.1 us
  transfers between devices with their start and end apart: 25, of which 17 were waited for; matrix products, arithmetic and copies ran while one was open for 22% of the time, Pallas kernels for 12%

profile of v22, /device:TPU:0, one launch (start us, length us, event | category | flops | bytes accessed | tf_op | source)
XLA Modules:
  0.0 570.9 jit_solution(9684684891263719669)
XLA Ops:
  9.1 4.2 collective-permute-start.2
  13.3 7.0 %collective-permute-done.2 = bf16[144,1024]{1,0:T(8,128)(2,1)S(1)} collective-permute-done((bf16[144,1024]{1,0:T(8,128)(2,1)S(1)}, bf16[144,1024]{1,0:T(8,128)(2,1)S(1)}, u32[]{:S(2)}, u32[]{:S(2)}) %collective-permute-start.2) | collective-permute-done | bytes 294944 | tf_op jit(solution)/shard_map/ppermute | solution.py:199
  22.5 3.0 collective-permute-start
  26.0 14.8 %collective-permute-done = bf16[304,1024]{1,0:T(8,128)(2,1)S(1)} collective-permute-done((bf16[304,1024]{1,0:T(8,128)(2,1)S(1)}, bf16[304,1024]{1,0:T(8,128)(2,1)S(1)}, u32[]{:S(2)}, u32[]{:S(2)}) %collective-permute-start) | collective-permute-done | bytes 622624 | tf_op jit(solution)/shard_map/ppermute | solution.py:199
  42.0 12.4 %collective-permute-done.1 = bf16[64,5632]{1,0:T(8,128)(2,1)S(1)} collective-permute-done((bf16[64,5632]{1,0:T(8,128)(2,1)S(1)}, bf16[64,5632]{1,0:T(8,128)(2,1)S(1)}, u32[]{:S(2)}, u32[]{:S(2)}) %collective-permute-start.1) | collective-permute-done | bytes 720928 | tf_op jit(solution)/shard_map/ppermute | solution.py:199
  55.9 2.3 all-gather.7.cloned.1.call-done
  61.8 2.8 fusion.62
  67.4 2.3 copy.234
  69.7 2.3 copy.232
  78.2 2.5 broadcast_in_dim.76
  80.7 5.2 all-to-all-start
  87.7 48.2 %all-to-all-done = bf16[8,256,1024]{2,1,0:T(8,128)(2,1)} async-done(((bf16[8,256,1024]{2,1,0:T(8,128)(2,1)}), bf16[8,256,1024]{2,1,0:T(8,128)(2,1)}, u32[]{:S(2)}, u32[]{:S(2)}) %all-to-all-start) | async-done | bytes 4194336 | tf_op jit(solution)/shard_map/all_to_all | solution.py:322
  135.9 2.5 broadcast_in_dim.77
  138.4 17.8 %all-to-all-start.1 = ((bf16[8,256,1024]{2,1,0:T(8,128)(2,1)}), bf16[8,256,1024]{2,1,0:T(8,128)(2,1)}, u32[]{:S(2)}, u32[]{:S(2)}) async-start(bf16[8,256,1024]{2,1,0:T(8,128)(2,1)} %broadcast_in_dim.77), calls=%async_computation.1 | async-start | bytes 8388608 | tf_op jit(solution)/shard_map/all_to_all | solution.py:322
  158.8 4.1 fusion.61
  162.9 4.0 copy.181
  166.9 2.3 convolution_bitcast_fusion.3
  171.4 12.4 %shard_map.229 = bf16[256,512]{1,0:T(8,128)(2,1)S(1)} custom-call(s32[2]{0:T(128)S(1)} %pad_add_fusion.meta_ref, bf16[256,512]{1,0:T(8,128)(2,1)S(1)} %copy.233.q_ref, bf16[2048,1024]{1,0:T(8,128)(2,1)} %bitcast.24.k_ref.v_ref, bf16[2048,1024]{1,0:T(8,128)(2,1)} %bitcast.24.k_ref.v_ref), custom_call_target="tpu_custom_call" | custom-call | flops 1073741824 | bytes 4718592 | tf_op jit(solution)/shard_map/pallas_call | solution.py:80
  183.8 21.1 %all-to-all-done.1 = bf16[8,256,1024]{2,1,0:T(8,128)(2,1)} async-done(((bf16[8,256,1024]{2,1,0:T(8,128)(2,1)}), bf16[8,256,1024]{2,1,0:T(8,128)(2,1)}, u32[]{:S(2)}, u32[]{:S(2)}) %all-to-all-start.1) | async-done | bytes 4194336 | tf_op jit(solution)/shard_map/all_to_all | solution.py:322
  205.0 12.8 %shard_map.230 = bf16[256,512]{1,0:T(8,128)(2,1)S(1)} custom-call(s32[2]{0:T(128)S(1)} %pad_add_fusion.meta_ref, bf16[256,512]{1,0:T(8,128)(2,1)S(1)} %copy.235.q_ref, bf16[2048,1024]{1,0:T(8,128)(2,1)} %bitcast.39.k_ref.v_ref, bf16[2048,1024]{1,0:T(8,128)(2,1)} %bitcast.39.k_ref.v_ref), custom_call_target="tpu_custom_call" | custom-call | flops 1073741824 | bytes 4718592 | tf_op jit(solution)/shard_map/pallas_call | solution.py:80
  218.6 2.0 copy.188
  220.6 1.9 copy.189
  222.5 3.4 slice.174
  230.2 3.4 copy.196
  233.6 2.0 multiply_reduce_fusion.2
  237.5 2.0 copy.191
  239.6 1.9 copy.192
  241.5 6.4 %convolution_bitcast_fusion = f32[1,256,5632]{2,1,0:T(8,128)S(1)} fusion(bf16[256,1024]{0,1:T(8,128)(2,1)} %bitcast.276, bf16[1024,5632]{1,0:T(8,128)(2,1)} %bitcast.266), kind=kOutput, calls=%fused_computation.6 | convolution fusion | flops 2952790016 | bytes 17825792 | tf_op jit(solution)/shard_map/dot_general | solution.py:347
  247.9 2.7 multiply_convert_fusion.1
  250.6 3.2 fusion.6
  254.8 2.6 copy.199
  257.4 2.0 multiply_reduce_fusion
  259.4 2.1 subtract_add_fusion
  261.6 6.0 %convolution_convert_fusion = bf16[8,128,5632]{2,1,0:T(8,128)(2,1)} fusion(bf16[8,128,256]{2,1,0:T(8,128)(2,1)S(1)} %bitcast.277, bf16[1,256,2816]{2,1,0:T(8,128)(2,1)S(1)} %copy-done.21, bf16[1,256,2816]{2,1,0:T(8,128)(2,1)S(1)} %copy-done.19), kind=kOutput, calls=%fused_computation.3 | convolution fusion | flops 2964324352 | bytes 14942208 | tf_op jit(solution)/shard_map/srd,srf->df/dot_general | solution.py:365
  268.3 11.3 %pad_maximum_fusion = bf16[8,128,6656]{2,1,0:T(8,128)(2,1)} fusion(bf16[8,128,1024]{2,1,0:T(8,128)(2,1)S(1)} %convolution_convert_fusion.2, bf16[8,128,5632]{2,1,0:T(8,128)(2,1)} %convolution_convert_fusion), kind=kLoop, calls=%fused_computation.1 | loop fusion | flops 27262976 | bytes 27262976 | tf_op jit(solution)/shard_map/concatenate | solution.py:383
  279.7 2.8 convolution_convert_fusion.6
  284.6 21.3 %shard_map.232 = (f32[256,512]{1,0:T(8,128)S(1)}, bf16[2048,1024]{1,0:T(8,128)(2,1)S(1)}) custom-call(s32[2]{0:T(128)S(1)} %pad_add_fusion.meta_ref, bf16[256,512]{1,0:T(8,128)(2,1)S(1)} %copy.235.q_ref, bf16[2048,1024]{1,0:T(8,128)(2,1)} %bitcast.39.k_ref.v_ref, bf16[2048,1024]{1,0:T(8,128)(2,1)} %bitcast.39.k_ref.v_ref, bf16[256,512]{1,0:T(8,128)(2,1)S(1)} %copy.237.do_ref), custom_call_target="tpu_custom_call" | custom-call | flops 2684354560 | bytes 9699328 | tf_op jit(solution)/shard_map/pallas_call | solution.py:109
  305.9 2.0 copy-done
  307.9 15.1 %all-to-all-start.3 = ((bf16[8,256,1024]{2,1,0:T(8,128)(2,1)}), bf16[8,256,1024]{2,1,0:T(8,128)(2,1)}, u32[]{:S(2)}, u32[]{:S(2)}) async-start(bf16[8,256,1024]{2,1,0:T(8,128)(2,1)} %bitcast.248), calls=%async_computation.3 | async-start | bytes 8388608 | tf_op jit(solution)/shard_map/all_to_all | solution.py:418
  326.5 4.3 convolution_convert_fusion.1
  331.9 21.3 %shard_map.231 = (f32[256,512]{1,0:T(8,128)S(1)}, bf16[2048,1024]{1,0:T(8,128)(2,1)S(1)}) custom-call(s32[2]{0:T(128)S(1)} %pad_add_fusion.meta_ref, bf16[256,512]{1,0:T(8,128)(2,1)S(1)} %copy.233.q_ref, bf16[2048,1024]{1,0:T(8,128)(2,1)} %bitcast.24.k_ref.v_ref, bf16[2048,1024]{1,0:T(8,128)(2,1)} %bitcast.24.k_ref.v_ref, bf16[256,512]{1,0:T(8,128)(2,1)S(1)} %copy.236.do_ref), custom_call_target="tpu_custom_call" | custom-call | flops 2684354560 | bytes 9699328 | tf_op jit(solution)/shard_map/pallas_call | solution.py:109
  353.2 1.9 copy-done.1
  355.1 15.4 %all-to-all-done.3 = bf16[8,256,1024]{2,1,0:T(8,128)(2,1)} async-done(((bf16[8,256,1024]{2,1,0:T(8,128)(2,1)}), bf16[8,256,1024]{2,1,0:T(8,128)(2,1)}, u32[]{:S(2)}, u32[]{:S(2)}) %all-to-all-start.3) | async-done | bytes 4194336 | tf_op jit(solution)/shard_map/all_to_all | solution.py:418
  370.5 10.1 %all-to-all-start.2 = ((bf16[8,256,1024]{2,1,0:T(8,128)(2,1)}), bf16[8,256,1024]{2,1,0:T(8,128)(2,1)}, u32[]{:S(2)}, u32[]{:S(2)}) async-start(bf16[8,256,1024]{2,1,0:T(8,128)(2,1)} %bitcast.249), calls=%async_computation.2 | async-start | bytes 8388608 | tf_op jit(solution)/shard_map/all_to_all | solution.py:418
  381.6 3.3 convert_reduce_fusion
  386.2 40.7 %all-to-all-done.2 = bf16[8,256,1024]{2,1,0:T(8,128)(2,1)} async-done(((bf16[8,256,1024]{2,1,0:T(8,128)(2,1)}), bf16[8,256,1024]{2,1,0:T(8,128)(2,1)}, u32[]{:S(2)}, u32[]{:S(2)}) %all-to-all-start.2) | async-done | bytes 4194336 | tf_op jit(solution)/shard_map/all_to_all | solution.py:418
  426.9 3.2 convert_reduce_fusion.1
  431.4 2.8 fusion.59
  447.3 3.3 fusion.1
  451.8 2.0 collective-permute-start.7
  456.3 18.7 %collective-permute-done.7 = bf16[64,6656]{1,0:T(8,128)(2,1)S(1)} collective-permute-done((bf16[64,6656]{1,0:T(8,128)(2,1)S(1)}, bf16[64,6656]{1,0:T(8,128)(2,1)S(1)}, u32[]{:S(2)}, u32[]{:S(2)}) %collective-permute-start.7) | collective-permute-done | bytes 852000 | tf_op jit(solution)/shard_map/ppermute | solution.py:225
  476.9 4.4 collective-permute-done.11
  481.5 22.3 %collective-permute-done.12 = bf16[176,1024]{1,0:T(8,128)(2,1)S(1)} collective-permute-done((bf16[176,1024]{1,0:T(8,128)(2,1)S(1)}, bf16[176,1024]{1,0:T(8,128)(2,1)S(1)}, u32[]{:S(2)}, u32[]{:S(2)}) %collective-permute-start.12) | collective-permute-done | bytes 360480 | tf_op jit(solution)/shard_map/ppermute | solution.py:233
  505.2 3.5 collective-permute-start.9
  508.7 5.2 fusion.11
  515.2 2.6 collective-permute-done.13
  517.8 1.9 add_convert_fusion.7
  520.9 2.4 collective-permute-start.3
  523.3 7.0 %collective-permute-done.9 = bf16[64,6656]{1,0:T(8,128)(2,1)} collective-permute-done((bf16[64,6656]{1,0:T(8,128)(2,1)S(1)}, bf16[64,6656]{1,0:T(8,128)(2,1)}, u32[]{:S(2)}, u32[]{:S(2)}) %collective-permute-start.9) | collective-permute-done | bytes 852000 | tf_op jit(solution)/shard_map/ppermute | solution.py:233
  534.2 2.0 fusion.46
  536.2 7.8 %collective-permute-done.4 = bf16[208,1024]{1,0:T(8,128)(2,1)S(1)} collective-permute-done((bf16[208,1024]{1,0:T(8,128)(2,1)S(1)}, bf16[208,1024]{1,0:T(8,128)(2,1)S(1)}, u32[]{:S(2)}, u32[]{:S(2)}) %collective-permute-start.4) | collective-permute-done | bytes 426016 | tf_op jit(solution)/shard_map/ppermute | solution.py:233
  544.3 2.6 collective-permute-done.10
  547.8 6.1 %collective-permute-done.5 = bf16[208,1024]{1,0:T(8,128)(2,1)S(1)} collective-permute-done((bf16[208,1024]{1,0:T(8,128)(2,1)S(1)}, bf16[208,1024]{1,0:T(8,128)(2,1)S(1)}, u32[]{:S(2)}, u32[]{:S(2)}) %collective-permute-start.5) | collective-permute-done | bytes 426016 | tf_op jit(solution)/shard_map/ppermute | solution.py:233
  555.8 6.5 %collective-permute-done.6 = bf16[208,1024]{1,0:T(8,128)(2,1)S(1)} collective-permute-done((bf16[208,1024]{1,0:T(8,128)(2,1)S(1)}, bf16[208,1024]{1,0:T(8,128)(2,1)S(1)}, u32[]{:S(2)}, u32[]{:S(2)}) %collective-permute-start.6) | collective-permute-done | bytes 426016 | tf_op jit(solution)/shard_map/ppermute | solution.py:233
  (224 shorter events, 76.1 us)
Async XLA Ops:
  7.2 15.2 %copy-start.37 = (bf16[64,1024]{1,0:T(8,128)(2,1)S(1)}, bf16[64,1024]{1,0:T(8,128)(2,1)}, u32[]{:S(2)}) copy-start(bf16[64,1024]{1,0:T(8,128)(2,1)} %param.16) | copy-start | bytes 393220
  7.2 15.2 %copy-start.38 = (bf16[64,1024]{1,0:T(8,128)(2,1)S(1)}, bf16[64,1024]{1,0:T(8,128)(2,1)}, u32[]{:S(2)}) copy-start(bf16[64,1024]{1,0:T(8,128)(2,1)} %param.19) | copy-start | bytes 393220
  7.2 15.3 %copy-start.34 = (bf16[176,1024]{1,0:T(8,128)(2,1)S(1)}, bf16[176,1024]{1,0:T(8,128)(2,1)}, u32[]{:S(2)}) copy-start(bf16[176,1024]{1,0:T(8,128)(2,1)} %param.22) | copy-start | bytes 1081348
  7.2 18.3 %copy-start.35 = (bf16[64,2816]{1,0:T(8,128)(2,1)S(1)}, bf16[64,2816]{1,0:T(8,128)(2,1)}, u32[]{:S(2)}) copy-start(bf16[64,2816]{1,0:T(8,128)(2,1)} %param.20) | copy-start | bytes 1081348
  7.2 18.3 %copy-start.36 = (bf16[64,2816]{1,0:T(8,128)(2,1)S(1)}, bf16[64,2816]{1,0:T(8,128)(2,1)}, u32[]{:S(2)}) copy-start(bf16[64,2816]{1,0:T(8,128)(2,1)} %param.21) | copy-start | bytes 1081348
  7.2 50.9 %all-gather.7.cloned.1.call-start = ((), (), s32[]{:S(2)}) async-start(), calls=%async_computation.10 | async-start | bytes 5308416 | tf_op jit(solution)/shard_map/all_gather | solution.py:203
  9.1 11.2 %collective-permute-start.2 = (bf16[144,1024]{1,0:T(8,128)(2,1)S(1)}, bf16[144,1024]{1,0:T(8,128)(2,1)S(1)}, u32[]{:S(2)}, u32[]{:S(2)}) collective-permute-start(bf16[144,1024]{1,0:T(8,128)(2,1)S(1)} %fusion.47), channel_id=1, source_target_pairs={{0,68},{68,0},{4,64},{64,4},{1,69},{69,1},{5,65},{65,5},{2,70},{70... | collective-permute-start | bytes 884744 | tf_op jit(solution)/shard_map/ppermute | solution.py:199
  22.3 136.4 %all-gather.9.cloned.1.call-start = ((), (), s32[]{:S(2)}) async-start(), calls=%async_computation.11 | async-start | bytes 11206656 | tf_op jit(solution)/shard_map/all_gather | solution.py:203
  22.5 18.3 %collective-permute-start = (bf16[304,1024]{1,0:T(8,128)(2,1)S(1)}, bf16[304,1024]{1,0:T(8,128)(2,1)S(1)}, u32[]{:S(2)}, u32[]{:S(2)}) collective-permute-start(bf16[304,1024]{1,0:T(8,128)(2,1)S(1)} %constant_dynamic-update-slice_fusion), channel_id=1, source_target_pairs={{0,68},{68,0},{4,64},{64,4},{1,69},{69,1},{5,65},{65,5},{2,70},{70... | collective-permute-start | bytes 1867784 | tf_op jit(solution)/shard_map/ppermute | solution.py:199
  25.6 28.9 %collective-permute-start.1 = (bf16[64,5632]{1,0:T(8,128)(2,1)S(1)}, bf16[64,5632]{1,0:T(8,128)(2,1)S(1)}, u32[]{:S(2)}, u32[]{:S(2)}) collective-permute-start(bf16[64,5632]{1,0:T(8,128)(2,1)S(1)} %constant_dynamic-update-slice_fusion.3), channel_id=1, source_target_pairs={{0,68},{68,0},{4,64},{64,4},{1,69},{69,1},{5,65},{65,5},{2,70},{70... | collective-permute-start | bytes 2162696 | tf_op jit(solution)/shard_map/ppermute | solution.py:199
  54.6 4.3 copy-start.33
  54.6 5.4 copy-start.9
  58.1 183.3 %all-gather.11.cloned.1.call-start = ((), (), s32[]{:S(2)}) async-start(), calls=%async_computation.12 | async-start | bytes 12976128 | tf_op jit(solution)/shard_map/all_gather | solution.py:203
  64.6 21.5 %copy-start.14 = (bf16[16,64,1024]{2,1,0:T(8,128)(2,1)}, bf16[16,64,1024]{2,1,0:T(8,128)(2,1)S(1)}, u32[]{:S(2)}) copy-start(bf16[16,64,1024]{2,1,0:T(8,128)(2,1)S(1)} %get-tuple-element.100) | copy-start | bytes 6291460
  80.7 55.2 %all-to-all-start = ((bf16[8,256,1024]{2,1,0:T(8,128)(2,1)}), bf16[8,256,1024]{2,1,0:T(8,128)(2,1)}, u32[]{:S(2)}, u32[]{:S(2)}) async-start(bf16[8,256,1024]{2,1,0:T(8,128)(2,1)} %broadcast_in_dim.76), calls=%async_computation | async-start | bytes 8388608 | tf_op jit(solution)/shard_map/all_to_all | solution.py:322
  138.4 18.1 %copy-start.39 = (s32[16]{0:T(128)S(1)}, s32[16]{0:T(128)}, u32[]{:S(2)}) copy-start(s32[16]{0:T(128)} %param.26) | copy-start | bytes 196
  138.4 18.1 %copy-start.40 = (s32[16]{0:T(128)S(1)}, s32[16]{0:T(128)}, u32[]{:S(2)}) copy-start(s32[16]{0:T(128)} %param.27) | copy-start | bytes 196
  138.4 66.5 %all-to-all-start.1 = ((bf16[8,256,1024]{2,1,0:T(8,128)(2,1)}), bf16[8,256,1024]{2,1,0:T(8,128)(2,1)}, u32[]{:S(2)}, u32[]{:S(2)}) async-start(bf16[8,256,1024]{2,1,0:T(8,128)(2,1)} %broadcast_in_dim.77), calls=%async_computation.1 | async-start | bytes 8388608 | tf_op jit(solution)/shard_map/all_to_all | solution.py:322
  156.2 294.3 %reduce-scatter.4.cloned.1.call-start = ((), (), s32[]{:S(2)}) async-start(), calls=%async_computation.7 | async-start | bytes 15335424 | tf_op jit(solution)/shard_map/reduce_scatter | solution.py:215
  222.5 3.4 copy-start.27
  225.9 2.5 copy-start.22
  241.5 6.4 %copy-start.11 = (f32[1,256,2816]{2,1,0:T(8,128)S(1)}, f32[1,256,2816]{2,1,0:T(8,128)}, u32[]{:S(2)}) copy-start(f32[1,256,2816]{2,1,0:T(8,128)} %copy.196) | copy-start | bytes 8650756
  241.5 9.1 %slice-start = ((s8[11534336]{0:T(1024)(128)(4,1)}), s8[4194304]{0:T(1024)(128)(4,1)S(1)}, s32[]{:S(2)}) async-start(s8[11534336]{0:T(1024)(128)(4,1)} %bitcast.267), calls=%async_computation.13 | async-start | bytes 8388608
  241.5 9.1 %slice-start.1 = ((s8[11534336]{0:T(1024)(128)(4,1)}), s8[4194304]{0:T(1024)(128)(4,1)S(1)}, s32[]{:S(2)}) async-start(s8[11534336]{0:T(1024)(128)(4,1)} %bitcast.267), calls=%async_computation.14 | async-start | bytes 8388608
  247.9 2.7 slice-start.2
  250.6 3.2 copy-start.18
  250.6 3.2 copy-start.20
  257.4 4.1 copy-start.16
  257.4 4.1 copy-start.19
  257.4 4.1 copy-start.21
  261.5 6.0 %copy-start.5 = (f32[1,256,1024]{2,1,0:T(8,128)}, f32[1,256,1024]{2,1,0:T(8,128)S(1)}, u32[]{:S(2)}) copy-start(f32[1,256,1024]{2,1,0:T(8,128)S(1)} %subtract_add_fusion) | copy-start | bytes 3145732
  261.6 6.0 %copy-start.23 = (bf16[1,256,8,2,64]{1,4,3,2,0:T(8,128)(2,1)S(1)}, bf16[1,256,8,2,64]{1,4,3,2,0:T(8,128)(2,1)}, u32[]{:S(2)}) copy-start(bf16[1,256,8,2,64]{1,4,3,2,0:T(8,128)(2,1)} %copy.189) | copy-start | bytes 1572868
  305.9 2.0 copy-start
  307.9 15.2 %copy-start.17 = (bf16[1,256,2816]{2,1,0:T(8,128)(2,1)S(1)}, bf16[1,256,2816]{2,1,0:T(8,128)(2,1)}, u32[]{:S(2)}) copy-start(bf16[1,256,2816]{2,1,0:T(8,128)(2,1)} %get-tuple-element.96) | copy-start | bytes 4325380
  307.9 62.6 %all-to-all-start.3 = ((bf16[8,256,1024]{2,1,0:T(8,128)(2,1)}), bf16[8,256,1024]{2,1,0:T(8,128)(2,1)}, u32[]{:S(2)}, u32[]{:S(2)}) async-start(bf16[8,256,1024]{2,1,0:T(8,128)(2,1)} %bitcast.248), calls=%async_computation.3 | async-start | bytes 8388608 | tf_op jit(solution)/shard_map/all_to_all | solution.py:418
  323.0 130.8 %reduce-scatter.8.cloned.1.call-start = ((), (), s32[]{:S(2)}) async-start(), calls=%async_computation.9 | async-start | bytes 6488064 | tf_op jit(solution)/shard_map/reduce_scatter | solution.py:215
  323.1 3.4 copy-start.28
  326.5 4.3 copy-start.12
  353.2 2.0 copy-start.1
  370.5 56.3 %all-to-all-start.2 = ((bf16[8,256,1024]{2,1,0:T(8,128)(2,1)}), bf16[8,256,1024]{2,1,0:T(8,128)(2,1)}, u32[]{:S(2)}, u32[]{:S(2)}) async-start(bf16[8,256,1024]{2,1,0:T(8,128)(2,1)} %bitcast.249), calls=%async_computation.2 | async-start | bytes 8388608 | tf_op jit(solution)/shard_map/all_to_all | solution.py:418
  380.6 139.1 %reduce-scatter.6.cloned.1.call-start = ((), (), s32[]{:S(2)}) async-start(), calls=%async_computation.8 | async-start | bytes 7667712 | tf_op jit(solution)/shard_map/reduce_scatter | solution.py:215
  434.1 1.8 copy-start.4
  434.5 2.2 copy-start.3
  434.6 3.0 copy-start.24
  436.7 1.6 copy-start.15
  440.0 4.3 copy-start.10
  451.8 23.2 %collective-permute-start.7 = (bf16[64,6656]{1,0:T(8,128)(2,1)S(1)}, bf16[64,6656]{1,0:T(8,128)(2,1)S(1)}, u32[]{:S(2)}, u32[]{:S(2)}) collective-permute-start(bf16[64,6656]{1,0:T(8,128)(2,1)S(1)} %dynamic-slice_bitcast_fusion), channel_id=1, source_target_pairs={{0,68},{68,0},{4,64},{64,4},{1,69},{69,1},{5,65},{65,5},{2,70},{70... | collective-permute-start | bytes 2555912 | tf_op jit(solution)/shard_map/ppermute | solution.py:225
  453.8 27.5 %copy-start.32 = (bf16[1,352,1024]{2,1,0:T(8,128)(2,1)S(1)}, bf16[1,352,1024]{2,1,0:T(8,128)(2,1)}, u32[]{:S(2)}) copy-start(bf16[1,352,1024]{2,1,0:T(8,128)(2,1)} %reduce-scatter.8.cloned.1.call-done) | copy-start | bytes 2162692
  454.9 26.4 %collective-permute-start.11 = (bf16[176,1024]{1,0:T(8,128)(2,1)S(1)}, bf16[176,1024]{1,0:T(8,128)(2,1)S(1)}, u32[]{:S(2)}, u32[]{:S(2)}) collective-permute-start(bf16[176,1024]{1,0:T(8,128)(2,1)S(1)} %dynamic-slice_bitcast_fusion.2), channel_id=1, source_target_pairs={{0,68},{68,0},{4,64},{64,4},{1,69},{69,1},{5,65},{65,5},{2,70},{70... | collective-permute-start | bytes 1081352 | tf_op jit(solution)/shard_map/ppermute | solution.py:225
  476.3 32.3 %copy-start.8 = (f32[1,256,1024]{2,1,0:T(8,128)S(1)}, f32[1,256,1024]{2,1,0:T(8,128)}, u32[]{:S(2)}) copy-start(f32[1,256,1024]{2,1,0:T(8,128)} %copy-done.7) | copy-start | bytes 3145732
  476.3 32.3 %copy-start.13 = (bf16[1,256,8,2,176]{1,4,3,2,0:T(8,128)(2,1)S(1)}, bf16[1,256,8,2,176]{1,4,3,2,0:T(8,128)(2,1)}, u32[]{:S(2)}) copy-start(bf16[1,256,8,2,176]{1,4,3,2,0:T(8,128)(2,1)} %copy-done.12) | copy-start | bytes 4325380
  476.3 28.6 %collective-permute-start.8 = (bf16[64,6656]{1,0:T(8,128)(2,1)S(1)}, bf16[64,6656]{1,0:T(8,128)(2,1)S(1)}, u32[]{:S(2)}, u32[]{:S(2)}) collective-permute-start(bf16[64,6656]{1,0:T(8,128)(2,1)S(1)} %fusion.5), channel_id=1, source_target_pairs={{0,1},{1,0},{2,3},{3,2},{4,5},{5,4},{6,7},{7,6},{8,9},{9,8},{10,11... | collective-permute-start | bytes 2555912 | tf_op jit(solution)/shard_map/ppermute | solution.py:233
  481.4 22.4 %collective-permute-start.12 = (bf16[176,1024]{1,0:T(8,128)(2,1)S(1)}, bf16[176,1024]{1,0:T(8,128)(2,1)S(1)}, u32[]{:S(2)}, u32[]{:S(2)}) collective-permute-start(bf16[176,1024]{1,0:T(8,128)(2,1)S(1)} %fusion.38), channel_id=1, source_target_pairs={{0,1},{1,0},{2,3},{3,2},{4,5},{5,4},{6,7},{7,6},{8,9},{9,8},{10,11... | collective-permute-start | bytes 1081352 | tf_op jit(solution)/shard_map/ppermute | solution.py:233
  504.7 13.2 %collective-permute-start.13 = (bf16[176,1024]{1,0:T(8,128)(2,1)}, bf16[176,1024]{1,0:T(8,128)(2,1)}, u32[]{:S(2)}, u32[]{:S(2)}) collective-permute-start(bf16[176,1024]{1,0:T(8,128)(2,1)} %add_convert_fusion.8), channel_id=1, source_target_pairs={{0,2},{1,3},{2,0},{3,1},{4,6},{5,7},{6,4},{7,5},{8,10},{9,11},{10,... | collective-permute-start | bytes 1081352 | tf_op jit(solution)/shard_map/ppermute | solution.py:233
  505.2 25.1 %collective-permute-start.9 = (bf16[64,6656]{1,0:T(8,128)(2,1)S(1)}, bf16[64,6656]{1,0:T(8,128)(2,1)}, u32[]{:S(2)}, u32[]{:S(2)}) collective-permute-start(bf16[64,6656]{1,0:T(8,128)(2,1)S(1)} %add_convert_fusion.2), channel_id=1, source_target_pairs={{0,2},{1,3},{2,0},{3,1},{4,6},{5,7},{6,4},{7,5},{8,10},{9,11},{10,... | collective-permute-start | bytes 2555912 | tf_op jit(solution)/shard_map/ppermute | solution.py:233
  508.7 5.2 copy-start.26
  515.2 17.6 %copy-start.6 = (f32[1,256,1024]{2,1,0:T(8,128)S(1)}, f32[1,256,1024]{2,1,0:T(8,128)}, u32[]{:S(2)}) copy-start(f32[1,256,1024]{2,1,0:T(8,128)} %copy-done.5) | copy-start | bytes 3145732
  519.8 14.4 %collective-permute-start.14 = (bf16[176,1024]{1,0:T(8,128)(2,1)}, bf16[176,1024]{1,0:T(8,128)(2,1)}, u32[]{:S(2)}, u32[]{:S(2)}) collective-permute-start(bf16[176,1024]{1,0:T(8,128)(2,1)} %add_convert_fusion.7), channel_id=1, source_target_pairs={{0,4},{1,5},{2,6},{3,7},{4,0},{5,1},{6,2},{7,3},{8,12},{9,13},{10,... | collective-permute-start | bytes 1081352 | tf_op jit(solution)/shard_map/ppermute | solution.py:233
  519.8 12.8 %copy-start.31 = (bf16[1,416,1024]{2,1,0:T(8,128)(2,1)S(1)}, bf16[1,416,1024]{2,1,0:T(8,128)(2,1)}, u32[]{:S(2)}) copy-start(bf16[1,416,1024]{2,1,0:T(8,128)(2,1)} %reduce-scatter.6.cloned.1.call-done) | copy-start | bytes 2555908
  520.9 11.6 %collective-permute-start.3 = (bf16[208,1024]{1,0:T(8,128)(2,1)S(1)}, bf16[208,1024]{1,0:T(8,128)(2,1)S(1)}, u32[]{:S(2)}, u32[]{:S(2)}) collective-permute-start(bf16[208,1024]{1,0:T(8,128)(2,1)S(1)} %dynamic-slice_bitcast_fusion.1), channel_id=1, source_target_pairs={{0,68},{68,0},{4,64},{64,4},{1,69},{69,1},{5,65},{65,5},{2,70},{70... | collective-permute-start | bytes 1277960 | tf_op jit(solution)/shard_map/ppermute | solution.py:225
  531.7 15.3 %collective-permute-start.10 = (bf16[64,6656]{1,0:T(8,128)(2,1)S(1)}, bf16[64,6656]{1,0:T(8,128)(2,1)S(1)}, u32[]{:S(2)}, u32[]{:S(2)}) collective-permute-start(bf16[64,6656]{1,0:T(8,128)(2,1)S(1)} %add_convert_fusion.1), channel_id=1, source_target_pairs={{0,4},{1,5},{2,6},{3,7},{4,0},{5,1},{6,2},{7,3},{8,12},{9,13},{10,... | collective-permute-start | bytes 2555912 | tf_op jit(solution)/shard_map/ppermute | solution.py:233
  532.7 11.3 %collective-permute-start.4 = (bf16[208,1024]{1,0:T(8,128)(2,1)S(1)}, bf16[208,1024]{1,0:T(8,128)(2,1)S(1)}, u32[]{:S(2)}, u32[]{:S(2)}) collective-permute-start(bf16[208,1024]{1,0:T(8,128)(2,1)S(1)} %fusion.37), channel_id=1, source_target_pairs={{0,1},{1,0},{2,3},{3,2},{4,5},{5,4},{6,7},{7,6},{8,9},{9,8},{10,11... | collective-permute-start | bytes 1277960 | tf_op jit(solution)/shard_map/ppermute | solution.py:233
  544.2 9.7 %collective-permute-start.5 = (bf16[208,1024]{1,0:T(8,128)(2,1)S(1)}, bf16[208,1024]{1,0:T(8,128)(2,1)S(1)}, u32[]{:S(2)}, u32[]{:S(2)}) collective-permute-start(bf16[208,1024]{1,0:T(8,128)(2,1)S(1)} %add_convert_fusion.5), channel_id=1, source_target_pairs={{0,2},{1,3},{2,0},{3,1},{4,6},{5,7},{6,4},{7,5},{8,10},{9,11},{10,... | collective-permute-start | bytes 1277960 | tf_op jit(solution)/shard_map/ppermute | solution.py:233
  554.1 8.2 %collective-permute-start.6 = (bf16[208,1024]{1,0:T(8,128)(2,1)S(1)}, bf16[208,1024]{1,0:T(8,128)(2,1)S(1)}, u32[]{:S(2)}, u32[]{:S(2)}) collective-permute-start(bf16[208,1024]{1,0:T(8,128)(2,1)S(1)} %add_convert_fusion.4), channel_id=1, source_target_pairs={{0,4},{1,5},{2,6},{3,7},{4,0},{5,1},{6,2},{7,3},{8,12},{9,13},{10,... | collective-permute-start | bytes 1277960 | tf_op jit(solution)/shard_map/ppermute | solution.py:233
  (5 other events, 5.9 us)
Sparse Core Ops, SparseCore 0:
  22.5 35.6 all-gather.6
  59.8 56.3 all-gather.8
  117.9 63.1 all-gather.10
  279.8 86.6 reduce-scatter.3
  368.7 41.8 reduce-scatter.7
  450.7 43.3 reduce-scatter.5
